TPU v7x, 32 devices: a whole 2x2x4 slice. The times are simulated.
32 devices in a mesh: section: 2 (over core), dp: 8 (over z, x), mp: 2 (over y).
Axes of the slice: x: 2, y: 2, z: 4, core: 2. Of those that a mesh axis runs over, the one named last changes fastest.
Arguments:
- block_input: bfloat16 [2, 256, 16, 1024], P('section', 'dp'), may hold values from -6 to 6
- norm_gain: float32 [2, 1024], P('section'), may hold values from 0.5 to 1.5
- lstm_in: bfloat16 [2, 1024, 4, 1024], P('section', 'dp', None, 'mp'), may hold values from -0.1875 to 0.1875
- lstm_rec: bfloat16 [2, 1024, 4, 1024], P('section', 'dp', None, 'mp'), may hold values from -0.4375 to 0.4375
- lstm_bias: bfloat16 [2, 4, 1024], P('section', None, 'mp'), may hold values from -1.25 to 2.75
- mono_mem: bfloat16 [1024, 1024], P('dp', ('section', 'mp')), may hold values from -0.1875 to 0.1875
- mono_dec: bfloat16 [1024, 1024], P('dp', ('section', 'mp')), may hold values from -0.1875 to 0.1875
- mono_bias: float32 [1024], P(('section', 'mp')), may hold values from -3 to 3
- mono_vec: float32 [1024], P(('section', 'mp')), may hold values from -0.6 to 0.6
- span_mem: bfloat16 [1024, 1024], P('dp', ('section', 'mp')), may hold values from -0.1875 to 0.1875
- span_dec: bfloat16 [1024, 1024], P('dp', ('section', 'mp')), may hold values from -0.1875 to 0.1875
- span_bias: float32 [1024], P(('section', 'mp')), may hold values from -3 to 3
- span_vec: float32 [1024], P(('section', 'mp')), may hold values from -0.6 to 0.6
- out_weight: bfloat16 [2, 1024, 1024], P(None, 'dp', ('section', 'mp')), may hold values from -0.125 to 0.125
- out_bias: float32 [1024], P(('section', 'mp')), may hold values from -2 to 2
- vocab_weight: bfloat16 [1024, 1000], P(('section', 'mp')), may hold values from -1 to 1
- vocab_bias: float32 [1000], replicated, may hold values from -3 to 3
- noise: float32 [256, 16, 16], P('dp'), may hold values from 0 to 4
- enc_lengths: int32 [256], P('dp'), may hold values from 1 to 16, as said below
- label_lengths: int32 [256], P('dp'), may hold values from 1 to 16, as said below
- labels: int32 [256, 16], P('dp'), may hold values from 0 to 999
Outputs:
- input_grad: float32 [2, 256, 16, 1024], P('section', 'dp')
- norm_gain_grad: float32 [2, 1024], P('section')
- lstm_in_grad: float32 [2, 1024, 4, 1024], P('section', 'dp', None, 'mp')
- lstm_rec_grad: float32 [2, 1024, 4, 1024], P('section', 'dp', None, 'mp')
- lstm_bias_grad: float32 [2, 4, 1024], P('section', None, 'mp')
- mono_mem_grad: float32 [1024, 1024], P('dp', ('section', 'mp'))
- mono_dec_grad: float32 [1024, 1024], P('dp', ('section', 'mp'))
- mono_bias_grad: float32 [1024], P(('section', 'mp'))
- mono_vec_grad: float32 [1024], P(('section', 'mp'))
- span_mem_grad: float32 [1024, 1024], P('dp', ('section', 'mp'))
- span_dec_grad: float32 [1024, 1024], P('dp', ('section', 'mp'))
- span_bias_grad: float32 [1024], P(('section', 'mp'))
- span_vec_grad: float32 [1024], P(('section', 'mp'))
- out_weight_grad: float32 [2, 1024, 1024], P(None, 'dp', ('section', 'mp'))
- out_bias_grad: float32 [1024], P(('section', 'mp'))
- vocab_weight_grad: float32 [1024, 1000], P(('section', 'mp'))
- vocab_bias_grad: float32 [1000], replicated
Inputs may be any that keep to these rules, and one draw needn't show every extreme that they name: `enc_lengths`: each utterance has 1 to 16 valid frames; some utterance has exactly 16. `label_lengths`: each utterance has 1 to 16 counted decoder steps; some utterance has exactly 16.
All inputs are finite; a program needn't handle non-finite values.
Results may differ from a plain program's by a relative error of at most 0.02.
Values may be sent and summed in bfloat16 or wider, within the bound.
No kernel may reach another device: no remote copies, remote signals or barrier semaphores. Data moves between devices by JAX's collectives and lax.ppermute only.
A program may use at most 128 MiB of HBM per device.

v0:
```python
import jax
import jax.numpy as jnp
from jax import lax
from jax.sharding import PartitionSpec as P

highest = lax.Precision.HIGHEST
epsilon = 1e-05
offset = -4.0


def normalize(inputs, gain_row):
    average = jnp.mean(inputs, axis=-1, keepdims=True)
    centred = inputs - average
    spread = jnp.mean(centred * centred, axis=-1, keepdims=True)
    return centred * lax.rsqrt(spread + epsilon) * gain_row


def gate_split(gate_values):
    return (
        jax.nn.sigmoid(gate_values[:, 0]),
        jax.nn.sigmoid(gate_values[:, 1]),
        jnp.tanh(gate_values[:, 2]),
        jax.nn.sigmoid(gate_values[:, 3]),
    )


def cell_update(gate_values, cell_state):
    inflow, forget, candidate, outflow = gate_split(gate_values)
    new_cell = forget * cell_state + inflow * candidate
    return (new_cell, outflow * jnp.tanh(new_cell))


def link_pair(earlier, later):
    return (earlier[0] * later[0], later[0] * earlier[1] + later[1])


def monotonic(probable):
    keep_prob = jnp.concatenate(
        [jnp.ones_like(probable[:, :, :1]), 1.0 - probable[:, :, :-1]], axis=2
    )
    frame_count = probable.shape[2]
    initial = jnp.broadcast_to(
        (jnp.arange(frame_count) == 0).astype(jnp.float32), probable[:, 0].shape
    )

    def monotonic_advance(previous, row_pack):
        keep_row, prob_row = row_pack
        _, queued = lax.associative_scan(link_pair, (keep_row, previous), axis=1)
        attended = prob_row * queued
        return (attended, attended)

    _, history = lax.scan(
        monotonic_advance, initial, (jnp.swapaxes(keep_prob, 0, 1), jnp.swapaxes(probable, 0, 1))
    )
    return jnp.swapaxes(history, 0, 1)


def spanwise(span_energy, alphas, frame_mask):
    masked = jnp.where(frame_mask > 0, span_energy, -1e30)
    highest_value = jnp.max(masked, axis=2, keepdims=True)
    scaled = jnp.where(frame_mask > 0, jnp.exp(span_energy - highest_value), 0.0)
    window_sum = scaled + jnp.pad(scaled[:, :, :-1], ((0, 0), (0, 0), (1, 0)))
    ratio = alphas / jnp.where(frame_mask > 0, window_sum, 1.0)
    return scaled * (ratio + jnp.pad(ratio[:, :, 1:], ((0, 0), (0, 0), (0, 1))))


def attention_weights(mono_energy, span_energy, noise_rows, frame_mask):
    probable = jax.nn.sigmoid(mono_energy + offset + noise_rows) * frame_mask
    alphas = monotonic(probable)
    return spanwise(span_energy, alphas, frame_mask)


def forward_scan(project, weight_recur, bias_values, fetch, unit_count):
    row_count = project.shape[1]

    def forward_advance(carried, project_row):
        own_hidden, cell_state = carried
        full_hidden = fetch(own_hidden)
        gate_values = (
            project_row
            + jnp.einsum(
                "bd,dgh->bgh", full_hidden, weight_recur, preferred_element_type=jnp.float32
            )
            + bias_values
        )
        new_cell, emitted = cell_update(gate_values, cell_state)
        emitted_low = emitted.astype(jnp.bfloat16)
        return (
            (emitted_low, new_cell),
            (emitted_low, full_hidden, gate_values, cell_state, new_cell),
        )

    start_state = (
        jnp.zeros((row_count, unit_count), jnp.bfloat16),
        jnp.zeros((row_count, unit_count), jnp.float32),
    )
    _, history = lax.scan(forward_advance, start_state, project)
    return history


def backward_scan(grad_outside, gate_seq, cell_before, cell_after, weight_recur, reduce_fn):
    row_count = grad_outside.shape[1]
    unit_count = grad_outside.shape[2]

    def retreat(carried, row_pack):
        grad_hidden_next, grad_cell = carried
        outside_row, gate_row, before_row, after_row = row_pack
        grad_hidden = outside_row + grad_hidden_next
        inflow, forget, candidate, outflow = gate_split(gate_row)
        squash = jnp.tanh(after_row)
        grad_total = grad_cell + grad_hidden * outflow * (1.0 - squash * squash)
        grad_gates = jnp.stack(
            [
                grad_total * candidate * inflow * (1.0 - inflow),
                grad_total * before_row * forget * (1.0 - forget),
                grad_total * inflow * (1.0 - candidate * candidate),
                grad_hidden * squash * outflow * (1.0 - outflow),
            ],
            axis=1,
        )
        gates_low = grad_gates.astype(jnp.bfloat16)
        grad_prev = reduce_fn(
            jnp.einsum("bgh,dgh->bd", gates_low, weight_recur, preferred_element_type=jnp.float32)
        )
        return ((grad_prev, grad_total * forget), gates_low)

    start_state = (
        jnp.zeros((row_count, unit_count), jnp.float32),
        jnp.zeros((row_count, unit_count), jnp.float32),
    )
    _, gates_low_seq = lax.scan(
        retreat, start_state, (grad_outside, gate_seq, cell_before, cell_after), reverse=True
    )
    return gates_low_seq


def partial_energies(
    mono_query, mono_keys, span_query, span_keys, mono_bias, mono_vec, span_bias, span_vec
):

    def partial_single(row_pack):
        mono_rows, mono_cols, span_rows, span_cols = row_pack
        mono_squash = jnp.tanh(mono_rows[:, None, :] + mono_cols[None, :, :] + mono_bias)
        span_squash = jnp.tanh(span_rows[:, None, :] + span_cols[None, :, :] + span_bias)
        return (jnp.sum(mono_squash * mono_vec, axis=-1), jnp.sum(span_squash * span_vec, axis=-1))

    return lax.map(partial_single, (mono_query, mono_keys, span_query, span_keys))


def energy_backward(grad_energy, queries, keys_all, bias_vec, weight_vec):

    def energy_single(row_pack):
        grad_rows, query_rows, key_rows = row_pack
        squash = jnp.tanh(query_rows[:, None, :] + key_rows[None, :, :] + bias_vec)
        inner = grad_rows[:, :, None] * weight_vec * (1.0 - squash * squash)
        return (
            jnp.sum(inner, axis=1),
            jnp.sum(inner, axis=0),
            jnp.sum(grad_rows[:, :, None] * squash, axis=(0, 1)),
        )

    grad_query, grad_keys, grad_vec_rows = lax.map(energy_single, (grad_energy, queries, keys_all))
    return (grad_query, grad_keys, jnp.sum(grad_query, axis=(0, 1)), jnp.sum(grad_vec_rows, axis=0))


def local(
    block_input,
    norm_gain,
    lstm_in,
    lstm_rec,
    lstm_bias,
    mono_mem,
    mono_dec,
    mono_bias,
    mono_vec,
    span_mem,
    span_dec,
    span_bias,
    span_vec,
    out_weight,
    out_bias,
    vocab_weight,
    vocab_bias,
    noise,
    enc_lengths,
    label_lengths,
    labels,
):
    inputs = block_input[0].astype(jnp.float32)
    frame_count = inputs.shape[1]
    weight_input, weight_recur, mono_mem_all, mono_dec_all, span_mem_all, span_dec_all, out_all = (
        lax.all_gather(lstm_in[0], "dp", axis=0, tiled=True),
        lax.all_gather(lstm_rec[0], "dp", axis=0, tiled=True),
        lax.all_gather(mono_mem, "dp", axis=0, tiled=True),
        lax.all_gather(mono_dec, "dp", axis=0, tiled=True),
        lax.all_gather(span_mem, "dp", axis=0, tiled=True),
        lax.all_gather(span_dec, "dp", axis=0, tiled=True),
        lax.all_gather(out_weight, "dp", axis=1, tiled=True),
    )
    local_units = weight_input.shape[2]
    normed, norm_pullback = jax.vjp(normalize, inputs, norm_gain[0])
    normed_low = normed.astype(jnp.bfloat16)

    def fetch_units(own_hidden):
        return lax.all_gather(own_hidden, "mp", axis=1, tiled=True)

    project = jnp.einsum(
        "bld,dgh->lbgh", normed_low, weight_input, preferred_element_type=jnp.float32
    )
    own_seq, hidden_prev, gate_seq, cell_before, cell_after = forward_scan(
        project, weight_recur, lstm_bias[0].astype(jnp.float32), fetch_units, local_units
    )
    relayed = lax.all_gather(jnp.swapaxes(own_seq, 0, 1), ("section", "mp"), axis=2, tiled=True)
    hidden_width = relayed.shape[2] // 2
    memory = relayed[:, :, :hidden_width]
    decoded = relayed[:, :, hidden_width:]
    mono_keys = jnp.einsum("bjd,de->bje", memory, mono_mem_all, preferred_element_type=jnp.float32)
    mono_query = jnp.einsum(
        "bid,de->bie", decoded, mono_dec_all, preferred_element_type=jnp.float32
    )
    span_keys = jnp.einsum("bjd,de->bje", memory, span_mem_all, preferred_element_type=jnp.float32)
    span_query = jnp.einsum(
        "bid,de->bie", decoded, span_dec_all, preferred_element_type=jnp.float32
    )
    mono_part, span_part = partial_energies(
        mono_query, mono_keys, span_query, span_keys, mono_bias, mono_vec, span_bias, span_vec
    )
    mono_energy, span_energy = lax.psum((mono_part, span_part), ("section", "mp"))
    positions = jnp.arange(frame_count)
    frame_mask = (positions[None, :] < enc_lengths[:, None]).astype(jnp.float32)[:, None, :]
    step_mask = (positions[None, :] < label_lengths[:, None]).astype(jnp.float32)

    def attend(mono_values, span_values):
        return attention_weights(mono_values, span_values, noise, frame_mask)

    beta, attention_pullback = jax.vjp(attend, mono_energy, span_energy)
    beta_low = beta.astype(jnp.bfloat16)
    context_low = jnp.einsum(
        "bij,bjd->bid", beta_low, memory, preferred_element_type=jnp.float32
    ).astype(jnp.bfloat16)
    pre_out = (
        jnp.einsum("bid,dp->bip", decoded, out_all[0], preferred_element_type=jnp.float32)
        + jnp.einsum("bid,dp->bip", context_low, out_all[1], preferred_element_type=jnp.float32)
        + out_bias
    )
    emitted = jnp.tanh(pre_out)
    emitted_low = emitted.astype(jnp.bfloat16)
    logit_part = jnp.einsum(
        "bip,pv->biv", emitted_low, vocab_weight, preferred_element_type=jnp.float32
    )
    logits = lax.psum(logit_part, ("section", "mp")) + vocab_bias
    shifted = jnp.exp(logits - jnp.max(logits, axis=-1, keepdims=True))
    softmax_rows = shifted / jnp.sum(shifted, axis=-1, keepdims=True)
    onehot = (labels[:, :, None] == jnp.arange(vocab_weight.shape[1])[None, None, :]).astype(
        jnp.float32
    )
    grad_logits_low = ((softmax_rows - onehot) * step_mask[:, :, None]).astype(jnp.bfloat16)
    grad_vocab_bias = jnp.sum(grad_logits_low.astype(jnp.float32), axis=(0, 1))
    grad_vocab_weight = jnp.einsum(
        "bip,biv->pv", emitted_low, grad_logits_low, preferred_element_type=jnp.float32
    )
    grad_emitted = jnp.einsum(
        "biv,pv->bip", grad_logits_low, vocab_weight, preferred_element_type=jnp.float32
    )
    grad_pre_low = (grad_emitted * (1.0 - emitted * emitted)).astype(jnp.bfloat16)
    grad_out_bias = jnp.sum(grad_pre_low.astype(jnp.float32), axis=(0, 1))
    grad_out = jnp.stack(
        [
            jnp.einsum("bid,bip->dp", decoded, grad_pre_low, preferred_element_type=jnp.float32),
            jnp.einsum(
                "bid,bip->dp", context_low, grad_pre_low, preferred_element_type=jnp.float32
            ),
        ],
        axis=0,
    )
    grad_decoded = jnp.einsum(
        "bip,dp->bid", grad_pre_low, out_all[0], preferred_element_type=jnp.float32
    )
    grad_context = jnp.einsum(
        "bip,dp->bid", grad_pre_low, out_all[1], preferred_element_type=jnp.float32
    )
    memory_wide = memory.astype(jnp.float32)
    grad_beta_part = jnp.einsum("bid,bjd->bij", grad_context, memory_wide, precision=highest)
    grad_memory = jnp.einsum(
        "bij,bid->bjd", beta_low.astype(jnp.float32), grad_context, precision=highest
    )
    grad_beta = lax.psum(grad_beta_part, ("section", "mp"))
    grad_mono_energy, grad_span_energy = attention_pullback(grad_beta)
    mono_gq, mono_gk, grad_mono_bias, grad_mono_vec = energy_backward(
        grad_mono_energy, mono_query, mono_keys, mono_bias, mono_vec
    )
    span_gq, span_gk, grad_span_bias, grad_span_vec = energy_backward(
        grad_span_energy, span_query, span_keys, span_bias, span_vec
    )
    mono_gq_low = mono_gq.astype(jnp.bfloat16)
    mono_gk_low = mono_gk.astype(jnp.bfloat16)
    span_gq_low = span_gq.astype(jnp.bfloat16)
    span_gk_low = span_gk.astype(jnp.bfloat16)
    grad_mono_mem = jnp.einsum(
        "bjd,bje->de", memory, mono_gk_low, preferred_element_type=jnp.float32
    )
    grad_mono_dec = jnp.einsum(
        "bid,bie->de", decoded, mono_gq_low, preferred_element_type=jnp.float32
    )
    grad_span_mem = jnp.einsum(
        "bjd,bje->de", memory, span_gk_low, preferred_element_type=jnp.float32
    )
    grad_span_dec = jnp.einsum(
        "bid,bie->de", decoded, span_gq_low, preferred_element_type=jnp.float32
    )
    grad_memory = (
        grad_memory
        + jnp.einsum("bje,de->bjd", mono_gk_low, mono_mem_all, preferred_element_type=jnp.float32)
        + jnp.einsum("bje,de->bjd", span_gk_low, span_mem_all, preferred_element_type=jnp.float32)
    )
    grad_decoded = (
        grad_decoded
        + jnp.einsum("bie,de->bid", mono_gq_low, mono_dec_all, preferred_element_type=jnp.float32)
        + jnp.einsum("bie,de->bid", span_gq_low, span_dec_all, preferred_element_type=jnp.float32)
    )
    grad_own = lax.psum_scatter(
        jnp.concatenate([grad_memory, grad_decoded], axis=2),
        ("section", "mp"),
        scatter_dimension=2,
        tiled=True,
    )
    grad_own = jnp.swapaxes(grad_own, 0, 1)

    def reduce_units(partial_grad):
        return lax.psum_scatter(partial_grad, "mp", scatter_dimension=1, tiled=True)

    own_gates = backward_scan(
        grad_own, gate_seq, cell_before, cell_after, weight_recur, reduce_units
    )
    grad_normed = lax.psum(
        jnp.einsum("lbgh,dgh->bld", own_gates, weight_input, preferred_element_type=jnp.float32),
        "mp",
    )
    grad_input_weight = jnp.einsum(
        "bld,lbgh->dgh", normed_low, own_gates, preferred_element_type=jnp.float32
    )
    grad_recur_weight = jnp.einsum(
        "lbd,lbgh->dgh", hidden_prev, own_gates, preferred_element_type=jnp.float32
    )
    grad_lstm_bias = jnp.sum(own_gates.astype(jnp.float32), axis=(0, 1))
    grad_inputs, grad_gain = norm_pullback(grad_normed)
    (
        grad_input_weight,
        grad_recur_weight,
        grad_mono_mem,
        grad_mono_dec,
        grad_span_mem,
        grad_span_dec,
        grad_out,
    ) = (
        lax.psum_scatter(grad_input_weight, "dp", scatter_dimension=0, tiled=True),
        lax.psum_scatter(grad_recur_weight, "dp", scatter_dimension=0, tiled=True),
        lax.psum_scatter(grad_mono_mem, "dp", scatter_dimension=0, tiled=True),
        lax.psum_scatter(grad_mono_dec, "dp", scatter_dimension=0, tiled=True),
        lax.psum_scatter(grad_span_mem, "dp", scatter_dimension=0, tiled=True),
        lax.psum_scatter(grad_span_dec, "dp", scatter_dimension=0, tiled=True),
        lax.psum_scatter(grad_out, "dp", scatter_dimension=1, tiled=True),
    )
    (
        grad_gain,
        grad_lstm_bias,
        grad_mono_bias,
        grad_mono_vec,
        grad_span_bias,
        grad_span_vec,
        grad_out_bias,
        grad_vocab_weight,
        grad_vocab_bias,
    ) = lax.psum(
        (
            grad_gain,
            grad_lstm_bias,
            grad_mono_bias,
            grad_mono_vec,
            grad_span_bias,
            grad_span_vec,
            grad_out_bias,
            grad_vocab_weight,
            grad_vocab_bias,
        ),
        "dp",
    )
    return (
        grad_inputs[None],
        grad_gain[None],
        grad_input_weight[None],
        grad_recur_weight[None],
        grad_lstm_bias[None],
        grad_mono_mem,
        grad_mono_dec,
        grad_mono_bias,
        grad_mono_vec,
        grad_span_mem,
        grad_span_dec,
        grad_span_bias,
        grad_span_vec,
        grad_out,
        grad_out_bias,
        grad_vocab_weight,
        grad_vocab_bias,
    )


def solution(mesh):
    in_specs = (
        P("section", "dp", None, None),
        P("section", None),
        P("section", "dp", None, "mp"),
        P("section", "dp", None, "mp"),
        P("section", None, "mp"),
        P("dp", ("section", "mp")),
        P("dp", ("section", "mp")),
        P(("section", "mp")),
        P(("section", "mp")),
        P("dp", ("section", "mp")),
        P("dp", ("section", "mp")),
        P(("section", "mp")),
        P(("section", "mp")),
        P(None, "dp", ("section", "mp")),
        P(("section", "mp")),
        P(("section", "mp"), None),
        P(),
        P("dp", None, None),
        P("dp"),
        P("dp"),
        P("dp", None),
    )
    out_specs = (
        P("section", "dp", None, None),
        P("section", None),
        P("section", "dp", None, "mp"),
        P("section", "dp", None, "mp"),
        P("section", None, "mp"),
        P("dp", ("section", "mp")),
        P("dp", ("section", "mp")),
        P(("section", "mp")),
        P(("section", "mp")),
        P("dp", ("section", "mp")),
        P("dp", ("section", "mp")),
        P(("section", "mp")),
        P(("section", "mp")),
        P(None, "dp", ("section", "mp")),
        P(("section", "mp")),
        P(("section", "mp"), None),
        P(),
    )
    return jax.shard_map(local, mesh=mesh, in_specs=in_specs, out_specs=out_specs, check_vma=False)
```

profile of v0, /device:TPU:0, one launch (start us, length us, event | category | flops | bytes accessed | tf_op | source)
XLA Modules:
  0.0 2208.9 jit_solution(728719965784224133)
XLA Ops:
  15.1 71.8 %all-gather.11.cloned.1.call-done = bf16[1,1024,4,512]{3,1,2,0:T(8,128)(2,1)} async-done(((bf16[1,128,4,512]{3,1,2,0:T(8,128)(2,1)}), bf16[1,1024,4,512]{3,1,2,0:T(8,128)(2,1)}) %all-gather.11.cloned.1.call-update) | async-done | bytes 4194320 | tf_op jit(solution)/shard_map/all_gather | solution.py:192
  86.9 6.7 fusion.102
  93.7 67.7 %all-gather.13.cloned.1.call-done = bf16[1,1024,4,512]{3,1,2,0:T(8,128)(2,1)} async-done(((bf16[1,128,4,512]{3,1,2,0:T(8,128)(2,1)}), bf16[1,1024,4,512]{3,1,2,0:T(8,128)(2,1)}) %all-gather.13.cloned.1.call-update) | async-done | bytes 4194320 | tf_op jit(solution)/shard_map/all_gather | solution.py:193
  161.4 185.1 %while.160 = (s32[]{:T(128)}, bf16[32,512]{1,0:T(8,128)(2,1)S(1)}, f32[32,512]{1,0:T(8,128)S(1)}, bf16[16,32,512]{2,1,0:T(8,128)(2,1)S(1)}, bf16[16,32,1024]{2,1...) while((s32[]{:T(128)}, bf16[32,512]{1,0:T(8,128)(2,1)S(1)}, ...), condition=%wide.region_3.4_spmd.clone.clone, body=%wide.region_2.3_spmd.clone.sunk.clone | while | flops 134610944 | bytes 6530688 | solution.py:97
  161.4 4.7 all_gather.38
  173.1 4.6 all_gather.38
  184.6 4.6 all_gather.38
  196.2 4.6 all_gather.38
  207.7 4.6 all_gather.38
  219.2 4.6 all_gather.38
  230.8 4.6 all_gather.38
  242.3 4.9 all_gather.38
  254.2 4.6 all_gather.38
  265.7 4.6 all_gather.38
  277.3 4.6 all_gather.38
  288.8 4.6 all_gather.38
  300.3 4.6 all_gather.38
  311.9 4.6 all_gather.38
  323.4 4.6 all_gather.38
  335.0 4.6 all_gather.38
  348.9 31.6 %all_gather.33 = bf16[1024,256]{1,0:T(8,128)(2,1)S(1)} all-gather(bf16[128,256]{1,0:T(8,128)(2,1)S(1)} %copy-done.44), channel_id=1, replica_groups=mesh['section'=2,'dp'=8,'mp'=2] {'dp'}, dimensions={0}, use_global_device_ids=true | all-gather | bytes 589824 | tf_op jit(solution)/shard_map/all_gather | solution.py:196
  380.5 32.2 %all_gather.32 = bf16[1024,256]{1,0:T(8,128)(2,1)S(1)} all-gather(bf16[128,256]{1,0:T(8,128)(2,1)S(1)} %copy-done.45), channel_id=1, replica_groups=mesh['section'=2,'dp'=8,'mp'=2] {'dp'}, dimensions={0}, use_global_device_ids=true | all-gather | bytes 589824 | tf_op jit(solution)/shard_map/all_gather | solution.py:197
  412.7 33.5 %all_gather.31 = bf16[1024,256]{1,0:T(8,128)(2,1)} all-gather(bf16[128,256]{1,0:T(8,128)(2,1)S(1)} %copy-done.46), channel_id=1, replica_groups=mesh['section'=2,'dp'=8,'mp'=2] {'dp'}, dimensions={0}, use_global_device_ids=true | all-gather | bytes 589824 | tf_op jit(solution)/shard_map/all_gather | solution.py:194
  446.3 31.2 %all_gather.30 = bf16[1024,256]{1,0:T(8,128)(2,1)S(1)} all-gather(bf16[128,256]{1,0:T(8,128)(2,1)S(1)} %copy-done.47), channel_id=1, replica_groups=mesh['section'=2,'dp'=8,'mp'=2] {'dp'}, dimensions={0}, use_global_device_ids=true | all-gather | bytes 589824 | tf_op jit(solution)/shard_map/all_gather | solution.py:195
  483.6 90.0 %while.156 = (s32[]{:T(128)}, f32[32,16,16]{2,1,0:T(8,128)}, f32[32,16,16]{2,1,0:T(8,128)}, f32[32,16,256]{2,1,0:T(8,128)S(1)}, f32[32,16,256]{2,1,0:T(8,128)S(1...) while((s32[]{:T(128)}, f32[32,16,16]{2,1,0:T(8,128)}, ...), condition=%wide.region_7.8_spmd.clone, body=%wide.region_4.7_spmd.sunk.clone | while | flops 523778 | bytes 222333 | solution.py:147
  576.8 27.7 %all-reduce.54.cloned.1.call-done = (f32[32,16,16]{2,1,0:T(8,128)}, f32[32,16,16]{2,1,0:T(8,128)}) async-done(((f32[32,16,16]{2,1,0:T(8,128)}, f32[32,16,16]{2,1,0:T(8,128)}), (f32[32,16,16]{2,1,0:T(8,128)}, f32[32,16,16]{2,1,0:T(8,128)})) %all-reduce.54.cloned.1.call-update) | async-done | bytes 65552 | tf_op jit(solution)/shard_map/psum | solution.py:228
  608.5 102.4 %while.157 = (s32[]{:T(128)}, f32[32,16]{0,1:T(8,128)S(1)}, f32[16,32,16]{1,2,0:T(8,128)S(1)}, f32[16,32,8]{1,2,0:T(8,128)}, f32[16,32,8]{1,2,0:T(8,128)}, /*ind...) while((s32[]{:T(128)}, f32[32,16]{0,1:T(8,128)S(1)}, ...), condition=%wide.region_12.13_spmd.clone, body=%wide.region_11.12_spmd.sunk.clone | while | flops 4034 | bytes 159597 | solution.py:52
  718.2 49.9 %all-reduce.48.cloned.1.call-done = f32[32,16,1000]{2,1,0:T(8,128)} async-done(((f32[32,16,1000]{2,1,0:T(8,128)}), f32[32,16,1000]{2,1,0:T(8,128)}) %all-reduce.48.cloned.1.call-update) | async-done | bytes 2048016 | tf_op jit(solution)/shard_map/psum | solution.py:251
  768.1 4.4 convert_reduce_fusion.2
  780.0 17.9 psum.101
  801.8 139.8 %while.161 = (s32[]{:T(128)}, f32[32,16]{0,1:T(8,128)S(1)}, f32[16,32,16]{1,2,0:T(8,128)S(1)}, f32[16,32,16]{1,2,0:T(8,128)S(1)}, f32[16,32,16]{1,2,0:T(8,128)},...) while((s32[]{:T(128)}, f32[32,16]{0,1:T(8,128)S(1)}, ...), condition=%wide.region_18.19_spmd.clone.clone, body=%wide.region_17.18_spmd.clone.sunk.clone | while | flops 12036 | bytes 163430 | solution.py:52
  947.8 50.0 %while.159 = (s32[]{:T(128)}, f32[32,16,256]{2,1,0:T(8,128)S(1)}, bf16[32,16,256]{2,1,0:T(8,128)(2,1)}, f32[32,256]{1,0:T(8,128)S(1)}, f32[32,16,16]{2,1,0:T(8,1...) while((s32[]{:T(128)}, f32[32,16,256]{2,1,0:T(8,128)S(1)}, ...), condition=%wide.region_30.31_spmd.clone, body=%wide.region_26.30_spmd.sunk.clone | while | flops 646914 | bytes 180845 | solution.py:162
  998.0 54.3 %while.158 = (s32[]{:T(128)}, f32[32,16,256]{2,1,0:T(8,128)S(1)}, bf16[32,16,256]{2,1,0:T(8,128)(2,1)S(1)}, f32[32,256]{1,0:T(8,128)S(1)}, f32[32,16,16]{2,1,0:T...) while((s32[]{:T(128)}, f32[32,16,256]{2,1,0:T(8,128)S(1)}, ...), condition=%wide.region_23.24_spmd.clone, body=%wide.region_19.23_spmd.sunk.clone | while | flops 646914 | bytes 180337 | solution.py:162
  1061.1 45.2 %reduce-scatter.10.cloned.1.call-done = f32[32,16,512]{2,1,0:T(8,128)} async-done(((f32[32,16,2048]{2,1,0:T(8,128)}), f32[32,16,512]{2,1,0:T(8,128)}) %reduce-scatter.10.cloned.1.call-update) | async-done | bytes 1048592 | tf_op jit(solution)/shard_map/reduce_scatter | solution.py:321
  1108.5 296.8 %while.162 = (s32[]{:T(128)}, f32[32,512]{1,0:T(8,128)}, f32[32,512]{1,0:T(8,128)S(1)}, bf16[16,32,4,512]{3,1,2,0:T(8,128)(2,1)}, f32[16,32,512]{2,0,1:T(8,128)}...) while((s32[]{:T(128)}, f32[32,512]{1,0:T(8,128)}, ...), condition=%wide.region_34.35_spmd.clone.clone, body=%wide.region_32.34_spmd.clone.sunk.clone | while | flops 135593984 | bytes 6946991 | solution.py:131
  1117.3 9.7 reduce-scatter.26.cloned.1.call-done
  1135.8 9.7 reduce-scatter.26.cloned.1.call-done
  1154.4 9.7 reduce-scatter.26.cloned.1.call-done
  1172.9 9.7 reduce-scatter.26.cloned.1.call-done
  1191.5 9.7 reduce-scatter.26.cloned.1.call-done
  1210.0 9.7 reduce-scatter.26.cloned.1.call-done
  1228.6 9.7 reduce-scatter.26.cloned.1.call-done
  1247.1 9.7 reduce-scatter.26.cloned.1.call-done
  1265.7 9.7 reduce-scatter.26.cloned.1.call-done
  1284.2 9.7 reduce-scatter.26.cloned.1.call-done
  1302.8 9.7 reduce-scatter.26.cloned.1.call-done
  1321.3 9.7 reduce-scatter.26.cloned.1.call-done
  1339.9 9.7 reduce-scatter.26.cloned.1.call-done
  1358.4 9.7 reduce-scatter.26.cloned.1.call-done
  1376.9 9.7 reduce-scatter.26.cloned.1.call-done
  1395.5 9.7 reduce-scatter.26.cloned.1.call-done
  1405.2 6.5 fusion.117
  1411.9 7.8 convolution_bitcast_fusion.1
  1420.4 7.9 convolution_bitcast_fusion.2
  1449.5 25.4 %all-reduce.50.cloned.1.call-done = f32[32,16,1024]{2,0,1:T(8,128)} async-done(((f32[32,16,1024]{2,0,1:T(8,128)}), f32[32,16,1024]{2,0,1:T(8,128)}) %all-reduce.50.cloned.1.call-update) | async-done | bytes 2097168 | tf_op jit(solution)/shard_map/psum | solution.py:335
  1482.9 40.2 %all-reduce.41 = (f32[1,1024]{1,0:T(1,128)}, f32[1,4,512]{2,1,0:T(4,128)}, f32[256]{0:T(256)}, f32[256]{0:T(256)}, f32[256]{0:T(256)}, /*index=5*/f32[256]{0:T(256)}, f32[256]{0:T(256)}, f32[1000]{0:T(1024)}) all-reduce(f32[1,1024]{1,0:T(1,128)S(1)} %bitcast.683, ...), channel_id=1, replica_groups=mesh['section'=2,'dp'=8,'mp'=2] {'dp'}, use_global_device_ids=true, to_apply=%region_39.40 | all-reduce | flops 5352 | bytes 42816 | tf_op jit(solution)/shard_map/psum | solution.py:374
  1523.1 105.8 %reduce-scatter.14.cloned.1.call-done = f32[128,4,512]{2,0,1:T(8,128)} async-done(((f32[1024,4,512]{2,0,1:T(8,128)}), f32[128,4,512]{2,0,1:T(8,128)}) %reduce-scatter.14.cloned.1.call-update) | async-done | bytes 1048592 | tf_op jit(solution)/shard_map/reduce_scatter | solution.py:357
  1631.8 149.0 %reduce-scatter.12.cloned.1.call-done = f32[128,4,512]{2,0,1:T(8,128)} async-done(((f32[1024,4,512]{2,0,1:T(8,128)}), f32[128,4,512]{2,0,1:T(8,128)}) %reduce-scatter.12.cloned.1.call-update) | async-done | bytes 1048592 | tf_op jit(solution)/shard_map/reduce_scatter | solution.py:356
  1783.7 78.2 %all-reduce.52.cloned.1.call-done = f32[256,1000]{0,1:T(8,128)} async-done(((f32[256,1000]{0,1:T(8,128)}), f32[256,1000]{0,1:T(8,128)}) %all-reduce.52.cloned.1.call-update) | async-done | bytes 1024016 | tf_op jit(solution)/shard_map/psum | solution.py:374
  1861.9 66.7 %reduce-scatter.20.cloned.1.call-done = f32[128,256]{1,0:T(8,128)} async-done(((f32[1024,256]{1,0:T(8,128)}), f32[128,256]{1,0:T(8,128)}) %reduce-scatter.20.cloned.1.call-update) | async-done | bytes 131088 | tf_op jit(solution)/shard_map/reduce_scatter | solution.py:360
  1928.6 66.5 %reduce-scatter.22.cloned.1.call-done = f32[128,256]{1,0:T(8,128)} async-done(((f32[1024,256]{1,0:T(8,128)}), f32[128,256]{1,0:T(8,128)}) %reduce-scatter.22.cloned.1.call-update) | async-done | bytes 131088 | tf_op jit(solution)/shard_map/reduce_scatter | solution.py:361
  1995.2 66.8 %reduce-scatter.16.cloned.1.call-done = f32[128,256]{1,0:T(8,128)} async-done(((f32[1024,256]{1,0:T(8,128)}), f32[128,256]{1,0:T(8,128)}) %reduce-scatter.16.cloned.1.call-update) | async-done | bytes 131088 | tf_op jit(solution)/shard_map/reduce_scatter | solution.py:358
  2061.9 66.5 %reduce-scatter.18.cloned.1.call-done = f32[128,256]{1,0:T(8,128)} async-done(((f32[1024,256]{1,0:T(8,128)}), f32[128,256]{1,0:T(8,128)}) %reduce-scatter.18.cloned.1.call-update) | async-done | bytes 131088 | tf_op jit(solution)/shard_map/reduce_scatter | solution.py:359
  2128.5 71.4 %reduce-scatter.24.cloned.1.call-done = f32[2,128,256]{2,1,0:T(8,128)} async-done(((f32[2,1024,256]{2,1,0:T(8,128)}), f32[2,128,256]{2,1,0:T(8,128)}) %reduce-scatter.24.cloned.1.call-update) | async-done | bytes 262160 | tf_op jit(solution)/shard_map/reduce_scatter | solution.py:362
  (2594 shorter events, 779.4 us)
Async XLA Ops:
  7.2 707.5 %copy-start = (bf16[256,1000]{0,1:T(8,128)(2,1)S(1)}, bf16[256,1000]{0,1:T(8,128)(2,1)}, u32[]{:S(2)}) copy-start(bf16[256,1000]{0,1:T(8,128)(2,1)} %param.50) | copy-start | bytes 1536004
  7.2 4.2 copy-start.2
  7.2 79.7 %all-gather.11.cloned.1.call-start = ((), (), s32[]{:S(2)}) async-start(), calls=%async_computation.22 | async-start | bytes 4718592 | tf_op jit(solution)/shard_map/all_gather | solution.py:192
  9.3 3.9 copy-start.54
  9.3 5.1 copy-start.48
  9.3 152.0 %all-gather.13.cloned.1.call-start = ((), (), s32[]{:S(2)}) async-start(), calls=%async_computation.23 | async-start | bytes 4718592 | tf_op jit(solution)/shard_map/all_gather | solution.py:193
  11.3 467.4 %all-gather.7.cloned.1.call-start = ((), (), s32[]{:S(2)}) async-start(), calls=%async_computation.9 | async-start | bytes 2621440 | tf_op jit(solution)/shard_map/all_gather | solution.py:213
  161.4 187.6 %copy-start.44 = (bf16[128,256]{1,0:T(8,128)(2,1)S(1)}, bf16[128,256]{1,0:T(8,128)(2,1)}, u32[]{:S(2)}) copy-start(bf16[128,256]{1,0:T(8,128)(2,1)} %param.44) | copy-start | bytes 196612
  346.5 34.0 %copy-start.45 = (bf16[128,256]{1,0:T(8,128)(2,1)S(1)}, bf16[128,256]{1,0:T(8,128)(2,1)}, u32[]{:S(2)}) copy-start(bf16[128,256]{1,0:T(8,128)(2,1)} %param.45) | copy-start | bytes 196612
  346.5 66.2 %copy-start.46 = (bf16[128,256]{1,0:T(8,128)(2,1)S(1)}, bf16[128,256]{1,0:T(8,128)(2,1)}, u32[]{:S(2)}) copy-start(bf16[128,256]{1,0:T(8,128)(2,1)} %param.40) | copy-start | bytes 196612
  346.5 99.8 %copy-start.47 = (bf16[128,256]{1,0:T(8,128)(2,1)S(1)}, bf16[128,256]{1,0:T(8,128)(2,1)}, u32[]{:S(2)}) copy-start(bf16[128,256]{1,0:T(8,128)(2,1)} %param.41) | copy-start | bytes 196612
  346.5 130.9 %copy-start.60 = (s32[32]{0:T(128)S(1)}, s32[32]{0:T(128)}, u32[]{:S(2)}) copy-start(s32[32]{0:T(128)} %param.53) | copy-start | bytes 388
  347.6 226.6 %all-gather.9.cloned.1.call-start = ((), (), s32[]{:S(2)}) async-start(), calls=%async_computation.10 | async-start | bytes 1179648 | tf_op jit(solution)/shard_map/all_gather | solution.py:198
  348.2 256.4 %all-reduce.54.cloned.1.call-start = ((), (), s32[]{:S(2)}) async-start(), calls=%async_computation.24 | async-start | bytes 1048576 | tf_op jit(solution)/shard_map/psum | solution.py:228
  380.5 100.9 %copy-start.15 = (bf16[1024,256]{1,0:T(8,128)(2,1)}, bf16[1024,256]{1,0:T(8,128)(2,1)S(1)}, u32[]{:S(2)}) copy-start(bf16[1024,256]{1,0:T(8,128)(2,1)S(1)} %all_gather.33) | copy-start | bytes 1572868
  412.7 69.9 %copy-start.13 = (bf16[1024,256]{1,0:T(8,128)(2,1)}, bf16[1024,256]{1,0:T(8,128)(2,1)S(1)}, u32[]{:S(2)}) copy-start(bf16[1024,256]{1,0:T(8,128)(2,1)S(1)} %all_gather.32) | copy-start | bytes 1572868
  477.4 5.7 copy-start.21
  477.5 129.3 %copy-start.34 = (f32[32,16]{1,0:T(8,128)}, f32[32,16]{1,0:T(8,128)S(1)}, u32[]{:S(2)}) copy-start(f32[32,16]{1,0:T(8,128)S(1)} %get-tuple-element.1771) | copy-start | bytes 6148
  478.8 2.6 copy-start.17
  478.8 3.9 copy-start.23
  573.6 33.2 %copy-start.50 = (f32[32,16,256]{2,1,0:T(8,128)}, f32[32,16,256]{2,1,0:T(8,128)S(1)}, u32[]{:S(2)}) copy-start(f32[32,16,256]{2,1,0:T(8,128)S(1)} %get-tuple-element.3210) | copy-start | bytes 1572868
  573.6 33.2 %copy-start.51 = (f32[32,16,256]{2,1,0:T(8,128)}, f32[32,16,256]{2,1,0:T(8,128)S(1)}, u32[]{:S(2)}) copy-start(f32[32,16,256]{2,1,0:T(8,128)S(1)} %get-tuple-element.3211) | copy-start | bytes 1572868
  573.6 194.4 %all-reduce.48.cloned.1.call-start = ((), (), s32[]{:S(2)}) async-start(), calls=%async_computation.11 | async-start | bytes 4194304 | tf_op jit(solution)/shard_map/psum | solution.py:251
  576.8 31.5 %copy-start.59 = (f32[16]{0:T(128)S(1)}, f32[16]{0:T(128)}, u32[]{:S(2)}) copy-start(f32[16]{0:T(128)} %compare_convert_fusion) | copy-start | bytes 196
  608.0 103.0 %copy-start.4 = (f32[32,16,16]{2,1,0:T(8,128)S(1)}, f32[32,16,16]{2,1,0:T(8,128)}, u32[]{:S(2)}) copy-start(f32[32,16,16]{2,1,0:T(8,128)} %get-tuple-element.1678) | copy-start | bytes 98308
  716.5 51.6 %copy-start.61 = (f32[1000]{0:T(1024)S(1)}, f32[1000]{0:T(1024)}, u32[]{:S(2)}) copy-start(f32[1000]{0:T(1024)} %param.51) | copy-start | bytes 12004
  716.5 389.8 %reduce-scatter.10.cloned.1.call-start = ((), (), s32[]{:S(2)}) async-start(), calls=%async_computation.12 | async-start | bytes 5242880 | tf_op jit(solution)/shard_map/reduce_scatter | solution.py:321
  772.5 3.1 copy-start.8
  780.0 21.8 copy-start.52
  801.8 143.4 %copy-start.35 = (f32[32,16]{1,0:T(8,128)S(1)}, f32[32,16]{1,0:T(8,128)}, u32[]{:S(2)}) copy-start(f32[32,16]{1,0:T(8,128)} %copy-done.34) | copy-start | bytes 6148
  947.5 50.4 %copy-start.12 = (bf16[32,16,256]{2,1,0:T(8,128)(2,1)S(1)}, bf16[32,16,256]{2,1,0:T(8,128)(2,1)}, u32[]{:S(2)}) copy-start(bf16[32,16,256]{2,1,0:T(8,128)(2,1)} %copy-done.11) | copy-start | bytes 786436
  947.5 50.4 %copy-start.67 = (f32[256]{0:T(256)S(1)}, f32[256]{0:T(256)}, u32[]{:S(2)}) copy-start(f32[256]{0:T(256)} %param.42) | copy-start | bytes 3076
  947.6 50.4 %copy-start.69 = (f32[256]{0:T(256)S(1)}, f32[256]{0:T(256)}, u32[]{:S(2)}) copy-start(f32[256]{0:T(256)} %param.43) | copy-start | bytes 3076
  997.8 56.1 %copy-start.38 = (f32[32,256]{1,0:T(8,128)}, f32[32,256]{1,0:T(8,128)S(1)}, u32[]{:S(2)}) copy-start(f32[32,256]{1,0:T(8,128)S(1)} %get-tuple-element.1047) | copy-start | bytes 98308
  1108.5 18.5 reduce-scatter.26.cloned.1.call-start
  1127.0 18.5 reduce-scatter.26.cloned.1.call-start
  1145.6 18.5 reduce-scatter.26.cloned.1.call-start
  1164.1 18.5 reduce-scatter.26.cloned.1.call-start
  1182.7 18.5 reduce-scatter.26.cloned.1.call-start
  1201.2 18.5 reduce-scatter.26.cloned.1.call-start
  1219.8 18.5 reduce-scatter.26.cloned.1.call-start
  1238.3 18.5 reduce-scatter.26.cloned.1.call-start
  1256.9 18.5 reduce-scatter.26.cloned.1.call-start
  1275.4 18.5 reduce-scatter.26.cloned.1.call-start
  1294.0 18.5 reduce-scatter.26.cloned.1.call-start
  1312.5 18.5 reduce-scatter.26.cloned.1.call-start
  1331.0 18.5 reduce-scatter.26.cloned.1.call-start
  1349.6 18.5 reduce-scatter.26.cloned.1.call-start
  1368.1 18.5 reduce-scatter.26.cloned.1.call-start
  1386.7 18.5 reduce-scatter.26.cloned.1.call-start
  1405.2 69.6 %all-reduce.50.cloned.1.call-start = ((), (), s32[]{:S(2)}) async-start(), calls=%async_computation.13 | async-start | bytes 4194304 | tf_op jit(solution)/shard_map/psum | solution.py:335
  1411.8 217.1 %reduce-scatter.14.cloned.1.call-start = ((), (), s32[]{:S(2)}) async-start(), calls=%async_computation.15 | async-start | bytes 9437184 | tf_op jit(solution)/shard_map/reduce_scatter | solution.py:357
  1419.7 361.1 %reduce-scatter.12.cloned.1.call-start = ((), (), s32[]{:S(2)}) async-start(), calls=%async_computation.14 | async-start | bytes 9437184 | tf_op jit(solution)/shard_map/reduce_scatter | solution.py:356
  1428.3 2.9 copy-start.25
  1428.3 433.6 %all-reduce.52.cloned.1.call-start = ((), (), s32[]{:S(2)}) async-start(), calls=%async_computation.21 | async-start | bytes 2048000 | tf_op jit(solution)/shard_map/psum | solution.py:374
  1431.1 497.5 %reduce-scatter.20.cloned.1.call-start = ((), (), s32[]{:S(2)}) async-start(), calls=%async_computation.18 | async-start | bytes 1179648 | tf_op jit(solution)/shard_map/reduce_scatter | solution.py:360
  1434.0 561.2 %reduce-scatter.22.cloned.1.call-start = ((), (), s32[]{:S(2)}) async-start(), calls=%async_computation.19 | async-start | bytes 1179648 | tf_op jit(solution)/shard_map/reduce_scatter | solution.py:361
  1436.8 625.2 %reduce-scatter.16.cloned.1.call-start = ((), (), s32[]{:S(2)}) async-start(), calls=%async_computation.16 | async-start | bytes 1179648 | tf_op jit(solution)/shard_map/reduce_scatter | solution.py:358
  1439.6 3.1 copy-start.28
  1439.6 688.8 %reduce-scatter.18.cloned.1.call-start = ((), (), s32[]{:S(2)}) async-start(), calls=%async_computation.17 | async-start | bytes 1179648 | tf_op jit(solution)/shard_map/reduce_scatter | solution.py:359
  1442.4 757.5 %reduce-scatter.24.cloned.1.call-start = ((), (), s32[]{:S(2)}) async-start(), calls=%async_computation.20 | async-start | bytes 2359296 | tf_op jit(solution)/shard_map/reduce_scatter | solution.py:362
  1449.5 28.2 %copy-start.43 = (f32[32,16]{0,1:T(8,128)S(1)}, f32[32,16]{0,1:T(8,128)}, u32[]{:S(2)}) copy-start(f32[32,16]{0,1:T(8,128)} %copy-done.42) | copy-start | bytes 6148
  1474.9 2.9 copy-start.3
  1628.9 573.2 %copy-start.1 = (bf16[256,1000]{0,1:T(8,128)(2,1)S(1)}, bf16[256,1000]{0,1:T(8,128)(2,1)}, u32[]{:S(2)}) copy-start(bf16[256,1000]{0,1:T(8,128)(2,1)} %param.50) | copy-start | bytes 1536004
  (38 other events, 55.9 us)
Sparse Core Ops, SparseCore 0:
  10.8 76.0 all-gather.10
  89.7 71.6 all-gather.12
  347.7 20.6 all-gather.6
  370.4 43.0 all-gather.8
  573.8 30.7 all-reduce.53
  716.6 51.3 all-reduce.47
  1061.2 45.0 reduce-scatter.9
  1116.7 10.2 reduce-scatter.25
  1135.3 10.2 reduce-scatter.25
  1153.8 10.2 reduce-scatter.25
  1172.4 10.2 reduce-scatter.25
  1190.9 10.2 reduce-scatter.25
  1209.5 10.2 reduce-scatter.25
  1228.0 10.2 reduce-scatter.25
  1246.6 10.2 reduce-scatter.25
  1265.1 10.2 reduce-scatter.25
  1283.7 10.2 reduce-scatter.25
  1302.2 10.2 reduce-scatter.25
  1320.8 10.2 reduce-scatter.25
  1339.3 10.2 reduce-scatter.25
  1357.8 10.2 reduce-scatter.25
  1376.4 10.2 reduce-scatter.25
  1394.9 10.2 reduce-scatter.25
  1411.9 62.9 all-reduce.49
  1479.0 149.8 reduce-scatter.13
  1632.4 148.3 reduce-scatter.11
  1785.1 76.7 all-reduce.51
  1866.3 62.3 reduce-scatter.19
  1932.6 62.4 reduce-scatter.21
  1999.4 62.5 reduce-scatter.15
  2065.9 62.5 reduce-scatter.17
  2133.0 66.8 reduce-scatter.23
where the time goes:
time: 2250 us; the launch traced here: 2210 us
  waiting for transfers between devices  1120 us (50%)
  local copies, waits for them, and re-layouts  385 us (17%)
  blocking collectives  260 us (12%)
  other arithmetic  233 us (10%)
  matrix products  192 us (9%)
    reduce_scatter x16, waiting for transfers between devices, reduce_units(): return lax.psum_scatter(partial_grad, 'mp', scatter_dimension=1, tiled=True)  156 us
    reduce_scatter x1, waiting for transfers between devices, local(): lax.psum_scatter(grad_input_weight, 'dp', scatter_dimension=0, tiled=True)  149 us
    reduce_scatter x1, waiting for transfers between devices, local(): lax.psum_scatter(grad_recur_weight, 'dp', scatter_dimension=0, tiled=True)  106 us
    dynamic_update_slice x160, local copies, waits for them, and re-layouts, monotonic(): lax.scan(monotonic_advance, initial, (jnp.swapaxes(keep_prob, 0, 1), jnp....  93.1 us
    psum x1, waiting for transfers between devices, local(): lax.psum((grad_gain, grad_lstm_bias, grad_mono_bias, grad_mono_vec, grad_...  78.2 us
    all_gather x16, blocking collectives, fetch_units(): return lax.all_gather(own_hidden, 'mp', axis=1, tiled=True)  73.7 us
    all_gather x1, waiting for transfers between devices, local(): lax.all_gather(lstm_in[0], 'dp', axis=0, tiled=True)  71.8 us
    reduce_scatter x1, waiting for transfers between devices, local(): lax.psum_scatter(grad_out, 'dp', scatter_dimension=1, tiled=True)  71.4 us
  transfers between devices with their start and end apart: 32, of which 30 were waited for; matrix products, arithmetic and copies ran while one was open for 8% of the time, Pallas kernels for 0%

commit v1 on v0

v1 whole, which is shorter than its diff:
```python
import jax
import jax.numpy as jnp
from jax import lax
from jax.experimental import pallas as pl
from jax.experimental.pallas import tpu as pltpu
from jax.sharding import PartitionSpec as P

epsilon = 1e-05
offset = -4.0
wide = jnp.float32
low = jnp.bfloat16
in_vmem = pl.BlockSpec(memory_space=pltpu.VMEM)
in_smem = pl.BlockSpec(memory_space=pltpu.SMEM)
in_place = pl.BlockSpec(memory_space=pl.ANY)
core_swap = [(0, 1), (1, 0)]
corner_swap = [(0, 0), (1, 2), (2, 1), (3, 3)]


def normalize(inputs, gain_row):
    average = jnp.mean(inputs, axis=-1, keepdims=True)
    centred = inputs - average
    spread = jnp.mean(centred * centred, axis=-1, keepdims=True)
    return centred * lax.rsqrt(spread + epsilon) * gain_row


def across_cores(array):
    return lax.ppermute(array, "section", core_swap)


def across_chips(array):
    return lax.ppermute(array, "mp", core_swap)


def corners(array):
    return lax.ppermute(array, ("section", "mp"), corner_swap)


class Ring:
    def __init__(self, dp):
        self.dp = dp
        self.outer = dp // 2
        self.small = dp % 2 == 0 and self.outer <= 4
        pairs = [(z, x) for z in range(self.outer) for x in range(2)]
        self.pair = [(2 * z + x, 2 * z + 1 - x) for z, x in pairs]
        self.ring = [(2 * z + x, 2 * ((z + 1) % self.outer) + x) for z, x in pairs]

    def gather(self, shards):
        if not self.small:
            return [lax.all_gather(a, "dp", axis=0, tiled=True) for a in shards]
        place = lax.axis_index("dp")
        z, x = place // 2, place % 2
        held = list(shards)
        got = [[] for _ in shards]
        for k in range(self.outer):
            for i in range(len(shards)):
                got[i].append((k, held[i], lax.ppermute(held[i], "dp", self.pair)))
                if k < self.outer - 1:
                    held[i] = lax.ppermute(held[i], "dp", self.ring)
        whole = []
        for i, shard in enumerate(shards):
            r, c = shard.shape
            full = jnp.zeros((self.dp * r, c), shard.dtype)
            for k, own, other in got[i]:
                at = lax.rem(z - k + self.outer, self.outer)
                full = lax.dynamic_update_slice(full, own, ((at * 2 + x) * r, 0))
                full = lax.dynamic_update_slice(full, other, ((at * 2 + 1 - x) * r, 0))
            whole.append(full)
        return whole

    def scatter(self, totals):
        if not self.small:
            return [
                lax.psum_scatter(g, "dp", scatter_dimension=0, tiled=True).astype(wide)
                for g in totals
            ]
        place = lax.axis_index("dp")
        z, x = place // 2, place % 2
        sums = [None] * len(totals)
        for j in range(1, self.outer + 1):
            for i, g in enumerate(totals):
                r = g.shape[0] // self.dp
                at = lax.rem(z - j + self.outer, self.outer)
                mine = lax.dynamic_slice(g, ((at * 2 + x) * r, 0), (r, g.shape[1]))
                theirs = lax.dynamic_slice(g, ((at * 2 + 1 - x) * r, 0), (r, g.shape[1]))
                total = mine.astype(wide) + lax.ppermute(theirs, "dp", self.pair).astype(wide)
                if sums[i] is not None:
                    total = total + lax.ppermute(sums[i], "dp", self.ring).astype(wide)
                sums[i] = total.astype(low) if j < self.outer else total
        return sums

    def total(self, array):
        if not self.small:
            return lax.psum(array, "dp")
        array = array + lax.ppermute(array, "dp", self.pair)
        step = 1
        while step < self.outer:
            hop = [
                (2 * z + x, 2 * (z ^ step) + x) for z in range(self.outer) for x in range(2)
            ]
            array = array + lax.ppermute(array, "dp", hop)
            step *= 2
        return array


def sigmoid(x):
    return 0.5 * jnp.tanh(0.5 * x) + 0.5


def forward_kernel(
    side, z_own, z_other, w_own, w_other, b_own, b_other,
    quarters, before, gates, cells,
    z, w, b, state, cell, sems,
):
    steps, rows, wide_half = z_own.shape
    unit_half = wide_half // 4
    chunk = min(256, unit_half)
    s = side[0]
    copies = []
    for n, (src_z, src_w, src_b, at) in enumerate(
        ((z_own, w_own, b_own, s), (z_other, w_other, b_other, 1 - s))
    ):
        columns = pl.ds(pl.multiple_of(at * wide_half, wide_half), wide_half)
        copies.append(pltpu.make_async_copy(src_w, w.at[:, columns], sems.at[n]))
        copies.append(pltpu.make_async_copy(src_z, z.at[:, :, columns], sems.at[2 + n]))
        b[:, columns] = src_b[...]
    for copy in copies:
        copy.start()
    state[...] = jnp.zeros_like(state)
    cell[...] = jnp.zeros_like(cell)
    for copy in copies:
        copy.wait()
    eighth = rows // 2

    def advance(t, carried):
        hidden = state[...]
        before[t] = hidden
        for at in range(0, 2 * unit_half, chunk):
            half, inside = at // unit_half, at % unit_half
            acts = []
            for g in range(4):
                cols = pl.ds(half * wide_half + g * unit_half + inside, chunk)
                value = (
                    z[t, :, cols]
                    + jnp.dot(hidden, w[:, cols], preferred_element_type=wide)
                    + b[:, cols]
                )
                value = jnp.tanh(value) if g == 2 else sigmoid(value)
                gates[t, :, cols] = value
                acts.append(value)
            units = pl.ds(at, chunk)
            new_cell = acts[1] * cell[:, units] + acts[0] * acts[2]
            cell[:, units] = new_cell
            cells[t, :, units] = new_cell
            new_hidden = acts[3] * jnp.tanh(new_cell)
            state[:, units] = new_hidden.astype(low)
            quarters[0, t, :, units] = new_hidden[:eighth].astype(low)
            quarters[1, t, :, units] = new_hidden[eighth:].astype(low)
        return carried

    lax.fori_loop(0, steps, advance, 0)


def run_forward(side, z_own, z_other, w_own, w_other, b_own, b_other):
    steps, rows, wide_half = z_own.shape
    units = w_own.shape[0]
    return pl.pallas_call(
        forward_kernel,
        out_shape=(
            jax.ShapeDtypeStruct((2, steps, rows // 2, units), low),
            jax.ShapeDtypeStruct((steps, rows, units), low),
            jax.ShapeDtypeStruct((steps, rows, 2 * wide_half), wide),
            jax.ShapeDtypeStruct((steps, rows, units), wide),
        ),
        in_specs=[in_smem] + [in_place] * 4 + [in_vmem] * 2,
        out_specs=[in_vmem] * 4,
        scratch_shapes=[
            pltpu.VMEM((steps, rows, 2 * wide_half), wide),
            pltpu.VMEM((units, 2 * wide_half), low),
            pltpu.VMEM((1, 2 * wide_half), wide),
            pltpu.VMEM((rows, units), low),
            pltpu.VMEM((rows, units), wide),
            pltpu.SemaphoreType.DMA((4,)),
        ],
        compiler_params=pltpu.CompilerParams(vmem_limit_bytes=56 << 20),
        name="recur_forward",
    )(side, z_own, z_other, w_own, w_other, b_own, b_other)


def backward_kernel(side, outside, gates, cells, t_own, t_other, dz, w, dh, dc, sems):
    steps, rows, wide_full = gates.shape
    wide_half = wide_full // 2
    unit_half = wide_half // 4
    chunk = min(256, unit_half)
    eighth = rows // 2
    s = side[0]
    copies = []
    for n, (src, at) in enumerate(((t_own, s), (t_other, 1 - s))):
        span = pl.ds(pl.multiple_of(at * wide_half, wide_half), wide_half)
        copies.append(pltpu.make_async_copy(src, w.at[span, :], sems.at[n]))
    for copy in copies:
        copy.start()
    dh[...] = jnp.zeros_like(dh)
    dc[...] = jnp.zeros_like(dc)
    for copy in copies:
        copy.wait()

    def retreat(k, carried):
        t = steps - 1 - k
        earlier = jnp.maximum(t - 1, 0)
        live = jnp.where(t > 0, 1.0, 0.0).astype(wide)
        for at in range(0, 2 * unit_half, chunk):
            half, inside = at // unit_half, at % unit_half
            units = pl.ds(at, chunk)
            grad = (
                jnp.concatenate([outside[0, t, :, units], outside[1, t, :, units]], axis=0)
                + dh[:, units]
            )
            i, f, g, o = [
                gates[t, :, pl.ds(half * wide_half + n * unit_half + inside, chunk)]
                for n in range(4)
            ]
            squash = jnp.tanh(cells[t, :, units])
            total = dc[:, units] + grad * o * (1.0 - squash * squash)
            parts = (
                total * g * i * (1.0 - i),
                total * (cells[earlier, :, units] * live) * f * (1.0 - f),
                total * i * (1.0 - g * g),
                grad * squash * o * (1.0 - o),
            )
            for n, part in enumerate(parts):
                dz[half, t, :, pl.ds(n * unit_half + inside, chunk)] = part.astype(low)
            dc[:, units] = total * f
        first, second = dz[0, t], dz[1, t]
        for at in range(0, 2 * unit_half, chunk):
            units = pl.ds(at, chunk)
            dh[:, units] = jnp.dot(
                first, w[:wide_half, units], preferred_element_type=wide
            ) + jnp.dot(second, w[wide_half:, units], preferred_element_type=wide)
        return carried

    lax.fori_loop(0, steps, retreat, 0)


def run_backward(side, outside, gates, cells, t_own, t_other):
    steps, rows, wide_full = gates.shape
    units = cells.shape[2]
    return pl.pallas_call(
        backward_kernel,
        out_shape=jax.ShapeDtypeStruct((2, steps, rows, wide_full // 2), low),
        in_specs=[in_smem] + [in_vmem] * 3 + [in_place] * 2,
        out_specs=in_vmem,
        scratch_shapes=[
            pltpu.VMEM((wide_full, units), low),
            pltpu.VMEM((rows, units), wide),
            pltpu.VMEM((rows, units), wide),
            pltpu.SemaphoreType.DMA((2,)),
        ],
        compiler_params=pltpu.CompilerParams(vmem_limit_bytes=56 << 20),
        name="recur_backward",
    )(side, outside, gates, cells, t_own, t_other)


def dot_nt(a, b):
    return lax.dot_general(a, b, (((1,), (1,)), ((), ())), preferred_element_type=wide)


def dot_tn(a, b):
    return lax.dot_general(a, b, (((0,), (0,)), ((), ())), preferred_element_type=wide)


def attend_kernel(
    memory, decoded, w0, w1, w2, w3, v0, v1, v2, v3, vectors, vocab_bias, noise, lengths,
    labels, counted,
    grad_memory, grad_decoded, pack, seen, sums,
    w, v, sems, mk, sk, mq, sq, mono, span, keep, queue, scaled, ratio, window, mix, pre,
):
    rows, _ = memory.shape
    frames, group, _ = mk.shape
    block = w.shape[2] // 6
    lanes = 128
    chunks = 4 * block // lanes
    copies = [pltpu.make_async_copy(src, w.at[r], sems.at[r]) for r, src in enumerate((w0, w1, w2, w3))]
    copies += [
        pltpu.make_async_copy(src, v.at[r], sems.at[4 + r]) for r, src in enumerate((v0, v1, v2, v3))
    ]
    for copy in copies:
        copy.start()

    def split(value):
        return value.reshape(frames, group, value.shape[-1])

    mem, dec = memory[...], decoded[...]
    for r in range(4):
        copies[r].wait()
        cols = pl.ds(r * block, block)
        keys = jnp.dot(mem, w[r, :, : 2 * block], preferred_element_type=wide)
        queries = jnp.dot(dec, w[r, :, 2 * block : 5 * block], preferred_element_type=wide)
        mk[:, :, cols] = split(keys[:, :block])
        sk[:, :, cols] = split(keys[:, block:])
        mq[:, :, cols] = split(queries[:, :block] + vectors[0:1, cols])
        sq[:, :, cols] = split(queries[:, block : 2 * block] + vectors[2:3, cols])
        pre[:, cols] = queries[:, 2 * block :] + vectors[4:5, cols]

    def lane(c):
        return pl.ds(c * lanes, lanes)

    def spread(row, c):
        return jnp.broadcast_to(vectors[row : row + 1, lane(c)], (group, lanes))

    def energies(queries, keys, vec_row, energy):
        weights = [spread(vec_row, c) for c in range(chunks)]

        def one(i, carried):
            query = [queries[i, :, lane(c)] for c in range(chunks)]
            for j in range(frames):
                total = jnp.tanh(query[0] + keys[j, :, lane(0)]) * weights[0]
                for c in range(1, chunks):
                    total = total + jnp.tanh(query[c] + keys[j, :, lane(c)]) * weights[c]
                energy[i * frames + j] = jnp.broadcast_to(
                    jnp.sum(total, axis=-1, keepdims=True), (group, lanes)
                )
            return carried

        lax.fori_loop(0, frames, one, 0)

    energies(mq, mk, 1, mono)
    energies(sq, sk, 3, span)

    length = lengths[...]
    valid = [(length > j) for j in range(frames)]
    ones = jnp.ones((group, lanes), wide)
    zeros = jnp.zeros((group, lanes), wide)
    live = [jnp.where(valid[j], 1.0, 0.0).astype(wide) for j in range(frames)]
    diagonal = lax.broadcasted_iota(jnp.int32, (group, lanes), 1) - lax.broadcasted_iota(
        jnp.int32, (group, lanes), 0
    )

    def attend(i, previous):
        base = i * frames
        top = jnp.full((group, lanes), -1e30, wide)
        for j in range(frames):
            top = jnp.maximum(top, jnp.where(valid[j], span[base + j], -1e30))
        weight = [jnp.where(valid[j], jnp.exp(span[base + j] - top), 0.0) for j in range(frames)]
        current, ratios = [], []
        queued = previous[0]
        for j in range(frames):
            prob = sigmoid(mono[base + j] + offset + noise[base + j]) * live[j]
            keep[base + j] = prob
            queue[base + j] = queued
            alpha = prob * queued
            current.append(alpha)
            if j + 1 < frames:
                queued = (1.0 - prob) * queued + previous[j + 1]
            both = weight[j] + weight[j - 1] if j else weight[j]
            both = jnp.where(valid[j], both, 1.0)
            window[base + j] = both
            scaled[base + j] = weight[j]
            quotient = alpha / both
            ratio[base + j] = quotient
            ratios.append(quotient)
        row = zeros
        for j in range(frames):
            beta = weight[j] * (ratios[j] + (ratios[j + 1] if j + 1 < frames else zeros))
            row = jnp.where(diagonal == group * j, beta, row)
        mix[i] = row
        return tuple(current)

    lax.fori_loop(0, frames, attend, tuple([ones] + [zeros] * (frames - 1)))

    beta_low = mix[...].reshape(rows, lanes)[:, :rows].astype(low)
    context = jnp.dot(beta_low, mem, preferred_element_type=wide).astype(low)
    seen[0] = context
    for r in range(4):
        cols = pl.ds(r * block, block)
        value = jnp.tanh(
            pre[:, cols] + jnp.dot(context, w[r, :, 5 * block :], preferred_element_type=wide)
        )
        pre[:, cols] = value
        pack[r, :, 5 * block :] = value.astype(low)
    logits = vocab_bias[...]
    for r in range(4):
        copies[4 + r].wait()
        logits = logits + jnp.dot(pack[r, :, 5 * block :], v[r], preferred_element_type=wide)
    shifted = jnp.exp(logits - jnp.max(logits, axis=-1, keepdims=True))
    softmax = shifted / jnp.sum(shifted, axis=-1, keepdims=True)
    onehot = (labels[...] == lax.broadcasted_iota(jnp.int32, softmax.shape, 1)).astype(wide)
    grad_logits = ((softmax - onehot) * counted[...]).astype(low)
    seen[1] = grad_logits
    sums[5:6, :] = jnp.sum(grad_logits.astype(wide), axis=0, keepdims=True)
    sums[6:8, :] = jnp.zeros((2, sums.shape[1]), wide)

    grad_context = jnp.zeros((rows, memory.shape[1]), wide)
    for r in range(4):
        cols = pl.ds(r * block, block)
        value = pre[:, cols]
        grad_pre = (dot_nt(grad_logits, v[r]) * (1.0 - value * value)).astype(low)
        pack[r, :, 4 * block : 5 * block] = grad_pre
        sums[4:5, cols] = jnp.sum(grad_pre.astype(wide), axis=0, keepdims=True)
        grad_context = grad_context + dot_nt(grad_pre, w[r, :, 5 * block :])
    upper = grad_context.astype(low)
    lower = (grad_context - upper.astype(wide)).astype(low)
    grad_memory[...] = dot_tn(beta_low, upper) + dot_tn(beta_low, lower)
    cross = dot_nt(upper, mem) + dot_nt(lower, mem)
    if rows < lanes:
        cross = jnp.concatenate([cross, jnp.zeros((rows, lanes - rows), wide)], axis=1)
    mix[...] = split(cross)

    def unattend(k, later):
        i = frames - 1 - k
        base = i * frames
        cross_row = mix[i]
        grad_beta = [
            jnp.broadcast_to(
                jnp.sum(
                    jnp.where(diagonal == group * j, cross_row, 0.0), axis=-1, keepdims=True
                ),
                (group, lanes),
            )
            for j in range(frames)
        ]
        weight = [scaled[base + j] for j in range(frames)]
        share = [ratio[base + j] for j in range(frames)]
        direct, from_window, grad_weight = [], [], []
        for j in range(frames):
            grad_ratio = grad_beta[j] * weight[j]
            if j:
                grad_ratio = grad_ratio + grad_beta[j - 1] * weight[j - 1]
            pull = grad_ratio / window[base + j]
            direct.append(pull)
            from_window.append(jnp.where(valid[j], -pull * share[j], 0.0))
            grad_weight.append(
                grad_beta[j] * (share[j] + (share[j + 1] if j + 1 < frames else zeros))
            )
        top = jnp.full((group, lanes), -1e30, wide)
        for j in range(frames):
            top = jnp.maximum(top, jnp.where(valid[j], span[base + j], -1e30))
        total, ties, at_top, through = zeros, zeros, [], []
        for j in range(frames):
            pulled = grad_weight[j] + from_window[j]
            if j + 1 < frames:
                pulled = pulled + from_window[j + 1]
            pulled = weight[j] * pulled
            through.append(pulled)
            total = total + pulled
            hit = jnp.where(span[base + j] == top, live[j], 0.0)
            at_top.append(hit)
            ties = ties + hit
        back = total / ties
        for j in range(frames):
            span[base + j] = through[j] - at_top[j] * back
        grad_queue = zeros
        now = [None] * frames
        for j in reversed(range(frames)):
            prob = keep[base + j]
            grad_alpha = direct[j] + later[j]
            mono[base + j] = queue[base + j] * (grad_alpha - grad_queue) * prob * (1.0 - prob)
            grad_queue = prob * grad_alpha + (1.0 - prob) * grad_queue
            now[j] = grad_queue
        return tuple(now)

    lax.fori_loop(0, frames, unattend, tuple([zeros] * frames))

    def energy_back(queries, keys, energy, bias_row, vec_row):
        def one_chunk(c, carried):
            at = pl.ds(pl.multiple_of(c * lanes, lanes), lanes)
            weight = jnp.broadcast_to(vectors[vec_row : vec_row + 1, at], (group, lanes))

            def one(i, carry):
                grad_keys, vec_total, bias_total = carry
                query = queries[i, :, at]
                grad_query = zeros
                new_keys = []
                for j in range(frames):
                    squash = jnp.tanh(query + keys[j, :, at])
                    grad = energy[i * frames + j]
                    scaled_squash = grad * squash
                    vec_total = vec_total + scaled_squash
                    inner = grad - scaled_squash * squash
                    grad_query = grad_query + inner
                    new_keys.append(grad_keys[j] + inner)
                queries[i, :, at] = grad_query * weight
                return (tuple(new_keys), vec_total, bias_total + grad_query)

            grad_keys, vec_total, bias_total = lax.fori_loop(
                0, frames, one, (tuple([zeros] * frames), zeros, zeros)
            )
            for j in range(frames):
                keys[j, :, at] = grad_keys[j] * weight
            sums[bias_row : bias_row + 1, at] = jnp.sum(bias_total * weight, axis=0, keepdims=True)
            sums[vec_row : vec_row + 1, at] = jnp.sum(vec_total, axis=0, keepdims=True)
            return carried

        lax.fori_loop(0, chunks, one_chunk, 0)

    energy_back(mq, mk, mono, 0, 1)
    energy_back(sq, sk, span, 2, 3)

    total_memory = grad_memory[...]
    total_decoded = jnp.zeros_like(total_memory)
    for r in range(4):
        cols = pl.ds(r * block, block)
        for n, source in enumerate((mk, sk, mq, sq)):
            pack[r, :, n * block : (n + 1) * block] = (
                source[:, :, cols].reshape(rows, block).astype(low)
            )
        total_memory = total_memory + dot_nt(pack[r, :, : 2 * block], w[r, :, : 2 * block])
        total_decoded = total_decoded + dot_nt(
            pack[r, :, 2 * block : 5 * block], w[r, :, 2 * block : 5 * block]
        )
    grad_memory[...] = total_memory
    grad_decoded[...] = total_decoded


def run_attend(memory, decoded, weights, vocab, vectors, vocab_bias, noise, lengths, labels, counted, frames):
    rows, width = memory.shape
    group = rows // frames
    full = weights[0].shape[1] // 6 * 4
    vocab_width = vocab[0].shape[1]
    cell = (frames * frames, group, 128)
    return pl.pallas_call(
        attend_kernel,
        out_shape=(
            jax.ShapeDtypeStruct((rows, width), wide),
            jax.ShapeDtypeStruct((rows, width), wide),
            jax.ShapeDtypeStruct((4, rows, full // 4 * 6), low),
            jax.ShapeDtypeStruct((2, rows, vocab_width), low),
            jax.ShapeDtypeStruct((8, full), wide),
        ),
        in_specs=[in_vmem] * 2 + [in_place] * 8 + [in_vmem] * 6,
        out_specs=[in_vmem] * 5,
        scratch_shapes=[
            pltpu.VMEM((4,) + weights[0].shape, low),
            pltpu.VMEM((4,) + vocab[0].shape, low),
            pltpu.SemaphoreType.DMA((8,)),
        ]
        + [pltpu.VMEM((frames, group, full), wide)] * 4
        + [pltpu.VMEM(cell, wide)] * 7
        + [pltpu.VMEM((frames, group, 128), wide), pltpu.VMEM((rows, full), wide)],
        compiler_params=pltpu.CompilerParams(vmem_limit_bytes=56 << 20),
        name="attend",
    )(memory, decoded, *weights, *vocab, vectors, vocab_bias, noise, lengths, labels, counted)


def local(
    dp,
    block_input, norm_gain, lstm_in, lstm_rec, lstm_bias,
    mono_mem, mono_dec, mono_bias, mono_vec, span_mem, span_dec, span_bias, span_vec,
    out_weight, out_bias, vocab_weight, vocab_bias, noise, enc_lengths, label_lengths, labels,
):
    ring = Ring(dp)
    s, y = lax.axis_index("section"), lax.axis_index("mp")
    side = s.reshape(1).astype(jnp.int32)
    _, utts, frames, width = block_input.shape
    half, quarter = utts // 2, utts // 4
    shard_rows, _, unit_half = lstm_in.shape[1:]
    wide_half = 4 * unit_half
    block = mono_mem.shape[1]
    vocab_size = vocab_weight.shape[1]
    vocab_pad = 4 * block

    in_shard = corners(lstm_in[0].reshape(shard_rows, wide_half))
    rec_shard = corners(lstm_rec[0].reshape(shard_rows, wide_half))
    b_own = corners(lstm_bias[0].reshape(1, wide_half)).astype(wide)
    b_other = across_cores(b_own)

    inputs = jnp.swapaxes(block_input[0], 0, 1).astype(wide)
    normed, norm_pullback = jax.vjp(normalize, inputs, norm_gain[0])
    normed_low = normed.astype(low)
    normed_section = jnp.where(s == y, normed_low, across_cores(normed_low))
    normed_own = lax.dynamic_slice_in_dim(normed_section, s * half, half, axis=1)
    normed_other = lax.dynamic_slice_in_dim(normed_section, (1 - s) * half, half, axis=1)
    normed_own = normed_own.reshape(frames * half, width)
    normed_other = normed_other.reshape(frames * half, width)

    shards = jnp.concatenate(
        [mono_mem, span_mem, mono_dec, span_dec, out_weight[0], out_weight[1]], axis=1
    )
    weight_own = lax.all_gather(shards, "dp", axis=0, tiled=True)
    weight_chip = across_chips(weight_own)
    weights = [weight_own, weight_chip, across_cores(weight_own), across_cores(weight_chip)]
    vocab_own = jnp.pad(vocab_weight, ((0, 0), (0, vocab_pad - vocab_size)))
    vocab_chip = across_chips(vocab_own)
    vocab = [vocab_own, vocab_chip, across_cores(vocab_own), across_cores(vocab_chip)]
    vector_own = jnp.stack([mono_bias, mono_vec, span_bias, span_vec, out_bias])
    vector_pair = jnp.concatenate([vector_own, across_chips(vector_own)], axis=1)
    vectors = jnp.concatenate([vector_pair, across_cores(vector_pair)], axis=1)
    vectors = jnp.pad(vectors, ((0, 3), (0, 0)))

    in_own, rec_own = ring.gather([in_shard, rec_shard])
    in_other = across_cores(in_own)
    rec_other = across_cores(rec_own)

    def project(weight):
        value = jnp.dot(normed_own, weight, preferred_element_type=wide)
        return value.reshape(frames, half, wide_half)

    quarters, before, gates, cells = run_forward(
        side, project(in_own), project(in_other), rec_own, rec_other, b_own, b_other
    )

    kept = lax.dynamic_index_in_dim(quarters, y, axis=0, keepdims=False)
    given = lax.dynamic_index_in_dim(quarters, 1 - y, axis=0, keepdims=False)
    taken = across_chips(given)
    rows = frames * quarter
    memory = jnp.where(y == 0, kept, taken).reshape(rows, width)
    decoded = jnp.where(y == 0, taken, kept).reshape(rows, width)

    start = s * half + y * quarter
    noise_part = jnp.transpose(
        lax.dynamic_slice_in_dim(noise, start, quarter, axis=0), (1, 2, 0)
    ).reshape(frames * frames, quarter, 1)
    noise_part = jnp.broadcast_to(noise_part, (frames * frames, quarter, 128))
    length_part = lax.dynamic_slice_in_dim(enc_lengths, start, quarter, axis=0)
    length_part = jnp.broadcast_to(length_part[:, None], (quarter, 128))
    label_part = lax.dynamic_slice_in_dim(labels, start, quarter, axis=0).T.reshape(rows, 1)
    count_part = lax.dynamic_slice_in_dim(label_lengths, start, quarter, axis=0)
    counted = (jnp.arange(frames)[:, None] < count_part[None, :]).astype(wide).reshape(rows, 1)
    bias_row = jnp.pad(vocab_bias, (0, vocab_pad - vocab_size), constant_values=-1e30)[None]

    grad_memory, grad_decoded, pack, seen, sums = run_attend(
        memory, decoded, weights, vocab, vectors, bias_row, noise_part, length_part,
        label_part, counted, frames,
    )

    grad_kept = jnp.where(y == 0, grad_memory, grad_decoded)
    grad_given = jnp.where(y == 0, grad_decoded, grad_memory).astype(low)
    grad_taken = across_chips(grad_given).astype(wide)
    outside = jnp.stack(
        [jnp.where(y == 0, grad_kept, grad_taken), jnp.where(y == 0, grad_taken, grad_kept)]
    ).reshape(2, frames, quarter, width)
    dz = run_backward(side, outside, gates, cells, rec_own.T, rec_other.T)

    dz = dz.reshape(2, frames * half, wide_half)
    dz_kept = lax.dynamic_index_in_dim(dz, s, axis=0, keepdims=False)
    dz_given = lax.dynamic_index_in_dim(dz, 1 - s, axis=0, keepdims=False)
    dz_all = jnp.concatenate([dz_kept, across_cores(dz_given)], axis=0)
    before = before.reshape(frames * half, width)
    before_all = jnp.concatenate([before, across_cores(before)], axis=0)
    normed_all = jnp.concatenate([normed_own, normed_other], axis=0)
    rec_total = dot_tn(before_all, dz_all).astype(low)
    in_total = dot_tn(normed_all, dz_all).astype(low)
    rec_grad, in_grad = ring.scatter([rec_total, in_total])

    grad_part = dot_nt(dz_kept, in_own) + dot_nt(dz_given, in_other)
    grad_part = grad_part.reshape(frames, half, width)
    grad_peer = across_cores(grad_part)
    grad_section = jnp.concatenate(
        [jnp.where(s == 0, grad_part, grad_peer), jnp.where(s == 0, grad_peer, grad_part)], axis=1
    )
    grad_far = lax.ppermute(grad_section, ("section", "mp"), [(0, 1), (3, 2)])
    grad_inputs, grad_gain = norm_pullback(jnp.where(s == y, grad_section, grad_far))

    kept_far = across_chips(kept)
    memory_next = jnp.where(y == 0, given, kept_far).reshape(rows, width)
    decoded_next = jnp.where(y == 0, kept_far, given).reshape(rows, width)
    states = jnp.stack([memory, memory_next, decoded, decoded_next])
    states_core = across_cores(states)

    def gathered(n):
        return jnp.concatenate(
            [states[n], states_core[n], states[n + 1], states_core[n + 1]], axis=0
        )

    memory_all, decoded_all = gathered(0), gathered(2)
    pack_core = across_cores(pack[2:4])
    pack_far = across_chips(jnp.stack([pack[1], pack_core[1]]))
    pack_all = jnp.concatenate([pack[0], pack_core[0], pack_far[0], pack_far[1]], axis=0)
    seen_pair = jnp.concatenate([seen, across_chips(seen)], axis=0)
    seen_core = across_cores(seen_pair)
    seen_all = [
        jnp.concatenate([seen_pair[n], seen_core[n], seen_pair[2 + n], seen_core[2 + n]], axis=0)
        for n in range(2)
    ]
    grads = jnp.concatenate(
        [
            dot_tn(memory_all, pack_all[:, : 2 * block]),
            dot_tn(decoded_all, pack_all[:, 2 * block : 5 * block]),
            dot_tn(seen_all[0], pack_all[:, 4 * block : 5 * block]),
        ],
        axis=1,
    ).astype(low)
    grads = lax.psum_scatter(grads, "dp", scatter_dimension=0, tiled=True).astype(wide)
    vocab_grad = dot_tn(pack_all[:, 5 * block :], seen_all[1])[:, :vocab_size].astype(low)
    vocab_grad = lax.psum(vocab_grad, "dp").astype(wide)

    blocks = sums[:5].reshape(5, 4, block)
    pair = blocks[:, :2] + across_cores(blocks[:, 2:])
    vector_sum = pair[:, 0] + across_chips(pair[:, 1])
    bias_sum = sums[5] + across_cores(sums[5])
    bias_sum = bias_sum + across_chips(bias_sum)
    lstm_bias_sum = jnp.sum(dz_all.astype(wide), axis=0)
    flat = jnp.concatenate(
        [
            vector_sum.reshape(-1),
            bias_sum,
            lstm_bias_sum,
            grad_gain.reshape(-1),
        ]
    )
    flat = jnp.pad(flat, (0, -flat.shape[0] % 1024)).reshape(-1, 1024)
    flat = ring.total(flat).reshape(-1)
    ends = [5 * block, 5 * block + vocab_pad, 5 * block + vocab_pad + wide_half]
    vector_sum = flat[: ends[0]].reshape(5, block)
    bias_sum = flat[ends[0] : ends[0] + vocab_size]
    lstm_bias_sum = corners(flat[ends[1] : ends[2]].reshape(4, unit_half))
    gain_sum = flat[ends[2] : ends[2] + width]

    in_grad = corners(in_grad.astype(low)).astype(wide).reshape(1, shard_rows, 4, unit_half)
    rec_grad = corners(rec_grad.astype(low)).astype(wide).reshape(1, shard_rows, 4, unit_half)
    column = [grads[:, n * block : (n + 1) * block] for n in range(6)]
    return (
        jnp.swapaxes(grad_inputs, 0, 1)[None],
        gain_sum[None],
        in_grad,
        rec_grad,
        lstm_bias_sum[None],
        column[0],
        column[2],
        vector_sum[0],
        vector_sum[1],
        column[1],
        column[3],
        vector_sum[2],
        vector_sum[3],
        jnp.stack([column[4], column[5]]),
        vector_sum[4],
        vocab_grad,
        bias_sum,
    )


def solution(mesh):
    both = ("section", "mp")
    in_specs = (
        P("section", "dp", None, None),
        P("section", None),
        P("section", "dp", None, "mp"),
        P("section", "dp", None, "mp"),
        P("section", None, "mp"),
        P("dp", both),
        P("dp", both),
        P(both),
        P(both),
        P("dp", both),
        P("dp", both),
        P(both),
        P(both),
        P(None, "dp", both),
        P(both),
        P(both, None),
        P(),
        P("dp", None, None),
        P("dp"),
        P("dp"),
        P("dp", None),
    )
    out_specs = (
        P("section", "dp", None, None),
        P("section", None),
        P("section", "dp", None, "mp"),
        P("section", "dp", None, "mp"),
        P("section", None, "mp"),
        P("dp", both),
        P("dp", both),
        P(both),
        P(both),
        P("dp", both),
        P("dp", both),
        P(both),
        P(both),
        P(None, "dp", both),
        P(both),
        P(both, None),
        P(),
    )
    dp = mesh.shape["dp"]

    def step(*arrays):
        return local(dp, *arrays)

    return jax.shard_map(step, mesh=mesh, in_specs=in_specs, out_specs=out_specs, check_vma=False)
```

time: 2250 us -> 662 us (0.29); the launches traced: 2210 us -> 653 us
  waiting for transfers between devices: 1120 us -> 248 us
  local copies, waits for them, and re-layouts: 385 us -> 86.3 us
  blocking collectives: 260 us -> 0 us
  other arithmetic: 233 us -> 41.9 us
  matrix products: 192 us -> 29.2 us
  starting transfers between devices: 1.67 us -> 147 us
  Pallas kernels: 0 us -> 86.1 us
    reduce_scatter x24 -> x0, waiting for transfers between devices: 794 us -> none  [the longest x16 156 us: reduce_units(): return lax.psum_scatter(partial_grad, 'mp', scatter_dimension=1, tiled=True)]
    all_gather x20 -> x0, blocking collectives: 202 us -> none  [the longest x16 73.7 us: fetch_units(): return lax.all_gather(own_hidden, 'mp', axis=1, tiled=True)]
    ppermute x0 -> x65, waiting for transfers between devices: none -> 171 us  [the longest x6 63.5 us: gather(): held[i] = lax.ppermute(held[i], 'dp', self.ring)]
    dot_general x60 -> x10, matrix products: 192 us -> 29.2 us  [the longest x6 11.7 us: dot_tn(): lax.dot_general(a, b, (((0,), (0,)), ((), ())), preferred_element_type=wide)]
    ppermute x0 -> x65, starting transfers between devices: none -> 146 us  [the longest x17 75.4 us: across_cores(): return lax.ppermute(array, 'section', core_swap)]
    dynamic_update_slice x432 -> x17, local copies, waits for them, and re-layouts: 164 us -> 20.8 us  [the longest x9 13.7 us: gather(): full = lax.dynamic_update_slice(full, other, ((at * 2 + 1 - x) * r, 0))]
    all_gather x4 -> x1, waiting for transfers between devices: 140 us -> 0.01 us  [local(): weight_own = lax.all_gather(shards, 'dp', axis=0, tiled=True)]
    psum x4 -> x1, waiting for transfers between devices: 181 us -> 54.3 us  [local(): vocab_grad = lax.psum(vocab_grad, 'dp').astype(wide)]
  transfers between devices with their start and end apart: 32 -> 68, of which waited for: 30 -> 20; matrix products, arithmetic and copies ran while one was open for 8% -> 22% of each run, Pallas kernels for 0% -> 13%
where the time goes in v1:
time: 662 us; the launch traced here: 653 us
  waiting for transfers between devices  248 us (37%)
  starting transfers between devices  147 us (22%)
  local copies, waits for them, and re-layouts  86.3 us (13%)
  Pallas kernels  86.1 us (13%)
  other arithmetic  41.9 us (6%)
  matrix products  29.2 us (4%)
  between operations  15.1 us (2%)
    ppermute x17, starting transfers between devices, across_cores(): return lax.ppermute(array, 'section', core_swap)  75.4 us
    ppermute x6, waiting for transfers between devices, gather(): held[i] = lax.ppermute(held[i], 'dp', self.ring)  63.5 us
    psum x1, waiting for transfers between devices, local(): vocab_grad = lax.psum(vocab_grad, 'dp').astype(wide)  54.3 us
    ppermute x10, waiting for transfers between devices, across_chips(): return lax.ppermute(array, 'mp', core_swap)  45.2 us
    ppermute x6, waiting for transfers between devices, scatter(): total = total + lax.ppermute(sums[i], 'dp', self.ring).astype(wide)  44.2 us
    pallas_call x1, Pallas kernels, run_attend(): pl.pallas_call(attend_kernel, out_shape=(jax.ShapeDtypeStruct((rows, widt...  32.4 us
    pallas_call x1, Pallas kernels, run_forward(): pl.pallas_call(forward_kernel, out_shape=(jax.ShapeDtypeStruct((2, steps,...  27.5 us
    pallas_call x1, Pallas kernels, run_backward(): pl.pallas_call(backward_kernel, out_shape=jax.ShapeDtypeStruct((2, steps,...  26.2 us
  transfers between devices with their start and end apart: 68, of which 20 were waited for; matrix products, arithmetic and copies ran while one was open for 22% of the time, Pallas kernels for 13%

profile of v1, /device:TPU:0, one launch (start us, length us, event | category | flops | bytes accessed | tf_op | source)
XLA Modules:
  0.0 652.9 jit_solution(12990808986586866650)
XLA Ops:
  16.5 3.1 collective-permute-start.12
  23.2 2.6 broadcast.60.clone.1
  26.7 2.6 broadcast.60.clone
  31.6 1.8 collective-permute-start.14
  33.4 16.9 %collective-permute-done.3 = bf16[128,2048]{0,1:T(8,128)(2,1)S(1)} collective-permute-done((bf16[128,2048]{0,1:T(8,128)(2,1)S(1)}, bf16[128,2048]{0,1:T(8,128)(2,1)S(1)}, u32[]{:S(2)}, u32[]{:S(2)}) %collective-permute-start.3) | collective-permute-done | bytes 524320 | tf_op jit(solution)/shard_map/ppermute | solution.py:58
  50.4 2.3 collective-permute-start.4
  57.7 8.4 %collective-permute-done.14 = bf16[128,2048]{0,1:T(8,128)(2,1)S(1)} collective-permute-done((bf16[128,2048]{0,1:T(8,128)(2,1)S(1)}, bf16[128,2048]{0,1:T(8,128)(2,1)S(1)}, u32[]{:S(2)}, u32[]{:S(2)}) %collective-permute-start.14) | collective-permute-done | bytes 524320 | tf_op jit(solution)/shard_map/ppermute | solution.py:58
  67.4 5.5 collective-permute-start.16
  72.8 15.7 %collective-permute-done.5 = bf16[128,2048]{0,1:T(8,128)(2,1)S(1)} collective-permute-done((bf16[128,2048]{0,1:T(8,128)(2,1)S(1)}, bf16[128,2048]{0,1:T(8,128)(2,1)S(1)}, u32[]{:S(2)}, u32[]{:S(2)}) %collective-permute-start.5) | collective-permute-done | bytes 524320 | tf_op jit(solution)/shard_map/ppermute | solution.py:58
  89.9 3.2 collective-permute-start.7
  96.6 11.4 %collective-permute-done.16 = bf16[128,2048]{0,1:T(8,128)(2,1)S(1)} collective-permute-done((bf16[128,2048]{0,1:T(8,128)(2,1)S(1)}, bf16[128,2048]{0,1:T(8,128)(2,1)S(1)}, u32[]{:S(2)}, u32[]{:S(2)}) %collective-permute-start.16) | collective-permute-done | bytes 524320 | tf_op jit(solution)/shard_map/ppermute | solution.py:58
  108.0 3.0 collective-permute-start.17
  111.0 11.1 %collective-permute-done.7 = bf16[128,2048]{0,1:T(8,128)(2,1)S(1)} collective-permute-done((bf16[128,2048]{0,1:T(8,128)(2,1)S(1)}, bf16[128,2048]{0,1:T(8,128)(2,1)S(1)}, u32[]{:S(2)}, u32[]{:S(2)}) %collective-permute-start.7) | collective-permute-done | bytes 524320 | tf_op jit(solution)/shard_map/ppermute | solution.py:58
  122.0 1.9 collective-permute-start.8
  126.7 10.1 %collective-permute-done.8 = bf16[128,2048]{0,1:T(8,128)(2,1)S(1)} collective-permute-done((bf16[128,2048]{0,1:T(8,128)(2,1)S(1)}, bf16[128,2048]{0,1:T(8,128)(2,1)S(1)}, u32[]{:S(2)}, u32[]{:S(2)}) %collective-permute-start.8) | collective-permute-done | bytes 524320 | tf_op jit(solution)/shard_map/ppermute | solution.py:56
  137.7 5.2 collective-permute-start.9
  148.5 67.2 %collective-permute-start.20 = (f32[1,2048]{1,0:T(1,128)S(1)}, f32[1,2048]{1,0:T(1,128)S(1)}, u32[]{:S(2)}, u32[]{:S(2)}) collective-permute-start(f32[1,2048]{1,0:T(1,128)S(1)} %convert_element_type.153.b_own), channel_id=1, source_target_pairs={{0,16},{16,0},{1,17},{17,1},{2,18},{18,2},{3,19},{19,3},{4,20},{20... | collective-permute-start | bytes 24584 | tf_op jit(solution)/shard_map/ppermute | solution.py:27
  218.0 4.8 fusion.2.z_own
  222.8 6.7 %copy.77.w_own = bf16[1024,2048]{1,0:T(8,128)(2,1)} copy(bf16[1024,2048]{0,1:T(8,128)(2,1)} %constant_dynamic-update-slice_fusion.4) | data formatting | bytes 8388608 | tf_op jit(solution)/shard_map/dynamic_update_slice | solution.py:66
  229.4 4.8 fusion.z_other
  234.2 6.5 copy.78.w_other
  241.3 27.5 %recur_forward.1 = (bf16[2,16,8,1024]{3,2,1,0:T(8,128)(2,1)}, bf16[16,16,1024]{2,1,0:T(8,128)(2,1)}, f32[16,16,4096]{2,1,0:T(8,128)}, f32[16,16,1024]{2,1,0:T(8,128)}) custom-call(s32[1]{0:T(128)} %bitcast.side, f32[16,16,2048]{2,1,0:T(8,128)} %fusion.2.z_own, f32[16,16,2048]{2,1,0:T(8,128)} %fusion.z_other, bf16[1024,2048]{1,0:T(8,128)(2,1)} %copy.77.w_own, ...), custom_call_target="tpu_custom_call" | custom-call | tf_op jit(solution)/shard_map/recur_forward/pallas_call | solution.py:166
  270.1 8.2 %collective-permute-done.59 = bf16[16,8,1024]{2,1,0:T(8,128)(2,1)S(1)} collective-permute-done((bf16[16,8,1024]{2,1,0:T(8,128)(2,1)S(1)}, bf16[16,8,1024]{2,1,0:T(8,128)(2,1)S(1)}, u32[]{:S(2)}, u32[]{:S(2)}) %collective-permute-start.59) | collective-permute-done | bytes 262176 | tf_op jit(solution)/shard_map/ppermute | solution.py:31
  281.2 6.2 collective-permute-done.21
  293.0 12.3 %collective-permute-done.28 = f32[5,256]{1,0:T(8,128)S(1)} collective-permute-done((f32[5,256]{1,0:T(8,128)S(1)}, f32[5,256]{1,0:T(8,128)S(1)}, u32[]{:S(2)}, u32[]{:S(2)}) %collective-permute-start.28) | collective-permute-done | bytes 5152 | tf_op jit(solution)/shard_map/ppermute | solution.py:31
  313.1 32.4 %attend.1 = (f32[128,1024]{1,0:T(8,128)}, f32[128,1024]{1,0:T(8,128)}, bf16[4,128,1536]{2,1,0:T(8,128)(2,1)}, bf16[2,128,1024]{2,1,0:T(8,128)(2,1)}, f32[8,1024]{1,0:T(8,128)}) custom-call(bf16[128,1024]{1,0:T(8,128)(2,1)} %get-tuple-element.134.memory, bf16[128,1024]{1,0:T(8,128)(2,1)} %get-tuple-element.133.decoded, ...), custom_call_target="tpu_custom_call" | custom-call | tf_op jit(solution)/shard_map/attend/pallas_call | solution.py:520
  345.4 2.1 slice_bitcast_fusion.3
  354.9 7.1 %collective-permute-done.36 = f32[1024]{0:T(1024)S(1)} collective-permute-done((f32[1024]{0:T(1024)S(1)}, f32[1024]{0:T(1024)S(1)}, u32[]{:S(2)}, u32[]{:S(2)}) %collective-permute-start.36) | collective-permute-done | bytes 4128 | tf_op jit(solution)/shard_map/ppermute | solution.py:31
  364.1 5.7 collective-permute-done.30
  371.0 26.2 %recur_backward.1 = bf16[2,16,16,2048]{3,2,1,0:T(8,128)(2,1)} custom-call(s32[1]{0:T(128)} %bitcast.side, f32[2,16,8,1024]{3,2,1,0:T(8,128)} %pad_maximum_fusion.4.outside, f32[16,16,4096]{2,1,0:T(8,128)} %get-tuple-element.29.gates, f32[16,16,1024]{2,1,0:T(8,128)} %get-tuple-element.30.cells, bf16[2048,1024]{1,0:T(8,128)(2,1)} %bitcast.26.t_own, ...), custom_call_target="tpu_custom_call" | custom-call | tf_op jit(solution)/shard_map/recur_backward/pallas_call | solution.py:247
  399.0 3.5 fusion.91
  402.5 4.4 convolution_add_fusion
  409.4 3.8 convolution_convert_fusion
  417.6 2.4 convolution_convert_fusion.1
  422.7 5.8 collective-permute-done.62
  428.5 1.7 collective-permute-start.52
  434.2 2.6 convolution_convert_fusion.2
  436.8 1.9 convolution_convert_fusion.3
  439.3 2.1 pad_maximum_fusion
  441.4 4.7 copy.93
  446.2 1.8 collective-permute-start.43
  451.7 4.1 collective-permute-start.32
  455.8 2.1 add_convert_fusion.3
  458.0 2.1 add_convert_fusion.7
  461.7 14.2 %collective-permute-done.54 = bf16[128,2048]{1,0:T(8,128)(2,1)S(1)} collective-permute-done((bf16[128,2048]{1,0:T(8,128)(2,1)}, bf16[128,2048]{1,0:T(8,128)(2,1)S(1)}, u32[]{:S(2)}, u32[]{:S(2)}) %collective-permute-start.54) | collective-permute-done | bytes 524320 | tf_op jit(solution)/shard_map/ppermute | solution.py:87
  477.1 2.4 add_convert_fusion.2
  479.5 7.8 %collective-permute-done.45 = bf16[128,2048]{1,0:T(8,128)(2,1)} collective-permute-done((bf16[128,2048]{1,0:T(8,128)(2,1)}, bf16[128,2048]{1,0:T(8,128)(2,1)}, u32[]{:S(2)}, u32[]{:S(2)}) %collective-permute-start.45) | collective-permute-done | bytes 524320 | tf_op jit(solution)/shard_map/ppermute | solution.py:87
  487.3 2.2 add_convert_fusion.6
  489.9 54.3 %all-reduce.6.cloned.1.call-done = bf16[256,1000]{0,1:T(8,128)(2,1)} async-done(((bf16[256,1000]{0,1:T(8,128)(2,1)}), bf16[256,1000]{0,1:T(8,128)(2,1)}) %all-reduce.6.cloned.1.call-update) | async-done | bytes 512016 | tf_op jit(solution)/shard_map/psum | solution.py:684
  544.1 2.1 convert_element_type.192
  548.3 2.4 add_convert_fusion.1
  551.9 2.1 add_convert_fusion.5
  559.1 6.5 %collective-permute-done.50 = bf16[128,2048]{1,0:T(8,128)(2,1)} collective-permute-done((bf16[128,2048]{1,0:T(8,128)(2,1)}, bf16[128,2048]{1,0:T(8,128)(2,1)}, u32[]{:S(2)}, u32[]{:S(2)}) %collective-permute-start.50) | collective-permute-done | bytes 524320 | tf_op jit(solution)/shard_map/ppermute | solution.py:85
  565.6 10.9 %collective-permute-done.56 = bf16[128,2048]{1,0:T(8,128)(2,1)} collective-permute-done((bf16[128,2048]{1,0:T(8,128)(2,1)}, bf16[128,2048]{1,0:T(8,128)(2,1)}, u32[]{:S(2)}, u32[]{:S(2)}) %collective-permute-start.56) | collective-permute-done | bytes 524320 | tf_op jit(solution)/shard_map/ppermute | solution.py:87
  576.5 2.4 add_convert_fusion
  578.9 5.4 collective-permute-start.57
  584.7 11.2 %collective-permute-done.47 = bf16[128,2048]{1,0:T(8,128)(2,1)} collective-permute-done((bf16[128,2048]{1,0:T(8,128)(2,1)}, bf16[128,2048]{1,0:T(8,128)(2,1)}, u32[]{:S(2)}, u32[]{:S(2)}) %collective-permute-start.47) | collective-permute-done | bytes 524320 | tf_op jit(solution)/shard_map/ppermute | solution.py:87
  595.9 2.4 add_convert_fusion.4
  598.3 5.4 collective-permute-start.48
  603.7 1.9 collective-permute-start.40
  606.6 2.5 copy.83
  611.7 2.9 reshape.194
  614.5 2.8 reshape.192
  617.4 22.7 %reduce-scatter.4.cloned.1.call-done = bf16[128,1536]{1,0:T(8,128)(2,1)} async-done(((bf16[1024,1536]{1,0:T(8,128)(2,1)}), bf16[128,1536]{1,0:T(8,128)(2,1)}) %reduce-scatter.4.cloned.1.call-update) | async-done | bytes 393232
  (315 shorter events, 107.9 us)
Async XLA Ops:
  7.2 137.4 %all-gather.2.cloned.1.call-start = ((), (), s32[]{:S(2)}) async-start(), calls=%async_computation.1 | async-start | bytes 3538944 | tf_op jit(solution)/shard_map/all_gather | solution.py:578
  13.2 531.0 %all-reduce.6.cloned.1.call-start = ((), (), s32[]{:S(2)}) async-start(), calls=%async_computation.2 | async-start | bytes 1024000 | tf_op jit(solution)/shard_map/psum | solution.py:684
  15.8 3.8 collective-permute-start.1
  16.5 13.6 %collective-permute-start.12 = (bf16[128,2048]{0,1:T(8,128)(2,1)S(1)}, bf16[128,2048]{0,1:T(8,128)(2,1)S(1)}, u32[]{:S(2)}, u32[]{:S(2)}) collective-permute-start(bf16[128,2048]{0,1:T(8,128)(2,1)S(1)} %collective-permute-done.10), channel_id=1, source_target_pairs={{0,4},{2,6},{4,8},{6,10},{8,12},{10,14},{12,0},{14,2},{1,5},{3,7},... | collective-permute-start | bytes 1572872 | tf_op jit(solution)/shard_map/ppermute | solution.py:58
  19.6 30.8 %collective-permute-start.3 = (bf16[128,2048]{0,1:T(8,128)(2,1)S(1)}, bf16[128,2048]{0,1:T(8,128)(2,1)S(1)}, u32[]{:S(2)}, u32[]{:S(2)}) collective-permute-start(bf16[128,2048]{0,1:T(8,128)(2,1)S(1)} %collective-permute-done.1), channel_id=1, source_target_pairs={{0,4},{2,6},{4,8},{6,10},{8,12},{10,14},{12,0},{14,2},{1,5},{3,7},... | collective-permute-start | bytes 1572872 | tf_op jit(solution)/shard_map/ppermute | solution.py:58
  21.2 31.5 %collective-permute-start.11 = (bf16[128,2048]{0,1:T(8,128)(2,1)S(1)}, bf16[128,2048]{0,1:T(8,128)(2,1)S(1)}, u32[]{:S(2)}, u32[]{:S(2)}) collective-permute-start(bf16[128,2048]{0,1:T(8,128)(2,1)S(1)} %collective-permute-done.10), channel_id=1, source_target_pairs={{0,2},{2,0},{4,6},{6,4},{8,10},{10,8},{12,14},{14,12},{1,3},{3,1},... | collective-permute-start | bytes 1572872 | tf_op jit(solution)/shard_map/ppermute | solution.py:56
  22.7 33.3 %collective-permute-start.2 = (bf16[128,2048]{0,1:T(8,128)(2,1)S(1)}, bf16[128,2048]{0,1:T(8,128)(2,1)S(1)}, u32[]{:S(2)}, u32[]{:S(2)}) collective-permute-start(bf16[128,2048]{0,1:T(8,128)(2,1)S(1)} %collective-permute-done.1), channel_id=1, source_target_pairs={{0,2},{2,0},{4,6},{6,4},{8,10},{10,8},{12,14},{14,12},{1,3},{3,1},... | collective-permute-start | bytes 1572872 | tf_op jit(solution)/shard_map/ppermute | solution.py:56
  30.1 59.7 %collective-permute-start.13 = (bf16[128,2048]{0,1:T(8,128)(2,1)S(1)}, bf16[128,2048]{0,1:T(8,128)(2,1)S(1)}, u32[]{:S(2)}, u32[]{:S(2)}) collective-permute-start(bf16[128,2048]{0,1:T(8,128)(2,1)S(1)} %collective-permute-done.12), channel_id=1, source_target_pairs={{0,2},{2,0},{4,6},{6,4},{8,10},{10,8},{12,14},{14,12},{1,3},{3,1},... | collective-permute-start | bytes 1572872 | tf_op jit(solution)/shard_map/ppermute | solution.py:56
  31.6 34.5 %collective-permute-start.14 = (bf16[128,2048]{0,1:T(8,128)(2,1)S(1)}, bf16[128,2048]{0,1:T(8,128)(2,1)S(1)}, u32[]{:S(2)}, u32[]{:S(2)}) collective-permute-start(bf16[128,2048]{0,1:T(8,128)(2,1)S(1)} %collective-permute-done.12), channel_id=1, source_target_pairs={{0,4},{2,6},{4,8},{6,10},{8,12},{10,14},{12,0},{14,2},{1,5},{3,7},... | collective-permute-start | bytes 1572872 | tf_op jit(solution)/shard_map/ppermute | solution.py:58
  50.4 44.5 %collective-permute-start.4 = (bf16[128,2048]{0,1:T(8,128)(2,1)S(1)}, bf16[128,2048]{0,1:T(8,128)(2,1)S(1)}, u32[]{:S(2)}, u32[]{:S(2)}) collective-permute-start(bf16[128,2048]{0,1:T(8,128)(2,1)S(1)} %collective-permute-done.3), channel_id=1, source_target_pairs={{0,2},{2,0},{4,6},{6,4},{8,10},{10,8},{12,14},{14,12},{1,3},{3,1},... | collective-permute-start | bytes 1572872 | tf_op jit(solution)/shard_map/ppermute | solution.py:56
  52.7 35.9 %collective-permute-start.5 = (bf16[128,2048]{0,1:T(8,128)(2,1)S(1)}, bf16[128,2048]{0,1:T(8,128)(2,1)S(1)}, u32[]{:S(2)}, u32[]{:S(2)}) collective-permute-start(bf16[128,2048]{0,1:T(8,128)(2,1)S(1)} %collective-permute-done.3), channel_id=1, source_target_pairs={{0,4},{2,6},{4,8},{6,10},{8,12},{10,14},{12,0},{14,2},{1,5},{3,7},... | collective-permute-start | bytes 1572872 | tf_op jit(solution)/shard_map/ppermute | solution.py:58
  66.1 57.9 %collective-permute-start.15 = (bf16[128,2048]{0,1:T(8,128)(2,1)S(1)}, bf16[128,2048]{0,1:T(8,128)(2,1)S(1)}, u32[]{:S(2)}, u32[]{:S(2)}) collective-permute-start(bf16[128,2048]{0,1:T(8,128)(2,1)S(1)} %collective-permute-done.14), channel_id=1, source_target_pairs={{0,2},{2,0},{4,6},{6,4},{8,10},{10,8},{12,14},{14,12},{1,3},{3,1},... | collective-permute-start | bytes 1572872 | tf_op jit(solution)/shard_map/ppermute | solution.py:56
  67.4 40.6 %collective-permute-start.16 = (bf16[128,2048]{0,1:T(8,128)(2,1)S(1)}, bf16[128,2048]{0,1:T(8,128)(2,1)S(1)}, u32[]{:S(2)}, u32[]{:S(2)}) collective-permute-start(bf16[128,2048]{0,1:T(8,128)(2,1)S(1)} %collective-permute-done.14), channel_id=1, source_target_pairs={{0,4},{2,6},{4,8},{6,10},{8,12},{10,14},{12,0},{14,2},{1,5},{3,7},... | collective-permute-start | bytes 1572872 | tf_op jit(solution)/shard_map/ppermute | solution.py:58
  88.6 36.3 %collective-permute-start.6 = (bf16[128,2048]{0,1:T(8,128)(2,1)S(1)}, bf16[128,2048]{0,1:T(8,128)(2,1)S(1)}, u32[]{:S(2)}, u32[]{:S(2)}) collective-permute-start(bf16[128,2048]{0,1:T(8,128)(2,1)S(1)} %collective-permute-done.5), channel_id=1, source_target_pairs={{0,2},{2,0},{4,6},{6,4},{8,10},{10,8},{12,14},{14,12},{1,3},{3,1},... | collective-permute-start | bytes 1572872 | tf_op jit(solution)/shard_map/ppermute | solution.py:56
  89.9 32.2 %collective-permute-start.7 = (bf16[128,2048]{0,1:T(8,128)(2,1)S(1)}, bf16[128,2048]{0,1:T(8,128)(2,1)S(1)}, u32[]{:S(2)}, u32[]{:S(2)}) collective-permute-start(bf16[128,2048]{0,1:T(8,128)(2,1)S(1)} %collective-permute-done.5), channel_id=1, source_target_pairs={{0,4},{2,6},{4,8},{6,10},{8,12},{10,14},{12,0},{14,2},{1,5},{3,7},... | collective-permute-start | bytes 1572872 | tf_op jit(solution)/shard_map/ppermute | solution.py:58
  108.0 35.8 %collective-permute-start.17 = (bf16[128,2048]{0,1:T(8,128)(2,1)S(1)}, bf16[128,2048]{0,1:T(8,128)(2,1)S(1)}, u32[]{:S(2)}, u32[]{:S(2)}) collective-permute-start(bf16[128,2048]{0,1:T(8,128)(2,1)S(1)} %collective-permute-done.16), channel_id=1, source_target_pairs={{0,2},{2,0},{4,6},{6,4},{8,10},{10,8},{12,14},{14,12},{1,3},{3,1},... | collective-permute-start | bytes 1572872 | tf_op jit(solution)/shard_map/ppermute | solution.py:56
  122.0 14.8 %collective-permute-start.8 = (bf16[128,2048]{0,1:T(8,128)(2,1)S(1)}, bf16[128,2048]{0,1:T(8,128)(2,1)S(1)}, u32[]{:S(2)}, u32[]{:S(2)}) collective-permute-start(bf16[128,2048]{0,1:T(8,128)(2,1)S(1)} %collective-permute-done.7), channel_id=1, source_target_pairs={{0,2},{2,0},{4,6},{6,4},{8,10},{10,8},{12,14},{14,12},{1,3},{3,1},... | collective-permute-start | bytes 1572872 | tf_op jit(solution)/shard_map/ppermute | solution.py:56
  137.7 91.7 %collective-permute-start.9 = (bf16[1024,2048]{0,1:T(8,128)(2,1)}, bf16[1024,2048]{0,1:T(8,128)(2,1)}, u32[]{:S(2)}, u32[]{:S(2)}) collective-permute-start(bf16[1024,2048]{0,1:T(8,128)(2,1)} %constant_dynamic-update-slice_fusion.12), channel_id=1, source_target_pairs={{0,16},{16,0},{1,17},{17,1},{2,18},{18,2},{3,19},{19,3},{4,20},{20... | collective-permute-start | bytes 12582920 | tf_op jit(solution)/shard_map/ppermute | solution.py:27
  144.6 89.6 %collective-permute-start.18 = (bf16[1024,2048]{0,1:T(8,128)(2,1)}, bf16[1024,2048]{0,1:T(8,128)(2,1)}, u32[]{:S(2)}, u32[]{:S(2)}) collective-permute-start(bf16[1024,2048]{0,1:T(8,128)(2,1)} %constant_dynamic-update-slice_fusion.4), channel_id=1, source_target_pairs={{0,16},{16,0},{1,17},{17,1},{2,18},{18,2},{3,19},{19,3},{4,20},{20... | collective-permute-start | bytes 12582920 | tf_op jit(solution)/shard_map/ppermute | solution.py:27
  144.6 72.8 %collective-permute-start.22 = (bf16[1024,1536]{1,0:T(8,128)(2,1)}, bf16[1024,1536]{1,0:T(8,128)(2,1)}, u32[]{:S(2)}, u32[]{:S(2)}) collective-permute-start(bf16[1024,1536]{1,0:T(8,128)(2,1)} %all-gather.2.cloned.1.call-done.w0), channel_id=1, source_target_pairs={{0,1},{1,0},{2,3},{3,2},{4,5},{5,4},{6,7},{7,6},{8,9},{9,8},{10,11... | collective-permute-start | bytes 9437192 | tf_op jit(solution)/shard_map/ppermute | solution.py:31
  147.2 68.5 %collective-permute-start = (bf16[16,32,1024]{2,1,0:T(8,128)(2,1)S(1)}, bf16[16,32,1024]{2,1,0:T(8,128)(2,1)S(1)}, u32[]{:S(2)}, u32[]{:S(2)}) collective-permute-start(bf16[16,32,1024]{2,1,0:T(8,128)(2,1)S(1)} %fusion.12), channel_id=1, source_target_pairs={{0,16},{16,0},{1,17},{17,1},{2,18},{18,2},{3,19},{19,3},{4,20},{20... | collective-permute-start | bytes 3145736 | tf_op jit(solution)/shard_map/ppermute | solution.py:27
  148.5 92.3 %collective-permute-start.20 = (f32[1,2048]{1,0:T(1,128)S(1)}, f32[1,2048]{1,0:T(1,128)S(1)}, u32[]{:S(2)}, u32[]{:S(2)}) collective-permute-start(f32[1,2048]{1,0:T(1,128)S(1)} %convert_element_type.153.b_own), channel_id=1, source_target_pairs={{0,16},{16,0},{1,17},{17,1},{2,18},{18,2},{3,19},{19,3},{4,20},{20... | collective-permute-start | bytes 24584 | tf_op jit(solution)/shard_map/ppermute | solution.py:27
  217.5 93.6 %collective-permute-start.23 = (bf16[1024,1536]{1,0:T(8,128)(2,1)}, bf16[1024,1536]{1,0:T(8,128)(2,1)}, u32[]{:S(2)}, u32[]{:S(2)}) collective-permute-start(bf16[1024,1536]{1,0:T(8,128)(2,1)} %all-gather.2.cloned.1.call-done.w0), channel_id=1, source_target_pairs={{0,16},{16,0},{1,17},{17,1},{2,18},{18,2},{3,19},{19,3},{4,20},{20... | collective-permute-start | bytes 9437192 | tf_op jit(solution)/shard_map/ppermute | solution.py:27
  217.5 93.6 %collective-permute-start.24 = (bf16[1024,1536]{1,0:T(8,128)(2,1)}, bf16[1024,1536]{1,0:T(8,128)(2,1)}, u32[]{:S(2)}, u32[]{:S(2)}) collective-permute-start(bf16[1024,1536]{1,0:T(8,128)(2,1)} %collective-permute-done.22.w1), channel_id=1, source_target_pairs={{0,16},{16,0},{1,17},{17,1},{2,18},{18,2},{3,19},{19,3},{4,20},{20... | collective-permute-start | bytes 9437192 | tf_op jit(solution)/shard_map/ppermute | solution.py:27
  269.9 8.3 %collective-permute-start.59 = (bf16[16,8,1024]{2,1,0:T(8,128)(2,1)S(1)}, bf16[16,8,1024]{2,1,0:T(8,128)(2,1)S(1)}, u32[]{:S(2)}, u32[]{:S(2)}) collective-permute-start(bf16[16,8,1024]{2,1,0:T(8,128)(2,1)S(1)} %dynamic-slice_bitcast_fusion.3), channel_id=1, source_target_pairs={{0,1},{1,0},{2,3},{3,2},{4,5},{5,4},{6,7},{7,6},{8,9},{9,8},{10,11... | collective-permute-start | bytes 786440 | tf_op jit(solution)/shard_map/ppermute | solution.py:31
  279.9 7.4 %collective-permute-start.21 = (bf16[16,8,1024]{2,1,0:T(8,128)(2,1)S(1)}, bf16[16,8,1024]{2,1,0:T(8,128)(2,1)S(1)}, u32[]{:S(2)}, u32[]{:S(2)}) collective-permute-start(bf16[16,8,1024]{2,1,0:T(8,128)(2,1)S(1)} %get-tuple-element.89), channel_id=1, source_target_pairs={{0,1},{1,0},{2,3},{3,2},{4,5},{5,4},{6,7},{7,6},{8,9},{9,8},{10,11... | collective-permute-start | bytes 786440 | tf_op jit(solution)/shard_map/ppermute | solution.py:31
  289.4 20.5 %collective-permute-start.60 = (bf16[4,128,1024]{2,1,0:T(8,128)(2,1)}, bf16[4,128,1024]{2,1,0:T(8,128)(2,1)S(1)}, u32[]{:S(2)}, u32[]{:S(2)}) collective-permute-start(bf16[4,128,1024]{2,1,0:T(8,128)(2,1)} %pad_maximum_fusion.5), channel_id=1, source_target_pairs={{0,16},{16,0},{1,17},{17,1},{2,18},{18,2},{3,19},{19,3},{4,20},{20... | collective-permute-start | bytes 3145736 | tf_op jit(solution)/shard_map/ppermute | solution.py:27
  290.7 15.9 %collective-permute-start.25 = (bf16[256,1024]{1,0:T(8,128)(2,1)S(1)}, bf16[256,1024]{1,0:T(8,128)(2,1)S(1)}, u32[]{:S(2)}, u32[]{:S(2)}) collective-permute-start(bf16[256,1024]{1,0:T(8,128)(2,1)S(1)} %pad.16.v0), channel_id=1, source_target_pairs={{0,1},{1,0},{2,3},{3,2},{4,5},{5,4},{6,7},{7,6},{8,9},{9,8},{10,11... | collective-permute-start | bytes 1572872 | tf_op jit(solution)/shard_map/ppermute | solution.py:31
  291.8 13.6 %collective-permute-start.28 = (f32[5,256]{1,0:T(8,128)S(1)}, f32[5,256]{1,0:T(8,128)S(1)}, u32[]{:S(2)}, u32[]{:S(2)}) collective-permute-start(f32[5,256]{1,0:T(8,128)S(1)} %stack.47), channel_id=1, source_target_pairs={{0,1},{1,0},{2,3},{3,2},{4,5},{5,4},{6,7},{7,6},{8,9},{9,8},{10,11... | collective-permute-start | bytes 15368 | tf_op jit(solution)/shard_map/ppermute | solution.py:31
  306.5 4.6 collective-permute-start.26
  306.7 4.4 collective-permute-start.27
  309.9 98.5 %collective-permute-start.49 = (bf16[256,1024]{1,0:T(8,128)(2,1)}, bf16[256,1024]{1,0:T(8,128)(2,1)}, u32[]{:S(2)}, u32[]{:S(2)}) collective-permute-start(bf16[256,1024]{1,0:T(8,128)(2,1)} %bitcast.196), channel_id=1, source_target_pairs={{0,16},{16,0},{1,17},{17,1},{2,18},{18,2},{3,19},{19,3},{4,20},{20... | collective-permute-start | bytes 1572872 | tf_op jit(solution)/shard_map/ppermute | solution.py:27
  347.5 59.4 %collective-permute-start.63 = (bf16[2,128,1024]{2,1,0:T(8,128)(2,1)}, bf16[2,128,1024]{2,1,0:T(8,128)(2,1)S(1)}, u32[]{:S(2)}, u32[]{:S(2)}) collective-permute-start(bf16[2,128,1024]{2,1,0:T(8,128)(2,1)} %get-tuple-element.34), channel_id=1, source_target_pairs={{0,1},{1,0},{2,3},{3,2},{4,5},{5,4},{6,7},{7,6},{8,9},{9,8},{10,11... | collective-permute-start | bytes 1572872 | tf_op jit(solution)/shard_map/ppermute | solution.py:31
  350.0 12.9 %collective-permute-start.33 = (f32[5,2,256]{2,1,0:T(2,128)S(1)}, f32[5,2,256]{2,1,0:T(2,128)S(1)}, u32[]{:S(2)}, u32[]{:S(2)}) collective-permute-start(f32[5,2,256]{2,1,0:T(2,128)S(1)} %slice.198), channel_id=1, source_target_pairs={{0,16},{16,0},{1,17},{17,1},{2,18},{18,2},{3,19},{19,3},{4,20},{20... | collective-permute-start | bytes 30728 | tf_op jit(solution)/shard_map/ppermute | solution.py:27
  351.7 10.3 %collective-permute-start.36 = (f32[1024]{0:T(1024)S(1)}, f32[1024]{0:T(1024)S(1)}, u32[]{:S(2)}, u32[]{:S(2)}) collective-permute-start(f32[1024]{0:T(1024)S(1)} %add.301), channel_id=1, source_target_pairs={{0,1},{1,0},{2,3},{3,2},{4,5},{5,4},{6,7},{7,6},{8,9},{9,8},{10,11... | collective-permute-start | bytes 12296 | tf_op jit(solution)/shard_map/ppermute | solution.py:31
  354.8 53.5 %collective-permute-start.61 = (bf16[2,128,1536]{2,1,0:T(8,128)(2,1)S(1)}, bf16[2,128,1536]{2,1,0:T(8,128)(2,1)S(1)}, u32[]{:S(2)}, u32[]{:S(2)}) collective-permute-start(bf16[2,128,1536]{2,1,0:T(8,128)(2,1)S(1)} %slice.164), channel_id=1, source_target_pairs={{0,16},{16,0},{1,17},{17,1},{2,18},{18,2},{3,19},{19,3},{4,20},{20... | collective-permute-start | bytes 2359304 | tf_op jit(solution)/shard_map/ppermute | solution.py:27
  362.0 7.8 %collective-permute-start.30 = (bf16[128,1024]{1,0:T(8,128)(2,1)S(1)}, bf16[128,1024]{1,0:T(8,128)(2,1)S(1)}, u32[]{:S(2)}, u32[]{:S(2)}) collective-permute-start(bf16[128,1024]{1,0:T(8,128)(2,1)S(1)} %select_convert_fusion), channel_id=1, source_target_pairs={{0,1},{1,0},{2,3},{3,2},{4,5},{5,4},{6,7},{7,6},{8,9},{9,8},{10,11... | collective-permute-start | bytes 786440 | tf_op jit(solution)/shard_map/ppermute | solution.py:31
  363.0 97.1 %collective-permute-start.34 = (f32[5,256]{1,0:T(8,128)S(1)}, f32[5,256]{1,0:T(8,128)S(1)}, u32[]{:S(2)}, u32[]{:S(2)}) collective-permute-start(f32[5,256]{1,0:T(8,128)S(1)} %bitcast.188), channel_id=1, source_target_pairs={{0,1},{1,0},{2,3},{3,2},{4,5},{5,4},{6,7},{7,6},{8,9},{9,8},{10,11... | collective-permute-start | bytes 15368 | tf_op jit(solution)/shard_map/ppermute | solution.py:31
  399.0 10.5 %collective-permute-start.37 = (bf16[256,2048]{1,0:T(8,128)(2,1)S(1)}, bf16[256,2048]{1,0:T(8,128)(2,1)S(1)}, u32[]{:S(2)}, u32[]{:S(2)}) collective-permute-start(bf16[256,2048]{1,0:T(8,128)(2,1)S(1)} %get-tuple-element.103), channel_id=1, source_target_pairs={{0,16},{16,0},{1,17},{17,1},{2,18},{18,2},{3,19},{19,3},{4,20},{20... | collective-permute-start | bytes 3145736 | tf_op jit(solution)/shard_map/ppermute | solution.py:27
  406.9 39.2 %collective-permute-start.31 = (f32[16,16,1024]{2,1,0:T(8,128)}, f32[16,16,1024]{2,1,0:T(8,128)}, u32[]{:S(2)}, u32[]{:S(2)}) collective-permute-start(f32[16,16,1024]{2,1,0:T(8,128)} %bitcast.31), channel_id=1, source_target_pairs={{0,16},{16,0},{1,17},{17,1},{2,18},{18,2},{3,19},{19,3},{4,20},{20... | collective-permute-start | bytes 3145736 | tf_op jit(solution)/shard_map/ppermute | solution.py:27
  408.3 23.3 %collective-permute-start.64 = (bf16[4,128,1024]{2,1,0:T(8,128)(2,1)S(1)}, bf16[4,128,1024]{2,1,0:T(8,128)(2,1)S(1)}, u32[]{:S(2)}, u32[]{:S(2)}) collective-permute-start(bf16[4,128,1024]{2,1,0:T(8,128)(2,1)S(1)} %pad_maximum_fusion.6), channel_id=1, source_target_pairs={{0,16},{16,0},{1,17},{17,1},{2,18},{18,2},{3,19},{19,3},{4,20},{20... | collective-permute-start | bytes 3145736 | tf_op jit(solution)/shard_map/ppermute | solution.py:27
  408.5 20.0 %collective-permute-start.62 = (bf16[2,128,1536]{2,1,0:T(8,128)(2,1)S(1)}, bf16[2,128,1536]{2,1,0:T(8,128)(2,1)S(1)}, u32[]{:S(2)}, u32[]{:S(2)}) collective-permute-start(bf16[2,128,1536]{2,1,0:T(8,128)(2,1)S(1)} %pad_maximum_fusion.7), channel_id=1, source_target_pairs={{0,1},{1,0},{2,3},{3,2},{4,5},{5,4},{6,7},{7,6},{8,9},{9,8},{10,11... | collective-permute-start | bytes 2359304 | tf_op jit(solution)/shard_map/ppermute | solution.py:31
  415.9 35.8 %collective-permute-start.53 = (bf16[128,2048]{1,0:T(8,128)(2,1)}, bf16[128,2048]{1,0:T(8,128)(2,1)}, u32[]{:S(2)}, u32[]{:S(2)}) collective-permute-start(bf16[128,2048]{1,0:T(8,128)(2,1)} %get-tuple-element.93), channel_id=1, source_target_pairs={{0,2},{2,0},{4,6},{6,4},{8,10},{10,8},{12,14},{14,12},{1,3},{3,1},... | collective-permute-start | bytes 1572872 | tf_op jit(solution)/shard_map/ppermute | solution.py:85
  428.5 32.5 %collective-permute-start.52 = (bf16[128,2048]{1,0:T(8,128)(2,1)}, bf16[128,2048]{1,0:T(8,128)(2,1)}, u32[]{:S(2)}, u32[]{:S(2)}) collective-permute-start(bf16[128,2048]{1,0:T(8,128)(2,1)} %get-tuple-element.94), channel_id=1, source_target_pairs={{0,2},{2,0},{4,6},{6,4},{8,10},{10,8},{12,14},{14,12},{1,3},{3,1},... | collective-permute-start | bytes 1572872 | tf_op jit(solution)/shard_map/ppermute | solution.py:85
  431.5 26.4 %collective-permute-start.44 = (bf16[128,2048]{1,0:T(8,128)(2,1)}, bf16[128,2048]{1,0:T(8,128)(2,1)}, u32[]{:S(2)}, u32[]{:S(2)}) collective-permute-start(bf16[128,2048]{1,0:T(8,128)(2,1)} %get-tuple-element.97), channel_id=1, source_target_pairs={{0,2},{2,0},{4,6},{6,4},{8,10},{10,8},{12,14},{14,12},{1,3},{3,1},... | collective-permute-start | bytes 1572872 | tf_op jit(solution)/shard_map/ppermute | solution.py:85
  434.1 206.0 %reduce-scatter.4.cloned.1.call-start = ((), (), s32[]{:S(2)}) async-start(), calls=%async_computation.3 | async-start | bytes 3538944
  446.2 33.3 %collective-permute-start.43 = (bf16[128,2048]{1,0:T(8,128)(2,1)}, bf16[128,2048]{1,0:T(8,128)(2,1)S(1)}, u32[]{:S(2)}, u32[]{:S(2)}) collective-permute-start(bf16[128,2048]{1,0:T(8,128)(2,1)} %get-tuple-element.98), channel_id=1, source_target_pairs={{0,2},{2,0},{4,6},{6,4},{8,10},{10,8},{12,14},{14,12},{1,3},{3,1},... | collective-permute-start | bytes 1572872 | tf_op jit(solution)/shard_map/ppermute | solution.py:85
  451.7 103.3 %collective-permute-start.32 = (f32[16,32,1024]{2,1,0:T(8,128)}, f32[16,32,1024]{2,1,0:T(8,128)}, u32[]{:S(2)}, u32[]{:S(2)}) collective-permute-start(f32[16,32,1024]{2,1,0:T(8,128)} %pad_maximum_fusion.1), channel_id=1, source_target_pairs={{0,1},{17,16},{2,3},{19,18},{4,5},{21,20},{6,7},{23,22},{8,9},{25,... | collective-permute-start | bytes 6291464 | tf_op jit(solution)/shard_map/ppermute | solution.py:650
  458.0 18.0 %collective-permute-start.54 = (bf16[128,2048]{1,0:T(8,128)(2,1)}, bf16[128,2048]{1,0:T(8,128)(2,1)S(1)}, u32[]{:S(2)}, u32[]{:S(2)}) collective-permute-start(bf16[128,2048]{1,0:T(8,128)(2,1)} %add_convert_fusion.3), channel_id=1, source_target_pairs={{0,4},{2,6},{4,8},{6,10},{8,12},{10,14},{12,0},{14,2},{1,5},{3,7},... | collective-permute-start | bytes 1572872 | tf_op jit(solution)/shard_map/ppermute | solution.py:87
  460.1 27.2 %collective-permute-start.45 = (bf16[128,2048]{1,0:T(8,128)(2,1)}, bf16[128,2048]{1,0:T(8,128)(2,1)}, u32[]{:S(2)}, u32[]{:S(2)}) collective-permute-start(bf16[128,2048]{1,0:T(8,128)(2,1)} %add_convert_fusion.7), channel_id=1, source_target_pairs={{0,4},{2,6},{4,8},{6,10},{8,12},{10,14},{12,0},{14,2},{1,5},{3,7},... | collective-permute-start | bytes 1572872 | tf_op jit(solution)/shard_map/ppermute | solution.py:87
  461.0 85.2 %collective-permute-start.51 = (bf16[128,2048]{1,0:T(8,128)(2,1)}, bf16[128,2048]{1,0:T(8,128)(2,1)}, u32[]{:S(2)}, u32[]{:S(2)}) collective-permute-start(bf16[128,2048]{1,0:T(8,128)(2,1)} %get-tuple-element.95), channel_id=1, source_target_pairs={{0,2},{2,0},{4,6},{6,4},{8,10},{10,8},{12,14},{14,12},{1,3},{3,1},... | collective-permute-start | bytes 1572872 | tf_op jit(solution)/shard_map/ppermute | solution.py:85
  476.8 73.9 %collective-permute-start.42 = (bf16[128,2048]{1,0:T(8,128)(2,1)}, bf16[128,2048]{1,0:T(8,128)(2,1)S(1)}, u32[]{:S(2)}, u32[]{:S(2)}) collective-permute-start(bf16[128,2048]{1,0:T(8,128)(2,1)} %get-tuple-element.99), channel_id=1, source_target_pairs={{0,2},{2,0},{4,6},{6,4},{8,10},{10,8},{12,14},{14,12},{1,3},{3,1},... | collective-permute-start | bytes 1572872 | tf_op jit(solution)/shard_map/ppermute | solution.py:85
  479.5 67.6 %collective-permute-start.55 = (bf16[128,2048]{1,0:T(8,128)(2,1)}, bf16[128,2048]{1,0:T(8,128)(2,1)}, u32[]{:S(2)}, u32[]{:S(2)}) collective-permute-start(bf16[128,2048]{1,0:T(8,128)(2,1)} %add_convert_fusion.2), channel_id=1, source_target_pairs={{0,4},{2,6},{4,8},{6,10},{8,12},{10,14},{12,0},{14,2},{1,5},{3,7},... | collective-permute-start | bytes 1572872 | tf_op jit(solution)/shard_map/ppermute | solution.py:87
  489.5 62.4 %collective-permute-start.46 = (bf16[128,2048]{1,0:T(8,128)(2,1)}, bf16[128,2048]{1,0:T(8,128)(2,1)S(1)}, u32[]{:S(2)}, u32[]{:S(2)}) collective-permute-start(bf16[128,2048]{1,0:T(8,128)(2,1)} %add_convert_fusion.6), channel_id=1, source_target_pairs={{0,4},{2,6},{4,8},{6,10},{8,12},{10,14},{12,0},{14,2},{1,5},{3,7},... | collective-permute-start | bytes 1572872 | tf_op jit(solution)/shard_map/ppermute | solution.py:87
  546.2 19.4 %collective-permute-start.50 = (bf16[128,2048]{1,0:T(8,128)(2,1)}, bf16[128,2048]{1,0:T(8,128)(2,1)}, u32[]{:S(2)}, u32[]{:S(2)}) collective-permute-start(bf16[128,2048]{1,0:T(8,128)(2,1)} %get-tuple-element.92), channel_id=1, source_target_pairs={{0,2},{2,0},{4,6},{6,4},{8,10},{10,8},{12,14},{14,12},{1,3},{3,1},... | collective-permute-start | bytes 1572872 | tf_op jit(solution)/shard_map/ppermute | solution.py:85
  547.1 37.6 %collective-permute-start.41 = (bf16[128,2048]{1,0:T(8,128)(2,1)}, bf16[128,2048]{1,0:T(8,128)(2,1)}, u32[]{:S(2)}, u32[]{:S(2)}) collective-permute-start(bf16[128,2048]{1,0:T(8,128)(2,1)} %get-tuple-element.96), channel_id=1, source_target_pairs={{0,2},{2,0},{4,6},{6,4},{8,10},{10,8},{12,14},{14,12},{1,3},{3,1},... | collective-permute-start | bytes 1572872 | tf_op jit(solution)/shard_map/ppermute | solution.py:85
  550.7 25.8 %collective-permute-start.56 = (bf16[128,2048]{1,0:T(8,128)(2,1)}, bf16[128,2048]{1,0:T(8,128)(2,1)}, u32[]{:S(2)}, u32[]{:S(2)}) collective-permute-start(bf16[128,2048]{1,0:T(8,128)(2,1)} %add_convert_fusion.1), channel_id=1, source_target_pairs={{0,4},{2,6},{4,8},{6,10},{8,12},{10,14},{12,0},{14,2},{1,5},{3,7},... | collective-permute-start | bytes 1572872 | tf_op jit(solution)/shard_map/ppermute | solution.py:87
  554.0 41.9 %collective-permute-start.47 = (bf16[128,2048]{1,0:T(8,128)(2,1)}, bf16[128,2048]{1,0:T(8,128)(2,1)}, u32[]{:S(2)}, u32[]{:S(2)}) collective-permute-start(bf16[128,2048]{1,0:T(8,128)(2,1)} %add_convert_fusion.5), channel_id=1, source_target_pairs={{0,4},{2,6},{4,8},{6,10},{8,12},{10,14},{12,0},{14,2},{1,5},{3,7},... | collective-permute-start | bytes 1572872 | tf_op jit(solution)/shard_map/ppermute | solution.py:87
  557.6 26.6 %collective-permute-start.38 = (f32[6,1024]{1,0:T(8,128)S(1)}, f32[6,1024]{1,0:T(8,128)S(1)}, u32[]{:S(2)}, u32[]{:S(2)}) collective-permute-start(f32[6,1024]{1,0:T(8,128)S(1)} %reshape.180), channel_id=1, source_target_pairs={{0,2},{2,0},{4,6},{6,4},{8,10},{10,8},{12,14},{14,12},{1,3},{3,1},... | collective-permute-start | bytes 73736 | tf_op jit(solution)/shard_map/ppermute | solution.py:94
  578.9 32.8 %collective-permute-start.57 = (bf16[128,2048]{1,0:T(8,128)(2,1)}, bf16[128,2048]{1,0:T(8,128)(2,1)}, u32[]{:S(2)}, u32[]{:S(2)}) collective-permute-start(bf16[128,2048]{1,0:T(8,128)(2,1)} %add_convert_fusion), channel_id=1, source_target_pairs={{0,0},{1,16},{16,1},{17,17},{2,2},{3,18},{18,3},{19,19},{4,4},{5,2... | collective-permute-start | bytes 1572872 | tf_op jit(solution)/shard_map/ppermute | solution.py:35
  584.3 19.4 %collective-permute-start.39 = (f32[6,1024]{1,0:T(8,128)S(1)}, f32[6,1024]{1,0:T(8,128)S(1)}, u32[]{:S(2)}, u32[]{:S(2)}) collective-permute-start(f32[6,1024]{1,0:T(8,128)S(1)} %add.303), channel_id=1, source_target_pairs={{0,4},{2,6},{4,0},{6,2},{8,12},{10,14},{12,8},{14,10},{1,5},{3,7},... | collective-permute-start | bytes 73736 | tf_op jit(solution)/shard_map/ppermute | solution.py:100
  598.3 16.2 %collective-permute-start.48 = (bf16[128,2048]{1,0:T(8,128)(2,1)}, bf16[128,2048]{1,0:T(8,128)(2,1)}, u32[]{:S(2)}, u32[]{:S(2)}) collective-permute-start(bf16[128,2048]{1,0:T(8,128)(2,1)} %add_convert_fusion.4), channel_id=1, source_target_pairs={{0,0},{1,16},{16,1},{17,17},{2,2},{3,18},{18,3},{19,19},{4,4},{5,2... | collective-permute-start | bytes 1572872 | tf_op jit(solution)/shard_map/ppermute | solution.py:35
  603.7 5.5 collective-permute-start.40
  609.2 2.4 collective-permute-start.58
  (53 other events, 705.4 us)
Sparse Core Ops, SparseCore 0:
  13.3 100.8 all-gather.1
  434.2 109.8 all-reduce.5
  548.2 91.8 reduce-scatter.3

commit v2 on v1

--- a/solution.py
+++ b/solution.py
@@ -1,3 +1,5 @@
+import functools
+
 import jax
 import jax.numpy as jnp
 from jax import lax
@@ -35,99 +37,98 @@
     return lax.ppermute(array, ("section", "mp"), corner_swap)
 
 
+def tie(value, *others):
+    return lax.optimization_barrier((value,) + others)[0]
+
+
+def cut(array, block, rows):
+    return lax.dynamic_slice_in_dim(array, block * rows, rows, axis=0)
+
+
 class Ring:
     def __init__(self, dp):
         self.dp = dp
         self.outer = dp // 2
-        self.small = dp % 2 == 0 and self.outer <= 4
+        self.short = dp % 2 == 0 and self.outer == 4
         pairs = [(z, x) for z in range(self.outer) for x in range(2)]
         self.pair = [(2 * z + x, 2 * z + 1 - x) for z, x in pairs]
         self.ring = [(2 * z + x, 2 * ((z + 1) % self.outer) + x) for z, x in pairs]
-
-    def gather(self, shards):
-        if not self.small:
-            return [lax.all_gather(a, "dp", axis=0, tiled=True) for a in shards]
         place = lax.axis_index("dp")
-        z, x = place // 2, place % 2
-        held = list(shards)
-        got = [[] for _ in shards]
-        for k in range(self.outer):
-            for i in range(len(shards)):
-                got[i].append((k, held[i], lax.ppermute(held[i], "dp", self.pair)))
-                if k < self.outer - 1:
-                    held[i] = lax.ppermute(held[i], "dp", self.ring)
-        whole = []
-        for i, shard in enumerate(shards):
-            r, c = shard.shape
-            full = jnp.zeros((self.dp * r, c), shard.dtype)
-            for k, own, other in got[i]:
-                at = lax.rem(z - k + self.outer, self.outer)
-                full = lax.dynamic_update_slice(full, own, ((at * 2 + x) * r, 0))
-                full = lax.dynamic_update_slice(full, other, ((at * 2 + 1 - x) * r, 0))
-            whole.append(full)
-        return whole
-
-    def scatter(self, totals):
-        if not self.small:
-            return [
-                lax.psum_scatter(g, "dp", scatter_dimension=0, tiled=True).astype(wide)
-                for g in totals
-            ]
-        place = lax.axis_index("dp")
-        z, x = place // 2, place % 2
-        sums = [None] * len(totals)
-        for j in range(1, self.outer + 1):
-            for i, g in enumerate(totals):
-                r = g.shape[0] // self.dp
-                at = lax.rem(z - j + self.outer, self.outer)
-                mine = lax.dynamic_slice(g, ((at * 2 + x) * r, 0), (r, g.shape[1]))
-                theirs = lax.dynamic_slice(g, ((at * 2 + 1 - x) * r, 0), (r, g.shape[1]))
-                total = mine.astype(wide) + lax.ppermute(theirs, "dp", self.pair).astype(wide)
-                if sums[i] is not None:
-                    total = total + lax.ppermute(sums[i], "dp", self.ring).astype(wide)
-                sums[i] = total.astype(low) if j < self.outer else total
-        return sums
-
-    def total(self, array):
-        if not self.small:
-            return lax.psum(array, "dp")
-        array = array + lax.ppermute(array, "dp", self.pair)
-        step = 1
-        while step < self.outer:
-            hop = [
-                (2 * z + x, 2 * (z ^ step) + x) for z in range(self.outer) for x in range(2)
-            ]
-            array = array + lax.ppermute(array, "dp", hop)
-            step *= 2
-        return array
+        self.z, self.x = place // 2, place % 2
+
+    def across(self, array):
+        return lax.ppermute(array, "dp", self.pair)
+
+    def onward(self, array):
+        return lax.ppermute(array, "dp", self.ring)
+
+    def back(self, k):
+        return lax.rem(self.z - k + self.outer, self.outer)
+
+    def part(self, group, block, rows):
+        return jnp.concatenate([cut(a, block, rows) for a in group], axis=1)
+
+
+def halves(array, height):
+    array = array.reshape(height, -1)
+    upper = array.astype(low)
+    lower = (array - upper.astype(wide)).astype(low)
+    return jnp.pad(
+        jnp.concatenate([upper, lower], axis=1), ((0, 0), (0, -2 * array.shape[1] % 128))
+    )
+
+
+def joined(array, count):
+    return array[:, :count].astype(wide) + array[:, count : 2 * count].astype(wide)
 
 
 def sigmoid(x):
     return 0.5 * jnp.tanh(0.5 * x) + 0.5
 
 
-def forward_kernel(
-    side, z_own, z_other, w_own, w_other, b_own, b_other,
-    quarters, before, gates, cells,
-    z, w, b, state, cell, sems,
-):
-    steps, rows, wide_half = z_own.shape
+def fetch(blocks, places, side_blocks, target, sems, first=0):
+    wide_half = target.shape[1] // 2
+    columns = pl.ds(pl.multiple_of(side_blocks * wide_half, wide_half), wide_half)
+    copies = []
+    for k, block in enumerate(blocks):
+        height = block.shape[0]
+        span = pl.ds(pl.multiple_of(places[1 + k] * height, height), height)
+        copies.append(
+            pltpu.make_async_copy(
+                block.at[:, :wide_half], target.at[span, columns], sems.at[first + k]
+            )
+        )
+    return copies
+
+
+def forward_kernel(count, places, normed, b_own, b_other, *refs):
+    in_own, in_other, w_own, w_other = [refs[n * count : (n + 1) * count] for n in range(4)]
+    quarters, before, gates, cells, wi, w, b, state, cell, sems = refs[4 * count :]
+    steps, rows, wide_full = gates.shape
+    wide_half = wide_full // 2
     unit_half = wide_half // 4
     chunk = min(256, unit_half)
-    s = side[0]
-    copies = []
-    for n, (src_z, src_w, src_b, at) in enumerate(
-        ((z_own, w_own, b_own, s), (z_other, w_other, b_other, 1 - s))
-    ):
-        columns = pl.ds(pl.multiple_of(at * wide_half, wide_half), wide_half)
-        copies.append(pltpu.make_async_copy(src_w, w.at[:, columns], sems.at[n]))
-        copies.append(pltpu.make_async_copy(src_z, z.at[:, :, columns], sems.at[2 + n]))
-        b[:, columns] = src_b[...]
-    for copy in copies:
+    s = places[0]
+    copies = fetch(in_own, places, s, wi, sems) + fetch(in_other, places, 1 - s, wi, sems, count)
+    later = fetch(w_own, places, s, w, sems, 2 * count)
+    later += fetch(w_other, places, 1 - s, w, sems, 3 * count)
+    for copy in copies + later:
         copy.start()
+    for source, at in ((b_own, s), (b_other, 1 - s)):
+        b[:, pl.ds(pl.multiple_of(at * wide_half, wide_half), wide_half)] = source[...]
     state[...] = jnp.zeros_like(state)
     cell[...] = jnp.zeros_like(cell)
     for copy in copies:
+        copy.wait()
+
+    def project(g, carried):
+        cols = pl.ds(pl.multiple_of(g * unit_half, unit_half), unit_half)
+        value = jnp.dot(normed[...], wi[:, cols], preferred_element_type=wide) + b[:, cols]
+        gates[:, :, cols] = value.reshape(steps, rows, unit_half)
+        return carried
+
+    lax.fori_loop(0, 8, project, 0)
+    for copy in later:
         copy.wait()
     eighth = rows // 2
 
@@ -139,10 +140,8 @@
             acts = []
             for g in range(4):
                 cols = pl.ds(half * wide_half + g * unit_half + inside, chunk)
-                value = (
-                    z[t, :, cols]
-                    + jnp.dot(hidden, w[:, cols], preferred_element_type=wide)
-                    + b[:, cols]
+                value = gates[t, :, cols] + jnp.dot(
+                    hidden, w[:, cols], preferred_element_type=wide
                 )
                 value = jnp.tanh(value) if g == 2 else sigmoid(value)
                 gates[t, :, cols] = value
@@ -160,49 +159,67 @@
     lax.fori_loop(0, steps, advance, 0)
 
 
-def run_forward(side, z_own, z_other, w_own, w_other, b_own, b_other):
-    steps, rows, wide_half = z_own.shape
-    units = w_own.shape[0]
+def run_forward(places, normed, b_own, b_other, in_own, in_other, w_own, w_other, steps):
+    rows = normed.shape[0] // steps
+    units = normed.shape[1]
+    wide_half = b_own.shape[1]
+    count = len(w_own)
     return pl.pallas_call(
-        forward_kernel,
+        functools.partial(forward_kernel, count),
         out_shape=(
             jax.ShapeDtypeStruct((2, steps, rows // 2, units), low),
             jax.ShapeDtypeStruct((steps, rows, units), low),
             jax.ShapeDtypeStruct((steps, rows, 2 * wide_half), wide),
             jax.ShapeDtypeStruct((steps, rows, units), wide),
         ),
-        in_specs=[in_smem] + [in_place] * 4 + [in_vmem] * 2,
+        in_specs=[in_smem] + [in_vmem] * 3 + [in_place] * (4 * count),
         out_specs=[in_vmem] * 4,
         scratch_shapes=[
-            pltpu.VMEM((steps, rows, 2 * wide_half), wide),
+            pltpu.VMEM((units, 2 * wide_half), low),
             pltpu.VMEM((units, 2 * wide_half), low),
             pltpu.VMEM((1, 2 * wide_half), wide),
             pltpu.VMEM((rows, units), low),
             pltpu.VMEM((rows, units), wide),
-            pltpu.SemaphoreType.DMA((4,)),
+            pltpu.SemaphoreType.DMA((4 * count,)),
         ],
         compiler_params=pltpu.CompilerParams(vmem_limit_bytes=56 << 20),
         name="recur_forward",
-    )(side, z_own, z_other, w_own, w_other, b_own, b_other)
-
-
-def backward_kernel(side, outside, gates, cells, t_own, t_other, dz, w, dh, dc, sems):
+    )(places, normed, b_own, b_other, *in_own, *in_other, *w_own, *w_other)
+
+
+def backward_kernel(count, places, outside, gates, cells, *refs):
+    w_own, w_other = refs[:count], refs[count : 2 * count]
+    dz, stage, w, dh, dc, sems = refs[2 * count :]
     steps, rows, wide_full = gates.shape
     wide_half = wide_full // 2
     unit_half = wide_half // 4
     chunk = min(256, unit_half)
-    eighth = rows // 2
-    s = side[0]
-    copies = []
-    for n, (src, at) in enumerate(((t_own, s), (t_other, 1 - s))):
-        span = pl.ds(pl.multiple_of(at * wide_half, wide_half), wide_half)
-        copies.append(pltpu.make_async_copy(src, w.at[span, :], sems.at[n]))
-    for copy in copies:
-        copy.start()
+    s = places[0]
+    jobs = []
+    for n, (sources, at) in enumerate(((w_own, s), (w_other, 1 - s))):
+        for k, block in enumerate(sources):
+            slot = n * count + k
+            copy = pltpu.make_async_copy(
+                block.at[:, :wide_half], stage.at[slot], sems.at[slot]
+            )
+            copy.start()
+            jobs.append((copy, slot, at, places[1 + k] * block.shape[0]))
     dh[...] = jnp.zeros_like(dh)
     dc[...] = jnp.zeros_like(dc)
-    for copy in copies:
+    height = w_own[0].shape[0]
+    piece = min(height, 128)
+    for copy, slot, at, first in jobs:
         copy.wait()
+
+        def turn(g, carried, slot=slot, at=at, first=first):
+            columns = pl.ds(pl.multiple_of(g * unit_half, unit_half), unit_half)
+            span = pl.ds(pl.multiple_of(at * wide_half + g * unit_half, unit_half), unit_half)
+            for low_row in range(0, height, piece):
+                into = pl.ds(pl.multiple_of(first + low_row, piece), piece)
+                w[span, into] = stage[slot, low_row : low_row + piece, columns].T
+            return carried
+
+        lax.fori_loop(0, 4, turn, 0)
 
     def retreat(k, carried):
         t = steps - 1 - k
@@ -241,23 +258,69 @@
     lax.fori_loop(0, steps, retreat, 0)
 
 
-def run_backward(side, outside, gates, cells, t_own, t_other):
+def run_backward(places, outside, gates, cells, w_own, w_other):
     steps, rows, wide_full = gates.shape
     units = cells.shape[2]
+    count = len(w_own)
     return pl.pallas_call(
-        backward_kernel,
+        functools.partial(backward_kernel, count),
         out_shape=jax.ShapeDtypeStruct((2, steps, rows, wide_full // 2), low),
-        in_specs=[in_smem] + [in_vmem] * 3 + [in_place] * 2,
+        in_specs=[in_smem] + [in_vmem] * 3 + [in_place] * (2 * count),
         out_specs=in_vmem,
         scratch_shapes=[
+            pltpu.VMEM((2 * count, units // count, wide_full // 2), low),
             pltpu.VMEM((wide_full, units), low),
             pltpu.VMEM((rows, units), wide),
             pltpu.VMEM((rows, units), wide),
-            pltpu.SemaphoreType.DMA((2,)),
+            pltpu.SemaphoreType.DMA((2 * count,)),
         ],
         compiler_params=pltpu.CompilerParams(vmem_limit_bytes=56 << 20),
         name="recur_backward",
-    )(side, outside, gates, cells, t_own, t_other)
+    )(places, outside, gates, cells, *w_own, *w_other)
+
+
+def input_kernel(count, places, inputs, gain, dz, *refs):
+    in_own, in_other = refs[:count], refs[count : 2 * count]
+    grad_inputs, grad_gain, wi, sems = refs[2 * count :]
+    s = places[0]
+    copies = fetch(in_own, places, s, wi, sems) + fetch(in_other, places, 1 - s, wi, sems, count)
+    for copy in copies:
+        copy.start()
+    x = inputs[...].astype(wide)
+    centred = x - jnp.mean(x, axis=-1, keepdims=True)
+    scale = lax.rsqrt(jnp.mean(centred * centred, axis=-1, keepdims=True) + epsilon)
+    shape = centred * scale
+    for copy in copies:
+        copy.wait()
+    wide_half = wi.shape[1] // 2
+    grad = dot_nt(dz[0], wi[:, :wide_half]) + dot_nt(dz[1], wi[:, wide_half:])
+    grad_gain[...] = jnp.sum(grad * shape, axis=0, keepdims=True)
+    pulled = grad * gain[...]
+    grad_inputs[...] = scale * (
+        pulled
+        - jnp.mean(pulled, axis=-1, keepdims=True)
+        - shape * jnp.mean(pulled * shape, axis=-1, keepdims=True)
+    )
+
+
+def run_input(places, inputs, gain, dz, in_own, in_other):
+    count = len(in_own)
+    rows, width = inputs.shape
+    return pl.pallas_call(
+        functools.partial(input_kernel, count),
+        out_shape=(
+            jax.ShapeDtypeStruct((rows, width), wide),
+            jax.ShapeDtypeStruct((1, width), wide),
+        ),
+        in_specs=[in_smem] + [in_vmem] * 3 + [in_place] * (2 * count),
+        out_specs=[in_vmem] * 2,
+        scratch_shapes=[
+            pltpu.VMEM((width, 2 * dz.shape[2]), low),
+            pltpu.SemaphoreType.DMA((2 * count,)),
+        ],
+        compiler_params=pltpu.CompilerParams(vmem_limit_bytes=56 << 20),
+        name="input_back",
+    )(places, inputs, gain, dz, *in_own, *in_other)
 
 
 def dot_nt(a, b):
@@ -269,21 +332,36 @@
 
 
 def attend_kernel(
-    memory, decoded, w0, w1, w2, w3, v0, v1, v2, v3, vectors, vocab_bias, noise, lengths,
-    labels, counted,
-    grad_memory, grad_decoded, pack, seen, sums,
-    w, v, sems, mk, sk, mq, sq, mono, span, keep, queue, scaled, ratio, window, mix, pre,
+    count, places, memory, decoded, vectors, vocab_bias, noise, lengths, labels, counted, *refs
 ):
+    small, vocab = refs[: 4 * count], refs[4 * count : 4 * count + 4]
+    (
+        grad_memory, grad_decoded, pack, seen, sums,
+        w, v, sems, v_sems, mk, sk, mq, sq, mono, span, keep, queue, scaled, ratio, window, mix, pre,
+    ) = refs[4 * count + 4 :]
     rows, _ = memory.shape
     frames, group, _ = mk.shape
     block = w.shape[2] // 6
     lanes = 128
     chunks = 4 * block // lanes
-    copies = [pltpu.make_async_copy(src, w.at[r], sems.at[r]) for r, src in enumerate((w0, w1, w2, w3))]
-    copies += [
-        pltpu.make_async_copy(src, v.at[r], sems.at[4 + r]) for r, src in enumerate((v0, v1, v2, v3))
-    ]
-    for copy in copies:
+    copies = []
+    for r in range(4):
+        arrived = []
+        for k in range(count):
+            source = small[r * count + k]
+            height = source.shape[0]
+            for h in range(source.shape[1] // (6 * block)):
+                to = pl.ds(pl.multiple_of(places[1 + len(arrived)] * height, height), height)
+                arrived.append(
+                    pltpu.make_async_copy(
+                        source.at[:, 6 * block * h : 6 * block * (h + 1)],
+                        w.at[r, to, :],
+                        sems.at[r, len(arrived)],
+                    )
+                )
+        copies.append(arrived)
+    vocab_copies = [pltpu.make_async_copy(vocab[r], v.at[r], v_sems.at[r]) for r in range(4)]
+    for copy in sum(copies, []) + vocab_copies:
         copy.start()
 
     def split(value):
@@ -291,7 +369,8 @@
 
     mem, dec = memory[...], decoded[...]
     for r in range(4):
-        copies[r].wait()
+        for copy in copies[r]:
+            copy.wait()
         cols = pl.ds(r * block, block)
         keys = jnp.dot(mem, w[r, :, : 2 * block], preferred_element_type=wide)
         queries = jnp.dot(dec, w[r, :, 2 * block : 5 * block], preferred_element_type=wide)
@@ -379,7 +458,7 @@
         pack[r, :, 5 * block :] = value.astype(low)
     logits = vocab_bias[...]
     for r in range(4):
-        copies[4 + r].wait()
+        vocab_copies[r].wait()
         logits = logits + jnp.dot(pack[r, :, 5 * block :], v[r], preferred_element_type=wide)
     shifted = jnp.exp(logits - jnp.max(logits, axis=-1, keepdims=True))
     softmax = shifted / jnp.sum(shifted, axis=-1, keepdims=True)
@@ -511,14 +590,18 @@
     grad_decoded[...] = total_decoded
 
 
-def run_attend(memory, decoded, weights, vocab, vectors, vocab_bias, noise, lengths, labels, counted, frames):
+def run_attend(
+    places, memory, decoded, smalls, vocab, vectors, vocab_bias, noise, lengths, labels, counted,
+    frames,
+):
     rows, width = memory.shape
     group = rows // frames
-    full = weights[0].shape[1] // 6 * 4
+    full = vectors.shape[1]
     vocab_width = vocab[0].shape[1]
     cell = (frames * frames, group, 128)
+    count = len(smalls[0])
     return pl.pallas_call(
-        attend_kernel,
+        functools.partial(attend_kernel, count),
         out_shape=(
             jax.ShapeDtypeStruct((rows, width), wide),
             jax.ShapeDtypeStruct((rows, width), wide),
@@ -526,19 +609,23 @@
             jax.ShapeDtypeStruct((2, rows, vocab_width), low),
             jax.ShapeDtypeStruct((8, full), wide),
         ),
-        in_specs=[in_vmem] * 2 + [in_place] * 8 + [in_vmem] * 6,
+        in_specs=[in_smem] + [in_vmem] * 8 + [in_place] * (4 * count + 4),
         out_specs=[in_vmem] * 5,
         scratch_shapes=[
-            pltpu.VMEM((4,) + weights[0].shape, low),
+            pltpu.VMEM((4, width, full // 4 * 6), low),
             pltpu.VMEM((4,) + vocab[0].shape, low),
-            pltpu.SemaphoreType.DMA((8,)),
+            pltpu.SemaphoreType.DMA((4, places.shape[0] - 1)),
+            pltpu.SemaphoreType.DMA((4,)),
         ]
         + [pltpu.VMEM((frames, group, full), wide)] * 4
         + [pltpu.VMEM(cell, wide)] * 7
         + [pltpu.VMEM((frames, group, 128), wide), pltpu.VMEM((rows, full), wide)],
         compiler_params=pltpu.CompilerParams(vmem_limit_bytes=56 << 20),
         name="attend",
-    )(memory, decoded, *weights, *vocab, vectors, vocab_bias, noise, lengths, labels, counted)
+    )(
+        places, memory, decoded, vectors, vocab_bias, noise, lengths, labels, counted,
+        *sum(smalls, []), *vocab,
+    )
 
 
 def local(
@@ -549,9 +636,9 @@
 ):
     ring = Ring(dp)
     s, y = lax.axis_index("section"), lax.axis_index("mp")
-    side = s.reshape(1).astype(jnp.int32)
     _, utts, frames, width = block_input.shape
     half, quarter = utts // 2, utts // 4
+    rows = frames * quarter
     shard_rows, _, unit_half = lstm_in.shape[1:]
     wide_half = 4 * unit_half
     block = mono_mem.shape[1]
@@ -563,47 +650,17 @@
     b_own = corners(lstm_bias[0].reshape(1, wide_half)).astype(wide)
     b_other = across_cores(b_own)
 
-    inputs = jnp.swapaxes(block_input[0], 0, 1).astype(wide)
-    normed, norm_pullback = jax.vjp(normalize, inputs, norm_gain[0])
-    normed_low = normed.astype(low)
-    normed_section = jnp.where(s == y, normed_low, across_cores(normed_low))
-    normed_own = lax.dynamic_slice_in_dim(normed_section, s * half, half, axis=1)
-    normed_other = lax.dynamic_slice_in_dim(normed_section, (1 - s) * half, half, axis=1)
-    normed_own = normed_own.reshape(frames * half, width)
-    normed_other = normed_other.reshape(frames * half, width)
-
-    shards = jnp.concatenate(
-        [mono_mem, span_mem, mono_dec, span_dec, out_weight[0], out_weight[1]], axis=1
-    )
-    weight_own = lax.all_gather(shards, "dp", axis=0, tiled=True)
-    weight_chip = across_chips(weight_own)
-    weights = [weight_own, weight_chip, across_cores(weight_own), across_cores(weight_chip)]
-    vocab_own = jnp.pad(vocab_weight, ((0, 0), (0, vocab_pad - vocab_size)))
-    vocab_chip = across_chips(vocab_own)
-    vocab = [vocab_own, vocab_chip, across_cores(vocab_own), across_cores(vocab_chip)]
-    vector_own = jnp.stack([mono_bias, mono_vec, span_bias, span_vec, out_bias])
-    vector_pair = jnp.concatenate([vector_own, across_chips(vector_own)], axis=1)
-    vectors = jnp.concatenate([vector_pair, across_cores(vector_pair)], axis=1)
-    vectors = jnp.pad(vectors, ((0, 3), (0, 0)))
-
-    in_own, rec_own = ring.gather([in_shard, rec_shard])
-    in_other = across_cores(in_own)
-    rec_other = across_cores(rec_own)
-
-    def project(weight):
-        value = jnp.dot(normed_own, weight, preferred_element_type=wide)
-        return value.reshape(frames, half, wide_half)
-
-    quarters, before, gates, cells = run_forward(
-        side, project(in_own), project(in_other), rec_own, rec_other, b_own, b_other
-    )
-
-    kept = lax.dynamic_index_in_dim(quarters, y, axis=0, keepdims=False)
-    given = lax.dynamic_index_in_dim(quarters, 1 - y, axis=0, keepdims=False)
-    taken = across_chips(given)
-    rows = frames * quarter
-    memory = jnp.where(y == 0, kept, taken).reshape(rows, width)
-    decoded = jnp.where(y == 0, taken, kept).reshape(rows, width)
+    def of_section(array):
+        return jnp.where(s == y, array, across_cores(array))
+
+    inputs = of_section(jnp.swapaxes(block_input[0], 0, 1))
+    gain = of_section(norm_gain[0])
+    inputs_own = lax.dynamic_slice_in_dim(inputs, s * half, half, axis=1)
+    inputs_other = lax.dynamic_slice_in_dim(inputs, (1 - s) * half, half, axis=1)
+    normed_own = normalize(inputs_own.astype(wide), gain)
+    normed_own = normed_own.astype(low).reshape(frames * half, width)
+    normed_other = normalize(inputs_other.astype(wide), gain)
+    normed_other = normed_other.astype(low).reshape(frames * half, width)
 
     start = s * half + y * quarter
     noise_part = jnp.transpose(
@@ -617,44 +674,124 @@
     counted = (jnp.arange(frames)[:, None] < count_part[None, :]).astype(wide).reshape(rows, 1)
     bias_row = jnp.pad(vocab_bias, (0, vocab_pad - vocab_size), constant_values=-1e30)[None]
 
+    vector_own = jnp.stack([mono_bias, mono_vec, span_bias, span_vec, out_bias])
+    vector_pair = jnp.concatenate([vector_own, across_chips(vector_own)], axis=1)
+    vectors = jnp.concatenate([vector_pair, across_cores(vector_pair)], axis=1)
+    vectors = jnp.pad(vectors, ((0, 3), (0, 0)))
+    vocab_own = jnp.pad(vocab_weight, ((0, 0), (0, vocab_pad - vocab_size)))
+    ready = (noise_part, length_part, label_part, counted, bias_row, normed_own, normed_other)
+    places, in_own, rec_own, small_own, small_chip = [], [], [], [], []
+    small = jnp.concatenate(
+        [mono_mem, span_mem, mono_dec, span_dec, out_weight[0], out_weight[1]], axis=1
+    )
+    if ring.short:
+        small_far, small_next = ring.across(small), ring.onward(small)
+        in_shard, rec_shard, b_own, small_far, small_next = lax.optimization_barrier(
+            (in_shard, rec_shard, b_own, small_far, small_next)
+        )
+        vocab_chip = across_chips(tie(vocab_own, in_shard))
+        small_own.append(jnp.concatenate([small, small_far], axis=1))
+        first = jnp.concatenate([in_shard, small_next], axis=1)
+        second = rec_shard
+        places = [ring.back(k // 2) * 2 + (ring.x if k % 2 == 0 else 1 - ring.x) for k in range(8)]
+        in_other, rec_other, small_core = [], [], []
+        earlier = ()
+        for k in range(ring.outer):
+            if k:
+                first = tie(first, *earlier, *ready)
+                ready = ()
+            earlier = (second,)
+            if k == 1:
+                earlier += (vocab_chip, vectors, b_other)
+            if k == 2:
+                earlier += (vocab[2], vocab[3])
+            in_other += [across_cores(part) for part in in_own[len(in_other) :]]
+            rec_other += [across_cores(part) for part in rec_own[len(rec_other) :]]
+            small_core += [across_cores(small_own[-1])]
+            small_chip += [across_chips(small_own[-1])]
+            if k:
+                earlier += (*in_other[-2:], *rec_other[-2:], small_core[-1], small_chip[-2])
+            if k == 1:
+                vocab = [vocab_own, vocab_chip, across_cores(vocab_own), across_cores(vocab_chip)]
+            far, far_rec = ring.across(first), ring.across(second)
+            in_own += [first, far]
+            rec_own += [second, far_rec]
+            earlier += (far, far_rec)
+            if k < ring.outer - 1:
+                small_own.append(
+                    jnp.concatenate([first[:, wide_half:], far[:, wide_half:]], axis=1)
+                )
+                first = ring.onward(first if k < ring.outer - 2 else first[:, :wide_half])
+                second = ring.onward(second)
+        in_other += [across_cores(part) for part in in_own[len(in_other) :]]
+        rec_other += [across_cores(part) for part in rec_own[len(rec_other) :]]
+    else:
+        vocab_chip = across_chips(vocab_own)
+        small, in_block, rec_block = [
+            lax.all_gather(a, "dp", axis=0, tiled=True) for a in (small, in_shard, rec_shard)
+        ]
+        places, in_own, rec_own = [jnp.int32(0)], [in_block], [rec_block]
+        small_own, small_chip = [small], [across_chips(small)]
+        vocab = [vocab_own, vocab_chip, across_cores(vocab_own), across_cores(vocab_chip)]
+        in_other, rec_other = [across_cores(in_block)], [across_cores(rec_block)]
+        small_core = [across_cores(small)]
+    places = jnp.stack([s] + places).astype(jnp.int32)
+    places = tie(places, vectors, *vocab, *ready, *small_chip[:-1], *small_core)
+
+    quarters, before, gates, cells = run_forward(
+        places, normed_own, b_own, b_other, in_own, in_other, rec_own, rec_other, frames
+    )
+
+    kept = lax.dynamic_index_in_dim(quarters, y, axis=0, keepdims=False)
+    given = lax.dynamic_index_in_dim(quarters, 1 - y, axis=0, keepdims=False)
+    taken = across_chips(given)
+    memory = jnp.where(y == 0, kept, taken).reshape(rows, width)
+    decoded = jnp.where(y == 0, taken, kept).reshape(rows, width)
+    small_both = [across_cores(part) for part in small_chip]
+    smalls = [small_own, small_chip, small_core, small_both]
     grad_memory, grad_decoded, pack, seen, sums = run_attend(
-        memory, decoded, weights, vocab, vectors, bias_row, noise_part, length_part,
+        places, memory, decoded, smalls, vocab, vectors, bias_row, noise_part, length_part,
         label_part, counted, frames,
     )
+    kept_far = across_chips(tie(kept, taken))
+    before = before.reshape(frames * half, width)
+    before_peer = across_cores(tie(before, taken))
 
     grad_kept = jnp.where(y == 0, grad_memory, grad_decoded)
     grad_given = jnp.where(y == 0, grad_decoded, grad_memory).astype(low)
-    grad_taken = across_chips(grad_given).astype(wide)
+    grad_taken = across_chips(grad_given)
     outside = jnp.stack(
         [jnp.where(y == 0, grad_kept, grad_taken), jnp.where(y == 0, grad_taken, grad_kept)]
     ).reshape(2, frames, quarter, width)
-    dz = run_backward(side, outside, gates, cells, rec_own.T, rec_other.T)
+    pack_core = across_cores(pack[2:4])
+    pack_out = jnp.stack([pack[1], pack_core[1]])
+    memory_next = jnp.where(y == 0, given, kept_far).reshape(rows, width)
+    decoded_next = jnp.where(y == 0, kept_far, given).reshape(rows, width)
+    states = jnp.stack([memory, memory_next, decoded, decoded_next])
+    states_core = across_cores(states)
+    blocks = sums[:5].reshape(5, 4, block)
+    vector_pair = blocks[:, :2] + across_cores(blocks[:, 2:])
+    bias_pair = sums[5] + across_cores(sums[5])
+    vector_out = jnp.concatenate([vector_pair[:, 1].reshape(-1), bias_pair])
+    places_back, pack_out, vector_out, states_core = lax.optimization_barrier(
+        (places, pack_out, vector_out, states_core, outside, before_peer)
+    )[:4]
+    dz = run_backward(places_back, outside, gates, cells, rec_own, rec_other)
 
     dz = dz.reshape(2, frames * half, wide_half)
     dz_kept = lax.dynamic_index_in_dim(dz, s, axis=0, keepdims=False)
     dz_given = lax.dynamic_index_in_dim(dz, 1 - s, axis=0, keepdims=False)
     dz_all = jnp.concatenate([dz_kept, across_cores(dz_given)], axis=0)
-    before = before.reshape(frames * half, width)
-    before_all = jnp.concatenate([before, across_cores(before)], axis=0)
+    before_all = jnp.concatenate([before, before_peer], axis=0)
     normed_all = jnp.concatenate([normed_own, normed_other], axis=0)
     rec_total = dot_tn(before_all, dz_all).astype(low)
     in_total = dot_tn(normed_all, dz_all).astype(low)
-    rec_grad, in_grad = ring.scatter([rec_total, in_total])
-
-    grad_part = dot_nt(dz_kept, in_own) + dot_nt(dz_given, in_other)
-    grad_part = grad_part.reshape(frames, half, width)
-    grad_peer = across_cores(grad_part)
-    grad_section = jnp.concatenate(
-        [jnp.where(s == 0, grad_part, grad_peer), jnp.where(s == 0, grad_peer, grad_part)], axis=1
-    )
-    grad_far = lax.ppermute(grad_section, ("section", "mp"), [(0, 1), (3, 2)])
-    grad_inputs, grad_gain = norm_pullback(jnp.where(s == y, grad_section, grad_far))
-
-    kept_far = across_chips(kept)
-    memory_next = jnp.where(y == 0, given, kept_far).reshape(rows, width)
-    decoded_next = jnp.where(y == 0, kept_far, given).reshape(rows, width)
-    states = jnp.stack([memory, memory_next, decoded, decoded_next])
-    states_core = across_cores(states)
+
+    pack_far = across_chips(pack_out)
+    seen_far = across_chips(tie(seen, pack_out))
+    vector_far = across_chips(vector_out)
+    seen_pair = jnp.concatenate([seen, seen_far], axis=0)
+    seen_core = across_cores(seen_pair)
 
     def gathered(n):
         return jnp.concatenate(
@@ -662,67 +799,148 @@
         )
 
     memory_all, decoded_all = gathered(0), gathered(2)
-    pack_core = across_cores(pack[2:4])
-    pack_far = across_chips(jnp.stack([pack[1], pack_core[1]]))
     pack_all = jnp.concatenate([pack[0], pack_core[0], pack_far[0], pack_far[1]], axis=0)
-    seen_pair = jnp.concatenate([seen, across_chips(seen)], axis=0)
-    seen_core = across_cores(seen_pair)
     seen_all = [
         jnp.concatenate([seen_pair[n], seen_core[n], seen_pair[2 + n], seen_core[2 + n]], axis=0)
         for n in range(2)
     ]
-    grads = jnp.concatenate(
-        [
-            dot_tn(memory_all, pack_all[:, : 2 * block]),
-            dot_tn(decoded_all, pack_all[:, 2 * block : 5 * block]),
-            dot_tn(seen_all[0], pack_all[:, 4 * block : 5 * block]),
-        ],
-        axis=1,
-    ).astype(low)
-    grads = lax.psum_scatter(grads, "dp", scatter_dimension=0, tiled=True).astype(wide)
-    vocab_grad = dot_tn(pack_all[:, 5 * block :], seen_all[1])[:, :vocab_size].astype(low)
-    vocab_grad = lax.psum(vocab_grad, "dp").astype(wide)
-
-    blocks = sums[:5].reshape(5, 4, block)
-    pair = blocks[:, :2] + across_cores(blocks[:, 2:])
-    vector_sum = pair[:, 0] + across_chips(pair[:, 1])
-    bias_sum = sums[5] + across_cores(sums[5])
-    bias_sum = bias_sum + across_chips(bias_sum)
-    lstm_bias_sum = jnp.sum(dz_all.astype(wide), axis=0)
-    flat = jnp.concatenate(
-        [
-            vector_sum.reshape(-1),
-            bias_sum,
-            lstm_bias_sum,
-            grad_gain.reshape(-1),
-        ]
-    )
-    flat = jnp.pad(flat, (0, -flat.shape[0] % 1024)).reshape(-1, 1024)
-    flat = ring.total(flat).reshape(-1)
-    ends = [5 * block, 5 * block + vocab_pad, 5 * block + vocab_pad + wide_half]
+    energy_total = [
+        dot_tn(memory_all, pack_all[:, : 2 * block]).astype(low),
+        dot_tn(decoded_all, pack_all[:, 2 * block : 4 * block]).astype(low),
+    ]
+    grad_pre = pack_all[:, 4 * block : 5 * block]
+    output_total = [
+        dot_tn(decoded_all, grad_pre).astype(low),
+        dot_tn(seen_all[0], grad_pre).astype(low),
+        dot_tn(seen_all[1], pack_all[:, 5 * block :]).astype(low),
+    ]
+
+    def input_back(dz):
+        grad_inputs, grad_gain = run_input(
+            places, inputs_own.reshape(frames * half, width), gain[None], dz, in_own, in_other
+        )
+        grad_inputs = jnp.swapaxes(grad_inputs.reshape(frames, half, width), 0, 1)
+        grad_peer = across_cores(grad_inputs)
+        section = jnp.concatenate(
+            [
+                jnp.where(s == 0, grad_inputs, grad_peer),
+                jnp.where(s == 0, grad_peer, grad_inputs),
+            ],
+            axis=0,
+        )
+        far = lax.ppermute(section, ("section", "mp"), [(0, 1), (3, 2)])
+        grad_gain = grad_gain.reshape(width)
+        gain_sum = grad_gain + across_cores(grad_gain)
+        flat = jnp.concatenate(
+            [
+                vector_pair[:, 0].reshape(-1) + vector_far[: 5 * block],
+                bias_pair + vector_far[5 * block :],
+                jnp.sum(dz_all.astype(wide), axis=0),
+                gain_sum,
+            ]
+        )
+        return section, far, jnp.pad(flat, (0, -flat.shape[0] % (2 * shard_rows)))
+
+    if ring.short:
+        r = shard_rows
+        back, x, onward, across = ring.back, ring.x, ring.onward, ring.across
+        chains = [[rec_total], [in_total], energy_total]
+        sums_so_far = [None] * 3
+        arrived, passed = {}, {}
+        held = flat_sum = None
+        for k in range(1, 5):
+            for n, group in enumerate(chains):
+                theirs = ring.part(group, back(k) * 2 + 1 - x, r)
+                if k > 2:
+                    theirs = tie(theirs, passed[n, k - 2], arrived[n, k - 1], passed[3, k - 2])
+                if k == 4:
+                    theirs = tie(theirs, grad_far)
+                arrived[n, k] = across(theirs)
+                total = ring.part(group, back(k) * 2 + x, r).astype(wide)
+                total = total + arrived[n, k].astype(wide)
+                if k > 1:
+                    total = total + passed[n, k - 1].astype(wide)
+                sums_so_far[n] = total
+                if k < 4:
+                    passed[n, k] = onward(total.astype(low))
+            if k == 1:
+                grad_section, grad_far, flat = input_back(tie(dz, arrived[0, 1]))
+                flat_sum = flat
+                flat_width = flat.shape[0] // (2 * r)
+                held = jnp.concatenate(
+                    [ring.part(output_total, back(1), 2 * r), halves(flat, 2 * r)], axis=1
+                )
+            if k < 4:
+                passed[3, k] = onward(held)
+                ours = ring.part(output_total, back(k + 1), 2 * r).astype(wide)
+                columns = ours.shape[1]
+                ours = (ours + passed[3, k][:, :columns].astype(wide)).astype(low)
+                flat_sum = flat_sum + joined(passed[3, k][:, columns:], flat_width).reshape(-1)
+                held = jnp.concatenate([ours, passed[3, k][:, columns:]], axis=1)
+        ours = held[:, :columns]
+        message = jnp.concatenate(
+            [cut(ours, 1 - x, r), halves(flat_sum, 2 * r).reshape(r, -1)], axis=1
+        )
+        message = across(tie(message, arrived[2, 3]))
+        output_grad = cut(ours, x, r).astype(wide) + message[:, :columns].astype(wide)
+        flat = flat_sum + joined(
+            message[:, columns:].reshape(2 * r, -1), flat_width
+        ).reshape(-1)
+        shard = output_grad[:, 2 * block :].astype(low)
+        held = jnp.concatenate([shard, across(shard)], axis=1)
+        vocab_grad = jnp.zeros((vocab_pad, block), low)
+        for k in range(4):
+            for n, at in enumerate((x, 1 - x)):
+                vocab_grad = lax.dynamic_update_slice(
+                    vocab_grad, held[:, n * block : (n + 1) * block], ((back(k) * 2 + at) * r, 0)
+                )
+            if k < 3:
+                held = onward(held)
+        rec_grad, in_grad, energy_grad = sums_so_far
+    else:
+        grad_section, grad_far, flat = input_back(dz)
+
+        def scatter(total):
+            return lax.psum_scatter(total, "dp", scatter_dimension=0, tiled=True).astype(wide)
+
+        rec_grad, in_grad = scatter(rec_total), scatter(in_total)
+        energy_grad = jnp.concatenate([scatter(a) for a in energy_total], axis=1)
+        output_grad = jnp.concatenate([scatter(a) for a in output_total], axis=1)
+        flat = lax.psum(flat, "dp")
+        vocab_grad = lax.all_gather(
+            output_grad[:, 2 * block :].astype(low), "dp", axis=0, tiled=True
+        )
+
+    input_grad = jnp.where(s == y, grad_section, grad_far)
+    vocab_grad = vocab_grad.T[:, :vocab_size].astype(wide)
+    ends = [5 * block, 5 * block + vocab_pad, 5 * block + vocab_pad + wide_half + width]
     vector_sum = flat[: ends[0]].reshape(5, block)
     bias_sum = flat[ends[0] : ends[0] + vocab_size]
-    lstm_bias_sum = corners(flat[ends[1] : ends[2]].reshape(4, unit_half))
-    gain_sum = flat[ends[2] : ends[2] + width]
-
+    moved = halves(flat[ends[1] : ends[2]], shard_rows)
+    moved = corners(jnp.concatenate([rec_grad.astype(low), moved], axis=1))
+    rec_grad = moved[:, :wide_half].astype(wide).reshape(1, shard_rows, 4, unit_half)
+    moved = joined(moved[:, wide_half:], (ends[2] - ends[1]) // shard_rows).reshape(-1)
+    lstm_bias_sum = moved[:wide_half].reshape(1, 4, unit_half)
+    gain_sum = moved[wide_half:][None]
     in_grad = corners(in_grad.astype(low)).astype(wide).reshape(1, shard_rows, 4, unit_half)
-    rec_grad = corners(rec_grad.astype(low)).astype(wide).reshape(1, shard_rows, 4, unit_half)
-    column = [grads[:, n * block : (n + 1) * block] for n in range(6)]
+    mono_mem_grad, span_mem_grad, mono_dec_grad, span_dec_grad = [
+        energy_grad[:, n * block : (n + 1) * block] for n in range(4)
+    ]
     return (
-        jnp.swapaxes(grad_inputs, 0, 1)[None],
-        gain_sum[None],
+        input_grad[None],
+        gain_sum,
         in_grad,
         rec_grad,
-        lstm_bias_sum[None],
-        column[0],
-        column[2],
+        lstm_bias_sum,
+        mono_mem_grad,
+        mono_dec_grad,
         vector_sum[0],
         vector_sum[1],
-        column[1],
-        column[3],
+        span_mem_grad,
+        span_dec_grad,
         vector_sum[2],
         vector_sum[3],
-        jnp.stack([column[4], column[5]]),
+        jnp.stack([output_grad[:, :block], output_grad[:, block : 2 * block]]),
         vector_sum[4],
         vocab_grad,
         bias_sum,

time: 662 us -> 549 us (0.83)
  starting transfers between devices: 147 us -> 71.9 us
  local copies, waits for them, and re-layouts: 86.3 us -> 64.3 us
  matrix products: 29.2 us -> 9.02 us
  Pallas kernels: 86.1 us -> 103 us
  between operations: 15.1 us -> 2.86 us
    ppermute x32 -> x46, waiting for transfers between devices: 124 us -> 193 us  [the longest x23 102 us: across(): return lax.ppermute(array, 'dp', self.pair)]
    ppermute x17 -> x39, starting transfers between devices: 75.4 us -> 8.4 us  [across_cores(): return lax.ppermute(array, 'section', core_swap)]
    psum x1 -> x0, waiting for transfers between devices: 54.3 us -> none  [local(): vocab_grad = lax.psum(vocab_grad, 'dp').astype(wide)]
    unnamed x4 -> x0, waiting for transfers between devices: 22.8 us -> none
    dynamic_update_slice x17 -> x8, local copies, waits for them, and re-layouts: 20.8 us -> 0.1 us  [local(): lax.dynamic_update_slice(vocab_grad, held[:, n * block:(n + 1) * block],...]
    dot_general x4 -> x0, matrix products: 17.4 us -> none  [the longest x2 9.57 us: project(): value = jnp.dot(normed_own, weight, preferred_element_type=wide)]
    pallas_call x3 -> x4, Pallas kernels: 86.1 us -> 103 us  [the longest x1 33.1 us: run_attend(): pl.pallas_call(functools.partial(attend_kernel, count), out_shape=(jax.Sh...]
    ppermute x32 -> x46, starting transfers between devices: 49.6 us -> 36.2 us  [the longest x23 26.2 us: across(): return lax.ppermute(array, 'dp', self.pair)]
  transfers between devices with their start and end apart: 68 -> 102, of which waited for: 20 -> 38; matrix products, arithmetic and copies ran while one was open for 22% -> 20% of each run, Pallas kernels for 13% -> 19%
where the time goes in v2:
time: 549 us; the launch traced here: 540 us
  waiting for transfers between devices  243 us (44%)
  Pallas kernels  103 us (19%)
  starting transfers between devices  71.9 us (13%)
  local copies, waits for them, and re-layouts  64.3 us (12%)
  other arithmetic  46 us (8%)
  matrix products  9.02 us (2%)
    ppermute x23, waiting for transfers between devices, across(): return lax.ppermute(array, 'dp', self.pair)  102 us
    ppermute x22, waiting for transfers between devices, onward(): return lax.ppermute(array, 'dp', self.ring)  90.8 us
    ppermute x12, waiting for transfers between devices, across_chips(): return lax.ppermute(array, 'mp', core_swap)  45.1 us
    pallas_call x1, Pallas kernels, run_attend(): pl.pallas_call(functools.partial(attend_kernel, count), out_shape=(jax.Sh...  33.1 us
    pallas_call x1, Pallas kernels, run_forward(): pl.pallas_call(functools.partial(forward_kernel, count), out_shape=(jax.S...  30.7 us
    pallas_call x1, Pallas kernels, run_backward(): pl.pallas_call(functools.partial(backward_kernel, count), out_shape=jax.S...  29.8 us
    ppermute x23, starting transfers between devices, across(): return lax.ppermute(array, 'dp', self.pair)  26.2 us
    unnamed x219, local copies, waits for them, and re-layouts  21.3 us
  transfers between devices with their start and end apart: 102, of which 38 were waited for; matrix products, arithmetic and copies ran while one was open for 20% of the time, Pallas kernels for 19%

profile of v2, /device:TPU:0, one launch (start us, length us, event | category | flops | bytes accessed | tf_op | source)
XLA Modules:
  0.0 540.0 jit_solution(10470898885833219866)
XLA Ops:
  0.8 2.1 copy.205
  2.9 5.4 collective-permute-start.2
  8.3 1.9 copy.206
  10.3 1.8 collective-permute-start.3
  16.8 2.9 collective-permute-start.5
  21.1 1.6 collective-permute-start.6
  26.4 2.8 collective-permute-done.5
  30.0 4.3 collective-permute-done.6
  36.5 1.8 constant_dynamic-update-slice_fusion.4.refs_0_
  42.5 6.2 %collective-permute-done.7.refs_17_ = bf16[256,1024]{1,0:T(8,128)(2,1)S(1)} collective-permute-done((bf16[256,1024]{1,0:T(8,128)(2,1)S(1)}, bf16[256,1024]{1,0:T(8,128)(2,1)S(1)}, u32[]{:S(2)}, u32[]{:S(2)}) %collective-permute-start.7) | collective-permute-done | bytes 524320 | tf_op jit(solution)/shard_map/ppermute | solution.py:33
  49.4 22.4 %collective-permute-done.14.refs_17_.refs_1_ = bf16[128,2048]{1,0:T(8,128)(2,1)S(1)} collective-permute-done((bf16[128,2048]{1,0:T(8,128)(2,1)S(1)}, bf16[128,2048]{1,0:T(8,128)(2,1)S(1)}, u32[]{:S(2)}, u32[]{:S(2)}) %collective-permute-start.14) | collective-permute-done | bytes 524320 | tf_op jit(solution)/shard_map/ppermute | solution.py:60
  73.1 3.0 collective-permute-done.27.refs_24_.refs_8_
  84.7 6.2 %collective-permute-done.29.refs_19_.refs_3_ = bf16[128,2048]{1,0:T(8,128)(2,1)S(1)} collective-permute-done((bf16[128,2048]{1,0:T(8,128)(2,1)S(1)}, bf16[128,2048]{1,0:T(8,128)(2,1)S(1)}, u32[]{:S(2)}, u32[]{:S(2)}) %collective-permute-start.29) | collective-permute-done | bytes 524320 | tf_op jit(solution)/shard_map/ppermute | solution.py:60
  90.9 2.8 collective-permute-done.33.refs_20_.refs_4_
  93.6 1.9 collective-permute-done.36.refs_26_.refs_10_
  96.8 13.7 %collective-permute-done.17.refs_3_ = bf16[128,3584]{1,0:T(8,128)(2,1)S(1)} collective-permute-done((bf16[128,3584]{1,0:T(8,128)(2,1)S(1)}, bf16[128,3584]{1,0:T(8,128)(2,1)S(1)}, u32[]{:S(2)}, u32[]{:S(2)}) %collective-permute-start.17) | collective-permute-done | bytes 917536 | tf_op jit(solution)/shard_map/ppermute | solution.py:60
  110.5 1.6 collective-permute-done.22.refs_4_
  112.2 1.5 collective-permute-start.12
  115.3 5.7 %collective-permute-done.38.refs_21_.refs_5_ = bf16[128,2048]{1,0:T(8,128)(2,1)S(1)} collective-permute-done((bf16[128,2048]{1,0:T(8,128)(2,1)S(1)}, bf16[128,2048]{1,0:T(8,128)(2,1)S(1)}, u32[]{:S(2)}, u32[]{:S(2)}) %collective-permute-start.38) | collective-permute-done | bytes 524320 | tf_op jit(solution)/shard_map/ppermute | solution.py:60
  122.0 6.1 %collective-permute-done.44.refs_22_.refs_6_ = bf16[128,2048]{1,0:T(8,128)(2,1)S(1)} collective-permute-done((bf16[128,2048]{1,0:T(8,128)(2,1)S(1)}, bf16[128,2048]{1,0:T(8,128)(2,1)S(1)}, u32[]{:S(2)}, u32[]{:S(2)}) %collective-permute-start.44) | collective-permute-done | bytes 524320 | tf_op jit(solution)/shard_map/ppermute | solution.py:63
  128.7 1.9 collective-permute-done.12.refs_5_
  131.7 12.5 %collective-permute-done.30.refs_5_ = bf16[128,3584]{1,0:T(8,128)(2,1)S(1)} collective-permute-done((bf16[128,3584]{1,0:T(8,128)(2,1)S(1)}, bf16[128,3584]{1,0:T(8,128)(2,1)S(1)}, u32[]{:S(2)}, u32[]{:S(2)}) %collective-permute-start.30) | collective-permute-done | bytes 917536 | tf_op jit(solution)/shard_map/ppermute | solution.py:60
  145.7 8.1 %collective-permute-done.45.refs_23_.refs_7_ = bf16[128,2048]{1,0:T(8,128)(2,1)S(1)} collective-permute-done((bf16[128,2048]{1,0:T(8,128)(2,1)S(1)}, bf16[128,2048]{1,0:T(8,128)(2,1)S(1)}, u32[]{:S(2)}, u32[]{:S(2)}) %collective-permute-start.45) | collective-permute-done | bytes 524320 | tf_op jit(solution)/shard_map/ppermute | solution.py:60
  157.7 2.8 collective-permute-done.18.refs_6_
  161.9 9.0 %collective-permute-done.39.refs_7_ = bf16[128,2048]{1,0:T(8,128)(2,1)} collective-permute-done((bf16[128,2048]{1,0:T(8,128)(2,1)}, bf16[128,2048]{1,0:T(8,128)(2,1)}, u32[]{:S(2)}, u32[]{:S(2)}) %collective-permute-start.39) | collective-permute-done | bytes 524320 | tf_op jit(solution)/shard_map/ppermute | solution.py:60
  173.5 7.3 %collective-permute-done.51.refs_7_ = bf16[128,3072]{1,0:T(8,128)(2,1)} collective-permute-done((bf16[128,3072]{1,0:T(8,128)(2,1)}, bf16[128,3072]{1,0:T(8,128)(2,1)}, u32[]{:S(2)}, u32[]{:S(2)}) %collective-permute-start.51) | collective-permute-done | bytes 786464 | tf_op jit(solution)/shard_map/ppermute | solution.py:33
  181.4 30.7 %recur_forward.1 = (bf16[2,16,8,1024]{3,2,1,0:T(8,128)(2,1)}, bf16[16,16,1024]{2,1,0:T(8,128)(2,1)}, f32[16,16,4096]{2,1,0:T(8,128)}, f32[16,16,1024]{2,1,0:T(8,128)}) custom-call(s32[9]{0:T(128)} %stack.81.places, bf16[256,1024]{1,0:T(8,128)(2,1)} %bitcast.133, f32[1,2048]{1,0:T(1,128)} %copy-done.85, f32[1,2048]{1,0:T(1,128)} %copy-done.86, ...), custom_call_target="tpu_custom_call" | custom-call | tf_op jit(solution)/shard_map/recur_forward/pallas_call | solution.py:167
  217.1 4.3 collective-permute-done.50
  224.7 33.1 %attend.1 = (f32[128,1024]{1,0:T(8,128)}, f32[128,1024]{1,0:T(8,128)}, bf16[4,128,1536]{2,1,0:T(8,128)(2,1)}, bf16[2,128,1024]{2,1,0:T(8,128)(2,1)}, f32[8,1024]{1,0:T(8,128)}) custom-call(s32[9]{0:T(128)} %stack.81.places, bf16[128,1024]{1,0:T(8,128)(2,1)} %get-tuple-element.263.memory, bf16[128,1024]{1,0:T(8,128)(2,1)} %get-tuple-element.262.decoded, ...), custom_call_target="tpu_custom_call" | custom-call | tf_op jit(solution)/shard_map/attend/pallas_call | solution.py:603
  257.9 2.3 slice.275
  262.9 1.9 fusion.62
  264.8 2.1 pad_maximum_fusion.2
  269.3 8.2 %collective-permute-done.61 = bf16[128,1024]{1,0:T(8,128)(2,1)} collective-permute-done((bf16[128,1024]{1,0:T(8,128)(2,1)}, bf16[128,1024]{1,0:T(8,128)(2,1)}, u32[]{:S(2)}, u32[]{:S(2)}) %collective-permute-start.61) | collective-permute-done | bytes 262176 | tf_op jit(solution)/shard_map/ppermute | solution.py:33
  281.8 29.8 %recur_backward.1 = bf16[2,16,16,2048]{3,2,1,0:T(8,128)(2,1)} custom-call(s32[9]{0:T(128)} %stack.81.places, f32[2,16,8,1024]{3,2,1,0:T(8,128)} %pad_maximum_fusion.3.outside, f32[16,16,4096]{2,1,0:T(8,128)} %get-tuple-element.75.gates, f32[16,16,1024]{2,1,0:T(8,128)} %get-tuple-element.76.cells, bf16[128,2048]{1,0:T(8,128)(2,1)} %copy-done.18, ...), custom_call_target="tpu_custom_call" | custom-call | tf_op jit(solution)/shard_map/recur_backward/pallas_call | solution.py:265
  311.6 1.7 dynamic-slice_bitcast_fusion.1
  315.5 1.6 collective-permute-done.73
  317.1 11.6 %collective-permute-done.71 = bf16[2,128,1024]{2,1,0:T(8,128)(2,1)S(1)} collective-permute-done((bf16[2,128,1024]{2,1,0:T(8,128)(2,1)S(1)}, bf16[2,128,1024]{2,1,0:T(8,128)(2,1)S(1)}, u32[]{:S(2)}, u32[]{:S(2)}) %collective-permute-start.71) | collective-permute-done | bytes 524320 | tf_op jit(solution)/shard_map/ppermute | solution.py:33
  337.1 3.6 convolution_convert_fusion.1
  344.8 2.4 convolution_convert_fusion
  351.0 2.1 collective-permute-done.82
  358.2 9.1 %input_back.1 = (f32[256,1024]{1,0:T(8,128)}, f32[1,1024]{1,0:T(1,128)}) custom-call(s32[9]{0:T(128)} %stack.81.places, bf16[256,1024]{1,0:T(8,128)(2,1)} %bitcast.135, f32[1,1024]{1,0:T(1,128)} %bitcast.143, bf16[2,256,2048]{2,1,0:T(8,128)(2,1)} %bitcast.130, bf16[128,3584]{1,0:T(8,128)(2,1)} %copy-done.3, bf16[128,3584]{1,0:T(8,128)(2,1)} %copy-done.4, ...), custom_call_target="tpu_custom_call" | custom-call | tf_op jit(solution)/shard_map/input_back/pallas_call | solution.py:309
  367.4 2.0 add_convert_fusion.7
  371.7 9.1 %collective-permute-done.88 = bf16[128,2048]{1,0:T(8,128)(2,1)} collective-permute-done((bf16[128,2048]{1,0:T(8,128)(2,1)}, bf16[128,2048]{1,0:T(8,128)(2,1)}, u32[]{:S(2)}, u32[]{:S(2)}) %collective-permute-start.88) | collective-permute-done | bytes 524320 | tf_op jit(solution)/shard_map/ppermute | solution.py:60
  380.8 2.1 add_convert_fusion.3
  385.8 9.9 %collective-permute-done.75 = bf16[256,896]{0,1:T(8,128)(2,1)} collective-permute-done((bf16[256,896]{0,1:T(8,128)(2,1)}, bf16[256,896]{0,1:T(8,128)(2,1)}, u32[]{:S(2)}, u32[]{:S(2)}) %collective-permute-start.75) | collective-permute-done | bytes 458784 | tf_op jit(solution)/shard_map/ppermute | solution.py:63
  400.7 11.9 %collective-permute-done.89 = bf16[128,2048]{1,0:T(8,128)(2,1)S(1)} collective-permute-done((bf16[128,2048]{1,0:T(8,128)(2,1)}, bf16[128,2048]{1,0:T(8,128)(2,1)S(1)}, u32[]{:S(2)}, u32[]{:S(2)}) %collective-permute-start.89) | collective-permute-done | bytes 524320 | tf_op jit(solution)/shard_map/ppermute | solution.py:63
  412.5 2.2 add_convert_fusion.2
  415.9 1.8 add_convert_fusion.11
  417.7 4.7 collective-permute-done.77
  425.9 7.7 %collective-permute-done.69 = bf16[128,2048]{1,0:T(8,128)(2,1)S(1)} collective-permute-done((bf16[128,2048]{1,0:T(8,128)(2,1)S(1)}, bf16[128,2048]{1,0:T(8,128)(2,1)S(1)}, u32[]{:S(2)}, u32[]{:S(2)}) %collective-permute-start.69) | collective-permute-done | bytes 524320 | tf_op jit(solution)/shard_map/ppermute | solution.py:63
  433.6 4.1 collective-permute-start.66
  437.7 2.1 add_convert_fusion.5
  439.8 18.8 %collective-permute-done.80 = bf16[256,896]{0,1:T(8,128)(2,1)S(1)} collective-permute-done((bf16[256,896]{0,1:T(8,128)(2,1)S(1)}, bf16[256,896]{0,1:T(8,128)(2,1)S(1)}, u32[]{:S(2)}, u32[]{:S(2)}) %collective-permute-start.80) | collective-permute-done | bytes 458784 | tf_op jit(solution)/shard_map/ppermute | solution.py:63
  461.8 2.4 add_convert_fusion.1
  478.4 8.6 %collective-permute-done.99 = bf16[128,512]{0,1:T(8,128)(2,1)S(1)} collective-permute-done((bf16[128,512]{0,1:T(8,128)(2,1)S(1)}, bf16[128,512]{0,1:T(8,128)(2,1)S(1)}, u32[]{:S(2)}, u32[]{:S(2)}) %collective-permute-start.99) | collective-permute-done | bytes 131104 | tf_op jit(solution)/shard_map/ppermute | solution.py:63
  487.6 6.7 %collective-permute-done.100 = bf16[128,512]{0,1:T(8,128)(2,1)} collective-permute-done((bf16[128,512]{0,1:T(8,128)(2,1)S(1)}, bf16[128,512]{0,1:T(8,128)(2,1)}, u32[]{:S(2)}, u32[]{:S(2)}) %collective-permute-start.100) | collective-permute-done | bytes 131104 | tf_op jit(solution)/shard_map/ppermute | solution.py:63
  496.7 5.7 %collective-permute-done.101 = bf16[128,512]{0,1:T(8,128)(2,1)} collective-permute-done((bf16[128,512]{0,1:T(8,128)(2,1)}, bf16[128,512]{0,1:T(8,128)(2,1)}, u32[]{:S(2)}, u32[]{:S(2)}) %collective-permute-start.101) | collective-permute-done | bytes 131104 | tf_op jit(solution)/shard_map/ppermute | solution.py:63
  506.6 2.8 collective-permute-done.78
  511.6 8.5 %collective-permute-done.92 = bf16[128,2048]{1,0:T(8,128)(2,1)S(1)} collective-permute-done((bf16[128,2048]{1,0:T(8,128)(2,1)}, bf16[128,2048]{1,0:T(8,128)(2,1)S(1)}, u32[]{:S(2)}, u32[]{:S(2)}) %collective-permute-start.92) | collective-permute-done | bytes 524320 | tf_op jit(solution)/shard_map/ppermute | solution.py:60
  520.2 2.2 add_convert_fusion
  522.4 5.5 %collective-permute-start.94 = (bf16[128,2048]{1,0:T(8,128)(2,1)}, bf16[128,2048]{1,0:T(8,128)(2,1)}, u32[]{:S(2)}, u32[]{:S(2)}) collective-permute-start(bf16[128,2048]{1,0:T(8,128)(2,1)} %add_convert_fusion), channel_id=1, source_target_pairs={{0,0},{1,16},{16,1},{17,17},{2,2},{3,18},{18,3},{19,19},{4,4},{5,2... | collective-permute-start | bytes 1572872 | tf_op jit(solution)/shard_map/ppermute | solution.py:37
  527.9 1.7 select_bitcast_fusion
  533.7 2.9 reshape.226
  537.5 1.7 reshape.228
  (554 shorter events, 130.1 us)
Async XLA Ops:
  2.9 31.3 %collective-permute-start.2 = (bf16[128,2048]{1,0:T(8,128)(2,1)}, bf16[128,2048]{1,0:T(8,128)(2,1)}, u32[]{:S(2)}, u32[]{:S(2)}) collective-permute-start(bf16[128,2048]{1,0:T(8,128)(2,1)} %bitcast.72), channel_id=1, source_target_pairs={{0,0},{1,16},{16,1},{17,17},{2,2},{3,18},{18,3},{19,19},{4,4},{5,2... | collective-permute-start | bytes 1572872 | tf_op jit(solution)/shard_map/ppermute | solution.py:37
  10.3 24.5 %collective-permute-start.3 = (bf16[128,2048]{1,0:T(8,128)(2,1)}, bf16[128,2048]{1,0:T(8,128)(2,1)S(1)}, u32[]{:S(2)}, u32[]{:S(2)}) collective-permute-start(bf16[128,2048]{1,0:T(8,128)(2,1)} %bitcast.75), channel_id=1, source_target_pairs={{0,0},{1,16},{16,1},{17,17},{2,2},{3,18},{18,3},{19,19},{4,4},{5,2... | collective-permute-start | bytes 1572872 | tf_op jit(solution)/shard_map/ppermute | solution.py:37
  38.4 34.3 %collective-permute-start.11 = (bf16[128,3584]{1,0:T(8,128)(2,1)S(1)}, bf16[128,3584]{1,0:T(8,128)(2,1)S(1)}, u32[]{:S(2)}, u32[]{:S(2)}) collective-permute-start(bf16[128,3584]{1,0:T(8,128)(2,1)S(1)} %constant_dynamic-update-slice_fusion.9.refs_0_), channel_id=1, source_target_pairs={{0,2},{2,0},{4,6},{6,4},{8,10},{10,8},{12,14},{14,12},{1,3},{3,1},... | collective-permute-start | bytes 2752520 | tf_op jit(solution)/shard_map/ppermute | solution.py:60
  39.4 32.3 %collective-permute-start.14 = (bf16[128,2048]{1,0:T(8,128)(2,1)S(1)}, bf16[128,2048]{1,0:T(8,128)(2,1)S(1)}, u32[]{:S(2)}, u32[]{:S(2)}) collective-permute-start(bf16[128,2048]{1,0:T(8,128)(2,1)S(1)} %collective-permute-done.3.refs_16_.refs_0_), channel_id=1, source_target_pairs={{0,2},{2,0},{4,6},{6,4},{8,10},{10,8},{12,14},{14,12},{1,3},{3,1},... | collective-permute-start | bytes 1572872 | tf_op jit(solution)/shard_map/ppermute | solution.py:60
  40.9 31.2 %collective-permute-start.23 = (bf16[128,2048]{1,0:T(8,128)(2,1)S(1)}, bf16[128,2048]{1,0:T(8,128)(2,1)S(1)}, u32[]{:S(2)}, u32[]{:S(2)}) collective-permute-start(bf16[128,2048]{1,0:T(8,128)(2,1)S(1)} %collective-permute-done.3.refs_16_.refs_0_), channel_id=1, source_target_pairs={{0,4},{2,6},{4,8},{6,10},{8,12},{10,14},{12,0},{14,2},{1,5},{3,7},... | collective-permute-start | bytes 1572872 | tf_op jit(solution)/shard_map/ppermute | solution.py:63
  41.2 35.9 %collective-permute-start.13 = (bf16[128,3584]{1,0:T(8,128)(2,1)S(1)}, bf16[128,3584]{1,0:T(8,128)(2,1)S(1)}, u32[]{:S(2)}, u32[]{:S(2)}) collective-permute-start(bf16[128,3584]{1,0:T(8,128)(2,1)S(1)} %constant_dynamic-update-slice_fusion.9.refs_0_), channel_id=1, source_target_pairs={{0,4},{2,6},{4,8},{6,10},{8,12},{10,14},{12,0},{14,2},{1,5},{3,7},... | collective-permute-start | bytes 2752520 | tf_op jit(solution)/shard_map/ppermute | solution.py:63
  48.7 28.3 %collective-permute-start.10 = (bf16[128,3072]{1,0:T(8,128)(2,1)}, bf16[128,3072]{1,0:T(8,128)(2,1)}, u32[]{:S(2)}, u32[]{:S(2)}) collective-permute-start(bf16[128,3072]{1,0:T(8,128)(2,1)} %constant_dynamic-update-slice_fusion.4.refs_0_), channel_id=1, source_target_pairs={{0,1},{1,0},{2,3},{3,2},{4,5},{5,4},{6,7},{7,6},{8,9},{9,8},{10,11... | collective-permute-start | bytes 2359304 | tf_op jit(solution)/shard_map/ppermute | solution.py:33
  76.1 14.8 %collective-permute-start.29 = (bf16[128,2048]{1,0:T(8,128)(2,1)S(1)}, bf16[128,2048]{1,0:T(8,128)(2,1)S(1)}, u32[]{:S(2)}, u32[]{:S(2)}) collective-permute-start(bf16[128,2048]{1,0:T(8,128)(2,1)S(1)} %collective-permute-done.23.refs_18_.refs_2_), channel_id=1, source_target_pairs={{0,2},{2,0},{4,6},{6,4},{8,10},{10,8},{12,14},{14,12},{1,3},{3,1},... | collective-permute-start | bytes 1572872 | tf_op jit(solution)/shard_map/ppermute | solution.py:60
  77.0 16.6 %collective-permute-start.33 = (bf16[128,2048]{1,0:T(8,128)(2,1)S(1)}, bf16[128,2048]{1,0:T(8,128)(2,1)S(1)}, u32[]{:S(2)}, u32[]{:S(2)}) collective-permute-start(bf16[128,2048]{1,0:T(8,128)(2,1)S(1)} %collective-permute-done.23.refs_18_.refs_2_), channel_id=1, source_target_pairs={{0,4},{2,6},{4,8},{6,10},{8,12},{10,14},{12,0},{14,2},{1,5},{3,7},... | collective-permute-start | bytes 1572872 | tf_op jit(solution)/shard_map/ppermute | solution.py:63
  77.8 17.9 %collective-permute-start.20 = (bf16[128,3072]{1,0:T(8,128)(2,1)S(1)}, bf16[128,3072]{1,0:T(8,128)(2,1)S(1)}, u32[]{:S(2)}, u32[]{:S(2)}) collective-permute-start(bf16[128,3072]{1,0:T(8,128)(2,1)S(1)} %pad_maximum_fusion.6.refs_1_), channel_id=1, source_target_pairs={{0,16},{16,0},{1,17},{17,1},{2,18},{18,2},{3,19},{19,3},{4,20},{20... | collective-permute-start | bytes 2359304 | tf_op jit(solution)/shard_map/ppermute | solution.py:29
  82.4 28.1 %collective-permute-start.17 = (bf16[128,3584]{1,0:T(8,128)(2,1)S(1)}, bf16[128,3584]{1,0:T(8,128)(2,1)S(1)}, u32[]{:S(2)}, u32[]{:S(2)}) collective-permute-start(bf16[128,3584]{1,0:T(8,128)(2,1)S(1)} %collective-permute-done.13.refs_2_), channel_id=1, source_target_pairs={{0,2},{2,0},{4,6},{6,4},{8,10},{10,8},{12,14},{14,12},{1,3},{3,1},... | collective-permute-start | bytes 2752520 | tf_op jit(solution)/shard_map/ppermute | solution.py:60
  83.5 28.7 %collective-permute-start.22 = (bf16[128,3584]{1,0:T(8,128)(2,1)S(1)}, bf16[128,3584]{1,0:T(8,128)(2,1)S(1)}, u32[]{:S(2)}, u32[]{:S(2)}) collective-permute-start(bf16[128,3584]{1,0:T(8,128)(2,1)S(1)} %collective-permute-done.13.refs_2_), channel_id=1, source_target_pairs={{0,4},{2,6},{4,8},{6,10},{8,12},{10,14},{12,0},{14,2},{1,5},{3,7},... | collective-permute-start | bytes 2752520 | tf_op jit(solution)/shard_map/ppermute | solution.py:63
  90.9 22.9 %collective-permute-start.26 = (bf16[128,3584]{1,0:T(8,128)(2,1)S(1)}, bf16[128,3584]{1,0:T(8,128)(2,1)S(1)}, u32[]{:S(2)}, u32[]{:S(2)}) collective-permute-start(bf16[128,3584]{1,0:T(8,128)(2,1)S(1)} %collective-permute-done.11.refs_1_), channel_id=1, source_target_pairs={{0,16},{16,0},{1,17},{17,1},{2,18},{18,2},{3,19},{19,3},{4,20},{20... | collective-permute-start | bytes 2752520 | tf_op jit(solution)/shard_map/ppermute | solution.py:29
  95.5 18.9 %collective-permute-start.37 = (bf16[128,2048]{1,0:T(8,128)(2,1)S(1)}, bf16[128,2048]{1,0:T(8,128)(2,1)S(1)}, u32[]{:S(2)}, u32[]{:S(2)}) collective-permute-start(bf16[128,2048]{1,0:T(8,128)(2,1)S(1)} %collective-permute-done.29.refs_19_.refs_3_), channel_id=1, source_target_pairs={{0,16},{16,0},{1,17},{17,1},{2,18},{18,2},{3,19},{19,3},{4,20},{20... | collective-permute-start | bytes 1572872 | tf_op jit(solution)/shard_map/ppermute | solution.py:29
  95.7 25.3 %collective-permute-start.38 = (bf16[128,2048]{1,0:T(8,128)(2,1)S(1)}, bf16[128,2048]{1,0:T(8,128)(2,1)S(1)}, u32[]{:S(2)}, u32[]{:S(2)}) collective-permute-start(bf16[128,2048]{1,0:T(8,128)(2,1)S(1)} %collective-permute-done.33.refs_20_.refs_4_), channel_id=1, source_target_pairs={{0,2},{2,0},{4,6},{6,4},{8,10},{10,8},{12,14},{14,12},{1,3},{3,1},... | collective-permute-start | bytes 1572872 | tf_op jit(solution)/shard_map/ppermute | solution.py:60
  110.5 21.2 %collective-permute-start.34 = (bf16[128,3584]{1,0:T(8,128)(2,1)S(1)}, bf16[128,3584]{1,0:T(8,128)(2,1)S(1)}, u32[]{:S(2)}, u32[]{:S(2)}) collective-permute-start(bf16[128,3584]{1,0:T(8,128)(2,1)S(1)} %collective-permute-done.13.refs_2_), channel_id=1, source_target_pairs={{0,16},{16,0},{1,17},{17,1},{2,18},{18,2},{3,19},{19,3},{4,20},{20... | collective-permute-start | bytes 2752520 | tf_op jit(solution)/shard_map/ppermute | solution.py:29
  112.2 18.4 %collective-permute-start.12 = (bf16[128,3072]{1,0:T(8,128)(2,1)S(1)}, bf16[128,3072]{1,0:T(8,128)(2,1)S(1)}, u32[]{:S(2)}, u32[]{:S(2)}) collective-permute-start(bf16[128,3072]{1,0:T(8,128)(2,1)S(1)} %pad_maximum_fusion.6.refs_1_), channel_id=1, source_target_pairs={{0,1},{1,0},{2,3},{3,2},{4,5},{5,4},{6,7},{7,6},{8,9},{9,8},{10,11... | collective-permute-start | bytes 2359304 | tf_op jit(solution)/shard_map/ppermute | solution.py:33
  113.7 14.3 %collective-permute-start.44 = (bf16[128,2048]{1,0:T(8,128)(2,1)S(1)}, bf16[128,2048]{1,0:T(8,128)(2,1)S(1)}, u32[]{:S(2)}, u32[]{:S(2)}) collective-permute-start(bf16[128,2048]{1,0:T(8,128)(2,1)S(1)} %collective-permute-done.33.refs_20_.refs_4_), channel_id=1, source_target_pairs={{0,4},{2,6},{4,8},{6,10},{8,12},{10,14},{12,0},{14,2},{1,5},{3,7},... | collective-permute-start | bytes 1572872 | tf_op jit(solution)/shard_map/ppermute | solution.py:63
  121.0 23.3 %collective-permute-start.30 = (bf16[128,3584]{1,0:T(8,128)(2,1)S(1)}, bf16[128,3584]{1,0:T(8,128)(2,1)S(1)}, u32[]{:S(2)}, u32[]{:S(2)}) collective-permute-start(bf16[128,3584]{1,0:T(8,128)(2,1)S(1)} %collective-permute-done.22.refs_4_), channel_id=1, source_target_pairs={{0,2},{2,0},{4,6},{6,4},{8,10},{10,8},{12,14},{14,12},{1,3},{3,1},... | collective-permute-start | bytes 2752520 | tf_op jit(solution)/shard_map/ppermute | solution.py:60
  128.1 26.2 %collective-permute-start.21 = (bf16[128,3072]{1,0:T(8,128)(2,1)S(1)}, bf16[128,3072]{1,0:T(8,128)(2,1)S(1)}, u32[]{:S(2)}, u32[]{:S(2)}) collective-permute-start(bf16[128,3072]{1,0:T(8,128)(2,1)S(1)} %pad_maximum_fusion.7.refs_2_), channel_id=1, source_target_pairs={{0,16},{16,0},{1,17},{17,1},{2,18},{18,2},{3,19},{19,3},{4,20},{20... | collective-permute-start | bytes 2359304 | tf_op jit(solution)/shard_map/ppermute | solution.py:29
  128.1 28.2 %collective-permute-start.35 = (bf16[128,3584]{1,0:T(8,128)(2,1)S(1)}, bf16[128,3584]{1,0:T(8,128)(2,1)S(1)}, u32[]{:S(2)}, u32[]{:S(2)}) collective-permute-start(bf16[128,3584]{1,0:T(8,128)(2,1)S(1)} %collective-permute-done.17.refs_3_), channel_id=1, source_target_pairs={{0,16},{16,0},{1,17},{17,1},{2,18},{18,2},{3,19},{19,3},{4,20},{20... | collective-permute-start | bytes 2752520 | tf_op jit(solution)/shard_map/ppermute | solution.py:29
  130.6 23.1 %collective-permute-start.45 = (bf16[128,2048]{1,0:T(8,128)(2,1)S(1)}, bf16[128,2048]{1,0:T(8,128)(2,1)S(1)}, u32[]{:S(2)}, u32[]{:S(2)}) collective-permute-start(bf16[128,2048]{1,0:T(8,128)(2,1)S(1)} %collective-permute-done.44.refs_22_.refs_6_), channel_id=1, source_target_pairs={{0,2},{2,0},{4,6},{6,4},{8,10},{10,8},{12,14},{14,12},{1,3},{3,1},... | collective-permute-start | bytes 1572872 | tf_op jit(solution)/shard_map/ppermute | solution.py:60
  131.7 22.0 %collective-permute-start.32 = (bf16[128,2048]{1,0:T(8,128)(2,1)S(1)}, bf16[128,2048]{1,0:T(8,128)(2,1)}, u32[]{:S(2)}, u32[]{:S(2)}) collective-permute-start(bf16[128,2048]{1,0:T(8,128)(2,1)S(1)} %slice.273), channel_id=1, source_target_pairs={{0,4},{2,6},{4,8},{6,10},{8,12},{10,14},{12,0},{14,2},{1,5},{3,7},... | collective-permute-start | bytes 1572872 | tf_op jit(solution)/shard_map/ppermute | solution.py:63
  144.2 16.2 %collective-permute-start.18 = (bf16[128,3072]{1,0:T(8,128)(2,1)S(1)}, bf16[128,3072]{1,0:T(8,128)(2,1)S(1)}, u32[]{:S(2)}, u32[]{:S(2)}) collective-permute-start(bf16[128,3072]{1,0:T(8,128)(2,1)S(1)} %pad_maximum_fusion.7.refs_2_), channel_id=1, source_target_pairs={{0,1},{1,0},{2,3},{3,2},{4,5},{5,4},{6,7},{7,6},{8,9},{9,8},{10,11... | collective-permute-start | bytes 2359304 | tf_op jit(solution)/shard_map/ppermute | solution.py:33
  156.2 14.7 %collective-permute-start.31 = (bf16[128,3072]{1,0:T(8,128)(2,1)}, bf16[128,3072]{1,0:T(8,128)(2,1)S(1)}, u32[]{:S(2)}, u32[]{:S(2)}) collective-permute-start(bf16[128,3072]{1,0:T(8,128)(2,1)} %pad_maximum_fusion.8.refs_3_), channel_id=1, source_target_pairs={{0,16},{16,0},{1,17},{17,1},{2,18},{18,2},{3,19},{19,3},{4,20},{20... | collective-permute-start | bytes 2359304 | tf_op jit(solution)/shard_map/ppermute | solution.py:29
  156.7 14.2 %collective-permute-start.39 = (bf16[128,2048]{1,0:T(8,128)(2,1)}, bf16[128,2048]{1,0:T(8,128)(2,1)}, u32[]{:S(2)}, u32[]{:S(2)}) collective-permute-start(bf16[128,2048]{1,0:T(8,128)(2,1)} %collective-permute-done.32.refs_6_), channel_id=1, source_target_pairs={{0,2},{2,0},{4,6},{6,4},{8,10},{10,8},{12,14},{14,12},{1,3},{3,1},... | collective-permute-start | bytes 1572872 | tf_op jit(solution)/shard_map/ppermute | solution.py:60
  157.6 15.4 %collective-permute-start.40 = (bf16[128,3584]{1,0:T(8,128)(2,1)S(1)}, bf16[128,3584]{1,0:T(8,128)(2,1)S(1)}, u32[]{:S(2)}, u32[]{:S(2)}) collective-permute-start(bf16[128,3584]{1,0:T(8,128)(2,1)S(1)} %collective-permute-done.22.refs_4_), channel_id=1, source_target_pairs={{0,16},{16,0},{1,17},{17,1},{2,18},{18,2},{3,19},{19,3},{4,20},{20... | collective-permute-start | bytes 2752520 | tf_op jit(solution)/shard_map/ppermute | solution.py:29
  160.5 20.4 %collective-permute-start.41 = (bf16[128,3584]{1,0:T(8,128)(2,1)S(1)}, bf16[128,3584]{1,0:T(8,128)(2,1)}, u32[]{:S(2)}, u32[]{:S(2)}) collective-permute-start(bf16[128,3584]{1,0:T(8,128)(2,1)S(1)} %collective-permute-done.30.refs_5_), channel_id=1, source_target_pairs={{0,16},{16,0},{1,17},{17,1},{2,18},{18,2},{3,19},{19,3},{4,20},{20... | collective-permute-start | bytes 2752520 | tf_op jit(solution)/shard_map/ppermute | solution.py:29
  160.5 20.3 %collective-permute-start.51 = (bf16[128,3072]{1,0:T(8,128)(2,1)}, bf16[128,3072]{1,0:T(8,128)(2,1)}, u32[]{:S(2)}, u32[]{:S(2)}) collective-permute-start(bf16[128,3072]{1,0:T(8,128)(2,1)} %pad_maximum_fusion.8.refs_3_), channel_id=1, source_target_pairs={{0,1},{1,0},{2,3},{3,2},{4,5},{5,4},{6,7},{7,6},{8,9},{9,8},{10,11... | collective-permute-start | bytes 2359304 | tf_op jit(solution)/shard_map/ppermute | solution.py:33
  173.0 51.7 %collective-permute-start.52 = (bf16[128,3072]{1,0:T(8,128)(2,1)}, bf16[128,3072]{1,0:T(8,128)(2,1)}, u32[]{:S(2)}, u32[]{:S(2)}) collective-permute-start(bf16[128,3072]{1,0:T(8,128)(2,1)} %collective-permute-done.10.refs_4_), channel_id=1, source_target_pairs={{0,16},{16,0},{1,17},{17,1},{2,18},{18,2},{3,19},{19,3},{4,20},{20... | collective-permute-start | bytes 2359304 | tf_op jit(solution)/shard_map/ppermute | solution.py:29
  173.2 51.6 %collective-permute-start.53 = (bf16[128,3072]{1,0:T(8,128)(2,1)}, bf16[128,3072]{1,0:T(8,128)(2,1)}, u32[]{:S(2)}, u32[]{:S(2)}) collective-permute-start(bf16[128,3072]{1,0:T(8,128)(2,1)} %copy-done.46), channel_id=1, source_target_pairs={{0,16},{16,0},{1,17},{17,1},{2,18},{18,2},{3,19},{19,3},{4,20},{20... | collective-permute-start | bytes 2359304 | tf_op jit(solution)/shard_map/ppermute | solution.py:29
  180.8 43.9 %collective-permute-start.54 = (bf16[128,3072]{1,0:T(8,128)(2,1)}, bf16[128,3072]{1,0:T(8,128)(2,1)}, u32[]{:S(2)}, u32[]{:S(2)}) collective-permute-start(bf16[128,3072]{1,0:T(8,128)(2,1)} %copy-done.48), channel_id=1, source_target_pairs={{0,16},{16,0},{1,17},{17,1},{2,18},{18,2},{3,19},{19,3},{4,20},{20... | collective-permute-start | bytes 2359304 | tf_op jit(solution)/shard_map/ppermute | solution.py:29
  180.8 43.9 %collective-permute-start.55 = (bf16[128,3072]{1,0:T(8,128)(2,1)}, bf16[128,3072]{1,0:T(8,128)(2,1)}, u32[]{:S(2)}, u32[]{:S(2)}) collective-permute-start(bf16[128,3072]{1,0:T(8,128)(2,1)} %collective-permute-done.51.refs_7_), channel_id=1, source_target_pairs={{0,16},{16,0},{1,17},{17,1},{2,18},{18,2},{3,19},{19,3},{4,20},{20... | collective-permute-start | bytes 2359304 | tf_op jit(solution)/shard_map/ppermute | solution.py:29
  222.4 40.5 %collective-permute-start.59 = (bf16[16,8,1024]{2,1,0:T(8,128)(2,1)S(1)}, bf16[16,8,1024]{2,1,0:T(8,128)(2,1)}, u32[]{:S(2)}, u32[]{:S(2)}) collective-permute-start(bf16[16,8,1024]{2,1,0:T(8,128)(2,1)S(1)} %get-tuple-element.69), channel_id=1, source_target_pairs={{0,1},{1,0},{2,3},{3,2},{4,5},{5,4},{6,7},{7,6},{8,9},{9,8},{10,11... | collective-permute-start | bytes 786440 | tf_op jit(solution)/shard_map/ppermute | solution.py:33
  224.7 56.3 %collective-permute-start.62 = (bf16[256,1024]{1,0:T(8,128)(2,1)}, bf16[256,1024]{1,0:T(8,128)(2,1)}, u32[]{:S(2)}, u32[]{:S(2)}) collective-permute-start(bf16[256,1024]{1,0:T(8,128)(2,1)} %bitcast.39), channel_id=1, source_target_pairs={{0,16},{16,0},{1,17},{17,1},{2,18},{18,2},{3,19},{19,3},{4,20},{20... | collective-permute-start | bytes 1572872 | tf_op jit(solution)/shard_map/ppermute | solution.py:29
  260.2 19.6 %collective-permute-start.56 = (bf16[2,128,1536]{2,1,0:T(8,128)(2,1)}, bf16[2,128,1536]{2,1,0:T(8,128)(2,1)}, u32[]{:S(2)}, u32[]{:S(2)}) collective-permute-start(bf16[2,128,1536]{2,1,0:T(8,128)(2,1)} %slice.275), channel_id=1, source_target_pairs={{0,16},{16,0},{1,17},{17,1},{2,18},{18,2},{3,19},{19,3},{4,20},{20... | collective-permute-start | bytes 2359304 | tf_op jit(solution)/shard_map/ppermute | solution.py:29
  266.9 14.1 %collective-permute-start.60 = (bf16[4,128,1024]{2,1,0:T(8,128)(2,1)}, bf16[4,128,1024]{2,1,0:T(8,128)(2,1)S(1)}, u32[]{:S(2)}, u32[]{:S(2)}) collective-permute-start(bf16[4,128,1024]{2,1,0:T(8,128)(2,1)} %pad_maximum_fusion.2), channel_id=1, source_target_pairs={{0,16},{16,0},{1,17},{17,1},{2,18},{18,2},{3,19},{19,3},{4,20},{20... | collective-permute-start | bytes 3145736 | tf_op jit(solution)/shard_map/ppermute | solution.py:29
  281.0 48.0 %collective-permute-start.70 = (bf16[2,128,1536]{2,1,0:T(8,128)(2,1)S(1)}, bf16[2,128,1536]{2,1,0:T(8,128)(2,1)S(1)}, u32[]{:S(2)}, u32[]{:S(2)}) collective-permute-start(bf16[2,128,1536]{2,1,0:T(8,128)(2,1)S(1)} %pad_maximum_fusion.9), channel_id=1, source_target_pairs={{0,1},{1,0},{2,3},{3,2},{4,5},{5,4},{6,7},{7,6},{8,9},{9,8},{10,11... | collective-permute-start | bytes 2359304 | tf_op jit(solution)/shard_map/ppermute | solution.py:33
  313.3 23.9 %collective-permute-start.63 = (bf16[256,2048]{1,0:T(8,128)(2,1)S(1)}, bf16[256,2048]{1,0:T(8,128)(2,1)S(1)}, u32[]{:S(2)}, u32[]{:S(2)}) collective-permute-start(bf16[256,2048]{1,0:T(8,128)(2,1)S(1)} %get-tuple-element.203), channel_id=1, source_target_pairs={{0,16},{16,0},{1,17},{17,1},{2,18},{18,2},{3,19},{19,3},{4,20},{20... | collective-permute-start | bytes 3145736 | tf_op jit(solution)/shard_map/ppermute | solution.py:29
  328.9 25.9 %collective-permute-start.72 = (bf16[4,128,1024]{2,1,0:T(8,128)(2,1)S(1)}, bf16[4,128,1024]{2,1,0:T(8,128)(2,1)S(1)}, u32[]{:S(2)}, u32[]{:S(2)}) collective-permute-start(bf16[4,128,1024]{2,1,0:T(8,128)(2,1)S(1)} %pad_maximum_fusion.5), channel_id=1, source_target_pairs={{0,16},{16,0},{1,17},{17,1},{2,18},{18,2},{3,19},{19,3},{4,20},{20... | collective-permute-start | bytes 3145736 | tf_op jit(solution)/shard_map/ppermute | solution.py:29
  333.4 16.5 %collective-permute-start.83 = (bf16[128,1024]{0,1:T(8,128)(2,1)S(1)}, bf16[128,1024]{0,1:T(8,128)(2,1)S(1)}, u32[]{:S(2)}, u32[]{:S(2)}) collective-permute-start(bf16[128,1024]{0,1:T(8,128)(2,1)S(1)} %pad_maximum_fusion.25), channel_id=1, source_target_pairs={{0,2},{2,0},{4,6},{6,4},{8,10},{10,8},{12,14},{14,12},{1,3},{3,1},... | collective-permute-start | bytes 786440 | tf_op jit(solution)/shard_map/ppermute | solution.py:60
  342.2 16.0 %collective-permute-start.64 = (bf16[128,2048]{1,0:T(8,128)(2,1)S(1)}, bf16[128,2048]{1,0:T(8,128)(2,1)S(1)}, u32[]{:S(2)}, u32[]{:S(2)}) collective-permute-start(bf16[128,2048]{1,0:T(8,128)(2,1)S(1)} %get-tuple-element.199), channel_id=1, source_target_pairs={{0,2},{2,0},{4,6},{6,4},{8,10},{10,8},{12,14},{14,12},{1,3},{3,1},... | collective-permute-start | bytes 1572872 | tf_op jit(solution)/shard_map/ppermute | solution.py:60
  343.4 54.4 %collective-permute-start.67 = (bf16[128,2048]{1,0:T(8,128)(2,1)}, bf16[128,2048]{1,0:T(8,128)(2,1)S(1)}, u32[]{:S(2)}, u32[]{:S(2)}) collective-permute-start(bf16[128,2048]{1,0:T(8,128)(2,1)} %get-tuple-element.198), channel_id=1, source_target_pairs={{0,2},{2,0},{4,6},{6,4},{8,10},{10,8},{12,14},{14,12},{1,3},{3,1},... | collective-permute-start | bytes 1572872 | tf_op jit(solution)/shard_map/ppermute | solution.py:60
  349.8 30.9 %collective-permute-start.88 = (bf16[128,2048]{1,0:T(8,128)(2,1)}, bf16[128,2048]{1,0:T(8,128)(2,1)}, u32[]{:S(2)}, u32[]{:S(2)}) collective-permute-start(bf16[128,2048]{1,0:T(8,128)(2,1)} %get-tuple-element.194), channel_id=1, source_target_pairs={{0,2},{2,0},{4,6},{6,4},{8,10},{10,8},{12,14},{14,12},{1,3},{3,1},... | collective-permute-start | bytes 1572872 | tf_op jit(solution)/shard_map/ppermute | solution.py:60
  353.1 46.4 %collective-permute-start.87 = (bf16[128,2048]{1,0:T(8,128)(2,1)}, bf16[128,2048]{1,0:T(8,128)(2,1)}, u32[]{:S(2)}, u32[]{:S(2)}) collective-permute-start(bf16[128,2048]{1,0:T(8,128)(2,1)} %get-tuple-element.195), channel_id=1, source_target_pairs={{0,2},{2,0},{4,6},{6,4},{8,10},{10,8},{12,14},{14,12},{1,3},{3,1},... | collective-permute-start | bytes 1572872 | tf_op jit(solution)/shard_map/ppermute | solution.py:60
  354.8 60.0 %collective-permute-start.95 = (bf16[128,1024]{0,1:T(8,128)(2,1)}, bf16[128,1024]{0,1:T(8,128)(2,1)}, u32[]{:S(2)}, u32[]{:S(2)}) collective-permute-start(bf16[128,1024]{0,1:T(8,128)(2,1)} %add_convert_fusion.12), channel_id=1, source_target_pairs={{0,4},{2,6},{4,8},{6,10},{8,12},{10,14},{12,0},{14,2},{1,5},{3,7},... | collective-permute-start | bytes 786440 | tf_op jit(solution)/shard_map/ppermute | solution.py:63
  369.4 28.5 %collective-permute-start.68 = (bf16[128,2048]{1,0:T(8,128)(2,1)}, bf16[128,2048]{1,0:T(8,128)(2,1)S(1)}, u32[]{:S(2)}, u32[]{:S(2)}) collective-permute-start(bf16[128,2048]{1,0:T(8,128)(2,1)} %add_convert_fusion.7), channel_id=1, source_target_pairs={{0,4},{2,6},{4,8},{6,10},{8,12},{10,14},{12,0},{14,2},{1,5},{3,7},... | collective-permute-start | bytes 1572872 | tf_op jit(solution)/shard_map/ppermute | solution.py:63
  380.8 14.9 %collective-permute-start.75 = (bf16[256,896]{0,1:T(8,128)(2,1)}, bf16[256,896]{0,1:T(8,128)(2,1)}, u32[]{:S(2)}, u32[]{:S(2)}) collective-permute-start(bf16[256,896]{0,1:T(8,128)(2,1)} %pad_maximum_fusion.18), channel_id=1, source_target_pairs={{0,4},{2,6},{4,8},{6,10},{8,12},{10,14},{12,0},{14,2},{1,5},{3,7},... | collective-permute-start | bytes 1376264 | tf_op jit(solution)/shard_map/ppermute | solution.py:63
  395.6 16.9 %collective-permute-start.89 = (bf16[128,2048]{1,0:T(8,128)(2,1)}, bf16[128,2048]{1,0:T(8,128)(2,1)S(1)}, u32[]{:S(2)}, u32[]{:S(2)}) collective-permute-start(bf16[128,2048]{1,0:T(8,128)(2,1)} %add_convert_fusion.3), channel_id=1, source_target_pairs={{0,4},{2,6},{4,8},{6,10},{8,12},{10,14},{12,0},{14,2},{1,5},{3,7},... | collective-permute-start | bytes 1572872 | tf_op jit(solution)/shard_map/ppermute | solution.py:63
  397.8 25.8 %collective-permute-start.65 = (f32[16,16,1024]{2,1,0:T(8,128)S(1)}, f32[16,16,1024]{2,1,0:T(8,128)S(1)}, u32[]{:S(2)}, u32[]{:S(2)}) collective-permute-start(f32[16,16,1024]{2,1,0:T(8,128)S(1)} %bitcast.138), channel_id=1, source_target_pairs={{0,16},{16,0},{1,17},{17,1},{2,18},{18,2},{3,19},{19,3},{4,20},{20... | collective-permute-start | bytes 3145736 | tf_op jit(solution)/shard_map/ppermute | solution.py:29
  397.9 24.4 %collective-permute-start.77 = (bf16[256,896]{0,1:T(8,128)(2,1)S(1)}, bf16[256,896]{0,1:T(8,128)(2,1)S(1)}, u32[]{:S(2)}, u32[]{:S(2)}) collective-permute-start(bf16[256,896]{0,1:T(8,128)(2,1)S(1)} %pad_maximum_fusion.19), channel_id=1, source_target_pairs={{0,4},{2,6},{4,8},{6,10},{8,12},{10,14},{12,0},{14,2},{1,5},{3,7},... | collective-permute-start | bytes 1376264 | tf_op jit(solution)/shard_map/ppermute | solution.py:63
  399.5 16.4 %collective-permute-start.84 = (bf16[128,1024]{0,1:T(8,128)(2,1)S(1)}, bf16[128,1024]{0,1:T(8,128)(2,1)S(1)}, u32[]{:S(2)}, u32[]{:S(2)}) collective-permute-start(bf16[128,1024]{0,1:T(8,128)(2,1)S(1)} %copy-done.65), channel_id=1, source_target_pairs={{0,2},{2,0},{4,6},{6,4},{8,10},{10,8},{12,14},{14,12},{1,3},{3,1},... | collective-permute-start | bytes 786440 | tf_op jit(solution)/shard_map/ppermute | solution.py:60
  412.5 21.1 %collective-permute-start.69 = (bf16[128,2048]{1,0:T(8,128)(2,1)S(1)}, bf16[128,2048]{1,0:T(8,128)(2,1)S(1)}, u32[]{:S(2)}, u32[]{:S(2)}) collective-permute-start(bf16[128,2048]{1,0:T(8,128)(2,1)S(1)} %add_convert_fusion.6), channel_id=1, source_target_pairs={{0,4},{2,6},{4,8},{6,10},{8,12},{10,14},{12,0},{14,2},{1,5},{3,7},... | collective-permute-start | bytes 1572872 | tf_op jit(solution)/shard_map/ppermute | solution.py:63
  414.8 18.8 %collective-permute-start.76 = (bf16[128,2048]{1,0:T(8,128)(2,1)S(1)}, bf16[128,2048]{1,0:T(8,128)(2,1)S(1)}, u32[]{:S(2)}, u32[]{:S(2)}) collective-permute-start(bf16[128,2048]{1,0:T(8,128)(2,1)S(1)} %copy-done.63), channel_id=1, source_target_pairs={{0,2},{2,0},{4,6},{6,4},{8,10},{10,8},{12,14},{14,12},{1,3},{3,1},... | collective-permute-start | bytes 1572872 | tf_op jit(solution)/shard_map/ppermute | solution.py:60
  415.9 44.7 %collective-permute-start.90 = (bf16[128,2048]{1,0:T(8,128)(2,1)}, bf16[128,2048]{1,0:T(8,128)(2,1)}, u32[]{:S(2)}, u32[]{:S(2)}) collective-permute-start(bf16[128,2048]{1,0:T(8,128)(2,1)} %add_convert_fusion.2), channel_id=1, source_target_pairs={{0,4},{2,6},{4,8},{6,10},{8,12},{10,14},{12,0},{14,2},{1,5},{3,7},... | collective-permute-start | bytes 1572872 | tf_op jit(solution)/shard_map/ppermute | solution.py:63
  422.3 39.5 %collective-permute-start.91 = (bf16[128,2048]{1,0:T(8,128)(2,1)}, bf16[128,2048]{1,0:T(8,128)(2,1)}, u32[]{:S(2)}, u32[]{:S(2)}) collective-permute-start(bf16[128,2048]{1,0:T(8,128)(2,1)} %get-tuple-element.90), channel_id=1, source_target_pairs={{0,2},{2,0},{4,6},{6,4},{8,10},{10,8},{12,14},{14,12},{1,3},{3,1},... | collective-permute-start | bytes 1572872 | tf_op jit(solution)/shard_map/ppermute | solution.py:60
  423.7 105.9 %collective-permute-start.97 = (bf16[128,1024]{0,1:T(8,128)(2,1)}, bf16[128,1024]{0,1:T(8,128)(2,1)}, u32[]{:S(2)}, u32[]{:S(2)}) collective-permute-start(bf16[128,1024]{0,1:T(8,128)(2,1)} %add_convert_fusion.11), channel_id=1, source_target_pairs={{0,4},{2,6},{4,8},{6,10},{8,12},{10,14},{12,0},{14,2},{1,5},{3,7},... | collective-permute-start | bytes 786440 | tf_op jit(solution)/shard_map/ppermute | solution.py:63
  433.6 25.1 %collective-permute-start.80 = (bf16[256,896]{0,1:T(8,128)(2,1)S(1)}, bf16[256,896]{0,1:T(8,128)(2,1)S(1)}, u32[]{:S(2)}, u32[]{:S(2)}) collective-permute-start(bf16[256,896]{0,1:T(8,128)(2,1)S(1)} %pad_maximum_fusion.20), channel_id=1, source_target_pairs={{0,4},{2,6},{4,8},{6,10},{8,12},{10,14},{12,0},{14,2},{1,5},{3,7},... | collective-permute-start | bytes 1376264 | tf_op jit(solution)/shard_map/ppermute | solution.py:63
  433.6 61.9 %collective-permute-start.66 = (f32[32,16,1024]{2,1,0:T(8,128)}, f32[32,16,1024]{2,1,0:T(8,128)}, u32[]{:S(2)}, u32[]{:S(2)}) collective-permute-start(f32[32,16,1024]{2,1,0:T(8,128)} %pad_maximum_fusion.1), channel_id=1, source_target_pairs={{0,1},{17,16},{2,3},{19,18},{4,5},{21,20},{6,7},{23,22},{8,9},{25,... | collective-permute-start | bytes 6291464 | tf_op jit(solution)/shard_map/ppermute | solution.py:831
  458.6 47.1 %collective-permute-start.79 = (bf16[128,2048]{1,0:T(8,128)(2,1)}, bf16[128,2048]{1,0:T(8,128)(2,1)}, u32[]{:S(2)}, u32[]{:S(2)}) collective-permute-start(bf16[128,2048]{1,0:T(8,128)(2,1)} %add_convert_fusion.5), channel_id=1, source_target_pairs={{0,4},{2,6},{4,8},{6,10},{8,12},{10,14},{12,0},{14,2},{1,5},{3,7},... | collective-permute-start | bytes 1572872 | tf_op jit(solution)/shard_map/ppermute | solution.py:63
  464.2 47.4 %collective-permute-start.93 = (bf16[128,2048]{1,0:T(8,128)(2,1)}, bf16[128,2048]{1,0:T(8,128)(2,1)}, u32[]{:S(2)}, u32[]{:S(2)}) collective-permute-start(bf16[128,2048]{1,0:T(8,128)(2,1)} %add_convert_fusion.1), channel_id=1, source_target_pairs={{0,4},{2,6},{4,8},{6,10},{8,12},{10,14},{12,0},{14,2},{1,5},{3,7},... | collective-permute-start | bytes 1572872 | tf_op jit(solution)/shard_map/ppermute | solution.py:63
  504.6 15.6 %collective-permute-start.92 = (bf16[128,2048]{1,0:T(8,128)(2,1)}, bf16[128,2048]{1,0:T(8,128)(2,1)S(1)}, u32[]{:S(2)}, u32[]{:S(2)}) collective-permute-start(bf16[128,2048]{1,0:T(8,128)(2,1)} %get-tuple-element.92), channel_id=1, source_target_pairs={{0,2},{2,0},{4,6},{6,4},{8,10},{10,8},{12,14},{14,12},{1,3},{3,1},... | collective-permute-start | bytes 1572872 | tf_op jit(solution)/shard_map/ppermute | solution.py:60
  505.7 23.9 %collective-permute-start.96 = (bf16[128,1024]{0,1:T(8,128)(2,1)}, bf16[128,1024]{0,1:T(8,128)(2,1)S(1)}, u32[]{:S(2)}, u32[]{:S(2)}) collective-permute-start(bf16[128,1024]{0,1:T(8,128)(2,1)} %pad_maximum_fusion.26), channel_id=1, source_target_pairs={{0,2},{2,0},{4,6},{6,4},{8,10},{10,8},{12,14},{14,12},{1,3},{3,1},... | collective-permute-start | bytes 786440 | tf_op jit(solution)/shard_map/ppermute | solution.py:60
  510.9 25.7 %collective-permute-start.86 = (bf16[128,2176]{1,0:T(8,128)(2,1)S(1)}, bf16[128,2176]{1,0:T(8,128)(2,1)S(1)}, u32[]{:S(2)}, u32[]{:S(2)}) collective-permute-start(bf16[128,2176]{1,0:T(8,128)(2,1)S(1)} %fusion.38), channel_id=1, source_target_pairs={{0,0},{1,16},{16,1},{17,17},{2,2},{3,18},{18,3},{19,19},{4,4},{5,2... | collective-permute-start | bytes 1671176 | tf_op jit(solution)/shard_map/ppermute | solution.py:37
  (136 other events, 1929.8 us)

commit v3 on v2

--- a/solution.py
+++ b/solution.py
@@ -45,6 +45,18 @@
     return lax.dynamic_slice_in_dim(array, block * rows, rows, axis=0)
 
 
+class Flow:
+    def __init__(self):
+        self.landed = ()
+
+    def step(self, *jobs, also=()):
+        operands = tuple(operand for _, operand in jobs)
+        operands = lax.optimization_barrier(operands + self.landed + tuple(also))[: len(jobs)]
+        results = [send(operand) for (send, _), operand in zip(jobs, operands)]
+        self.landed = tuple(results)
+        return results
+
+
 class Ring:
     def __init__(self, dp):
         self.dp = dp
@@ -53,6 +65,7 @@
         pairs = [(z, x) for z in range(self.outer) for x in range(2)]
         self.pair = [(2 * z + x, 2 * z + 1 - x) for z, x in pairs]
         self.ring = [(2 * z + x, 2 * ((z + 1) % self.outer) + x) for z, x in pairs]
+        self.turn = [(b, a) for a, b in self.ring]
         place = lax.axis_index("dp")
         self.z, self.x = place // 2, place % 2
 
@@ -61,6 +74,9 @@
 
     def onward(self, array):
         return lax.ppermute(array, "dp", self.ring)
+
+    def astern(self, array):
+        return lax.ppermute(array, "dp", self.turn)
 
     def back(self, k):
         return lax.rem(self.z - k + self.outer, self.outer)
@@ -86,7 +102,7 @@
     return 0.5 * jnp.tanh(0.5 * x) + 0.5
 
 
-def fetch(blocks, places, side_blocks, target, sems, first=0):
+def fetch(blocks, places, side_blocks, target, sems, first=0, column=0):
     wide_half = target.shape[1] // 2
     columns = pl.ds(pl.multiple_of(side_blocks * wide_half, wide_half), wide_half)
     copies = []
@@ -95,13 +111,15 @@
         span = pl.ds(pl.multiple_of(places[1 + k] * height, height), height)
         copies.append(
             pltpu.make_async_copy(
-                block.at[:, :wide_half], target.at[span, columns], sems.at[first + k]
+                block.at[:, column : column + wide_half],
+                target.at[span, columns],
+                sems.at[first + k],
             )
         )
     return copies
 
 
-def forward_kernel(count, places, normed, b_own, b_other, *refs):
+def forward_kernel(count, column, places, normed, b_own, b_other, *refs):
     in_own, in_other, w_own, w_other = [refs[n * count : (n + 1) * count] for n in range(4)]
     quarters, before, gates, cells, wi, w, b, state, cell, sems = refs[4 * count :]
     steps, rows, wide_full = gates.shape
@@ -110,8 +128,8 @@
     chunk = min(256, unit_half)
     s = places[0]
     copies = fetch(in_own, places, s, wi, sems) + fetch(in_other, places, 1 - s, wi, sems, count)
-    later = fetch(w_own, places, s, w, sems, 2 * count)
-    later += fetch(w_other, places, 1 - s, w, sems, 3 * count)
+    later = fetch(w_own, places, s, w, sems, 2 * count, column)
+    later += fetch(w_other, places, 1 - s, w, sems, 3 * count, column)
     for copy in copies + later:
         copy.start()
     for source, at in ((b_own, s), (b_other, 1 - s)):
@@ -159,13 +177,13 @@
     lax.fori_loop(0, steps, advance, 0)
 
 
-def run_forward(places, normed, b_own, b_other, in_own, in_other, w_own, w_other, steps):
+def run_forward(places, normed, b_own, b_other, in_own, in_other, w_own, w_other, steps, column):
     rows = normed.shape[0] // steps
     units = normed.shape[1]
     wide_half = b_own.shape[1]
     count = len(w_own)
     return pl.pallas_call(
-        functools.partial(forward_kernel, count),
+        functools.partial(forward_kernel, count, column),
         out_shape=(
             jax.ShapeDtypeStruct((2, steps, rows // 2, units), low),
             jax.ShapeDtypeStruct((steps, rows, units), low),
@@ -187,42 +205,14 @@
     )(places, normed, b_own, b_other, *in_own, *in_other, *w_own, *w_other)
 
 
-def backward_kernel(count, places, outside, gates, cells, *refs):
-    w_own, w_other = refs[:count], refs[count : 2 * count]
-    dz, stage, w, dh, dc, sems = refs[2 * count :]
-    steps, rows, wide_full = gates.shape
+def backward_steps(first, last, outside, gates, cells, dz, w, dh, dc):
+    _, rows, wide_full = gates.shape
     wide_half = wide_full // 2
     unit_half = wide_half // 4
     chunk = min(256, unit_half)
-    s = places[0]
-    jobs = []
-    for n, (sources, at) in enumerate(((w_own, s), (w_other, 1 - s))):
-        for k, block in enumerate(sources):
-            slot = n * count + k
-            copy = pltpu.make_async_copy(
-                block.at[:, :wide_half], stage.at[slot], sems.at[slot]
-            )
-            copy.start()
-            jobs.append((copy, slot, at, places[1 + k] * block.shape[0]))
-    dh[...] = jnp.zeros_like(dh)
-    dc[...] = jnp.zeros_like(dc)
-    height = w_own[0].shape[0]
-    piece = min(height, 128)
-    for copy, slot, at, first in jobs:
-        copy.wait()
-
-        def turn(g, carried, slot=slot, at=at, first=first):
-            columns = pl.ds(pl.multiple_of(g * unit_half, unit_half), unit_half)
-            span = pl.ds(pl.multiple_of(at * wide_half + g * unit_half, unit_half), unit_half)
-            for low_row in range(0, height, piece):
-                into = pl.ds(pl.multiple_of(first + low_row, piece), piece)
-                w[span, into] = stage[slot, low_row : low_row + piece, columns].T
-            return carried
-
-        lax.fori_loop(0, 4, turn, 0)
 
     def retreat(k, carried):
-        t = steps - 1 - k
+        t = first - 1 - k
         earlier = jnp.maximum(t - 1, 0)
         live = jnp.where(t > 0, 1.0, 0.0).astype(wide)
         for at in range(0, 2 * unit_half, chunk):
@@ -245,41 +235,111 @@
                 grad * squash * o * (1.0 - o),
             )
             for n, part in enumerate(parts):
-                dz[half, t, :, pl.ds(n * unit_half + inside, chunk)] = part.astype(low)
+                dz[half, t - last, :, pl.ds(n * unit_half + inside, chunk)] = part.astype(low)
             dc[:, units] = total * f
-        first, second = dz[0, t], dz[1, t]
+        upper, lower = dz[0, t - last], dz[1, t - last]
         for at in range(0, 2 * unit_half, chunk):
             units = pl.ds(at, chunk)
             dh[:, units] = jnp.dot(
-                first, w[:wide_half, units], preferred_element_type=wide
-            ) + jnp.dot(second, w[wide_half:, units], preferred_element_type=wide)
+                upper, w[:wide_half, units], preferred_element_type=wide
+            ) + jnp.dot(lower, w[wide_half:, units], preferred_element_type=wide)
         return carried
 
-    lax.fori_loop(0, steps, retreat, 0)
-
-
-def run_backward(places, outside, gates, cells, w_own, w_other):
+    lax.fori_loop(0, first - last, retreat, 0)
+
+
+def late_kernel(count, column, middle, places, outside, gates, cells, *refs):
+    w_own, w_other = refs[:count], refs[count : 2 * count]
+    dz, turned, dh, dc, stage, w, sems, out_sem = refs[2 * count :]
+    steps, _, wide_full = gates.shape
+    wide_half = wide_full // 2
+    unit_half = wide_half // 4
+    s = places[0]
+    jobs = []
+    for n, (sources, at) in enumerate(((w_own, s), (w_other, 1 - s))):
+        for k, block in enumerate(sources):
+            slot = n * count + k
+            copy = pltpu.make_async_copy(
+                block.at[:, column : column + wide_half], stage.at[slot], sems.at[slot]
+            )
+            copy.start()
+            jobs.append((copy, slot, at, places[1 + k] * block.shape[0]))
+    dh[...] = jnp.zeros_like(dh)
+    dc[...] = jnp.zeros_like(dc)
+    height = w_own[0].shape[0]
+    piece = min(height, 128)
+    for copy, slot, at, first in jobs:
+        copy.wait()
+
+        def turn(g, carried, slot=slot, at=at, first=first):
+            columns = pl.ds(pl.multiple_of(g * unit_half, unit_half), unit_half)
+            span = pl.ds(pl.multiple_of(at * wide_half + g * unit_half, unit_half), unit_half)
+            for low_row in range(0, height, piece):
+                into = pl.ds(pl.multiple_of(first + low_row, piece), piece)
+                w[span, into] = stage[slot, low_row : low_row + piece, columns].T
+            return carried
+
+        lax.fori_loop(0, 4, turn, 0)
+    save = pltpu.make_async_copy(w, turned, out_sem)
+    save.start()
+    backward_steps(steps, middle, outside, gates, cells, dz, w, dh, dc)
+    save.wait()
+
+
+def early_kernel(middle, outside, gates, cells, dh_in, dc_in, turned, dz, w, dh, dc, sem):
+    load = pltpu.make_async_copy(turned, w, sem)
+    load.start()
+    dh[...] = dh_in[...]
+    dc[...] = dc_in[...]
+    load.wait()
+    backward_steps(middle, 0, outside, gates, cells, dz, w, dh, dc)
+
+
+def run_late(places, outside, gates, cells, w_own, w_other, column, middle):
     steps, rows, wide_full = gates.shape
     units = cells.shape[2]
     count = len(w_own)
     return pl.pallas_call(
-        functools.partial(backward_kernel, count),
-        out_shape=jax.ShapeDtypeStruct((2, steps, rows, wide_full // 2), low),
+        functools.partial(late_kernel, count, column, middle),
+        out_shape=(
+            jax.ShapeDtypeStruct((2, steps - middle, rows, wide_full // 2), low),
+            jax.ShapeDtypeStruct((wide_full, units), low),
+            jax.ShapeDtypeStruct((rows, units), wide),
+            jax.ShapeDtypeStruct((rows, units), wide),
+        ),
         in_specs=[in_smem] + [in_vmem] * 3 + [in_place] * (2 * count),
-        out_specs=in_vmem,
+        out_specs=[in_vmem, in_place, in_vmem, in_vmem],
         scratch_shapes=[
             pltpu.VMEM((2 * count, units // count, wide_full // 2), low),
             pltpu.VMEM((wide_full, units), low),
+            pltpu.SemaphoreType.DMA((2 * count,)),
+            pltpu.SemaphoreType.DMA,
+        ],
+        compiler_params=pltpu.CompilerParams(vmem_limit_bytes=56 << 20),
+        name="recur_backward_late",
+    )(places, outside, gates, cells, *w_own, *w_other)
+
+
+def run_early(outside, gates, cells, dh, dc, turned, middle):
+    steps, rows, wide_full = gates.shape
+    units = cells.shape[2]
+    return pl.pallas_call(
+        functools.partial(early_kernel, middle),
+        out_shape=jax.ShapeDtypeStruct((2, middle, rows, wide_full // 2), low),
+        in_specs=[in_vmem] * 5 + [in_place],
+        out_specs=in_vmem,
+        scratch_shapes=[
+            pltpu.VMEM((wide_full, units), low),
             pltpu.VMEM((rows, units), wide),
             pltpu.VMEM((rows, units), wide),
-            pltpu.SemaphoreType.DMA((2 * count,)),
+            pltpu.SemaphoreType.DMA,
         ],
         compiler_params=pltpu.CompilerParams(vmem_limit_bytes=56 << 20),
-        name="recur_backward",
-    )(places, outside, gates, cells, *w_own, *w_other)
-
-
-def input_kernel(count, places, inputs, gain, dz, *refs):
+        name="recur_backward_early",
+    )(outside, gates, cells, dh, dc, turned)
+
+
+def input_kernel(count, places, inputs, gain, dz, dz_given, *refs):
     in_own, in_other = refs[:count], refs[count : 2 * count]
     grad_inputs, grad_gain, wi, sems = refs[2 * count :]
     s = places[0]
@@ -293,7 +353,9 @@
     for copy in copies:
         copy.wait()
     wide_half = wi.shape[1] // 2
-    grad = dot_nt(dz[0], wi[:, :wide_half]) + dot_nt(dz[1], wi[:, wide_half:])
+    own = pl.ds(pl.multiple_of(s * wide_half, wide_half), wide_half)
+    other = pl.ds(pl.multiple_of((1 - s) * wide_half, wide_half), wide_half)
+    grad = dot_nt(dz[...], wi[:, own]) + dot_nt(dz_given[...], wi[:, other])
     grad_gain[...] = jnp.sum(grad * shape, axis=0, keepdims=True)
     pulled = grad * gain[...]
     grad_inputs[...] = scale * (
@@ -303,7 +365,7 @@
     )
 
 
-def run_input(places, inputs, gain, dz, in_own, in_other):
+def run_input(places, inputs, gain, dz, dz_given, in_own, in_other):
     count = len(in_own)
     rows, width = inputs.shape
     return pl.pallas_call(
@@ -312,15 +374,15 @@
             jax.ShapeDtypeStruct((rows, width), wide),
             jax.ShapeDtypeStruct((1, width), wide),
         ),
-        in_specs=[in_smem] + [in_vmem] * 3 + [in_place] * (2 * count),
+        in_specs=[in_smem] + [in_vmem] * 4 + [in_place] * (2 * count),
         out_specs=[in_vmem] * 2,
         scratch_shapes=[
-            pltpu.VMEM((width, 2 * dz.shape[2]), low),
+            pltpu.VMEM((width, 2 * dz.shape[1]), low),
             pltpu.SemaphoreType.DMA((2 * count,)),
         ],
         compiler_params=pltpu.CompilerParams(vmem_limit_bytes=56 << 20),
         name="input_back",
-    )(places, inputs, gain, dz, *in_own, *in_other)
+    )(places, inputs, gain, dz, dz_given, *in_own, *in_other)
 
 
 def dot_nt(a, b):
@@ -645,10 +707,9 @@
     vocab_size = vocab_weight.shape[1]
     vocab_pad = 4 * block
 
-    in_shard = corners(lstm_in[0].reshape(shard_rows, wide_half))
-    rec_shard = corners(lstm_rec[0].reshape(shard_rows, wide_half))
-    b_own = corners(lstm_bias[0].reshape(1, wide_half)).astype(wide)
-    b_other = across_cores(b_own)
+    in_shard = lstm_in[0].reshape(shard_rows, wide_half)
+    rec_shard = lstm_rec[0].reshape(shard_rows, wide_half)
+    bias_shard = lstm_bias[0].reshape(1, wide_half)
 
     def of_section(array):
         return jnp.where(s == y, array, across_cores(array))
@@ -675,9 +736,6 @@
     bias_row = jnp.pad(vocab_bias, (0, vocab_pad - vocab_size), constant_values=-1e30)[None]
 
     vector_own = jnp.stack([mono_bias, mono_vec, span_bias, span_vec, out_bias])
-    vector_pair = jnp.concatenate([vector_own, across_chips(vector_own)], axis=1)
-    vectors = jnp.concatenate([vector_pair, across_cores(vector_pair)], axis=1)
-    vectors = jnp.pad(vectors, ((0, 3), (0, 0)))
     vocab_own = jnp.pad(vocab_weight, ((0, 0), (0, vocab_pad - vocab_size)))
     ready = (noise_part, length_part, label_part, counted, bias_row, normed_own, normed_other)
     places, in_own, rec_own, small_own, small_chip = [], [], [], [], []
@@ -685,61 +743,70 @@
         [mono_mem, span_mem, mono_dec, span_dec, out_weight[0], out_weight[1]], axis=1
     )
     if ring.short:
-        small_far, small_next = ring.across(small), ring.onward(small)
-        in_shard, rec_shard, b_own, small_far, small_next = lax.optimization_barrier(
-            (in_shard, rec_shard, b_own, small_far, small_next)
-        )
-        vocab_chip = across_chips(tie(vocab_own, in_shard))
-        small_own.append(jnp.concatenate([small, small_far], axis=1))
-        first = jnp.concatenate([in_shard, small_next], axis=1)
-        second = rec_shard
-        places = [ring.back(k // 2) * 2 + (ring.x if k % 2 == 0 else 1 - ring.x) for k in range(8)]
-        in_other, rec_other, small_core = [], [], []
-        earlier = ()
+        flow, across, onward = Flow(), ring.across, ring.onward
+        both = 2 * wide_half
+        corner = jnp.pad(bias_shard.reshape(shard_rows, -1), ((0, 0), (0, 128 - 16)))
+        corner = jnp.concatenate([in_shard, rec_shard, corner], axis=1)
+        corner, vector_pair, small_far, small_next = flow.step(
+            (corners, corner), (across_chips, vector_own), (across, small), (onward, small)
+        )
+        b_own = corner[:, both : both + 16].astype(wide).reshape(1, wide_half)
+        vector_pair = jnp.concatenate([vector_own, vector_pair], axis=1)
+        small_own = [jnp.concatenate([small, small_far], axis=1)]
+        small_chip, small_core = [], []
+        held = jnp.concatenate([corner[:, :both], small_next], axis=1)
+        near, far, near_core, far_core = [], [], [], []
         for k in range(ring.outer):
-            if k:
-                first = tie(first, *earlier, *ready)
-                ready = ()
-            earlier = (second,)
-            if k == 1:
-                earlier += (vocab_chip, vectors, b_other)
-            if k == 2:
-                earlier += (vocab[2], vocab[3])
-            in_other += [across_cores(part) for part in in_own[len(in_other) :]]
-            rec_other += [across_cores(part) for part in rec_own[len(rec_other) :]]
-            small_core += [across_cores(small_own[-1])]
-            small_chip += [across_chips(small_own[-1])]
-            if k:
-                earlier += (*in_other[-2:], *rec_other[-2:], small_core[-1], small_chip[-2])
-            if k == 1:
-                vocab = [vocab_own, vocab_chip, across_cores(vocab_own), across_cores(vocab_chip)]
-            far, far_rec = ring.across(first), ring.across(second)
-            in_own += [first, far]
-            rec_own += [second, far_rec]
-            earlier += (far, far_rec)
+            near.append(held)
+            jobs = [(across, held), (across_chips, small_own[k])]
             if k < ring.outer - 1:
-                small_own.append(
-                    jnp.concatenate([first[:, wide_half:], far[:, wide_half:]], axis=1)
-                )
-                first = ring.onward(first if k < ring.outer - 2 else first[:, :wide_half])
-                second = ring.onward(second)
-        in_other += [across_cores(part) for part in in_own[len(in_other) :]]
-        rec_other += [across_cores(part) for part in rec_own[len(rec_other) :]]
+                jobs.append((onward, held[:, :both] if k == ring.outer - 2 else held))
+            if k == 0:
+                jobs.append((across_chips, vocab_own))
+            results = flow.step(*jobs, also=ready if k == 1 else ())
+            far.append(results[0])
+            small_chip.append(results[1])
+            if k == 0:
+                vocab_chip = results[3]
+            if k < ring.outer - 1:
+                small_own.append(jnp.concatenate([held[:, both:], far[k][:, both:]], axis=1))
+                held = results[2]
+        for a, b in zip(near, far):
+            near_core.append(across_cores(a))
+            far_core.append(across_cores(b))
+        small_core = [across_cores(a) for a in small_own]
+        b_other = across_cores(b_own)
+        vocab = [vocab_own, vocab_chip, across_cores(vocab_own), across_cores(vocab_chip)]
+        vector_core = across_cores(vector_pair)
+        in_own = [a for pair in zip(near, far) for a in pair]
+        in_other = [a for pair in zip(near_core, far_core) for a in pair]
+        rec_own, rec_other, rec_column = in_own, in_other, wide_half
+        for k in range(ring.outer):
+            places += [ring.back(k) * 2 + ring.x, ring.back(k) * 2 + 1 - ring.x]
     else:
         vocab_chip = across_chips(vocab_own)
         small, in_block, rec_block = [
-            lax.all_gather(a, "dp", axis=0, tiled=True) for a in (small, in_shard, rec_shard)
+            lax.all_gather(a, "dp", axis=0, tiled=True)
+            for a in (small, corners(in_shard), corners(rec_shard))
         ]
         places, in_own, rec_own = [jnp.int32(0)], [in_block], [rec_block]
         small_own, small_chip = [small], [across_chips(small)]
         vocab = [vocab_own, vocab_chip, across_cores(vocab_own), across_cores(vocab_chip)]
-        in_other, rec_other = [across_cores(in_block)], [across_cores(rec_block)]
+        in_other, rec_other, rec_column = [across_cores(in_block)], [across_cores(rec_block)], 0
         small_core = [across_cores(small)]
+        b_own = corners(bias_shard).astype(wide)
+        b_other = across_cores(b_own)
+        vector_pair = across_chips(vector_own)
+        vector_pair = jnp.concatenate([vector_own, vector_pair], axis=1)
+        vector_core = across_cores(vector_pair)
+    vectors = jnp.concatenate([vector_pair, vector_core], axis=1)
+    vectors = jnp.pad(vectors, ((0, 3), (0, 0)))
     places = jnp.stack([s] + places).astype(jnp.int32)
     places = tie(places, vectors, *vocab, *ready, *small_chip[:-1], *small_core)
 
     quarters, before, gates, cells = run_forward(
-        places, normed_own, b_own, b_other, in_own, in_other, rec_own, rec_other, frames
+        places, normed_own, b_own, b_other, in_own, in_other, rec_own, rec_other, frames,
+        rec_column,
     )
 
     kept = lax.dynamic_index_in_dim(quarters, y, axis=0, keepdims=False)
@@ -747,6 +814,7 @@
     taken = across_chips(given)
     memory = jnp.where(y == 0, kept, taken).reshape(rows, width)
     decoded = jnp.where(y == 0, taken, kept).reshape(rows, width)
+    small_chip[-1] = tie(small_chip[-1], kept)
     small_both = [across_cores(part) for part in small_chip]
     smalls = [small_own, small_chip, small_core, small_both]
     grad_memory, grad_decoded, pack, seen, sums = run_attend(
@@ -773,51 +841,68 @@
     vector_pair = blocks[:, :2] + across_cores(blocks[:, 2:])
     bias_pair = sums[5] + across_cores(sums[5])
     vector_out = jnp.concatenate([vector_pair[:, 1].reshape(-1), bias_pair])
-    places_back, pack_out, vector_out, states_core = lax.optimization_barrier(
-        (places, pack_out, vector_out, states_core, outside, before_peer)
-    )[:4]
-    dz = run_backward(places_back, outside, gates, cells, rec_own, rec_other)
-
-    dz = dz.reshape(2, frames * half, wide_half)
-    dz_kept = lax.dynamic_index_in_dim(dz, s, axis=0, keepdims=False)
-    dz_given = lax.dynamic_index_in_dim(dz, 1 - s, axis=0, keepdims=False)
-    dz_all = jnp.concatenate([dz_kept, across_cores(dz_given)], axis=0)
-    before_all = jnp.concatenate([before, before_peer], axis=0)
-    normed_all = jnp.concatenate([normed_own, normed_other], axis=0)
-    rec_total = dot_tn(before_all, dz_all).astype(low)
-    in_total = dot_tn(normed_all, dz_all).astype(low)
-
+    vector_count = vector_out.shape[0] // (2 * rows)
+    places_back, pack_out, states_core = lax.optimization_barrier(
+        (places, pack_out, states_core, outside, before_peer)
+    )[:3]
+    middle = frames * 3 // 8
+    dz_late, turned, dh, dc = run_late(
+        places_back, outside, gates, cells, rec_own, rec_other, rec_column, middle
+    )
     pack_far = across_chips(pack_out)
-    seen_far = across_chips(tie(seen, pack_out))
-    vector_far = across_chips(vector_out)
-    seen_pair = jnp.concatenate([seen, seen_far], axis=0)
-    seen_core = across_cores(seen_pair)
-
-    def gathered(n):
-        return jnp.concatenate(
-            [states[n], states_core[n], states[n + 1], states_core[n + 1]], axis=0
-        )
-
-    memory_all, decoded_all = gathered(0), gathered(2)
+    seen_out = jnp.concatenate(
+        [seen, halves(vector_out, 2 * rows).reshape(2, rows, -1)], axis=2
+    )
+    seen_far = across_chips(tie(seen_out, pack_out))
     pack_all = jnp.concatenate([pack[0], pack_core[0], pack_far[0], pack_far[1]], axis=0)
-    seen_all = [
-        jnp.concatenate([seen_pair[n], seen_core[n], seen_pair[2 + n], seen_core[2 + n]], axis=0)
-        for n in range(2)
+    memory_all, decoded_all = [
+        jnp.concatenate([states[n], states_core[n], states[n + 1], states_core[n + 1]], axis=0)
+        for n in (0, 2)
     ]
     energy_total = [
         dot_tn(memory_all, pack_all[:, : 2 * block]).astype(low),
         dot_tn(decoded_all, pack_all[:, 2 * block : 4 * block]).astype(low),
     ]
     grad_pre = pack_all[:, 4 * block : 5 * block]
+    decoded_total = dot_tn(decoded_all, grad_pre).astype(low)
+    dh, *energy_total, decoded_total = lax.optimization_barrier((dh, *energy_total, decoded_total))
+    dz_early = run_early(outside, gates, cells, dh, dc, turned, middle)
+
+    def rows_of(part, at):
+        part = lax.dynamic_index_in_dim(part, at, axis=0, keepdims=False)
+        return part.reshape(-1, wide_half)
+
+    dz_kept = jnp.concatenate([rows_of(dz_early, s), rows_of(dz_late, s)], axis=0)
+    dz_given = jnp.concatenate([rows_of(dz_early, 1 - s), rows_of(dz_late, 1 - s)], axis=0)
+    dz_all = jnp.concatenate([dz_kept, across_cores(dz_given)], axis=0)
+    before_all = jnp.concatenate([before, before_peer], axis=0)
+    normed_all = jnp.concatenate([normed_own, normed_other], axis=0)
+    rec_total = dot_tn(before_all, dz_all).astype(low)
+    in_total = dot_tn(normed_all, dz_all).astype(low)
+
+    vector_far = joined(seen_far[:, :, seen.shape[2] :].reshape(2 * rows, -1), vector_count)
+    vector_far = vector_far.reshape(-1)
+    seen_far = seen_far[:, :, : seen.shape[2]]
+    seen_pair = jnp.concatenate([seen, seen_far], axis=0)
+    seen_core = across_cores(seen_pair)
+
+    seen_all = [
+        jnp.concatenate([seen_pair[n], seen_core[n], seen_pair[2 + n], seen_core[2 + n]], axis=0)
+        for n in range(2)
+    ]
     output_total = [
-        dot_tn(decoded_all, grad_pre).astype(low),
+        decoded_total,
         dot_tn(seen_all[0], grad_pre).astype(low),
         dot_tn(seen_all[1], pack_all[:, 5 * block :]).astype(low),
     ]
 
-    def input_back(dz):
+    def to_other_chip(section):
+        return lax.ppermute(section, ("section", "mp"), [(0, 1), (3, 2)])
+
+    def input_back(dz_kept):
         grad_inputs, grad_gain = run_input(
-            places, inputs_own.reshape(frames * half, width), gain[None], dz, in_own, in_other
+            places, inputs_own.reshape(frames * half, width), gain[None], dz_kept, dz_given,
+            in_own, in_other,
         )
         grad_inputs = jnp.swapaxes(grad_inputs.reshape(frames, half, width), 0, 1)
         grad_peer = across_cores(grad_inputs)
@@ -828,7 +913,6 @@
             ],
             axis=0,
         )
-        far = lax.ppermute(section, ("section", "mp"), [(0, 1), (3, 2)])
         grad_gain = grad_gain.reshape(width)
         gain_sum = grad_gain + across_cores(grad_gain)
         flat = jnp.concatenate(
@@ -839,71 +923,78 @@
                 gain_sum,
             ]
         )
-        return section, far, jnp.pad(flat, (0, -flat.shape[0] % (2 * shard_rows)))
+        return section, jnp.pad(flat, (0, -flat.shape[0] % (2 * shard_rows)))
 
     if ring.short:
-        r = shard_rows
-        back, x, onward, across = ring.back, ring.x, ring.onward, ring.across
-        chains = [[rec_total], [in_total], energy_total]
-        sums_so_far = [None] * 3
-        arrived, passed = {}, {}
-        held = flat_sum = None
-        for k in range(1, 5):
-            for n, group in enumerate(chains):
-                theirs = ring.part(group, back(k) * 2 + 1 - x, r)
-                if k > 2:
-                    theirs = tie(theirs, passed[n, k - 2], arrived[n, k - 1], passed[3, k - 2])
-                if k == 4:
-                    theirs = tie(theirs, grad_far)
-                arrived[n, k] = across(theirs)
-                total = ring.part(group, back(k) * 2 + x, r).astype(wide)
-                total = total + arrived[n, k].astype(wide)
-                if k > 1:
-                    total = total + passed[n, k - 1].astype(wide)
-                sums_so_far[n] = total
-                if k < 4:
-                    passed[n, k] = onward(total.astype(low))
-            if k == 1:
-                grad_section, grad_far, flat = input_back(tie(dz, arrived[0, 1]))
-                flat_sum = flat
-                flat_width = flat.shape[0] // (2 * r)
-                held = jnp.concatenate(
-                    [ring.part(output_total, back(1), 2 * r), halves(flat, 2 * r)], axis=1
-                )
-            if k < 4:
-                passed[3, k] = onward(held)
-                ours = ring.part(output_total, back(k + 1), 2 * r).astype(wide)
-                columns = ours.shape[1]
-                ours = (ours + passed[3, k][:, :columns].astype(wide)).astype(low)
-                flat_sum = flat_sum + joined(passed[3, k][:, columns:], flat_width).reshape(-1)
-                held = jnp.concatenate([ours, passed[3, k][:, columns:]], axis=1)
-        ours = held[:, :columns]
-        message = jnp.concatenate(
-            [cut(ours, 1 - x, r), halves(flat_sum, 2 * r).reshape(r, -1)], axis=1
-        )
-        message = across(tie(message, arrived[2, 3]))
-        output_grad = cut(ours, x, r).astype(wide) + message[:, :columns].astype(wide)
-        flat = flat_sum + joined(
-            message[:, columns:].reshape(2 * r, -1), flat_width
-        ).reshape(-1)
-        shard = output_grad[:, 2 * block :].astype(low)
-        held = jnp.concatenate([shard, across(shard)], axis=1)
+        r, x = shard_rows, ring.x
+        columns = 3 * block
+        flow, across, onward = Flow(), ring.across, ring.onward
+        chain = [rec_total, in_total] + energy_total
+
+        def theirs(k):
+            return ring.part(chain, ring.back(k) * 2 + 1 - x, r)
+
+        def total(k, arrived, passed):
+            value = ring.part(chain, ring.back(k) * 2 + x, r).astype(wide)
+            value = value + arrived.astype(wide)
+            return value if passed is None else value + passed.astype(wide)
+
+        def output_part(k):
+            return ring.part(output_total, ring.back(k), 2 * r)
+
+        def output_sum(k, arrived):
+            return output_part(k).astype(wide) + arrived.astype(wide)
+
+        arrived, out = flow.step((across, theirs(1)), (onward, output_part(1)))
+        grad_section, flat = input_back(tie(dz_kept, arrived))
+        out = onward(output_sum(2, out).astype(low))
+        value = total(1, arrived, None).astype(low)
+        passed, arrived, out, grad_far = flow.step(
+            (onward, value), (across, theirs(2)), (onward, output_sum(3, out).astype(low)),
+            (to_other_chip, grad_section), also=(out,),
+        )
+        out = output_sum(4, out)
+        value = total(2, arrived, passed).astype(low)
+        passed, arrived, out_far = flow.step(
+            (onward, value), (across, theirs(3)), (across, cut(out, 1 - x, r).astype(low))
+        )
+        output_grad = cut(out, x, r) + out_far.astype(wide)
+        flat_width = flat.shape[0] // r
+        shard = jnp.concatenate(
+            [output_grad[:, 2 * block :].astype(low), halves(flat, r)], axis=1
+        )
+        value = total(3, arrived, passed).astype(low)
+        passed, arrived, shard_far = flow.step(
+            (onward, value), (across, theirs(4)), (across, shard)
+        )
+        flat = flat + joined(shard_far[:, block:], flat_width).reshape(-1)
+        shard = jnp.concatenate([shard[:, :block], shard_far[:, :block], halves(flat, r)], axis=1)
+        chain_grad = total(4, arrived, passed)
+        moved = chain_grad[:, : 2 * wide_half].astype(low)
+        moved, next_one, next_three = flow.step(
+            (corners, moved), (onward, shard), (ring.astern, shard)
+        )
+        shards = {0: shard, 1: next_one, 3: next_three, 2: onward(next_one)}
         vocab_grad = jnp.zeros((vocab_pad, block), low)
-        for k in range(4):
+        flat = 0.0
+        for k, held in shards.items():
+            flat = flat + joined(held[:, 2 * block :], flat_width).reshape(-1)
             for n, at in enumerate((x, 1 - x)):
                 vocab_grad = lax.dynamic_update_slice(
-                    vocab_grad, held[:, n * block : (n + 1) * block], ((back(k) * 2 + at) * r, 0)
+                    vocab_grad,
+                    held[:, n * block : (n + 1) * block],
+                    ((ring.back(k) * 2 + at) * r, 0),
                 )
-            if k < 3:
-                held = onward(held)
-        rec_grad, in_grad, energy_grad = sums_so_far
+        energy_grad = chain_grad[:, 2 * wide_half :]
     else:
-        grad_section, grad_far, flat = input_back(dz)
+        grad_section, flat = input_back(dz_kept)
+        grad_far = to_other_chip(grad_section)
 
         def scatter(total):
             return lax.psum_scatter(total, "dp", scatter_dimension=0, tiled=True).astype(wide)
 
-        rec_grad, in_grad = scatter(rec_total), scatter(in_total)
+        moved = jnp.concatenate([scatter(rec_total), scatter(in_total)], axis=1)
+        moved = corners(moved.astype(low))
         energy_grad = jnp.concatenate([scatter(a) for a in energy_total], axis=1)
         output_grad = jnp.concatenate([scatter(a) for a in output_total], axis=1)
         flat = lax.psum(flat, "dp")
@@ -916,13 +1007,11 @@
     ends = [5 * block, 5 * block + vocab_pad, 5 * block + vocab_pad + wide_half + width]
     vector_sum = flat[: ends[0]].reshape(5, block)
     bias_sum = flat[ends[0] : ends[0] + vocab_size]
-    moved = halves(flat[ends[1] : ends[2]], shard_rows)
-    moved = corners(jnp.concatenate([rec_grad.astype(low), moved], axis=1))
+    sides = corners(flat[ends[1] : ends[2]])
+    lstm_bias_sum = sides[:wide_half].reshape(1, 4, unit_half)
+    gain_sum = sides[wide_half:][None]
     rec_grad = moved[:, :wide_half].astype(wide).reshape(1, shard_rows, 4, unit_half)
-    moved = joined(moved[:, wide_half:], (ends[2] - ends[1]) // shard_rows).reshape(-1)
-    lstm_bias_sum = moved[:wide_half].reshape(1, 4, unit_half)
-    gain_sum = moved[wide_half:][None]
-    in_grad = corners(in_grad.astype(low)).astype(wide).reshape(1, shard_rows, 4, unit_half)
+    in_grad = moved[:, wide_half:].astype(wide).reshape(1, shard_rows, 4, unit_half)
     mono_mem_grad, span_mem_grad, mono_dec_grad, span_dec_grad = [
         energy_grad[:, n * block : (n + 1) * block] for n in range(4)
     ]

time: 549 us -> 543 us (0.989)
  starting transfers between devices: 71.9 us -> 51 us
  waiting for transfers between devices: 243 us -> 263 us
  other arithmetic: 46 us -> 38.9 us
  Pallas kernels: 103 us -> 109 us
    ppermute x23 -> x11, waiting for transfers between devices: 102 us -> 148 us  [across(): return lax.ppermute(array, 'dp', self.pair)]
    ppermute x22 -> x12, waiting for transfers between devices: 90.8 us -> 73.6 us  [onward(): return lax.ppermute(array, 'dp', self.ring)]
    ppermute x12 -> x11, waiting for transfers between devices: 45.1 us -> 29.9 us  [across_chips(): return lax.ppermute(array, 'mp', core_swap)]
    ppermute x23 -> x11, starting transfers between devices: 26.2 us -> 13 us  [across(): return lax.ppermute(array, 'dp', self.pair)]
    convert_element_type x15 -> x5, other arithmetic: 20 us -> 6.91 us  [the longest x1 2.8 us: local(): value = total(3, arrived, passed).astype(low)]
    ppermute x5 -> x3, starting transfers between devices: 14 us -> 3.26 us  [corners(): return lax.ppermute(array, ('section', 'mp'), corner_swap)]
    pallas_call x2 -> x3, Pallas kernels: 60.6 us -> 67.5 us  [the longest x1 30.6 us: run_forward(): pl.pallas_call(functools.partial(forward_kernel, count, column), out_shap...]
    ppermute x39 -> x31, waiting for transfers between devices: 5.14 us -> 11.9 us  [across_cores(): return lax.ppermute(array, 'section', core_swap)]
  transfers between devices with their start and end apart: 102 -> 70, of which waited for: 38 -> 30; matrix products, arithmetic and copies ran while one was open for 20% -> 15% of each run, Pallas kernels for 19% -> 19%
where the time goes in v3:
time: 543 us; the launch traced here: 535 us
  waiting for transfers between devices  263 us (48%)
  Pallas kernels  109 us (20%)
  local copies, waits for them, and re-layouts  59.9 us (11%)
  starting transfers between devices  51 us (9%)
  other arithmetic  38.9 us (7%)
  matrix products  9.96 us (2%)
    ppermute x11, waiting for transfers between devices, across(): return lax.ppermute(array, 'dp', self.pair)  148 us
    ppermute x12, waiting for transfers between devices, onward(): return lax.ppermute(array, 'dp', self.ring)  73.6 us
    pallas_call x1, Pallas kernels, run_attend(): pl.pallas_call(functools.partial(attend_kernel, count), out_shape=(jax.Sh...  33 us
    pallas_call x1, Pallas kernels, run_forward(): pl.pallas_call(functools.partial(forward_kernel, count, column), out_shap...  30.6 us
    ppermute x11, waiting for transfers between devices, across_chips(): return lax.ppermute(array, 'mp', core_swap)  29.9 us
    pallas_call x1, Pallas kernels, run_late(): pl.pallas_call(functools.partial(late_kernel, count, column, middle), out...  23.3 us
    ppermute x11, starting transfers between devices, across_chips(): return lax.ppermute(array, 'mp', core_swap)  17.2 us
    unnamed x200, local copies, waits for them, and re-layouts  16.1 us
  transfers between devices with their start and end apart: 70, of which 30 were waited for; matrix products, arithmetic and copies ran while one was open for 15% of the time, Pallas kernels for 19%

profile of v3, /device:TPU:0, one launch (start us, length us, event | category | flops | bytes accessed | tf_op | source)
XLA Modules:
  0.0 535.0 jit_solution(17999909778215475109)
XLA Ops:
  9.7 2.5 collective-permute-start
  12.2 1.9 collective-permute-start.2
  14.1 1.5 collective-permute-start.4
  19.9 1.6 collective-permute-start.3
  21.5 4.3 collective-permute-done.4
  26.6 1.3 broadcast_select_fusion
  29.1 4.0 collective-permute-done.3
  34.7 2.0 collective-permute-start.10
  39.3 26.7 %collective-permute-done.12.refs_1_.refs_17_ = bf16[128,5632]{1,0:T(8,128)(2,1)S(1)} collective-permute-done((bf16[128,5632]{1,0:T(8,128)(2,1)S(1)}, bf16[128,5632]{1,0:T(8,128)(2,1)S(1)}, u32[]{:S(2)}, u32[]{:S(2)}) %collective-permute-start.12) | collective-permute-done | bytes 1441824 | tf_op jit(solution)/shard_map/ppermute | solution.py:73
  66.2 2.4 collective-permute-done.11.refs_2_.refs_18_
  68.6 1.4 broadcast_in_dim.17.noise
  72.1 2.4 collective-permute-start.13
  74.5 28.0 %collective-permute-done.15.refs_3_.refs_19_ = bf16[128,5632]{1,0:T(8,128)(2,1)S(1)} collective-permute-done((bf16[128,5632]{1,0:T(8,128)(2,1)S(1)}, bf16[128,5632]{1,0:T(8,128)(2,1)S(1)}, u32[]{:S(2)}, u32[]{:S(2)}) %collective-permute-start.15) | collective-permute-done | bytes 1441824 | tf_op jit(solution)/shard_map/ppermute | solution.py:73
  109.3 2.6 collective-permute-start.16
  114.3 2.0 collective-permute-done.7.refs_19_
  116.4 13.9 %collective-permute-done.16.refs_6_ = bf16[128,3072]{1,0:T(8,128)(2,1)} collective-permute-done((bf16[128,3072]{1,0:T(8,128)(2,1)}, bf16[128,3072]{1,0:T(8,128)(2,1)}, u32[]{:S(2)}, u32[]{:S(2)}) %collective-permute-start.16) | collective-permute-done | bytes 786464 | tf_op jit(solution)/shard_map/ppermute | solution.py:33
  130.3 6.6 %collective-permute-done.20.refs_5_.refs_21_ = bf16[128,5632]{1,0:T(8,128)(2,1)} collective-permute-done((bf16[128,5632]{1,0:T(8,128)(2,1)S(1)}, bf16[128,5632]{1,0:T(8,128)(2,1)}, u32[]{:S(2)}, u32[]{:S(2)}) %collective-permute-start.20) | collective-permute-done | bytes 1441824 | tf_op jit(solution)/shard_map/ppermute | solution.py:73
  137.9 3.4 collective-permute-done.23.refs_6_.refs_22_
  142.4 1.4 collective-permute-start.24
  147.8 20.5 %collective-permute-done.24.refs_7_.refs_23_ = bf16[128,4096]{1,0:T(8,128)(2,1)} collective-permute-done((bf16[128,4096]{1,0:T(8,128)(2,1)}, bf16[128,4096]{1,0:T(8,128)(2,1)}, u32[]{:S(2)}, u32[]{:S(2)}) %collective-permute-start.24) | collective-permute-done | bytes 1048608 | tf_op jit(solution)/shard_map/ppermute | solution.py:73
  168.8 3.6 collective-permute-done.21.refs_11_
  173.3 1.3 select_maximum_fusion.vectors
  175.8 30.6 %recur_forward.1 = (bf16[2,16,8,1024]{3,2,1,0:T(8,128)(2,1)}, bf16[16,16,1024]{2,1,0:T(8,128)(2,1)}, f32[16,16,4096]{2,1,0:T(8,128)}, f32[16,16,1024]{2,1,0:T(8,128)}) custom-call(s32[9]{0:T(128)} %stack.81.places, bf16[256,1024]{1,0:T(8,128)(2,1)} %bitcast.140, f32[1,2048]{1,0:T(1,128)} %copy-done.80, f32[1,2048]{1,0:T(1,128)} %copy-done.82, ...), custom_call_target="tpu_custom_call" | custom-call | tf_op jit(solution)/shard_map/recur_forward/pallas_call | solution.py:185
  207.4 1.8 collective-permute-start.33
  209.8 5.8 %collective-permute-done.33 = bf16[16,8,1024]{2,1,0:T(8,128)(2,1)S(1)} collective-permute-done((bf16[16,8,1024]{2,1,0:T(8,128)(2,1)S(1)}, bf16[16,8,1024]{2,1,0:T(8,128)(2,1)S(1)}, u32[]{:S(2)}, u32[]{:S(2)}) %collective-permute-start.33) | collective-permute-done | bytes 262176 | tf_op jit(solution)/shard_map/ppermute | solution.py:33
  216.6 1.8 collective-permute-start.41
  221.8 3.6 collective-permute-done.41
  225.5 1.8 fusion.56
  229.8 33.0 %attend.1 = (f32[128,1024]{1,0:T(8,128)}, f32[128,1024]{1,0:T(8,128)}, bf16[4,128,1536]{2,1,0:T(8,128)(2,1)}, bf16[2,128,1024]{2,1,0:T(8,128)(2,1)}, f32[8,1024]{1,0:T(8,128)}) custom-call(s32[9]{0:T(128)} %stack.81.places, bf16[128,1024]{1,0:T(8,128)(2,1)} %get-tuple-element.232.memory, bf16[128,1024]{1,0:T(8,128)(2,1)} %get-tuple-element.231.decoded, ...), custom_call_target="tpu_custom_call" | custom-call | tf_op jit(solution)/shard_map/attend/pallas_call | solution.py:665
  262.9 2.2 slice.288
  268.6 1.7 collective-permute-start.39
  271.8 5.4 %collective-permute-done.39 = bf16[128,1024]{1,0:T(8,128)(2,1)S(1)} collective-permute-done((bf16[128,1024]{1,0:T(8,128)(2,1)S(1)}, bf16[128,1024]{1,0:T(8,128)(2,1)S(1)}, u32[]{:S(2)}, u32[]{:S(2)}) %collective-permute-start.39) | collective-permute-done | bytes 262176 | tf_op jit(solution)/shard_map/ppermute | solution.py:33
  280.5 1.7 collective-permute-start.48
  284.0 23.3 %recur_backward_late.1 = (bf16[2,10,16,2048]{3,2,1,0:T(8,128)(2,1)}, bf16[4096,1024]{1,0:T(8,128)(2,1)}, f32[16,1024]{1,0:T(8,128)}, f32[16,1024]{1,0:T(8,128)}) custom-call(s32[9]{0:T(128)} %stack.81.places, f32[2,16,8,1024]{3,2,1,0:T(8,128)} %pad_maximum_fusion.8.outside, f32[16,16,4096]{2,1,0:T(8,128)} %get-tuple-element.97.gates, ...), custom_call_target="tpu_custom_call" | custom-call | tf_op jit(solution)/shard_map/recur_backward_late/pallas_call | solution.py:302
  307.4 1.4 slice_bitcast_fusion.13
  313.6 1.7 convolution_convert_fusion.2
  316.0 13.6 %recur_backward_early.1 = bf16[2,6,16,2048]{3,2,1,0:T(8,128)(2,1)} custom-call(f32[2,16,8,1024]{3,2,1,0:T(8,128)} %pad_maximum_fusion.8.outside, f32[16,16,4096]{2,1,0:T(8,128)} %get-tuple-element.97.gates, f32[16,16,1024]{2,1,0:T(8,128)} %get-tuple-element.98.cells, f32[16,1024]{1,0:T(8,128)} %get-tuple-element.107.dh_in, ...), custom_call_target="tpu_custom_call" | custom-call | tf_op jit(solution)/shard_map/recur_backward_early/pallas_call | solution.py:326
  338.0 2.4 convolution_convert_fusion
  340.4 3.6 convolution_convert_fusion.1
  344.0 2.6 constant_dynamic-slice_fusion.2
  349.6 1.5 collective-permute-start.50
  352.1 9.0 %collective-permute-done.52 = bf16[256,768]{1,0:T(8,128)(2,1)} collective-permute-done((bf16[256,768]{1,0:T(8,128)(2,1)}, bf16[256,768]{1,0:T(8,128)(2,1)}, u32[]{:S(2)}, u32[]{:S(2)}) %collective-permute-start.52) | collective-permute-done | bytes 393248 | tf_op jit(solution)/shard_map/ppermute | solution.py:76
  363.7 11.1 %collective-permute-done.53 = bf16[256,768]{1,0:T(8,128)(2,1)S(1)} collective-permute-done((bf16[256,768]{1,0:T(8,128)(2,1)S(1)}, bf16[256,768]{1,0:T(8,128)(2,1)S(1)}, u32[]{:S(2)}, u32[]{:S(2)}) %collective-permute-start.53) | collective-permute-done | bytes 393248 | tf_op jit(solution)/shard_map/ppermute | solution.py:76
  375.8 5.1 collective-permute-done.50
  380.8 8.8 %input_back.1 = (f32[256,1024]{1,0:T(8,128)}, f32[1,1024]{1,0:T(1,128)}) custom-call(s32[9]{0:T(128)} %stack.81.places, bf16[256,1024]{1,0:T(8,128)(2,1)} %bitcast.142, f32[1,1024]{1,0:T(1,128)} %bitcast.154, bf16[256,2048]{1,0:T(8,128)(2,1)} %pad_maximum_fusion.11.dz, bf16[256,2048]{1,0:T(8,128)(2,1)} %copy-done.11, bf16[128,5632]{1,0:T(8,128)(2,1)} %copy-done.2, ...), custom_call_target="tpu_custom_call" | custom-call | tf_op jit(solution)/shard_map/input_back/pallas_call | solution.py:371
  389.7 1.9 copy.90
  392.0 2.3 collective-permute-done.51
  395.3 1.5 collective-permute-start.56
  396.8 3.8 collective-permute-start.54
  402.2 34.2 %collective-permute-done.58 = bf16[256,768]{1,0:T(8,128)(2,1)S(1)} collective-permute-done((bf16[256,768]{1,0:T(8,128)(2,1)S(1)}, bf16[256,768]{1,0:T(8,128)(2,1)S(1)}, u32[]{:S(2)}, u32[]{:S(2)}) %collective-permute-start.58) | collective-permute-done | bytes 393248 | tf_op jit(solution)/shard_map/ppermute | solution.py:76
  438.1 1.7 add_convert_fusion.1
  439.9 1.5 collective-permute-start.59
  444.7 29.7 %collective-permute-done.61 = bf16[128,768]{1,0:T(8,128)(2,1)S(1)} collective-permute-done((bf16[128,768]{1,0:T(8,128)(2,1)}, bf16[128,768]{1,0:T(8,128)(2,1)S(1)}, u32[]{:S(2)}, u32[]{:S(2)}) %collective-permute-start.61) | collective-permute-done | bytes 196640 | tf_op jit(solution)/shard_map/ppermute | solution.py:73
  475.5 2.8 add_convert_fusion
  478.4 1.5 collective-permute-start.63
  479.9 1.7 select_bitcast_fusion
  483.0 26.6 %collective-permute-done.62 = bf16[128,384]{1,0:T(8,128)(2,1)S(1)} collective-permute-done((bf16[128,384]{1,0:T(8,128)(2,1)S(1)}, bf16[128,384]{1,0:T(8,128)(2,1)S(1)}, u32[]{:S(2)}, u32[]{:S(2)}) %collective-permute-start.62) | collective-permute-done | bytes 98336 | tf_op jit(solution)/shard_map/ppermute | solution.py:73
  510.6 1.9 collective-permute-start.65
  512.5 2.0 collective-permute-start.66
  516.0 1.9 collective-permute-done.65
  517.9 1.3 collective-permute-start.67
  519.5 7.0 %collective-permute-done.67 = bf16[128,640]{1,0:T(8,128)(2,1)S(1)} collective-permute-done((bf16[128,640]{1,0:T(8,128)(2,1)S(1)}, bf16[128,640]{1,0:T(8,128)(2,1)S(1)}, u32[]{:S(2)}, u32[]{:S(2)}) %collective-permute-start.67) | collective-permute-done | bytes 163872 | tf_op jit(solution)/shard_map/ppermute | solution.py:76
  531.2 1.7 reshape.225
  532.9 1.7 reshape.227
  (438 shorter events, 96.7 us)
Async XLA Ops:
  0.7 25.9 %collective-permute-start.8 = (bf16[16,32,1024]{2,0,1:T(8,128)(2,1)}, bf16[16,32,1024]{2,0,1:T(8,128)(2,1)}, u32[]{:S(2)}, u32[]{:S(2)}) collective-permute-start(bf16[16,32,1024]{2,0,1:T(8,128)(2,1)} %bitcast.147), channel_id=1, source_target_pairs={{0,16},{16,0},{1,17},{17,1},{2,18},{18,2},{3,19},{19,3},{4,20},{20... | collective-permute-start | bytes 3145736 | tf_op jit(solution)/shard_map/ppermute | solution.py:29
  9.7 23.5 %collective-permute-start = (f32[5,256]{1,0:T(8,128)S(1)}, f32[5,256]{1,0:T(8,128)}, u32[]{:S(2)}, u32[]{:S(2)}) collective-permute-start(f32[5,256]{1,0:T(8,128)S(1)} %stack.87), channel_id=1, source_target_pairs={{0,1},{1,0},{2,3},{3,2},{4,5},{5,4},{6,7},{7,6},{8,9},{9,8},{10,11... | collective-permute-start | bytes 15368 | tf_op jit(solution)/shard_map/ppermute | solution.py:33
  12.2 15.9 %collective-permute-start.2 = (bf16[128,4224]{1,0:T(8,128)(2,1)}, bf16[128,4224]{1,0:T(8,128)(2,1)S(1)}, u32[]{:S(2)}, u32[]{:S(2)}) collective-permute-start(bf16[128,4224]{1,0:T(8,128)(2,1)} %fusion.5), channel_id=1, source_target_pairs={{0,0},{1,16},{16,1},{17,17},{2,2},{3,18},{18,3},{19,19},{4,4},{5,2... | collective-permute-start | bytes 3244040 | tf_op jit(solution)/shard_map/ppermute | solution.py:37
  14.1 11.7 %collective-permute-start.4 = (bf16[128,1536]{1,0:T(8,128)(2,1)}, bf16[128,1536]{1,0:T(8,128)(2,1)S(1)}, u32[]{:S(2)}, u32[]{:S(2)}) collective-permute-start(bf16[128,1536]{1,0:T(8,128)(2,1)} %get-tuple-element.79), channel_id=1, source_target_pairs={{0,2},{2,0},{4,6},{6,4},{8,10},{10,8},{12,14},{14,12},{1,3},{3,1},... | collective-permute-start | bytes 1179656 | tf_op jit(solution)/shard_map/ppermute | solution.py:73
  15.6 4.3 collective-permute-start.9
  19.9 13.2 %collective-permute-start.3 = (bf16[128,1536]{1,0:T(8,128)(2,1)}, bf16[128,1536]{1,0:T(8,128)(2,1)S(1)}, u32[]{:S(2)}, u32[]{:S(2)}) collective-permute-start(bf16[128,1536]{1,0:T(8,128)(2,1)} %get-tuple-element.79), channel_id=1, source_target_pairs={{0,4},{2,6},{4,8},{6,10},{8,12},{10,14},{12,0},{14,2},{1,5},{3,7},... | collective-permute-start | bytes 1179656 | tf_op jit(solution)/shard_map/ppermute | solution.py:76
  33.2 32.9 %collective-permute-start.12 = (bf16[128,5632]{1,0:T(8,128)(2,1)S(1)}, bf16[128,5632]{1,0:T(8,128)(2,1)S(1)}, u32[]{:S(2)}, u32[]{:S(2)}) collective-permute-start(bf16[128,5632]{1,0:T(8,128)(2,1)S(1)} %pad_maximum_fusion.3.refs_0_.refs_16_), channel_id=1, source_target_pairs={{0,2},{2,0},{4,6},{6,4},{8,10},{10,8},{12,14},{14,12},{1,3},{3,1},... | collective-permute-start | bytes 4325384 | tf_op jit(solution)/shard_map/ppermute | solution.py:73
  34.1 34.6 %collective-permute-start.11 = (bf16[128,5632]{1,0:T(8,128)(2,1)S(1)}, bf16[128,5632]{1,0:T(8,128)(2,1)S(1)}, u32[]{:S(2)}, u32[]{:S(2)}) collective-permute-start(bf16[128,5632]{1,0:T(8,128)(2,1)S(1)} %pad_maximum_fusion.3.refs_0_.refs_16_), channel_id=1, source_target_pairs={{0,4},{2,6},{4,8},{6,10},{8,12},{10,14},{12,0},{14,2},{1,5},{3,7},... | collective-permute-start | bytes 4325384 | tf_op jit(solution)/shard_map/ppermute | solution.py:76
  34.7 31.5 %collective-permute-start.10 = (bf16[128,3072]{1,0:T(8,128)(2,1)}, bf16[128,3072]{1,0:T(8,128)(2,1)S(1)}, u32[]{:S(2)}, u32[]{:S(2)}) collective-permute-start(bf16[128,3072]{1,0:T(8,128)(2,1)} %constant_dynamic-update-slice_fusion.4.refs_0_), channel_id=1, source_target_pairs={{0,1},{1,0},{2,3},{3,2},{4,5},{5,4},{6,7},{7,6},{8,9},{9,8},{10,11... | collective-permute-start | bytes 2359304 | tf_op jit(solution)/shard_map/ppermute | solution.py:33
  36.7 29.5 %collective-permute-start.5 = (bf16[256,1024]{1,0:T(8,128)(2,1)}, bf16[256,1024]{1,0:T(8,128)(2,1)S(1)}, u32[]{:S(2)}, u32[]{:S(2)}) collective-permute-start(bf16[256,1024]{1,0:T(8,128)(2,1)} %pad.29.refs_16_), channel_id=1, source_target_pairs={{0,1},{1,0},{2,3},{3,2},{4,5},{5,4},{6,7},{7,6},{8,9},{9,8},{10,11... | collective-permute-start | bytes 1572872 | tf_op jit(solution)/shard_map/ppermute | solution.py:33
  70.8 31.8 %collective-permute-start.15 = (bf16[128,5632]{1,0:T(8,128)(2,1)S(1)}, bf16[128,5632]{1,0:T(8,128)(2,1)S(1)}, u32[]{:S(2)}, u32[]{:S(2)}) collective-permute-start(bf16[128,5632]{1,0:T(8,128)(2,1)S(1)} %collective-permute-done.11.refs_2_.refs_18_), channel_id=1, source_target_pairs={{0,2},{2,0},{4,6},{6,4},{8,10},{10,8},{12,14},{14,12},{1,3},{3,1},... | collective-permute-start | bytes 4325384 | tf_op jit(solution)/shard_map/ppermute | solution.py:73
  72.1 33.1 %collective-permute-start.14 = (bf16[128,5632]{1,0:T(8,128)(2,1)S(1)}, bf16[128,5632]{1,0:T(8,128)(2,1)S(1)}, u32[]{:S(2)}, u32[]{:S(2)}) collective-permute-start(bf16[128,5632]{1,0:T(8,128)(2,1)S(1)} %collective-permute-done.11.refs_2_.refs_18_), channel_id=1, source_target_pairs={{0,4},{2,6},{4,8},{6,10},{8,12},{10,14},{12,0},{14,2},{1,5},{3,7},... | collective-permute-start | bytes 4325384 | tf_op jit(solution)/shard_map/ppermute | solution.py:76
  72.1 34.3 %collective-permute-start.13 = (bf16[128,3072]{1,0:T(8,128)(2,1)S(1)}, bf16[128,3072]{1,0:T(8,128)(2,1)S(1)}, u32[]{:S(2)}, u32[]{:S(2)}) collective-permute-start(bf16[128,3072]{1,0:T(8,128)(2,1)S(1)} %pad_maximum_fusion.14.refs_1_), channel_id=1, source_target_pairs={{0,1},{1,0},{2,3},{3,2},{4,5},{5,4},{6,7},{7,6},{8,9},{9,8},{10,11... | collective-permute-start | bytes 2359304 | tf_op jit(solution)/shard_map/ppermute | solution.py:33
  74.5 39.6 %collective-permute-start.17 = (bf16[128,3072]{1,0:T(8,128)(2,1)}, bf16[128,3072]{1,0:T(8,128)(2,1)}, u32[]{:S(2)}, u32[]{:S(2)}) collective-permute-start(bf16[128,3072]{1,0:T(8,128)(2,1)} %constant_dynamic-update-slice_fusion.4.refs_0_), channel_id=1, source_target_pairs={{0,16},{16,0},{1,17},{17,1},{2,18},{18,2},{3,19},{19,3},{4,20},{20... | collective-permute-start | bytes 2359304 | tf_op jit(solution)/shard_map/ppermute | solution.py:29
  106.4 30.5 %collective-permute-start.20 = (bf16[128,5632]{1,0:T(8,128)(2,1)S(1)}, bf16[128,5632]{1,0:T(8,128)(2,1)}, u32[]{:S(2)}, u32[]{:S(2)}) collective-permute-start(bf16[128,5632]{1,0:T(8,128)(2,1)S(1)} %collective-permute-done.14.refs_4_.refs_20_), channel_id=1, source_target_pairs={{0,2},{2,0},{4,6},{6,4},{8,10},{10,8},{12,14},{14,12},{1,3},{3,1},... | collective-permute-start | bytes 4325384 | tf_op jit(solution)/shard_map/ppermute | solution.py:73
  107.3 5.5 %collective-permute-start.6 = (bf16[256,1024]{1,0:T(8,128)(2,1)}, bf16[256,1024]{1,0:T(8,128)(2,1)}, u32[]{:S(2)}, u32[]{:S(2)}) collective-permute-start(bf16[256,1024]{1,0:T(8,128)(2,1)} %pad.29.refs_16_), channel_id=1, source_target_pairs={{0,16},{16,0},{1,17},{17,1},{2,18},{18,2},{3,19},{19,3},{4,20},{20... | collective-permute-start | bytes 1572872 | tf_op jit(solution)/shard_map/ppermute | solution.py:29
  108.5 33.9 %collective-permute-start.25 = (bf16[128,5632]{1,0:T(8,128)(2,1)S(1)}, bf16[128,5632]{1,0:T(8,128)(2,1)}, u32[]{:S(2)}, u32[]{:S(2)}) collective-permute-start(bf16[128,5632]{1,0:T(8,128)(2,1)S(1)} %pad_maximum_fusion.3.refs_0_.refs_16_), channel_id=1, source_target_pairs={{0,16},{16,0},{1,17},{17,1},{2,18},{18,2},{3,19},{19,3},{4,20},{20... | collective-permute-start | bytes 4325384 | tf_op jit(solution)/shard_map/ppermute | solution.py:29
  109.3 20.9 %collective-permute-start.16 = (bf16[128,3072]{1,0:T(8,128)(2,1)}, bf16[128,3072]{1,0:T(8,128)(2,1)}, u32[]{:S(2)}, u32[]{:S(2)}) collective-permute-start(bf16[128,3072]{1,0:T(8,128)(2,1)} %pad_maximum_fusion.15.refs_2_), channel_id=1, source_target_pairs={{0,1},{1,0},{2,3},{3,2},{4,5},{5,4},{6,7},{7,6},{8,9},{9,8},{10,11... | collective-permute-start | bytes 2359304 | tf_op jit(solution)/shard_map/ppermute | solution.py:33
  114.0 27.3 %collective-permute-start.23 = (bf16[128,4096]{1,0:T(8,128)(2,1)}, bf16[128,4096]{1,0:T(8,128)(2,1)}, u32[]{:S(2)}, u32[]{:S(2)}) collective-permute-start(bf16[128,4096]{1,0:T(8,128)(2,1)} %slice.361), channel_id=1, source_target_pairs={{0,4},{2,6},{4,8},{6,10},{8,12},{10,14},{12,0},{14,2},{1,5},{3,7},... | collective-permute-start | bytes 3145736 | tf_op jit(solution)/shard_map/ppermute | solution.py:76
  116.2 27.9 %collective-permute-start.26 = (bf16[128,5632]{1,0:T(8,128)(2,1)}, bf16[128,5632]{1,0:T(8,128)(2,1)S(1)}, u32[]{:S(2)}, u32[]{:S(2)}) collective-permute-start(bf16[128,5632]{1,0:T(8,128)(2,1)} %copy-done.4), channel_id=1, source_target_pairs={{0,16},{16,0},{1,17},{17,1},{2,18},{18,2},{3,19},{19,3},{4,20},{20... | collective-permute-start | bytes 4325384 | tf_op jit(solution)/shard_map/ppermute | solution.py:29
  130.3 15.0 %collective-permute-start.27 = (bf16[128,5632]{1,0:T(8,128)(2,1)}, bf16[128,5632]{1,0:T(8,128)(2,1)S(1)}, u32[]{:S(2)}, u32[]{:S(2)}) collective-permute-start(bf16[128,5632]{1,0:T(8,128)(2,1)} %copy-done.5), channel_id=1, source_target_pairs={{0,16},{16,0},{1,17},{17,1},{2,18},{18,2},{3,19},{19,3},{4,20},{20... | collective-permute-start | bytes 4325384 | tf_op jit(solution)/shard_map/ppermute | solution.py:29
  136.9 7.0 %collective-permute-start.18 = (bf16[128,3072]{1,0:T(8,128)(2,1)}, bf16[128,3072]{1,0:T(8,128)(2,1)S(1)}, u32[]{:S(2)}, u32[]{:S(2)}) collective-permute-start(bf16[128,3072]{1,0:T(8,128)(2,1)} %copy-done.13), channel_id=1, source_target_pairs={{0,16},{16,0},{1,17},{17,1},{2,18},{18,2},{3,19},{19,3},{4,20},{20... | collective-permute-start | bytes 2359304 | tf_op jit(solution)/shard_map/ppermute | solution.py:29
  141.4 27.0 %collective-permute-start.28 = (bf16[128,5632]{1,0:T(8,128)(2,1)}, bf16[128,5632]{1,0:T(8,128)(2,1)}, u32[]{:S(2)}, u32[]{:S(2)}) collective-permute-start(bf16[128,5632]{1,0:T(8,128)(2,1)} %copy-done.6), channel_id=1, source_target_pairs={{0,16},{16,0},{1,17},{17,1},{2,18},{18,2},{3,19},{19,3},{4,20},{20... | collective-permute-start | bytes 4325384 | tf_op jit(solution)/shard_map/ppermute | solution.py:29
  142.4 25.9 %collective-permute-start.24 = (bf16[128,4096]{1,0:T(8,128)(2,1)}, bf16[128,4096]{1,0:T(8,128)(2,1)}, u32[]{:S(2)}, u32[]{:S(2)}) collective-permute-start(bf16[128,4096]{1,0:T(8,128)(2,1)} %collective-permute-done.23.refs_6_.refs_22_), channel_id=1, source_target_pairs={{0,2},{2,0},{4,6},{6,4},{8,10},{10,8},{12,14},{14,12},{1,3},{3,1},... | collective-permute-start | bytes 3145736 | tf_op jit(solution)/shard_map/ppermute | solution.py:73
  143.9 2.8 collective-permute-start.19
  144.1 30.6 %collective-permute-start.29 = (bf16[128,5632]{1,0:T(8,128)(2,1)S(1)}, bf16[128,5632]{1,0:T(8,128)(2,1)S(1)}, u32[]{:S(2)}, u32[]{:S(2)}) collective-permute-start(bf16[128,5632]{1,0:T(8,128)(2,1)S(1)} %collective-permute-done.14.refs_4_.refs_20_), channel_id=1, source_target_pairs={{0,16},{16,0},{1,17},{17,1},{2,18},{18,2},{3,19},{19,3},{4,20},{20... | collective-permute-start | bytes 4325384 | tf_op jit(solution)/shard_map/ppermute | solution.py:29
  146.4 28.3 %collective-permute-start.30 = (bf16[128,5632]{1,0:T(8,128)(2,1)}, bf16[128,5632]{1,0:T(8,128)(2,1)}, u32[]{:S(2)}, u32[]{:S(2)}) collective-permute-start(bf16[128,5632]{1,0:T(8,128)(2,1)} %collective-permute-done.20.refs_5_.refs_21_), channel_id=1, source_target_pairs={{0,16},{16,0},{1,17},{17,1},{2,18},{18,2},{3,19},{19,3},{4,20},{20... | collective-permute-start | bytes 4325384 | tf_op jit(solution)/shard_map/ppermute | solution.py:29
  147.6 27.1 %collective-permute-start.31 = (bf16[128,4096]{1,0:T(8,128)(2,1)}, bf16[128,4096]{1,0:T(8,128)(2,1)}, u32[]{:S(2)}, u32[]{:S(2)}) collective-permute-start(bf16[128,4096]{1,0:T(8,128)(2,1)} %collective-permute-done.23.refs_6_.refs_22_), channel_id=1, source_target_pairs={{0,16},{16,0},{1,17},{17,1},{2,18},{18,2},{3,19},{19,3},{4,20},{20... | collective-permute-start | bytes 3145736 | tf_op jit(solution)/shard_map/ppermute | solution.py:29
  168.3 6.3 %collective-permute-start.32 = (bf16[128,4096]{1,0:T(8,128)(2,1)}, bf16[128,4096]{1,0:T(8,128)(2,1)}, u32[]{:S(2)}, u32[]{:S(2)}) collective-permute-start(bf16[128,4096]{1,0:T(8,128)(2,1)} %collective-permute-done.24.refs_7_.refs_23_), channel_id=1, source_target_pairs={{0,16},{16,0},{1,17},{17,1},{2,18},{18,2},{3,19},{19,3},{4,20},{20... | collective-permute-start | bytes 3145736 | tf_op jit(solution)/shard_map/ppermute | solution.py:29
  168.3 4.1 collective-permute-start.21
  172.4 44.1 %collective-permute-start.34 = (bf16[128,3072]{1,0:T(8,128)(2,1)}, bf16[128,3072]{1,0:T(8,128)(2,1)}, u32[]{:S(2)}, u32[]{:S(2)}) collective-permute-start(bf16[128,3072]{1,0:T(8,128)(2,1)} %pad_maximum_fusion.16.refs_3_), channel_id=1, source_target_pairs={{0,1},{1,0},{2,3},{3,2},{4,5},{5,4},{6,7},{7,6},{8,9},{9,8},{10,11... | collective-permute-start | bytes 2359304 | tf_op jit(solution)/shard_map/ppermute | solution.py:33
  207.4 8.2 %collective-permute-start.33 = (bf16[16,8,1024]{2,1,0:T(8,128)(2,1)S(1)}, bf16[16,8,1024]{2,1,0:T(8,128)(2,1)S(1)}, u32[]{:S(2)}, u32[]{:S(2)}) collective-permute-start(bf16[16,8,1024]{2,1,0:T(8,128)(2,1)S(1)} %dynamic-slice_bitcast_fusion), channel_id=1, source_target_pairs={{0,1},{1,0},{2,3},{3,2},{4,5},{5,4},{6,7},{7,6},{8,9},{9,8},{10,11... | collective-permute-start | bytes 786440 | tf_op jit(solution)/shard_map/ppermute | solution.py:33
  209.2 19.2 %collective-permute-start.35 = (bf16[128,3072]{1,0:T(8,128)(2,1)}, bf16[128,3072]{1,0:T(8,128)(2,1)S(1)}, u32[]{:S(2)}, u32[]{:S(2)}) collective-permute-start(bf16[128,3072]{1,0:T(8,128)(2,1)} %copy-done.38), channel_id=1, source_target_pairs={{0,16},{16,0},{1,17},{17,1},{2,18},{18,2},{3,19},{19,3},{4,20},{20... | collective-permute-start | bytes 2359304 | tf_op jit(solution)/shard_map/ppermute | solution.py:29
  209.2 19.7 %collective-permute-start.36 = (bf16[128,3072]{1,0:T(8,128)(2,1)}, bf16[128,3072]{1,0:T(8,128)(2,1)S(1)}, u32[]{:S(2)}, u32[]{:S(2)}) collective-permute-start(bf16[128,3072]{1,0:T(8,128)(2,1)} %copy-done.39), channel_id=1, source_target_pairs={{0,16},{16,0},{1,17},{17,1},{2,18},{18,2},{3,19},{19,3},{4,20},{20... | collective-permute-start | bytes 2359304 | tf_op jit(solution)/shard_map/ppermute | solution.py:29
  209.7 19.2 %collective-permute-start.37 = (bf16[128,3072]{1,0:T(8,128)(2,1)}, bf16[128,3072]{1,0:T(8,128)(2,1)}, u32[]{:S(2)}, u32[]{:S(2)}) collective-permute-start(bf16[128,3072]{1,0:T(8,128)(2,1)} %collective-permute-done.16.refs_6_), channel_id=1, source_target_pairs={{0,16},{16,0},{1,17},{17,1},{2,18},{18,2},{3,19},{19,3},{4,20},{20... | collective-permute-start | bytes 2359304 | tf_op jit(solution)/shard_map/ppermute | solution.py:29
  216.6 12.4 %collective-permute-start.38 = (bf16[128,3072]{1,0:T(8,128)(2,1)}, bf16[128,3072]{1,0:T(8,128)(2,1)}, u32[]{:S(2)}, u32[]{:S(2)}) collective-permute-start(bf16[128,3072]{1,0:T(8,128)(2,1)} %collective-permute-done.34.refs_7_), channel_id=1, source_target_pairs={{0,16},{16,0},{1,17},{17,1},{2,18},{18,2},{3,19},{19,3},{4,20},{20... | collective-permute-start | bytes 2359304 | tf_op jit(solution)/shard_map/ppermute | solution.py:29
  216.6 8.8 %collective-permute-start.41 = (bf16[16,8,1024]{2,1,0:T(8,128)(2,1)S(1)}, bf16[16,8,1024]{2,1,0:T(8,128)(2,1)}, u32[]{:S(2)}, u32[]{:S(2)}) collective-permute-start(bf16[16,8,1024]{2,1,0:T(8,128)(2,1)S(1)} %get-tuple-element.100), channel_id=1, source_target_pairs={{0,1},{1,0},{2,3},{3,2},{4,5},{5,4},{6,7},{7,6},{8,9},{9,8},{10,11... | collective-permute-start | bytes 786440 | tf_op jit(solution)/shard_map/ppermute | solution.py:33
  225.5 55.0 %collective-permute-start.43 = (bf16[256,1024]{1,0:T(8,128)(2,1)}, bf16[256,1024]{1,0:T(8,128)(2,1)}, u32[]{:S(2)}, u32[]{:S(2)}) collective-permute-start(bf16[256,1024]{1,0:T(8,128)(2,1)} %bitcast.38), channel_id=1, source_target_pairs={{0,16},{16,0},{1,17},{17,1},{2,18},{18,2},{3,19},{19,3},{4,20},{20... | collective-permute-start | bytes 1572872 | tf_op jit(solution)/shard_map/ppermute | solution.py:29
  228.4 52.1 %collective-permute-start.42 = (bf16[4,128,1024]{2,1,0:T(8,128)(2,1)}, bf16[4,128,1024]{2,1,0:T(8,128)(2,1)}, u32[]{:S(2)}, u32[]{:S(2)}) collective-permute-start(bf16[4,128,1024]{2,1,0:T(8,128)(2,1)} %pad_maximum_fusion.9), channel_id=1, source_target_pairs={{0,16},{16,0},{1,17},{17,1},{2,18},{18,2},{3,19},{19,3},{4,20},{20... | collective-permute-start | bytes 3145736 | tf_op jit(solution)/shard_map/ppermute | solution.py:29
  266.3 12.1 %collective-permute-start.40 = (bf16[2,128,1536]{2,1,0:T(8,128)(2,1)}, bf16[2,128,1536]{2,1,0:T(8,128)(2,1)}, u32[]{:S(2)}, u32[]{:S(2)}) collective-permute-start(bf16[2,128,1536]{2,1,0:T(8,128)(2,1)} %slice.288), channel_id=1, source_target_pairs={{0,16},{16,0},{1,17},{17,1},{2,18},{18,2},{3,19},{19,3},{4,20},{20... | collective-permute-start | bytes 2359304 | tf_op jit(solution)/shard_map/ppermute | solution.py:29
  267.0 3.4 collective-permute-start.46
  268.6 8.5 %collective-permute-start.39 = (bf16[128,1024]{1,0:T(8,128)(2,1)S(1)}, bf16[128,1024]{1,0:T(8,128)(2,1)S(1)}, u32[]{:S(2)}, u32[]{:S(2)}) collective-permute-start(bf16[128,1024]{1,0:T(8,128)(2,1)S(1)} %select_convert_fusion), channel_id=1, source_target_pairs={{0,1},{1,0},{2,3},{3,2},{4,5},{5,4},{6,7},{7,6},{8,9},{9,8},{10,11... | collective-permute-start | bytes 786440 | tf_op jit(solution)/shard_map/ppermute | solution.py:33
  280.5 28.6 %collective-permute-start.48 = (bf16[2,128,1152]{2,1,0:T(8,128)(2,1)}, bf16[2,128,1152]{2,1,0:T(8,128)(2,1)S(1)}, u32[]{:S(2)}, u32[]{:S(2)}) collective-permute-start(bf16[2,128,1152]{2,1,0:T(8,128)(2,1)} %pad_maximum_fusion.18), channel_id=1, source_target_pairs={{0,1},{1,0},{2,3},{3,2},{4,5},{5,4},{6,7},{7,6},{8,9},{9,8},{10,11... | collective-permute-start | bytes 1769480 | tf_op jit(solution)/shard_map/ppermute | solution.py:33
  283.7 28.6 %collective-permute-start.44 = (bf16[2,128,1536]{2,1,0:T(8,128)(2,1)}, bf16[2,128,1536]{2,1,0:T(8,128)(2,1)S(1)}, u32[]{:S(2)}, u32[]{:S(2)}) collective-permute-start(bf16[2,128,1536]{2,1,0:T(8,128)(2,1)} %pad_maximum_fusion.17), channel_id=1, source_target_pairs={{0,1},{1,0},{2,3},{3,2},{4,5},{5,4},{6,7},{7,6},{8,9},{9,8},{10,11... | collective-permute-start | bytes 2359304 | tf_op jit(solution)/shard_map/ppermute | solution.py:33
  310.3 23.1 %collective-permute-start.49 = (bf16[4,128,1024]{2,1,0:T(8,128)(2,1)}, bf16[4,128,1024]{2,1,0:T(8,128)(2,1)}, u32[]{:S(2)}, u32[]{:S(2)}) collective-permute-start(bf16[4,128,1024]{2,1,0:T(8,128)(2,1)} %pad_maximum_fusion.13), channel_id=1, source_target_pairs={{0,16},{16,0},{1,17},{17,1},{2,18},{18,2},{3,19},{19,3},{4,20},{20... | collective-permute-start | bytes 3145736 | tf_op jit(solution)/shard_map/ppermute | solution.py:29
  331.1 6.9 %collective-permute-start.45 = (bf16[256,2048]{1,0:T(8,128)(2,1)S(1)}, bf16[256,2048]{1,0:T(8,128)(2,1)S(1)}, u32[]{:S(2)}, u32[]{:S(2)}) collective-permute-start(bf16[256,2048]{1,0:T(8,128)(2,1)S(1)} %pad_maximum_fusion.12.dz_given), channel_id=1, source_target_pairs={{0,16},{16,0},{1,17},{17,1},{2,18},{18,2},{3,19},{19,3},{4,20},{20... | collective-permute-start | bytes 3145736 | tf_op jit(solution)/shard_map/ppermute | solution.py:29
  347.7 13.4 %collective-permute-start.52 = (bf16[256,768]{1,0:T(8,128)(2,1)}, bf16[256,768]{1,0:T(8,128)(2,1)}, u32[]{:S(2)}, u32[]{:S(2)}) collective-permute-start(bf16[256,768]{1,0:T(8,128)(2,1)} %pad_maximum_fusion.19), channel_id=1, source_target_pairs={{0,4},{2,6},{4,8},{6,10},{8,12},{10,14},{12,0},{14,2},{1,5},{3,7},... | collective-permute-start | bytes 1179656 | tf_op jit(solution)/shard_map/ppermute | solution.py:76
  349.6 31.2 %collective-permute-start.50 = (bf16[128,5120]{1,0:T(8,128)(2,1)}, bf16[128,5120]{1,0:T(8,128)(2,1)S(1)}, u32[]{:S(2)}, u32[]{:S(2)}) collective-permute-start(bf16[128,5120]{1,0:T(8,128)(2,1)} %pad_maximum_fusion.4), channel_id=1, source_target_pairs={{0,2},{2,0},{4,6},{6,4},{8,10},{10,8},{12,14},{14,12},{1,3},{3,1},... | collective-permute-start | bytes 3932168 | tf_op jit(solution)/shard_map/ppermute | solution.py:73
  362.3 12.5 %collective-permute-start.53 = (bf16[256,768]{1,0:T(8,128)(2,1)S(1)}, bf16[256,768]{1,0:T(8,128)(2,1)S(1)}, u32[]{:S(2)}, u32[]{:S(2)}) collective-permute-start(bf16[256,768]{1,0:T(8,128)(2,1)S(1)} %add_convert_fusion.4), channel_id=1, source_target_pairs={{0,4},{2,6},{4,8},{6,10},{8,12},{10,14},{12,0},{14,2},{1,5},{3,7},... | collective-permute-start | bytes 1179656 | tf_op jit(solution)/shard_map/ppermute | solution.py:76
  395.2 42.8 %collective-permute-start.57 = (bf16[128,5120]{1,0:T(8,128)(2,1)S(1)}, bf16[128,5120]{1,0:T(8,128)(2,1)S(1)}, u32[]{:S(2)}, u32[]{:S(2)}) collective-permute-start(bf16[128,5120]{1,0:T(8,128)(2,1)S(1)} %add_convert_fusion.2), channel_id=1, source_target_pairs={{0,4},{2,6},{4,8},{6,10},{8,12},{10,14},{12,0},{14,2},{1,5},{3,7},... | collective-permute-start | bytes 3932168 | tf_op jit(solution)/shard_map/ppermute | solution.py:76
  395.3 42.7 %collective-permute-start.56 = (bf16[128,5120]{1,0:T(8,128)(2,1)S(1)}, bf16[128,5120]{1,0:T(8,128)(2,1)S(1)}, u32[]{:S(2)}, u32[]{:S(2)}) collective-permute-start(bf16[128,5120]{1,0:T(8,128)(2,1)S(1)} %pad_maximum_fusion.5), channel_id=1, source_target_pairs={{0,2},{2,0},{4,6},{6,4},{8,10},{10,8},{12,14},{14,12},{1,3},{3,1},... | collective-permute-start | bytes 3932168 | tf_op jit(solution)/shard_map/ppermute | solution.py:73
  396.8 43.1 %collective-permute-start.54 = (f32[32,16,1024]{2,1,0:T(8,128)S(1)}, f32[32,16,1024]{2,1,0:T(8,128)S(1)}, u32[]{:S(2)}, u32[]{:S(2)}) collective-permute-start(f32[32,16,1024]{2,1,0:T(8,128)S(1)} %pad_maximum_fusion.1), channel_id=1, source_target_pairs={{0,1},{17,16},{2,3},{19,18},{4,5},{21,20},{6,7},{23,22},{8,9},{25,... | collective-permute-start | bytes 6291464 | tf_op jit(solution)/shard_map/ppermute | solution.py:900
  400.5 35.8 %collective-permute-start.58 = (bf16[256,768]{1,0:T(8,128)(2,1)S(1)}, bf16[256,768]{1,0:T(8,128)(2,1)S(1)}, u32[]{:S(2)}, u32[]{:S(2)}) collective-permute-start(bf16[256,768]{1,0:T(8,128)(2,1)S(1)} %copy-done.63), channel_id=1, source_target_pairs={{0,4},{2,6},{4,8},{6,10},{8,12},{10,14},{12,0},{14,2},{1,5},{3,7},... | collective-permute-start | bytes 1179656 | tf_op jit(solution)/shard_map/ppermute | solution.py:76
  439.8 35.7 %collective-permute-start.60 = (bf16[128,5120]{1,0:T(8,128)(2,1)}, bf16[128,5120]{1,0:T(8,128)(2,1)}, u32[]{:S(2)}, u32[]{:S(2)}) collective-permute-start(bf16[128,5120]{1,0:T(8,128)(2,1)} %add_convert_fusion.1), channel_id=1, source_target_pairs={{0,4},{2,6},{4,8},{6,10},{8,12},{10,14},{12,0},{14,2},{1,5},{3,7},... | collective-permute-start | bytes 3932168 | tf_op jit(solution)/shard_map/ppermute | solution.py:76
  439.9 35.6 %collective-permute-start.59 = (bf16[128,5120]{1,0:T(8,128)(2,1)}, bf16[128,5120]{1,0:T(8,128)(2,1)}, u32[]{:S(2)}, u32[]{:S(2)}) collective-permute-start(bf16[128,5120]{1,0:T(8,128)(2,1)} %pad_maximum_fusion.6), channel_id=1, source_target_pairs={{0,2},{2,0},{4,6},{6,4},{8,10},{10,8},{12,14},{14,12},{1,3},{3,1},... | collective-permute-start | bytes 3932168 | tf_op jit(solution)/shard_map/ppermute | solution.py:73
  443.9 30.5 %collective-permute-start.61 = (bf16[128,768]{1,0:T(8,128)(2,1)}, bf16[128,768]{1,0:T(8,128)(2,1)S(1)}, u32[]{:S(2)}, u32[]{:S(2)}) collective-permute-start(bf16[128,768]{1,0:T(8,128)(2,1)} %dynamic-slice_convert_fusion), channel_id=1, source_target_pairs={{0,2},{2,0},{4,6},{6,4},{8,10},{10,8},{12,14},{14,12},{1,3},{3,1},... | collective-permute-start | bytes 589832 | tf_op jit(solution)/shard_map/ppermute | solution.py:73
  478.3 31.5 %collective-permute-start.64 = (bf16[128,5120]{1,0:T(8,128)(2,1)S(1)}, bf16[128,5120]{1,0:T(8,128)(2,1)S(1)}, u32[]{:S(2)}, u32[]{:S(2)}) collective-permute-start(bf16[128,5120]{1,0:T(8,128)(2,1)S(1)} %add_convert_fusion), channel_id=1, source_target_pairs={{0,4},{2,6},{4,8},{6,10},{8,12},{10,14},{12,0},{14,2},{1,5},{3,7},... | collective-permute-start | bytes 3932168 | tf_op jit(solution)/shard_map/ppermute | solution.py:76
  478.4 31.5 %collective-permute-start.63 = (bf16[128,5120]{1,0:T(8,128)(2,1)S(1)}, bf16[128,5120]{1,0:T(8,128)(2,1)S(1)}, u32[]{:S(2)}, u32[]{:S(2)}) collective-permute-start(bf16[128,5120]{1,0:T(8,128)(2,1)S(1)} %copy-done.29), channel_id=1, source_target_pairs={{0,2},{2,0},{4,6},{6,4},{8,10},{10,8},{12,14},{14,12},{1,3},{3,1},... | collective-permute-start | bytes 3932168 | tf_op jit(solution)/shard_map/ppermute | solution.py:73
  481.6 28.0 %collective-permute-start.62 = (bf16[128,384]{1,0:T(8,128)(2,1)S(1)}, bf16[128,384]{1,0:T(8,128)(2,1)S(1)}, u32[]{:S(2)}, u32[]{:S(2)}) collective-permute-start(bf16[128,384]{1,0:T(8,128)(2,1)S(1)} %pad_maximum_fusion.25), channel_id=1, source_target_pairs={{0,2},{2,0},{4,6},{6,4},{8,10},{10,8},{12,14},{14,12},{1,3},{3,1},... | collective-permute-start | bytes 294920 | tf_op jit(solution)/shard_map/ppermute | solution.py:73
  510.6 7.3 %collective-permute-start.65 = (bf16[128,640]{1,0:T(8,128)(2,1)S(1)}, bf16[128,640]{1,0:T(8,128)(2,1)S(1)}, u32[]{:S(2)}, u32[]{:S(2)}) collective-permute-start(bf16[128,640]{1,0:T(8,128)(2,1)S(1)} %pad_maximum_fusion.24), channel_id=1, source_target_pairs={{0,4},{2,6},{4,8},{6,10},{8,12},{10,14},{12,0},{14,2},{1,5},{3,7},... | collective-permute-start | bytes 491528 | tf_op jit(solution)/shard_map/ppermute | solution.py:76
  512.5 7.0 %collective-permute-start.66 = (bf16[128,640]{1,0:T(8,128)(2,1)S(1)}, bf16[128,640]{1,0:T(8,128)(2,1)S(1)}, u32[]{:S(2)}, u32[]{:S(2)}) collective-permute-start(bf16[128,640]{1,0:T(8,128)(2,1)S(1)} %pad_maximum_fusion.24), channel_id=1, source_target_pairs={{4,0},{6,2},{8,4},{10,6},{12,8},{14,10},{0,12},{2,14},{5,1},{7,3},... | collective-permute-start | bytes 491528 | tf_op jit(solution)/shard_map/ppermute | solution.py:79
  514.5 16.5 %collective-permute-start.69 = (bf16[128,4096]{1,0:T(8,128)(2,1)S(1)}, bf16[128,4096]{1,0:T(8,128)(2,1)S(1)}, u32[]{:S(2)}, u32[]{:S(2)}) collective-permute-start(bf16[128,4096]{1,0:T(8,128)(2,1)S(1)} %slice.484), channel_id=1, source_target_pairs={{0,0},{1,16},{16,1},{17,17},{2,2},{3,18},{18,3},{19,19},{4,4},{5,2... | collective-permute-start | bytes 3145736 | tf_op jit(solution)/shard_map/ppermute | solution.py:37
  517.9 8.7 %collective-permute-start.67 = (bf16[128,640]{1,0:T(8,128)(2,1)S(1)}, bf16[128,640]{1,0:T(8,128)(2,1)S(1)}, u32[]{:S(2)}, u32[]{:S(2)}) collective-permute-start(bf16[128,640]{1,0:T(8,128)(2,1)S(1)} %collective-permute-done.65), channel_id=1, source_target_pairs={{0,4},{2,6},{4,8},{6,10},{8,12},{10,14},{12,0},{14,2},{1,5},{3,7},... | collective-permute-start | bytes 491528 | tf_op jit(solution)/shard_map/ppermute | solution.py:76
  526.8 2.9 collective-permute-start.68
  (102 other events, 1178.3 us)

commit v4 on v3

--- a/solution.py
+++ b/solution.py
@@ -108,7 +108,7 @@
     copies = []
     for k, block in enumerate(blocks):
         height = block.shape[0]
-        span = pl.ds(pl.multiple_of(places[1 + k] * height, height), height)
+        span = pl.ds(pl.multiple_of(places[2 + k] * height, height), height)
         copies.append(
             pltpu.make_async_copy(
                 block.at[:, column : column + wide_half],
@@ -121,7 +121,7 @@
 
 def forward_kernel(count, column, places, normed, b_own, b_other, *refs):
     in_own, in_other, w_own, w_other = [refs[n * count : (n + 1) * count] for n in range(4)]
-    quarters, before, gates, cells, wi, w, b, state, cell, sems = refs[4 * count :]
+    kept, given, before, gates, cells, wi, w, b, state, cell, sems = refs[4 * count :]
     steps, rows, wide_full = gates.shape
     wide_half = wide_full // 2
     unit_half = wide_half // 4
@@ -149,6 +149,7 @@
     for copy in later:
         copy.wait()
     eighth = rows // 2
+    first_chip = places[1] == 0
 
     def advance(t, carried):
         hidden = state[...]
@@ -170,8 +171,9 @@
             cells[t, :, units] = new_cell
             new_hidden = acts[3] * jnp.tanh(new_cell)
             state[:, units] = new_hidden.astype(low)
-            quarters[0, t, :, units] = new_hidden[:eighth].astype(low)
-            quarters[1, t, :, units] = new_hidden[eighth:].astype(low)
+            upper, lower = new_hidden[:eighth], new_hidden[eighth:]
+            kept[t, :, units] = jnp.where(first_chip, upper, lower).astype(low)
+            given[t, :, units] = jnp.where(first_chip, lower, upper).astype(low)
         return carried
 
     lax.fori_loop(0, steps, advance, 0)
@@ -185,13 +187,14 @@
     return pl.pallas_call(
         functools.partial(forward_kernel, count, column),
         out_shape=(
-            jax.ShapeDtypeStruct((2, steps, rows // 2, units), low),
+            jax.ShapeDtypeStruct((steps, rows // 2, units), low),
+            jax.ShapeDtypeStruct((steps, rows // 2, units), low),
             jax.ShapeDtypeStruct((steps, rows, units), low),
             jax.ShapeDtypeStruct((steps, rows, 2 * wide_half), wide),
             jax.ShapeDtypeStruct((steps, rows, units), wide),
         ),
         in_specs=[in_smem] + [in_vmem] * 3 + [in_place] * (4 * count),
-        out_specs=[in_vmem] * 4,
+        out_specs=[in_vmem] * 5,
         scratch_shapes=[
             pltpu.VMEM((units, 2 * wide_half), low),
             pltpu.VMEM((units, 2 * wide_half), low),
@@ -205,22 +208,53 @@
     )(places, normed, b_own, b_other, *in_own, *in_other, *w_own, *w_other)
 
 
-def backward_steps(first, last, outside, gates, cells, dz, w, dh, dc):
-    _, rows, wide_full = gates.shape
+def backward_kernel(count, column, places, kept, taken, gates, cells, *refs):
+    w_own, w_other = refs[:count], refs[count : 2 * count]
+    dz, stage, w, dh, dc, sems = refs[2 * count :]
+    steps, rows, wide_full = gates.shape
     wide_half = wide_full // 2
     unit_half = wide_half // 4
     chunk = min(256, unit_half)
+    s = places[0]
+    first_chip = places[1] == 0
+    jobs = []
+    for n, (sources, at) in enumerate(((w_own, s), (w_other, 1 - s))):
+        for k, block in enumerate(sources):
+            slot = n * count + k
+            copy = pltpu.make_async_copy(
+                block.at[:, column : column + wide_half], stage.at[slot], sems.at[slot]
+            )
+            copy.start()
+            jobs.append((copy, slot, at, places[2 + k] * block.shape[0]))
+    dh[...] = jnp.zeros_like(dh)
+    dc[...] = jnp.zeros_like(dc)
+    height = w_own[0].shape[0]
+    piece = min(height, 128)
+    for copy, slot, at, first in jobs:
+        copy.wait()
+
+        def turn(g, carried, slot=slot, at=at, first=first):
+            columns = pl.ds(pl.multiple_of(g * unit_half, unit_half), unit_half)
+            span = pl.ds(pl.multiple_of(at * wide_half + g * unit_half, unit_half), unit_half)
+            for low_row in range(0, height, piece):
+                into = pl.ds(pl.multiple_of(first + low_row, piece), piece)
+                w[span, into] = stage[slot, low_row : low_row + piece, columns].T
+            return carried
+
+        lax.fori_loop(0, 4, turn, 0)
+
+    place_of = (s, 1 - s)
 
     def retreat(k, carried):
-        t = first - 1 - k
+        t = steps - 1 - k
         earlier = jnp.maximum(t - 1, 0)
         live = jnp.where(t > 0, 1.0, 0.0).astype(wide)
         for at in range(0, 2 * unit_half, chunk):
             half, inside = at // unit_half, at % unit_half
             units = pl.ds(at, chunk)
-            grad = (
-                jnp.concatenate([outside[0, t, :, units], outside[1, t, :, units]], axis=0)
-                + dh[:, units]
+            ours, theirs = kept[t, :, units], taken[t, :, units].astype(wide)
+            grad = dh[:, units] + jnp.concatenate(
+                [jnp.where(first_chip, ours, theirs), jnp.where(first_chip, theirs, ours)], axis=0
             )
             i, f, g, o = [
                 gates[t, :, pl.ds(half * wide_half + n * unit_half + inside, chunk)]
@@ -235,9 +269,9 @@
                 grad * squash * o * (1.0 - o),
             )
             for n, part in enumerate(parts):
-                dz[half, t - last, :, pl.ds(n * unit_half + inside, chunk)] = part.astype(low)
+                dz[place_of[half], t, :, pl.ds(n * unit_half + inside, chunk)] = part.astype(low)
             dc[:, units] = total * f
-        upper, lower = dz[0, t - last], dz[1, t - last]
+        upper, lower = dz[place_of[0], t], dz[place_of[1], t]
         for at in range(0, 2 * unit_half, chunk):
             units = pl.ds(at, chunk)
             dh[:, units] = jnp.dot(
@@ -245,98 +279,28 @@
             ) + jnp.dot(lower, w[wide_half:, units], preferred_element_type=wide)
         return carried
 
-    lax.fori_loop(0, first - last, retreat, 0)
-
-
-def late_kernel(count, column, middle, places, outside, gates, cells, *refs):
-    w_own, w_other = refs[:count], refs[count : 2 * count]
-    dz, turned, dh, dc, stage, w, sems, out_sem = refs[2 * count :]
-    steps, _, wide_full = gates.shape
-    wide_half = wide_full // 2
-    unit_half = wide_half // 4
-    s = places[0]
-    jobs = []
-    for n, (sources, at) in enumerate(((w_own, s), (w_other, 1 - s))):
-        for k, block in enumerate(sources):
-            slot = n * count + k
-            copy = pltpu.make_async_copy(
-                block.at[:, column : column + wide_half], stage.at[slot], sems.at[slot]
-            )
-            copy.start()
-            jobs.append((copy, slot, at, places[1 + k] * block.shape[0]))
-    dh[...] = jnp.zeros_like(dh)
-    dc[...] = jnp.zeros_like(dc)
-    height = w_own[0].shape[0]
-    piece = min(height, 128)
-    for copy, slot, at, first in jobs:
-        copy.wait()
-
-        def turn(g, carried, slot=slot, at=at, first=first):
-            columns = pl.ds(pl.multiple_of(g * unit_half, unit_half), unit_half)
-            span = pl.ds(pl.multiple_of(at * wide_half + g * unit_half, unit_half), unit_half)
-            for low_row in range(0, height, piece):
-                into = pl.ds(pl.multiple_of(first + low_row, piece), piece)
-                w[span, into] = stage[slot, low_row : low_row + piece, columns].T
-            return carried
-
-        lax.fori_loop(0, 4, turn, 0)
-    save = pltpu.make_async_copy(w, turned, out_sem)
-    save.start()
-    backward_steps(steps, middle, outside, gates, cells, dz, w, dh, dc)
-    save.wait()
-
-
-def early_kernel(middle, outside, gates, cells, dh_in, dc_in, turned, dz, w, dh, dc, sem):
-    load = pltpu.make_async_copy(turned, w, sem)
-    load.start()
-    dh[...] = dh_in[...]
-    dc[...] = dc_in[...]
-    load.wait()
-    backward_steps(middle, 0, outside, gates, cells, dz, w, dh, dc)
-
-
-def run_late(places, outside, gates, cells, w_own, w_other, column, middle):
+    lax.fori_loop(0, steps, retreat, 0)
+
+
+def run_backward(places, kept, taken, gates, cells, w_own, w_other, column):
     steps, rows, wide_full = gates.shape
     units = cells.shape[2]
     count = len(w_own)
     return pl.pallas_call(
-        functools.partial(late_kernel, count, column, middle),
-        out_shape=(
-            jax.ShapeDtypeStruct((2, steps - middle, rows, wide_full // 2), low),
-            jax.ShapeDtypeStruct((wide_full, units), low),
-            jax.ShapeDtypeStruct((rows, units), wide),
-            jax.ShapeDtypeStruct((rows, units), wide),
-        ),
-        in_specs=[in_smem] + [in_vmem] * 3 + [in_place] * (2 * count),
-        out_specs=[in_vmem, in_place, in_vmem, in_vmem],
+        functools.partial(backward_kernel, count, column),
+        out_shape=jax.ShapeDtypeStruct((2, steps, rows, wide_full // 2), low),
+        in_specs=[in_smem] + [in_vmem] * 4 + [in_place] * (2 * count),
+        out_specs=in_vmem,
         scratch_shapes=[
             pltpu.VMEM((2 * count, units // count, wide_full // 2), low),
             pltpu.VMEM((wide_full, units), low),
+            pltpu.VMEM((rows, units), wide),
+            pltpu.VMEM((rows, units), wide),
             pltpu.SemaphoreType.DMA((2 * count,)),
-            pltpu.SemaphoreType.DMA,
         ],
         compiler_params=pltpu.CompilerParams(vmem_limit_bytes=56 << 20),
-        name="recur_backward_late",
-    )(places, outside, gates, cells, *w_own, *w_other)
-
-
-def run_early(outside, gates, cells, dh, dc, turned, middle):
-    steps, rows, wide_full = gates.shape
-    units = cells.shape[2]
-    return pl.pallas_call(
-        functools.partial(early_kernel, middle),
-        out_shape=jax.ShapeDtypeStruct((2, middle, rows, wide_full // 2), low),
-        in_specs=[in_vmem] * 5 + [in_place],
-        out_specs=in_vmem,
-        scratch_shapes=[
-            pltpu.VMEM((wide_full, units), low),
-            pltpu.VMEM((rows, units), wide),
-            pltpu.VMEM((rows, units), wide),
-            pltpu.SemaphoreType.DMA,
-        ],
-        compiler_params=pltpu.CompilerParams(vmem_limit_bytes=56 << 20),
-        name="recur_backward_early",
-    )(outside, gates, cells, dh, dc, turned)
+        name="recur_backward",
+    )(places, kept, taken, gates, cells, *w_own, *w_other)
 
 
 def input_kernel(count, places, inputs, gain, dz, dz_given, *refs):
@@ -394,14 +358,14 @@
 
 
 def attend_kernel(
-    count, places, memory, decoded, vectors, vocab_bias, noise, lengths, labels, counted, *refs
+    count, places, kept, taken, vectors, vocab_bias, noise, lengths, labels, counted, *refs
 ):
     small, vocab = refs[: 4 * count], refs[4 * count : 4 * count + 4]
     (
-        grad_memory, grad_decoded, pack, seen, sums,
-        w, v, sems, v_sems, mk, sk, mq, sq, mono, span, keep, queue, scaled, ratio, window, mix, pre,
+        grad_own, grad_given, pack, seen, sums,
+        memory, decoded, grad_memory, w, v, sems, v_sems, mk, sk, mq, sq, mono, span, keep, queue, scaled, ratio, window, mix, pre,
     ) = refs[4 * count + 4 :]
-    rows, _ = memory.shape
+    rows, _ = kept.shape
     frames, group, _ = mk.shape
     block = w.shape[2] // 6
     lanes = 128
@@ -413,7 +377,7 @@
             source = small[r * count + k]
             height = source.shape[0]
             for h in range(source.shape[1] // (6 * block)):
-                to = pl.ds(pl.multiple_of(places[1 + len(arrived)] * height, height), height)
+                to = pl.ds(pl.multiple_of(places[2 + len(arrived)] * height, height), height)
                 arrived.append(
                     pltpu.make_async_copy(
                         source.at[:, 6 * block * h : 6 * block * (h + 1)],
@@ -425,6 +389,18 @@
     vocab_copies = [pltpu.make_async_copy(vocab[r], v.at[r], v_sems.at[r]) for r in range(4)]
     for copy in sum(copies, []) + vocab_copies:
         copy.start()
+
+    first_chip = places[1] == 0
+
+    @pl.when(first_chip)
+    def _():
+        memory[...] = kept[...]
+        decoded[...] = taken[...]
+
+    @pl.when(jnp.logical_not(first_chip))
+    def _():
+        memory[...] = taken[...]
+        decoded[...] = kept[...]
 
     def split(value):
         return value.reshape(frames, group, value.shape[-1])
@@ -648,15 +624,15 @@
         total_decoded = total_decoded + dot_nt(
             pack[r, :, 2 * block : 5 * block], w[r, :, 2 * block : 5 * block]
         )
-    grad_memory[...] = total_memory
-    grad_decoded[...] = total_decoded
+    grad_own[...] = jnp.where(first_chip, total_memory, total_decoded)
+    grad_given[...] = jnp.where(first_chip, total_decoded, total_memory).astype(low)
 
 
 def run_attend(
-    places, memory, decoded, smalls, vocab, vectors, vocab_bias, noise, lengths, labels, counted,
+    places, kept, taken, smalls, vocab, vectors, vocab_bias, noise, lengths, labels, counted,
     frames,
 ):
-    rows, width = memory.shape
+    rows, width = kept.shape
     group = rows // frames
     full = vectors.shape[1]
     vocab_width = vocab[0].shape[1]
@@ -666,7 +642,7 @@
         functools.partial(attend_kernel, count),
         out_shape=(
             jax.ShapeDtypeStruct((rows, width), wide),
-            jax.ShapeDtypeStruct((rows, width), wide),
+            jax.ShapeDtypeStruct((rows, width), low),
             jax.ShapeDtypeStruct((4, rows, full // 4 * 6), low),
             jax.ShapeDtypeStruct((2, rows, vocab_width), low),
             jax.ShapeDtypeStruct((8, full), wide),
@@ -674,9 +650,12 @@
         in_specs=[in_smem] + [in_vmem] * 8 + [in_place] * (4 * count + 4),
         out_specs=[in_vmem] * 5,
         scratch_shapes=[
+            pltpu.VMEM((rows, width), low),
+            pltpu.VMEM((rows, width), low),
+            pltpu.VMEM((rows, width), wide),
             pltpu.VMEM((4, width, full // 4 * 6), low),
             pltpu.VMEM((4,) + vocab[0].shape, low),
-            pltpu.SemaphoreType.DMA((4, places.shape[0] - 1)),
+            pltpu.SemaphoreType.DMA((4, places.shape[0] - 2)),
             pltpu.SemaphoreType.DMA((4,)),
         ]
         + [pltpu.VMEM((frames, group, full), wide)] * 4
@@ -685,7 +664,7 @@
         compiler_params=pltpu.CompilerParams(vmem_limit_bytes=56 << 20),
         name="attend",
     )(
-        places, memory, decoded, vectors, vocab_bias, noise, lengths, labels, counted,
+        places, kept, taken, vectors, vocab_bias, noise, lengths, labels, counted,
         *sum(smalls, []), *vocab,
     )
 
@@ -740,21 +719,24 @@
     ready = (noise_part, length_part, label_part, counted, bias_row, normed_own, normed_other)
     places, in_own, rec_own, small_own, small_chip = [], [], [], [], []
     small = jnp.concatenate(
-        [mono_mem, span_mem, mono_dec, span_dec, out_weight[0], out_weight[1]], axis=1
+        [
+            tie(mono_mem, in_shard, rec_shard), span_mem, mono_dec, span_dec,
+            out_weight[0], out_weight[1],
+        ],
+        axis=1,
     )
     if ring.short:
         flow, across, onward = Flow(), ring.across, ring.onward
         both = 2 * wide_half
-        corner = jnp.pad(bias_shard.reshape(shard_rows, -1), ((0, 0), (0, 128 - 16)))
-        corner = jnp.concatenate([in_shard, rec_shard, corner], axis=1)
-        corner, vector_pair, small_far, small_next = flow.step(
-            (corners, corner), (across_chips, vector_own), (across, small), (onward, small)
-        )
-        b_own = corner[:, both : both + 16].astype(wide).reshape(1, wide_half)
-        vector_pair = jnp.concatenate([vector_own, vector_pair], axis=1)
+        corner_in, corner_rec, b_own = flow.step(
+            (corners, in_shard), (corners, rec_shard), (corners, bias_shard)
+        )
+        small_far, small_next = across(small), onward(small)
+        flow.landed += (small_far, small_next)
+        b_own = b_own.astype(wide)
         small_own = [jnp.concatenate([small, small_far], axis=1)]
         small_chip, small_core = [], []
-        held = jnp.concatenate([corner[:, :both], small_next], axis=1)
+        held = jnp.concatenate([corner_in, corner_rec, small_next], axis=1)
         near, far, near_core, far_core = [], [], [], []
         for k in range(ring.outer):
             near.append(held)
@@ -762,12 +744,13 @@
             if k < ring.outer - 1:
                 jobs.append((onward, held[:, :both] if k == ring.outer - 2 else held))
             if k == 0:
-                jobs.append((across_chips, vocab_own))
+                jobs += [(across_chips, vocab_own), (across_chips, vector_own)]
             results = flow.step(*jobs, also=ready if k == 1 else ())
             far.append(results[0])
             small_chip.append(results[1])
             if k == 0:
-                vocab_chip = results[3]
+                vocab_chip, vector_pair = results[3:]
+                vector_pair = jnp.concatenate([vector_own, vector_pair], axis=1)
             if k < ring.outer - 1:
                 small_own.append(jnp.concatenate([held[:, both:], far[k][:, both:]], axis=1))
                 held = results[2]
@@ -775,9 +758,12 @@
             near_core.append(across_cores(a))
             far_core.append(across_cores(b))
         small_core = [across_cores(a) for a in small_own]
-        b_other = across_cores(b_own)
-        vocab = [vocab_own, vocab_chip, across_cores(vocab_own), across_cores(vocab_chip)]
-        vector_core = across_cores(vector_pair)
+        b_last, vocab_last, chip_last, vector_last = lax.optimization_barrier(
+            (b_own, vocab_own, vocab_chip, vector_pair, held)
+        )[:4]
+        b_other = across_cores(b_last)
+        vocab = [vocab_own, vocab_chip, across_cores(vocab_last), across_cores(chip_last)]
+        vector_core = across_cores(vector_last)
         in_own = [a for pair in zip(near, far) for a in pair]
         in_other = [a for pair in zip(near_core, far_core) for a in pair]
         rec_own, rec_other, rec_column = in_own, in_other, wide_half
@@ -801,100 +787,93 @@
         vector_core = across_cores(vector_pair)
     vectors = jnp.concatenate([vector_pair, vector_core], axis=1)
     vectors = jnp.pad(vectors, ((0, 3), (0, 0)))
-    places = jnp.stack([s] + places).astype(jnp.int32)
+    places = jnp.stack([s, y] + places).astype(jnp.int32)
     places = tie(places, vectors, *vocab, *ready, *small_chip[:-1], *small_core)
 
-    quarters, before, gates, cells = run_forward(
+    kept, given, before, gates, cells = run_forward(
         places, normed_own, b_own, b_other, in_own, in_other, rec_own, rec_other, frames,
         rec_column,
     )
 
-    kept = lax.dynamic_index_in_dim(quarters, y, axis=0, keepdims=False)
-    given = lax.dynamic_index_in_dim(quarters, 1 - y, axis=0, keepdims=False)
+    kept, given = kept.reshape(rows, width), given.reshape(rows, width)
     taken = across_chips(given)
-    memory = jnp.where(y == 0, kept, taken).reshape(rows, width)
-    decoded = jnp.where(y == 0, taken, kept).reshape(rows, width)
     small_chip[-1] = tie(small_chip[-1], kept)
     small_both = [across_cores(part) for part in small_chip]
     smalls = [small_own, small_chip, small_core, small_both]
-    grad_memory, grad_decoded, pack, seen, sums = run_attend(
-        places, memory, decoded, smalls, vocab, vectors, bias_row, noise_part, length_part,
+    grad_own, grad_given, pack, seen, sums = run_attend(
+        places, kept, taken, smalls, vocab, vectors, bias_row, noise_part, length_part,
         label_part, counted, frames,
     )
-    kept_far = across_chips(tie(kept, taken))
-    before = before.reshape(frames * half, width)
-    before_peer = across_cores(tie(before, taken))
-
-    grad_kept = jnp.where(y == 0, grad_memory, grad_decoded)
-    grad_given = jnp.where(y == 0, grad_decoded, grad_memory).astype(low)
     grad_taken = across_chips(grad_given)
-    outside = jnp.stack(
-        [jnp.where(y == 0, grad_kept, grad_taken), jnp.where(y == 0, grad_taken, grad_kept)]
-    ).reshape(2, frames, quarter, width)
     pack_core = across_cores(pack[2:4])
     pack_out = jnp.stack([pack[1], pack_core[1]])
-    memory_next = jnp.where(y == 0, given, kept_far).reshape(rows, width)
-    decoded_next = jnp.where(y == 0, kept_far, given).reshape(rows, width)
-    states = jnp.stack([memory, memory_next, decoded, decoded_next])
-    states_core = across_cores(states)
     blocks = sums[:5].reshape(5, 4, block)
     vector_pair = blocks[:, :2] + across_cores(blocks[:, 2:])
     bias_pair = sums[5] + across_cores(sums[5])
     vector_out = jnp.concatenate([vector_pair[:, 1].reshape(-1), bias_pair])
-    vector_count = vector_out.shape[0] // (2 * rows)
-    places_back, pack_out, states_core = lax.optimization_barrier(
-        (places, pack_out, states_core, outside, before_peer)
+    vector_count = vector_out.shape[0] // (3 * rows)
+    seen_out = jnp.concatenate(
+        [
+            jnp.concatenate([seen, kept[None]], axis=0),
+            halves(vector_out, 3 * rows).reshape(3, rows, -1),
+        ],
+        axis=2,
+    )
+    before = before.reshape(frames * half, width)
+    before_peer = across_cores(tie(before, taken))
+    states = jnp.stack([kept, taken])
+    states_core = across_cores(tie(states, grad_given))
+    places_back, pack_out, seen_out = lax.optimization_barrier(
+        (places, pack_out, seen_out, grad_taken, before_peer, states_core)
     )[:3]
-    middle = frames * 3 // 8
-    dz_late, turned, dh, dc = run_late(
-        places_back, outside, gates, cells, rec_own, rec_other, rec_column, middle
+    dz = run_backward(
+        places_back, grad_own.reshape(frames, quarter, width),
+        grad_taken.reshape(frames, quarter, width), gates, cells, rec_own, rec_other, rec_column,
     )
     pack_far = across_chips(pack_out)
-    seen_out = jnp.concatenate(
-        [seen, halves(vector_out, 2 * rows).reshape(2, rows, -1)], axis=2
-    )
     seen_far = across_chips(tie(seen_out, pack_out))
+
+    dz = dz.reshape(2, frames * half, wide_half)
+    dz_kept, dz_given, pack_far, seen_far = lax.optimization_barrier(
+        (dz[0], dz[1], pack_far, seen_far)
+    )
+    dz_all = jnp.concatenate([dz_kept, across_cores(dz_given)], axis=0)
+    before_all = jnp.concatenate([before, before_peer], axis=0)
+    normed_all = jnp.concatenate([normed_own, normed_other], axis=0)
+    rec_total = dot_tn(before_all, dz_all).astype(low)
+    in_total = dot_tn(normed_all, dz_all).astype(low)
+
+    vector_far = joined(seen_far[:, :, width:].reshape(3 * rows, -1), vector_count).reshape(-1)
+    chip_rows = jnp.concatenate(
+        [seen, seen_far[:2, :, :width], jnp.stack([given, seen_far[2, :, :width]])], axis=0
+    )
+    core_rows = across_cores(chip_rows)
+    section_all = jnp.concatenate([kept, states_core[0], chip_rows[4], core_rows[4]], axis=0)
+    other_all = jnp.concatenate([taken, states_core[1], chip_rows[5], core_rows[5]], axis=0)
+    memory_all = jnp.where(y == 0, section_all, other_all)
+    decoded_all = jnp.where(y == 0, other_all, section_all)
+    seen_all = [
+        jnp.concatenate([chip_rows[n], core_rows[n], chip_rows[2 + n], core_rows[2 + n]], axis=0)
+        for n in range(2)
+    ]
     pack_all = jnp.concatenate([pack[0], pack_core[0], pack_far[0], pack_far[1]], axis=0)
-    memory_all, decoded_all = [
-        jnp.concatenate([states[n], states_core[n], states[n + 1], states_core[n + 1]], axis=0)
-        for n in (0, 2)
-    ]
+    if ring.short:
+        first_rec, first_in = [
+            cut(a, ring.back(1) * 2 + 1 - ring.x, shard_rows) for a in (rec_total, in_total)
+        ]
+        pack_all = tie(pack_all, first_rec, first_in)
     energy_total = [
         dot_tn(memory_all, pack_all[:, : 2 * block]).astype(low),
         dot_tn(decoded_all, pack_all[:, 2 * block : 4 * block]).astype(low),
     ]
     grad_pre = pack_all[:, 4 * block : 5 * block]
-    decoded_total = dot_tn(decoded_all, grad_pre).astype(low)
-    dh, *energy_total, decoded_total = lax.optimization_barrier((dh, *energy_total, decoded_total))
-    dz_early = run_early(outside, gates, cells, dh, dc, turned, middle)
-
-    def rows_of(part, at):
-        part = lax.dynamic_index_in_dim(part, at, axis=0, keepdims=False)
-        return part.reshape(-1, wide_half)
-
-    dz_kept = jnp.concatenate([rows_of(dz_early, s), rows_of(dz_late, s)], axis=0)
-    dz_given = jnp.concatenate([rows_of(dz_early, 1 - s), rows_of(dz_late, 1 - s)], axis=0)
-    dz_all = jnp.concatenate([dz_kept, across_cores(dz_given)], axis=0)
-    before_all = jnp.concatenate([before, before_peer], axis=0)
-    normed_all = jnp.concatenate([normed_own, normed_other], axis=0)
-    rec_total = dot_tn(before_all, dz_all).astype(low)
-    in_total = dot_tn(normed_all, dz_all).astype(low)
-
-    vector_far = joined(seen_far[:, :, seen.shape[2] :].reshape(2 * rows, -1), vector_count)
-    vector_far = vector_far.reshape(-1)
-    seen_far = seen_far[:, :, : seen.shape[2]]
-    seen_pair = jnp.concatenate([seen, seen_far], axis=0)
-    seen_core = across_cores(seen_pair)
-
-    seen_all = [
-        jnp.concatenate([seen_pair[n], seen_core[n], seen_pair[2 + n], seen_core[2 + n]], axis=0)
-        for n in range(2)
-    ]
     output_total = [
-        decoded_total,
+        dot_tn(decoded_all, grad_pre).astype(low),
         dot_tn(seen_all[0], grad_pre).astype(low),
         dot_tn(seen_all[1], pack_all[:, 5 * block :]).astype(low),
     ]
+
+    sides_at = 5 * block + vocab_pad
 
     def to_other_chip(section):
         return lax.ppermute(section, ("section", "mp"), [(0, 1), (3, 2)])
@@ -927,65 +906,74 @@
 
     if ring.short:
         r, x = shard_rows, ring.x
-        columns = 3 * block
+        both, width_out = 2 * wide_half, 2 * block
         flow, across, onward = Flow(), ring.across, ring.onward
         chain = [rec_total, in_total] + energy_total
 
-        def theirs(k):
-            return ring.part(chain, ring.back(k) * 2 + 1 - x, r)
+        def theirs(group, k):
+            return ring.part(group, ring.back(k) * 2 + 1 - x, r)
 
         def total(k, arrived, passed):
             value = ring.part(chain, ring.back(k) * 2 + x, r).astype(wide)
             value = value + arrived.astype(wide)
             return value if passed is None else value + passed.astype(wide)
 
+        def cornered(hop):
+            index = lambda at, place, chip: (at * ring.dp + place) * 2 + chip
+            pairs = [
+                (index(p, a, q), index(q, b, p)) for a, b in hop for p in range(2) for q in range(2)
+            ]
+            return lambda array: lax.ppermute(array, ("section", "dp", "mp"), pairs)
+
         def output_part(k):
             return ring.part(output_total, ring.back(k), 2 * r)
 
-        def output_sum(k, arrived):
-            return output_part(k).astype(wide) + arrived.astype(wide)
-
-        arrived, out = flow.step((across, theirs(1)), (onward, output_part(1)))
-        grad_section, flat = input_back(tie(dz_kept, arrived))
-        out = onward(output_sum(2, out).astype(low))
+        arrived = [across(a) for a in (first_rec, first_in, theirs(energy_total, 1))]
+        out_two, out_before = onward(output_part(2)), ring.astern(output_part(1))
+        grad_section, flat = input_back(tie(dz_kept, first_in, *output_total))
+        flat_width = flat.shape[0] // r
+        out_one = output_part(3).astype(wide) + out_two.astype(wide)
+        out_one = onward(out_one.astype(low))
+        flat_far = across(tie(halves(flat, r), out_two, out_before))
+        arrived = jnp.concatenate(arrived, axis=1)
+        flow.landed = (arrived, out_one, flat_far)
         value = total(1, arrived, None).astype(low)
-        passed, arrived, out, grad_far = flow.step(
-            (onward, value), (across, theirs(2)), (onward, output_sum(3, out).astype(low)),
-            (to_other_chip, grad_section), also=(out,),
-        )
-        out = output_sum(4, out)
+        out = output_part(4).astype(wide) + out_before.astype(wide) + out_one.astype(wide)
+        vocab_rows = out[:, width_out:].astype(low)
+        message = jnp.concatenate(
+            [cut(out, 1 - x, r)[:, :width_out].astype(low), vocab_rows[:r], vocab_rows[r:]], axis=1
+        )
+        passed, arrived, out_far, grad_far = flow.step(
+            (onward, value), (across, theirs(chain, 2)), (across, message),
+            (to_other_chip, grad_section),
+        )
+        output_grad = cut(out, x, r)[:, :width_out] + out_far[:, :width_out].astype(wide)
+        flat = flat + joined(flat_far, flat_width).reshape(-1)
+        shard = jnp.concatenate([out[:r, width_out:], out[r:, width_out:]], axis=1)
+        shard = (shard + out_far[:, width_out:].astype(wide)).astype(low)
+        shard = jnp.concatenate([shard, halves(flat, r)], axis=1)
         value = total(2, arrived, passed).astype(low)
-        passed, arrived, out_far = flow.step(
-            (onward, value), (across, theirs(3)), (across, cut(out, 1 - x, r).astype(low))
-        )
-        output_grad = cut(out, x, r) + out_far.astype(wide)
-        flat_width = flat.shape[0] // r
-        shard = jnp.concatenate(
-            [output_grad[:, 2 * block :].astype(low), halves(flat, r)], axis=1
-        )
+        mine = ring.part([rec_total, in_total], ring.back(4) * 2 + x, r)
+        passed, arrived, next_one, next_three, mine = flow.step(
+            (onward, value), (across, theirs(chain, 3)), (onward, shard), (ring.astern, shard),
+            (corners, mine),
+        )
+        shards = {0: shard, 1: next_one, 3: next_three, 2: onward(next_one)}
+        flat = sum(joined(a[:, 2 * block :], flat_width).reshape(-1) for a in shards.values())
         value = total(3, arrived, passed).astype(low)
-        passed, arrived, shard_far = flow.step(
-            (onward, value), (across, theirs(4)), (across, shard)
-        )
-        flat = flat + joined(shard_far[:, block:], flat_width).reshape(-1)
-        shard = jnp.concatenate([shard[:, :block], shard_far[:, :block], halves(flat, r)], axis=1)
-        chain_grad = total(4, arrived, passed)
-        moved = chain_grad[:, : 2 * wide_half].astype(low)
-        moved, next_one, next_three = flow.step(
-            (corners, moved), (onward, shard), (ring.astern, shard)
-        )
-        shards = {0: shard, 1: next_one, 3: next_three, 2: onward(next_one)}
+        passed, arrived, energy_passed, energy_arrived = flow.step(
+            (cornered(ring.ring), value[:, :both]),
+            (cornered(ring.pair), theirs([rec_total, in_total], 4)),
+            (onward, value[:, both:]), (across, theirs(energy_total, 4)),
+        )
+        sides = corners(flat[sides_at : sides_at + wide_half + width])
+        moved = mine.astype(wide) + arrived.astype(wide) + passed.astype(wide)
+        energy_grad = ring.part(energy_total, ring.back(4) * 2 + x, r).astype(wide)
+        energy_grad = energy_grad + energy_arrived.astype(wide) + energy_passed.astype(wide)
         vocab_grad = jnp.zeros((vocab_pad, block), low)
-        flat = 0.0
         for k, held in shards.items():
-            flat = flat + joined(held[:, 2 * block :], flat_width).reshape(-1)
-            for n, at in enumerate((x, 1 - x)):
-                vocab_grad = lax.dynamic_update_slice(
-                    vocab_grad,
-                    held[:, n * block : (n + 1) * block],
-                    ((ring.back(k) * 2 + at) * r, 0),
-                )
-        energy_grad = chain_grad[:, 2 * wide_half :]
+            held = jnp.concatenate([held[:, :block], held[:, block : 2 * block]], axis=0)
+            vocab_grad = lax.dynamic_update_slice(vocab_grad, held, (ring.back(k) * 2 * r, 0))
     else:
         grad_section, flat = input_back(dz_kept)
         grad_far = to_other_chip(grad_section)
@@ -994,24 +982,23 @@
             return lax.psum_scatter(total, "dp", scatter_dimension=0, tiled=True).astype(wide)
 
         moved = jnp.concatenate([scatter(rec_total), scatter(in_total)], axis=1)
-        moved = corners(moved.astype(low))
+        moved = corners(moved.astype(low)).astype(wide)
         energy_grad = jnp.concatenate([scatter(a) for a in energy_total], axis=1)
         output_grad = jnp.concatenate([scatter(a) for a in output_total], axis=1)
         flat = lax.psum(flat, "dp")
+        sides = corners(flat[sides_at : sides_at + wide_half + width])
         vocab_grad = lax.all_gather(
             output_grad[:, 2 * block :].astype(low), "dp", axis=0, tiled=True
         )
 
     input_grad = jnp.where(s == y, grad_section, grad_far)
     vocab_grad = vocab_grad.T[:, :vocab_size].astype(wide)
-    ends = [5 * block, 5 * block + vocab_pad, 5 * block + vocab_pad + wide_half + width]
-    vector_sum = flat[: ends[0]].reshape(5, block)
-    bias_sum = flat[ends[0] : ends[0] + vocab_size]
-    sides = corners(flat[ends[1] : ends[2]])
+    vector_sum = flat[: 5 * block].reshape(5, block)
+    bias_sum = flat[5 * block : 5 * block + vocab_size]
     lstm_bias_sum = sides[:wide_half].reshape(1, 4, unit_half)
     gain_sum = sides[wide_half:][None]
-    rec_grad = moved[:, :wide_half].astype(wide).reshape(1, shard_rows, 4, unit_half)
-    in_grad = moved[:, wide_half:].astype(wide).reshape(1, shard_rows, 4, unit_half)
+    rec_grad = moved[:, :wide_half].reshape(1, shard_rows, 4, unit_half)
+    in_grad = moved[:, wide_half:].reshape(1, shard_rows, 4, unit_half)
     mono_mem_grad, span_mem_grad, mono_dec_grad, span_dec_grad = [
         energy_grad[:, n * block : (n + 1) * block] for n in range(4)
     ]

time: 543 us -> 520 us (0.958)
  waiting for transfers between devices: 263 us -> 202 us
  starting transfers between devices: 51 us -> 72.4 us
  local copies, waits for them, and re-layouts: 59.9 us -> 79.5 us
  Pallas kernels: 109 us -> 103 us
    ppermute x11 -> x13, waiting for transfers between devices: 148 us -> 94 us  [across(): return lax.ppermute(array, 'dp', self.pair)]
    ppermute x3 -> x5, starting transfers between devices: 3.26 us -> 22.2 us  [corners(): return lax.ppermute(array, ('section', 'mp'), corner_swap)]
    ppermute x31, waiting for transfers between devices: 11.9 us -> 4.6 us  [across_cores(): return lax.ppermute(array, 'section', core_swap)]
    slice x7 -> x14, local copies, waits for them, and re-layouts: 0.87 us -> 7.8 us  [the longest x1 1.68 us: local(): dz[1]]
    pallas_call x2 -> x1, Pallas kernels: 37 us -> 30.2 us  [run_backward(): pl.pallas_call(functools.partial(backward_kernel, count, column), out_sha...]
    ppermute x11 -> x10, starting transfers between devices: 17.2 us -> 10.5 us  [across_chips(): return lax.ppermute(array, 'mp', core_swap)]
    ppermute x1 -> x2, starting transfers between devices: 1.96 us -> 7.87 us  [astern(): return lax.ppermute(array, 'dp', self.turn)]
    ppermute x12 -> x11, waiting for transfers between devices: 73.6 us -> 76.5 us  [onward(): return lax.ppermute(array, 'dp', self.ring)]
  transfers between devices with their start and end apart: 70 -> 75, of which waited for: 30 -> 21; matrix products, arithmetic and copies ran while one was open for 15% -> 20% of each run, Pallas kernels for 19% -> 20%
where the time goes in v4:
time: 520 us; the launch traced here: 510 us
  waiting for transfers between devices  202 us (39%)
  Pallas kernels  103 us (20%)
  local copies, waits for them, and re-layouts  79.5 us (15%)
  starting transfers between devices  72.4 us (14%)
  other arithmetic  41.4 us (8%)
  matrix products  8.81 us (2%)
    ppermute x13, waiting for transfers between devices, across(): return lax.ppermute(array, 'dp', self.pair)  94 us
    ppermute x11, waiting for transfers between devices, onward(): return lax.ppermute(array, 'dp', self.ring)  76.5 us
    pallas_call x1, Pallas kernels, run_attend(): pl.pallas_call(functools.partial(attend_kernel, count), out_shape=(jax.Sh...  33.4 us
    pallas_call x1, Pallas kernels, run_forward(): pl.pallas_call(functools.partial(forward_kernel, count, column), out_shap...  30.7 us
    pallas_call x1, Pallas kernels, run_backward(): pl.pallas_call(functools.partial(backward_kernel, count, column), out_sha...  30.2 us
    ppermute x10, waiting for transfers between devices, across_chips(): return lax.ppermute(array, 'mp', core_swap)  27.3 us
    ppermute x5, starting transfers between devices, corners(): return lax.ppermute(array, ('section', 'mp'), corner_swap)  22.2 us
    unnamed x169, local copies, waits for them, and re-layouts  18.7 us
  transfers between devices with their start and end apart: 75, of which 21 were waited for; matrix products, arithmetic and copies ran while one was open for 20% of the time, Pallas kernels for 20%

profile of v4, /device:TPU:0, one launch (start us, length us, event | category | flops | bytes accessed | tf_op | source)
XLA Modules:
  0.0 510.5 jit_solution(12123219828145604467)
XLA Ops:
  0.8 2.1 copy.115
  2.9 1.9 copy.116
  8.7 3.0 collective-permute-start.2
  11.7 1.5 collective-permute-start.3
  13.2 5.4 %collective-permute-start = (bf16[128,2048]{1,0:T(8,128)(2,1)}, bf16[128,2048]{1,0:T(8,128)(2,1)}, u32[]{:S(2)}, u32[]{:S(2)}) collective-permute-start(bf16[128,2048]{1,0:T(8,128)(2,1)} %bitcast.70), channel_id=1, source_target_pairs={{0,0},{1,16},{16,1},{17,17},{2,2},{3,18},{18,3},{19,19},{4,4},{5,2... | collective-permute-start | bytes 1572872 | tf_op jit(solution)/shard_map/ppermute | solution.py:37
  18.6 5.4 %collective-permute-start.1 = (bf16[128,2048]{1,0:T(8,128)(2,1)}, bf16[128,2048]{1,0:T(8,128)(2,1)}, u32[]{:S(2)}, u32[]{:S(2)}) collective-permute-start(bf16[128,2048]{1,0:T(8,128)(2,1)} %bitcast.73), channel_id=1, source_target_pairs={{0,0},{1,16},{16,1},{17,17},{2,2},{3,18},{18,3},{19,19},{4,4},{5,2... | collective-permute-start | bytes 1572872 | tf_op jit(solution)/shard_map/ppermute | solution.py:37
  32.9 3.6 collective-permute-start.6
  36.6 1.6 collective-permute-start.7
  38.7 1.9 collective-permute-start.9
  44.3 27.2 %collective-permute-done.8.refs_1_.refs_17_ = bf16[128,5632]{1,0:T(8,128)(2,1)S(1)} collective-permute-done((bf16[128,5632]{1,0:T(8,128)(2,1)S(1)}, bf16[128,5632]{1,0:T(8,128)(2,1)S(1)}, u32[]{:S(2)}, u32[]{:S(2)}) %collective-permute-start.8) | collective-permute-done | bytes 1441824 | tf_op jit(solution)/shard_map/ppermute | solution.py:73
  72.0 1.7 broadcast_in_dim.17.noise
  76.6 30.7 %collective-permute-done.13.refs_3_.refs_19_ = bf16[128,5632]{1,0:T(8,128)(2,1)S(1)} collective-permute-done((bf16[128,5632]{1,0:T(8,128)(2,1)S(1)}, bf16[128,5632]{1,0:T(8,128)(2,1)S(1)}, u32[]{:S(2)}, u32[]{:S(2)}) %collective-permute-start.13) | collective-permute-done | bytes 1441824 | tf_op jit(solution)/shard_map/ppermute | solution.py:73
  107.4 1.9 collective-permute-done.12.refs_4_.refs_20_
  109.5 1.6 collective-permute-start.23
  111.1 2.3 collective-permute-done.20.refs_8_
  114.1 17.0 %collective-permute-done.19.refs_6_ = bf16[128,3072]{1,0:T(8,128)(2,1)S(1)} collective-permute-done((bf16[128,3072]{1,0:T(8,128)(2,1)S(1)}, bf16[128,3072]{1,0:T(8,128)(2,1)S(1)}, u32[]{:S(2)}, u32[]{:S(2)}) %collective-permute-start.19) | collective-permute-done | bytes 786464 | tf_op jit(solution)/shard_map/ppermute | solution.py:33
  131.0 10.3 %collective-permute-done.23.refs_5_.refs_21_ = bf16[128,5632]{1,0:T(8,128)(2,1)} collective-permute-done((bf16[128,5632]{1,0:T(8,128)(2,1)S(1)}, bf16[128,5632]{1,0:T(8,128)(2,1)}, u32[]{:S(2)}, u32[]{:S(2)}) %collective-permute-start.23) | collective-permute-done | bytes 1441824 | tf_op jit(solution)/shard_map/ppermute | solution.py:73
  144.1 1.6 collective-permute-start.26
  149.7 19.8 %collective-permute-done.26.refs_7_.refs_23_ = bf16[128,4096]{1,0:T(8,128)(2,1)} collective-permute-done((bf16[128,4096]{1,0:T(8,128)(2,1)}, bf16[128,4096]{1,0:T(8,128)(2,1)}, u32[]{:S(2)}, u32[]{:S(2)}) %collective-permute-start.26) | collective-permute-done | bytes 1048608 | tf_op jit(solution)/shard_map/ppermute | solution.py:73
  172.5 30.7 %recur_forward.1 = (bf16[16,8,1024]{2,1,0:T(8,128)(2,1)}, bf16[16,8,1024]{2,1,0:T(8,128)(2,1)}, bf16[16,16,1024]{2,1,0:T(8,128)(2,1)}, f32[16,16,4096]{2,1,0:T(8,128)}, f32[16,16,1024]{2,1,0:T(8,128)}) custom-call(s32[10]{0:T(128)} %stack.79.places, bf16[256,1024]{1,0:T(8,128)(2,1)} %bitcast.123, f32[1,2048]{1,0:T(1,128)} %copy-done.67, ...), custom_call_target="tpu_custom_call" | custom-call | tf_op jit(solution)/shard_map/recur_forward/pallas_call | solution.py:187
  207.3 5.0 collective-permute-done.35.taken
  212.3 1.9 pad_maximum_fusion.14
  215.9 33.4 %attend.1 = (f32[128,1024]{1,0:T(8,128)}, bf16[128,1024]{1,0:T(8,128)(2,1)}, bf16[4,128,1536]{2,1,0:T(8,128)(2,1)}, bf16[2,128,1024]{2,1,0:T(8,128)(2,1)}, f32[8,1024]{1,0:T(8,128)}) custom-call(s32[10]{0:T(128)} %stack.79.places, bf16[128,1024]{1,0:T(8,128)(2,1)} %bitcast.118, bf16[128,1024]{1,0:T(8,128)(2,1)} %copy-done.23, ...), custom_call_target="tpu_custom_call" | custom-call | tf_op jit(solution)/shard_map/attend/pallas_call | solution.py:641
  251.6 1.9 slice_bitcast_fusion.3
  259.6 4.1 collective-permute-done.44
  266.6 1.9 slice_bitcast_fusion.11
  268.5 30.2 %recur_backward.1 = bf16[2,16,16,2048]{3,2,1,0:T(8,128)(2,1)} custom-call(s32[10]{0:T(128)} %stack.79.places, f32[16,8,1024]{2,1,0:T(8,128)} %bitcast.129, bf16[16,8,1024]{2,1,0:T(8,128)(2,1)} %bitcast.135, f32[16,16,4096]{2,1,0:T(8,128)} %get-tuple-element.112.gates, f32[16,16,1024]{2,1,0:T(8,128)} %get-tuple-element.113.cells, ...), custom_call_target="tpu_custom_call" | custom-call | tf_op jit(solution)/shard_map/recur_backward/pallas_call | solution.py:289
  298.7 1.7 fusion.58
  301.7 2.0 slice_bitcast_fusion.14
  309.2 1.4 constant_dynamic-update-slice_fusion.12
  310.7 2.4 convolution_convert_fusion.1
  313.1 3.5 convolution_convert_fusion
  316.5 1.5 constant_dynamic-slice_fusion.5
  318.1 1.5 collective-permute-start.52
  319.6 1.5 constant_dynamic-slice_fusion.4
  324.2 1.5 slice_bitcast_fusion.7
  333.5 1.5 collective-permute-start.54
  336.6 4.1 collective-permute-start.55
  340.6 8.8 %input_back.1 = (f32[256,1024]{1,0:T(8,128)}, f32[1,1024]{1,0:T(1,128)}) custom-call(s32[10]{0:T(128)} %stack.79.places, bf16[256,1024]{1,0:T(8,128)(2,1)} %bitcast.125, f32[1,1024]{1,0:T(1,128)} %bitcast.141, bf16[256,2048]{1,0:T(8,128)(2,1)} %bitcast.112, bf16[256,2048]{1,0:T(8,128)(2,1)} %bitcast.116, bf16[128,5632]{1,0:T(8,128)(2,1)} %copy-done.3, ...), custom_call_target="tpu_custom_call" | custom-call | tf_op jit(solution)/shard_map/input_back/pallas_call | solution.py:335
  349.5 2.8 copy.123
  358.8 1.5 reshape.193
  360.3 1.5 copy.103
  365.5 2.4 add_convert_fusion.2
  369.0 8.8 %collective-permute-done.57 = bf16[256,768]{0,1:T(8,128)(2,1)S(1)} collective-permute-done((bf16[256,768]{0,1:T(8,128)(2,1)S(1)}, bf16[256,768]{0,1:T(8,128)(2,1)S(1)}, u32[]{:S(2)}, u32[]{:S(2)}) %collective-permute-start.57) | collective-permute-done | bytes 393248 | tf_op jit(solution)/shard_map/ppermute | solution.py:76
  379.1 1.9 broadcast_select_fusion.3
  381.0 1.5 pad_maximum_fusion
  383.6 1.5 collective-permute-start.61
  385.1 4.3 collective-permute-start.60
  389.5 2.2 collective-permute-done.63
  395.1 20.2 %collective-permute-done.62 = bf16[128,5120]{1,0:T(8,128)(2,1)} collective-permute-done((bf16[128,5120]{1,0:T(8,128)(2,1)}, bf16[128,5120]{1,0:T(8,128)(2,1)}, u32[]{:S(2)}, u32[]{:S(2)}) %collective-permute-start.62) | collective-permute-done | bytes 1310752 | tf_op jit(solution)/shard_map/ppermute | solution.py:76
  415.3 2.8 collective-permute-done.61
  418.0 3.7 add_convert_fusion.1
  421.8 3.8 collective-permute-start.65
  426.1 9.5 %collective-permute-start.68 = (bf16[128,4096]{1,0:T(8,128)(2,1)}, bf16[128,4096]{1,0:T(8,128)(2,1)}, u32[]{:S(2)}, u32[]{:S(2)}) collective-permute-start(bf16[128,4096]{1,0:T(8,128)(2,1)} %pad_maximum_fusion.7), channel_id=1, source_target_pairs={{0,0},{1,16},{16,1},{17,17},{2,2},{3,18},{18,3},{19,19},{4,4},{5,2... | collective-permute-start | bytes 3145736 | tf_op jit(solution)/shard_map/ppermute | solution.py:37
  435.6 1.7 select_bitcast_fusion
  440.5 22.5 %collective-permute-done.66 = bf16[128,640]{0,1:T(8,128)(2,1)S(1)} collective-permute-done((bf16[128,640]{0,1:T(8,128)(2,1)}, bf16[128,640]{0,1:T(8,128)(2,1)S(1)}, u32[]{:S(2)}, u32[]{:S(2)}) %collective-permute-start.66) | collective-permute-done | bytes 163872 | tf_op jit(solution)/shard_map/ppermute | solution.py:76
  465.6 2.3 add_convert_fusion
  471.2 1.6 collective-permute-start.73
  472.8 2.1 slice_convert_fusion
  474.8 1.4 fusion.66
  480.1 22.7 %collective-permute-done.74 = bf16[128,1024]{1,0:T(8,128)(2,1)} collective-permute-done((bf16[128,1024]{1,0:T(8,128)(2,1)}, bf16[128,1024]{1,0:T(8,128)(2,1)}, u32[]{:S(2)}, u32[]{:S(2)}) %collective-permute-start.74) | collective-permute-done | bytes 262176 | tf_op jit(solution)/shard_map/ppermute | solution.py:76
  504.8 1.6 convert_add_fusion
  506.6 1.7 reshape.194
  508.3 1.7 reshape.195
  (419 shorter events, 98.8 us)
Async XLA Ops:
  8.7 24.1 %collective-permute-start.2 = (bf16[128,1536]{1,0:T(8,128)(2,1)}, bf16[128,1536]{1,0:T(8,128)(2,1)S(1)}, u32[]{:S(2)}, u32[]{:S(2)}) collective-permute-start(bf16[128,1536]{1,0:T(8,128)(2,1)} %get-tuple-element.311), channel_id=1, source_target_pairs={{0,4},{2,6},{4,8},{6,10},{8,12},{10,14},{12,0},{14,2},{1,5},{3,7},... | collective-permute-start | bytes 1179656 | tf_op jit(solution)/shard_map/ppermute | solution.py:76
  11.7 16.9 %collective-permute-start.3 = (bf16[128,1536]{1,0:T(8,128)(2,1)}, bf16[128,1536]{1,0:T(8,128)(2,1)}, u32[]{:S(2)}, u32[]{:S(2)}) collective-permute-start(bf16[128,1536]{1,0:T(8,128)(2,1)} %get-tuple-element.311), channel_id=1, source_target_pairs={{0,2},{2,0},{4,6},{6,4},{8,10},{10,8},{12,14},{14,12},{1,3},{3,1},... | collective-permute-start | bytes 1179656 | tf_op jit(solution)/shard_map/ppermute | solution.py:73
  13.2 17.1 %collective-permute-start = (bf16[128,2048]{1,0:T(8,128)(2,1)}, bf16[128,2048]{1,0:T(8,128)(2,1)}, u32[]{:S(2)}, u32[]{:S(2)}) collective-permute-start(bf16[128,2048]{1,0:T(8,128)(2,1)} %bitcast.70), channel_id=1, source_target_pairs={{0,0},{1,16},{16,1},{17,17},{2,2},{3,18},{18,3},{19,19},{4,4},{5,2... | collective-permute-start | bytes 1572872 | tf_op jit(solution)/shard_map/ppermute | solution.py:37
  18.6 13.1 %collective-permute-start.1 = (bf16[128,2048]{1,0:T(8,128)(2,1)}, bf16[128,2048]{1,0:T(8,128)(2,1)}, u32[]{:S(2)}, u32[]{:S(2)}) collective-permute-start(bf16[128,2048]{1,0:T(8,128)(2,1)} %bitcast.73), channel_id=1, source_target_pairs={{0,0},{1,16},{16,1},{17,17},{2,2},{3,18},{18,3},{19,19},{4,4},{5,2... | collective-permute-start | bytes 1572872 | tf_op jit(solution)/shard_map/ppermute | solution.py:37
  28.1 10.6 %collective-permute-start.10 = (bf16[16,32,1024]{2,0,1:T(8,128)(2,1)S(1)}, bf16[16,32,1024]{2,0,1:T(8,128)(2,1)S(1)}, u32[]{:S(2)}, u32[]{:S(2)}) collective-permute-start(bf16[16,32,1024]{2,0,1:T(8,128)(2,1)S(1)} %bitcast.127), channel_id=1, source_target_pairs={{0,16},{16,0},{1,17},{17,1},{2,18},{18,2},{3,19},{19,3},{4,20},{20... | collective-permute-start | bytes 3145736 | tf_op jit(solution)/shard_map/ppermute | solution.py:29
  28.7 4.2 collective-permute-start.4
  32.9 38.8 %collective-permute-start.6 = (bf16[256,1024]{1,0:T(8,128)(2,1)S(1)}, bf16[256,1024]{1,0:T(8,128)(2,1)S(1)}, u32[]{:S(2)}, u32[]{:S(2)}) collective-permute-start(bf16[256,1024]{1,0:T(8,128)(2,1)S(1)} %pad.23.refs_16_), channel_id=1, source_target_pairs={{0,1},{1,0},{2,3},{3,2},{4,5},{5,4},{6,7},{7,6},{8,9},{9,8},{10,11... | collective-permute-start | bytes 1572872 | tf_op jit(solution)/shard_map/ppermute | solution.py:33
  36.5 35.1 %collective-permute-start.5 = (f32[5,256]{1,0:T(8,128)S(1)}, f32[5,256]{1,0:T(8,128)S(1)}, u32[]{:S(2)}, u32[]{:S(2)}) collective-permute-start(f32[5,256]{1,0:T(8,128)S(1)} %stack.85), channel_id=1, source_target_pairs={{0,1},{1,0},{2,3},{3,2},{4,5},{5,4},{6,7},{7,6},{8,9},{9,8},{10,11... | collective-permute-start | bytes 15368 | tf_op jit(solution)/shard_map/ppermute | solution.py:33
  36.6 35.4 %collective-permute-start.7 = (bf16[128,5632]{1,0:T(8,128)(2,1)S(1)}, bf16[128,5632]{1,0:T(8,128)(2,1)S(1)}, u32[]{:S(2)}, u32[]{:S(2)}) collective-permute-start(bf16[128,5632]{1,0:T(8,128)(2,1)S(1)} %constant_dynamic-update-slice_fusion.4.refs_0_.refs_16_), channel_id=1, source_target_pairs={{0,4},{2,6},{4,8},{6,10},{8,12},{10,14},{12,0},{14,2},{1,5},{3,7},... | collective-permute-start | bytes 4325384 | tf_op jit(solution)/shard_map/ppermute | solution.py:76
  38.2 33.4 %collective-permute-start.8 = (bf16[128,5632]{1,0:T(8,128)(2,1)S(1)}, bf16[128,5632]{1,0:T(8,128)(2,1)S(1)}, u32[]{:S(2)}, u32[]{:S(2)}) collective-permute-start(bf16[128,5632]{1,0:T(8,128)(2,1)S(1)} %constant_dynamic-update-slice_fusion.4.refs_0_.refs_16_), channel_id=1, source_target_pairs={{0,2},{2,0},{4,6},{6,4},{8,10},{10,8},{12,14},{14,12},{1,3},{3,1},... | collective-permute-start | bytes 4325384 | tf_op jit(solution)/shard_map/ppermute | solution.py:73
  38.7 33.0 %collective-permute-start.9 = (bf16[128,3072]{1,0:T(8,128)(2,1)S(1)}, bf16[128,3072]{1,0:T(8,128)(2,1)S(1)}, u32[]{:S(2)}, u32[]{:S(2)}) collective-permute-start(bf16[128,3072]{1,0:T(8,128)(2,1)S(1)} %constant_dynamic-update-slice_fusion.7.refs_0_), channel_id=1, source_target_pairs={{0,1},{1,0},{2,3},{3,2},{4,5},{5,4},{6,7},{7,6},{8,9},{9,8},{10,11... | collective-permute-start | bytes 2359304 | tf_op jit(solution)/shard_map/ppermute | solution.py:33
  74.4 32.9 %collective-permute-start.13 = (bf16[128,5632]{1,0:T(8,128)(2,1)S(1)}, bf16[128,5632]{1,0:T(8,128)(2,1)S(1)}, u32[]{:S(2)}, u32[]{:S(2)}) collective-permute-start(bf16[128,5632]{1,0:T(8,128)(2,1)S(1)} %collective-permute-done.7.refs_2_.refs_18_), channel_id=1, source_target_pairs={{0,2},{2,0},{4,6},{6,4},{8,10},{10,8},{12,14},{14,12},{1,3},{3,1},... | collective-permute-start | bytes 4325384 | tf_op jit(solution)/shard_map/ppermute | solution.py:73
  75.0 34.4 %collective-permute-start.12 = (bf16[128,5632]{1,0:T(8,128)(2,1)S(1)}, bf16[128,5632]{1,0:T(8,128)(2,1)S(1)}, u32[]{:S(2)}, u32[]{:S(2)}) collective-permute-start(bf16[128,5632]{1,0:T(8,128)(2,1)S(1)} %collective-permute-done.7.refs_2_.refs_18_), channel_id=1, source_target_pairs={{0,4},{2,6},{4,8},{6,10},{8,12},{10,14},{12,0},{14,2},{1,5},{3,7},... | collective-permute-start | bytes 4325384 | tf_op jit(solution)/shard_map/ppermute | solution.py:76
  76.2 33.3 %collective-permute-start.14 = (bf16[128,3072]{1,0:T(8,128)(2,1)S(1)}, bf16[128,3072]{1,0:T(8,128)(2,1)S(1)}, u32[]{:S(2)}, u32[]{:S(2)}) collective-permute-start(bf16[128,3072]{1,0:T(8,128)(2,1)S(1)} %pad_maximum_fusion.10.refs_1_), channel_id=1, source_target_pairs={{0,1},{1,0},{2,3},{3,2},{4,5},{5,4},{6,7},{7,6},{8,9},{9,8},{10,11... | collective-permute-start | bytes 2359304 | tf_op jit(solution)/shard_map/ppermute | solution.py:33
  76.5 37.1 %collective-permute-start.27 = (bf16[128,5632]{1,0:T(8,128)(2,1)S(1)}, bf16[128,5632]{1,0:T(8,128)(2,1)S(1)}, u32[]{:S(2)}, u32[]{:S(2)}) collective-permute-start(bf16[128,5632]{1,0:T(8,128)(2,1)S(1)} %constant_dynamic-update-slice_fusion.4.refs_0_.refs_16_), channel_id=1, source_target_pairs={{0,16},{16,0},{1,17},{17,1},{2,18},{18,2},{3,19},{19,3},{4,20},{20... | collective-permute-start | bytes 4325384 | tf_op jit(solution)/shard_map/ppermute | solution.py:29
  109.5 31.8 %collective-permute-start.23 = (bf16[128,5632]{1,0:T(8,128)(2,1)S(1)}, bf16[128,5632]{1,0:T(8,128)(2,1)}, u32[]{:S(2)}, u32[]{:S(2)}) collective-permute-start(bf16[128,5632]{1,0:T(8,128)(2,1)S(1)} %collective-permute-done.12.refs_4_.refs_20_), channel_id=1, source_target_pairs={{0,2},{2,0},{4,6},{6,4},{8,10},{10,8},{12,14},{14,12},{1,3},{3,1},... | collective-permute-start | bytes 4325384 | tf_op jit(solution)/shard_map/ppermute | solution.py:73
  111.1 20.0 %collective-permute-start.19 = (bf16[128,3072]{1,0:T(8,128)(2,1)S(1)}, bf16[128,3072]{1,0:T(8,128)(2,1)S(1)}, u32[]{:S(2)}, u32[]{:S(2)}) collective-permute-start(bf16[128,3072]{1,0:T(8,128)(2,1)S(1)} %pad_maximum_fusion.11.refs_2_), channel_id=1, source_target_pairs={{0,1},{1,0},{2,3},{3,2},{4,5},{5,4},{6,7},{7,6},{8,9},{9,8},{10,11... | collective-permute-start | bytes 2359304 | tf_op jit(solution)/shard_map/ppermute | solution.py:33
  111.1 31.4 %collective-permute-start.15 = (bf16[128,4096]{1,0:T(8,128)(2,1)S(1)}, bf16[128,4096]{1,0:T(8,128)(2,1)}, u32[]{:S(2)}, u32[]{:S(2)}) collective-permute-start(bf16[128,4096]{1,0:T(8,128)(2,1)S(1)} %slice.397), channel_id=1, source_target_pairs={{0,4},{2,6},{4,8},{6,10},{8,12},{10,14},{12,0},{14,2},{1,5},{3,7},... | collective-permute-start | bytes 3145736 | tf_op jit(solution)/shard_map/ppermute | solution.py:76
  113.5 32.1 %collective-permute-start.28 = (bf16[128,5632]{1,0:T(8,128)(2,1)S(1)}, bf16[128,5632]{1,0:T(8,128)(2,1)S(1)}, u32[]{:S(2)}, u32[]{:S(2)}) collective-permute-start(bf16[128,5632]{1,0:T(8,128)(2,1)S(1)} %collective-permute-done.8.refs_1_.refs_17_), channel_id=1, source_target_pairs={{0,16},{16,0},{1,17},{17,1},{2,18},{18,2},{3,19},{19,3},{4,20},{20... | collective-permute-start | bytes 4325384 | tf_op jit(solution)/shard_map/ppermute | solution.py:29
  113.6 32.1 %collective-permute-start.29 = (bf16[128,5632]{1,0:T(8,128)(2,1)S(1)}, bf16[128,5632]{1,0:T(8,128)(2,1)S(1)}, u32[]{:S(2)}, u32[]{:S(2)}) collective-permute-start(bf16[128,5632]{1,0:T(8,128)(2,1)S(1)} %collective-permute-done.7.refs_2_.refs_18_), channel_id=1, source_target_pairs={{0,16},{16,0},{1,17},{17,1},{2,18},{18,2},{3,19},{19,3},{4,20},{20... | collective-permute-start | bytes 4325384 | tf_op jit(solution)/shard_map/ppermute | solution.py:29
  131.0 17.2 %collective-permute-start.30 = (bf16[128,5632]{1,0:T(8,128)(2,1)S(1)}, bf16[128,5632]{1,0:T(8,128)(2,1)S(1)}, u32[]{:S(2)}, u32[]{:S(2)}) collective-permute-start(bf16[128,5632]{1,0:T(8,128)(2,1)S(1)} %collective-permute-done.13.refs_3_.refs_19_), channel_id=1, source_target_pairs={{0,16},{16,0},{1,17},{17,1},{2,18},{18,2},{3,19},{19,3},{4,20},{20... | collective-permute-start | bytes 4325384 | tf_op jit(solution)/shard_map/ppermute | solution.py:29
  142.5 3.7 collective-permute-start.22
  144.1 25.5 %collective-permute-start.26 = (bf16[128,4096]{1,0:T(8,128)(2,1)}, bf16[128,4096]{1,0:T(8,128)(2,1)}, u32[]{:S(2)}, u32[]{:S(2)}) collective-permute-start(bf16[128,4096]{1,0:T(8,128)(2,1)} %collective-permute-done.15.refs_6_.refs_22_), channel_id=1, source_target_pairs={{0,2},{2,0},{4,6},{6,4},{8,10},{10,8},{12,14},{14,12},{1,3},{3,1},... | collective-permute-start | bytes 3145736 | tf_op jit(solution)/shard_map/ppermute | solution.py:73
  147.8 21.7 %collective-permute-start.24 = (bf16[128,3072]{1,0:T(8,128)(2,1)}, bf16[128,3072]{1,0:T(8,128)(2,1)}, u32[]{:S(2)}, u32[]{:S(2)}) collective-permute-start(bf16[128,3072]{1,0:T(8,128)(2,1)} %pad_maximum_fusion.12.refs_3_), channel_id=1, source_target_pairs={{0,16},{16,0},{1,17},{17,1},{2,18},{18,2},{3,19},{19,3},{4,20},{20... | collective-permute-start | bytes 2359304 | tf_op jit(solution)/shard_map/ppermute | solution.py:29
  148.2 22.7 %collective-permute-start.31 = (bf16[128,5632]{1,0:T(8,128)(2,1)S(1)}, bf16[128,5632]{1,0:T(8,128)(2,1)}, u32[]{:S(2)}, u32[]{:S(2)}) collective-permute-start(bf16[128,5632]{1,0:T(8,128)(2,1)S(1)} %collective-permute-done.12.refs_4_.refs_20_), channel_id=1, source_target_pairs={{0,16},{16,0},{1,17},{17,1},{2,18},{18,2},{3,19},{19,3},{4,20},{20... | collective-permute-start | bytes 4325384 | tf_op jit(solution)/shard_map/ppermute | solution.py:29
  148.4 23.1 %collective-permute-start.32 = (bf16[128,5632]{1,0:T(8,128)(2,1)}, bf16[128,5632]{1,0:T(8,128)(2,1)}, u32[]{:S(2)}, u32[]{:S(2)}) collective-permute-start(bf16[128,5632]{1,0:T(8,128)(2,1)} %collective-permute-done.23.refs_5_.refs_21_), channel_id=1, source_target_pairs={{0,16},{16,0},{1,17},{17,1},{2,18},{18,2},{3,19},{19,3},{4,20},{20... | collective-permute-start | bytes 4325384 | tf_op jit(solution)/shard_map/ppermute | solution.py:29
  149.6 21.8 %collective-permute-start.33 = (bf16[128,4096]{1,0:T(8,128)(2,1)}, bf16[128,4096]{1,0:T(8,128)(2,1)}, u32[]{:S(2)}, u32[]{:S(2)}) collective-permute-start(bf16[128,4096]{1,0:T(8,128)(2,1)} %collective-permute-done.15.refs_6_.refs_22_), channel_id=1, source_target_pairs={{0,16},{16,0},{1,17},{17,1},{2,18},{18,2},{3,19},{19,3},{4,20},{20... | collective-permute-start | bytes 3145736 | tf_op jit(solution)/shard_map/ppermute | solution.py:29
  169.5 33.7 %collective-permute-start.36 = (bf16[128,3072]{1,0:T(8,128)(2,1)}, bf16[128,3072]{1,0:T(8,128)(2,1)}, u32[]{:S(2)}, u32[]{:S(2)}) collective-permute-start(bf16[128,3072]{1,0:T(8,128)(2,1)} %pad_maximum_fusion.12.refs_3_), channel_id=1, source_target_pairs={{0,1},{1,0},{2,3},{3,2},{4,5},{5,4},{6,7},{7,6},{8,9},{9,8},{10,11... | collective-permute-start | bytes 2359304 | tf_op jit(solution)/shard_map/ppermute | solution.py:33
  170.9 43.2 %collective-permute-start.37 = (bf16[128,3072]{1,0:T(8,128)(2,1)}, bf16[128,3072]{1,0:T(8,128)(2,1)S(1)}, u32[]{:S(2)}, u32[]{:S(2)}) collective-permute-start(bf16[128,3072]{1,0:T(8,128)(2,1)} %copy-done.28), channel_id=1, source_target_pairs={{0,16},{16,0},{1,17},{17,1},{2,18},{18,2},{3,19},{19,3},{4,20},{20... | collective-permute-start | bytes 2359304 | tf_op jit(solution)/shard_map/ppermute | solution.py:29
  171.4 42.7 %collective-permute-start.38 = (bf16[128,3072]{1,0:T(8,128)(2,1)}, bf16[128,3072]{1,0:T(8,128)(2,1)}, u32[]{:S(2)}, u32[]{:S(2)}) collective-permute-start(bf16[128,3072]{1,0:T(8,128)(2,1)} %copy-done.29), channel_id=1, source_target_pairs={{0,16},{16,0},{1,17},{17,1},{2,18},{18,2},{3,19},{19,3},{4,20},{20... | collective-permute-start | bytes 2359304 | tf_op jit(solution)/shard_map/ppermute | solution.py:29
  171.5 42.7 %collective-permute-start.39 = (bf16[128,3072]{1,0:T(8,128)(2,1)}, bf16[128,3072]{1,0:T(8,128)(2,1)}, u32[]{:S(2)}, u32[]{:S(2)}) collective-permute-start(bf16[128,3072]{1,0:T(8,128)(2,1)} %copy-done.30), channel_id=1, source_target_pairs={{0,16},{16,0},{1,17},{17,1},{2,18},{18,2},{3,19},{19,3},{4,20},{20... | collective-permute-start | bytes 2359304 | tf_op jit(solution)/shard_map/ppermute | solution.py:29
  203.2 11.0 %collective-permute-start.40 = (bf16[128,3072]{1,0:T(8,128)(2,1)}, bf16[128,3072]{1,0:T(8,128)(2,1)S(1)}, u32[]{:S(2)}, u32[]{:S(2)}) collective-permute-start(bf16[128,3072]{1,0:T(8,128)(2,1)} %collective-permute-done.36.refs_7_), channel_id=1, source_target_pairs={{0,16},{16,0},{1,17},{17,1},{2,18},{18,2},{3,19},{19,3},{4,20},{20... | collective-permute-start | bytes 2359304 | tf_op jit(solution)/shard_map/ppermute | solution.py:29
  203.4 8.9 %collective-permute-start.35 = (bf16[128,1024]{1,0:T(8,128)(2,1)}, bf16[128,1024]{1,0:T(8,128)(2,1)S(1)}, u32[]{:S(2)}, u32[]{:S(2)}) collective-permute-start(bf16[128,1024]{1,0:T(8,128)(2,1)} %bitcast.136), channel_id=1, source_target_pairs={{0,1},{1,0},{2,3},{3,2},{4,5},{5,4},{6,7},{7,6},{8,9},{9,8},{10,11... | collective-permute-start | bytes 786440 | tf_op jit(solution)/shard_map/ppermute | solution.py:33
  212.2 47.4 %collective-permute-start.45 = (bf16[256,1024]{1,0:T(8,128)(2,1)}, bf16[256,1024]{1,0:T(8,128)(2,1)}, u32[]{:S(2)}, u32[]{:S(2)}) collective-permute-start(bf16[256,1024]{1,0:T(8,128)(2,1)} %bitcast.158), channel_id=1, source_target_pairs={{0,16},{16,0},{1,17},{17,1},{2,18},{18,2},{3,19},{19,3},{4,20},{20... | collective-permute-start | bytes 1572872 | tf_op jit(solution)/shard_map/ppermute | solution.py:29
  250.2 6.0 %collective-permute-start.43 = (f32[1024]{0:T(1024)S(1)}, f32[1024]{0:T(1024)S(1)}, u32[]{:S(2)}, u32[]{:S(2)}) collective-permute-start(f32[1024]{0:T(1024)S(1)} %bitcast.144), channel_id=1, source_target_pairs={{0,16},{16,0},{1,17},{17,1},{2,18},{18,2},{3,19},{19,3},{4,20},{20... | collective-permute-start | bytes 12296 | tf_op jit(solution)/shard_map/ppermute | solution.py:29
  251.4 4.8 collective-permute-start.42
  255.2 8.5 %collective-permute-start.44 = (bf16[128,1024]{1,0:T(8,128)(2,1)}, bf16[128,1024]{1,0:T(8,128)(2,1)S(1)}, u32[]{:S(2)}, u32[]{:S(2)}) collective-permute-start(bf16[128,1024]{1,0:T(8,128)(2,1)} %get-tuple-element.106), channel_id=1, source_target_pairs={{0,1},{1,0},{2,3},{3,2},{4,5},{5,4},{6,7},{7,6},{8,9},{9,8},{10,11... | collective-permute-start | bytes 786440 | tf_op jit(solution)/shard_map/ppermute | solution.py:33
  256.2 7.4 %collective-permute-start.46 = (bf16[2,128,1024]{2,1,0:T(8,128)(2,1)}, bf16[2,128,1024]{2,1,0:T(8,128)(2,1)}, u32[]{:S(2)}, u32[]{:S(2)}) collective-permute-start(bf16[2,128,1024]{2,1,0:T(8,128)(2,1)} %pad_maximum_fusion.14), channel_id=1, source_target_pairs={{0,16},{16,0},{1,17},{17,1},{2,18},{18,2},{3,19},{19,3},{4,20},{20... | collective-permute-start | bytes 1572872 | tf_op jit(solution)/shard_map/ppermute | solution.py:29
  263.7 36.7 %collective-permute-start.47 = (bf16[2,128,1536]{2,1,0:T(8,128)(2,1)}, bf16[2,128,1536]{2,1,0:T(8,128)(2,1)}, u32[]{:S(2)}, u32[]{:S(2)}) collective-permute-start(bf16[2,128,1536]{2,1,0:T(8,128)(2,1)} %pad_maximum_fusion.13), channel_id=1, source_target_pairs={{0,1},{1,0},{2,3},{3,2},{4,5},{5,4},{6,7},{7,6},{8,9},{9,8},{10,11... | collective-permute-start | bytes 2359304 | tf_op jit(solution)/shard_map/ppermute | solution.py:33
  264.8 36.9 %collective-permute-start.48 = (bf16[3,128,1152]{2,1,0:T(8,128)(2,1)}, bf16[3,128,1152]{2,1,0:T(8,128)(2,1)}, u32[]{:S(2)}, u32[]{:S(2)}) collective-permute-start(bf16[3,128,1152]{2,1,0:T(8,128)(2,1)} %pad_maximum_fusion.9), channel_id=1, source_target_pairs={{0,1},{1,0},{2,3},{3,2},{4,5},{5,4},{6,7},{7,6},{8,9},{9,8},{10,11... | collective-permute-start | bytes 2654216 | tf_op jit(solution)/shard_map/ppermute | solution.py:33
  307.1 17.2 %collective-permute-start.50 = (bf16[6,128,1024]{2,1,0:T(8,128)(2,1)}, bf16[6,128,1024]{2,1,0:T(8,128)(2,1)}, u32[]{:S(2)}, u32[]{:S(2)}) collective-permute-start(bf16[6,128,1024]{2,1,0:T(8,128)(2,1)} %pad_maximum_fusion.1), channel_id=1, source_target_pairs={{0,16},{16,0},{1,17},{17,1},{2,18},{18,2},{3,19},{19,3},{4,20},{20... | collective-permute-start | bytes 4718600 | tf_op jit(solution)/shard_map/ppermute | solution.py:29
  318.1 35.4 %collective-permute-start.52 = (bf16[128,2048]{1,0:T(8,128)(2,1)}, bf16[128,2048]{1,0:T(8,128)(2,1)}, u32[]{:S(2)}, u32[]{:S(2)}) collective-permute-start(bf16[128,2048]{1,0:T(8,128)(2,1)} %get-tuple-element.226), channel_id=1, source_target_pairs={{0,2},{2,0},{4,6},{6,4},{8,10},{10,8},{12,14},{14,12},{1,3},{3,1},... | collective-permute-start | bytes 1572872 | tf_op jit(solution)/shard_map/ppermute | solution.py:73
  321.1 34.7 %collective-permute-start.53 = (bf16[128,2048]{1,0:T(8,128)(2,1)}, bf16[128,2048]{1,0:T(8,128)(2,1)}, u32[]{:S(2)}, u32[]{:S(2)}) collective-permute-start(bf16[128,2048]{1,0:T(8,128)(2,1)} %get-tuple-element.234), channel_id=1, source_target_pairs={{0,2},{2,0},{4,6},{6,4},{8,10},{10,8},{12,14},{14,12},{1,3},{3,1},... | collective-permute-start | bytes 1572872 | tf_op jit(solution)/shard_map/ppermute | solution.py:73
  333.5 29.2 %collective-permute-start.54 = (bf16[128,1024]{1,0:T(8,128)(2,1)}, bf16[128,1024]{1,0:T(8,128)(2,1)}, u32[]{:S(2)}, u32[]{:S(2)}) collective-permute-start(bf16[128,1024]{1,0:T(8,128)(2,1)} %pad_maximum_fusion.17), channel_id=1, source_target_pairs={{0,2},{2,0},{4,6},{6,4},{8,10},{10,8},{12,14},{14,12},{1,3},{3,1},... | collective-permute-start | bytes 786440 | tf_op jit(solution)/shard_map/ppermute | solution.py:73
  335.8 27.8 %collective-permute-start.56 = (bf16[256,768]{0,1:T(8,128)(2,1)}, bf16[256,768]{0,1:T(8,128)(2,1)}, u32[]{:S(2)}, u32[]{:S(2)}) collective-permute-start(bf16[256,768]{0,1:T(8,128)(2,1)} %pad_maximum_fusion.16), channel_id=1, source_target_pairs={{0,4},{2,6},{4,8},{6,10},{8,12},{10,14},{12,0},{14,2},{1,5},{3,7},... | collective-permute-start | bytes 1179656 | tf_op jit(solution)/shard_map/ppermute | solution.py:76
  336.6 28.4 %collective-permute-start.55 = (bf16[256,768]{0,1:T(8,128)(2,1)}, bf16[256,768]{0,1:T(8,128)(2,1)}, u32[]{:S(2)}, u32[]{:S(2)}) collective-permute-start(bf16[256,768]{0,1:T(8,128)(2,1)} %pad_maximum_fusion.15), channel_id=1, source_target_pairs={{4,0},{6,2},{8,4},{10,6},{12,8},{14,10},{0,12},{2,14},{5,1},{7,3},... | collective-permute-start | bytes 1179656 | tf_op jit(solution)/shard_map/ppermute | solution.py:79
  353.5 25.6 %collective-permute-start.51 = (f32[16,16,1024]{2,1,0:T(8,128)}, f32[16,16,1024]{2,1,0:T(8,128)}, u32[]{:S(2)}, u32[]{:S(2)}) collective-permute-start(f32[16,16,1024]{2,1,0:T(8,128)} %bitcast.109), channel_id=1, source_target_pairs={{0,16},{16,0},{1,17},{17,1},{2,18},{18,2},{3,19},{19,3},{4,20},{20... | collective-permute-start | bytes 3145736 | tf_op jit(solution)/shard_map/ppermute | solution.py:29
  364.9 12.9 %collective-permute-start.57 = (bf16[256,768]{0,1:T(8,128)(2,1)S(1)}, bf16[256,768]{0,1:T(8,128)(2,1)S(1)}, u32[]{:S(2)}, u32[]{:S(2)}) collective-permute-start(bf16[256,768]{0,1:T(8,128)(2,1)S(1)} %add_convert_fusion.3), channel_id=1, source_target_pairs={{0,4},{2,6},{4,8},{6,10},{8,12},{10,14},{12,0},{14,2},{1,5},{3,7},... | collective-permute-start | bytes 1179656 | tf_op jit(solution)/shard_map/ppermute | solution.py:76
  365.0 4.0 collective-permute-start.59
  382.5 9.2 %collective-permute-start.63 = (bf16[128,1024]{0,1:T(8,128)(2,1)S(1)}, bf16[128,1024]{0,1:T(8,128)(2,1)S(1)}, u32[]{:S(2)}, u32[]{:S(2)}) collective-permute-start(bf16[128,1024]{0,1:T(8,128)(2,1)S(1)} %pad_maximum_fusion.18), channel_id=1, source_target_pairs={{0,2},{2,0},{4,6},{6,4},{8,10},{10,8},{12,14},{14,12},{1,3},{3,1},... | collective-permute-start | bytes 786440 | tf_op jit(solution)/shard_map/ppermute | solution.py:73
  383.6 31.7 %collective-permute-start.62 = (bf16[128,5120]{1,0:T(8,128)(2,1)}, bf16[128,5120]{1,0:T(8,128)(2,1)}, u32[]{:S(2)}, u32[]{:S(2)}) collective-permute-start(bf16[128,5120]{1,0:T(8,128)(2,1)} %add_convert_fusion.2), channel_id=1, source_target_pairs={{0,4},{2,6},{4,8},{6,10},{8,12},{10,14},{12,0},{14,2},{1,5},{3,7},... | collective-permute-start | bytes 3932168 | tf_op jit(solution)/shard_map/ppermute | solution.py:76
  383.6 34.4 %collective-permute-start.61 = (bf16[128,5120]{1,0:T(8,128)(2,1)}, bf16[128,5120]{1,0:T(8,128)(2,1)}, u32[]{:S(2)}, u32[]{:S(2)}) collective-permute-start(bf16[128,5120]{1,0:T(8,128)(2,1)} %pad_maximum_fusion.3), channel_id=1, source_target_pairs={{0,2},{2,0},{4,6},{6,4},{8,10},{10,8},{12,14},{14,12},{1,3},{3,1},... | collective-permute-start | bytes 3932168 | tf_op jit(solution)/shard_map/ppermute | solution.py:73
  385.1 36.6 %collective-permute-start.60 = (f32[32,16,1024]{2,1,0:T(8,128)}, f32[32,16,1024]{2,1,0:T(8,128)}, u32[]{:S(2)}, u32[]{:S(2)}) collective-permute-start(f32[32,16,1024]{2,1,0:T(8,128)} %pad_maximum_fusion), channel_id=1, source_target_pairs={{0,1},{17,16},{2,3},{19,18},{4,5},{21,20},{6,7},{23,22},{8,9},{25,... | collective-permute-start | bytes 6291464 | tf_op jit(solution)/shard_map/ppermute | solution.py:879
  421.8 15.6 %collective-permute-start.64 = (bf16[128,640]{0,1:T(8,128)(2,1)S(1)}, bf16[128,640]{0,1:T(8,128)(2,1)S(1)}, u32[]{:S(2)}, u32[]{:S(2)}) collective-permute-start(bf16[128,640]{0,1:T(8,128)(2,1)S(1)} %pad_maximum_fusion.21), channel_id=1, source_target_pairs={{0,4},{2,6},{4,8},{6,10},{8,12},{10,14},{12,0},{14,2},{1,5},{3,7},... | collective-permute-start | bytes 491528 | tf_op jit(solution)/shard_map/ppermute | solution.py:76
  421.8 17.1 %collective-permute-start.65 = (bf16[128,640]{0,1:T(8,128)(2,1)S(1)}, bf16[128,640]{0,1:T(8,128)(2,1)}, u32[]{:S(2)}, u32[]{:S(2)}) collective-permute-start(bf16[128,640]{0,1:T(8,128)(2,1)S(1)} %pad_maximum_fusion.21), channel_id=1, source_target_pairs={{4,0},{6,2},{8,4},{10,6},{12,8},{14,10},{0,12},{2,14},{5,1},{7,3},... | collective-permute-start | bytes 491528 | tf_op jit(solution)/shard_map/ppermute | solution.py:79
  425.6 40.0 %collective-permute-start.70 = (bf16[128,5120]{1,0:T(8,128)(2,1)}, bf16[128,5120]{1,0:T(8,128)(2,1)}, u32[]{:S(2)}, u32[]{:S(2)}) collective-permute-start(bf16[128,5120]{1,0:T(8,128)(2,1)} %add_convert_fusion.1), channel_id=1, source_target_pairs={{0,4},{2,6},{4,8},{6,10},{8,12},{10,14},{12,0},{14,2},{1,5},{3,7},... | collective-permute-start | bytes 3932168 | tf_op jit(solution)/shard_map/ppermute | solution.py:76
  425.6 40.0 %collective-permute-start.69 = (bf16[128,5120]{1,0:T(8,128)(2,1)}, bf16[128,5120]{1,0:T(8,128)(2,1)}, u32[]{:S(2)}, u32[]{:S(2)}) collective-permute-start(bf16[128,5120]{1,0:T(8,128)(2,1)} %pad_maximum_fusion.4), channel_id=1, source_target_pairs={{0,2},{2,0},{4,6},{6,4},{8,10},{10,8},{12,14},{14,12},{1,3},{3,1},... | collective-permute-start | bytes 3932168 | tf_op jit(solution)/shard_map/ppermute | solution.py:73
  426.1 43.6 %collective-permute-start.68 = (bf16[128,4096]{1,0:T(8,128)(2,1)}, bf16[128,4096]{1,0:T(8,128)(2,1)}, u32[]{:S(2)}, u32[]{:S(2)}) collective-permute-start(bf16[128,4096]{1,0:T(8,128)(2,1)} %pad_maximum_fusion.7), channel_id=1, source_target_pairs={{0,0},{1,16},{16,1},{17,17},{2,2},{3,18},{18,3},{19,19},{4,4},{5,2... | collective-permute-start | bytes 3145736 | tf_op jit(solution)/shard_map/ppermute | solution.py:37
  438.1 24.9 %collective-permute-start.66 = (bf16[128,640]{0,1:T(8,128)(2,1)}, bf16[128,640]{0,1:T(8,128)(2,1)S(1)}, u32[]{:S(2)}, u32[]{:S(2)}) collective-permute-start(bf16[128,640]{0,1:T(8,128)(2,1)} %copy-done.57), channel_id=1, source_target_pairs={{0,4},{2,6},{4,8},{6,10},{8,12},{10,14},{12,0},{14,2},{1,5},{3,7},... | collective-permute-start | bytes 491528 | tf_op jit(solution)/shard_map/ppermute | solution.py:76
  464.1 13.4 %collective-permute-start.67 = (f32[3072]{0:T(1024)S(1)}, f32[3072]{0:T(1024)}, u32[]{:S(2)}, u32[]{:S(2)}) collective-permute-start(f32[3072]{0:T(1024)S(1)} %slice.433), channel_id=1, source_target_pairs={{0,0},{1,16},{16,1},{17,17},{2,2},{3,18},{18,3},{19,19},{4,4},{5,2... | collective-permute-start | bytes 36872 | tf_op jit(solution)/shard_map/ppermute | solution.py:37
  469.7 35.1 %collective-permute-start.72 = (bf16[128,4096]{1,0:T(8,128)(2,1)}, bf16[128,4096]{1,0:T(8,128)(2,1)S(1)}, u32[]{:S(2)}, u32[]{:S(2)}) collective-permute-start(bf16[128,4096]{1,0:T(8,128)(2,1)} %slice.435), channel_id=1, source_target_pairs={{0,4},{1,20},{16,5},{17,21},{2,6},{3,22},{18,7},{19,23},{4,8},{5,2... | collective-permute-start | bytes 3145736 | tf_op jit(solution)/shard_map/ppermute | solution.py:926
  469.7 35.1 %collective-permute-start.71 = (bf16[128,4096]{1,0:T(8,128)(2,1)S(1)}, bf16[128,4096]{1,0:T(8,128)(2,1)S(1)}, u32[]{:S(2)}, u32[]{:S(2)}) collective-permute-start(bf16[128,4096]{1,0:T(8,128)(2,1)S(1)} %copy-done.26), channel_id=1, source_target_pairs={{0,2},{1,18},{16,3},{17,19},{2,0},{3,16},{18,1},{19,17},{4,6},{5,2... | collective-permute-start | bytes 3145736 | tf_op jit(solution)/shard_map/ppermute | solution.py:926
  470.9 32.0 %collective-permute-start.74 = (bf16[128,1024]{1,0:T(8,128)(2,1)}, bf16[128,1024]{1,0:T(8,128)(2,1)}, u32[]{:S(2)}, u32[]{:S(2)}) collective-permute-start(bf16[128,1024]{1,0:T(8,128)(2,1)} %slice.436), channel_id=1, source_target_pairs={{0,4},{2,6},{4,8},{6,10},{8,12},{10,14},{12,0},{14,2},{1,5},{3,7},... | collective-permute-start | bytes 786440 | tf_op jit(solution)/shard_map/ppermute | solution.py:76
  471.2 31.7 %collective-permute-start.73 = (bf16[128,1024]{1,0:T(8,128)(2,1)}, bf16[128,1024]{1,0:T(8,128)(2,1)}, u32[]{:S(2)}, u32[]{:S(2)}) collective-permute-start(bf16[128,1024]{1,0:T(8,128)(2,1)} %pad_maximum_fusion.19), channel_id=1, source_target_pairs={{0,2},{2,0},{4,6},{6,4},{8,10},{10,8},{12,14},{14,12},{1,3},{3,1},... | collective-permute-start | bytes 786440 | tf_op jit(solution)/shard_map/ppermute | solution.py:73
  (87 other events, 1272.4 us)

commit v5 on v4

--- a/solution.py
+++ b/solution.py
@@ -80,9 +80,6 @@
 
     def back(self, k):
         return lax.rem(self.z - k + self.outer, self.outer)
-
-    def part(self, group, block, rows):
-        return jnp.concatenate([cut(a, block, rows) for a in group], axis=1)
 
 
 def halves(array, height):
@@ -303,7 +300,7 @@
     )(places, kept, taken, gates, cells, *w_own, *w_other)
 
 
-def input_kernel(count, places, inputs, gain, dz, dz_given, *refs):
+def input_kernel(count, places, inputs, gain, dz, *refs):
     in_own, in_other = refs[:count], refs[count : 2 * count]
     grad_inputs, grad_gain, wi, sems = refs[2 * count :]
     s = places[0]
@@ -319,7 +316,7 @@
     wide_half = wi.shape[1] // 2
     own = pl.ds(pl.multiple_of(s * wide_half, wide_half), wide_half)
     other = pl.ds(pl.multiple_of((1 - s) * wide_half, wide_half), wide_half)
-    grad = dot_nt(dz[...], wi[:, own]) + dot_nt(dz_given[...], wi[:, other])
+    grad = dot_nt(dz[0], wi[:, own]) + dot_nt(dz[1], wi[:, other])
     grad_gain[...] = jnp.sum(grad * shape, axis=0, keepdims=True)
     pulled = grad * gain[...]
     grad_inputs[...] = scale * (
@@ -329,7 +326,7 @@
     )
 
 
-def run_input(places, inputs, gain, dz, dz_given, in_own, in_other):
+def run_input(places, inputs, gain, dz, in_own, in_other):
     count = len(in_own)
     rows, width = inputs.shape
     return pl.pallas_call(
@@ -338,15 +335,15 @@
             jax.ShapeDtypeStruct((rows, width), wide),
             jax.ShapeDtypeStruct((1, width), wide),
         ),
-        in_specs=[in_smem] + [in_vmem] * 4 + [in_place] * (2 * count),
+        in_specs=[in_smem] + [in_vmem] * 3 + [in_place] * (2 * count),
         out_specs=[in_vmem] * 2,
         scratch_shapes=[
-            pltpu.VMEM((width, 2 * dz.shape[1]), low),
+            pltpu.VMEM((width, 2 * dz.shape[2]), low),
             pltpu.SemaphoreType.DMA((2 * count,)),
         ],
         compiler_params=pltpu.CompilerParams(vmem_limit_bytes=56 << 20),
         name="input_back",
-    )(places, inputs, gain, dz, dz_given, *in_own, *in_other)
+    )(places, inputs, gain, dz, *in_own, *in_other)
 
 
 def dot_nt(a, b):
@@ -362,8 +359,8 @@
 ):
     small, vocab = refs[: 4 * count], refs[4 * count : 4 * count + 4]
     (
-        grad_own, grad_given, pack, seen, sums,
-        memory, decoded, grad_memory, w, v, sems, v_sems, mk, sk, mq, sq, mono, span, keep, queue, scaled, ratio, window, mix, pre,
+        grad_own, grad_given, pack_me, pack_chip, pack_cores, seen, near, far,
+        memory, decoded, grad_memory, pack, sums, w, v, sems, v_sems, mk, sk, mq, sq, mono, span, keep, queue, scaled, ratio, window, mix, pre,
     ) = refs[4 * count + 4 :]
     rows, _ = kept.shape
     frames, group, _ = mk.shape
@@ -624,6 +621,15 @@
         total_decoded = total_decoded + dot_nt(
             pack[r, :, 2 * block : 5 * block], w[r, :, 2 * block : 5 * block]
         )
+    pack_me[...] = pack[0]
+    pack_chip[...] = pack[1]
+    pack_cores[...] = pack[2:4]
+    middle = 2 * block
+    near[...] = sums[:, :middle]
+    far[:8, :] = sums[:, middle:]
+    far[8:9, :] = sums[5:6, :middle]
+    far[9:10, :] = sums[5:6, middle:]
+    far[10:, :] = jnp.zeros((6, middle), wide)
     grad_own[...] = jnp.where(first_chip, total_memory, total_decoded)
     grad_given[...] = jnp.where(first_chip, total_decoded, total_memory).astype(low)
 
@@ -643,16 +649,21 @@
         out_shape=(
             jax.ShapeDtypeStruct((rows, width), wide),
             jax.ShapeDtypeStruct((rows, width), low),
-            jax.ShapeDtypeStruct((4, rows, full // 4 * 6), low),
+            jax.ShapeDtypeStruct((rows, full // 4 * 6), low),
+            jax.ShapeDtypeStruct((rows, full // 4 * 6), low),
+            jax.ShapeDtypeStruct((2, rows, full // 4 * 6), low),
             jax.ShapeDtypeStruct((2, rows, vocab_width), low),
-            jax.ShapeDtypeStruct((8, full), wide),
+            jax.ShapeDtypeStruct((8, full // 2), wide),
+            jax.ShapeDtypeStruct((16, full // 2), wide),
         ),
         in_specs=[in_smem] + [in_vmem] * 8 + [in_place] * (4 * count + 4),
-        out_specs=[in_vmem] * 5,
+        out_specs=[in_vmem] * 8,
         scratch_shapes=[
             pltpu.VMEM((rows, width), low),
             pltpu.VMEM((rows, width), low),
             pltpu.VMEM((rows, width), wide),
+            pltpu.VMEM((4, rows, full // 4 * 6), low),
+            pltpu.VMEM((8, full), wide),
             pltpu.VMEM((4, width, full // 4 * 6), low),
             pltpu.VMEM((4,) + vocab[0].shape, low),
             pltpu.SemaphoreType.DMA((4, places.shape[0] - 2)),
@@ -667,6 +678,128 @@
         places, kept, taken, vectors, vocab_bias, noise, lengths, labels, counted,
         *sum(smalls, []), *vocab,
     )
+
+
+def gradient_kernel(
+    order, before, before_peer, normed, normed_peer, dz, dz_peer, states_own, states_core,
+    seen, seen_core, far, far_core, pack_me, pack_core, pack_far, *refs
+):
+    outputs, paired = refs[:8], refs[8:12]
+    a_rec, a_in, a_dz, states, a_context, a_grads, a_pack, block, paired_block, sems, out_sems = (
+        refs[12:]
+    )
+    y = order[0]
+    height = block.shape[1]
+    wide_half = a_dz.shape[1]
+    part = a_pack.shape[1] // 6
+    width = a_rec.shape[1]
+    jobs = []
+    for sources, target in (
+        ((dz.at[0], dz_peer), a_dz),
+        ((before, before_peer), a_rec),
+        ((normed, normed_peer), a_in),
+        (
+            (states_own.at[0], states_core.at[0], states_own.at[2], states_core.at[2]),
+            states.at[y],
+        ),
+        (
+            (
+                states_own.at[1], states_core.at[1],
+                far.at[2, :, :width], far_core.at[2, :, :width],
+            ),
+            states.at[1 - y],
+        ),
+        ((pack_me, pack_core.at[0], pack_far.at[0], pack_far.at[1]), a_pack),
+        ((seen.at[0], seen_core.at[0], far.at[0, :, :width], far_core.at[0, :, :width]), a_context),
+        ((seen.at[1], seen_core.at[1], far.at[1, :, :width], far_core.at[1, :, :width]), a_grads),
+    ):
+        rows = target.shape[0] // len(sources)
+        for r, source in enumerate(sources):
+            jobs.append(
+                pltpu.make_async_copy(
+                    source, target.at[r * rows : (r + 1) * rows, :], sems.at[len(jobs)]
+                )
+            )
+    for job in jobs:
+        job.start()
+    for job in jobs:
+        job.wait()
+
+    def one(n, carried):
+        cols = pl.ds(pl.multiple_of(order[1 + n] * height, height), height)
+        both = jnp.concatenate([a_rec[:, cols], a_in[:, cols]], axis=1)
+        for at in range(0, wide_half, 1024):
+            value = dot_tn(both, a_dz[:, at : at + 1024]).astype(low)
+            block[n, :, at : at + 1024] = value[:height]
+            block[n, :, wide_half + at : wide_half + at + 1024] = value[height:]
+        for m in range(2):
+            to = 2 * wide_half + 2 * m * part
+            block[n, :, to : to + 2 * part] = dot_tn(
+                states[m, :, cols], a_pack[:, 2 * m * part : 2 * (m + 1) * part]
+            ).astype(low)
+        for m, output in enumerate(outputs):
+
+            @pl.when(n == m)
+            def _(m=m, output=output):
+                pltpu.make_async_copy(block.at[m], output, out_sems.at[m]).start()
+
+        return carried
+
+    lax.fori_loop(0, 8, one, 0)
+
+    def pair(n, carried):
+        cols = pl.ds(pl.multiple_of(order[9 + n] * 2 * height, 2 * height), 2 * height)
+        grad_pre = a_pack[:, 4 * part : 5 * part]
+        for m, (a, b) in enumerate(
+            (
+                (states[1, :, cols], grad_pre),
+                (a_context[:, cols], grad_pre),
+                (a_grads[:, cols], a_pack[:, 5 * part :]),
+            )
+        ):
+            paired_block[n, :, m * part : (m + 1) * part] = dot_tn(a, b).astype(low)
+        return carried
+
+    lax.fori_loop(0, 4, pair, 0)
+    for m, output in enumerate(paired):
+        pltpu.make_async_copy(paired_block.at[m], output, out_sems.at[8 + m]).start()
+    for m, output in enumerate(outputs):
+        pltpu.make_async_copy(block.at[m], output, out_sems.at[m]).wait()
+    for m, output in enumerate(paired):
+        pltpu.make_async_copy(paired_block.at[m], output, out_sems.at[8 + m]).wait()
+
+
+def run_gradients(order, *arrays):
+    rows, width = arrays[0].shape
+    wide_half = arrays[5].shape[1]
+    part = arrays[12].shape[1] // 6
+    columns = 2 * wide_half + 4 * part
+    height = width // 8
+    deep = 2 * rows
+    return pl.pallas_call(
+        gradient_kernel,
+        out_shape=tuple(
+            [jax.ShapeDtypeStruct((height, columns), low)] * 8
+            + [jax.ShapeDtypeStruct((2 * height, 3 * part), low)] * 4
+        ),
+        in_specs=[in_smem] + [in_place] * 15,
+        out_specs=[in_place] * 12,
+        scratch_shapes=[
+            pltpu.VMEM((deep, width), low),
+            pltpu.VMEM((deep, width), low),
+            pltpu.VMEM((deep, wide_half), low),
+            pltpu.VMEM((2, deep, width), low),
+            pltpu.VMEM((deep, width), low),
+            pltpu.VMEM((deep, width), low),
+            pltpu.VMEM((deep, 6 * part), low),
+            pltpu.VMEM((8, height, columns), low),
+            pltpu.VMEM((4, 2 * height, 3 * part), low),
+            pltpu.SemaphoreType.DMA((26,)),
+            pltpu.SemaphoreType.DMA((12,)),
+        ],
+        compiler_params=pltpu.CompilerParams(vmem_limit_bytes=56 << 20),
+        name="weight_gradients",
+    )(order, *arrays)
 
 
 def local(
@@ -800,16 +933,16 @@
     small_chip[-1] = tie(small_chip[-1], kept)
     small_both = [across_cores(part) for part in small_chip]
     smalls = [small_own, small_chip, small_core, small_both]
-    grad_own, grad_given, pack, seen, sums = run_attend(
+    grad_own, grad_given, pack_me, pack_chip, pack_cores, seen, near, far = run_attend(
         places, kept, taken, smalls, vocab, vectors, bias_row, noise_part, length_part,
         label_part, counted, frames,
     )
     grad_taken = across_chips(grad_given)
-    pack_core = across_cores(pack[2:4])
-    pack_out = jnp.stack([pack[1], pack_core[1]])
-    blocks = sums[:5].reshape(5, 4, block)
-    vector_pair = blocks[:, :2] + across_cores(blocks[:, 2:])
-    bias_pair = sums[5] + across_cores(sums[5])
+    pack_core = across_cores(pack_cores)
+    pack_out = jnp.stack([pack_chip, pack_core[1]])
+    far_peer = across_cores(far)
+    vector_pair = (near[:5] + far_peer[:5]).reshape(5, 2, block)
+    bias_pair = (far[8:10] + far_peer[8:10]).reshape(-1)
     vector_out = jnp.concatenate([vector_pair[:, 1].reshape(-1), bias_pair])
     vector_count = vector_out.shape[0] // (3 * rows)
     seen_out = jnp.concatenate(
@@ -821,10 +954,10 @@
     )
     before = before.reshape(frames * half, width)
     before_peer = across_cores(tie(before, taken))
-    states = jnp.stack([kept, taken])
-    states_core = across_cores(tie(states, grad_given))
+    states = jnp.stack([tie(kept, grad_given), taken, given])
+    states_core, seen_core = across_cores(states), across_cores(seen)
     places_back, pack_out, seen_out = lax.optimization_barrier(
-        (places, pack_out, seen_out, grad_taken, before_peer, states_core)
+        (places, pack_out, seen_out, grad_taken, before_peer, states_core, seen_core)
     )[:3]
     dz = run_backward(
         places_back, grad_own.reshape(frames, quarter, width),
@@ -834,88 +967,58 @@
     seen_far = across_chips(tie(seen_out, pack_out))
 
     dz = dz.reshape(2, frames * half, wide_half)
-    dz_kept, dz_given, pack_far, seen_far = lax.optimization_barrier(
-        (dz[0], dz[1], pack_far, seen_far)
-    )
-    dz_all = jnp.concatenate([dz_kept, across_cores(dz_given)], axis=0)
-    before_all = jnp.concatenate([before, before_peer], axis=0)
-    normed_all = jnp.concatenate([normed_own, normed_other], axis=0)
-    rec_total = dot_tn(before_all, dz_all).astype(low)
-    in_total = dot_tn(normed_all, dz_all).astype(low)
-
+    dz, pack_far, seen_far = lax.optimization_barrier((dz, pack_far, seen_far))
+    dz_peer = across_cores(dz[1])
+    grad_inputs, grad_gain = run_input(
+        places, inputs_own.reshape(frames * half, width), gain[None], dz, in_own, in_other
+    )
+    grad_gain = grad_gain.reshape(width)
+    z, x = ring.z, ring.x
+    if ring.short:
+        steps_back = [ring.back(k) for k in range(1, 5)]
+        order = [at * 2 + 1 - x for at in steps_back] + [at * 2 + x for at in steps_back]
+        order = [y] + order + steps_back
+    else:
+        order = [y] + [jnp.int32(k) for k in [*range(8), *range(4)]]
+    totals = run_gradients(
+        tie(jnp.stack(order).astype(jnp.int32), grad_gain), before, before_peer, normed_own, normed_other, dz,
+        dz_peer, states, states_core, seen, seen_core, seen_far, across_cores(seen_far),
+        pack_me, pack_core, pack_far,
+    )
+    grad_inputs = jnp.swapaxes(grad_inputs.reshape(frames, half, width), 0, 1)
     vector_far = joined(seen_far[:, :, width:].reshape(3 * rows, -1), vector_count).reshape(-1)
-    chip_rows = jnp.concatenate(
-        [seen, seen_far[:2, :, :width], jnp.stack([given, seen_far[2, :, :width]])], axis=0
-    )
-    core_rows = across_cores(chip_rows)
-    section_all = jnp.concatenate([kept, states_core[0], chip_rows[4], core_rows[4]], axis=0)
-    other_all = jnp.concatenate([taken, states_core[1], chip_rows[5], core_rows[5]], axis=0)
-    memory_all = jnp.where(y == 0, section_all, other_all)
-    decoded_all = jnp.where(y == 0, other_all, section_all)
-    seen_all = [
-        jnp.concatenate([chip_rows[n], core_rows[n], chip_rows[2 + n], core_rows[2 + n]], axis=0)
-        for n in range(2)
-    ]
-    pack_all = jnp.concatenate([pack[0], pack_core[0], pack_far[0], pack_far[1]], axis=0)
-    if ring.short:
-        first_rec, first_in = [
-            cut(a, ring.back(1) * 2 + 1 - ring.x, shard_rows) for a in (rec_total, in_total)
+
+    sides_at = 5 * block + vocab_pad
+    grad_peer = across_cores(grad_inputs)
+    grad_section = jnp.concatenate(
+        [
+            jnp.where(s == 0, grad_inputs, grad_peer),
+            jnp.where(s == 0, grad_peer, grad_inputs),
+        ],
+        axis=0,
+    )
+    gain_sum = grad_gain + across_cores(grad_gain)
+    flat = jnp.concatenate(
+        [
+            vector_pair[:, 0].reshape(-1) + vector_far[: 5 * block],
+            bias_pair + vector_far[5 * block :],
+            jnp.sum(dz[0].astype(wide), axis=0) + jnp.sum(dz_peer.astype(wide), axis=0),
+            gain_sum,
         ]
-        pack_all = tie(pack_all, first_rec, first_in)
-    energy_total = [
-        dot_tn(memory_all, pack_all[:, : 2 * block]).astype(low),
-        dot_tn(decoded_all, pack_all[:, 2 * block : 4 * block]).astype(low),
-    ]
-    grad_pre = pack_all[:, 4 * block : 5 * block]
-    output_total = [
-        dot_tn(decoded_all, grad_pre).astype(low),
-        dot_tn(seen_all[0], grad_pre).astype(low),
-        dot_tn(seen_all[1], pack_all[:, 5 * block :]).astype(low),
-    ]
-
-    sides_at = 5 * block + vocab_pad
+    )
+    flat = jnp.pad(flat, (0, -flat.shape[0] % (8 * shard_rows)))
 
     def to_other_chip(section):
         return lax.ppermute(section, ("section", "mp"), [(0, 1), (3, 2)])
 
-    def input_back(dz_kept):
-        grad_inputs, grad_gain = run_input(
-            places, inputs_own.reshape(frames * half, width), gain[None], dz_kept, dz_given,
-            in_own, in_other,
-        )
-        grad_inputs = jnp.swapaxes(grad_inputs.reshape(frames, half, width), 0, 1)
-        grad_peer = across_cores(grad_inputs)
-        section = jnp.concatenate(
-            [
-                jnp.where(s == 0, grad_inputs, grad_peer),
-                jnp.where(s == 0, grad_peer, grad_inputs),
-            ],
-            axis=0,
-        )
-        grad_gain = grad_gain.reshape(width)
-        gain_sum = grad_gain + across_cores(grad_gain)
-        flat = jnp.concatenate(
-            [
-                vector_pair[:, 0].reshape(-1) + vector_far[: 5 * block],
-                bias_pair + vector_far[5 * block :],
-                jnp.sum(dz_all.astype(wide), axis=0),
-                gain_sum,
-            ]
-        )
-        return section, jnp.pad(flat, (0, -flat.shape[0] % (2 * shard_rows)))
-
     if ring.short:
-        r, x = shard_rows, ring.x
+        r = shard_rows
         both, width_out = 2 * wide_half, 2 * block
         flow, across, onward = Flow(), ring.across, ring.onward
-        chain = [rec_total, in_total] + energy_total
-
-        def theirs(group, k):
-            return ring.part(group, ring.back(k) * 2 + 1 - x, r)
+        theirs, mine, outputs = totals[:4], totals[4:8], totals[8:]
 
         def total(k, arrived, passed):
-            value = ring.part(chain, ring.back(k) * 2 + x, r).astype(wide)
-            value = value + arrived.astype(wide)
+            value = mine[k - 1].astype(wide) + arrived.astype(wide)
             return value if passed is None else value + passed.astype(wide)
 
         def cornered(hop):
@@ -925,66 +1028,59 @@
             ]
             return lambda array: lax.ppermute(array, ("section", "dp", "mp"), pairs)
 
-        def output_part(k):
-            return ring.part(output_total, ring.back(k), 2 * r)
-
-        arrived = [across(a) for a in (first_rec, first_in, theirs(energy_total, 1))]
-        out_two, out_before = onward(output_part(2)), ring.astern(output_part(1))
-        grad_section, flat = input_back(tie(dz_kept, first_in, *output_total))
-        flat_width = flat.shape[0] // r
-        out_one = output_part(3).astype(wide) + out_two.astype(wide)
-        out_one = onward(out_one.astype(low))
-        flat_far = across(tie(halves(flat, r), out_two, out_before))
-        arrived = jnp.concatenate(arrived, axis=1)
-        flow.landed = (arrived, out_one, flat_far)
+        arrived, out_two, out_before = flow.step(
+            (across, theirs[0]), (onward, outputs[1]), (ring.astern, outputs[0])
+        )
+        grad_far = to_other_chip(grad_section)
+        flat = flat.reshape(8, -1)
+        flat = flat + across(flat)
+        flow.landed = (arrived,)
         value = total(1, arrived, None).astype(low)
-        out = output_part(4).astype(wide) + out_before.astype(wide) + out_one.astype(wide)
+        out = (outputs[2].astype(wide) + out_two.astype(wide)).astype(low)
+        passed, arrived, out_one = flow.step((onward, value), (across, theirs[1]), (onward, out))
+        flat_one, flat_three = onward(flat), ring.astern(flat)
+        out = outputs[3].astype(wide) + out_before.astype(wide) + out_one.astype(wide)
         vocab_rows = out[:, width_out:].astype(low)
         message = jnp.concatenate(
             [cut(out, 1 - x, r)[:, :width_out].astype(low), vocab_rows[:r], vocab_rows[r:]], axis=1
         )
-        passed, arrived, out_far, grad_far = flow.step(
-            (onward, value), (across, theirs(chain, 2)), (across, message),
-            (to_other_chip, grad_section),
+        value = total(2, arrived, passed).astype(low)
+        passed, arrived, out_far, kept_rows = flow.step(
+            (onward, value), (across, theirs[2]), (across, message), (corners, mine[3][:, :both]),
+            also=(flat_one, flat_three),
         )
+        flat = flat + flat_one + flat_three + onward(flat_one)
         output_grad = cut(out, x, r)[:, :width_out] + out_far[:, :width_out].astype(wide)
-        flat = flat + joined(flat_far, flat_width).reshape(-1)
         shard = jnp.concatenate([out[:r, width_out:], out[r:, width_out:]], axis=1)
         shard = (shard + out_far[:, width_out:].astype(wide)).astype(low)
-        shard = jnp.concatenate([shard, halves(flat, r)], axis=1)
-        value = total(2, arrived, passed).astype(low)
-        mine = ring.part([rec_total, in_total], ring.back(4) * 2 + x, r)
-        passed, arrived, next_one, next_three, mine = flow.step(
-            (onward, value), (across, theirs(chain, 3)), (onward, shard), (ring.astern, shard),
-            (corners, mine),
+        value = total(3, arrived, passed).astype(low)
+        passed, arrived, energy_passed, energy_arrived, next_three = flow.step(
+            (cornered(ring.ring), value[:, :both]), (cornered(ring.pair), theirs[3][:, :both]),
+            (onward, jnp.concatenate([value[:, both:], shard], axis=1)),
+            (across, theirs[3][:, both:]), (ring.astern, shard),
+            also=(grad_far, flat),
         )
+        flat = flat.reshape(-1)
+        sides = corners(tie(flat[sides_at : sides_at + wide_half + width], value))
+        next_one, energy_passed = energy_passed[:, 4 * block :], energy_passed[:, : 4 * block]
         shards = {0: shard, 1: next_one, 3: next_three, 2: onward(next_one)}
-        flat = sum(joined(a[:, 2 * block :], flat_width).reshape(-1) for a in shards.values())
-        value = total(3, arrived, passed).astype(low)
-        passed, arrived, energy_passed, energy_arrived = flow.step(
-            (cornered(ring.ring), value[:, :both]),
-            (cornered(ring.pair), theirs([rec_total, in_total], 4)),
-            (onward, value[:, both:]), (across, theirs(energy_total, 4)),
-        )
-        sides = corners(flat[sides_at : sides_at + wide_half + width])
-        moved = mine.astype(wide) + arrived.astype(wide) + passed.astype(wide)
-        energy_grad = ring.part(energy_total, ring.back(4) * 2 + x, r).astype(wide)
-        energy_grad = energy_grad + energy_arrived.astype(wide) + energy_passed.astype(wide)
+        moved = kept_rows.astype(wide) + arrived.astype(wide) + passed.astype(wide)
+        energy_grad = mine[3][:, both:].astype(wide) + energy_arrived.astype(wide)
+        energy_grad = energy_grad + energy_passed.astype(wide)
         vocab_grad = jnp.zeros((vocab_pad, block), low)
         for k, held in shards.items():
             held = jnp.concatenate([held[:, :block], held[:, block : 2 * block]], axis=0)
             vocab_grad = lax.dynamic_update_slice(vocab_grad, held, (ring.back(k) * 2 * r, 0))
     else:
-        grad_section, flat = input_back(dz_kept)
         grad_far = to_other_chip(grad_section)
 
-        def scatter(total):
+        def scatter(parts):
+            total = jnp.concatenate(parts, axis=0)
             return lax.psum_scatter(total, "dp", scatter_dimension=0, tiled=True).astype(wide)
 
-        moved = jnp.concatenate([scatter(rec_total), scatter(in_total)], axis=1)
+        moved, output_grad = scatter(totals[:8]), scatter(totals[8:])
+        moved, energy_grad = moved[:, : 2 * wide_half], moved[:, 2 * wide_half :]
         moved = corners(moved.astype(low)).astype(wide)
-        energy_grad = jnp.concatenate([scatter(a) for a in energy_total], axis=1)
-        output_grad = jnp.concatenate([scatter(a) for a in output_total], axis=1)
         flat = lax.psum(flat, "dp")
         sides = corners(flat[sides_at : sides_at + wide_half + width])
         vocab_grad = lax.all_gather(

time: 520 us -> 493 us (0.948); the launches traced: 510 us -> 492 us
  local copies, waits for them, and re-layouts: 79.5 us -> 45.7 us
  waiting for transfers between devices: 202 us -> 233 us
  Pallas kernels: 103 us -> 118 us
  other arithmetic: 41.4 us -> 29.3 us
  starting transfers between devices: 72.4 us -> 63.2 us
  matrix products: 8.81 us -> 0 us
    ppermute x5, starting transfers between devices: 22.2 us -> 5 us  [corners(): return lax.ppermute(array, ('section', 'mp'), corner_swap)]
    ppermute x11 -> x12, waiting for transfers between devices: 76.5 us -> 59.8 us  [onward(): return lax.ppermute(array, 'dp', self.ring)]
    pallas_call x0 -> x1, Pallas kernels: none -> 15.2 us  [run_gradients(): pl.pallas_call(gradient_kernel, out_shape=tuple([jax.ShapeDtypeStruct((he...]
    ppermute x13 -> x11, waiting for transfers between devices: 94 us -> 109 us  [across(): return lax.ppermute(array, 'dp', self.pair)]
    ppermute x1, waiting for transfers between devices: 0.01 us -> 14.1 us  [to_other_chip(): return lax.ppermute(section, ('section', 'mp'), [(0, 1), (3, 2)])]
    ppermute x10, waiting for transfers between devices: 27.3 us -> 39.8 us  [across_chips(): return lax.ppermute(array, 'mp', core_swap)]
    concatenate x17 -> x3, other arithmetic: 12.1 us -> 1.49 us  [the longest x1 1.45 us: local(): jnp.concatenate([jnp.where(s == 0, grad_inputs, grad_peer), jnp.where(s =...]
    dot_general x7 -> x0, matrix products: 8.81 us -> none  [dot_tn(): lax.dot_general(a, b, (((0,), (0,)), ((), ())), preferred_element_type=wide)]
  transfers between devices with their start and end apart: 75 -> 75, of which waited for: 21 -> 19; matrix products, arithmetic and copies ran while one was open for 20% -> 11% of each run, Pallas kernels for 20% -> 24%
where the time goes in v5:
time: 493 us; the launch traced here: 492 us
  waiting for transfers between devices  233 us (47%)
  Pallas kernels  118 us (24%)
  starting transfers between devices  63.2 us (13%)
  local copies, waits for them, and re-layouts  45.7 us (9%)
  other arithmetic  29.3 us (6%)
    ppermute x11, waiting for transfers between devices, across(): return lax.ppermute(array, 'dp', self.pair)  109 us
    ppermute x12, waiting for transfers between devices, onward(): return lax.ppermute(array, 'dp', self.ring)  59.8 us
    ppermute x10, waiting for transfers between devices, across_chips(): return lax.ppermute(array, 'mp', core_swap)  39.8 us
    pallas_call x1, Pallas kernels, run_attend(): pl.pallas_call(functools.partial(attend_kernel, count), out_shape=(jax.Sh...  33.4 us
    pallas_call x1, Pallas kernels, run_forward(): pl.pallas_call(functools.partial(forward_kernel, count, column), out_shap...  30.6 us
    pallas_call x1, Pallas kernels, run_backward(): pl.pallas_call(functools.partial(backward_kernel, count, column), out_sha...  30.2 us
    ppermute x10, starting transfers between devices, across_chips(): return lax.ppermute(array, 'mp', core_swap)  16.7 us
    unnamed x144, local copies, waits for them, and re-layouts  15.4 us
  transfers between devices with their start and end apart: 75, of which 19 were waited for; matrix products, arithmetic and copies ran while one was open for 11% of the time, Pallas kernels for 24%

profile of v5, /device:TPU:0, one launch (start us, length us, event | category | flops | bytes accessed | tf_op | source)
XLA Modules:
  0.0 491.7 jit_solution(17234295036060493821)
XLA Ops:
  0.8 1.3 copy.73
  7.1 2.9 collective-permute-start.3
  10.1 1.6 collective-permute-start.2
  12.8 1.5 collective-permute-start
  14.5 1.2 copy.62
  19.7 1.4 collective-permute-start.4
  23.0 1.1 constant_dynamic-update-slice_fusion.6
  24.3 1.6 collective-permute-start.8
  25.9 1.6 collective-permute-start.7
  27.4 6.5 %collective-permute-start.9 = (bf16[128,3072]{1,0:T(8,128)(2,1)S(1)}, bf16[128,3072]{1,0:T(8,128)(2,1)S(1)}, u32[]{:S(2)}, u32[]{:S(2)}) collective-permute-start(bf16[128,3072]{1,0:T(8,128)(2,1)S(1)} %copy-done.31), channel_id=1, source_target_pairs={{0,1},{1,0},{2,3},{3,2},{4,5},{5,4},{6,7},{7,6},{8,9},{9,8},{10,11... | collective-permute-start | bytes 2359304 | tf_op jit(solution)/shard_map/ppermute | solution.py:33
  34.0 2.0 collective-permute-start.5
  35.9 1.3 broadcast_select_fusion
  40.9 11.1 %collective-permute-done.8.refs_1_.refs_17_ = bf16[128,5632]{1,0:T(8,128)(2,1)S(1)} collective-permute-done((bf16[128,5632]{1,0:T(8,128)(2,1)S(1)}, bf16[128,5632]{1,0:T(8,128)(2,1)S(1)}, u32[]{:S(2)}, u32[]{:S(2)}) %collective-permute-start.8) | collective-permute-done | bytes 1441824 | tf_op jit(solution)/shard_map/ppermute | solution.py:73
  52.1 10.8 %collective-permute-done.5 = f32[5,256]{1,0:T(8,128)S(1)} collective-permute-done((f32[5,256]{1,0:T(8,128)S(1)}, f32[5,256]{1,0:T(8,128)S(1)}, u32[]{:S(2)}, u32[]{:S(2)}) %collective-permute-start.5) | collective-permute-done | bytes 5152 | tf_op jit(solution)/shard_map/ppermute | solution.py:33
  63.0 1.6 broadcast_in_dim.17.noise
  65.2 1.5 collective-permute-start.13
  66.7 1.6 collective-permute-start.12
  68.3 1.8 collective-permute-start.14
  70.2 29.1 %collective-permute-done.13.refs_3_.refs_19_ = bf16[128,5632]{1,0:T(8,128)(2,1)S(1)} collective-permute-done((bf16[128,5632]{1,0:T(8,128)(2,1)S(1)}, bf16[128,5632]{1,0:T(8,128)(2,1)S(1)}, u32[]{:S(2)}, u32[]{:S(2)}) %collective-permute-start.13) | collective-permute-done | bytes 1441824 | tf_op jit(solution)/shard_map/ppermute | solution.py:73
  99.4 2.9 collective-permute-done.12.refs_4_.refs_20_
  103.5 2.0 collective-permute-done.20.refs_8_
  106.0 17.1 %collective-permute-done.19.refs_6_ = bf16[128,3072]{1,0:T(8,128)(2,1)} collective-permute-done((bf16[128,3072]{1,0:T(8,128)(2,1)S(1)}, bf16[128,3072]{1,0:T(8,128)(2,1)}, u32[]{:S(2)}, u32[]{:S(2)}) %collective-permute-start.19) | collective-permute-done | bytes 786464 | tf_op jit(solution)/shard_map/ppermute | solution.py:33
  123.1 12.5 %collective-permute-done.23.refs_5_.refs_21_ = bf16[128,5632]{1,0:T(8,128)(2,1)} collective-permute-done((bf16[128,5632]{1,0:T(8,128)(2,1)S(1)}, bf16[128,5632]{1,0:T(8,128)(2,1)}, u32[]{:S(2)}, u32[]{:S(2)}) %collective-permute-start.23) | collective-permute-done | bytes 1441824 | tf_op jit(solution)/shard_map/ppermute | solution.py:73
  139.6 1.3 collective-permute-done.25.b_other
  143.4 20.3 %collective-permute-done.26.refs_7_.refs_23_ = bf16[128,4096]{1,0:T(8,128)(2,1)} collective-permute-done((bf16[128,4096]{1,0:T(8,128)(2,1)}, bf16[128,4096]{1,0:T(8,128)(2,1)}, u32[]{:S(2)}, u32[]{:S(2)}) %collective-permute-start.26) | collective-permute-done | bytes 1048608 | tf_op jit(solution)/shard_map/ppermute | solution.py:73
  164.5 1.3 select_maximum_fusion.vectors
  166.8 30.6 %recur_forward.1 = (bf16[16,8,1024]{2,1,0:T(8,128)(2,1)}, bf16[16,8,1024]{2,1,0:T(8,128)(2,1)}, bf16[16,16,1024]{2,1,0:T(8,128)(2,1)}, f32[16,16,4096]{2,1,0:T(8,128)}, f32[16,16,1024]{2,1,0:T(8,128)}) custom-call(s32[10]{0:T(128)} %stack.113.places, bf16[256,1024]{1,0:T(8,128)(2,1)} %bitcast.89, f32[1,2048]{1,0:T(1,128)} %copy-done.50, ...), custom_call_target="tpu_custom_call" | custom-call | tf_op jit(solution)/shard_map/recur_forward/pallas_call | solution.py:184
  197.7 1.9 collective-permute-start.35
  201.1 5.4 %collective-permute-done.35.taken = bf16[128,1024]{1,0:T(8,128)(2,1)S(1)} collective-permute-done((bf16[128,1024]{1,0:T(8,128)(2,1)}, bf16[128,1024]{1,0:T(8,128)(2,1)S(1)}, u32[]{:S(2)}, u32[]{:S(2)}) %collective-permute-start.35) | collective-permute-done | bytes 262176 | tf_op jit(solution)/shard_map/ppermute | solution.py:33
  208.0 33.4 %attend.1 = (f32[128,1024]{1,0:T(8,128)}, bf16[128,1024]{1,0:T(8,128)(2,1)}, bf16[128,1536]{1,0:T(8,128)(2,1)}, bf16[128,1536]{1,0:T(8,128)(2,1)}, bf16[2,128,15...) custom-call(s32[10]{0:T(128)} %stack.113.places, ...), custom_call_target="tpu_custom_call" | custom-call | tf_op jit(solution)/shard_map/attend/pallas_call | solution.py:647
  241.5 1.8 collective-permute-start.43
  246.8 2.1 collective-permute-done.41.pack_core
  248.9 1.3 pad_maximum_fusion.5
  250.3 1.4 collective-permute-start.48
  252.4 30.2 %recur_backward.1 = bf16[2,16,16,2048]{3,2,1,0:T(8,128)(2,1)} custom-call(s32[10]{0:T(128)} %stack.113.places, f32[16,8,1024]{2,1,0:T(8,128)} %bitcast.102, bf16[16,8,1024]{2,1,0:T(8,128)(2,1)} %bitcast.39.taken, f32[16,16,4096]{2,1,0:T(8,128)} %get-tuple-element.129.gates, f32[16,16,1024]{2,1,0:T(8,128)} %get-tuple-element.130.cells, ...), custom_call_target="tpu_custom_call" | custom-call | tf_op jit(solution)/shard_map/recur_backward/pallas_call | solution.py:286
  282.6 6.6 %collective-permute-done.47.pack_far = bf16[2,128,1536]{2,1,0:T(8,128)(2,1)S(1)} collective-permute-done((bf16[2,128,1536]{2,1,0:T(8,128)(2,1)S(1)}, bf16[2,128,1536]{2,1,0:T(8,128)(2,1)S(1)}, u32[]{:S(2)}, u32[]{:S(2)}) %collective-permute-start.47) | collective-permute-done | bytes 786464 | tf_op jit(solution)/shard_map/ppermute | solution.py:33
  289.2 2.9 slice_bitcast_fusion
  294.3 8.9 %input_back.1 = (f32[256,1024]{1,0:T(8,128)}, f32[1,1024]{1,0:T(1,128)}) custom-call(s32[10]{0:T(128)} %stack.113.places, bf16[256,1024]{1,0:T(8,128)(2,1)} %bitcast.97, f32[1,1024]{1,0:T(1,128)} %bitcast.114, bf16[2,256,2048]{2,1,0:T(8,128)(2,1)} %bitcast.86, bf16[128,5632]{1,0:T(8,128)(2,1)} %copy-done.4, bf16[128,5632]{1,0:T(8,128)(2,1)} %copy-done.5, ...), custom_call_target="tpu_custom_call" | custom-call | tf_op jit(solution)/shard_map/input_back/pallas_call | solution.py:332
  304.3 15.2 %weight_gradients.1 = (bf16[128,5120]{1,0:T(8,128)(2,1)}, bf16[128,5120]{1,0:T(8,128)(2,1)}, bf16[128,5120]{1,0:T(8,128)(2,1)}, bf16[128,5120]{1,0:T(8,128)(2,1)...) custom-call(s32[13]{0:T(128)} %stack.131.order, ...), custom_call_target="tpu_custom_call" | custom-call | tf_op jit(solution)/shard_map/weight_gradients/pallas_call | solution.py:779
  320.8 1.4 convert_reduce_fusion
  322.3 1.5 collective-permute-start.53
  324.5 3.9 collective-permute-start.62
  328.4 23.2 %collective-permute-done.53 = f32[8,768]{1,0:T(8,128)S(1)} collective-permute-done((f32[8,768]{1,0:T(8,128)S(1)}, f32[8,768]{1,0:T(8,128)S(1)}, u32[]{:S(2)}, u32[]{:S(2)}) %collective-permute-start.53) | collective-permute-done | bytes 24608 | tf_op jit(solution)/shard_map/ppermute | solution.py:73
  351.6 3.8 collective-permute-start.55
  356.2 2.7 add_convert_fusion.2
  360.2 1.2 collective-permute-start.56
  361.4 1.5 pad_maximum_fusion
  366.1 33.7 %collective-permute-done.56 = f32[8,768]{1,0:T(8,128)S(1)} collective-permute-done((f32[8,768]{1,0:T(8,128)S(1)}, f32[8,768]{1,0:T(8,128)S(1)}, u32[]{:S(2)}, u32[]{:S(2)}) %collective-permute-start.56) | collective-permute-done | bytes 24608 | tf_op jit(solution)/shard_map/ppermute | solution.py:76
  399.8 3.5 collective-permute-start.50
  403.4 1.4 fusion.13
  404.9 3.5 add_convert_fusion.1
  410.2 1.5 collective-permute-start.68
  411.7 14.1 %collective-permute-done.50 = f32[32,16,1024]{2,1,0:T(8,128)} collective-permute-done((f32[32,16,1024]{2,1,0:T(8,128)}, f32[32,16,1024]{2,1,0:T(8,128)}, u32[]{:S(2)}, u32[]{:S(2)}) %collective-permute-start.50) | collective-permute-done | bytes 2097184 | tf_op jit(solution)/shard_map/ppermute | solution.py:1012
  425.9 1.7 select_bitcast_fusion
  428.4 12.7 %collective-permute-done.68 = bf16[128,1024]{1,0:T(8,128)(2,1)S(1)} collective-permute-done((bf16[128,1024]{1,0:T(8,128)(2,1)S(1)}, bf16[128,1024]{1,0:T(8,128)(2,1)S(1)}, u32[]{:S(2)}, u32[]{:S(2)}) %collective-permute-start.68) | collective-permute-done | bytes 262176 | tf_op jit(solution)/shard_map/ppermute | solution.py:73
  441.3 2.3 add_convert_fusion
  444.7 3.8 collective-permute-start.73
  450.6 1.5 collective-permute-start.69
  453.3 1.3 slice.296
  454.6 4.7 collective-permute-done.73
  462.2 23.2 %collective-permute-done.74 = bf16[128,512]{1,0:T(8,128)(2,1)S(1)} collective-permute-done((bf16[128,512]{1,0:T(8,128)(2,1)S(1)}, bf16[128,512]{1,0:T(8,128)(2,1)S(1)}, u32[]{:S(2)}, u32[]{:S(2)}) %collective-permute-start.74) | collective-permute-done | bytes 131104 | tf_op jit(solution)/shard_map/ppermute | solution.py:76
  486.5 1.6 convert_add_fusion
  488.3 1.7 reshape.192
  490.0 1.7 reshape.193
  (356 shorter events, 56.0 us)
Async XLA Ops:
  7.1 12.6 %collective-permute-start.3 = (bf16[128,1536]{1,0:T(8,128)(2,1)}, bf16[128,1536]{1,0:T(8,128)(2,1)}, u32[]{:S(2)}, u32[]{:S(2)}) collective-permute-start(bf16[128,1536]{1,0:T(8,128)(2,1)} %get-tuple-element.203), channel_id=1, source_target_pairs={{0,2},{2,0},{4,6},{6,4},{8,10},{10,8},{12,14},{14,12},{1,3},{3,1},... | collective-permute-start | bytes 1179656 | tf_op jit(solution)/shard_map/ppermute | solution.py:73
  10.1 14.2 %collective-permute-start.2 = (bf16[128,1536]{1,0:T(8,128)(2,1)}, bf16[128,1536]{1,0:T(8,128)(2,1)S(1)}, u32[]{:S(2)}, u32[]{:S(2)}) collective-permute-start(bf16[128,1536]{1,0:T(8,128)(2,1)} %get-tuple-element.203), channel_id=1, source_target_pairs={{0,4},{2,6},{4,8},{6,10},{8,12},{10,14},{12,0},{14,2},{1,5},{3,7},... | collective-permute-start | bytes 1179656 | tf_op jit(solution)/shard_map/ppermute | solution.py:76
  11.7 22.3 %collective-permute-start.10 = (bf16[16,32,1024]{2,0,1:T(8,128)(2,1)}, bf16[16,32,1024]{2,0,1:T(8,128)(2,1)}, u32[]{:S(2)}, u32[]{:S(2)}) collective-permute-start(bf16[16,32,1024]{2,0,1:T(8,128)(2,1)} %bitcast.22), channel_id=1, source_target_pairs={{0,16},{16,0},{1,17},{17,1},{2,18},{18,2},{3,19},{19,3},{4,20},{20... | collective-permute-start | bytes 3145736 | tf_op jit(solution)/shard_map/ppermute | solution.py:29
  11.7 7.3 %collective-permute-start.11 = (f32[1024]{0:T(1024)S(1)}, f32[1024]{0:T(1024)S(1)}, u32[]{:S(2)}, u32[]{:S(2)}) collective-permute-start(f32[1024]{0:T(1024)S(1)} %bitcast.119), channel_id=1, source_target_pairs={{0,16},{16,0},{1,17},{17,1},{2,18},{18,2},{3,19},{19,3},{4,20},{20... | collective-permute-start | bytes 12296 | tf_op jit(solution)/shard_map/ppermute | solution.py:29
  12.8 10.2 %collective-permute-start = (bf16[128,2048]{1,0:T(8,128)(2,1)S(1)}, bf16[128,2048]{1,0:T(8,128)(2,1)}, u32[]{:S(2)}, u32[]{:S(2)}) collective-permute-start(bf16[128,2048]{1,0:T(8,128)(2,1)S(1)} %bitcast.109), channel_id=1, source_target_pairs={{0,0},{1,16},{16,1},{17,17},{2,2},{3,18},{18,3},{19,19},{4,4},{5,2... | collective-permute-start | bytes 1572872 | tf_op jit(solution)/shard_map/ppermute | solution.py:37
  19.0 5.2 %collective-permute-start.1 = (bf16[128,2048]{1,0:T(8,128)(2,1)S(1)}, bf16[128,2048]{1,0:T(8,128)(2,1)S(1)}, u32[]{:S(2)}, u32[]{:S(2)}) collective-permute-start(bf16[128,2048]{1,0:T(8,128)(2,1)S(1)} %bitcast.108), channel_id=1, source_target_pairs={{0,0},{1,16},{16,1},{17,17},{2,2},{3,18},{18,3},{19,19},{4,4},{5,2... | collective-permute-start | bytes 1572872 | tf_op jit(solution)/shard_map/ppermute | solution.py:37
  19.7 4.5 collective-permute-start.4
  24.3 27.7 %collective-permute-start.8 = (bf16[128,5632]{1,0:T(8,128)(2,1)S(1)}, bf16[128,5632]{1,0:T(8,128)(2,1)S(1)}, u32[]{:S(2)}, u32[]{:S(2)}) collective-permute-start(bf16[128,5632]{1,0:T(8,128)(2,1)S(1)} %constant_dynamic-update-slice_fusion.4.refs_0_.refs_16_), channel_id=1, source_target_pairs={{0,2},{2,0},{4,6},{6,4},{8,10},{10,8},{12,14},{14,12},{1,3},{3,1},... | collective-permute-start | bytes 4325384 | tf_op jit(solution)/shard_map/ppermute | solution.py:73
  25.9 37.1 %collective-permute-start.7 = (bf16[128,5632]{1,0:T(8,128)(2,1)S(1)}, bf16[128,5632]{1,0:T(8,128)(2,1)S(1)}, u32[]{:S(2)}, u32[]{:S(2)}) collective-permute-start(bf16[128,5632]{1,0:T(8,128)(2,1)S(1)} %constant_dynamic-update-slice_fusion.4.refs_0_.refs_16_), channel_id=1, source_target_pairs={{0,4},{2,6},{4,8},{6,10},{8,12},{10,14},{12,0},{14,2},{1,5},{3,7},... | collective-permute-start | bytes 4325384 | tf_op jit(solution)/shard_map/ppermute | solution.py:76
  27.4 35.5 %collective-permute-start.9 = (bf16[128,3072]{1,0:T(8,128)(2,1)S(1)}, bf16[128,3072]{1,0:T(8,128)(2,1)S(1)}, u32[]{:S(2)}, u32[]{:S(2)}) collective-permute-start(bf16[128,3072]{1,0:T(8,128)(2,1)S(1)} %copy-done.31), channel_id=1, source_target_pairs={{0,1},{1,0},{2,3},{3,2},{4,5},{5,4},{6,7},{7,6},{8,9},{9,8},{10,11... | collective-permute-start | bytes 2359304 | tf_op jit(solution)/shard_map/ppermute | solution.py:33
  33.9 29.1 %collective-permute-start.6 = (bf16[256,1024]{1,0:T(8,128)(2,1)S(1)}, bf16[256,1024]{1,0:T(8,128)(2,1)S(1)}, u32[]{:S(2)}, u32[]{:S(2)}) collective-permute-start(bf16[256,1024]{1,0:T(8,128)(2,1)S(1)} %pad.20.refs_16_), channel_id=1, source_target_pairs={{0,1},{1,0},{2,3},{3,2},{4,5},{5,4},{6,7},{7,6},{8,9},{9,8},{10,11... | collective-permute-start | bytes 1572872 | tf_op jit(solution)/shard_map/ppermute | solution.py:33
  34.0 29.0 %collective-permute-start.5 = (f32[5,256]{1,0:T(8,128)S(1)}, f32[5,256]{1,0:T(8,128)S(1)}, u32[]{:S(2)}, u32[]{:S(2)}) collective-permute-start(f32[5,256]{1,0:T(8,128)S(1)} %stack.119), channel_id=1, source_target_pairs={{0,1},{1,0},{2,3},{3,2},{4,5},{5,4},{6,7},{7,6},{8,9},{9,8},{10,11... | collective-permute-start | bytes 15368 | tf_op jit(solution)/shard_map/ppermute | solution.py:33
  65.2 34.1 %collective-permute-start.13 = (bf16[128,5632]{1,0:T(8,128)(2,1)S(1)}, bf16[128,5632]{1,0:T(8,128)(2,1)S(1)}, u32[]{:S(2)}, u32[]{:S(2)}) collective-permute-start(bf16[128,5632]{1,0:T(8,128)(2,1)S(1)} %collective-permute-done.7.refs_2_.refs_18_), channel_id=1, source_target_pairs={{0,2},{2,0},{4,6},{6,4},{8,10},{10,8},{12,14},{14,12},{1,3},{3,1},... | collective-permute-start | bytes 4325384 | tf_op jit(solution)/shard_map/ppermute | solution.py:73
  66.7 35.6 %collective-permute-start.12 = (bf16[128,5632]{1,0:T(8,128)(2,1)S(1)}, bf16[128,5632]{1,0:T(8,128)(2,1)S(1)}, u32[]{:S(2)}, u32[]{:S(2)}) collective-permute-start(bf16[128,5632]{1,0:T(8,128)(2,1)S(1)} %collective-permute-done.7.refs_2_.refs_18_), channel_id=1, source_target_pairs={{0,4},{2,6},{4,8},{6,10},{8,12},{10,14},{12,0},{14,2},{1,5},{3,7},... | collective-permute-start | bytes 4325384 | tf_op jit(solution)/shard_map/ppermute | solution.py:76
  68.3 34.1 %collective-permute-start.14 = (bf16[128,3072]{1,0:T(8,128)(2,1)S(1)}, bf16[128,3072]{1,0:T(8,128)(2,1)}, u32[]{:S(2)}, u32[]{:S(2)}) collective-permute-start(bf16[128,3072]{1,0:T(8,128)(2,1)S(1)} %pad_maximum_fusion.2.refs_1_), channel_id=1, source_target_pairs={{0,1},{1,0},{2,3},{3,2},{4,5},{5,4},{6,7},{7,6},{8,9},{9,8},{10,11... | collective-permute-start | bytes 2359304 | tf_op jit(solution)/shard_map/ppermute | solution.py:33
  70.1 35.5 %collective-permute-start.27 = (bf16[128,5632]{1,0:T(8,128)(2,1)S(1)}, bf16[128,5632]{1,0:T(8,128)(2,1)S(1)}, u32[]{:S(2)}, u32[]{:S(2)}) collective-permute-start(bf16[128,5632]{1,0:T(8,128)(2,1)S(1)} %constant_dynamic-update-slice_fusion.4.refs_0_.refs_16_), channel_id=1, source_target_pairs={{0,16},{16,0},{1,17},{17,1},{2,18},{18,2},{3,19},{19,3},{4,20},{20... | collective-permute-start | bytes 4325384 | tf_op jit(solution)/shard_map/ppermute | solution.py:29
  102.4 33.2 %collective-permute-start.23 = (bf16[128,5632]{1,0:T(8,128)(2,1)S(1)}, bf16[128,5632]{1,0:T(8,128)(2,1)}, u32[]{:S(2)}, u32[]{:S(2)}) collective-permute-start(bf16[128,5632]{1,0:T(8,128)(2,1)S(1)} %collective-permute-done.12.refs_4_.refs_20_), channel_id=1, source_target_pairs={{0,2},{2,0},{4,6},{6,4},{8,10},{10,8},{12,14},{14,12},{1,3},{3,1},... | collective-permute-start | bytes 4325384 | tf_op jit(solution)/shard_map/ppermute | solution.py:73
  103.0 20.1 %collective-permute-start.19 = (bf16[128,3072]{1,0:T(8,128)(2,1)S(1)}, bf16[128,3072]{1,0:T(8,128)(2,1)}, u32[]{:S(2)}, u32[]{:S(2)}) collective-permute-start(bf16[128,3072]{1,0:T(8,128)(2,1)S(1)} %pad_maximum_fusion.3.refs_2_), channel_id=1, source_target_pairs={{0,1},{1,0},{2,3},{3,2},{4,5},{5,4},{6,7},{7,6},{8,9},{9,8},{10,11... | collective-permute-start | bytes 2359304 | tf_op jit(solution)/shard_map/ppermute | solution.py:33
  103.5 33.2 %collective-permute-start.15 = (bf16[128,4096]{1,0:T(8,128)(2,1)S(1)}, bf16[128,4096]{1,0:T(8,128)(2,1)}, u32[]{:S(2)}, u32[]{:S(2)}) collective-permute-start(bf16[128,4096]{1,0:T(8,128)(2,1)S(1)} %slice.281), channel_id=1, source_target_pairs={{0,4},{2,6},{4,8},{6,10},{8,12},{10,14},{12,0},{14,2},{1,5},{3,7},... | collective-permute-start | bytes 3145736 | tf_op jit(solution)/shard_map/ppermute | solution.py:76
  105.5 33.4 %collective-permute-start.28 = (bf16[128,5632]{1,0:T(8,128)(2,1)S(1)}, bf16[128,5632]{1,0:T(8,128)(2,1)S(1)}, u32[]{:S(2)}, u32[]{:S(2)}) collective-permute-start(bf16[128,5632]{1,0:T(8,128)(2,1)S(1)} %collective-permute-done.8.refs_1_.refs_17_), channel_id=1, source_target_pairs={{0,16},{16,0},{1,17},{17,1},{2,18},{18,2},{3,19},{19,3},{4,20},{20... | collective-permute-start | bytes 4325384 | tf_op jit(solution)/shard_map/ppermute | solution.py:29
  105.6 33.4 %collective-permute-start.29 = (bf16[128,5632]{1,0:T(8,128)(2,1)S(1)}, bf16[128,5632]{1,0:T(8,128)(2,1)S(1)}, u32[]{:S(2)}, u32[]{:S(2)}) collective-permute-start(bf16[128,5632]{1,0:T(8,128)(2,1)S(1)} %collective-permute-done.7.refs_2_.refs_18_), channel_id=1, source_target_pairs={{0,16},{16,0},{1,17},{17,1},{2,18},{18,2},{3,19},{19,3},{4,20},{20... | collective-permute-start | bytes 4325384 | tf_op jit(solution)/shard_map/ppermute | solution.py:29
  123.1 18.3 %collective-permute-start.30 = (bf16[128,5632]{1,0:T(8,128)(2,1)S(1)}, bf16[128,5632]{1,0:T(8,128)(2,1)S(1)}, u32[]{:S(2)}, u32[]{:S(2)}) collective-permute-start(bf16[128,5632]{1,0:T(8,128)(2,1)S(1)} %collective-permute-done.13.refs_3_.refs_19_), channel_id=1, source_target_pairs={{0,16},{16,0},{1,17},{17,1},{2,18},{18,2},{3,19},{19,3},{4,20},{20... | collective-permute-start | bytes 4325384 | tf_op jit(solution)/shard_map/ppermute | solution.py:29
  138.2 25.5 %collective-permute-start.26 = (bf16[128,4096]{1,0:T(8,128)(2,1)}, bf16[128,4096]{1,0:T(8,128)(2,1)}, u32[]{:S(2)}, u32[]{:S(2)}) collective-permute-start(bf16[128,4096]{1,0:T(8,128)(2,1)} %collective-permute-done.15.refs_6_.refs_22_), channel_id=1, source_target_pairs={{0,2},{2,0},{4,6},{6,4},{8,10},{10,8},{12,14},{14,12},{1,3},{3,1},... | collective-permute-start | bytes 3145736 | tf_op jit(solution)/shard_map/ppermute | solution.py:73
  141.0 22.6 %collective-permute-start.24 = (bf16[128,3072]{1,0:T(8,128)(2,1)}, bf16[128,3072]{1,0:T(8,128)(2,1)}, u32[]{:S(2)}, u32[]{:S(2)}) collective-permute-start(bf16[128,3072]{1,0:T(8,128)(2,1)} %pad_maximum_fusion.4.refs_3_), channel_id=1, source_target_pairs={{0,16},{16,0},{1,17},{17,1},{2,18},{18,2},{3,19},{19,3},{4,20},{20... | collective-permute-start | bytes 2359304 | tf_op jit(solution)/shard_map/ppermute | solution.py:29
  141.4 24.4 %collective-permute-start.31 = (bf16[128,5632]{1,0:T(8,128)(2,1)S(1)}, bf16[128,5632]{1,0:T(8,128)(2,1)}, u32[]{:S(2)}, u32[]{:S(2)}) collective-permute-start(bf16[128,5632]{1,0:T(8,128)(2,1)S(1)} %collective-permute-done.12.refs_4_.refs_20_), channel_id=1, source_target_pairs={{0,16},{16,0},{1,17},{17,1},{2,18},{18,2},{3,19},{19,3},{4,20},{20... | collective-permute-start | bytes 4325384 | tf_op jit(solution)/shard_map/ppermute | solution.py:29
  142.5 23.9 %collective-permute-start.32 = (bf16[128,5632]{1,0:T(8,128)(2,1)}, bf16[128,5632]{1,0:T(8,128)(2,1)}, u32[]{:S(2)}, u32[]{:S(2)}) collective-permute-start(bf16[128,5632]{1,0:T(8,128)(2,1)} %collective-permute-done.23.refs_5_.refs_21_), channel_id=1, source_target_pairs={{0,16},{16,0},{1,17},{17,1},{2,18},{18,2},{3,19},{19,3},{4,20},{20... | collective-permute-start | bytes 4325384 | tf_op jit(solution)/shard_map/ppermute | solution.py:29
  142.8 23.4 %collective-permute-start.33 = (bf16[128,4096]{1,0:T(8,128)(2,1)}, bf16[128,4096]{1,0:T(8,128)(2,1)}, u32[]{:S(2)}, u32[]{:S(2)}) collective-permute-start(bf16[128,4096]{1,0:T(8,128)(2,1)} %collective-permute-done.15.refs_6_.refs_22_), channel_id=1, source_target_pairs={{0,16},{16,0},{1,17},{17,1},{2,18},{18,2},{3,19},{19,3},{4,20},{20... | collective-permute-start | bytes 3145736 | tf_op jit(solution)/shard_map/ppermute | solution.py:29
  163.7 33.8 %collective-permute-start.36 = (bf16[128,3072]{1,0:T(8,128)(2,1)}, bf16[128,3072]{1,0:T(8,128)(2,1)}, u32[]{:S(2)}, u32[]{:S(2)}) collective-permute-start(bf16[128,3072]{1,0:T(8,128)(2,1)} %pad_maximum_fusion.4.refs_3_), channel_id=1, source_target_pairs={{0,1},{1,0},{2,3},{3,2},{4,5},{5,4},{6,7},{7,6},{8,9},{9,8},{10,11... | collective-permute-start | bytes 2359304 | tf_op jit(solution)/shard_map/ppermute | solution.py:33
  165.9 40.6 %collective-permute-start.37 = (bf16[128,3072]{1,0:T(8,128)(2,1)}, bf16[128,3072]{1,0:T(8,128)(2,1)}, u32[]{:S(2)}, u32[]{:S(2)}) collective-permute-start(bf16[128,3072]{1,0:T(8,128)(2,1)} %copy-done.32), channel_id=1, source_target_pairs={{0,16},{16,0},{1,17},{17,1},{2,18},{18,2},{3,19},{19,3},{4,20},{20... | collective-permute-start | bytes 2359304 | tf_op jit(solution)/shard_map/ppermute | solution.py:29
  166.3 40.2 %collective-permute-start.38 = (bf16[128,3072]{1,0:T(8,128)(2,1)}, bf16[128,3072]{1,0:T(8,128)(2,1)}, u32[]{:S(2)}, u32[]{:S(2)}) collective-permute-start(bf16[128,3072]{1,0:T(8,128)(2,1)} %collective-permute-done.14.refs_5_), channel_id=1, source_target_pairs={{0,16},{16,0},{1,17},{17,1},{2,18},{18,2},{3,19},{19,3},{4,20},{20... | collective-permute-start | bytes 2359304 | tf_op jit(solution)/shard_map/ppermute | solution.py:29
  166.4 40.1 %collective-permute-start.39 = (bf16[128,3072]{1,0:T(8,128)(2,1)}, bf16[128,3072]{1,0:T(8,128)(2,1)}, u32[]{:S(2)}, u32[]{:S(2)}) collective-permute-start(bf16[128,3072]{1,0:T(8,128)(2,1)} %collective-permute-done.19.refs_6_), channel_id=1, source_target_pairs={{0,16},{16,0},{1,17},{17,1},{2,18},{18,2},{3,19},{19,3},{4,20},{20... | collective-permute-start | bytes 2359304 | tf_op jit(solution)/shard_map/ppermute | solution.py:29
  197.5 9.0 %collective-permute-start.40 = (bf16[128,3072]{1,0:T(8,128)(2,1)}, bf16[128,3072]{1,0:T(8,128)(2,1)S(1)}, u32[]{:S(2)}, u32[]{:S(2)}) collective-permute-start(bf16[128,3072]{1,0:T(8,128)(2,1)} %collective-permute-done.36.refs_7_), channel_id=1, source_target_pairs={{0,16},{16,0},{1,17},{17,1},{2,18},{18,2},{3,19},{19,3},{4,20},{20... | collective-permute-start | bytes 2359304 | tf_op jit(solution)/shard_map/ppermute | solution.py:29
  197.7 8.8 %collective-permute-start.35 = (bf16[128,1024]{1,0:T(8,128)(2,1)}, bf16[128,1024]{1,0:T(8,128)(2,1)S(1)}, u32[]{:S(2)}, u32[]{:S(2)}) collective-permute-start(bf16[128,1024]{1,0:T(8,128)(2,1)} %bitcast.112), channel_id=1, source_target_pairs={{0,1},{1,0},{2,3},{3,2},{4,5},{5,4},{6,7},{7,6},{8,9},{9,8},{10,11... | collective-permute-start | bytes 786440 | tf_op jit(solution)/shard_map/ppermute | solution.py:33
  206.5 43.8 %collective-permute-start.44 = (bf16[256,1024]{1,0:T(8,128)(2,1)}, bf16[256,1024]{1,0:T(8,128)(2,1)}, u32[]{:S(2)}, u32[]{:S(2)}) collective-permute-start(bf16[256,1024]{1,0:T(8,128)(2,1)} %bitcast.103), channel_id=1, source_target_pairs={{0,16},{16,0},{1,17},{17,1},{2,18},{18,2},{3,19},{19,3},{4,20},{20... | collective-permute-start | bytes 1572872 | tf_op jit(solution)/shard_map/ppermute | solution.py:29
  241.5 8.8 %collective-permute-start.43 = (bf16[128,1024]{1,0:T(8,128)(2,1)}, bf16[128,1024]{1,0:T(8,128)(2,1)}, u32[]{:S(2)}, u32[]{:S(2)}) collective-permute-start(bf16[128,1024]{1,0:T(8,128)(2,1)} %get-tuple-element.123), channel_id=1, source_target_pairs={{0,1},{1,0},{2,3},{3,2},{4,5},{5,4},{6,7},{7,6},{8,9},{9,8},{10,11... | collective-permute-start | bytes 786440 | tf_op jit(solution)/shard_map/ppermute | solution.py:33
  244.3 6.0 %collective-permute-start.45 = (bf16[3,128,1024]{2,1,0:T(8,128)(2,1)S(1)}, bf16[3,128,1024]{2,1,0:T(8,128)(2,1)}, u32[]{:S(2)}, u32[]{:S(2)}) collective-permute-start(bf16[3,128,1024]{2,1,0:T(8,128)(2,1)S(1)} %pad_maximum_fusion.6.states_own), channel_id=1, source_target_pairs={{0,16},{16,0},{1,17},{17,1},{2,18},{18,2},{3,19},{19,3},{4,20},{20... | collective-permute-start | bytes 2359304 | tf_op jit(solution)/shard_map/ppermute | solution.py:29
  245.0 5.3 %collective-permute-start.46 = (bf16[2,128,1024]{2,1,0:T(8,128)(2,1)S(1)}, bf16[2,128,1024]{2,1,0:T(8,128)(2,1)}, u32[]{:S(2)}, u32[]{:S(2)}) collective-permute-start(bf16[2,128,1024]{2,1,0:T(8,128)(2,1)S(1)} %copy-done.18), channel_id=1, source_target_pairs={{0,16},{16,0},{1,17},{17,1},{2,18},{18,2},{3,19},{19,3},{4,20},{20... | collective-permute-start | bytes 1572872 | tf_op jit(solution)/shard_map/ppermute | solution.py:29
  250.3 38.9 %collective-permute-start.48 = (bf16[3,128,1152]{2,1,0:T(8,128)(2,1)S(1)}, bf16[3,128,1152]{2,1,0:T(8,128)(2,1)S(1)}, u32[]{:S(2)}, u32[]{:S(2)}) collective-permute-start(bf16[3,128,1152]{2,1,0:T(8,128)(2,1)S(1)} %pad_maximum_fusion.1), channel_id=1, source_target_pairs={{0,1},{1,0},{2,3},{3,2},{4,5},{5,4},{6,7},{7,6},{8,9},{9,8},{10,11... | collective-permute-start | bytes 2654216 | tf_op jit(solution)/shard_map/ppermute | solution.py:33
  251.7 37.5 %collective-permute-start.47 = (bf16[2,128,1536]{2,1,0:T(8,128)(2,1)S(1)}, bf16[2,128,1536]{2,1,0:T(8,128)(2,1)S(1)}, u32[]{:S(2)}, u32[]{:S(2)}) collective-permute-start(bf16[2,128,1536]{2,1,0:T(8,128)(2,1)S(1)} %pad_maximum_fusion.5), channel_id=1, source_target_pairs={{0,1},{1,0},{2,3},{3,2},{4,5},{5,4},{6,7},{7,6},{8,9},{9,8},{10,11... | collective-permute-start | bytes 2359304 | tf_op jit(solution)/shard_map/ppermute | solution.py:33
  292.1 11.3 %collective-permute-start.51 = (bf16[256,2048]{1,0:T(8,128)(2,1)}, bf16[256,2048]{1,0:T(8,128)(2,1)S(1)}, u32[]{:S(2)}, u32[]{:S(2)}) collective-permute-start(bf16[256,2048]{1,0:T(8,128)(2,1)} %slice_bitcast_fusion), channel_id=1, source_target_pairs={{0,16},{16,0},{1,17},{17,1},{2,18},{18,2},{3,19},{19,3},{4,20},{20... | collective-permute-start | bytes 3145736 | tf_op jit(solution)/shard_map/ppermute | solution.py:29
  292.1 11.3 %collective-permute-start.57 = (bf16[3,128,1152]{2,1,0:T(8,128)(2,1)S(1)}, bf16[3,128,1152]{2,1,0:T(8,128)(2,1)}, u32[]{:S(2)}, u32[]{:S(2)}) collective-permute-start(bf16[3,128,1152]{2,1,0:T(8,128)(2,1)S(1)} %collective-permute-done.48.far), channel_id=1, source_target_pairs={{0,16},{16,0},{1,17},{17,1},{2,18},{18,2},{3,19},{19,3},{4,20},{20... | collective-permute-start | bytes 2654216 | tf_op jit(solution)/shard_map/ppermute | solution.py:29
  303.3 17.5 %collective-permute-start.52 = (f32[1024]{0:T(1024)}, f32[1024]{0:T(1024)S(1)}, u32[]{:S(2)}, u32[]{:S(2)}) collective-permute-start(f32[1024]{0:T(1024)} %bitcast.121), channel_id=1, source_target_pairs={{0,16},{16,0},{1,17},{17,1},{2,18},{18,2},{3,19},{19,3},{4,20},{20... | collective-permute-start | bytes 12296 | tf_op jit(solution)/shard_map/ppermute | solution.py:29
  319.6 36.6 %collective-permute-start.58 = (bf16[128,5120]{1,0:T(8,128)(2,1)}, bf16[128,5120]{1,0:T(8,128)(2,1)}, u32[]{:S(2)}, u32[]{:S(2)}) collective-permute-start(bf16[128,5120]{1,0:T(8,128)(2,1)} %get-tuple-element.147), channel_id=1, source_target_pairs={{0,2},{2,0},{4,6},{6,4},{8,10},{10,8},{12,14},{14,12},{1,3},{3,1},... | collective-permute-start | bytes 3932168 | tf_op jit(solution)/shard_map/ppermute | solution.py:73
  320.5 31.1 %collective-permute-start.59 = (bf16[256,768]{1,0:T(8,128)(2,1)}, bf16[256,768]{1,0:T(8,128)(2,1)S(1)}, u32[]{:S(2)}, u32[]{:S(2)}) collective-permute-start(bf16[256,768]{1,0:T(8,128)(2,1)} %get-tuple-element.150), channel_id=1, source_target_pairs={{0,4},{2,6},{4,8},{6,10},{8,12},{10,14},{12,0},{14,2},{1,5},{3,7},... | collective-permute-start | bytes 1179656 | tf_op jit(solution)/shard_map/ppermute | solution.py:76
  322.3 29.3 %collective-permute-start.53 = (f32[8,768]{1,0:T(8,128)S(1)}, f32[8,768]{1,0:T(8,128)S(1)}, u32[]{:S(2)}, u32[]{:S(2)}) collective-permute-start(f32[8,768]{1,0:T(8,128)S(1)} %reshape.191), channel_id=1, source_target_pairs={{0,2},{2,0},{4,6},{6,4},{8,10},{10,8},{12,14},{14,12},{1,3},{3,1},... | collective-permute-start | bytes 73736 | tf_op jit(solution)/shard_map/ppermute | solution.py:73
  324.4 34.5 %collective-permute-start.49 = (f32[16,16,1024]{2,1,0:T(8,128)S(1)}, f32[16,16,1024]{2,1,0:T(8,128)S(1)}, u32[]{:S(2)}, u32[]{:S(2)}) collective-permute-start(f32[16,16,1024]{2,1,0:T(8,128)S(1)} %bitcast.100), channel_id=1, source_target_pairs={{0,16},{16,0},{1,17},{17,1},{2,18},{18,2},{3,19},{19,3},{4,20},{20... | collective-permute-start | bytes 3145736 | tf_op jit(solution)/shard_map/ppermute | solution.py:29
  324.5 78.8 %collective-permute-start.62 = (bf16[256,768]{1,0:T(8,128)(2,1)}, bf16[256,768]{1,0:T(8,128)(2,1)}, u32[]{:S(2)}, u32[]{:S(2)}) collective-permute-start(bf16[256,768]{1,0:T(8,128)(2,1)} %get-tuple-element.155), channel_id=1, source_target_pairs={{4,0},{6,2},{8,4},{10,6},{12,8},{14,10},{0,12},{2,14},{5,1},{7,3},... | collective-permute-start | bytes 1179656 | tf_op jit(solution)/shard_map/ppermute | solution.py:79
  351.6 7.9 %collective-permute-start.54 = (f32[8,768]{1,0:T(8,128)S(1)}, f32[8,768]{1,0:T(8,128)S(1)}, u32[]{:S(2)}, u32[]{:S(2)}) collective-permute-start(f32[8,768]{1,0:T(8,128)S(1)} %add.237), channel_id=1, source_target_pairs={{0,4},{2,6},{4,8},{6,10},{8,12},{10,14},{12,0},{14,2},{1,5},{3,7},... | collective-permute-start | bytes 73736 | tf_op jit(solution)/shard_map/ppermute | solution.py:76
  351.6 8.6 %collective-permute-start.55 = (f32[8,768]{1,0:T(8,128)S(1)}, f32[8,768]{1,0:T(8,128)S(1)}, u32[]{:S(2)}, u32[]{:S(2)}) collective-permute-start(f32[8,768]{1,0:T(8,128)S(1)} %add.237), channel_id=1, source_target_pairs={{4,0},{6,2},{8,4},{10,6},{12,8},{14,10},{0,12},{2,14},{5,1},{7,3},... | collective-permute-start | bytes 73736 | tf_op jit(solution)/shard_map/ppermute | solution.py:79
  358.9 44.4 %collective-permute-start.63 = (bf16[256,768]{1,0:T(8,128)(2,1)}, bf16[256,768]{1,0:T(8,128)(2,1)}, u32[]{:S(2)}, u32[]{:S(2)}) collective-permute-start(bf16[256,768]{1,0:T(8,128)(2,1)} %add_convert_fusion.3), channel_id=1, source_target_pairs={{0,4},{2,6},{4,8},{6,10},{8,12},{10,14},{12,0},{14,2},{1,5},{3,7},... | collective-permute-start | bytes 1179656 | tf_op jit(solution)/shard_map/ppermute | solution.py:76
  358.9 45.9 %collective-permute-start.60 = (bf16[128,5120]{1,0:T(8,128)(2,1)}, bf16[128,5120]{1,0:T(8,128)(2,1)}, u32[]{:S(2)}, u32[]{:S(2)}) collective-permute-start(bf16[128,5120]{1,0:T(8,128)(2,1)} %get-tuple-element.151), channel_id=1, source_target_pairs={{0,2},{2,0},{4,6},{6,4},{8,10},{10,8},{12,14},{14,12},{1,3},{3,1},... | collective-permute-start | bytes 3932168 | tf_op jit(solution)/shard_map/ppermute | solution.py:73
  359.5 45.3 %collective-permute-start.61 = (bf16[128,5120]{1,0:T(8,128)(2,1)}, bf16[128,5120]{1,0:T(8,128)(2,1)}, u32[]{:S(2)}, u32[]{:S(2)}) collective-permute-start(bf16[128,5120]{1,0:T(8,128)(2,1)} %add_convert_fusion.2), channel_id=1, source_target_pairs={{0,4},{2,6},{4,8},{6,10},{8,12},{10,14},{12,0},{14,2},{1,5},{3,7},... | collective-permute-start | bytes 3932168 | tf_op jit(solution)/shard_map/ppermute | solution.py:76
  360.2 39.6 %collective-permute-start.56 = (f32[8,768]{1,0:T(8,128)S(1)}, f32[8,768]{1,0:T(8,128)S(1)}, u32[]{:S(2)}, u32[]{:S(2)}) collective-permute-start(f32[8,768]{1,0:T(8,128)S(1)} %collective-permute-done.54), channel_id=1, source_target_pairs={{0,4},{2,6},{4,8},{6,10},{8,12},{10,14},{12,0},{14,2},{1,5},{3,7},... | collective-permute-start | bytes 73736 | tf_op jit(solution)/shard_map/ppermute | solution.py:76
  399.8 26.0 %collective-permute-start.50 = (f32[32,16,1024]{2,1,0:T(8,128)}, f32[32,16,1024]{2,1,0:T(8,128)}, u32[]{:S(2)}, u32[]{:S(2)}) collective-permute-start(f32[32,16,1024]{2,1,0:T(8,128)} %pad_maximum_fusion), channel_id=1, source_target_pairs={{0,1},{17,16},{2,3},{19,18},{4,5},{21,20},{6,7},{23,22},{8,9},{25,... | collective-permute-start | bytes 6291464 | tf_op jit(solution)/shard_map/ppermute | solution.py:1012
  408.4 32.8 %collective-permute-start.64 = (bf16[128,5120]{1,0:T(8,128)(2,1)}, bf16[128,5120]{1,0:T(8,128)(2,1)}, u32[]{:S(2)}, u32[]{:S(2)}) collective-permute-start(bf16[128,5120]{1,0:T(8,128)(2,1)} %get-tuple-element.158), channel_id=1, source_target_pairs={{0,2},{2,0},{4,6},{6,4},{8,10},{10,8},{12,14},{14,12},{1,3},{3,1},... | collective-permute-start | bytes 3932168 | tf_op jit(solution)/shard_map/ppermute | solution.py:73
  409.0 32.3 %collective-permute-start.65 = (bf16[128,5120]{1,0:T(8,128)(2,1)}, bf16[128,5120]{1,0:T(8,128)(2,1)}, u32[]{:S(2)}, u32[]{:S(2)}) collective-permute-start(bf16[128,5120]{1,0:T(8,128)(2,1)} %add_convert_fusion.1), channel_id=1, source_target_pairs={{0,4},{2,6},{4,8},{6,10},{8,12},{10,14},{12,0},{14,2},{1,5},{3,7},... | collective-permute-start | bytes 3932168 | tf_op jit(solution)/shard_map/ppermute | solution.py:76
  410.2 30.9 %collective-permute-start.68 = (bf16[128,1024]{1,0:T(8,128)(2,1)S(1)}, bf16[128,1024]{1,0:T(8,128)(2,1)S(1)}, u32[]{:S(2)}, u32[]{:S(2)}) collective-permute-start(bf16[128,1024]{1,0:T(8,128)(2,1)S(1)} %pad_maximum_fusion.8), channel_id=1, source_target_pairs={{0,2},{2,0},{4,6},{6,4},{8,10},{10,8},{12,14},{14,12},{1,3},{3,1},... | collective-permute-start | bytes 786440 | tf_op jit(solution)/shard_map/ppermute | solution.py:73
  427.6 17.1 %collective-permute-start.67 = (bf16[128,4096]{1,0:T(8,128)(2,1)S(1)}, bf16[128,4096]{1,0:T(8,128)(2,1)S(1)}, u32[]{:S(2)}, u32[]{:S(2)}) collective-permute-start(bf16[128,4096]{1,0:T(8,128)(2,1)S(1)} %copy-done.29), channel_id=1, source_target_pairs={{0,0},{1,16},{16,1},{17,17},{2,2},{3,18},{18,3},{19,19},{4,4},{5,2... | collective-permute-start | bytes 3145736 | tf_op jit(solution)/shard_map/ppermute | solution.py:37
  444.7 15.5 %collective-permute-start.72 = (bf16[128,1536]{1,0:T(8,128)(2,1)S(1)}, bf16[128,1536]{1,0:T(8,128)(2,1)S(1)}, u32[]{:S(2)}, u32[]{:S(2)}) collective-permute-start(bf16[128,1536]{1,0:T(8,128)(2,1)S(1)} %pad_maximum_fusion.7), channel_id=1, source_target_pairs={{0,4},{2,6},{4,8},{6,10},{8,12},{10,14},{12,0},{14,2},{1,5},{3,7},... | collective-permute-start | bytes 1179656 | tf_op jit(solution)/shard_map/ppermute | solution.py:76
  444.7 14.5 %collective-permute-start.73 = (bf16[128,512]{1,0:T(8,128)(2,1)S(1)}, bf16[128,512]{1,0:T(8,128)(2,1)}, u32[]{:S(2)}, u32[]{:S(2)}) collective-permute-start(bf16[128,512]{1,0:T(8,128)(2,1)S(1)} %get-tuple-element.168), channel_id=1, source_target_pairs={{4,0},{6,2},{8,4},{10,6},{12,8},{14,10},{0,12},{2,14},{5,1},{7,3},... | collective-permute-start | bytes 393224 | tf_op jit(solution)/shard_map/ppermute | solution.py:79
  449.3 11.0 %collective-permute-start.71 = (bf16[128,1024]{1,0:T(8,128)(2,1)}, bf16[128,1024]{1,0:T(8,128)(2,1)}, u32[]{:S(2)}, u32[]{:S(2)}) collective-permute-start(bf16[128,1024]{1,0:T(8,128)(2,1)} %slice.248), channel_id=1, source_target_pairs={{0,2},{2,0},{4,6},{6,4},{8,10},{10,8},{12,14},{14,12},{1,3},{3,1},... | collective-permute-start | bytes 786440 | tf_op jit(solution)/shard_map/ppermute | solution.py:73
  450.6 35.9 %collective-permute-start.69 = (bf16[128,4096]{1,0:T(8,128)(2,1)}, bf16[128,4096]{1,0:T(8,128)(2,1)S(1)}, u32[]{:S(2)}, u32[]{:S(2)}) collective-permute-start(bf16[128,4096]{1,0:T(8,128)(2,1)} %slice.243), channel_id=1, source_target_pairs={{0,2},{1,18},{16,3},{17,19},{2,0},{3,16},{18,1},{19,17},{4,6},{5,2... | collective-permute-start | bytes 3145736 | tf_op jit(solution)/shard_map/ppermute | solution.py:1029
  452.1 34.4 %collective-permute-start.70 = (bf16[128,4096]{1,0:T(8,128)(2,1)}, bf16[128,4096]{1,0:T(8,128)(2,1)}, u32[]{:S(2)}, u32[]{:S(2)}) collective-permute-start(bf16[128,4096]{1,0:T(8,128)(2,1)} %slice.297), channel_id=1, source_target_pairs={{0,4},{1,20},{16,5},{17,21},{2,6},{3,22},{18,7},{19,23},{4,8},{5,2... | collective-permute-start | bytes 3145736 | tf_op jit(solution)/shard_map/ppermute | solution.py:1029
  460.2 25.3 %collective-permute-start.74 = (bf16[128,512]{1,0:T(8,128)(2,1)S(1)}, bf16[128,512]{1,0:T(8,128)(2,1)S(1)}, u32[]{:S(2)}, u32[]{:S(2)}) collective-permute-start(bf16[128,512]{1,0:T(8,128)(2,1)S(1)} %slice.324), channel_id=1, source_target_pairs={{0,4},{2,6},{4,8},{6,10},{8,12},{10,14},{12,0},{14,2},{1,5},{3,7},... | collective-permute-start | bytes 393224 | tf_op jit(solution)/shard_map/ppermute | solution.py:76
  (76 other events, 1269.1 us)

commit v6 on v5

--- a/solution.py
+++ b/solution.py
@@ -361,6 +361,7 @@
     (
         grad_own, grad_given, pack_me, pack_chip, pack_cores, seen, near, far,
         memory, decoded, grad_memory, pack, sums, w, v, sems, v_sems, mk, sk, mq, sq, mono, span, keep, queue, scaled, ratio, window, mix, pre,
+        mono_squash, span_squash,
     ) = refs[4 * count + 4 :]
     rows, _ = kept.shape
     frames, group, _ = mk.shape
@@ -421,15 +422,18 @@
     def spread(row, c):
         return jnp.broadcast_to(vectors[row : row + 1, lane(c)], (group, lanes))
 
-    def energies(queries, keys, vec_row, energy):
+    def energies(queries, keys, vec_row, energy, kept_squash):
         weights = [spread(vec_row, c) for c in range(chunks)]
 
         def one(i, carried):
             query = [queries[i, :, lane(c)] for c in range(chunks)]
             for j in range(frames):
-                total = jnp.tanh(query[0] + keys[j, :, lane(0)]) * weights[0]
-                for c in range(1, chunks):
-                    total = total + jnp.tanh(query[c] + keys[j, :, lane(c)]) * weights[c]
+                total = None
+                for c in range(chunks):
+                    squash = jnp.tanh(query[c] + keys[j, :, lane(c)])
+                    kept_squash[i * frames + j, :, lane(c)] = squash
+                    part = squash * weights[c]
+                    total = part if total is None else total + part
                 energy[i * frames + j] = jnp.broadcast_to(
                     jnp.sum(total, axis=-1, keepdims=True), (group, lanes)
                 )
@@ -437,8 +441,8 @@
 
         lax.fori_loop(0, frames, one, 0)
 
-    energies(mq, mk, 1, mono)
-    energies(sq, sk, 3, span)
+    energies(mq, mk, 1, mono, mono_squash)
+    energies(sq, sk, 3, span, span_squash)
 
     length = lengths[...]
     valid = [(length > j) for j in range(frames)]
@@ -574,18 +578,17 @@
 
     lax.fori_loop(0, frames, unattend, tuple([zeros] * frames))
 
-    def energy_back(queries, keys, energy, bias_row, vec_row):
+    def energy_back(queries, keys, energy, kept_squash, bias_row, vec_row):
         def one_chunk(c, carried):
             at = pl.ds(pl.multiple_of(c * lanes, lanes), lanes)
             weight = jnp.broadcast_to(vectors[vec_row : vec_row + 1, at], (group, lanes))
 
             def one(i, carry):
                 grad_keys, vec_total, bias_total = carry
-                query = queries[i, :, at]
                 grad_query = zeros
                 new_keys = []
                 for j in range(frames):
-                    squash = jnp.tanh(query + keys[j, :, at])
+                    squash = kept_squash[i * frames + j, :, at]
                     grad = energy[i * frames + j]
                     scaled_squash = grad * squash
                     vec_total = vec_total + scaled_squash
@@ -606,8 +609,8 @@
 
         lax.fori_loop(0, chunks, one_chunk, 0)
 
-    energy_back(mq, mk, mono, 0, 1)
-    energy_back(sq, sk, span, 2, 3)
+    energy_back(mq, mk, mono, mono_squash, 0, 1)
+    energy_back(sq, sk, span, span_squash, 2, 3)
 
     total_memory = grad_memory[...]
     total_decoded = jnp.zeros_like(total_memory)
@@ -671,7 +674,8 @@
         ]
         + [pltpu.VMEM((frames, group, full), wide)] * 4
         + [pltpu.VMEM(cell, wide)] * 7
-        + [pltpu.VMEM((frames, group, 128), wide), pltpu.VMEM((rows, full), wide)],
+        + [pltpu.VMEM((frames, group, 128), wide), pltpu.VMEM((rows, full), wide)]
+        + [pltpu.VMEM((frames * frames, group, full), wide)] * 2,
         compiler_params=pltpu.CompilerParams(vmem_limit_bytes=56 << 20),
         name="attend",
     )(
@@ -705,7 +709,7 @@
         (
             (
                 states_own.at[1], states_core.at[1],
-                far.at[2, :, :width], far_core.at[2, :, :width],
+                states_own.at[3], states_core.at[3],
             ),
             states.at[1 - y],
         ),
@@ -722,18 +726,35 @@
             )
     for job in jobs:
         job.start()
-    for job in jobs:
+    for job in jobs[:6]:
         job.wait()
+    both = 2 * wide_half
 
     def one(n, carried):
         cols = pl.ds(pl.multiple_of(order[1 + n] * height, height), height)
-        both = jnp.concatenate([a_rec[:, cols], a_in[:, cols]], axis=1)
+        pair = jnp.concatenate([a_rec[:, cols], a_in[:, cols]], axis=1)
         for at in range(0, wide_half, 1024):
-            value = dot_tn(both, a_dz[:, at : at + 1024]).astype(low)
+            value = dot_tn(pair, a_dz[:, at : at + 1024]).astype(low)
             block[n, :, at : at + 1024] = value[:height]
             block[n, :, wide_half + at : wide_half + at + 1024] = value[height:]
+        for m, output in enumerate(outputs):
+
+            @pl.when(n == m)
+            def _(m=m, output=output):
+                pltpu.make_async_copy(
+                    block.at[m, :, :both], output.at[:, :both], out_sems.at[m]
+                ).start()
+
+        return carried
+
+    lax.fori_loop(0, 8, one, 0)
+    for job in jobs[6:]:
+        job.wait()
+
+    def two(n, carried):
+        cols = pl.ds(pl.multiple_of(order[1 + n] * height, height), height)
         for m in range(2):
-            to = 2 * wide_half + 2 * m * part
+            to = both + 2 * m * part
             block[n, :, to : to + 2 * part] = dot_tn(
                 states[m, :, cols], a_pack[:, 2 * m * part : 2 * (m + 1) * part]
             ).astype(low)
@@ -741,11 +762,13 @@
 
             @pl.when(n == m)
             def _(m=m, output=output):
-                pltpu.make_async_copy(block.at[m], output, out_sems.at[m]).start()
+                pltpu.make_async_copy(
+                    block.at[m, :, both:], output.at[:, both:], out_sems.at[12 + m]
+                ).start()
 
         return carried
 
-    lax.fori_loop(0, 8, one, 0)
+    lax.fori_loop(0, 8, two, 0)
 
     def pair(n, carried):
         cols = pl.ds(pl.multiple_of(order[9 + n] * 2 * height, 2 * height), 2 * height)
@@ -764,7 +787,12 @@
     for m, output in enumerate(paired):
         pltpu.make_async_copy(paired_block.at[m], output, out_sems.at[8 + m]).start()
     for m, output in enumerate(outputs):
-        pltpu.make_async_copy(block.at[m], output, out_sems.at[m]).wait()
+        pltpu.make_async_copy(
+            block.at[m, :, :both], output.at[:, :both], out_sems.at[m]
+        ).wait()
+        pltpu.make_async_copy(
+            block.at[m, :, both:], output.at[:, both:], out_sems.at[12 + m]
+        ).wait()
     for m, output in enumerate(paired):
         pltpu.make_async_copy(paired_block.at[m], output, out_sems.at[8 + m]).wait()
 
@@ -795,7 +823,7 @@
             pltpu.VMEM((8, height, columns), low),
             pltpu.VMEM((4, 2 * height, 3 * part), low),
             pltpu.SemaphoreType.DMA((26,)),
-            pltpu.SemaphoreType.DMA((12,)),
+            pltpu.SemaphoreType.DMA((20,)),
         ],
         compiler_params=pltpu.CompilerParams(vmem_limit_bytes=56 << 20),
         name="weight_gradients",
@@ -853,7 +881,7 @@
     places, in_own, rec_own, small_own, small_chip = [], [], [], [], []
     small = jnp.concatenate(
         [
-            tie(mono_mem, in_shard, rec_shard), span_mem, mono_dec, span_dec,
+            mono_mem, span_mem, mono_dec, span_dec,
             out_weight[0], out_weight[1],
         ],
         axis=1,
@@ -861,15 +889,21 @@
     if ring.short:
         flow, across, onward = Flow(), ring.across, ring.onward
         both = 2 * wide_half
-        corner_in, corner_rec, b_own = flow.step(
-            (corners, in_shard), (corners, rec_shard), (corners, bias_shard)
+        for k in range(ring.outer):
+            places += [ring.back(k) * 2 + ring.x, ring.back(k) * 2 + 1 - ring.x]
+        places = jnp.stack([s, y] + places).astype(jnp.int32)
+        corner = jnp.concatenate([in_shard, rec_shard], axis=1)
+        small = jnp.concatenate(
+            [
+                tie(mono_mem, corner), span_mem, mono_dec, span_dec, out_weight[0], out_weight[1]
+            ],
+            axis=1,
         )
-        small_far, small_next = across(small), onward(small)
-        flow.landed += (small_far, small_next)
-        b_own = b_own.astype(wide)
+        corner, small_far, small_next = corners(corner), across(small), onward(small)
+        flow.landed = (corner, small_far, small_next)
         small_own = [jnp.concatenate([small, small_far], axis=1)]
         small_chip, small_core = [], []
-        held = jnp.concatenate([corner_in, corner_rec, small_next], axis=1)
+        held = jnp.concatenate([corner, small_next], axis=1)
         near, far, near_core, far_core = [], [], [], []
         for k in range(ring.outer):
             near.append(held)
@@ -877,13 +911,21 @@
             if k < ring.outer - 1:
                 jobs.append((onward, held[:, :both] if k == ring.outer - 2 else held))
             if k == 0:
-                jobs += [(across_chips, vocab_own), (across_chips, vector_own)]
-            results = flow.step(*jobs, also=ready if k == 1 else ())
+                jobs += [(across_chips, vocab_own), (corners, bias_shard)]
+            if k == 1:
+                jobs.append((across_chips, vector_own))
+            also = ready if k == 1 else ()
+            if k == ring.outer - 1:
+                vectors = jnp.concatenate([vector_pair, across_cores(vector_pair)], axis=1)
+                vectors = jnp.pad(vectors, ((0, 3), (0, 0)))
+                also = (vectors, places)
+            results = flow.step(*jobs, also=also)
             far.append(results[0])
             small_chip.append(results[1])
             if k == 0:
-                vocab_chip, vector_pair = results[3:]
-                vector_pair = jnp.concatenate([vector_own, vector_pair], axis=1)
+                vocab_chip, b_own = results[3], results[4].astype(wide)
+            if k == 1:
+                vector_pair = jnp.concatenate([vector_own, results[3]], axis=1)
             if k < ring.outer - 1:
                 small_own.append(jnp.concatenate([held[:, both:], far[k][:, both:]], axis=1))
                 held = results[2]
@@ -891,17 +933,14 @@
             near_core.append(across_cores(a))
             far_core.append(across_cores(b))
         small_core = [across_cores(a) for a in small_own]
-        b_last, vocab_last, chip_last, vector_last = lax.optimization_barrier(
-            (b_own, vocab_own, vocab_chip, vector_pair, held)
-        )[:4]
+        b_last, vocab_last, chip_last = lax.optimization_barrier(
+            (b_own, vocab_own, vocab_chip, held)
+        )[:3]
         b_other = across_cores(b_last)
         vocab = [vocab_own, vocab_chip, across_cores(vocab_last), across_cores(chip_last)]
-        vector_core = across_cores(vector_last)
         in_own = [a for pair in zip(near, far) for a in pair]
         in_other = [a for pair in zip(near_core, far_core) for a in pair]
         rec_own, rec_other, rec_column = in_own, in_other, wide_half
-        for k in range(ring.outer):
-            places += [ring.back(k) * 2 + ring.x, ring.back(k) * 2 + 1 - ring.x]
     else:
         vocab_chip = across_chips(vocab_own)
         small, in_block, rec_block = [
@@ -917,10 +956,9 @@
         b_other = across_cores(b_own)
         vector_pair = across_chips(vector_own)
         vector_pair = jnp.concatenate([vector_own, vector_pair], axis=1)
-        vector_core = across_cores(vector_pair)
-    vectors = jnp.concatenate([vector_pair, vector_core], axis=1)
-    vectors = jnp.pad(vectors, ((0, 3), (0, 0)))
-    places = jnp.stack([s, y] + places).astype(jnp.int32)
+        vectors = jnp.concatenate([vector_pair, across_cores(vector_pair)], axis=1)
+        vectors = jnp.pad(vectors, ((0, 3), (0, 0)))
+        places = jnp.stack([s, y] + places).astype(jnp.int32)
     places = tie(places, vectors, *vocab, *ready, *small_chip[:-1], *small_core)
 
     kept, given, before, gates, cells = run_forward(
@@ -937,6 +975,7 @@
         places, kept, taken, smalls, vocab, vectors, bias_row, noise_part, length_part,
         label_part, counted, frames,
     )
+    grad_given, kept_far = lax.optimization_barrier((grad_given, across_chips(tie(kept, taken))))
     grad_taken = across_chips(grad_given)
     pack_core = across_cores(pack_cores)
     pack_out = jnp.stack([pack_chip, pack_core[1]])
@@ -944,17 +983,13 @@
     vector_pair = (near[:5] + far_peer[:5]).reshape(5, 2, block)
     bias_pair = (far[8:10] + far_peer[8:10]).reshape(-1)
     vector_out = jnp.concatenate([vector_pair[:, 1].reshape(-1), bias_pair])
-    vector_count = vector_out.shape[0] // (3 * rows)
+    vector_count = vector_out.shape[0] // (2 * rows)
     seen_out = jnp.concatenate(
-        [
-            jnp.concatenate([seen, kept[None]], axis=0),
-            halves(vector_out, 3 * rows).reshape(3, rows, -1),
-        ],
-        axis=2,
+        [seen, halves(vector_out, 2 * rows).reshape(2, rows, -1)], axis=2
     )
     before = before.reshape(frames * half, width)
     before_peer = across_cores(tie(before, taken))
-    states = jnp.stack([tie(kept, grad_given), taken, given])
+    states = jnp.stack([tie(kept, grad_given), taken, given, kept_far])
     states_core, seen_core = across_cores(states), across_cores(seen)
     places_back, pack_out, seen_out = lax.optimization_barrier(
         (places, pack_out, seen_out, grad_taken, before_peer, states_core, seen_core)
@@ -986,7 +1021,7 @@
         pack_me, pack_core, pack_far,
     )
     grad_inputs = jnp.swapaxes(grad_inputs.reshape(frames, half, width), 0, 1)
-    vector_far = joined(seen_far[:, :, width:].reshape(3 * rows, -1), vector_count).reshape(-1)
+    vector_far = joined(seen_far[:, :, width:].reshape(2 * rows, -1), vector_count).reshape(-1)
 
     sides_at = 5 * block + vocab_pad
     grad_peer = across_cores(grad_inputs)

time: 493 us -> 492 us (level)
  waiting for transfers between devices: 233 us -> 216 us
  starting transfers between devices: 63.2 us -> 78.7 us
    ppermute x10 -> x11, waiting for transfers between devices: 39.8 us -> 24.3 us  [across_chips(): return lax.ppermute(array, 'mp', core_swap)]
    ppermute x5 -> x4, starting transfers between devices: 5 us -> 12.5 us  [corners(): return lax.ppermute(array, ('section', 'mp'), corner_swap)]
    ppermute x12, starting transfers between devices: 6.1 us -> 13.1 us  [onward(): return lax.ppermute(array, 'dp', self.ring)]
    ppermute x10 -> x11, starting transfers between devices: 16.7 us -> 19.3 us  [across_chips(): return lax.ppermute(array, 'mp', core_swap)]
    unnamed x144 -> x156, local copies, waits for them, and re-layouts: 15.4 us -> 13.8 us
  transfers between devices with their start and end apart: 75 -> 75, of which waited for: 19 -> 23; matrix products, arithmetic and copies ran while one was open for 11% -> 12% of each run, Pallas kernels for 24% -> 24%
where the time goes in v6:
time: 492 us; the launch traced here: 489 us
  waiting for transfers between devices  216 us (44%)
  Pallas kernels  117 us (24%)
  starting transfers between devices  78.7 us (16%)
  local copies, waits for them, and re-layouts  46.7 us (9%)
  other arithmetic  29.4 us (6%)
    ppermute x11, waiting for transfers between devices, across(): return lax.ppermute(array, 'dp', self.pair)  113 us
    ppermute x12, waiting for transfers between devices, onward(): return lax.ppermute(array, 'dp', self.ring)  58.6 us
    pallas_call x1, Pallas kernels, run_attend(): pl.pallas_call(functools.partial(attend_kernel, count), out_shape=(jax.Sh...  31.9 us
    pallas_call x1, Pallas kernels, run_forward(): pl.pallas_call(functools.partial(forward_kernel, count, column), out_shap...  30.6 us
    pallas_call x1, Pallas kernels, run_backward(): pl.pallas_call(functools.partial(backward_kernel, count, column), out_sha...  30.2 us
    ppermute x11, waiting for transfers between devices, across_chips(): return lax.ppermute(array, 'mp', core_swap)  24.3 us
    ppermute x11, starting transfers between devices, across_chips(): return lax.ppermute(array, 'mp', core_swap)  19.3 us
    pallas_call x1, Pallas kernels, run_gradients(): pl.pallas_call(gradient_kernel, out_shape=tuple([jax.ShapeDtypeStruct((he...  15.2 us
  transfers between devices with their start and end apart: 75, of which 23 were waited for; matrix products, arithmetic and copies ran while one was open for 12% of the time, Pallas kernels for 24%

profile of v6, /device:TPU:0, one launch (start us, length us, event | category | flops | bytes accessed | tf_op | source)
XLA Modules:
  0.0 489.1 jit_solution(6602633046435069326)
XLA Ops:
  0.7 1.2 copy.73
  3.8 9.6 %collective-permute-start = (bf16[128,4096]{1,0:T(8,128)(2,1)}, bf16[128,4096]{1,0:T(8,128)(2,1)}, u32[]{:S(2)}, u32[]{:S(2)}) collective-permute-start(bf16[128,4096]{1,0:T(8,128)(2,1)} %constant_dynamic-update-slice_fusion), channel_id=1, source_target_pairs={{0,0},{1,16},{16,1},{17,17},{2,2},{3,18},{18,3},{19,19},{4,4},{5,2... | collective-permute-start | bytes 3145736 | tf_op jit(solution)/shard_map/ppermute | solution.py:37
  17.3 3.0 collective-permute-start.1
  20.3 1.5 collective-permute-start.2
  26.1 1.9 collective-permute-done.2
  28.9 1.3 constant_dynamic-update-slice_fusion.7
  30.2 1.6 collective-permute-start.3
  31.8 1.5 collective-permute-start.4
  33.3 2.0 collective-permute-start.6
  35.4 1.3 collective-permute-start.7
  38.2 1.1 copy.63
  40.4 22.9 %collective-permute-done.4.refs_1_.refs_17_ = bf16[128,5632]{1,0:T(8,128)(2,1)} collective-permute-done((bf16[128,5632]{1,0:T(8,128)(2,1)S(1)}, bf16[128,5632]{1,0:T(8,128)(2,1)}, u32[]{:S(2)}, u32[]{:S(2)}) %collective-permute-start.4) | collective-permute-done | bytes 1441824 | tf_op jit(solution)/shard_map/ppermute | solution.py:73
  65.4 1.3 broadcast_in_dim.17.noise
  67.9 1.6 collective-permute-start.12
  70.2 1.3 collective-permute-start.10
  72.5 25.6 %collective-permute-done.13.refs_3_.refs_19_ = bf16[128,5632]{1,0:T(8,128)(2,1)} collective-permute-done((bf16[128,5632]{1,0:T(8,128)(2,1)}, bf16[128,5632]{1,0:T(8,128)(2,1)}, u32[]{:S(2)}, u32[]{:S(2)}) %collective-permute-start.13) | collective-permute-done | bytes 1441824 | tf_op jit(solution)/shard_map/ppermute | solution.py:73
  99.9 1.2 slice.281
  101.1 1.6 collective-permute-start.22
  102.7 4.5 collective-permute-start.18
  107.9 2.7 collective-permute-done.11
  110.7 14.8 %collective-permute-done.18.refs_6_ = bf16[128,3072]{1,0:T(8,128)(2,1)} collective-permute-done((bf16[128,3072]{1,0:T(8,128)(2,1)S(1)}, bf16[128,3072]{1,0:T(8,128)(2,1)}, u32[]{:S(2)}, u32[]{:S(2)}) %collective-permute-start.18) | collective-permute-done | bytes 786464 | tf_op jit(solution)/shard_map/ppermute | solution.py:33
  125.5 4.7 collective-permute-done.22.refs_5_.refs_21_
  131.9 2.7 collective-permute-done.15.refs_6_.refs_22_
  137.0 1.1 collective-permute-done.24.b_other
  139.2 22.1 %collective-permute-done.25.refs_7_.refs_23_ = bf16[128,4096]{1,0:T(8,128)(2,1)S(1)} collective-permute-done((bf16[128,4096]{1,0:T(8,128)(2,1)}, bf16[128,4096]{1,0:T(8,128)(2,1)S(1)}, u32[]{:S(2)}, u32[]{:S(2)}) %collective-permute-start.25) | collective-permute-done | bytes 1048608 | tf_op jit(solution)/shard_map/ppermute | solution.py:73
  161.4 6.2 %collective-permute-start.35 = (bf16[128,3072]{1,0:T(8,128)(2,1)}, bf16[128,3072]{1,0:T(8,128)(2,1)}, u32[]{:S(2)}, u32[]{:S(2)}) collective-permute-start(bf16[128,3072]{1,0:T(8,128)(2,1)} %pad_maximum_fusion.4.refs_3_), channel_id=1, source_target_pairs={{0,1},{1,0},{2,3},{3,2},{4,5},{5,4},{6,7},{7,6},{8,9},{9,8},{10,11... | collective-permute-start | bytes 2359304 | tf_op jit(solution)/shard_map/ppermute | solution.py:33
  170.0 30.6 %recur_forward.1 = (bf16[16,8,1024]{2,1,0:T(8,128)(2,1)}, bf16[16,8,1024]{2,1,0:T(8,128)(2,1)}, bf16[16,16,1024]{2,1,0:T(8,128)(2,1)}, f32[16,16,4096]{2,1,0:T(8,128)}, f32[16,16,1024]{2,1,0:T(8,128)}) custom-call(s32[10]{0:T(128)} %stack.116.places, bf16[256,1024]{1,0:T(8,128)(2,1)} %bitcast.89, f32[1,2048]{1,0:T(1,128)} %copy-done.51, ...), custom_call_target="tpu_custom_call" | custom-call | tf_op jit(solution)/shard_map/recur_forward/pallas_call | solution.py:184
  201.4 8.2 %collective-permute-done.34.taken = bf16[128,1024]{1,0:T(8,128)(2,1)S(1)} collective-permute-done((bf16[128,1024]{1,0:T(8,128)(2,1)}, bf16[128,1024]{1,0:T(8,128)(2,1)S(1)}, u32[]{:S(2)}, u32[]{:S(2)}) %collective-permute-start.34) | collective-permute-done | bytes 262176 | tf_op jit(solution)/shard_map/ppermute | solution.py:33
  213.6 31.9 %attend.1 = (f32[128,1024]{1,0:T(8,128)}, bf16[128,1024]{1,0:T(8,128)(2,1)}, bf16[128,1536]{1,0:T(8,128)(2,1)}, bf16[128,1536]{1,0:T(8,128)(2,1)}, bf16[2,128,15...) custom-call(s32[10]{0:T(128)} %stack.116.places, ...), custom_call_target="tpu_custom_call" | custom-call | tf_op jit(solution)/shard_map/attend/pallas_call | solution.py:650
  245.5 1.4 collective-permute-start.43
  247.5 1.2 pad_maximum_fusion.1.states_own
  251.0 1.3 pad_maximum_fusion.5
  252.4 1.4 collective-permute-done.43
  254.4 1.4 collective-permute-start.47
  256.5 30.2 %recur_backward.1 = bf16[2,16,16,2048]{3,2,1,0:T(8,128)(2,1)} custom-call(s32[10]{0:T(128)} %stack.116.places, f32[16,8,1024]{2,1,0:T(8,128)} %bitcast.105, bf16[16,8,1024]{2,1,0:T(8,128)(2,1)} %bitcast.112, f32[16,16,4096]{2,1,0:T(8,128)} %get-tuple-element.129.gates, f32[16,16,1024]{2,1,0:T(8,128)} %get-tuple-element.130.cells, ...), custom_call_target="tpu_custom_call" | custom-call | tf_op jit(solution)/shard_map/recur_backward/pallas_call | solution.py:286
  286.7 1.6 slice_bitcast_fusion
  291.4 8.9 %input_back.1 = (f32[256,1024]{1,0:T(8,128)}, f32[1,1024]{1,0:T(1,128)}) custom-call(s32[10]{0:T(128)} %stack.116.places, bf16[256,1024]{1,0:T(8,128)(2,1)} %bitcast.94, f32[1,1024]{1,0:T(1,128)} %bitcast.117, bf16[2,256,2048]{2,1,0:T(8,128)(2,1)} %bitcast.86, bf16[128,5632]{1,0:T(8,128)(2,1)} %copy-done.4, ...), custom_call_target="tpu_custom_call" | custom-call | tf_op jit(solution)/shard_map/input_back/pallas_call | solution.py:332
  301.4 15.2 %weight_gradients.1 = (bf16[128,5120]{1,0:T(8,128)(2,1)}, bf16[128,5120]{1,0:T(8,128)(2,1)}, bf16[128,5120]{1,0:T(8,128)(2,1)}, bf16[128,5120]{1,0:T(8,128)(2,1)...) custom-call(s32[13]{0:T(128)} %stack.135.order, ...), custom_call_target="tpu_custom_call" | custom-call | tf_op jit(solution)/shard_map/weight_gradients/pallas_call | solution.py:807
  316.6 1.1 collective-permute-start.58
  318.9 1.4 convert_reduce_fusion
  322.1 3.2 collective-permute-start.62
  325.4 23.1 %collective-permute-done.53 = f32[8,768]{1,0:T(8,128)S(1)} collective-permute-done((f32[8,768]{1,0:T(8,128)S(1)}, f32[8,768]{1,0:T(8,128)S(1)}, u32[]{:S(2)}, u32[]{:S(2)}) %collective-permute-start.53) | collective-permute-done | bytes 24608 | tf_op jit(solution)/shard_map/ppermute | solution.py:73
  349.2 3.2 collective-permute-start.55
  352.3 1.8 add_convert_fusion.3
  354.2 2.7 add_convert_fusion.2
  358.6 1.2 collective-permute-start.56
  359.8 1.5 pad_maximum_fusion
  364.5 33.2 %collective-permute-done.56 = f32[8,768]{1,0:T(8,128)S(1)} collective-permute-done((f32[8,768]{1,0:T(8,128)S(1)}, f32[8,768]{1,0:T(8,128)S(1)}, u32[]{:S(2)}, u32[]{:S(2)}) %collective-permute-start.56) | collective-permute-done | bytes 24608 | tf_op jit(solution)/shard_map/ppermute | solution.py:76
  397.7 4.6 collective-permute-start.50
  402.4 1.4 fusion.13
  403.9 3.5 add_convert_fusion.1
  410.7 14.2 %collective-permute-done.50 = f32[32,16,1024]{2,1,0:T(8,128)} collective-permute-done((f32[32,16,1024]{2,1,0:T(8,128)}, f32[32,16,1024]{2,1,0:T(8,128)}, u32[]{:S(2)}, u32[]{:S(2)}) %collective-permute-start.50) | collective-permute-done | bytes 2097184 | tf_op jit(solution)/shard_map/ppermute | solution.py:1047
  424.8 1.7 select_bitcast_fusion
  427.4 11.6 %collective-permute-done.68 = bf16[128,1024]{1,0:T(8,128)(2,1)S(1)} collective-permute-done((bf16[128,1024]{1,0:T(8,128)(2,1)S(1)}, bf16[128,1024]{1,0:T(8,128)(2,1)S(1)}, u32[]{:S(2)}, u32[]{:S(2)}) %collective-permute-start.68) | collective-permute-done | bytes 262176 | tf_op jit(solution)/shard_map/ppermute | solution.py:73
  439.1 2.3 add_convert_fusion
  442.6 3.8 collective-permute-start.73
  449.0 1.1 collective-permute-start.69
  450.7 1.3 slice.296
  454.8 1.1 convert_add_fusion.2
  456.8 4.2 collective-permute-start.74
  461.1 21.7 %collective-permute-done.74 = bf16[128,512]{1,0:T(8,128)(2,1)S(1)} collective-permute-done((bf16[128,512]{1,0:T(8,128)(2,1)S(1)}, bf16[128,512]{1,0:T(8,128)(2,1)S(1)}, u32[]{:S(2)}, u32[]{:S(2)}) %collective-permute-start.74) | collective-permute-done | bytes 131104 | tf_op jit(solution)/shard_map/ppermute | solution.py:76
  483.9 1.6 convert_add_fusion
  485.7 1.7 reshape.192
  487.4 1.7 reshape.193
  (369 shorter events, 63.7 us)
Async XLA Ops:
  3.8 25.1 %collective-permute-start = (bf16[128,4096]{1,0:T(8,128)(2,1)}, bf16[128,4096]{1,0:T(8,128)(2,1)}, u32[]{:S(2)}, u32[]{:S(2)}) collective-permute-start(bf16[128,4096]{1,0:T(8,128)(2,1)} %constant_dynamic-update-slice_fusion), channel_id=1, source_target_pairs={{0,0},{1,16},{16,1},{17,17},{2,2},{3,18},{18,3},{19,19},{4,4},{5,2... | collective-permute-start | bytes 3145736 | tf_op jit(solution)/shard_map/ppermute | solution.py:37
  17.3 12.9 %collective-permute-start.1 = (bf16[128,1536]{1,0:T(8,128)(2,1)S(1)}, bf16[128,1536]{1,0:T(8,128)(2,1)S(1)}, u32[]{:S(2)}, u32[]{:S(2)}) collective-permute-start(bf16[128,1536]{1,0:T(8,128)(2,1)S(1)} %get-tuple-element.203), channel_id=1, source_target_pairs={{0,4},{2,6},{4,8},{6,10},{8,12},{10,14},{12,0},{14,2},{1,5},{3,7},... | collective-permute-start | bytes 1179656 | tf_op jit(solution)/shard_map/ppermute | solution.py:76
  20.3 7.8 %collective-permute-start.2 = (bf16[128,1536]{1,0:T(8,128)(2,1)S(1)}, bf16[128,1536]{1,0:T(8,128)(2,1)S(1)}, u32[]{:S(2)}, u32[]{:S(2)}) collective-permute-start(bf16[128,1536]{1,0:T(8,128)(2,1)S(1)} %get-tuple-element.203), channel_id=1, source_target_pairs={{0,2},{2,0},{4,6},{6,4},{8,10},{10,8},{12,14},{14,12},{1,3},{3,1},... | collective-permute-start | bytes 1179656 | tf_op jit(solution)/shard_map/ppermute | solution.py:73
  21.8 13.6 %collective-permute-start.8 = (bf16[16,32,1024]{2,0,1:T(8,128)(2,1)S(1)}, bf16[16,32,1024]{2,0,1:T(8,128)(2,1)}, u32[]{:S(2)}, u32[]{:S(2)}) collective-permute-start(bf16[16,32,1024]{2,0,1:T(8,128)(2,1)S(1)} %bitcast.102), channel_id=1, source_target_pairs={{0,16},{16,0},{1,17},{17,1},{2,18},{18,2},{3,19},{19,3},{4,20},{20... | collective-permute-start | bytes 3145736 | tf_op jit(solution)/shard_map/ppermute | solution.py:29
  30.2 35.2 %collective-permute-start.3 = (bf16[128,5632]{1,0:T(8,128)(2,1)S(1)}, bf16[128,5632]{1,0:T(8,128)(2,1)}, u32[]{:S(2)}, u32[]{:S(2)}) collective-permute-start(bf16[128,5632]{1,0:T(8,128)(2,1)S(1)} %constant_dynamic-update-slice_fusion.6.refs_0_.refs_16_), channel_id=1, source_target_pairs={{0,4},{2,6},{4,8},{6,10},{8,12},{10,14},{12,0},{14,2},{1,5},{3,7},... | collective-permute-start | bytes 4325384 | tf_op jit(solution)/shard_map/ppermute | solution.py:76
  31.8 31.5 %collective-permute-start.4 = (bf16[128,5632]{1,0:T(8,128)(2,1)S(1)}, bf16[128,5632]{1,0:T(8,128)(2,1)}, u32[]{:S(2)}, u32[]{:S(2)}) collective-permute-start(bf16[128,5632]{1,0:T(8,128)(2,1)S(1)} %constant_dynamic-update-slice_fusion.6.refs_0_.refs_16_), channel_id=1, source_target_pairs={{0,2},{2,0},{4,6},{6,4},{8,10},{10,8},{12,14},{14,12},{1,3},{3,1},... | collective-permute-start | bytes 4325384 | tf_op jit(solution)/shard_map/ppermute | solution.py:73
  33.3 32.0 %collective-permute-start.5 = (bf16[128,3072]{1,0:T(8,128)(2,1)}, bf16[128,3072]{1,0:T(8,128)(2,1)}, u32[]{:S(2)}, u32[]{:S(2)}) collective-permute-start(bf16[128,3072]{1,0:T(8,128)(2,1)} %constant_dynamic-update-slice_fusion.8.refs_0_), channel_id=1, source_target_pairs={{0,1},{1,0},{2,3},{3,2},{4,5},{5,4},{6,7},{7,6},{8,9},{9,8},{10,11... | collective-permute-start | bytes 2359304 | tf_op jit(solution)/shard_map/ppermute | solution.py:33
  33.3 32.0 %collective-permute-start.6 = (bf16[256,1024]{1,0:T(8,128)(2,1)S(1)}, bf16[256,1024]{1,0:T(8,128)(2,1)S(1)}, u32[]{:S(2)}, u32[]{:S(2)}) collective-permute-start(bf16[256,1024]{1,0:T(8,128)(2,1)S(1)} %pad.20.refs_16_), channel_id=1, source_target_pairs={{0,1},{1,0},{2,3},{3,2},{4,5},{5,4},{6,7},{7,6},{8,9},{9,8},{10,11... | collective-permute-start | bytes 1572872 | tf_op jit(solution)/shard_map/ppermute | solution.py:33
  35.4 30.0 %collective-permute-start.7 = (bf16[1,2048]{1,0:T(2,128)(2,1)}, bf16[1,2048]{1,0:T(2,128)(2,1)S(1)}, u32[]{:S(2)}, u32[]{:S(2)}) collective-permute-start(bf16[1,2048]{1,0:T(2,128)(2,1)} %bitcast.65), channel_id=1, source_target_pairs={{0,0},{1,16},{16,1},{17,17},{2,2},{3,18},{18,3},{19,19},{4,4},{5,2... | collective-permute-start | bytes 12296 | tf_op jit(solution)/shard_map/ppermute | solution.py:37
  67.4 30.8 %collective-permute-start.13 = (bf16[128,5632]{1,0:T(8,128)(2,1)}, bf16[128,5632]{1,0:T(8,128)(2,1)}, u32[]{:S(2)}, u32[]{:S(2)}) collective-permute-start(bf16[128,5632]{1,0:T(8,128)(2,1)} %collective-permute-done.3.refs_2_.refs_18_), channel_id=1, source_target_pairs={{0,2},{2,0},{4,6},{6,4},{8,10},{10,8},{12,14},{14,12},{1,3},{3,1},... | collective-permute-start | bytes 4325384 | tf_op jit(solution)/shard_map/ppermute | solution.py:73
  67.9 32.0 %collective-permute-start.12 = (bf16[128,5632]{1,0:T(8,128)(2,1)}, bf16[128,5632]{1,0:T(8,128)(2,1)S(1)}, u32[]{:S(2)}, u32[]{:S(2)}) collective-permute-start(bf16[128,5632]{1,0:T(8,128)(2,1)} %collective-permute-done.3.refs_2_.refs_18_), channel_id=1, source_target_pairs={{0,4},{2,6},{4,8},{6,10},{8,12},{10,14},{12,0},{14,2},{1,5},{3,7},... | collective-permute-start | bytes 4325384 | tf_op jit(solution)/shard_map/ppermute | solution.py:76
  69.5 31.6 %collective-permute-start.14 = (bf16[128,3072]{1,0:T(8,128)(2,1)}, bf16[128,3072]{1,0:T(8,128)(2,1)}, u32[]{:S(2)}, u32[]{:S(2)}) collective-permute-start(bf16[128,3072]{1,0:T(8,128)(2,1)} %pad_maximum_fusion.2.refs_1_), channel_id=1, source_target_pairs={{0,1},{1,0},{2,3},{3,2},{4,5},{5,4},{6,7},{7,6},{8,9},{9,8},{10,11... | collective-permute-start | bytes 2359304 | tf_op jit(solution)/shard_map/ppermute | solution.py:33
  70.2 37.3 %collective-permute-start.26 = (bf16[128,5632]{1,0:T(8,128)(2,1)S(1)}, bf16[128,5632]{1,0:T(8,128)(2,1)S(1)}, u32[]{:S(2)}, u32[]{:S(2)}) collective-permute-start(bf16[128,5632]{1,0:T(8,128)(2,1)S(1)} %constant_dynamic-update-slice_fusion.6.refs_0_.refs_16_), channel_id=1, source_target_pairs={{0,16},{16,0},{1,17},{17,1},{2,18},{18,2},{3,19},{19,3},{4,20},{20... | collective-permute-start | bytes 4325384 | tf_op jit(solution)/shard_map/ppermute | solution.py:29
  70.2 30.9 %collective-permute-start.10 = (f32[5,256]{1,0:T(8,128)S(1)}, f32[5,256]{1,0:T(8,128)S(1)}, u32[]{:S(2)}, u32[]{:S(2)}) collective-permute-start(f32[5,256]{1,0:T(8,128)S(1)} %stack.122), channel_id=1, source_target_pairs={{0,1},{1,0},{2,3},{3,2},{4,5},{5,4},{6,7},{7,6},{8,9},{9,8},{10,11... | collective-permute-start | bytes 15368 | tf_op jit(solution)/shard_map/ppermute | solution.py:33
  101.1 29.1 %collective-permute-start.22 = (bf16[128,5632]{1,0:T(8,128)(2,1)S(1)}, bf16[128,5632]{1,0:T(8,128)(2,1)S(1)}, u32[]{:S(2)}, u32[]{:S(2)}) collective-permute-start(bf16[128,5632]{1,0:T(8,128)(2,1)S(1)} %collective-permute-done.12.refs_4_.refs_20_), channel_id=1, source_target_pairs={{0,2},{2,0},{4,6},{6,4},{8,10},{10,8},{12,14},{14,12},{1,3},{3,1},... | collective-permute-start | bytes 4325384 | tf_op jit(solution)/shard_map/ppermute | solution.py:73
  102.7 22.8 %collective-permute-start.18 = (bf16[128,3072]{1,0:T(8,128)(2,1)S(1)}, bf16[128,3072]{1,0:T(8,128)(2,1)}, u32[]{:S(2)}, u32[]{:S(2)}) collective-permute-start(bf16[128,3072]{1,0:T(8,128)(2,1)S(1)} %pad_maximum_fusion.3.refs_2_), channel_id=1, source_target_pairs={{0,1},{1,0},{2,3},{3,2},{4,5},{5,4},{6,7},{7,6},{8,9},{9,8},{10,11... | collective-permute-start | bytes 2359304 | tf_op jit(solution)/shard_map/ppermute | solution.py:33
  107.2 27.4 %collective-permute-start.15 = (bf16[128,4096]{1,0:T(8,128)(2,1)}, bf16[128,4096]{1,0:T(8,128)(2,1)}, u32[]{:S(2)}, u32[]{:S(2)}) collective-permute-start(bf16[128,4096]{1,0:T(8,128)(2,1)} %slice.281), channel_id=1, source_target_pairs={{0,4},{2,6},{4,8},{6,10},{8,12},{10,14},{12,0},{14,2},{1,5},{3,7},... | collective-permute-start | bytes 3145736 | tf_op jit(solution)/shard_map/ppermute | solution.py:76
  107.2 28.9 %collective-permute-start.27 = (bf16[128,5632]{1,0:T(8,128)(2,1)}, bf16[128,5632]{1,0:T(8,128)(2,1)}, u32[]{:S(2)}, u32[]{:S(2)}) collective-permute-start(bf16[128,5632]{1,0:T(8,128)(2,1)} %collective-permute-done.4.refs_1_.refs_17_), channel_id=1, source_target_pairs={{0,16},{16,0},{1,17},{17,1},{2,18},{18,2},{3,19},{19,3},{4,20},{20... | collective-permute-start | bytes 4325384 | tf_op jit(solution)/shard_map/ppermute | solution.py:29
  110.5 25.9 %collective-permute-start.28 = (bf16[128,5632]{1,0:T(8,128)(2,1)}, bf16[128,5632]{1,0:T(8,128)(2,1)}, u32[]{:S(2)}, u32[]{:S(2)}) collective-permute-start(bf16[128,5632]{1,0:T(8,128)(2,1)} %collective-permute-done.3.refs_2_.refs_18_), channel_id=1, source_target_pairs={{0,16},{16,0},{1,17},{17,1},{2,18},{18,2},{3,19},{19,3},{4,20},{20... | collective-permute-start | bytes 4325384 | tf_op jit(solution)/shard_map/ppermute | solution.py:29
  125.5 12.9 %collective-permute-start.29 = (bf16[128,5632]{1,0:T(8,128)(2,1)}, bf16[128,5632]{1,0:T(8,128)(2,1)}, u32[]{:S(2)}, u32[]{:S(2)}) collective-permute-start(bf16[128,5632]{1,0:T(8,128)(2,1)} %collective-permute-done.13.refs_3_.refs_19_), channel_id=1, source_target_pairs={{0,16},{16,0},{1,17},{17,1},{2,18},{18,2},{3,19},{19,3},{4,20},{20... | collective-permute-start | bytes 4325384 | tf_op jit(solution)/shard_map/ppermute | solution.py:29
  130.2 5.4 %collective-permute-start.20 = (bf16[128,3072]{1,0:T(8,128)(2,1)}, bf16[128,3072]{1,0:T(8,128)(2,1)}, u32[]{:S(2)}, u32[]{:S(2)}) collective-permute-start(bf16[128,3072]{1,0:T(8,128)(2,1)} %pad_maximum_fusion.2.refs_1_), channel_id=1, source_target_pairs={{0,16},{16,0},{1,17},{17,1},{2,18},{18,2},{3,19},{19,3},{4,20},{20... | collective-permute-start | bytes 2359304 | tf_op jit(solution)/shard_map/ppermute | solution.py:29
  135.6 25.8 %collective-permute-start.25 = (bf16[128,4096]{1,0:T(8,128)(2,1)}, bf16[128,4096]{1,0:T(8,128)(2,1)S(1)}, u32[]{:S(2)}, u32[]{:S(2)}) collective-permute-start(bf16[128,4096]{1,0:T(8,128)(2,1)} %collective-permute-done.15.refs_6_.refs_22_), channel_id=1, source_target_pairs={{0,2},{2,0},{4,6},{6,4},{8,10},{10,8},{12,14},{14,12},{1,3},{3,1},... | collective-permute-start | bytes 3145736 | tf_op jit(solution)/shard_map/ppermute | solution.py:73
  138.1 23.3 %collective-permute-start.23 = (bf16[128,3072]{1,0:T(8,128)(2,1)}, bf16[128,3072]{1,0:T(8,128)(2,1)S(1)}, u32[]{:S(2)}, u32[]{:S(2)}) collective-permute-start(bf16[128,3072]{1,0:T(8,128)(2,1)} %pad_maximum_fusion.4.refs_3_), channel_id=1, source_target_pairs={{0,16},{16,0},{1,17},{17,1},{2,18},{18,2},{3,19},{19,3},{4,20},{20... | collective-permute-start | bytes 2359304 | tf_op jit(solution)/shard_map/ppermute | solution.py:29
  138.4 29.3 %collective-permute-start.30 = (bf16[128,5632]{1,0:T(8,128)(2,1)S(1)}, bf16[128,5632]{1,0:T(8,128)(2,1)S(1)}, u32[]{:S(2)}, u32[]{:S(2)}) collective-permute-start(bf16[128,5632]{1,0:T(8,128)(2,1)S(1)} %collective-permute-done.12.refs_4_.refs_20_), channel_id=1, source_target_pairs={{0,16},{16,0},{1,17},{17,1},{2,18},{18,2},{3,19},{19,3},{4,20},{20... | collective-permute-start | bytes 4325384 | tf_op jit(solution)/shard_map/ppermute | solution.py:29
  138.7 29.5 %collective-permute-start.31 = (bf16[128,5632]{1,0:T(8,128)(2,1)S(1)}, bf16[128,5632]{1,0:T(8,128)(2,1)S(1)}, u32[]{:S(2)}, u32[]{:S(2)}) collective-permute-start(bf16[128,5632]{1,0:T(8,128)(2,1)S(1)} %collective-permute-done.22.refs_5_.refs_21_), channel_id=1, source_target_pairs={{0,16},{16,0},{1,17},{17,1},{2,18},{18,2},{3,19},{19,3},{4,20},{20... | collective-permute-start | bytes 4325384 | tf_op jit(solution)/shard_map/ppermute | solution.py:29
  139.0 28.8 %collective-permute-start.32 = (bf16[128,4096]{1,0:T(8,128)(2,1)}, bf16[128,4096]{1,0:T(8,128)(2,1)S(1)}, u32[]{:S(2)}, u32[]{:S(2)}) collective-permute-start(bf16[128,4096]{1,0:T(8,128)(2,1)} %collective-permute-done.15.refs_6_.refs_22_), channel_id=1, source_target_pairs={{0,16},{16,0},{1,17},{17,1},{2,18},{18,2},{3,19},{19,3},{4,20},{20... | collective-permute-start | bytes 3145736 | tf_op jit(solution)/shard_map/ppermute | solution.py:29
  161.4 7.9 %collective-permute-start.33 = (bf16[128,4096]{1,0:T(8,128)(2,1)S(1)}, bf16[128,4096]{1,0:T(8,128)(2,1)}, u32[]{:S(2)}, u32[]{:S(2)}) collective-permute-start(bf16[128,4096]{1,0:T(8,128)(2,1)S(1)} %collective-permute-done.25.refs_7_.refs_23_), channel_id=1, source_target_pairs={{0,16},{16,0},{1,17},{17,1},{2,18},{18,2},{3,19},{19,3},{4,20},{20... | collective-permute-start | bytes 3145736 | tf_op jit(solution)/shard_map/ppermute | solution.py:29
  161.4 39.2 %collective-permute-start.35 = (bf16[128,3072]{1,0:T(8,128)(2,1)}, bf16[128,3072]{1,0:T(8,128)(2,1)}, u32[]{:S(2)}, u32[]{:S(2)}) collective-permute-start(bf16[128,3072]{1,0:T(8,128)(2,1)} %pad_maximum_fusion.4.refs_3_), channel_id=1, source_target_pairs={{0,1},{1,0},{2,3},{3,2},{4,5},{5,4},{6,7},{7,6},{8,9},{9,8},{10,11... | collective-permute-start | bytes 2359304 | tf_op jit(solution)/shard_map/ppermute | solution.py:33
  167.6 44.2 %collective-permute-start.36 = (bf16[128,3072]{1,0:T(8,128)(2,1)}, bf16[128,3072]{1,0:T(8,128)(2,1)S(1)}, u32[]{:S(2)}, u32[]{:S(2)}) collective-permute-start(bf16[128,3072]{1,0:T(8,128)(2,1)} %collective-permute-done.5.refs_4_), channel_id=1, source_target_pairs={{0,16},{16,0},{1,17},{17,1},{2,18},{18,2},{3,19},{19,3},{4,20},{20... | collective-permute-start | bytes 2359304 | tf_op jit(solution)/shard_map/ppermute | solution.py:29
  167.8 44.1 %collective-permute-start.37 = (bf16[128,3072]{1,0:T(8,128)(2,1)}, bf16[128,3072]{1,0:T(8,128)(2,1)}, u32[]{:S(2)}, u32[]{:S(2)}) collective-permute-start(bf16[128,3072]{1,0:T(8,128)(2,1)} %collective-permute-done.14.refs_5_), channel_id=1, source_target_pairs={{0,16},{16,0},{1,17},{17,1},{2,18},{18,2},{3,19},{19,3},{4,20},{20... | collective-permute-start | bytes 2359304 | tf_op jit(solution)/shard_map/ppermute | solution.py:29
  168.9 43.0 %collective-permute-start.38 = (bf16[128,3072]{1,0:T(8,128)(2,1)}, bf16[128,3072]{1,0:T(8,128)(2,1)}, u32[]{:S(2)}, u32[]{:S(2)}) collective-permute-start(bf16[128,3072]{1,0:T(8,128)(2,1)} %collective-permute-done.18.refs_6_), channel_id=1, source_target_pairs={{0,16},{16,0},{1,17},{17,1},{2,18},{18,2},{3,19},{19,3},{4,20},{20... | collective-permute-start | bytes 2359304 | tf_op jit(solution)/shard_map/ppermute | solution.py:29
  200.6 11.3 %collective-permute-start.39 = (bf16[128,3072]{1,0:T(8,128)(2,1)}, bf16[128,3072]{1,0:T(8,128)(2,1)S(1)}, u32[]{:S(2)}, u32[]{:S(2)}) collective-permute-start(bf16[128,3072]{1,0:T(8,128)(2,1)} %collective-permute-done.35.refs_7_), channel_id=1, source_target_pairs={{0,16},{16,0},{1,17},{17,1},{2,18},{18,2},{3,19},{19,3},{4,20},{20... | collective-permute-start | bytes 2359304 | tf_op jit(solution)/shard_map/ppermute | solution.py:29
  201.0 8.6 %collective-permute-start.34 = (bf16[128,1024]{1,0:T(8,128)(2,1)}, bf16[128,1024]{1,0:T(8,128)(2,1)S(1)}, u32[]{:S(2)}, u32[]{:S(2)}) collective-permute-start(bf16[128,1024]{1,0:T(8,128)(2,1)} %bitcast.114), channel_id=1, source_target_pairs={{0,1},{1,0},{2,3},{3,2},{4,5},{5,4},{6,7},{7,6},{8,9},{9,8},{10,11... | collective-permute-start | bytes 786440 | tf_op jit(solution)/shard_map/ppermute | solution.py:33
  209.6 35.9 %collective-permute-start.42 = (bf16[128,1024]{1,0:T(8,128)(2,1)}, bf16[128,1024]{1,0:T(8,128)(2,1)S(1)}, u32[]{:S(2)}, u32[]{:S(2)}) collective-permute-start(bf16[128,1024]{1,0:T(8,128)(2,1)} %bitcast.98), channel_id=1, source_target_pairs={{0,1},{1,0},{2,3},{3,2},{4,5},{5,4},{6,7},{7,6},{8,9},{9,8},{10,11... | collective-permute-start | bytes 786440 | tf_op jit(solution)/shard_map/ppermute | solution.py:33
  211.8 40.6 %collective-permute-start.44 = (bf16[256,1024]{1,0:T(8,128)(2,1)}, bf16[256,1024]{1,0:T(8,128)(2,1)}, u32[]{:S(2)}, u32[]{:S(2)}) collective-permute-start(bf16[256,1024]{1,0:T(8,128)(2,1)} %bitcast.106), channel_id=1, source_target_pairs={{0,16},{16,0},{1,17},{17,1},{2,18},{18,2},{3,19},{19,3},{4,20},{20... | collective-permute-start | bytes 1572872 | tf_op jit(solution)/shard_map/ppermute | solution.py:29
  245.5 8.2 %collective-permute-start.43 = (bf16[128,1024]{1,0:T(8,128)(2,1)}, bf16[128,1024]{1,0:T(8,128)(2,1)S(1)}, u32[]{:S(2)}, u32[]{:S(2)}) collective-permute-start(bf16[128,1024]{1,0:T(8,128)(2,1)} %get-tuple-element.122), channel_id=1, source_target_pairs={{0,1},{1,0},{2,3},{3,2},{4,5},{5,4},{6,7},{7,6},{8,9},{9,8},{10,11... | collective-permute-start | bytes 786440 | tf_op jit(solution)/shard_map/ppermute | solution.py:33
  248.6 5.8 %collective-permute-start.45 = (bf16[4,128,1024]{2,1,0:T(8,128)(2,1)S(1)}, bf16[4,128,1024]{2,1,0:T(8,128)(2,1)}, u32[]{:S(2)}, u32[]{:S(2)}) collective-permute-start(bf16[4,128,1024]{2,1,0:T(8,128)(2,1)S(1)} %pad_maximum_fusion.1.states_own), channel_id=1, source_target_pairs={{0,16},{16,0},{1,17},{17,1},{2,18},{18,2},{3,19},{19,3},{4,20},{20... | collective-permute-start | bytes 3145736 | tf_op jit(solution)/shard_map/ppermute | solution.py:29
  254.4 32.2 %collective-permute-start.47 = (bf16[2,128,1536]{2,1,0:T(8,128)(2,1)S(1)}, bf16[2,128,1536]{2,1,0:T(8,128)(2,1)S(1)}, u32[]{:S(2)}, u32[]{:S(2)}) collective-permute-start(bf16[2,128,1536]{2,1,0:T(8,128)(2,1)S(1)} %pad_maximum_fusion.5), channel_id=1, source_target_pairs={{0,1},{1,0},{2,3},{3,2},{4,5},{5,4},{6,7},{7,6},{8,9},{9,8},{10,11... | collective-permute-start | bytes 2359304 | tf_op jit(solution)/shard_map/ppermute | solution.py:33
  255.8 30.9 %collective-permute-start.48 = (bf16[2,128,1152]{2,1,0:T(8,128)(2,1)S(1)}, bf16[2,128,1152]{2,1,0:T(8,128)(2,1)}, u32[]{:S(2)}, u32[]{:S(2)}) collective-permute-start(bf16[2,128,1152]{2,1,0:T(8,128)(2,1)S(1)} %pad_maximum_fusion.6), channel_id=1, source_target_pairs={{0,1},{1,0},{2,3},{3,2},{4,5},{5,4},{6,7},{7,6},{8,9},{9,8},{10,11... | collective-permute-start | bytes 1769480 | tf_op jit(solution)/shard_map/ppermute | solution.py:33
  288.3 12.2 %collective-permute-start.51 = (bf16[256,2048]{1,0:T(8,128)(2,1)S(1)}, bf16[256,2048]{1,0:T(8,128)(2,1)S(1)}, u32[]{:S(2)}, u32[]{:S(2)}) collective-permute-start(bf16[256,2048]{1,0:T(8,128)(2,1)S(1)} %slice_bitcast_fusion), channel_id=1, source_target_pairs={{0,16},{16,0},{1,17},{17,1},{2,18},{18,2},{3,19},{19,3},{4,20},{20... | collective-permute-start | bytes 3145736 | tf_op jit(solution)/shard_map/ppermute | solution.py:29
  288.3 12.1 %collective-permute-start.57 = (bf16[2,128,1152]{2,1,0:T(8,128)(2,1)}, bf16[2,128,1152]{2,1,0:T(8,128)(2,1)}, u32[]{:S(2)}, u32[]{:S(2)}) collective-permute-start(bf16[2,128,1152]{2,1,0:T(8,128)(2,1)} %collective-permute-done.48.far), channel_id=1, source_target_pairs={{0,16},{16,0},{1,17},{17,1},{2,18},{18,2},{3,19},{19,3},{4,20},{20... | collective-permute-start | bytes 1769480 | tf_op jit(solution)/shard_map/ppermute | solution.py:29
  300.3 18.6 %collective-permute-start.52 = (f32[1024]{0:T(1024)}, f32[1024]{0:T(1024)S(1)}, u32[]{:S(2)}, u32[]{:S(2)}) collective-permute-start(f32[1024]{0:T(1024)} %bitcast.124), channel_id=1, source_target_pairs={{0,16},{16,0},{1,17},{17,1},{2,18},{18,2},{3,19},{19,3},{4,20},{20... | collective-permute-start | bytes 12296 | tf_op jit(solution)/shard_map/ppermute | solution.py:29
  316.6 37.6 %collective-permute-start.58 = (bf16[128,5120]{1,0:T(8,128)(2,1)}, bf16[128,5120]{1,0:T(8,128)(2,1)}, u32[]{:S(2)}, u32[]{:S(2)}) collective-permute-start(bf16[128,5120]{1,0:T(8,128)(2,1)} %get-tuple-element.147), channel_id=1, source_target_pairs={{0,2},{2,0},{4,6},{6,4},{8,10},{10,8},{12,14},{14,12},{1,3},{3,1},... | collective-permute-start | bytes 3932168 | tf_op jit(solution)/shard_map/ppermute | solution.py:73
  318.0 31.2 %collective-permute-start.59 = (bf16[256,768]{1,0:T(8,128)(2,1)}, bf16[256,768]{1,0:T(8,128)(2,1)}, u32[]{:S(2)}, u32[]{:S(2)}) collective-permute-start(bf16[256,768]{1,0:T(8,128)(2,1)} %get-tuple-element.150), channel_id=1, source_target_pairs={{0,4},{2,6},{4,8},{6,10},{8,12},{10,14},{12,0},{14,2},{1,5},{3,7},... | collective-permute-start | bytes 1179656 | tf_op jit(solution)/shard_map/ppermute | solution.py:76
  320.4 28.1 %collective-permute-start.53 = (f32[8,768]{1,0:T(8,128)S(1)}, f32[8,768]{1,0:T(8,128)S(1)}, u32[]{:S(2)}, u32[]{:S(2)}) collective-permute-start(f32[8,768]{1,0:T(8,128)S(1)} %reshape.191), channel_id=1, source_target_pairs={{0,2},{2,0},{4,6},{6,4},{8,10},{10,8},{12,14},{14,12},{1,3},{3,1},... | collective-permute-start | bytes 73736 | tf_op jit(solution)/shard_map/ppermute | solution.py:73
  322.1 34.8 %collective-permute-start.49 = (f32[16,16,1024]{2,1,0:T(8,128)S(1)}, f32[16,16,1024]{2,1,0:T(8,128)S(1)}, u32[]{:S(2)}, u32[]{:S(2)}) collective-permute-start(f32[16,16,1024]{2,1,0:T(8,128)S(1)} %bitcast.103), channel_id=1, source_target_pairs={{0,16},{16,0},{1,17},{17,1},{2,18},{18,2},{3,19},{19,3},{4,20},{20... | collective-permute-start | bytes 3145736 | tf_op jit(solution)/shard_map/ppermute | solution.py:29
  322.1 80.2 %collective-permute-start.62 = (bf16[256,768]{1,0:T(8,128)(2,1)}, bf16[256,768]{1,0:T(8,128)(2,1)}, u32[]{:S(2)}, u32[]{:S(2)}) collective-permute-start(bf16[256,768]{1,0:T(8,128)(2,1)} %get-tuple-element.155), channel_id=1, source_target_pairs={{4,0},{6,2},{8,4},{10,6},{12,8},{14,10},{0,12},{2,14},{5,1},{7,3},... | collective-permute-start | bytes 1179656 | tf_op jit(solution)/shard_map/ppermute | solution.py:79
  348.5 9.4 %collective-permute-start.54 = (f32[8,768]{1,0:T(8,128)S(1)}, f32[8,768]{1,0:T(8,128)S(1)}, u32[]{:S(2)}, u32[]{:S(2)}) collective-permute-start(f32[8,768]{1,0:T(8,128)S(1)} %add.237), channel_id=1, source_target_pairs={{0,4},{2,6},{4,8},{6,10},{8,12},{10,14},{12,0},{14,2},{1,5},{3,7},... | collective-permute-start | bytes 73736 | tf_op jit(solution)/shard_map/ppermute | solution.py:76
  349.2 9.4 %collective-permute-start.55 = (f32[8,768]{1,0:T(8,128)S(1)}, f32[8,768]{1,0:T(8,128)S(1)}, u32[]{:S(2)}, u32[]{:S(2)}) collective-permute-start(f32[8,768]{1,0:T(8,128)S(1)} %add.237), channel_id=1, source_target_pairs={{4,0},{6,2},{8,4},{10,6},{12,8},{14,10},{0,12},{2,14},{5,1},{7,3},... | collective-permute-start | bytes 73736 | tf_op jit(solution)/shard_map/ppermute | solution.py:79
  356.9 46.9 %collective-permute-start.61 = (bf16[128,5120]{1,0:T(8,128)(2,1)}, bf16[128,5120]{1,0:T(8,128)(2,1)}, u32[]{:S(2)}, u32[]{:S(2)}) collective-permute-start(bf16[128,5120]{1,0:T(8,128)(2,1)} %add_convert_fusion.2), channel_id=1, source_target_pairs={{0,4},{2,6},{4,8},{6,10},{8,12},{10,14},{12,0},{14,2},{1,5},{3,7},... | collective-permute-start | bytes 3932168 | tf_op jit(solution)/shard_map/ppermute | solution.py:76
  356.9 46.9 %collective-permute-start.60 = (bf16[128,5120]{1,0:T(8,128)(2,1)}, bf16[128,5120]{1,0:T(8,128)(2,1)}, u32[]{:S(2)}, u32[]{:S(2)}) collective-permute-start(bf16[128,5120]{1,0:T(8,128)(2,1)} %get-tuple-element.151), channel_id=1, source_target_pairs={{0,2},{2,0},{4,6},{6,4},{8,10},{10,8},{12,14},{14,12},{1,3},{3,1},... | collective-permute-start | bytes 3932168 | tf_op jit(solution)/shard_map/ppermute | solution.py:73
  357.9 44.4 %collective-permute-start.63 = (bf16[256,768]{1,0:T(8,128)(2,1)}, bf16[256,768]{1,0:T(8,128)(2,1)}, u32[]{:S(2)}, u32[]{:S(2)}) collective-permute-start(bf16[256,768]{1,0:T(8,128)(2,1)} %add_convert_fusion.3), channel_id=1, source_target_pairs={{0,4},{2,6},{4,8},{6,10},{8,12},{10,14},{12,0},{14,2},{1,5},{3,7},... | collective-permute-start | bytes 1179656 | tf_op jit(solution)/shard_map/ppermute | solution.py:76
  358.6 39.1 %collective-permute-start.56 = (f32[8,768]{1,0:T(8,128)S(1)}, f32[8,768]{1,0:T(8,128)S(1)}, u32[]{:S(2)}, u32[]{:S(2)}) collective-permute-start(f32[8,768]{1,0:T(8,128)S(1)} %collective-permute-done.54), channel_id=1, source_target_pairs={{0,4},{2,6},{4,8},{6,10},{8,12},{10,14},{12,0},{14,2},{1,5},{3,7},... | collective-permute-start | bytes 73736 | tf_op jit(solution)/shard_map/ppermute | solution.py:76
  397.7 27.1 %collective-permute-start.50 = (f32[32,16,1024]{2,1,0:T(8,128)}, f32[32,16,1024]{2,1,0:T(8,128)}, u32[]{:S(2)}, u32[]{:S(2)}) collective-permute-start(f32[32,16,1024]{2,1,0:T(8,128)} %pad_maximum_fusion), channel_id=1, source_target_pairs={{0,1},{17,16},{2,3},{19,18},{4,5},{21,20},{6,7},{23,22},{8,9},{25,... | collective-permute-start | bytes 6291464 | tf_op jit(solution)/shard_map/ppermute | solution.py:1047
  407.4 31.8 %collective-permute-start.65 = (bf16[128,5120]{1,0:T(8,128)(2,1)}, bf16[128,5120]{1,0:T(8,128)(2,1)}, u32[]{:S(2)}, u32[]{:S(2)}) collective-permute-start(bf16[128,5120]{1,0:T(8,128)(2,1)} %add_convert_fusion.1), channel_id=1, source_target_pairs={{0,4},{2,6},{4,8},{6,10},{8,12},{10,14},{12,0},{14,2},{1,5},{3,7},... | collective-permute-start | bytes 3932168 | tf_op jit(solution)/shard_map/ppermute | solution.py:76
  407.4 31.8 %collective-permute-start.64 = (bf16[128,5120]{1,0:T(8,128)(2,1)}, bf16[128,5120]{1,0:T(8,128)(2,1)}, u32[]{:S(2)}, u32[]{:S(2)}) collective-permute-start(bf16[128,5120]{1,0:T(8,128)(2,1)} %get-tuple-element.158), channel_id=1, source_target_pairs={{0,2},{2,0},{4,6},{6,4},{8,10},{10,8},{12,14},{14,12},{1,3},{3,1},... | collective-permute-start | bytes 3932168 | tf_op jit(solution)/shard_map/ppermute | solution.py:73
  409.6 29.4 %collective-permute-start.68 = (bf16[128,1024]{1,0:T(8,128)(2,1)S(1)}, bf16[128,1024]{1,0:T(8,128)(2,1)S(1)}, u32[]{:S(2)}, u32[]{:S(2)}) collective-permute-start(bf16[128,1024]{1,0:T(8,128)(2,1)S(1)} %pad_maximum_fusion.8), channel_id=1, source_target_pairs={{0,2},{2,0},{4,6},{6,4},{8,10},{10,8},{12,14},{14,12},{1,3},{3,1},... | collective-permute-start | bytes 786440 | tf_op jit(solution)/shard_map/ppermute | solution.py:73
  426.6 16.0 %collective-permute-start.67 = (bf16[128,4096]{1,0:T(8,128)(2,1)S(1)}, bf16[128,4096]{1,0:T(8,128)(2,1)S(1)}, u32[]{:S(2)}, u32[]{:S(2)}) collective-permute-start(bf16[128,4096]{1,0:T(8,128)(2,1)S(1)} %copy-done.28), channel_id=1, source_target_pairs={{0,0},{1,16},{16,1},{17,17},{2,2},{3,18},{18,3},{19,19},{4,4},{5,2... | collective-permute-start | bytes 3145736 | tf_op jit(solution)/shard_map/ppermute | solution.py:37
  442.6 12.3 %collective-permute-start.72 = (bf16[128,1536]{1,0:T(8,128)(2,1)S(1)}, bf16[128,1536]{1,0:T(8,128)(2,1)S(1)}, u32[]{:S(2)}, u32[]{:S(2)}) collective-permute-start(bf16[128,1536]{1,0:T(8,128)(2,1)S(1)} %pad_maximum_fusion.7), channel_id=1, source_target_pairs={{0,4},{2,6},{4,8},{6,10},{8,12},{10,14},{12,0},{14,2},{1,5},{3,7},... | collective-permute-start | bytes 1179656 | tf_op jit(solution)/shard_map/ppermute | solution.py:76
  442.6 10.3 %collective-permute-start.73 = (bf16[128,512]{1,0:T(8,128)(2,1)S(1)}, bf16[128,512]{1,0:T(8,128)(2,1)}, u32[]{:S(2)}, u32[]{:S(2)}) collective-permute-start(bf16[128,512]{1,0:T(8,128)(2,1)S(1)} %get-tuple-element.168), channel_id=1, source_target_pairs={{4,0},{6,2},{8,4},{10,6},{12,8},{14,10},{0,12},{2,14},{5,1},{7,3},... | collective-permute-start | bytes 393224 | tf_op jit(solution)/shard_map/ppermute | solution.py:79
  447.8 6.8 %collective-permute-start.71 = (bf16[128,1024]{1,0:T(8,128)(2,1)}, bf16[128,1024]{1,0:T(8,128)(2,1)}, u32[]{:S(2)}, u32[]{:S(2)}) collective-permute-start(bf16[128,1024]{1,0:T(8,128)(2,1)} %slice.248), channel_id=1, source_target_pairs={{0,2},{2,0},{4,6},{6,4},{8,10},{10,8},{12,14},{14,12},{1,3},{3,1},... | collective-permute-start | bytes 786440 | tf_op jit(solution)/shard_map/ppermute | solution.py:73
  448.9 34.9 %collective-permute-start.70 = (bf16[128,4096]{1,0:T(8,128)(2,1)}, bf16[128,4096]{1,0:T(8,128)(2,1)S(1)}, u32[]{:S(2)}, u32[]{:S(2)}) collective-permute-start(bf16[128,4096]{1,0:T(8,128)(2,1)} %slice.297), channel_id=1, source_target_pairs={{0,4},{1,20},{16,5},{17,21},{2,6},{3,22},{18,7},{19,23},{4,8},{5,2... | collective-permute-start | bytes 3145736 | tf_op jit(solution)/shard_map/ppermute | solution.py:1064
  449.0 34.9 %collective-permute-start.69 = (bf16[128,4096]{1,0:T(8,128)(2,1)}, bf16[128,4096]{1,0:T(8,128)(2,1)}, u32[]{:S(2)}, u32[]{:S(2)}) collective-permute-start(bf16[128,4096]{1,0:T(8,128)(2,1)} %slice.243), channel_id=1, source_target_pairs={{0,2},{1,18},{16,3},{17,19},{2,0},{3,16},{18,1},{19,17},{4,6},{5,2... | collective-permute-start | bytes 3145736 | tf_op jit(solution)/shard_map/ppermute | solution.py:1064
  456.8 26.0 %collective-permute-start.74 = (bf16[128,512]{1,0:T(8,128)(2,1)S(1)}, bf16[128,512]{1,0:T(8,128)(2,1)S(1)}, u32[]{:S(2)}, u32[]{:S(2)}) collective-permute-start(bf16[128,512]{1,0:T(8,128)(2,1)S(1)} %slice.324), channel_id=1, source_target_pairs={{0,4},{2,6},{4,8},{6,10},{8,12},{10,14},{12,0},{14,2},{1,5},{3,7},... | collective-permute-start | bytes 393224 | tf_op jit(solution)/shard_map/ppermute | solution.py:76
  (82 other events, 1165.6 us)

commit v7 on v6

--- a/solution.py
+++ b/solution.py
@@ -1066,39 +1066,39 @@
         arrived, out_two, out_before = flow.step(
             (across, theirs[0]), (onward, outputs[1]), (ring.astern, outputs[0])
         )
+        out_one = onward(
+            tie((outputs[2].astype(wide) + out_two.astype(wide)).astype(low), arrived)
+        )
         grad_far = to_other_chip(grad_section)
         flat = flat.reshape(8, -1)
-        flat = flat + across(flat)
+        flat = (flat + across(flat)).reshape(-1)
+        flat_width = flat.shape[0] // r
         flow.landed = (arrived,)
         value = total(1, arrived, None).astype(low)
-        out = (outputs[2].astype(wide) + out_two.astype(wide)).astype(low)
-        passed, arrived, out_one = flow.step((onward, value), (across, theirs[1]), (onward, out))
-        flat_one, flat_three = onward(flat), ring.astern(flat)
+        passed, arrived = flow.step((onward, value), (across, theirs[1]))
         out = outputs[3].astype(wide) + out_before.astype(wide) + out_one.astype(wide)
         vocab_rows = out[:, width_out:].astype(low)
         message = jnp.concatenate(
             [cut(out, 1 - x, r)[:, :width_out].astype(low), vocab_rows[:r], vocab_rows[r:]], axis=1
         )
-        value = total(2, arrived, passed).astype(low)
-        passed, arrived, out_far, kept_rows = flow.step(
-            (onward, value), (across, theirs[2]), (across, message), (corners, mine[3][:, :both]),
-            also=(flat_one, flat_three),
-        )
-        flat = flat + flat_one + flat_three + onward(flat_one)
+        out_far = across(message)
+        kept_rows = corners(tie(mine[3][:, :both], out_one))
         output_grad = cut(out, x, r)[:, :width_out] + out_far[:, :width_out].astype(wide)
         shard = jnp.concatenate([out[:r, width_out:], out[r:, width_out:]], axis=1)
         shard = (shard + out_far[:, width_out:].astype(wide)).astype(low)
+        shard = jnp.concatenate([shard, halves(flat, r)], axis=1)
+        value = total(2, arrived, passed).astype(low)
+        passed, arrived = flow.step((onward, value), (across, theirs[2]), also=(grad_far,))
+        next_one, next_three = onward(shard), ring.astern(shard)
         value = total(3, arrived, passed).astype(low)
-        passed, arrived, energy_passed, energy_arrived, next_three = flow.step(
+        passed, arrived, energy_passed, energy_arrived = flow.step(
             (cornered(ring.ring), value[:, :both]), (cornered(ring.pair), theirs[3][:, :both]),
-            (onward, jnp.concatenate([value[:, both:], shard], axis=1)),
-            (across, theirs[3][:, both:]), (ring.astern, shard),
-            also=(grad_far, flat),
+            (onward, value[:, both:]), (across, theirs[3][:, both:]),
+            also=(kept_rows, next_one, next_three),
         )
-        flat = flat.reshape(-1)
-        sides = corners(tie(flat[sides_at : sides_at + wide_half + width], value))
-        next_one, energy_passed = energy_passed[:, 4 * block :], energy_passed[:, : 4 * block]
         shards = {0: shard, 1: next_one, 3: next_three, 2: onward(next_one)}
+        flat = sum(joined(a[:, 2 * block :], flat_width).reshape(-1) for a in shards.values())
+        sides = corners(flat[sides_at : sides_at + wide_half + width])
         moved = kept_rows.astype(wide) + arrived.astype(wide) + passed.astype(wide)
         energy_grad = mine[3][:, both:].astype(wide) + energy_arrived.astype(wide)
         energy_grad = energy_grad + energy_passed.astype(wide)

time: 492 us -> 483 us (0.982)
  waiting for transfers between devices: 216 us -> 210 us
    ppermute x11, waiting for transfers between devices: 113 us -> 92.1 us  [across(): return lax.ppermute(array, 'dp', self.pair)]
    ppermute x12 -> x11, waiting for transfers between devices: 58.6 us -> 74.5 us  [onward(): return lax.ppermute(array, 'dp', self.ring)]
    ppermute x4, starting transfers between devices: 12.5 us -> 21.1 us  [corners(): return lax.ppermute(array, ('section', 'mp'), corner_swap)]
    ppermute x12 -> x11, starting transfers between devices: 13.1 us -> 7.92 us  [onward(): return lax.ppermute(array, 'dp', self.ring)]
    ppermute x3 -> x2, starting transfers between devices: 10.2 us -> 5.75 us  [astern(): return lax.ppermute(array, 'dp', self.turn)]
    unnamed x156 -> x158, local copies, waits for them, and re-layouts: 13.8 us -> 13.2 us
  transfers between devices with their start and end apart: 75 -> 73, of which waited for: 23 -> 24; matrix products, arithmetic and copies ran while one was open for 12% -> 12% of each run, Pallas kernels for 24% -> 24%
where the time goes in v7:
time: 483 us; the launch traced here: 481 us
  waiting for transfers between devices  210 us (43%)
  Pallas kernels  117 us (24%)
  starting transfers between devices  78 us (16%)
  local copies, waits for them, and re-layouts  47.8 us (10%)
  other arithmetic  26 us (5%)
    ppermute x11, waiting for transfers between devices, across(): return lax.ppermute(array, 'dp', self.pair)  92.1 us
    ppermute x11, waiting for transfers between devices, onward(): return lax.ppermute(array, 'dp', self.ring)  74.5 us
    pallas_call x1, Pallas kernels, run_attend(): pl.pallas_call(functools.partial(attend_kernel, count), out_shape=(jax.Sh...  31.8 us
    pallas_call x1, Pallas kernels, run_forward(): pl.pallas_call(functools.partial(forward_kernel, count, column), out_shap...  30.6 us
    pallas_call x1, Pallas kernels, run_backward(): pl.pallas_call(functools.partial(backward_kernel, count, column), out_sha...  30.2 us
    ppermute x11, waiting for transfers between devices, across_chips(): return lax.ppermute(array, 'mp', core_swap)  24.4 us
    ppermute x4, starting transfers between devices, corners(): return lax.ppermute(array, ('section', 'mp'), corner_swap)  21.1 us
    ppermute x11, starting transfers between devices, across_chips(): return lax.ppermute(array, 'mp', core_swap)  19.3 us
  transfers between devices with their start and end apart: 73, of which 24 were waited for; matrix products, arithmetic and copies ran while one was open for 12% of the time, Pallas kernels for 24%

profile of v7, /device:TPU:0, one launch (start us, length us, event | category | flops | bytes accessed | tf_op | source)
XLA Modules:
  0.0 480.7 jit_solution(3199614336910818163)
XLA Ops:
  0.7 1.2 copy.73
  3.8 9.6 %collective-permute-start = (bf16[128,4096]{1,0:T(8,128)(2,1)}, bf16[128,4096]{1,0:T(8,128)(2,1)}, u32[]{:S(2)}, u32[]{:S(2)}) collective-permute-start(bf16[128,4096]{1,0:T(8,128)(2,1)} %constant_dynamic-update-slice_fusion), channel_id=1, source_target_pairs={{0,0},{1,16},{16,1},{17,17},{2,2},{3,18},{18,3},{19,19},{4,4},{5,2... | collective-permute-start | bytes 3145736 | tf_op jit(solution)/shard_map/ppermute | solution.py:37
  17.3 3.0 collective-permute-start.1
  20.3 1.5 collective-permute-start.2
  26.1 1.9 collective-permute-done.2
  28.9 1.3 constant_dynamic-update-slice_fusion.7
  30.2 1.6 collective-permute-start.3
  31.8 1.5 collective-permute-start.4
  33.3 2.0 collective-permute-start.6
  35.4 1.3 collective-permute-start.7
  38.2 1.1 copy.63
  40.4 22.9 %collective-permute-done.4.refs_1_.refs_17_ = bf16[128,5632]{1,0:T(8,128)(2,1)} collective-permute-done((bf16[128,5632]{1,0:T(8,128)(2,1)S(1)}, bf16[128,5632]{1,0:T(8,128)(2,1)}, u32[]{:S(2)}, u32[]{:S(2)}) %collective-permute-start.4) | collective-permute-done | bytes 1441824 | tf_op jit(solution)/shard_map/ppermute | solution.py:73
  65.4 1.3 broadcast_in_dim.17.noise
  67.9 1.6 collective-permute-start.12
  70.2 1.3 collective-permute-start.10
  72.5 25.6 %collective-permute-done.13.refs_3_.refs_19_ = bf16[128,5632]{1,0:T(8,128)(2,1)} collective-permute-done((bf16[128,5632]{1,0:T(8,128)(2,1)}, bf16[128,5632]{1,0:T(8,128)(2,1)}, u32[]{:S(2)}, u32[]{:S(2)}) %collective-permute-start.13) | collective-permute-done | bytes 1441824 | tf_op jit(solution)/shard_map/ppermute | solution.py:73
  99.9 1.2 slice.304
  101.1 1.6 collective-permute-start.22
  102.7 4.5 collective-permute-start.18
  107.9 2.7 collective-permute-done.11
  110.7 14.8 %collective-permute-done.18.refs_6_ = bf16[128,3072]{1,0:T(8,128)(2,1)} collective-permute-done((bf16[128,3072]{1,0:T(8,128)(2,1)S(1)}, bf16[128,3072]{1,0:T(8,128)(2,1)}, u32[]{:S(2)}, u32[]{:S(2)}) %collective-permute-start.18) | collective-permute-done | bytes 786464 | tf_op jit(solution)/shard_map/ppermute | solution.py:33
  125.5 4.7 collective-permute-done.22.refs_5_.refs_21_
  131.9 2.7 collective-permute-done.15.refs_6_.refs_22_
  137.0 1.1 collective-permute-done.24.b_other
  139.2 22.1 %collective-permute-done.25.refs_7_.refs_23_ = bf16[128,4096]{1,0:T(8,128)(2,1)S(1)} collective-permute-done((bf16[128,4096]{1,0:T(8,128)(2,1)}, bf16[128,4096]{1,0:T(8,128)(2,1)S(1)}, u32[]{:S(2)}, u32[]{:S(2)}) %collective-permute-start.25) | collective-permute-done | bytes 1048608 | tf_op jit(solution)/shard_map/ppermute | solution.py:73
  161.4 6.3 %collective-permute-start.35 = (bf16[128,3072]{1,0:T(8,128)(2,1)}, bf16[128,3072]{1,0:T(8,128)(2,1)}, u32[]{:S(2)}, u32[]{:S(2)}) collective-permute-start(bf16[128,3072]{1,0:T(8,128)(2,1)} %pad_maximum_fusion.4.refs_3_), channel_id=1, source_target_pairs={{0,1},{1,0},{2,3},{3,2},{4,5},{5,4},{6,7},{7,6},{8,9},{9,8},{10,11... | collective-permute-start | bytes 2359304 | tf_op jit(solution)/shard_map/ppermute | solution.py:33
  170.0 30.6 %recur_forward.1 = (bf16[16,8,1024]{2,1,0:T(8,128)(2,1)}, bf16[16,8,1024]{2,1,0:T(8,128)(2,1)}, bf16[16,16,1024]{2,1,0:T(8,128)(2,1)}, f32[16,16,4096]{2,1,0:T(8,128)}, f32[16,16,1024]{2,1,0:T(8,128)}) custom-call(s32[10]{0:T(128)} %stack.116.places, bf16[256,1024]{1,0:T(8,128)(2,1)} %bitcast.89, f32[1,2048]{1,0:T(1,128)} %copy-done.52, ...), custom_call_target="tpu_custom_call" | custom-call | tf_op jit(solution)/shard_map/recur_forward/pallas_call | solution.py:184
  201.5 8.2 %collective-permute-done.34.taken = bf16[128,1024]{1,0:T(8,128)(2,1)S(1)} collective-permute-done((bf16[128,1024]{1,0:T(8,128)(2,1)}, bf16[128,1024]{1,0:T(8,128)(2,1)S(1)}, u32[]{:S(2)}, u32[]{:S(2)}) %collective-permute-start.34) | collective-permute-done | bytes 262176 | tf_op jit(solution)/shard_map/ppermute | solution.py:33
  213.6 31.8 %attend.1 = (f32[128,1024]{1,0:T(8,128)}, bf16[128,1024]{1,0:T(8,128)(2,1)}, bf16[128,1536]{1,0:T(8,128)(2,1)}, bf16[128,1536]{1,0:T(8,128)(2,1)}, bf16[2,128,15...) custom-call(s32[10]{0:T(128)} %stack.116.places, ...), custom_call_target="tpu_custom_call" | custom-call | tf_op jit(solution)/shard_map/attend/pallas_call | solution.py:650
  245.4 1.4 collective-permute-start.43
  247.3 1.2 pad_maximum_fusion.1.states_own
  250.9 1.3 pad_maximum_fusion.5
  252.3 1.5 collective-permute-done.43
  253.7 1.3 collective-permute-start.47
  255.8 30.2 %recur_backward.1 = bf16[2,16,16,2048]{3,2,1,0:T(8,128)(2,1)} custom-call(s32[10]{0:T(128)} %stack.116.places, f32[16,8,1024]{2,1,0:T(8,128)} %bitcast.104, bf16[16,8,1024]{2,1,0:T(8,128)(2,1)} %bitcast.39.taken, f32[16,16,4096]{2,1,0:T(8,128)} %get-tuple-element.126.gates, f32[16,16,1024]{2,1,0:T(8,128)} %get-tuple-element.127.cells, ...), custom_call_target="tpu_custom_call" | custom-call | tf_op jit(solution)/shard_map/recur_backward/pallas_call | solution.py:286
  286.0 1.6 slice_bitcast_fusion
  290.7 8.9 %input_back.1 = (f32[256,1024]{1,0:T(8,128)}, f32[1,1024]{1,0:T(1,128)}) custom-call(s32[10]{0:T(128)} %stack.116.places, bf16[256,1024]{1,0:T(8,128)(2,1)} %bitcast.94, f32[1,1024]{1,0:T(1,128)} %bitcast.115, bf16[2,256,2048]{2,1,0:T(8,128)(2,1)} %bitcast.86, bf16[128,5632]{1,0:T(8,128)(2,1)} %copy-done.4, ...), custom_call_target="tpu_custom_call" | custom-call | tf_op jit(solution)/shard_map/input_back/pallas_call | solution.py:332
  299.6 2.8 copy.82
  304.4 15.2 %weight_gradients.1 = (bf16[128,5120]{1,0:T(8,128)(2,1)}, bf16[128,5120]{1,0:T(8,128)(2,1)}, bf16[128,5120]{1,0:T(8,128)(2,1)}, bf16[128,5120]{1,0:T(8,128)(2,1)...) custom-call(s32[13]{0:T(128)} %stack.135.order, ...), custom_call_target="tpu_custom_call" | custom-call | tf_op jit(solution)/shard_map/weight_gradients/pallas_call | solution.py:807
  323.0 3.2 collective-permute-start.55
  326.1 1.9 broadcast_select_fusion.2
  328.0 7.1 %collective-permute-done.56 = bf16[256,768]{1,0:T(8,128)(2,1)} collective-permute-done((bf16[256,768]{1,0:T(8,128)(2,1)}, bf16[256,768]{1,0:T(8,128)(2,1)}, u32[]{:S(2)}, u32[]{:S(2)}) %collective-permute-start.56) | collective-permute-done | bytes 393248 | tf_op jit(solution)/shard_map/ppermute | solution.py:76
  335.1 1.1 add_convert_fusion.3
  336.2 14.9 %collective-permute-done.57 = bf16[128,5120]{1,0:T(8,128)(2,1)} collective-permute-done((bf16[128,5120]{1,0:T(8,128)(2,1)}, bf16[128,5120]{1,0:T(8,128)(2,1)}, u32[]{:S(2)}, u32[]{:S(2)}) %collective-permute-start.57) | collective-permute-done | bytes 1310752 | tf_op jit(solution)/shard_map/ppermute | solution.py:73
  351.7 1.5 pad_maximum_fusion
  355.4 4.6 collective-permute-start.50
  360.0 1.1 slice.269
  361.3 1.6 collective-permute-done.58
  362.9 1.2 fusion.20
  364.2 1.1 collective-permute-start.59
  365.3 1.7 add_convert_fusion.2
  368.2 9.5 %collective-permute-start.64 = (bf16[128,4096]{1,0:T(8,128)(2,1)}, bf16[128,4096]{1,0:T(8,128)(2,1)}, u32[]{:S(2)}, u32[]{:S(2)}) collective-permute-start(bf16[128,4096]{1,0:T(8,128)(2,1)} %slice.269), channel_id=1, source_target_pairs={{0,0},{1,16},{16,1},{17,17},{2,2},{3,18},{18,3},{19,19},{4,4},{5,2... | collective-permute-start | bytes 3145736 | tf_op jit(solution)/shard_map/ppermute | solution.py:37
  378.8 13.8 %collective-permute-done.50 = f32[32,16,1024]{2,1,0:T(8,128)} collective-permute-done((f32[32,16,1024]{2,1,0:T(8,128)}, f32[32,16,1024]{2,1,0:T(8,128)}, u32[]{:S(2)}, u32[]{:S(2)}) %collective-permute-start.50) | collective-permute-done | bytes 2097184 | tf_op jit(solution)/shard_map/ppermute | solution.py:1047
  392.7 2.6 collective-permute-start.61
  395.3 1.7 select_bitcast_fusion
  397.0 6.2 %collective-permute-done.60 = bf16[128,640]{1,0:T(8,128)(2,1)S(1)} collective-permute-done((bf16[128,640]{1,0:T(8,128)(2,1)S(1)}, bf16[128,640]{1,0:T(8,128)(2,1)S(1)}, u32[]{:S(2)}, u32[]{:S(2)}) %collective-permute-start.60) | collective-permute-done | bytes 163872 | tf_op jit(solution)/shard_map/ppermute | solution.py:76
  403.3 1.7 add_convert_fusion.1
  406.8 5.3 %collective-permute-done.62 = bf16[128,640]{1,0:T(8,128)(2,1)S(1)} collective-permute-done((bf16[128,640]{1,0:T(8,128)(2,1)S(1)}, bf16[128,640]{1,0:T(8,128)(2,1)S(1)}, u32[]{:S(2)}, u32[]{:S(2)}) %collective-permute-start.62) | collective-permute-done | bytes 163872 | tf_op jit(solution)/shard_map/ppermute | solution.py:76
  413.0 23.1 %collective-permute-done.68 = bf16[128,5120]{1,0:T(8,128)(2,1)} collective-permute-done((bf16[128,5120]{1,0:T(8,128)(2,1)}, bf16[128,5120]{1,0:T(8,128)(2,1)}, u32[]{:S(2)}, u32[]{:S(2)}) %collective-permute-start.68) | collective-permute-done | bytes 1310752 | tf_op jit(solution)/shard_map/ppermute | solution.py:76
  436.1 2.3 add_convert_fusion
  445.8 27.8 %collective-permute-done.72 = bf16[128,1024]{1,0:T(8,128)(2,1)S(1)} collective-permute-done((bf16[128,1024]{1,0:T(8,128)(2,1)}, bf16[128,1024]{1,0:T(8,128)(2,1)S(1)}, u32[]{:S(2)}, u32[]{:S(2)}) %collective-permute-start.72) | collective-permute-done | bytes 262176 | tf_op jit(solution)/shard_map/ppermute | solution.py:76
  475.5 1.6 convert_add_fusion
  477.3 1.7 reshape.202
  479.0 1.7 reshape.203
  (374 shorter events, 62.4 us)
Async XLA Ops:
  3.8 25.1 %collective-permute-start = (bf16[128,4096]{1,0:T(8,128)(2,1)}, bf16[128,4096]{1,0:T(8,128)(2,1)}, u32[]{:S(2)}, u32[]{:S(2)}) collective-permute-start(bf16[128,4096]{1,0:T(8,128)(2,1)} %constant_dynamic-update-slice_fusion), channel_id=1, source_target_pairs={{0,0},{1,16},{16,1},{17,17},{2,2},{3,18},{18,3},{19,19},{4,4},{5,2... | collective-permute-start | bytes 3145736 | tf_op jit(solution)/shard_map/ppermute | solution.py:37
  17.3 12.9 %collective-permute-start.1 = (bf16[128,1536]{1,0:T(8,128)(2,1)S(1)}, bf16[128,1536]{1,0:T(8,128)(2,1)S(1)}, u32[]{:S(2)}, u32[]{:S(2)}) collective-permute-start(bf16[128,1536]{1,0:T(8,128)(2,1)S(1)} %get-tuple-element.199), channel_id=1, source_target_pairs={{0,4},{2,6},{4,8},{6,10},{8,12},{10,14},{12,0},{14,2},{1,5},{3,7},... | collective-permute-start | bytes 1179656 | tf_op jit(solution)/shard_map/ppermute | solution.py:76
  20.3 7.8 %collective-permute-start.2 = (bf16[128,1536]{1,0:T(8,128)(2,1)S(1)}, bf16[128,1536]{1,0:T(8,128)(2,1)S(1)}, u32[]{:S(2)}, u32[]{:S(2)}) collective-permute-start(bf16[128,1536]{1,0:T(8,128)(2,1)S(1)} %get-tuple-element.199), channel_id=1, source_target_pairs={{0,2},{2,0},{4,6},{6,4},{8,10},{10,8},{12,14},{14,12},{1,3},{3,1},... | collective-permute-start | bytes 1179656 | tf_op jit(solution)/shard_map/ppermute | solution.py:73
  21.8 13.6 %collective-permute-start.8 = (bf16[16,32,1024]{2,0,1:T(8,128)(2,1)S(1)}, bf16[16,32,1024]{2,0,1:T(8,128)(2,1)}, u32[]{:S(2)}, u32[]{:S(2)}) collective-permute-start(bf16[16,32,1024]{2,0,1:T(8,128)(2,1)S(1)} %bitcast.102), channel_id=1, source_target_pairs={{0,16},{16,0},{1,17},{17,1},{2,18},{18,2},{3,19},{19,3},{4,20},{20... | collective-permute-start | bytes 3145736 | tf_op jit(solution)/shard_map/ppermute | solution.py:29
  30.2 35.2 %collective-permute-start.3 = (bf16[128,5632]{1,0:T(8,128)(2,1)S(1)}, bf16[128,5632]{1,0:T(8,128)(2,1)}, u32[]{:S(2)}, u32[]{:S(2)}) collective-permute-start(bf16[128,5632]{1,0:T(8,128)(2,1)S(1)} %constant_dynamic-update-slice_fusion.6.refs_0_.refs_16_), channel_id=1, source_target_pairs={{0,4},{2,6},{4,8},{6,10},{8,12},{10,14},{12,0},{14,2},{1,5},{3,7},... | collective-permute-start | bytes 4325384 | tf_op jit(solution)/shard_map/ppermute | solution.py:76
  31.8 31.5 %collective-permute-start.4 = (bf16[128,5632]{1,0:T(8,128)(2,1)S(1)}, bf16[128,5632]{1,0:T(8,128)(2,1)}, u32[]{:S(2)}, u32[]{:S(2)}) collective-permute-start(bf16[128,5632]{1,0:T(8,128)(2,1)S(1)} %constant_dynamic-update-slice_fusion.6.refs_0_.refs_16_), channel_id=1, source_target_pairs={{0,2},{2,0},{4,6},{6,4},{8,10},{10,8},{12,14},{14,12},{1,3},{3,1},... | collective-permute-start | bytes 4325384 | tf_op jit(solution)/shard_map/ppermute | solution.py:73
  33.3 32.0 %collective-permute-start.5 = (bf16[128,3072]{1,0:T(8,128)(2,1)}, bf16[128,3072]{1,0:T(8,128)(2,1)}, u32[]{:S(2)}, u32[]{:S(2)}) collective-permute-start(bf16[128,3072]{1,0:T(8,128)(2,1)} %constant_dynamic-update-slice_fusion.8.refs_0_), channel_id=1, source_target_pairs={{0,1},{1,0},{2,3},{3,2},{4,5},{5,4},{6,7},{7,6},{8,9},{9,8},{10,11... | collective-permute-start | bytes 2359304 | tf_op jit(solution)/shard_map/ppermute | solution.py:33
  33.3 32.0 %collective-permute-start.6 = (bf16[256,1024]{1,0:T(8,128)(2,1)S(1)}, bf16[256,1024]{1,0:T(8,128)(2,1)S(1)}, u32[]{:S(2)}, u32[]{:S(2)}) collective-permute-start(bf16[256,1024]{1,0:T(8,128)(2,1)S(1)} %pad.24.refs_16_), channel_id=1, source_target_pairs={{0,1},{1,0},{2,3},{3,2},{4,5},{5,4},{6,7},{7,6},{8,9},{9,8},{10,11... | collective-permute-start | bytes 1572872 | tf_op jit(solution)/shard_map/ppermute | solution.py:33
  35.4 30.0 %collective-permute-start.7 = (bf16[1,2048]{1,0:T(2,128)(2,1)}, bf16[1,2048]{1,0:T(2,128)(2,1)S(1)}, u32[]{:S(2)}, u32[]{:S(2)}) collective-permute-start(bf16[1,2048]{1,0:T(2,128)(2,1)} %bitcast.65), channel_id=1, source_target_pairs={{0,0},{1,16},{16,1},{17,17},{2,2},{3,18},{18,3},{19,19},{4,4},{5,2... | collective-permute-start | bytes 12296 | tf_op jit(solution)/shard_map/ppermute | solution.py:37
  67.4 30.8 %collective-permute-start.13 = (bf16[128,5632]{1,0:T(8,128)(2,1)}, bf16[128,5632]{1,0:T(8,128)(2,1)}, u32[]{:S(2)}, u32[]{:S(2)}) collective-permute-start(bf16[128,5632]{1,0:T(8,128)(2,1)} %collective-permute-done.3.refs_2_.refs_18_), channel_id=1, source_target_pairs={{0,2},{2,0},{4,6},{6,4},{8,10},{10,8},{12,14},{14,12},{1,3},{3,1},... | collective-permute-start | bytes 4325384 | tf_op jit(solution)/shard_map/ppermute | solution.py:73
  67.9 32.0 %collective-permute-start.12 = (bf16[128,5632]{1,0:T(8,128)(2,1)}, bf16[128,5632]{1,0:T(8,128)(2,1)S(1)}, u32[]{:S(2)}, u32[]{:S(2)}) collective-permute-start(bf16[128,5632]{1,0:T(8,128)(2,1)} %collective-permute-done.3.refs_2_.refs_18_), channel_id=1, source_target_pairs={{0,4},{2,6},{4,8},{6,10},{8,12},{10,14},{12,0},{14,2},{1,5},{3,7},... | collective-permute-start | bytes 4325384 | tf_op jit(solution)/shard_map/ppermute | solution.py:76
  69.5 31.6 %collective-permute-start.14 = (bf16[128,3072]{1,0:T(8,128)(2,1)}, bf16[128,3072]{1,0:T(8,128)(2,1)}, u32[]{:S(2)}, u32[]{:S(2)}) collective-permute-start(bf16[128,3072]{1,0:T(8,128)(2,1)} %pad_maximum_fusion.2.refs_1_), channel_id=1, source_target_pairs={{0,1},{1,0},{2,3},{3,2},{4,5},{5,4},{6,7},{7,6},{8,9},{9,8},{10,11... | collective-permute-start | bytes 2359304 | tf_op jit(solution)/shard_map/ppermute | solution.py:33
  70.2 37.3 %collective-permute-start.26 = (bf16[128,5632]{1,0:T(8,128)(2,1)S(1)}, bf16[128,5632]{1,0:T(8,128)(2,1)S(1)}, u32[]{:S(2)}, u32[]{:S(2)}) collective-permute-start(bf16[128,5632]{1,0:T(8,128)(2,1)S(1)} %constant_dynamic-update-slice_fusion.6.refs_0_.refs_16_), channel_id=1, source_target_pairs={{0,16},{16,0},{1,17},{17,1},{2,18},{18,2},{3,19},{19,3},{4,20},{20... | collective-permute-start | bytes 4325384 | tf_op jit(solution)/shard_map/ppermute | solution.py:29
  70.2 30.9 %collective-permute-start.10 = (f32[5,256]{1,0:T(8,128)S(1)}, f32[5,256]{1,0:T(8,128)S(1)}, u32[]{:S(2)}, u32[]{:S(2)}) collective-permute-start(f32[5,256]{1,0:T(8,128)S(1)} %stack.122), channel_id=1, source_target_pairs={{0,1},{1,0},{2,3},{3,2},{4,5},{5,4},{6,7},{7,6},{8,9},{9,8},{10,11... | collective-permute-start | bytes 15368 | tf_op jit(solution)/shard_map/ppermute | solution.py:33
  101.1 29.1 %collective-permute-start.22 = (bf16[128,5632]{1,0:T(8,128)(2,1)S(1)}, bf16[128,5632]{1,0:T(8,128)(2,1)S(1)}, u32[]{:S(2)}, u32[]{:S(2)}) collective-permute-start(bf16[128,5632]{1,0:T(8,128)(2,1)S(1)} %collective-permute-done.12.refs_4_.refs_20_), channel_id=1, source_target_pairs={{0,2},{2,0},{4,6},{6,4},{8,10},{10,8},{12,14},{14,12},{1,3},{3,1},... | collective-permute-start | bytes 4325384 | tf_op jit(solution)/shard_map/ppermute | solution.py:73
  102.7 4.5 collective-permute-start.19
  102.7 22.8 %collective-permute-start.18 = (bf16[128,3072]{1,0:T(8,128)(2,1)S(1)}, bf16[128,3072]{1,0:T(8,128)(2,1)}, u32[]{:S(2)}, u32[]{:S(2)}) collective-permute-start(bf16[128,3072]{1,0:T(8,128)(2,1)S(1)} %pad_maximum_fusion.3.refs_2_), channel_id=1, source_target_pairs={{0,1},{1,0},{2,3},{3,2},{4,5},{5,4},{6,7},{7,6},{8,9},{9,8},{10,11... | collective-permute-start | bytes 2359304 | tf_op jit(solution)/shard_map/ppermute | solution.py:33
  107.2 27.4 %collective-permute-start.15 = (bf16[128,4096]{1,0:T(8,128)(2,1)}, bf16[128,4096]{1,0:T(8,128)(2,1)}, u32[]{:S(2)}, u32[]{:S(2)}) collective-permute-start(bf16[128,4096]{1,0:T(8,128)(2,1)} %slice.304), channel_id=1, source_target_pairs={{0,4},{2,6},{4,8},{6,10},{8,12},{10,14},{12,0},{14,2},{1,5},{3,7},... | collective-permute-start | bytes 3145736 | tf_op jit(solution)/shard_map/ppermute | solution.py:76
  107.2 28.9 %collective-permute-start.27 = (bf16[128,5632]{1,0:T(8,128)(2,1)}, bf16[128,5632]{1,0:T(8,128)(2,1)}, u32[]{:S(2)}, u32[]{:S(2)}) collective-permute-start(bf16[128,5632]{1,0:T(8,128)(2,1)} %collective-permute-done.4.refs_1_.refs_17_), channel_id=1, source_target_pairs={{0,16},{16,0},{1,17},{17,1},{2,18},{18,2},{3,19},{19,3},{4,20},{20... | collective-permute-start | bytes 4325384 | tf_op jit(solution)/shard_map/ppermute | solution.py:29
  110.5 25.9 %collective-permute-start.28 = (bf16[128,5632]{1,0:T(8,128)(2,1)}, bf16[128,5632]{1,0:T(8,128)(2,1)}, u32[]{:S(2)}, u32[]{:S(2)}) collective-permute-start(bf16[128,5632]{1,0:T(8,128)(2,1)} %collective-permute-done.3.refs_2_.refs_18_), channel_id=1, source_target_pairs={{0,16},{16,0},{1,17},{17,1},{2,18},{18,2},{3,19},{19,3},{4,20},{20... | collective-permute-start | bytes 4325384 | tf_op jit(solution)/shard_map/ppermute | solution.py:29
  125.5 12.9 %collective-permute-start.29 = (bf16[128,5632]{1,0:T(8,128)(2,1)}, bf16[128,5632]{1,0:T(8,128)(2,1)}, u32[]{:S(2)}, u32[]{:S(2)}) collective-permute-start(bf16[128,5632]{1,0:T(8,128)(2,1)} %collective-permute-done.13.refs_3_.refs_19_), channel_id=1, source_target_pairs={{0,16},{16,0},{1,17},{17,1},{2,18},{18,2},{3,19},{19,3},{4,20},{20... | collective-permute-start | bytes 4325384 | tf_op jit(solution)/shard_map/ppermute | solution.py:29
  130.2 5.4 %collective-permute-start.20 = (bf16[128,3072]{1,0:T(8,128)(2,1)}, bf16[128,3072]{1,0:T(8,128)(2,1)}, u32[]{:S(2)}, u32[]{:S(2)}) collective-permute-start(bf16[128,3072]{1,0:T(8,128)(2,1)} %pad_maximum_fusion.2.refs_1_), channel_id=1, source_target_pairs={{0,16},{16,0},{1,17},{17,1},{2,18},{18,2},{3,19},{19,3},{4,20},{20... | collective-permute-start | bytes 2359304 | tf_op jit(solution)/shard_map/ppermute | solution.py:29
  135.6 25.8 %collective-permute-start.25 = (bf16[128,4096]{1,0:T(8,128)(2,1)}, bf16[128,4096]{1,0:T(8,128)(2,1)S(1)}, u32[]{:S(2)}, u32[]{:S(2)}) collective-permute-start(bf16[128,4096]{1,0:T(8,128)(2,1)} %collective-permute-done.15.refs_6_.refs_22_), channel_id=1, source_target_pairs={{0,2},{2,0},{4,6},{6,4},{8,10},{10,8},{12,14},{14,12},{1,3},{3,1},... | collective-permute-start | bytes 3145736 | tf_op jit(solution)/shard_map/ppermute | solution.py:73
  138.1 23.3 %collective-permute-start.23 = (bf16[128,3072]{1,0:T(8,128)(2,1)}, bf16[128,3072]{1,0:T(8,128)(2,1)S(1)}, u32[]{:S(2)}, u32[]{:S(2)}) collective-permute-start(bf16[128,3072]{1,0:T(8,128)(2,1)} %pad_maximum_fusion.4.refs_3_), channel_id=1, source_target_pairs={{0,16},{16,0},{1,17},{17,1},{2,18},{18,2},{3,19},{19,3},{4,20},{20... | collective-permute-start | bytes 2359304 | tf_op jit(solution)/shard_map/ppermute | solution.py:29
  138.4 29.3 %collective-permute-start.30 = (bf16[128,5632]{1,0:T(8,128)(2,1)S(1)}, bf16[128,5632]{1,0:T(8,128)(2,1)S(1)}, u32[]{:S(2)}, u32[]{:S(2)}) collective-permute-start(bf16[128,5632]{1,0:T(8,128)(2,1)S(1)} %collective-permute-done.12.refs_4_.refs_20_), channel_id=1, source_target_pairs={{0,16},{16,0},{1,17},{17,1},{2,18},{18,2},{3,19},{19,3},{4,20},{20... | collective-permute-start | bytes 4325384 | tf_op jit(solution)/shard_map/ppermute | solution.py:29
  138.7 29.5 %collective-permute-start.31 = (bf16[128,5632]{1,0:T(8,128)(2,1)S(1)}, bf16[128,5632]{1,0:T(8,128)(2,1)S(1)}, u32[]{:S(2)}, u32[]{:S(2)}) collective-permute-start(bf16[128,5632]{1,0:T(8,128)(2,1)S(1)} %collective-permute-done.22.refs_5_.refs_21_), channel_id=1, source_target_pairs={{0,16},{16,0},{1,17},{17,1},{2,18},{18,2},{3,19},{19,3},{4,20},{20... | collective-permute-start | bytes 4325384 | tf_op jit(solution)/shard_map/ppermute | solution.py:29
  139.0 28.8 %collective-permute-start.32 = (bf16[128,4096]{1,0:T(8,128)(2,1)}, bf16[128,4096]{1,0:T(8,128)(2,1)S(1)}, u32[]{:S(2)}, u32[]{:S(2)}) collective-permute-start(bf16[128,4096]{1,0:T(8,128)(2,1)} %collective-permute-done.15.refs_6_.refs_22_), channel_id=1, source_target_pairs={{0,16},{16,0},{1,17},{17,1},{2,18},{18,2},{3,19},{19,3},{4,20},{20... | collective-permute-start | bytes 3145736 | tf_op jit(solution)/shard_map/ppermute | solution.py:29
  161.4 7.9 %collective-permute-start.33 = (bf16[128,4096]{1,0:T(8,128)(2,1)S(1)}, bf16[128,4096]{1,0:T(8,128)(2,1)}, u32[]{:S(2)}, u32[]{:S(2)}) collective-permute-start(bf16[128,4096]{1,0:T(8,128)(2,1)S(1)} %collective-permute-done.25.refs_7_.refs_23_), channel_id=1, source_target_pairs={{0,16},{16,0},{1,17},{17,1},{2,18},{18,2},{3,19},{19,3},{4,20},{20... | collective-permute-start | bytes 3145736 | tf_op jit(solution)/shard_map/ppermute | solution.py:29
  161.4 39.2 %collective-permute-start.35 = (bf16[128,3072]{1,0:T(8,128)(2,1)}, bf16[128,3072]{1,0:T(8,128)(2,1)}, u32[]{:S(2)}, u32[]{:S(2)}) collective-permute-start(bf16[128,3072]{1,0:T(8,128)(2,1)} %pad_maximum_fusion.4.refs_3_), channel_id=1, source_target_pairs={{0,1},{1,0},{2,3},{3,2},{4,5},{5,4},{6,7},{7,6},{8,9},{9,8},{10,11... | collective-permute-start | bytes 2359304 | tf_op jit(solution)/shard_map/ppermute | solution.py:33
  167.7 44.2 %collective-permute-start.36 = (bf16[128,3072]{1,0:T(8,128)(2,1)}, bf16[128,3072]{1,0:T(8,128)(2,1)S(1)}, u32[]{:S(2)}, u32[]{:S(2)}) collective-permute-start(bf16[128,3072]{1,0:T(8,128)(2,1)} %collective-permute-done.5.refs_4_), channel_id=1, source_target_pairs={{0,16},{16,0},{1,17},{17,1},{2,18},{18,2},{3,19},{19,3},{4,20},{20... | collective-permute-start | bytes 2359304 | tf_op jit(solution)/shard_map/ppermute | solution.py:29
  167.8 44.1 %collective-permute-start.37 = (bf16[128,3072]{1,0:T(8,128)(2,1)}, bf16[128,3072]{1,0:T(8,128)(2,1)}, u32[]{:S(2)}, u32[]{:S(2)}) collective-permute-start(bf16[128,3072]{1,0:T(8,128)(2,1)} %collective-permute-done.14.refs_5_), channel_id=1, source_target_pairs={{0,16},{16,0},{1,17},{17,1},{2,18},{18,2},{3,19},{19,3},{4,20},{20... | collective-permute-start | bytes 2359304 | tf_op jit(solution)/shard_map/ppermute | solution.py:29
  168.9 43.0 %collective-permute-start.38 = (bf16[128,3072]{1,0:T(8,128)(2,1)}, bf16[128,3072]{1,0:T(8,128)(2,1)}, u32[]{:S(2)}, u32[]{:S(2)}) collective-permute-start(bf16[128,3072]{1,0:T(8,128)(2,1)} %collective-permute-done.18.refs_6_), channel_id=1, source_target_pairs={{0,16},{16,0},{1,17},{17,1},{2,18},{18,2},{3,19},{19,3},{4,20},{20... | collective-permute-start | bytes 2359304 | tf_op jit(solution)/shard_map/ppermute | solution.py:29
  200.6 11.3 %collective-permute-start.39 = (bf16[128,3072]{1,0:T(8,128)(2,1)}, bf16[128,3072]{1,0:T(8,128)(2,1)S(1)}, u32[]{:S(2)}, u32[]{:S(2)}) collective-permute-start(bf16[128,3072]{1,0:T(8,128)(2,1)} %collective-permute-done.35.refs_7_), channel_id=1, source_target_pairs={{0,16},{16,0},{1,17},{17,1},{2,18},{18,2},{3,19},{19,3},{4,20},{20... | collective-permute-start | bytes 2359304 | tf_op jit(solution)/shard_map/ppermute | solution.py:29
  201.0 8.6 %collective-permute-start.34 = (bf16[128,1024]{1,0:T(8,128)(2,1)}, bf16[128,1024]{1,0:T(8,128)(2,1)S(1)}, u32[]{:S(2)}, u32[]{:S(2)}) collective-permute-start(bf16[128,1024]{1,0:T(8,128)(2,1)} %bitcast.112), channel_id=1, source_target_pairs={{0,1},{1,0},{2,3},{3,2},{4,5},{5,4},{6,7},{7,6},{8,9},{9,8},{10,11... | collective-permute-start | bytes 786440 | tf_op jit(solution)/shard_map/ppermute | solution.py:33
  209.6 35.7 %collective-permute-start.42 = (bf16[128,1024]{1,0:T(8,128)(2,1)}, bf16[128,1024]{1,0:T(8,128)(2,1)S(1)}, u32[]{:S(2)}, u32[]{:S(2)}) collective-permute-start(bf16[128,1024]{1,0:T(8,128)(2,1)} %bitcast.98), channel_id=1, source_target_pairs={{0,1},{1,0},{2,3},{3,2},{4,5},{5,4},{6,7},{7,6},{8,9},{9,8},{10,11... | collective-permute-start | bytes 786440 | tf_op jit(solution)/shard_map/ppermute | solution.py:33
  211.8 40.4 %collective-permute-start.44 = (bf16[256,1024]{1,0:T(8,128)(2,1)}, bf16[256,1024]{1,0:T(8,128)(2,1)}, u32[]{:S(2)}, u32[]{:S(2)}) collective-permute-start(bf16[256,1024]{1,0:T(8,128)(2,1)} %bitcast.105), channel_id=1, source_target_pairs={{0,16},{16,0},{1,17},{17,1},{2,18},{18,2},{3,19},{19,3},{4,20},{20... | collective-permute-start | bytes 1572872 | tf_op jit(solution)/shard_map/ppermute | solution.py:29
  245.4 8.3 %collective-permute-start.43 = (bf16[128,1024]{1,0:T(8,128)(2,1)}, bf16[128,1024]{1,0:T(8,128)(2,1)}, u32[]{:S(2)}, u32[]{:S(2)}) collective-permute-start(bf16[128,1024]{1,0:T(8,128)(2,1)} %get-tuple-element.119), channel_id=1, source_target_pairs={{0,1},{1,0},{2,3},{3,2},{4,5},{5,4},{6,7},{7,6},{8,9},{9,8},{10,11... | collective-permute-start | bytes 786440 | tf_op jit(solution)/shard_map/ppermute | solution.py:33
  248.5 5.2 %collective-permute-start.45 = (bf16[4,128,1024]{2,1,0:T(8,128)(2,1)S(1)}, bf16[4,128,1024]{2,1,0:T(8,128)(2,1)}, u32[]{:S(2)}, u32[]{:S(2)}) collective-permute-start(bf16[4,128,1024]{2,1,0:T(8,128)(2,1)S(1)} %pad_maximum_fusion.1.states_own), channel_id=1, source_target_pairs={{0,16},{16,0},{1,17},{17,1},{2,18},{18,2},{3,19},{19,3},{4,20},{20... | collective-permute-start | bytes 3145736 | tf_op jit(solution)/shard_map/ppermute | solution.py:29
  253.7 32.2 %collective-permute-start.47 = (bf16[2,128,1536]{2,1,0:T(8,128)(2,1)S(1)}, bf16[2,128,1536]{2,1,0:T(8,128)(2,1)S(1)}, u32[]{:S(2)}, u32[]{:S(2)}) collective-permute-start(bf16[2,128,1536]{2,1,0:T(8,128)(2,1)S(1)} %pad_maximum_fusion.5), channel_id=1, source_target_pairs={{0,1},{1,0},{2,3},{3,2},{4,5},{5,4},{6,7},{7,6},{8,9},{9,8},{10,11... | collective-permute-start | bytes 2359304 | tf_op jit(solution)/shard_map/ppermute | solution.py:33
  255.1 30.9 %collective-permute-start.48 = (bf16[2,128,1152]{2,1,0:T(8,128)(2,1)S(1)}, bf16[2,128,1152]{2,1,0:T(8,128)(2,1)}, u32[]{:S(2)}, u32[]{:S(2)}) collective-permute-start(bf16[2,128,1152]{2,1,0:T(8,128)(2,1)S(1)} %pad_maximum_fusion.6), channel_id=1, source_target_pairs={{0,1},{1,0},{2,3},{3,2},{4,5},{5,4},{6,7},{7,6},{8,9},{9,8},{10,11... | collective-permute-start | bytes 1769480 | tf_op jit(solution)/shard_map/ppermute | solution.py:33
  287.5 15.7 %collective-permute-start.51 = (bf16[256,2048]{1,0:T(8,128)(2,1)S(1)}, bf16[256,2048]{1,0:T(8,128)(2,1)S(1)}, u32[]{:S(2)}, u32[]{:S(2)}) collective-permute-start(bf16[256,2048]{1,0:T(8,128)(2,1)S(1)} %slice_bitcast_fusion), channel_id=1, source_target_pairs={{0,16},{16,0},{1,17},{17,1},{2,18},{18,2},{3,19},{19,3},{4,20},{20... | collective-permute-start | bytes 3145736 | tf_op jit(solution)/shard_map/ppermute | solution.py:29
  287.6 15.6 %collective-permute-start.54 = (bf16[2,128,1152]{2,1,0:T(8,128)(2,1)}, bf16[2,128,1152]{2,1,0:T(8,128)(2,1)S(1)}, u32[]{:S(2)}, u32[]{:S(2)}) collective-permute-start(bf16[2,128,1152]{2,1,0:T(8,128)(2,1)} %collective-permute-done.48.far), channel_id=1, source_target_pairs={{0,16},{16,0},{1,17},{17,1},{2,18},{18,2},{3,19},{19,3},{4,20},{20... | collective-permute-start | bytes 1769480 | tf_op jit(solution)/shard_map/ppermute | solution.py:29
  302.4 23.7 %collective-permute-start.49 = (f32[16,16,1024]{2,1,0:T(8,128)}, f32[16,16,1024]{2,1,0:T(8,128)}, u32[]{:S(2)}, u32[]{:S(2)}) collective-permute-start(f32[16,16,1024]{2,1,0:T(8,128)} %bitcast.84), channel_id=1, source_target_pairs={{0,16},{16,0},{1,17},{17,1},{2,18},{18,2},{3,19},{19,3},{4,20},{20... | collective-permute-start | bytes 3145736 | tf_op jit(solution)/shard_map/ppermute | solution.py:29
  302.5 18.4 %collective-permute-start.52 = (f32[1024]{0:T(1024)S(1)}, f32[1024]{0:T(1024)S(1)}, u32[]{:S(2)}, u32[]{:S(2)}) collective-permute-start(f32[1024]{0:T(1024)S(1)} %bitcast.122), channel_id=1, source_target_pairs={{0,16},{16,0},{1,17},{17,1},{2,18},{18,2},{3,19},{19,3},{4,20},{20... | collective-permute-start | bytes 12296 | tf_op jit(solution)/shard_map/ppermute | solution.py:29
  319.6 31.4 %collective-permute-start.57 = (bf16[128,5120]{1,0:T(8,128)(2,1)}, bf16[128,5120]{1,0:T(8,128)(2,1)}, u32[]{:S(2)}, u32[]{:S(2)}) collective-permute-start(bf16[128,5120]{1,0:T(8,128)(2,1)} %get-tuple-element.145), channel_id=1, source_target_pairs={{0,2},{2,0},{4,6},{6,4},{8,10},{10,8},{12,14},{14,12},{1,3},{3,1},... | collective-permute-start | bytes 3932168 | tf_op jit(solution)/shard_map/ppermute | solution.py:73
  320.9 14.2 %collective-permute-start.56 = (bf16[256,768]{1,0:T(8,128)(2,1)}, bf16[256,768]{1,0:T(8,128)(2,1)}, u32[]{:S(2)}, u32[]{:S(2)}) collective-permute-start(bf16[256,768]{1,0:T(8,128)(2,1)} %get-tuple-element.144), channel_id=1, source_target_pairs={{0,4},{2,6},{4,8},{6,10},{8,12},{10,14},{12,0},{14,2},{1,5},{3,7},... | collective-permute-start | bytes 1179656 | tf_op jit(solution)/shard_map/ppermute | solution.py:76
  321.9 39.2 %collective-permute-start.53 = (f32[8,768]{1,0:T(8,128)S(1)}, f32[8,768]{1,0:T(8,128)S(1)}, u32[]{:S(2)}, u32[]{:S(2)}) collective-permute-start(f32[8,768]{1,0:T(8,128)S(1)} %reshape.198), channel_id=1, source_target_pairs={{0,2},{2,0},{4,6},{6,4},{8,10},{10,8},{12,14},{14,12},{1,3},{3,1},... | collective-permute-start | bytes 73736 | tf_op jit(solution)/shard_map/ppermute | solution.py:73
  323.0 38.3 %collective-permute-start.55 = (bf16[256,768]{1,0:T(8,128)(2,1)}, bf16[256,768]{1,0:T(8,128)(2,1)}, u32[]{:S(2)}, u32[]{:S(2)}) collective-permute-start(bf16[256,768]{1,0:T(8,128)(2,1)} %get-tuple-element.142), channel_id=1, source_target_pairs={{4,0},{6,2},{8,4},{10,6},{12,8},{14,10},{0,12},{2,14},{5,1},{7,3},... | collective-permute-start | bytes 1179656 | tf_op jit(solution)/shard_map/ppermute | solution.py:79
  351.1 11.8 %collective-permute-start.58 = (bf16[256,768]{1,0:T(8,128)(2,1)S(1)}, bf16[256,768]{1,0:T(8,128)(2,1)S(1)}, u32[]{:S(2)}, u32[]{:S(2)}) collective-permute-start(bf16[256,768]{1,0:T(8,128)(2,1)S(1)} %add_convert_fusion.3), channel_id=1, source_target_pairs={{0,4},{2,6},{4,8},{6,10},{8,12},{10,14},{12,0},{14,2},{1,5},{3,7},... | collective-permute-start | bytes 1179656 | tf_op jit(solution)/shard_map/ppermute | solution.py:76
  355.4 37.3 %collective-permute-start.50 = (f32[32,16,1024]{2,1,0:T(8,128)}, f32[32,16,1024]{2,1,0:T(8,128)}, u32[]{:S(2)}, u32[]{:S(2)}) collective-permute-start(f32[32,16,1024]{2,1,0:T(8,128)} %pad_maximum_fusion), channel_id=1, source_target_pairs={{0,1},{17,16},{2,3},{19,18},{4,5},{21,20},{6,7},{23,22},{8,9},{25,... | collective-permute-start | bytes 6291464 | tf_op jit(solution)/shard_map/ppermute | solution.py:1047
  364.2 13.5 %collective-permute-start.59 = (bf16[128,1024]{1,0:T(8,128)(2,1)S(1)}, bf16[128,1024]{1,0:T(8,128)(2,1)S(1)}, u32[]{:S(2)}, u32[]{:S(2)}) collective-permute-start(bf16[128,1024]{1,0:T(8,128)(2,1)S(1)} %pad_maximum_fusion.7), channel_id=1, source_target_pairs={{0,2},{2,0},{4,6},{6,4},{8,10},{10,8},{12,14},{14,12},{1,3},{3,1},... | collective-permute-start | bytes 786440 | tf_op jit(solution)/shard_map/ppermute | solution.py:73
  367.0 36.3 %collective-permute-start.66 = (bf16[128,5120]{1,0:T(8,128)(2,1)S(1)}, bf16[128,5120]{1,0:T(8,128)(2,1)S(1)}, u32[]{:S(2)}, u32[]{:S(2)}) collective-permute-start(bf16[128,5120]{1,0:T(8,128)(2,1)S(1)} %add_convert_fusion.2), channel_id=1, source_target_pairs={{0,4},{2,6},{4,8},{6,10},{8,12},{10,14},{12,0},{14,2},{1,5},{3,7},... | collective-permute-start | bytes 3932168 | tf_op jit(solution)/shard_map/ppermute | solution.py:76
  367.1 36.2 %collective-permute-start.65 = (bf16[128,5120]{1,0:T(8,128)(2,1)S(1)}, bf16[128,5120]{1,0:T(8,128)(2,1)S(1)}, u32[]{:S(2)}, u32[]{:S(2)}) collective-permute-start(bf16[128,5120]{1,0:T(8,128)(2,1)S(1)} %copy-done.69), channel_id=1, source_target_pairs={{0,2},{2,0},{4,6},{6,4},{8,10},{10,8},{12,14},{14,12},{1,3},{3,1},... | collective-permute-start | bytes 3932168 | tf_op jit(solution)/shard_map/ppermute | solution.py:73
  368.2 72.0 %collective-permute-start.64 = (bf16[128,4096]{1,0:T(8,128)(2,1)}, bf16[128,4096]{1,0:T(8,128)(2,1)}, u32[]{:S(2)}, u32[]{:S(2)}) collective-permute-start(bf16[128,4096]{1,0:T(8,128)(2,1)} %slice.269), channel_id=1, source_target_pairs={{0,0},{1,16},{16,1},{17,17},{2,2},{3,18},{18,3},{19,19},{4,4},{5,2... | collective-permute-start | bytes 3145736 | tf_op jit(solution)/shard_map/ppermute | solution.py:37
  377.8 25.4 %collective-permute-start.60 = (bf16[128,640]{1,0:T(8,128)(2,1)S(1)}, bf16[128,640]{1,0:T(8,128)(2,1)S(1)}, u32[]{:S(2)}, u32[]{:S(2)}) collective-permute-start(bf16[128,640]{1,0:T(8,128)(2,1)S(1)} %pad_maximum_fusion.9), channel_id=1, source_target_pairs={{0,4},{2,6},{4,8},{6,10},{8,12},{10,14},{12,0},{14,2},{1,5},{3,7},... | collective-permute-start | bytes 491528 | tf_op jit(solution)/shard_map/ppermute | solution.py:76
  392.7 13.8 %collective-permute-start.61 = (bf16[128,640]{1,0:T(8,128)(2,1)S(1)}, bf16[128,640]{1,0:T(8,128)(2,1)S(1)}, u32[]{:S(2)}, u32[]{:S(2)}) collective-permute-start(bf16[128,640]{1,0:T(8,128)(2,1)S(1)} %pad_maximum_fusion.9), channel_id=1, source_target_pairs={{4,0},{6,2},{8,4},{10,6},{12,8},{14,10},{0,12},{2,14},{5,1},{7,3},... | collective-permute-start | bytes 491528 | tf_op jit(solution)/shard_map/ppermute | solution.py:79
  403.2 8.9 %collective-permute-start.62 = (bf16[128,640]{1,0:T(8,128)(2,1)S(1)}, bf16[128,640]{1,0:T(8,128)(2,1)S(1)}, u32[]{:S(2)}, u32[]{:S(2)}) collective-permute-start(bf16[128,640]{1,0:T(8,128)(2,1)S(1)} %collective-permute-done.60), channel_id=1, source_target_pairs={{0,4},{2,6},{4,8},{6,10},{8,12},{10,14},{12,0},{14,2},{1,5},{3,7},... | collective-permute-start | bytes 491528 | tf_op jit(solution)/shard_map/ppermute | solution.py:76
  405.0 31.1 %collective-permute-start.68 = (bf16[128,5120]{1,0:T(8,128)(2,1)}, bf16[128,5120]{1,0:T(8,128)(2,1)}, u32[]{:S(2)}, u32[]{:S(2)}) collective-permute-start(bf16[128,5120]{1,0:T(8,128)(2,1)} %add_convert_fusion.1), channel_id=1, source_target_pairs={{0,4},{2,6},{4,8},{6,10},{8,12},{10,14},{12,0},{14,2},{1,5},{3,7},... | collective-permute-start | bytes 3932168 | tf_op jit(solution)/shard_map/ppermute | solution.py:76
  405.0 31.1 %collective-permute-start.67 = (bf16[128,5120]{1,0:T(8,128)(2,1)}, bf16[128,5120]{1,0:T(8,128)(2,1)}, u32[]{:S(2)}, u32[]{:S(2)}) collective-permute-start(bf16[128,5120]{1,0:T(8,128)(2,1)} %get-tuple-element.156), channel_id=1, source_target_pairs={{0,2},{2,0},{4,6},{6,4},{8,10},{10,8},{12,14},{14,12},{1,3},{3,1},... | collective-permute-start | bytes 3932168 | tf_op jit(solution)/shard_map/ppermute | solution.py:73
  412.4 32.3 %collective-permute-start.63 = (f32[3072]{0:T(1024)S(1)}, f32[3072]{0:T(1024)S(1)}, u32[]{:S(2)}, u32[]{:S(2)}) collective-permute-start(f32[3072]{0:T(1024)S(1)} %slice.327), channel_id=1, source_target_pairs={{0,0},{1,16},{16,1},{17,17},{2,2},{3,18},{18,3},{19,19},{4,4},{5,2... | collective-permute-start | bytes 36872 | tf_op jit(solution)/shard_map/ppermute | solution.py:37
  440.2 35.3 %collective-permute-start.70 = (bf16[128,4096]{1,0:T(8,128)(2,1)}, bf16[128,4096]{1,0:T(8,128)(2,1)S(1)}, u32[]{:S(2)}, u32[]{:S(2)}) collective-permute-start(bf16[128,4096]{1,0:T(8,128)(2,1)} %slice.329), channel_id=1, source_target_pairs={{0,4},{1,20},{16,5},{17,21},{2,6},{3,22},{18,7},{19,23},{4,8},{5,2... | collective-permute-start | bytes 3145736 | tf_op jit(solution)/shard_map/ppermute | solution.py:1064
  440.2 35.3 %collective-permute-start.69 = (bf16[128,4096]{1,0:T(8,128)(2,1)}, bf16[128,4096]{1,0:T(8,128)(2,1)S(1)}, u32[]{:S(2)}, u32[]{:S(2)}) collective-permute-start(bf16[128,4096]{1,0:T(8,128)(2,1)} %slice.271), channel_id=1, source_target_pairs={{0,2},{1,18},{16,3},{17,19},{2,0},{3,16},{18,1},{19,17},{4,6},{5,2... | collective-permute-start | bytes 3145736 | tf_op jit(solution)/shard_map/ppermute | solution.py:1064
  441.2 32.4 %collective-permute-start.72 = (bf16[128,1024]{1,0:T(8,128)(2,1)}, bf16[128,1024]{1,0:T(8,128)(2,1)S(1)}, u32[]{:S(2)}, u32[]{:S(2)}) collective-permute-start(bf16[128,1024]{1,0:T(8,128)(2,1)} %slice.330), channel_id=1, source_target_pairs={{0,4},{2,6},{4,8},{6,10},{8,12},{10,14},{12,0},{14,2},{1,5},{3,7},... | collective-permute-start | bytes 786440 | tf_op jit(solution)/shard_map/ppermute | solution.py:76
  441.3 32.4 %collective-permute-start.71 = (bf16[128,1024]{1,0:T(8,128)(2,1)S(1)}, bf16[128,1024]{1,0:T(8,128)(2,1)S(1)}, u32[]{:S(2)}, u32[]{:S(2)}) collective-permute-start(bf16[128,1024]{1,0:T(8,128)(2,1)S(1)} %copy-done.43), channel_id=1, source_target_pairs={{0,2},{2,0},{4,6},{6,4},{8,10},{10,8},{12,14},{14,12},{1,3},{3,1},... | collective-permute-start | bytes 786440 | tf_op jit(solution)/shard_map/ppermute | solution.py:73
  (81 other events, 1110.8 us)

commit v8 on v7

--- a/solution.py
+++ b/solution.py
@@ -207,7 +207,7 @@
 
 def backward_kernel(count, column, places, kept, taken, gates, cells, *refs):
     w_own, w_other = refs[:count], refs[count : 2 * count]
-    dz, stage, w, dh, dc, sems = refs[2 * count :]
+    dz_own, dz_other, dz, stage, w, dh, dc, sems = refs[2 * count :]
     steps, rows, wide_full = gates.shape
     wide_half = wide_full // 2
     unit_half = wide_half // 4
@@ -239,8 +239,6 @@
             return carried
 
         lax.fori_loop(0, 4, turn, 0)
-
-    place_of = (s, 1 - s)
 
     def retreat(k, carried):
         t = steps - 1 - k
@@ -266,9 +264,11 @@
                 grad * squash * o * (1.0 - o),
             )
             for n, part in enumerate(parts):
-                dz[place_of[half], t, :, pl.ds(n * unit_half + inside, chunk)] = part.astype(low)
+                dz[half, :, pl.ds(n * unit_half + inside, chunk)] = part.astype(low)
             dc[:, units] = total * f
-        upper, lower = dz[place_of[0], t], dz[place_of[1], t]
+        dz_own[t] = dz[s]
+        dz_other[t] = dz[1 - s]
+        upper, lower = dz[0], dz[1]
         for at in range(0, 2 * unit_half, chunk):
             units = pl.ds(at, chunk)
             dh[:, units] = jnp.dot(
@@ -285,10 +285,11 @@
     count = len(w_own)
     return pl.pallas_call(
         functools.partial(backward_kernel, count, column),
-        out_shape=jax.ShapeDtypeStruct((2, steps, rows, wide_full // 2), low),
+        out_shape=(jax.ShapeDtypeStruct((steps, rows, wide_full // 2), low),) * 2,
         in_specs=[in_smem] + [in_vmem] * 4 + [in_place] * (2 * count),
-        out_specs=in_vmem,
+        out_specs=[in_vmem] * 2,
         scratch_shapes=[
+            pltpu.VMEM((2, rows, wide_full // 2), low),
             pltpu.VMEM((2 * count, units // count, wide_full // 2), low),
             pltpu.VMEM((wide_full, units), low),
             pltpu.VMEM((rows, units), wide),
@@ -300,7 +301,7 @@
     )(places, kept, taken, gates, cells, *w_own, *w_other)
 
 
-def input_kernel(count, places, inputs, gain, dz, *refs):
+def input_kernel(count, places, inputs, gain, dz, dz_given, *refs):
     in_own, in_other = refs[:count], refs[count : 2 * count]
     grad_inputs, grad_gain, wi, sems = refs[2 * count :]
     s = places[0]
@@ -316,7 +317,7 @@
     wide_half = wi.shape[1] // 2
     own = pl.ds(pl.multiple_of(s * wide_half, wide_half), wide_half)
     other = pl.ds(pl.multiple_of((1 - s) * wide_half, wide_half), wide_half)
-    grad = dot_nt(dz[0], wi[:, own]) + dot_nt(dz[1], wi[:, other])
+    grad = dot_nt(dz[...], wi[:, own]) + dot_nt(dz_given[...], wi[:, other])
     grad_gain[...] = jnp.sum(grad * shape, axis=0, keepdims=True)
     pulled = grad * gain[...]
     grad_inputs[...] = scale * (
@@ -326,7 +327,7 @@
     )
 
 
-def run_input(places, inputs, gain, dz, in_own, in_other):
+def run_input(places, inputs, gain, dz, dz_given, in_own, in_other):
     count = len(in_own)
     rows, width = inputs.shape
     return pl.pallas_call(
@@ -335,15 +336,15 @@
             jax.ShapeDtypeStruct((rows, width), wide),
             jax.ShapeDtypeStruct((1, width), wide),
         ),
-        in_specs=[in_smem] + [in_vmem] * 3 + [in_place] * (2 * count),
+        in_specs=[in_smem] + [in_vmem] * 4 + [in_place] * (2 * count),
         out_specs=[in_vmem] * 2,
         scratch_shapes=[
-            pltpu.VMEM((width, 2 * dz.shape[2]), low),
+            pltpu.VMEM((width, 2 * dz.shape[1]), low),
             pltpu.SemaphoreType.DMA((2 * count,)),
         ],
         compiler_params=pltpu.CompilerParams(vmem_limit_bytes=56 << 20),
         name="input_back",
-    )(places, inputs, gain, dz, *in_own, *in_other)
+    )(places, inputs, gain, dz, dz_given, *in_own, *in_other)
 
 
 def dot_nt(a, b):
@@ -404,6 +405,35 @@
         return value.reshape(frames, group, value.shape[-1])
 
     mem, dec = memory[...], decoded[...]
+
+    def lane(c):
+        return pl.ds(c * lanes, lanes)
+
+    def spread(row, c):
+        return jnp.broadcast_to(vectors[row : row + 1, lane(c)], (group, lanes))
+
+    def energies(queries, keys, vec_row, energy, kept_squash, r):
+        mine = range(r * chunks // 4, (r + 1) * chunks // 4)
+        weights = {c: spread(vec_row, c) for c in mine}
+
+        def one(i, carried):
+            query = {c: queries[i, :, lane(c)] for c in mine}
+            for j in range(frames):
+                total = None if r == 0 else energy[i * frames + j]
+                for c in mine:
+                    squash = jnp.tanh(query[c] + keys[j, :, lane(c)])
+                    kept_squash[i * frames + j, :, lane(c)] = squash
+                    part = squash * weights[c]
+                    total = part if total is None else total + part
+                if r == 3:
+                    total = jnp.broadcast_to(
+                        jnp.sum(total, axis=-1, keepdims=True), (group, lanes)
+                    )
+                energy[i * frames + j] = total
+            return carried
+
+        lax.fori_loop(0, frames, one, 0)
+
     for r in range(4):
         for copy in copies[r]:
             copy.wait()
@@ -415,34 +445,8 @@
         mq[:, :, cols] = split(queries[:, :block] + vectors[0:1, cols])
         sq[:, :, cols] = split(queries[:, block : 2 * block] + vectors[2:3, cols])
         pre[:, cols] = queries[:, 2 * block :] + vectors[4:5, cols]
-
-    def lane(c):
-        return pl.ds(c * lanes, lanes)
-
-    def spread(row, c):
-        return jnp.broadcast_to(vectors[row : row + 1, lane(c)], (group, lanes))
-
-    def energies(queries, keys, vec_row, energy, kept_squash):
-        weights = [spread(vec_row, c) for c in range(chunks)]
-
-        def one(i, carried):
-            query = [queries[i, :, lane(c)] for c in range(chunks)]
-            for j in range(frames):
-                total = None
-                for c in range(chunks):
-                    squash = jnp.tanh(query[c] + keys[j, :, lane(c)])
-                    kept_squash[i * frames + j, :, lane(c)] = squash
-                    part = squash * weights[c]
-                    total = part if total is None else total + part
-                energy[i * frames + j] = jnp.broadcast_to(
-                    jnp.sum(total, axis=-1, keepdims=True), (group, lanes)
-                )
-            return carried
-
-        lax.fori_loop(0, frames, one, 0)
-
-    energies(mq, mk, 1, mono, mono_squash)
-    energies(sq, sk, 3, span, span_squash)
+        energies(mq, mk, 1, mono, mono_squash, r)
+        energies(sq, sk, 3, span, span_squash, r)
 
     length = lengths[...]
     valid = [(length > j) for j in range(frames)]
@@ -699,7 +703,7 @@
     width = a_rec.shape[1]
     jobs = []
     for sources, target in (
-        ((dz.at[0], dz_peer), a_dz),
+        ((dz, dz_peer), a_dz),
         ((before, before_peer), a_rec),
         ((normed, normed_peer), a_in),
         (
@@ -881,7 +885,7 @@
     places, in_own, rec_own, small_own, small_chip = [], [], [], [], []
     small = jnp.concatenate(
         [
-            mono_mem, span_mem, mono_dec, span_dec,
+            tie(mono_mem, in_shard, rec_shard), span_mem, mono_dec, span_dec,
             out_weight[0], out_weight[1],
         ],
         axis=1,
@@ -889,21 +893,15 @@
     if ring.short:
         flow, across, onward = Flow(), ring.across, ring.onward
         both = 2 * wide_half
-        for k in range(ring.outer):
-            places += [ring.back(k) * 2 + ring.x, ring.back(k) * 2 + 1 - ring.x]
-        places = jnp.stack([s, y] + places).astype(jnp.int32)
-        corner = jnp.concatenate([in_shard, rec_shard], axis=1)
-        small = jnp.concatenate(
-            [
-                tie(mono_mem, corner), span_mem, mono_dec, span_dec, out_weight[0], out_weight[1]
-            ],
-            axis=1,
+        corner_in, corner_rec, b_own = flow.step(
+            (corners, in_shard), (corners, rec_shard), (corners, bias_shard)
         )
-        corner, small_far, small_next = corners(corner), across(small), onward(small)
-        flow.landed = (corner, small_far, small_next)
+        small_far, small_next = across(small), onward(small)
+        flow.landed += (small_far, small_next)
+        b_own = b_own.astype(wide)
         small_own = [jnp.concatenate([small, small_far], axis=1)]
         small_chip, small_core = [], []
-        held = jnp.concatenate([corner, small_next], axis=1)
+        held = jnp.concatenate([corner_in, corner_rec, small_next], axis=1)
         near, far, near_core, far_core = [], [], [], []
         for k in range(ring.outer):
             near.append(held)
@@ -911,21 +909,13 @@
             if k < ring.outer - 1:
                 jobs.append((onward, held[:, :both] if k == ring.outer - 2 else held))
             if k == 0:
-                jobs += [(across_chips, vocab_own), (corners, bias_shard)]
-            if k == 1:
-                jobs.append((across_chips, vector_own))
-            also = ready if k == 1 else ()
-            if k == ring.outer - 1:
-                vectors = jnp.concatenate([vector_pair, across_cores(vector_pair)], axis=1)
-                vectors = jnp.pad(vectors, ((0, 3), (0, 0)))
-                also = (vectors, places)
-            results = flow.step(*jobs, also=also)
+                jobs += [(across_chips, vocab_own), (across_chips, vector_own)]
+            results = flow.step(*jobs, also=ready if k == 1 else ())
             far.append(results[0])
             small_chip.append(results[1])
             if k == 0:
-                vocab_chip, b_own = results[3], results[4].astype(wide)
-            if k == 1:
-                vector_pair = jnp.concatenate([vector_own, results[3]], axis=1)
+                vocab_chip, vector_pair = results[3:]
+                vector_pair = jnp.concatenate([vector_own, vector_pair], axis=1)
             if k < ring.outer - 1:
                 small_own.append(jnp.concatenate([held[:, both:], far[k][:, both:]], axis=1))
                 held = results[2]
@@ -933,14 +923,17 @@
             near_core.append(across_cores(a))
             far_core.append(across_cores(b))
         small_core = [across_cores(a) for a in small_own]
-        b_last, vocab_last, chip_last = lax.optimization_barrier(
-            (b_own, vocab_own, vocab_chip, held)
-        )[:3]
+        b_last, vocab_last, chip_last, vector_last = lax.optimization_barrier(
+            (b_own, vocab_own, vocab_chip, vector_pair, held)
+        )[:4]
         b_other = across_cores(b_last)
         vocab = [vocab_own, vocab_chip, across_cores(vocab_last), across_cores(chip_last)]
+        vector_core = across_cores(vector_last)
         in_own = [a for pair in zip(near, far) for a in pair]
         in_other = [a for pair in zip(near_core, far_core) for a in pair]
         rec_own, rec_other, rec_column = in_own, in_other, wide_half
+        for k in range(ring.outer):
+            places += [ring.back(k) * 2 + ring.x, ring.back(k) * 2 + 1 - ring.x]
     else:
         vocab_chip = across_chips(vocab_own)
         small, in_block, rec_block = [
@@ -956,9 +949,10 @@
         b_other = across_cores(b_own)
         vector_pair = across_chips(vector_own)
         vector_pair = jnp.concatenate([vector_own, vector_pair], axis=1)
-        vectors = jnp.concatenate([vector_pair, across_cores(vector_pair)], axis=1)
-        vectors = jnp.pad(vectors, ((0, 3), (0, 0)))
-        places = jnp.stack([s, y] + places).astype(jnp.int32)
+        vector_core = across_cores(vector_pair)
+    vectors = jnp.concatenate([vector_pair, vector_core], axis=1)
+    vectors = jnp.pad(vectors, ((0, 3), (0, 0)))
+    places = jnp.stack([s, y] + places).astype(jnp.int32)
     places = tie(places, vectors, *vocab, *ready, *small_chip[:-1], *small_core)
 
     kept, given, before, gates, cells = run_forward(
@@ -994,18 +988,23 @@
     places_back, pack_out, seen_out = lax.optimization_barrier(
         (places, pack_out, seen_out, grad_taken, before_peer, states_core, seen_core)
     )[:3]
-    dz = run_backward(
+    dz_own, dz_other = run_backward(
         places_back, grad_own.reshape(frames, quarter, width),
         grad_taken.reshape(frames, quarter, width), gates, cells, rec_own, rec_other, rec_column,
     )
     pack_far = across_chips(pack_out)
     seen_far = across_chips(tie(seen_out, pack_out))
 
-    dz = dz.reshape(2, frames * half, wide_half)
-    dz, pack_far, seen_far = lax.optimization_barrier((dz, pack_far, seen_far))
-    dz_peer = across_cores(dz[1])
+    dz_own, dz_other, pack_far, seen_far = lax.optimization_barrier(
+        (
+            dz_own.reshape(frames * half, wide_half), dz_other.reshape(frames * half, wide_half),
+            pack_far, seen_far,
+        )
+    )
+    dz_peer = across_cores(dz_other)
     grad_inputs, grad_gain = run_input(
-        places, inputs_own.reshape(frames * half, width), gain[None], dz, in_own, in_other
+        places, inputs_own.reshape(frames * half, width), gain[None], dz_own, dz_other,
+        in_own, in_other,
     )
     grad_gain = grad_gain.reshape(width)
     z, x = ring.z, ring.x
@@ -1016,7 +1015,7 @@
     else:
         order = [y] + [jnp.int32(k) for k in [*range(8), *range(4)]]
     totals = run_gradients(
-        tie(jnp.stack(order).astype(jnp.int32), grad_gain), before, before_peer, normed_own, normed_other, dz,
+        tie(jnp.stack(order).astype(jnp.int32), grad_gain), before, before_peer, normed_own, normed_other, dz_own,
         dz_peer, states, states_core, seen, seen_core, seen_far, across_cores(seen_far),
         pack_me, pack_core, pack_far,
     )
@@ -1037,7 +1036,7 @@
         [
             vector_pair[:, 0].reshape(-1) + vector_far[: 5 * block],
             bias_pair + vector_far[5 * block :],
-            jnp.sum(dz[0].astype(wide), axis=0) + jnp.sum(dz_peer.astype(wide), axis=0),
+            jnp.sum(dz_own.astype(wide), axis=0) + jnp.sum(dz_peer.astype(wide), axis=0),
             gain_sum,
         ]
     )

time: 483 us -> 480 us (level)
  starting transfers between devices: 78 us -> 66.1 us
  waiting for transfers between devices: 210 us -> 219 us
    ppermute x11, waiting for transfers between devices: 92.1 us -> 102 us  [across(): return lax.ppermute(array, 'dp', self.pair)]
    ppermute x11, starting transfers between devices: 19.3 us -> 11.6 us  [across_chips(): return lax.ppermute(array, 'mp', core_swap)]
    ppermute x4 -> x5, starting transfers between devices: 21.1 us -> 14.4 us  [corners(): return lax.ppermute(array, ('section', 'mp'), corner_swap)]
    unnamed x158 -> x150, local copies, waits for them, and re-layouts: 13.2 us -> 17.3 us
  transfers between devices with their start and end apart: 73 -> 74, of which waited for: 24 -> 21; matrix products, arithmetic and copies ran while one was open for 12% -> 12% of each run, Pallas kernels for 24% -> 24%
where the time goes in v8:
time: 480 us; the launch traced here: 478 us
  waiting for transfers between devices  219 us (46%)
  Pallas kernels  116 us (24%)
  starting transfers between devices  66.1 us (14%)
  local copies, waits for them, and re-layouts  47.1 us (10%)
  other arithmetic  28.6 us (6%)
    ppermute x11, waiting for transfers between devices, across(): return lax.ppermute(array, 'dp', self.pair)  102 us
    ppermute x11, waiting for transfers between devices, onward(): return lax.ppermute(array, 'dp', self.ring)  73.1 us
    pallas_call x1, Pallas kernels, run_attend(): pl.pallas_call(functools.partial(attend_kernel, count), out_shape=(jax.Sh...  31 us
    pallas_call x1, Pallas kernels, run_forward(): pl.pallas_call(functools.partial(forward_kernel, count, column), out_shap...  30.7 us
    pallas_call x1, Pallas kernels, run_backward(): pl.pallas_call(functools.partial(backward_kernel, count, column), out_sha...  29.8 us
    ppermute x11, waiting for transfers between devices, across_chips(): return lax.ppermute(array, 'mp', core_swap)  26.2 us
    unnamed x150, local copies, waits for them, and re-layouts  17.3 us
    pallas_call x1, Pallas kernels, run_gradients(): pl.pallas_call(gradient_kernel, out_shape=tuple([jax.ShapeDtypeStruct((he...  15.2 us
  transfers between devices with their start and end apart: 74, of which 21 were waited for; matrix products, arithmetic and copies ran while one was open for 12% of the time, Pallas kernels for 24%

profile of v8, /device:TPU:0, one launch (start us, length us, event | category | flops | bytes accessed | tf_op | source)
XLA Modules:
  0.0 478.2 jit_solution(11539073319479391284)
XLA Ops:
  0.8 1.3 copy.73
  7.1 3.0 collective-permute-start.2
  10.1 1.5 collective-permute-start.3
  12.2 1.4 collective-permute-start
  13.7 1.4 collective-permute-start.1
  15.1 2.6 collective-permute-start.11
  18.0 1.2 copy.62
  22.7 1.4 collective-permute-start.4
  28.3 2.8 collective-permute-start.6
  31.2 1.6 collective-permute-start.7
  33.4 1.9 collective-permute-start.9
  35.3 1.3 broadcast_select_fusion
  40.2 26.9 %collective-permute-done.8.refs_1_.refs_17_ = bf16[128,5632]{1,0:T(8,128)(2,1)S(1)} collective-permute-done((bf16[128,5632]{1,0:T(8,128)(2,1)S(1)}, bf16[128,5632]{1,0:T(8,128)(2,1)S(1)}, u32[]{:S(2)}, u32[]{:S(2)}) %collective-permute-start.8) | collective-permute-done | bytes 1441824 | tf_op jit(solution)/shard_map/ppermute | solution.py:73
  67.3 1.7 broadcast_in_dim.17.noise
  70.3 1.6 collective-permute-start.12
  72.5 30.8 %collective-permute-done.13.refs_3_.refs_19_ = bf16[128,5632]{1,0:T(8,128)(2,1)S(1)} collective-permute-done((bf16[128,5632]{1,0:T(8,128)(2,1)S(1)}, bf16[128,5632]{1,0:T(8,128)(2,1)S(1)}, u32[]{:S(2)}, u32[]{:S(2)}) %collective-permute-start.13) | collective-permute-done | bytes 1441824 | tf_op jit(solution)/shard_map/ppermute | solution.py:73
  103.5 1.9 collective-permute-done.12.refs_4_.refs_20_
  105.6 1.6 collective-permute-start.23
  107.1 2.3 collective-permute-done.20.refs_8_
  110.0 17.2 %collective-permute-done.19.refs_6_ = bf16[128,3072]{1,0:T(8,128)(2,1)} collective-permute-done((bf16[128,3072]{1,0:T(8,128)(2,1)S(1)}, bf16[128,3072]{1,0:T(8,128)(2,1)}, u32[]{:S(2)}, u32[]{:S(2)}) %collective-permute-start.19) | collective-permute-done | bytes 786464 | tf_op jit(solution)/shard_map/ppermute | solution.py:33
  127.2 11.0 %collective-permute-done.23.refs_5_.refs_21_ = bf16[128,5632]{1,0:T(8,128)(2,1)} collective-permute-done((bf16[128,5632]{1,0:T(8,128)(2,1)S(1)}, bf16[128,5632]{1,0:T(8,128)(2,1)}, u32[]{:S(2)}, u32[]{:S(2)}) %collective-permute-start.23) | collective-permute-done | bytes 1441824 | tf_op jit(solution)/shard_map/ppermute | solution.py:73
  140.8 1.6 collective-permute-start.26
  143.2 1.3 collective-permute-done.25.b_other
  147.0 19.3 %collective-permute-done.26.refs_7_.refs_23_ = bf16[128,4096]{1,0:T(8,128)(2,1)} collective-permute-done((bf16[128,4096]{1,0:T(8,128)(2,1)}, bf16[128,4096]{1,0:T(8,128)(2,1)}, u32[]{:S(2)}, u32[]{:S(2)}) %collective-permute-start.26) | collective-permute-done | bytes 1048608 | tf_op jit(solution)/shard_map/ppermute | solution.py:73
  167.1 1.3 select_maximum_fusion.vectors
  169.4 30.7 %recur_forward.1 = (bf16[16,8,1024]{2,1,0:T(8,128)(2,1)}, bf16[16,8,1024]{2,1,0:T(8,128)(2,1)}, bf16[16,16,1024]{2,1,0:T(8,128)(2,1)}, f32[16,16,4096]{2,1,0:T(8,128)}, f32[16,16,1024]{2,1,0:T(8,128)}) custom-call(s32[10]{0:T(128)} %stack.116.places, bf16[256,1024]{1,0:T(8,128)(2,1)} %bitcast.87, f32[1,2048]{1,0:T(1,128)} %copy-done.53, ...), custom_call_target="tpu_custom_call" | custom-call | tf_op jit(solution)/shard_map/recur_forward/pallas_call | solution.py:184
  200.3 1.9 collective-permute-start.35
  202.3 6.8 %collective-permute-done.35.taken = bf16[128,1024]{1,0:T(8,128)(2,1)S(1)} collective-permute-done((bf16[128,1024]{1,0:T(8,128)(2,1)}, bf16[128,1024]{1,0:T(8,128)(2,1)S(1)}, u32[]{:S(2)}, u32[]{:S(2)}) %collective-permute-start.35) | collective-permute-done | bytes 262176 | tf_op jit(solution)/shard_map/ppermute | solution.py:33
  209.1 1.7 collective-permute-start.43
  214.2 31.0 %attend.1 = (f32[128,1024]{1,0:T(8,128)}, bf16[128,1024]{1,0:T(8,128)(2,1)}, bf16[128,1536]{1,0:T(8,128)(2,1)}, bf16[128,1536]{1,0:T(8,128)(2,1)}, bf16[2,128,15...) custom-call(s32[10]{0:T(128)} %stack.116.places, ...), custom_call_target="tpu_custom_call" | custom-call | tf_op jit(solution)/shard_map/attend/pallas_call | solution.py:654
  246.5 1.2 pad_maximum_fusion.1.states_own
  250.1 1.3 pad_maximum_fusion.5
  251.4 2.2 collective-permute-done.44
  253.9 1.7 collective-permute-start.49
  255.6 29.8 %recur_backward.1 = (bf16[16,16,2048]{2,1,0:T(8,128)(2,1)}, bf16[16,16,2048]{2,1,0:T(8,128)(2,1)}) custom-call(s32[10]{0:T(128)} %stack.116.places, f32[16,8,1024]{2,1,0:T(8,128)} %bitcast.102, bf16[16,8,1024]{2,1,0:T(8,128)(2,1)} %bitcast.39.taken, f32[16,16,4096]{2,1,0:T(8,128)} %get-tuple-element.135.gates, f32[16,16,1024]{2,1,0:T(8,128)} %get-tuple-element.136.cells, ...), custom_call_target="tpu_custom_call" | custom-call | tf_op jit(solution)/shard_map/recur_backward/pallas_call | solution.py:286
  289.4 8.9 %input_back.1 = (f32[256,1024]{1,0:T(8,128)}, f32[1,1024]{1,0:T(1,128)}) custom-call(s32[10]{0:T(128)} %stack.116.places, bf16[256,1024]{1,0:T(8,128)(2,1)} %bitcast.91, f32[1,1024]{1,0:T(1,128)} %bitcast.115, bf16[256,2048]{1,0:T(8,128)(2,1)} %bitcast.84, bf16[256,2048]{1,0:T(8,128)(2,1)} %bitcast.99, bf16[128,5632]{1,0:T(8,128)(2,1)} %copy-done.3, ...), custom_call_target="tpu_custom_call" | custom-call | tf_op jit(solution)/shard_map/input_back/pallas_call | solution.py:333
  298.3 1.8 copy.82
  302.2 15.2 %weight_gradients.1 = (bf16[128,5120]{1,0:T(8,128)(2,1)}, bf16[128,5120]{1,0:T(8,128)(2,1)}, bf16[128,5120]{1,0:T(8,128)(2,1)}, bf16[128,5120]{1,0:T(8,128)(2,1)...) custom-call(s32[13]{0:T(128)} %stack.135.order, ...), custom_call_target="tpu_custom_call" | custom-call | tf_op jit(solution)/shard_map/weight_gradients/pallas_call | solution.py:811
  317.4 1.6 collective-permute-start.58
  319.3 1.4 convert_reduce_fusion
  321.9 3.8 collective-permute-start.56
  325.7 1.9 broadcast_select_fusion.2
  327.6 5.9 %collective-permute-done.57 = bf16[256,768]{1,0:T(8,128)(2,1)} collective-permute-done((bf16[256,768]{1,0:T(8,128)(2,1)}, bf16[256,768]{1,0:T(8,128)(2,1)}, u32[]{:S(2)}, u32[]{:S(2)}) %collective-permute-start.57) | collective-permute-done | bytes 393248 | tf_op jit(solution)/shard_map/ppermute | solution.py:76
  333.4 1.8 add_convert_fusion.3
  335.3 13.6 %collective-permute-done.58 = bf16[128,5120]{1,0:T(8,128)(2,1)} collective-permute-done((bf16[128,5120]{1,0:T(8,128)(2,1)}, bf16[128,5120]{1,0:T(8,128)(2,1)}, u32[]{:S(2)}, u32[]{:S(2)}) %collective-permute-start.58) | collective-permute-done | bytes 1310752 | tf_op jit(solution)/shard_map/ppermute | solution.py:73
  348.9 1.5 pad_maximum_fusion
  352.6 3.5 collective-permute-start.51
  358.1 2.8 collective-permute-done.59
  361.1 1.5 collective-permute-start.60
  362.6 1.7 add_convert_fusion.2
  365.6 9.5 %collective-permute-start.65 = (bf16[128,4096]{1,0:T(8,128)(2,1)}, bf16[128,4096]{1,0:T(8,128)(2,1)}, u32[]{:S(2)}, u32[]{:S(2)}) collective-permute-start(bf16[128,4096]{1,0:T(8,128)(2,1)} %slice.261), channel_id=1, source_target_pairs={{0,0},{1,16},{16,1},{17,17},{2,2},{3,18},{18,3},{19,19},{4,4},{5,2... | collective-permute-start | bytes 3145736 | tf_op jit(solution)/shard_map/ppermute | solution.py:37
  376.1 12.5 %collective-permute-done.51 = f32[32,16,1024]{2,1,0:T(8,128)} collective-permute-done((f32[32,16,1024]{2,1,0:T(8,128)}, f32[32,16,1024]{2,1,0:T(8,128)}, u32[]{:S(2)}, u32[]{:S(2)}) %collective-permute-start.51) | collective-permute-done | bytes 2097184 | tf_op jit(solution)/shard_map/ppermute | solution.py:1046
  388.6 3.9 collective-permute-start.62
  392.5 1.7 select_bitcast_fusion
  394.2 6.4 %collective-permute-done.61 = bf16[128,640]{1,0:T(8,128)(2,1)S(1)} collective-permute-done((bf16[128,640]{1,0:T(8,128)(2,1)S(1)}, bf16[128,640]{1,0:T(8,128)(2,1)S(1)}, u32[]{:S(2)}, u32[]{:S(2)}) %collective-permute-start.61) | collective-permute-done | bytes 163872 | tf_op jit(solution)/shard_map/ppermute | solution.py:76
  400.7 1.7 add_convert_fusion.1
  404.2 5.3 %collective-permute-done.63 = bf16[128,640]{1,0:T(8,128)(2,1)S(1)} collective-permute-done((bf16[128,640]{1,0:T(8,128)(2,1)S(1)}, bf16[128,640]{1,0:T(8,128)(2,1)S(1)}, u32[]{:S(2)}, u32[]{:S(2)}) %collective-permute-start.63) | collective-permute-done | bytes 163872 | tf_op jit(solution)/shard_map/ppermute | solution.py:76
  410.4 23.1 %collective-permute-done.69 = bf16[128,5120]{1,0:T(8,128)(2,1)} collective-permute-done((bf16[128,5120]{1,0:T(8,128)(2,1)}, bf16[128,5120]{1,0:T(8,128)(2,1)}, u32[]{:S(2)}, u32[]{:S(2)}) %collective-permute-start.69) | collective-permute-done | bytes 1310752 | tf_op jit(solution)/shard_map/ppermute | solution.py:76
  433.5 2.3 add_convert_fusion
  437.6 1.3 collective-permute-start.70
  443.4 27.8 %collective-permute-done.73 = bf16[128,1024]{1,0:T(8,128)(2,1)S(1)} collective-permute-done((bf16[128,1024]{1,0:T(8,128)(2,1)}, bf16[128,1024]{1,0:T(8,128)(2,1)S(1)}, u32[]{:S(2)}, u32[]{:S(2)}) %collective-permute-start.73) | collective-permute-done | bytes 262176 | tf_op jit(solution)/shard_map/ppermute | solution.py:76
  473.1 1.6 convert_add_fusion
  474.9 1.7 reshape.205
  476.6 1.7 reshape.206
  (366 shorter events, 60.1 us)
Async XLA Ops:
  7.1 21.2 %collective-permute-start.2 = (bf16[128,1536]{1,0:T(8,128)(2,1)}, bf16[128,1536]{1,0:T(8,128)(2,1)S(1)}, u32[]{:S(2)}, u32[]{:S(2)}) collective-permute-start(bf16[128,1536]{1,0:T(8,128)(2,1)} %get-tuple-element.211), channel_id=1, source_target_pairs={{0,4},{2,6},{4,8},{6,10},{8,12},{10,14},{12,0},{14,2},{1,5},{3,7},... | collective-permute-start | bytes 1179656 | tf_op jit(solution)/shard_map/ppermute | solution.py:76
  10.1 12.6 %collective-permute-start.3 = (bf16[128,1536]{1,0:T(8,128)(2,1)}, bf16[128,1536]{1,0:T(8,128)(2,1)}, u32[]{:S(2)}, u32[]{:S(2)}) collective-permute-start(bf16[128,1536]{1,0:T(8,128)(2,1)} %get-tuple-element.211), channel_id=1, source_target_pairs={{0,2},{2,0},{4,6},{6,4},{8,10},{10,8},{12,14},{14,12},{1,3},{3,1},... | collective-permute-start | bytes 1179656 | tf_op jit(solution)/shard_map/ppermute | solution.py:73
  12.2 13.8 %collective-permute-start = (bf16[128,2048]{1,0:T(8,128)(2,1)S(1)}, bf16[128,2048]{1,0:T(8,128)(2,1)}, u32[]{:S(2)}, u32[]{:S(2)}) collective-permute-start(bf16[128,2048]{1,0:T(8,128)(2,1)S(1)} %bitcast.107), channel_id=1, source_target_pairs={{0,0},{1,16},{16,1},{17,17},{2,2},{3,18},{18,3},{19,19},{4,4},{5,2... | collective-permute-start | bytes 1572872 | tf_op jit(solution)/shard_map/ppermute | solution.py:37
  13.7 13.5 %collective-permute-start.1 = (bf16[128,2048]{1,0:T(8,128)(2,1)S(1)}, bf16[128,2048]{1,0:T(8,128)(2,1)}, u32[]{:S(2)}, u32[]{:S(2)}) collective-permute-start(bf16[128,2048]{1,0:T(8,128)(2,1)S(1)} %bitcast.106), channel_id=1, source_target_pairs={{0,0},{1,16},{16,1},{17,17},{2,2},{3,18},{18,3},{19,19},{4,4},{5,2... | collective-permute-start | bytes 1572872 | tf_op jit(solution)/shard_map/ppermute | solution.py:37
  15.1 7.5 %collective-permute-start.11 = (f32[1024]{0:T(1024)S(1)}, f32[1024]{0:T(1024)S(1)}, u32[]{:S(2)}, u32[]{:S(2)}) collective-permute-start(f32[1024]{0:T(1024)S(1)} %bitcast.120), channel_id=1, source_target_pairs={{0,16},{16,0},{1,17},{17,1},{2,18},{18,2},{3,19},{19,3},{4,20},{20... | collective-permute-start | bytes 12296 | tf_op jit(solution)/shard_map/ppermute | solution.py:29
  22.6 10.7 %collective-permute-start.10 = (bf16[16,32,1024]{2,0,1:T(8,128)(2,1)}, bf16[16,32,1024]{2,0,1:T(8,128)(2,1)S(1)}, u32[]{:S(2)}, u32[]{:S(2)}) collective-permute-start(bf16[16,32,1024]{2,0,1:T(8,128)(2,1)} %bitcast.22), channel_id=1, source_target_pairs={{0,16},{16,0},{1,17},{17,1},{2,18},{18,2},{3,19},{19,3},{4,20},{20... | collective-permute-start | bytes 3145736 | tf_op jit(solution)/shard_map/ppermute | solution.py:29
  22.7 5.6 %collective-permute-start.4 = (bf16[1,2048]{1,0:T(2,128)(2,1)}, bf16[1,2048]{1,0:T(2,128)(2,1)S(1)}, u32[]{:S(2)}, u32[]{:S(2)}) collective-permute-start(bf16[1,2048]{1,0:T(2,128)(2,1)} %bitcast.65), channel_id=1, source_target_pairs={{0,0},{1,16},{16,1},{17,17},{2,2},{3,18},{18,3},{19,19},{4,4},{5,2... | collective-permute-start | bytes 12296 | tf_op jit(solution)/shard_map/ppermute | solution.py:37
  28.3 39.0 %collective-permute-start.6 = (bf16[256,1024]{1,0:T(8,128)(2,1)S(1)}, bf16[256,1024]{1,0:T(8,128)(2,1)S(1)}, u32[]{:S(2)}, u32[]{:S(2)}) collective-permute-start(bf16[256,1024]{1,0:T(8,128)(2,1)S(1)} %pad.24.refs_16_), channel_id=1, source_target_pairs={{0,1},{1,0},{2,3},{3,2},{4,5},{5,4},{6,7},{7,6},{8,9},{9,8},{10,11... | collective-permute-start | bytes 1572872 | tf_op jit(solution)/shard_map/ppermute | solution.py:33
  31.2 36.1 %collective-permute-start.5 = (f32[5,256]{1,0:T(8,128)S(1)}, f32[5,256]{1,0:T(8,128)S(1)}, u32[]{:S(2)}, u32[]{:S(2)}) collective-permute-start(f32[5,256]{1,0:T(8,128)S(1)} %stack.122), channel_id=1, source_target_pairs={{0,1},{1,0},{2,3},{3,2},{4,5},{5,4},{6,7},{7,6},{8,9},{9,8},{10,11... | collective-permute-start | bytes 15368 | tf_op jit(solution)/shard_map/ppermute | solution.py:33
  31.2 36.1 %collective-permute-start.7 = (bf16[128,5632]{1,0:T(8,128)(2,1)S(1)}, bf16[128,5632]{1,0:T(8,128)(2,1)S(1)}, u32[]{:S(2)}, u32[]{:S(2)}) collective-permute-start(bf16[128,5632]{1,0:T(8,128)(2,1)S(1)} %constant_dynamic-update-slice_fusion.4.refs_0_.refs_16_), channel_id=1, source_target_pairs={{0,4},{2,6},{4,8},{6,10},{8,12},{10,14},{12,0},{14,2},{1,5},{3,7},... | collective-permute-start | bytes 4325384 | tf_op jit(solution)/shard_map/ppermute | solution.py:76
  32.8 34.3 %collective-permute-start.8 = (bf16[128,5632]{1,0:T(8,128)(2,1)S(1)}, bf16[128,5632]{1,0:T(8,128)(2,1)S(1)}, u32[]{:S(2)}, u32[]{:S(2)}) collective-permute-start(bf16[128,5632]{1,0:T(8,128)(2,1)S(1)} %constant_dynamic-update-slice_fusion.4.refs_0_.refs_16_), channel_id=1, source_target_pairs={{0,2},{2,0},{4,6},{6,4},{8,10},{10,8},{12,14},{14,12},{1,3},{3,1},... | collective-permute-start | bytes 4325384 | tf_op jit(solution)/shard_map/ppermute | solution.py:73
  33.4 33.9 %collective-permute-start.9 = (bf16[128,3072]{1,0:T(8,128)(2,1)S(1)}, bf16[128,3072]{1,0:T(8,128)(2,1)S(1)}, u32[]{:S(2)}, u32[]{:S(2)}) collective-permute-start(bf16[128,3072]{1,0:T(8,128)(2,1)S(1)} %copy-done.29), channel_id=1, source_target_pairs={{0,1},{1,0},{2,3},{3,2},{4,5},{5,4},{6,7},{7,6},{8,9},{9,8},{10,11... | collective-permute-start | bytes 2359304 | tf_op jit(solution)/shard_map/ppermute | solution.py:33
  69.7 33.6 %collective-permute-start.13 = (bf16[128,5632]{1,0:T(8,128)(2,1)S(1)}, bf16[128,5632]{1,0:T(8,128)(2,1)S(1)}, u32[]{:S(2)}, u32[]{:S(2)}) collective-permute-start(bf16[128,5632]{1,0:T(8,128)(2,1)S(1)} %collective-permute-done.7.refs_2_.refs_18_), channel_id=1, source_target_pairs={{0,2},{2,0},{4,6},{6,4},{8,10},{10,8},{12,14},{14,12},{1,3},{3,1},... | collective-permute-start | bytes 4325384 | tf_op jit(solution)/shard_map/ppermute | solution.py:73
  70.3 35.1 %collective-permute-start.12 = (bf16[128,5632]{1,0:T(8,128)(2,1)S(1)}, bf16[128,5632]{1,0:T(8,128)(2,1)S(1)}, u32[]{:S(2)}, u32[]{:S(2)}) collective-permute-start(bf16[128,5632]{1,0:T(8,128)(2,1)S(1)} %collective-permute-done.7.refs_2_.refs_18_), channel_id=1, source_target_pairs={{0,4},{2,6},{4,8},{6,10},{8,12},{10,14},{12,0},{14,2},{1,5},{3,7},... | collective-permute-start | bytes 4325384 | tf_op jit(solution)/shard_map/ppermute | solution.py:76
  71.9 33.7 %collective-permute-start.14 = (bf16[128,3072]{1,0:T(8,128)(2,1)S(1)}, bf16[128,3072]{1,0:T(8,128)(2,1)}, u32[]{:S(2)}, u32[]{:S(2)}) collective-permute-start(bf16[128,3072]{1,0:T(8,128)(2,1)S(1)} %pad_maximum_fusion.2.refs_1_), channel_id=1, source_target_pairs={{0,1},{1,0},{2,3},{3,2},{4,5},{5,4},{6,7},{7,6},{8,9},{9,8},{10,11... | collective-permute-start | bytes 2359304 | tf_op jit(solution)/shard_map/ppermute | solution.py:33
  72.5 37.0 %collective-permute-start.27 = (bf16[128,5632]{1,0:T(8,128)(2,1)S(1)}, bf16[128,5632]{1,0:T(8,128)(2,1)S(1)}, u32[]{:S(2)}, u32[]{:S(2)}) collective-permute-start(bf16[128,5632]{1,0:T(8,128)(2,1)S(1)} %constant_dynamic-update-slice_fusion.4.refs_0_.refs_16_), channel_id=1, source_target_pairs={{0,16},{16,0},{1,17},{17,1},{2,18},{18,2},{3,19},{19,3},{4,20},{20... | collective-permute-start | bytes 4325384 | tf_op jit(solution)/shard_map/ppermute | solution.py:29
  105.6 32.7 %collective-permute-start.23 = (bf16[128,5632]{1,0:T(8,128)(2,1)S(1)}, bf16[128,5632]{1,0:T(8,128)(2,1)}, u32[]{:S(2)}, u32[]{:S(2)}) collective-permute-start(bf16[128,5632]{1,0:T(8,128)(2,1)S(1)} %collective-permute-done.12.refs_4_.refs_20_), channel_id=1, source_target_pairs={{0,2},{2,0},{4,6},{6,4},{8,10},{10,8},{12,14},{14,12},{1,3},{3,1},... | collective-permute-start | bytes 4325384 | tf_op jit(solution)/shard_map/ppermute | solution.py:73
  107.1 20.1 %collective-permute-start.19 = (bf16[128,3072]{1,0:T(8,128)(2,1)S(1)}, bf16[128,3072]{1,0:T(8,128)(2,1)}, u32[]{:S(2)}, u32[]{:S(2)}) collective-permute-start(bf16[128,3072]{1,0:T(8,128)(2,1)S(1)} %pad_maximum_fusion.3.refs_2_), channel_id=1, source_target_pairs={{0,1},{1,0},{2,3},{3,2},{4,5},{5,4},{6,7},{7,6},{8,9},{9,8},{10,11... | collective-permute-start | bytes 2359304 | tf_op jit(solution)/shard_map/ppermute | solution.py:33
  107.1 32.2 %collective-permute-start.15 = (bf16[128,4096]{1,0:T(8,128)(2,1)S(1)}, bf16[128,4096]{1,0:T(8,128)(2,1)}, u32[]{:S(2)}, u32[]{:S(2)}) collective-permute-start(bf16[128,4096]{1,0:T(8,128)(2,1)S(1)} %slice.296), channel_id=1, source_target_pairs={{0,4},{2,6},{4,8},{6,10},{8,12},{10,14},{12,0},{14,2},{1,5},{3,7},... | collective-permute-start | bytes 3145736 | tf_op jit(solution)/shard_map/ppermute | solution.py:76
  109.4 33.0 %collective-permute-start.28 = (bf16[128,5632]{1,0:T(8,128)(2,1)S(1)}, bf16[128,5632]{1,0:T(8,128)(2,1)S(1)}, u32[]{:S(2)}, u32[]{:S(2)}) collective-permute-start(bf16[128,5632]{1,0:T(8,128)(2,1)S(1)} %collective-permute-done.8.refs_1_.refs_17_), channel_id=1, source_target_pairs={{0,16},{16,0},{1,17},{17,1},{2,18},{18,2},{3,19},{19,3},{4,20},{20... | collective-permute-start | bytes 4325384 | tf_op jit(solution)/shard_map/ppermute | solution.py:29
  109.6 33.0 %collective-permute-start.29 = (bf16[128,5632]{1,0:T(8,128)(2,1)S(1)}, bf16[128,5632]{1,0:T(8,128)(2,1)S(1)}, u32[]{:S(2)}, u32[]{:S(2)}) collective-permute-start(bf16[128,5632]{1,0:T(8,128)(2,1)S(1)} %collective-permute-done.7.refs_2_.refs_18_), channel_id=1, source_target_pairs={{0,16},{16,0},{1,17},{17,1},{2,18},{18,2},{3,19},{19,3},{4,20},{20... | collective-permute-start | bytes 4325384 | tf_op jit(solution)/shard_map/ppermute | solution.py:29
  127.2 17.8 %collective-permute-start.30 = (bf16[128,5632]{1,0:T(8,128)(2,1)S(1)}, bf16[128,5632]{1,0:T(8,128)(2,1)S(1)}, u32[]{:S(2)}, u32[]{:S(2)}) collective-permute-start(bf16[128,5632]{1,0:T(8,128)(2,1)S(1)} %collective-permute-done.13.refs_3_.refs_19_), channel_id=1, source_target_pairs={{0,16},{16,0},{1,17},{17,1},{2,18},{18,2},{3,19},{19,3},{4,20},{20... | collective-permute-start | bytes 4325384 | tf_op jit(solution)/shard_map/ppermute | solution.py:29
  140.8 25.5 %collective-permute-start.26 = (bf16[128,4096]{1,0:T(8,128)(2,1)}, bf16[128,4096]{1,0:T(8,128)(2,1)}, u32[]{:S(2)}, u32[]{:S(2)}) collective-permute-start(bf16[128,4096]{1,0:T(8,128)(2,1)} %collective-permute-done.15.refs_6_.refs_22_), channel_id=1, source_target_pairs={{0,2},{2,0},{4,6},{6,4},{8,10},{10,8},{12,14},{14,12},{1,3},{3,1},... | collective-permute-start | bytes 3145736 | tf_op jit(solution)/shard_map/ppermute | solution.py:73
  144.6 21.7 %collective-permute-start.24 = (bf16[128,3072]{1,0:T(8,128)(2,1)}, bf16[128,3072]{1,0:T(8,128)(2,1)}, u32[]{:S(2)}, u32[]{:S(2)}) collective-permute-start(bf16[128,3072]{1,0:T(8,128)(2,1)} %pad_maximum_fusion.4.refs_3_), channel_id=1, source_target_pairs={{0,16},{16,0},{1,17},{17,1},{2,18},{18,2},{3,19},{19,3},{4,20},{20... | collective-permute-start | bytes 2359304 | tf_op jit(solution)/shard_map/ppermute | solution.py:29
  145.0 23.4 %collective-permute-start.31 = (bf16[128,5632]{1,0:T(8,128)(2,1)S(1)}, bf16[128,5632]{1,0:T(8,128)(2,1)}, u32[]{:S(2)}, u32[]{:S(2)}) collective-permute-start(bf16[128,5632]{1,0:T(8,128)(2,1)S(1)} %collective-permute-done.12.refs_4_.refs_20_), channel_id=1, source_target_pairs={{0,16},{16,0},{1,17},{17,1},{2,18},{18,2},{3,19},{19,3},{4,20},{20... | collective-permute-start | bytes 4325384 | tf_op jit(solution)/shard_map/ppermute | solution.py:29
  146.2 22.8 %collective-permute-start.32 = (bf16[128,5632]{1,0:T(8,128)(2,1)}, bf16[128,5632]{1,0:T(8,128)(2,1)}, u32[]{:S(2)}, u32[]{:S(2)}) collective-permute-start(bf16[128,5632]{1,0:T(8,128)(2,1)} %collective-permute-done.23.refs_5_.refs_21_), channel_id=1, source_target_pairs={{0,16},{16,0},{1,17},{17,1},{2,18},{18,2},{3,19},{19,3},{4,20},{20... | collective-permute-start | bytes 4325384 | tf_op jit(solution)/shard_map/ppermute | solution.py:29
  146.4 22.4 %collective-permute-start.33 = (bf16[128,4096]{1,0:T(8,128)(2,1)}, bf16[128,4096]{1,0:T(8,128)(2,1)}, u32[]{:S(2)}, u32[]{:S(2)}) collective-permute-start(bf16[128,4096]{1,0:T(8,128)(2,1)} %collective-permute-done.15.refs_6_.refs_22_), channel_id=1, source_target_pairs={{0,16},{16,0},{1,17},{17,1},{2,18},{18,2},{3,19},{19,3},{4,20},{20... | collective-permute-start | bytes 3145736 | tf_op jit(solution)/shard_map/ppermute | solution.py:29
  166.3 33.8 %collective-permute-start.36 = (bf16[128,3072]{1,0:T(8,128)(2,1)}, bf16[128,3072]{1,0:T(8,128)(2,1)}, u32[]{:S(2)}, u32[]{:S(2)}) collective-permute-start(bf16[128,3072]{1,0:T(8,128)(2,1)} %pad_maximum_fusion.4.refs_3_), channel_id=1, source_target_pairs={{0,1},{1,0},{2,3},{3,2},{4,5},{5,4},{6,7},{7,6},{8,9},{9,8},{10,11... | collective-permute-start | bytes 2359304 | tf_op jit(solution)/shard_map/ppermute | solution.py:33
  168.4 43.9 %collective-permute-start.37 = (bf16[128,3072]{1,0:T(8,128)(2,1)}, bf16[128,3072]{1,0:T(8,128)(2,1)S(1)}, u32[]{:S(2)}, u32[]{:S(2)}) collective-permute-start(bf16[128,3072]{1,0:T(8,128)(2,1)} %copy-done.30), channel_id=1, source_target_pairs={{0,16},{16,0},{1,17},{17,1},{2,18},{18,2},{3,19},{19,3},{4,20},{20... | collective-permute-start | bytes 2359304 | tf_op jit(solution)/shard_map/ppermute | solution.py:29
  168.8 43.6 %collective-permute-start.38 = (bf16[128,3072]{1,0:T(8,128)(2,1)}, bf16[128,3072]{1,0:T(8,128)(2,1)}, u32[]{:S(2)}, u32[]{:S(2)}) collective-permute-start(bf16[128,3072]{1,0:T(8,128)(2,1)} %collective-permute-done.14.refs_5_), channel_id=1, source_target_pairs={{0,16},{16,0},{1,17},{17,1},{2,18},{18,2},{3,19},{19,3},{4,20},{20... | collective-permute-start | bytes 2359304 | tf_op jit(solution)/shard_map/ppermute | solution.py:29
  169.0 43.4 %collective-permute-start.39 = (bf16[128,3072]{1,0:T(8,128)(2,1)}, bf16[128,3072]{1,0:T(8,128)(2,1)}, u32[]{:S(2)}, u32[]{:S(2)}) collective-permute-start(bf16[128,3072]{1,0:T(8,128)(2,1)} %collective-permute-done.19.refs_6_), channel_id=1, source_target_pairs={{0,16},{16,0},{1,17},{17,1},{2,18},{18,2},{3,19},{19,3},{4,20},{20... | collective-permute-start | bytes 2359304 | tf_op jit(solution)/shard_map/ppermute | solution.py:29
  200.1 12.3 %collective-permute-start.40 = (bf16[128,3072]{1,0:T(8,128)(2,1)}, bf16[128,3072]{1,0:T(8,128)(2,1)S(1)}, u32[]{:S(2)}, u32[]{:S(2)}) collective-permute-start(bf16[128,3072]{1,0:T(8,128)(2,1)} %collective-permute-done.36.refs_7_), channel_id=1, source_target_pairs={{0,16},{16,0},{1,17},{17,1},{2,18},{18,2},{3,19},{19,3},{4,20},{20... | collective-permute-start | bytes 2359304 | tf_op jit(solution)/shard_map/ppermute | solution.py:29
  200.3 8.8 %collective-permute-start.35 = (bf16[128,1024]{1,0:T(8,128)(2,1)}, bf16[128,1024]{1,0:T(8,128)(2,1)S(1)}, u32[]{:S(2)}, u32[]{:S(2)}) collective-permute-start(bf16[128,1024]{1,0:T(8,128)(2,1)} %bitcast.112), channel_id=1, source_target_pairs={{0,1},{1,0},{2,3},{3,2},{4,5},{5,4},{6,7},{7,6},{8,9},{9,8},{10,11... | collective-permute-start | bytes 786440 | tf_op jit(solution)/shard_map/ppermute | solution.py:33
  209.1 36.1 %collective-permute-start.43 = (bf16[128,1024]{1,0:T(8,128)(2,1)}, bf16[128,1024]{1,0:T(8,128)(2,1)S(1)}, u32[]{:S(2)}, u32[]{:S(2)}) collective-permute-start(bf16[128,1024]{1,0:T(8,128)(2,1)} %bitcast.94), channel_id=1, source_target_pairs={{0,1},{1,0},{2,3},{3,2},{4,5},{5,4},{6,7},{7,6},{8,9},{9,8},{10,11... | collective-permute-start | bytes 786440 | tf_op jit(solution)/shard_map/ppermute | solution.py:33
  212.4 39.0 %collective-permute-start.45 = (bf16[256,1024]{1,0:T(8,128)(2,1)}, bf16[256,1024]{1,0:T(8,128)(2,1)}, u32[]{:S(2)}, u32[]{:S(2)}) collective-permute-start(bf16[256,1024]{1,0:T(8,128)(2,1)} %bitcast.108), channel_id=1, source_target_pairs={{0,16},{16,0},{1,17},{17,1},{2,18},{18,2},{3,19},{19,3},{4,20},{20... | collective-permute-start | bytes 1572872 | tf_op jit(solution)/shard_map/ppermute | solution.py:29
  245.3 8.3 %collective-permute-start.44 = (bf16[128,1024]{1,0:T(8,128)(2,1)}, bf16[128,1024]{1,0:T(8,128)(2,1)}, u32[]{:S(2)}, u32[]{:S(2)}) collective-permute-start(bf16[128,1024]{1,0:T(8,128)(2,1)} %get-tuple-element.128), channel_id=1, source_target_pairs={{0,1},{1,0},{2,3},{3,2},{4,5},{5,4},{6,7},{7,6},{8,9},{9,8},{10,11... | collective-permute-start | bytes 786440 | tf_op jit(solution)/shard_map/ppermute | solution.py:33
  247.7 5.9 %collective-permute-start.46 = (bf16[4,128,1024]{2,1,0:T(8,128)(2,1)S(1)}, bf16[4,128,1024]{2,1,0:T(8,128)(2,1)}, u32[]{:S(2)}, u32[]{:S(2)}) collective-permute-start(bf16[4,128,1024]{2,1,0:T(8,128)(2,1)S(1)} %pad_maximum_fusion.1.states_own), channel_id=1, source_target_pairs={{0,16},{16,0},{1,17},{17,1},{2,18},{18,2},{3,19},{19,3},{4,20},{20... | collective-permute-start | bytes 3145736 | tf_op jit(solution)/shard_map/ppermute | solution.py:29
  248.5 5.1 %collective-permute-start.47 = (bf16[2,128,1024]{2,1,0:T(8,128)(2,1)S(1)}, bf16[2,128,1024]{2,1,0:T(8,128)(2,1)}, u32[]{:S(2)}, u32[]{:S(2)}) collective-permute-start(bf16[2,128,1024]{2,1,0:T(8,128)(2,1)S(1)} %copy-done.19), channel_id=1, source_target_pairs={{0,16},{16,0},{1,17},{17,1},{2,18},{18,2},{3,19},{19,3},{4,20},{20... | collective-permute-start | bytes 1572872 | tf_op jit(solution)/shard_map/ppermute | solution.py:29
  253.6 31.9 %collective-permute-start.48 = (bf16[2,128,1536]{2,1,0:T(8,128)(2,1)S(1)}, bf16[2,128,1536]{2,1,0:T(8,128)(2,1)S(1)}, u32[]{:S(2)}, u32[]{:S(2)}) collective-permute-start(bf16[2,128,1536]{2,1,0:T(8,128)(2,1)S(1)} %pad_maximum_fusion.5), channel_id=1, source_target_pairs={{0,1},{1,0},{2,3},{3,2},{4,5},{5,4},{6,7},{7,6},{8,9},{9,8},{10,11... | collective-permute-start | bytes 2359304 | tf_op jit(solution)/shard_map/ppermute | solution.py:33
  253.9 31.6 %collective-permute-start.49 = (bf16[2,128,1152]{2,1,0:T(8,128)(2,1)S(1)}, bf16[2,128,1152]{2,1,0:T(8,128)(2,1)}, u32[]{:S(2)}, u32[]{:S(2)}) collective-permute-start(bf16[2,128,1152]{2,1,0:T(8,128)(2,1)S(1)} %pad_maximum_fusion.6), channel_id=1, source_target_pairs={{0,1},{1,0},{2,3},{3,2},{4,5},{5,4},{6,7},{7,6},{8,9},{9,8},{10,11... | collective-permute-start | bytes 1769480 | tf_op jit(solution)/shard_map/ppermute | solution.py:33
  286.4 14.7 %collective-permute-start.52 = (bf16[256,2048]{1,0:T(8,128)(2,1)}, bf16[256,2048]{1,0:T(8,128)(2,1)S(1)}, u32[]{:S(2)}, u32[]{:S(2)}) collective-permute-start(bf16[256,2048]{1,0:T(8,128)(2,1)} %bitcast.98), channel_id=1, source_target_pairs={{0,16},{16,0},{1,17},{17,1},{2,18},{18,2},{3,19},{19,3},{4,20},{20... | collective-permute-start | bytes 3145736 | tf_op jit(solution)/shard_map/ppermute | solution.py:29
  286.4 14.7 %collective-permute-start.55 = (bf16[2,128,1152]{2,1,0:T(8,128)(2,1)}, bf16[2,128,1152]{2,1,0:T(8,128)(2,1)S(1)}, u32[]{:S(2)}, u32[]{:S(2)}) collective-permute-start(bf16[2,128,1152]{2,1,0:T(8,128)(2,1)} %collective-permute-done.49.far), channel_id=1, source_target_pairs={{0,16},{16,0},{1,17},{17,1},{2,18},{18,2},{3,19},{19,3},{4,20},{20... | collective-permute-start | bytes 1769480 | tf_op jit(solution)/shard_map/ppermute | solution.py:29
  300.2 25.5 %collective-permute-start.50 = (f32[16,16,1024]{2,1,0:T(8,128)S(1)}, f32[16,16,1024]{2,1,0:T(8,128)}, u32[]{:S(2)}, u32[]{:S(2)}) collective-permute-start(f32[16,16,1024]{2,1,0:T(8,128)S(1)} %bitcast.100), channel_id=1, source_target_pairs={{0,16},{16,0},{1,17},{17,1},{2,18},{18,2},{3,19},{19,3},{4,20},{20... | collective-permute-start | bytes 3145736 | tf_op jit(solution)/shard_map/ppermute | solution.py:29
  300.3 19.0 %collective-permute-start.53 = (f32[1024]{0:T(1024)S(1)}, f32[1024]{0:T(1024)S(1)}, u32[]{:S(2)}, u32[]{:S(2)}) collective-permute-start(f32[1024]{0:T(1024)S(1)} %bitcast.122), channel_id=1, source_target_pairs={{0,16},{16,0},{1,17},{17,1},{2,18},{18,2},{3,19},{19,3},{4,20},{20... | collective-permute-start | bytes 12296 | tf_op jit(solution)/shard_map/ppermute | solution.py:29
  317.4 31.4 %collective-permute-start.58 = (bf16[128,5120]{1,0:T(8,128)(2,1)}, bf16[128,5120]{1,0:T(8,128)(2,1)}, u32[]{:S(2)}, u32[]{:S(2)}) collective-permute-start(bf16[128,5120]{1,0:T(8,128)(2,1)} %get-tuple-element.157), channel_id=1, source_target_pairs={{0,2},{2,0},{4,6},{6,4},{8,10},{10,8},{12,14},{14,12},{1,3},{3,1},... | collective-permute-start | bytes 3932168 | tf_op jit(solution)/shard_map/ppermute | solution.py:73
  319.2 14.2 %collective-permute-start.57 = (bf16[256,768]{1,0:T(8,128)(2,1)}, bf16[256,768]{1,0:T(8,128)(2,1)}, u32[]{:S(2)}, u32[]{:S(2)}) collective-permute-start(bf16[256,768]{1,0:T(8,128)(2,1)} %get-tuple-element.156), channel_id=1, source_target_pairs={{0,4},{2,6},{4,8},{6,10},{8,12},{10,14},{12,0},{14,2},{1,5},{3,7},... | collective-permute-start | bytes 1179656 | tf_op jit(solution)/shard_map/ppermute | solution.py:76
  321.3 35.8 %collective-permute-start.54 = (f32[8,768]{1,0:T(8,128)}, f32[8,768]{1,0:T(8,128)S(1)}, u32[]{:S(2)}, u32[]{:S(2)}) collective-permute-start(f32[8,768]{1,0:T(8,128)} %reshape.201), channel_id=1, source_target_pairs={{0,2},{2,0},{4,6},{6,4},{8,10},{10,8},{12,14},{14,12},{1,3},{3,1},... | collective-permute-start | bytes 73736 | tf_op jit(solution)/shard_map/ppermute | solution.py:73
  321.9 36.2 %collective-permute-start.56 = (bf16[256,768]{1,0:T(8,128)(2,1)}, bf16[256,768]{1,0:T(8,128)(2,1)S(1)}, u32[]{:S(2)}, u32[]{:S(2)}) collective-permute-start(bf16[256,768]{1,0:T(8,128)(2,1)} %get-tuple-element.154), channel_id=1, source_target_pairs={{4,0},{6,2},{8,4},{10,6},{12,8},{14,10},{0,12},{2,14},{5,1},{7,3},... | collective-permute-start | bytes 1179656 | tf_op jit(solution)/shard_map/ppermute | solution.py:79
  348.9 12.0 %collective-permute-start.59 = (bf16[256,768]{1,0:T(8,128)(2,1)}, bf16[256,768]{1,0:T(8,128)(2,1)S(1)}, u32[]{:S(2)}, u32[]{:S(2)}) collective-permute-start(bf16[256,768]{1,0:T(8,128)(2,1)} %add_convert_fusion.3), channel_id=1, source_target_pairs={{0,4},{2,6},{4,8},{6,10},{8,12},{10,14},{12,0},{14,2},{1,5},{3,7},... | collective-permute-start | bytes 1179656 | tf_op jit(solution)/shard_map/ppermute | solution.py:76
  352.6 36.0 %collective-permute-start.51 = (f32[32,16,1024]{2,1,0:T(8,128)}, f32[32,16,1024]{2,1,0:T(8,128)}, u32[]{:S(2)}, u32[]{:S(2)}) collective-permute-start(f32[32,16,1024]{2,1,0:T(8,128)} %pad_maximum_fusion), channel_id=1, source_target_pairs={{0,1},{17,16},{2,3},{19,18},{4,5},{21,20},{6,7},{23,22},{8,9},{25,... | collective-permute-start | bytes 6291464 | tf_op jit(solution)/shard_map/ppermute | solution.py:1046
  361.1 13.9 %collective-permute-start.60 = (bf16[128,1024]{1,0:T(8,128)(2,1)S(1)}, bf16[128,1024]{1,0:T(8,128)(2,1)S(1)}, u32[]{:S(2)}, u32[]{:S(2)}) collective-permute-start(bf16[128,1024]{1,0:T(8,128)(2,1)S(1)} %pad_maximum_fusion.7), channel_id=1, source_target_pairs={{0,2},{2,0},{4,6},{6,4},{8,10},{10,8},{12,14},{14,12},{1,3},{3,1},... | collective-permute-start | bytes 786440 | tf_op jit(solution)/shard_map/ppermute | solution.py:73
  364.4 36.3 %collective-permute-start.67 = (bf16[128,5120]{1,0:T(8,128)(2,1)S(1)}, bf16[128,5120]{1,0:T(8,128)(2,1)S(1)}, u32[]{:S(2)}, u32[]{:S(2)}) collective-permute-start(bf16[128,5120]{1,0:T(8,128)(2,1)S(1)} %add_convert_fusion.2), channel_id=1, source_target_pairs={{0,4},{2,6},{4,8},{6,10},{8,12},{10,14},{12,0},{14,2},{1,5},{3,7},... | collective-permute-start | bytes 3932168 | tf_op jit(solution)/shard_map/ppermute | solution.py:76
  364.5 36.2 %collective-permute-start.66 = (bf16[128,5120]{1,0:T(8,128)(2,1)S(1)}, bf16[128,5120]{1,0:T(8,128)(2,1)S(1)}, u32[]{:S(2)}, u32[]{:S(2)}) collective-permute-start(bf16[128,5120]{1,0:T(8,128)(2,1)S(1)} %copy-done.65), channel_id=1, source_target_pairs={{0,2},{2,0},{4,6},{6,4},{8,10},{10,8},{12,14},{14,12},{1,3},{3,1},... | collective-permute-start | bytes 3932168 | tf_op jit(solution)/shard_map/ppermute | solution.py:73
  365.6 72.0 %collective-permute-start.65 = (bf16[128,4096]{1,0:T(8,128)(2,1)}, bf16[128,4096]{1,0:T(8,128)(2,1)}, u32[]{:S(2)}, u32[]{:S(2)}) collective-permute-start(bf16[128,4096]{1,0:T(8,128)(2,1)} %slice.261), channel_id=1, source_target_pairs={{0,0},{1,16},{16,1},{17,17},{2,2},{3,18},{18,3},{19,19},{4,4},{5,2... | collective-permute-start | bytes 3145736 | tf_op jit(solution)/shard_map/ppermute | solution.py:37
  375.2 25.4 %collective-permute-start.61 = (bf16[128,640]{1,0:T(8,128)(2,1)S(1)}, bf16[128,640]{1,0:T(8,128)(2,1)S(1)}, u32[]{:S(2)}, u32[]{:S(2)}) collective-permute-start(bf16[128,640]{1,0:T(8,128)(2,1)S(1)} %pad_maximum_fusion.9), channel_id=1, source_target_pairs={{0,4},{2,6},{4,8},{6,10},{8,12},{10,14},{12,0},{14,2},{1,5},{3,7},... | collective-permute-start | bytes 491528 | tf_op jit(solution)/shard_map/ppermute | solution.py:76
  388.6 15.3 %collective-permute-start.62 = (bf16[128,640]{1,0:T(8,128)(2,1)S(1)}, bf16[128,640]{1,0:T(8,128)(2,1)S(1)}, u32[]{:S(2)}, u32[]{:S(2)}) collective-permute-start(bf16[128,640]{1,0:T(8,128)(2,1)S(1)} %pad_maximum_fusion.9), channel_id=1, source_target_pairs={{4,0},{6,2},{8,4},{10,6},{12,8},{14,10},{0,12},{2,14},{5,1},{7,3},... | collective-permute-start | bytes 491528 | tf_op jit(solution)/shard_map/ppermute | solution.py:79
  400.6 8.9 %collective-permute-start.63 = (bf16[128,640]{1,0:T(8,128)(2,1)S(1)}, bf16[128,640]{1,0:T(8,128)(2,1)S(1)}, u32[]{:S(2)}, u32[]{:S(2)}) collective-permute-start(bf16[128,640]{1,0:T(8,128)(2,1)S(1)} %collective-permute-done.61), channel_id=1, source_target_pairs={{0,4},{2,6},{4,8},{6,10},{8,12},{10,14},{12,0},{14,2},{1,5},{3,7},... | collective-permute-start | bytes 491528 | tf_op jit(solution)/shard_map/ppermute | solution.py:76
  402.4 31.1 %collective-permute-start.69 = (bf16[128,5120]{1,0:T(8,128)(2,1)}, bf16[128,5120]{1,0:T(8,128)(2,1)}, u32[]{:S(2)}, u32[]{:S(2)}) collective-permute-start(bf16[128,5120]{1,0:T(8,128)(2,1)} %add_convert_fusion.1), channel_id=1, source_target_pairs={{0,4},{2,6},{4,8},{6,10},{8,12},{10,14},{12,0},{14,2},{1,5},{3,7},... | collective-permute-start | bytes 3932168 | tf_op jit(solution)/shard_map/ppermute | solution.py:76
  402.4 31.1 %collective-permute-start.68 = (bf16[128,5120]{1,0:T(8,128)(2,1)}, bf16[128,5120]{1,0:T(8,128)(2,1)}, u32[]{:S(2)}, u32[]{:S(2)}) collective-permute-start(bf16[128,5120]{1,0:T(8,128)(2,1)} %get-tuple-element.168), channel_id=1, source_target_pairs={{0,2},{2,0},{4,6},{6,4},{8,10},{10,8},{12,14},{14,12},{1,3},{3,1},... | collective-permute-start | bytes 3932168 | tf_op jit(solution)/shard_map/ppermute | solution.py:73
  409.7 32.5 %collective-permute-start.64 = (f32[3072]{0:T(1024)S(1)}, f32[3072]{0:T(1024)S(1)}, u32[]{:S(2)}, u32[]{:S(2)}) collective-permute-start(f32[3072]{0:T(1024)S(1)} %slice.319), channel_id=1, source_target_pairs={{0,0},{1,16},{16,1},{17,17},{2,2},{3,18},{18,3},{19,19},{4,4},{5,2... | collective-permute-start | bytes 36872 | tf_op jit(solution)/shard_map/ppermute | solution.py:37
  437.6 35.5 %collective-permute-start.71 = (bf16[128,4096]{1,0:T(8,128)(2,1)}, bf16[128,4096]{1,0:T(8,128)(2,1)S(1)}, u32[]{:S(2)}, u32[]{:S(2)}) collective-permute-start(bf16[128,4096]{1,0:T(8,128)(2,1)} %slice.321), channel_id=1, source_target_pairs={{0,4},{1,20},{16,5},{17,21},{2,6},{3,22},{18,7},{19,23},{4,8},{5,2... | collective-permute-start | bytes 3145736 | tf_op jit(solution)/shard_map/ppermute | solution.py:1063
  437.6 35.5 %collective-permute-start.70 = (bf16[128,4096]{1,0:T(8,128)(2,1)}, bf16[128,4096]{1,0:T(8,128)(2,1)S(1)}, u32[]{:S(2)}, u32[]{:S(2)}) collective-permute-start(bf16[128,4096]{1,0:T(8,128)(2,1)} %slice.263), channel_id=1, source_target_pairs={{0,2},{1,18},{16,3},{17,19},{2,0},{3,16},{18,1},{19,17},{4,6},{5,2... | collective-permute-start | bytes 3145736 | tf_op jit(solution)/shard_map/ppermute | solution.py:1063
  438.9 32.3 %collective-permute-start.73 = (bf16[128,1024]{1,0:T(8,128)(2,1)}, bf16[128,1024]{1,0:T(8,128)(2,1)S(1)}, u32[]{:S(2)}, u32[]{:S(2)}) collective-permute-start(bf16[128,1024]{1,0:T(8,128)(2,1)} %slice.322), channel_id=1, source_target_pairs={{0,4},{2,6},{4,8},{6,10},{8,12},{10,14},{12,0},{14,2},{1,5},{3,7},... | collective-permute-start | bytes 786440 | tf_op jit(solution)/shard_map/ppermute | solution.py:76
  439.2 32.0 %collective-permute-start.72 = (bf16[128,1024]{1,0:T(8,128)(2,1)S(1)}, bf16[128,1024]{1,0:T(8,128)(2,1)S(1)}, u32[]{:S(2)}, u32[]{:S(2)}) collective-permute-start(bf16[128,1024]{1,0:T(8,128)(2,1)S(1)} %copy-done.43), channel_id=1, source_target_pairs={{0,2},{2,0},{4,6},{6,4},{8,10},{10,8},{12,14},{14,12},{1,3},{3,1},... | collective-permute-start | bytes 786440 | tf_op jit(solution)/shard_map/ppermute | solution.py:73
  (78 other events, 1228.1 us)

commit v9 on v8

--- a/solution.py
+++ b/solution.py
@@ -953,7 +953,15 @@
     vectors = jnp.concatenate([vector_pair, vector_core], axis=1)
     vectors = jnp.pad(vectors, ((0, 3), (0, 0)))
     places = jnp.stack([s, y] + places).astype(jnp.int32)
-    places = tie(places, vectors, *vocab, *ready, *small_chip[:-1], *small_core)
+    z, x = ring.z, ring.x
+    if ring.short:
+        steps_back = [ring.back(k) for k in range(1, 5)]
+        order = [at * 2 + 1 - x for at in steps_back] + [at * 2 + x for at in steps_back]
+        order = [y] + order + steps_back
+    else:
+        order = [y] + [jnp.int32(k) for k in [*range(8), *range(4)]]
+    order = jnp.stack(order).astype(jnp.int32)
+    places = tie(places, order, vectors, *vocab, *ready, *small_chip[:-1], *small_core)
 
     kept, given, before, gates, cells = run_forward(
         places, normed_own, b_own, b_other, in_own, in_other, rec_own, rec_other, frames,
@@ -1002,45 +1010,39 @@
         )
     )
     dz_peer = across_cores(dz_other)
-    grad_inputs, grad_gain = run_input(
-        places, inputs_own.reshape(frames * half, width), gain[None], dz_own, dz_other,
-        in_own, in_other,
-    )
-    grad_gain = grad_gain.reshape(width)
-    z, x = ring.z, ring.x
-    if ring.short:
-        steps_back = [ring.back(k) for k in range(1, 5)]
-        order = [at * 2 + 1 - x for at in steps_back] + [at * 2 + x for at in steps_back]
-        order = [y] + order + steps_back
-    else:
-        order = [y] + [jnp.int32(k) for k in [*range(8), *range(4)]]
     totals = run_gradients(
-        tie(jnp.stack(order).astype(jnp.int32), grad_gain), before, before_peer, normed_own, normed_other, dz_own,
+        order, before, before_peer, normed_own, normed_other, dz_own,
         dz_peer, states, states_core, seen, seen_core, seen_far, across_cores(seen_far),
         pack_me, pack_core, pack_far,
     )
-    grad_inputs = jnp.swapaxes(grad_inputs.reshape(frames, half, width), 0, 1)
     vector_far = joined(seen_far[:, :, width:].reshape(2 * rows, -1), vector_count).reshape(-1)
 
     sides_at = 5 * block + vocab_pad
-    grad_peer = across_cores(grad_inputs)
-    grad_section = jnp.concatenate(
-        [
-            jnp.where(s == 0, grad_inputs, grad_peer),
-            jnp.where(s == 0, grad_peer, grad_inputs),
-        ],
-        axis=0,
-    )
-    gain_sum = grad_gain + across_cores(grad_gain)
-    flat = jnp.concatenate(
-        [
-            vector_pair[:, 0].reshape(-1) + vector_far[: 5 * block],
-            bias_pair + vector_far[5 * block :],
-            jnp.sum(dz_own.astype(wide), axis=0) + jnp.sum(dz_peer.astype(wide), axis=0),
-            gain_sum,
-        ]
-    )
-    flat = jnp.pad(flat, (0, -flat.shape[0] % (8 * shard_rows)))
+    def input_back(places):
+        grad_inputs, grad_gain = run_input(
+            places, inputs_own.reshape(frames * half, width), gain[None], dz_own, dz_other,
+            in_own, in_other,
+        )
+        grad_gain = grad_gain.reshape(width)
+        grad_inputs = jnp.swapaxes(grad_inputs.reshape(frames, half, width), 0, 1)
+        grad_peer = across_cores(grad_inputs)
+        grad_section = jnp.concatenate(
+            [
+                jnp.where(s == 0, grad_inputs, grad_peer),
+                jnp.where(s == 0, grad_peer, grad_inputs),
+            ],
+            axis=0,
+        )
+        gain_sum = grad_gain + across_cores(grad_gain)
+        flat = jnp.concatenate(
+            [
+                vector_pair[:, 0].reshape(-1) + vector_far[: 5 * block],
+                bias_pair + vector_far[5 * block :],
+                jnp.sum(dz_own.astype(wide), axis=0) + jnp.sum(dz_peer.astype(wide), axis=0),
+                gain_sum,
+            ]
+        )
+        return grad_section, jnp.pad(flat, (0, -flat.shape[0] % (8 * shard_rows)))
 
     def to_other_chip(section):
         return lax.ppermute(section, ("section", "mp"), [(0, 1), (3, 2)])
@@ -1065,6 +1067,7 @@
         arrived, out_two, out_before = flow.step(
             (across, theirs[0]), (onward, outputs[1]), (ring.astern, outputs[0])
         )
+        grad_section, flat = input_back(tie(places, out_two))
         out_one = onward(
             tie((outputs[2].astype(wide) + out_two.astype(wide)).astype(low), arrived)
         )
@@ -1080,22 +1083,23 @@
         message = jnp.concatenate(
             [cut(out, 1 - x, r)[:, :width_out].astype(low), vocab_rows[:r], vocab_rows[r:]], axis=1
         )
-        out_far = across(message)
         kept_rows = corners(tie(mine[3][:, :both], out_one))
+        value = total(2, arrived, passed).astype(low)
+        passed, arrived, out_far = flow.step(
+            (onward, value), (across, theirs[2]), (across, message), also=(grad_far,)
+        )
         output_grad = cut(out, x, r)[:, :width_out] + out_far[:, :width_out].astype(wide)
         shard = jnp.concatenate([out[:r, width_out:], out[r:, width_out:]], axis=1)
         shard = (shard + out_far[:, width_out:].astype(wide)).astype(low)
         shard = jnp.concatenate([shard, halves(flat, r)], axis=1)
-        value = total(2, arrived, passed).astype(low)
-        passed, arrived = flow.step((onward, value), (across, theirs[2]), also=(grad_far,))
         next_one, next_three = onward(shard), ring.astern(shard)
         value = total(3, arrived, passed).astype(low)
-        passed, arrived, energy_passed, energy_arrived = flow.step(
+        passed, arrived, energy_passed, energy_arrived, next_two = flow.step(
             (cornered(ring.ring), value[:, :both]), (cornered(ring.pair), theirs[3][:, :both]),
-            (onward, value[:, both:]), (across, theirs[3][:, both:]),
-            also=(kept_rows, next_one, next_three),
-        )
-        shards = {0: shard, 1: next_one, 3: next_three, 2: onward(next_one)}
+            (onward, value[:, both:]), (across, theirs[3][:, both:]), (onward, next_one),
+            also=(kept_rows,),
+        )
+        shards = {0: shard, 1: next_one, 3: next_three, 2: next_two}
         flat = sum(joined(a[:, 2 * block :], flat_width).reshape(-1) for a in shards.values())
         sides = corners(flat[sides_at : sides_at + wide_half + width])
         moved = kept_rows.astype(wide) + arrived.astype(wide) + passed.astype(wide)
@@ -1106,6 +1110,7 @@
             held = jnp.concatenate([held[:, :block], held[:, block : 2 * block]], axis=0)
             vocab_grad = lax.dynamic_update_slice(vocab_grad, held, (ring.back(k) * 2 * r, 0))
     else:
+        grad_section, flat = input_back(places)
         grad_far = to_other_chip(grad_section)
 
         def scatter(parts):

time: 480 us -> 467 us (0.973)
  waiting for transfers between devices: 219 us -> 208 us
  other arithmetic: 28.6 us -> 21.7 us
    ppermute x11, waiting for transfers between devices: 73.1 us -> 48.2 us  [onward(): return lax.ppermute(array, 'dp', self.ring)]
    ppermute x2, waiting for transfers between devices: 0.01 us -> 19.9 us  [cornered(): return lambda array: lax.ppermute(array, ('section', 'dp', 'mp'), pairs)]
    ppermute x1, waiting for transfers between devices: 12.5 us -> 0.58 us  [to_other_chip(): return lax.ppermute(section, ('section', 'mp'), [(0, 1), (3, 2)])]
    ppermute x11, starting transfers between devices: 6.68 us -> 15.6 us  [onward(): return lax.ppermute(array, 'dp', self.ring)]
    ppermute x5, starting transfers between devices: 14.4 us -> 9.09 us  [corners(): return lax.ppermute(array, ('section', 'mp'), corner_swap)]
    unnamed x150 -> x154, local copies, waits for them, and re-layouts: 17.3 us -> 14.8 us
  transfers between devices with their start and end apart: 74 -> 74, of which waited for: 21 -> 27; matrix products, arithmetic and copies ran while one was open for 12% -> 11% of each run, Pallas kernels for 24% -> 22%
where the time goes in v9:
time: 467 us; the launch traced here: 464 us
  waiting for transfers between devices  208 us (45%)
  Pallas kernels  116 us (25%)
  starting transfers between devices  67.2 us (14%)
  local copies, waits for them, and re-layouts  49 us (10%)
  other arithmetic  21.7 us (5%)
    ppermute x11, waiting for transfers between devices, across(): return lax.ppermute(array, 'dp', self.pair)  101 us
    ppermute x11, waiting for transfers between devices, onward(): return lax.ppermute(array, 'dp', self.ring)  48.2 us
    pallas_call x1, Pallas kernels, run_attend(): pl.pallas_call(functools.partial(attend_kernel, count), out_shape=(jax.Sh...  31 us
    pallas_call x1, Pallas kernels, run_forward(): pl.pallas_call(functools.partial(forward_kernel, count, column), out_shap...  30.8 us
    ppermute x11, waiting for transfers between devices, across_chips(): return lax.ppermute(array, 'mp', core_swap)  30.5 us
    pallas_call x1, Pallas kernels, run_backward(): pl.pallas_call(functools.partial(backward_kernel, count, column), out_sha...  29.8 us
    ppermute x2, waiting for transfers between devices, cornered(): return lambda array: lax.ppermute(array, ('section', 'dp', 'mp'), pairs)  19.9 us
    ppermute x11, starting transfers between devices, onward(): return lax.ppermute(array, 'dp', self.ring)  15.6 us
  transfers between devices with their start and end apart: 74, of which 27 were waited for; matrix products, arithmetic and copies ran while one was open for 11% of the time, Pallas kernels for 22%

profile of v9, /device:TPU:0, one launch (start us, length us, event | category | flops | bytes accessed | tf_op | source)
XLA Modules:
  0.0 464.0 jit_solution(5548907950689468043)
XLA Ops:
  0.8 2.1 copy.73
  2.8 2.0 copy.74
  8.7 2.9 collective-permute-start.3
  11.6 1.6 collective-permute-start.2
  13.7 5.4 %collective-permute-start = (bf16[128,2048]{1,0:T(8,128)(2,1)}, bf16[128,2048]{1,0:T(8,128)(2,1)}, u32[]{:S(2)}, u32[]{:S(2)}) collective-permute-start(bf16[128,2048]{1,0:T(8,128)(2,1)} %bitcast.60), channel_id=1, source_target_pairs={{0,0},{1,16},{16,1},{17,17},{2,2},{3,18},{18,3},{19,19},{4,4},{5,2... | collective-permute-start | bytes 1572872 | tf_op jit(solution)/shard_map/ppermute | solution.py:37
  20.6 1.3 pad.25
  23.2 1.7 collective-permute-start.1
  26.7 1.4 constant_dynamic-update-slice_fusion.6
  28.8 1.6 collective-permute-start.7
  30.4 4.2 collective-permute-start.9
  34.5 2.0 collective-permute-start.5
  40.2 19.0 %collective-permute-done.8.refs_1_.refs_17_ = bf16[128,5632]{1,0:T(8,128)(2,1)S(1)} collective-permute-done((bf16[128,5632]{1,0:T(8,128)(2,1)S(1)}, bf16[128,5632]{1,0:T(8,128)(2,1)S(1)}, u32[]{:S(2)}, u32[]{:S(2)}) %collective-permute-start.8) | collective-permute-done | bytes 1441824 | tf_op jit(solution)/shard_map/ppermute | solution.py:73
  59.3 4.3 collective-permute-done.5
  63.7 1.6 broadcast_in_dim.17.noise
  66.0 1.5 collective-permute-start.13
  67.5 1.6 collective-permute-start.12
  69.1 1.7 collective-permute-start.14
  70.8 29.7 %collective-permute-done.13.refs_3_.refs_19_ = bf16[128,5632]{1,0:T(8,128)(2,1)S(1)} collective-permute-done((bf16[128,5632]{1,0:T(8,128)(2,1)S(1)}, bf16[128,5632]{1,0:T(8,128)(2,1)S(1)}, u32[]{:S(2)}, u32[]{:S(2)}) %collective-permute-start.13) | collective-permute-done | bytes 1441824 | tf_op jit(solution)/shard_map/ppermute | solution.py:73
  100.6 2.9 collective-permute-done.12.refs_4_.refs_20_
  104.3 2.3 collective-permute-done.20.refs_8_
  107.2 17.0 %collective-permute-done.19.refs_6_ = bf16[128,3072]{1,0:T(8,128)(2,1)S(1)} collective-permute-done((bf16[128,3072]{1,0:T(8,128)(2,1)S(1)}, bf16[128,3072]{1,0:T(8,128)(2,1)S(1)}, u32[]{:S(2)}, u32[]{:S(2)}) %collective-permute-start.19) | collective-permute-done | bytes 786464 | tf_op jit(solution)/shard_map/ppermute | solution.py:33
  124.2 12.9 %collective-permute-done.23.refs_5_.refs_21_ = bf16[128,5632]{1,0:T(8,128)(2,1)} collective-permute-done((bf16[128,5632]{1,0:T(8,128)(2,1)S(1)}, bf16[128,5632]{1,0:T(8,128)(2,1)}, u32[]{:S(2)}, u32[]{:S(2)}) %collective-permute-start.23) | collective-permute-done | bytes 1441824 | tf_op jit(solution)/shard_map/ppermute | solution.py:73
  141.1 1.3 collective-permute-done.25.b_other
  144.8 20.3 %collective-permute-done.26.refs_7_.refs_23_ = bf16[128,4096]{1,0:T(8,128)(2,1)} collective-permute-done((bf16[128,4096]{1,0:T(8,128)(2,1)}, bf16[128,4096]{1,0:T(8,128)(2,1)}, u32[]{:S(2)}, u32[]{:S(2)}) %collective-permute-start.26) | collective-permute-done | bytes 1048608 | tf_op jit(solution)/shard_map/ppermute | solution.py:73
  168.2 30.8 %recur_forward.1 = (bf16[16,8,1024]{2,1,0:T(8,128)(2,1)}, bf16[16,8,1024]{2,1,0:T(8,128)(2,1)}, bf16[16,16,1024]{2,1,0:T(8,128)(2,1)}, f32[16,16,4096]{2,1,0:T(8,128)}, f32[16,16,1024]{2,1,0:T(8,128)}) custom-call(s32[10]{0:T(128)} %stack.116.places, bf16[256,1024]{1,0:T(8,128)(2,1)} %bitcast.87, f32[1,2048]{1,0:T(1,128)} %copy-done.59, ...), custom_call_target="tpu_custom_call" | custom-call | tf_op jit(solution)/shard_map/recur_forward/pallas_call | solution.py:184
  199.2 1.8 collective-permute-start.35
  201.0 7.0 %collective-permute-done.35.taken = bf16[128,1024]{1,0:T(8,128)(2,1)S(1)} collective-permute-done((bf16[128,1024]{1,0:T(8,128)(2,1)}, bf16[128,1024]{1,0:T(8,128)(2,1)S(1)}, u32[]{:S(2)}, u32[]{:S(2)}) %collective-permute-start.35) | collective-permute-done | bytes 262176 | tf_op jit(solution)/shard_map/ppermute | solution.py:33
  208.0 1.6 collective-permute-start.44
  212.1 31.0 %attend.1 = (f32[128,1024]{1,0:T(8,128)}, bf16[128,1024]{1,0:T(8,128)(2,1)}, bf16[128,1536]{1,0:T(8,128)(2,1)}, bf16[128,1536]{1,0:T(8,128)(2,1)}, bf16[2,128,15...) custom-call(s32[10]{0:T(128)} %stack.116.places, ...), custom_call_target="tpu_custom_call" | custom-call | tf_op jit(solution)/shard_map/attend/pallas_call | solution.py:654
  243.9 1.2 pad_maximum_fusion.1.states_own
  248.6 1.3 collective-permute-done.42.pack_core
  250.0 2.2 collective-permute-done.45
  252.7 1.6 collective-permute-start.49
  254.3 29.8 %recur_backward.1 = (bf16[16,16,2048]{2,1,0:T(8,128)(2,1)}, bf16[16,16,2048]{2,1,0:T(8,128)(2,1)}) custom-call(s32[10]{0:T(128)} %stack.116.places, f32[16,8,1024]{2,1,0:T(8,128)} %bitcast.102, bf16[16,8,1024]{2,1,0:T(8,128)(2,1)} %bitcast.43.taken, f32[16,16,4096]{2,1,0:T(8,128)} %get-tuple-element.137.gates, f32[16,16,1024]{2,1,0:T(8,128)} %get-tuple-element.138.cells, ...), custom_call_target="tpu_custom_call" | custom-call | tf_op jit(solution)/shard_map/recur_backward/pallas_call | solution.py:286
  286.2 1.7 collective-permute-done.51.far_core
  288.9 15.2 %weight_gradients.1 = (bf16[128,5120]{1,0:T(8,128)(2,1)}, bf16[128,5120]{1,0:T(8,128)(2,1)}, bf16[128,5120]{1,0:T(8,128)(2,1)}, bf16[128,5120]{1,0:T(8,128)(2,1)...) custom-call(s32[13]{0:T(128)} %stack.123.order, ...), custom_call_target="tpu_custom_call" | custom-call | tf_op jit(solution)/shard_map/weight_gradients/pallas_call | solution.py:811
  305.2 2.3 slice.258
  307.5 1.7 slice.260
  309.2 3.7 collective-permute-start.57
  313.0 5.5 %collective-permute-done.52 = bf16[256,768]{1,0:T(8,128)(2,1)S(1)} collective-permute-done((bf16[256,768]{1,0:T(8,128)(2,1)}, bf16[256,768]{1,0:T(8,128)(2,1)S(1)}, u32[]{:S(2)}, u32[]{:S(2)}) %collective-permute-start.52) | collective-permute-done | bytes 393248 | tf_op jit(solution)/shard_map/ppermute | solution.py:76
  319.2 9.1 %input_back.1 = (f32[256,1024]{1,0:T(8,128)}, f32[1,1024]{1,0:T(1,128)}) custom-call(s32[10]{0:T(128)} %stack.116.places, bf16[256,1024]{1,0:T(8,128)(2,1)} %bitcast.91, f32[1,1024]{1,0:T(1,128)} %bitcast.114, bf16[256,2048]{1,0:T(8,128)(2,1)} %bitcast.85, bf16[256,2048]{1,0:T(8,128)(2,1)} %bitcast.99, bf16[128,5632]{1,0:T(8,128)(2,1)} %copy-done.3, ...), custom_call_target="tpu_custom_call" | custom-call | tf_op jit(solution)/shard_map/input_back/pallas_call | solution.py:333
  329.6 1.6 copy.82
  332.4 2.0 add_convert_fusion.3
  334.3 1.7 collective-permute-done.56
  336.9 2.1 add_convert_fusion.2
  341.1 2.8 collective-permute-start.54
  344.0 7.0 %collective-permute-done.59 = bf16[256,768]{1,0:T(8,128)(2,1)S(1)} collective-permute-done((bf16[256,768]{1,0:T(8,128)(2,1)}, bf16[256,768]{1,0:T(8,128)(2,1)S(1)}, u32[]{:S(2)}, u32[]{:S(2)}) %collective-permute-start.59) | collective-permute-done | bytes 393248 | tf_op jit(solution)/shard_map/ppermute | solution.py:76
  351.7 1.2 fusion.20
  353.1 16.1 %collective-permute-done.60 = bf16[128,5120]{1,0:T(8,128)(2,1)S(1)} collective-permute-done((bf16[128,5120]{1,0:T(8,128)(2,1)S(1)}, bf16[128,5120]{1,0:T(8,128)(2,1)S(1)}, u32[]{:S(2)}, u32[]{:S(2)}) %collective-permute-start.60) | collective-permute-done | bytes 1310752 | tf_op jit(solution)/shard_map/ppermute | solution.py:73
  369.2 8.2 %collective-permute-done.61 = bf16[128,5120]{1,0:T(8,128)(2,1)S(1)} collective-permute-done((bf16[128,5120]{1,0:T(8,128)(2,1)S(1)}, bf16[128,5120]{1,0:T(8,128)(2,1)S(1)}, u32[]{:S(2)}, u32[]{:S(2)}) %collective-permute-start.61) | collective-permute-done | bytes 1310752 | tf_op jit(solution)/shard_map/ppermute | solution.py:76
  378.6 1.3 collective-permute-start.62
  380.6 4.0 collective-permute-start.66
  384.7 1.7 select_bitcast_fusion
  386.4 1.4 collective-permute-done.62
  387.9 4.1 collective-permute-start.63
  392.9 24.5 %collective-permute-done.63 = bf16[128,640]{1,0:T(8,128)(2,1)} collective-permute-done((bf16[128,640]{1,0:T(8,128)(2,1)S(1)}, bf16[128,640]{1,0:T(8,128)(2,1)}, u32[]{:S(2)}, u32[]{:S(2)}) %collective-permute-start.63) | collective-permute-done | bytes 163872 | tf_op jit(solution)/shard_map/ppermute | solution.py:76
  422.2 1.2 collective-permute-start.68
  424.8 1.6 collective-permute-start.72
  427.6 3.0 collective-permute-start.71
  438.7 16.4 %collective-permute-done.70 = bf16[128,4096]{1,0:T(8,128)(2,1)} collective-permute-done((bf16[128,4096]{1,0:T(8,128)(2,1)}, bf16[128,4096]{1,0:T(8,128)(2,1)}, u32[]{:S(2)}, u32[]{:S(2)}) %collective-permute-start.70) | collective-permute-done | bytes 1048608 | tf_op jit(solution)/shard_map/ppermute | solution.py:1065
  455.0 3.5 collective-permute-done.71
  458.5 2.0 convert_add_fusion
  460.6 1.7 reshape.205
  462.3 1.7 reshape.206
  (370 shorter events, 61.6 us)
Async XLA Ops:
  8.7 16.2 %collective-permute-start.3 = (bf16[128,1536]{1,0:T(8,128)(2,1)}, bf16[128,1536]{1,0:T(8,128)(2,1)}, u32[]{:S(2)}, u32[]{:S(2)}) collective-permute-start(bf16[128,1536]{1,0:T(8,128)(2,1)} %get-tuple-element.215), channel_id=1, source_target_pairs={{0,2},{2,0},{4,6},{6,4},{8,10},{10,8},{12,14},{14,12},{1,3},{3,1},... | collective-permute-start | bytes 1179656 | tf_op jit(solution)/shard_map/ppermute | solution.py:73
  11.6 16.5 %collective-permute-start.2 = (bf16[128,1536]{1,0:T(8,128)(2,1)}, bf16[128,1536]{1,0:T(8,128)(2,1)S(1)}, u32[]{:S(2)}, u32[]{:S(2)}) collective-permute-start(bf16[128,1536]{1,0:T(8,128)(2,1)} %get-tuple-element.215), channel_id=1, source_target_pairs={{0,4},{2,6},{4,8},{6,10},{8,12},{10,14},{12,0},{14,2},{1,5},{3,7},... | collective-permute-start | bytes 1179656 | tf_op jit(solution)/shard_map/ppermute | solution.py:76
  13.2 21.3 %collective-permute-start.10 = (bf16[16,32,1024]{2,0,1:T(8,128)(2,1)S(1)}, bf16[16,32,1024]{2,0,1:T(8,128)(2,1)}, u32[]{:S(2)}, u32[]{:S(2)}) collective-permute-start(bf16[16,32,1024]{2,0,1:T(8,128)(2,1)S(1)} %bitcast.100), channel_id=1, source_target_pairs={{0,16},{16,0},{1,17},{17,1},{2,18},{18,2},{3,19},{19,3},{4,20},{20... | collective-permute-start | bytes 3145736 | tf_op jit(solution)/shard_map/ppermute | solution.py:29
  13.2 9.4 %collective-permute-start.11 = (f32[1024]{0:T(1024)S(1)}, f32[1024]{0:T(1024)S(1)}, u32[]{:S(2)}, u32[]{:S(2)}) collective-permute-start(f32[1024]{0:T(1024)S(1)} %bitcast.120), channel_id=1, source_target_pairs={{0,16},{16,0},{1,17},{17,1},{2,18},{18,2},{3,19},{19,3},{4,20},{20... | collective-permute-start | bytes 12296 | tf_op jit(solution)/shard_map/ppermute | solution.py:29
  13.7 12.9 %collective-permute-start = (bf16[128,2048]{1,0:T(8,128)(2,1)}, bf16[128,2048]{1,0:T(8,128)(2,1)}, u32[]{:S(2)}, u32[]{:S(2)}) collective-permute-start(bf16[128,2048]{1,0:T(8,128)(2,1)} %bitcast.60), channel_id=1, source_target_pairs={{0,0},{1,16},{16,1},{17,17},{2,2},{3,18},{18,3},{19,19},{4,4},{5,2... | collective-permute-start | bytes 1572872 | tf_op jit(solution)/shard_map/ppermute | solution.py:37
  23.2 4.8 %collective-permute-start.1 = (bf16[128,2048]{1,0:T(8,128)(2,1)}, bf16[128,2048]{1,0:T(8,128)(2,1)S(1)}, u32[]{:S(2)}, u32[]{:S(2)}) collective-permute-start(bf16[128,2048]{1,0:T(8,128)(2,1)} %bitcast.106), channel_id=1, source_target_pairs={{0,0},{1,16},{16,1},{17,17},{2,2},{3,18},{18,3},{19,19},{4,4},{5,2... | collective-permute-start | bytes 1572872 | tf_op jit(solution)/shard_map/ppermute | solution.py:37
  25.0 3.2 collective-permute-start.4
  28.2 31.0 %collective-permute-start.8 = (bf16[128,5632]{1,0:T(8,128)(2,1)S(1)}, bf16[128,5632]{1,0:T(8,128)(2,1)S(1)}, u32[]{:S(2)}, u32[]{:S(2)}) collective-permute-start(bf16[128,5632]{1,0:T(8,128)(2,1)S(1)} %constant_dynamic-update-slice_fusion.4.refs_0_.refs_16_), channel_id=1, source_target_pairs={{0,2},{2,0},{4,6},{6,4},{8,10},{10,8},{12,14},{14,12},{1,3},{3,1},... | collective-permute-start | bytes 4325384 | tf_op jit(solution)/shard_map/ppermute | solution.py:73
  28.8 34.9 %collective-permute-start.7 = (bf16[128,5632]{1,0:T(8,128)(2,1)S(1)}, bf16[128,5632]{1,0:T(8,128)(2,1)S(1)}, u32[]{:S(2)}, u32[]{:S(2)}) collective-permute-start(bf16[128,5632]{1,0:T(8,128)(2,1)S(1)} %constant_dynamic-update-slice_fusion.4.refs_0_.refs_16_), channel_id=1, source_target_pairs={{0,4},{2,6},{4,8},{6,10},{8,12},{10,14},{12,0},{14,2},{1,5},{3,7},... | collective-permute-start | bytes 4325384 | tf_op jit(solution)/shard_map/ppermute | solution.py:76
  30.4 33.3 %collective-permute-start.9 = (bf16[128,3072]{1,0:T(8,128)(2,1)S(1)}, bf16[128,3072]{1,0:T(8,128)(2,1)S(1)}, u32[]{:S(2)}, u32[]{:S(2)}) collective-permute-start(bf16[128,3072]{1,0:T(8,128)(2,1)S(1)} %constant_dynamic-update-slice_fusion.7.refs_0_), channel_id=1, source_target_pairs={{0,1},{1,0},{2,3},{3,2},{4,5},{5,4},{6,7},{7,6},{8,9},{9,8},{10,11... | collective-permute-start | bytes 2359304 | tf_op jit(solution)/shard_map/ppermute | solution.py:33
  34.5 29.1 %collective-permute-start.6 = (bf16[256,1024]{1,0:T(8,128)(2,1)S(1)}, bf16[256,1024]{1,0:T(8,128)(2,1)S(1)}, u32[]{:S(2)}, u32[]{:S(2)}) collective-permute-start(bf16[256,1024]{1,0:T(8,128)(2,1)S(1)} %pad.24.refs_16_), channel_id=1, source_target_pairs={{0,1},{1,0},{2,3},{3,2},{4,5},{5,4},{6,7},{7,6},{8,9},{9,8},{10,11... | collective-permute-start | bytes 1572872 | tf_op jit(solution)/shard_map/ppermute | solution.py:33
  34.5 29.1 %collective-permute-start.5 = (f32[5,256]{1,0:T(8,128)S(1)}, f32[5,256]{1,0:T(8,128)S(1)}, u32[]{:S(2)}, u32[]{:S(2)}) collective-permute-start(f32[5,256]{1,0:T(8,128)S(1)} %stack.129), channel_id=1, source_target_pairs={{0,1},{1,0},{2,3},{3,2},{4,5},{5,4},{6,7},{7,6},{8,9},{9,8},{10,11... | collective-permute-start | bytes 15368 | tf_op jit(solution)/shard_map/ppermute | solution.py:33
  66.0 34.5 %collective-permute-start.13 = (bf16[128,5632]{1,0:T(8,128)(2,1)S(1)}, bf16[128,5632]{1,0:T(8,128)(2,1)S(1)}, u32[]{:S(2)}, u32[]{:S(2)}) collective-permute-start(bf16[128,5632]{1,0:T(8,128)(2,1)S(1)} %collective-permute-done.7.refs_2_.refs_18_), channel_id=1, source_target_pairs={{0,2},{2,0},{4,6},{6,4},{8,10},{10,8},{12,14},{14,12},{1,3},{3,1},... | collective-permute-start | bytes 4325384 | tf_op jit(solution)/shard_map/ppermute | solution.py:73
  67.5 36.0 %collective-permute-start.12 = (bf16[128,5632]{1,0:T(8,128)(2,1)S(1)}, bf16[128,5632]{1,0:T(8,128)(2,1)S(1)}, u32[]{:S(2)}, u32[]{:S(2)}) collective-permute-start(bf16[128,5632]{1,0:T(8,128)(2,1)S(1)} %collective-permute-done.7.refs_2_.refs_18_), channel_id=1, source_target_pairs={{0,4},{2,6},{4,8},{6,10},{8,12},{10,14},{12,0},{14,2},{1,5},{3,7},... | collective-permute-start | bytes 4325384 | tf_op jit(solution)/shard_map/ppermute | solution.py:76
  69.1 34.5 %collective-permute-start.14 = (bf16[128,3072]{1,0:T(8,128)(2,1)S(1)}, bf16[128,3072]{1,0:T(8,128)(2,1)S(1)}, u32[]{:S(2)}, u32[]{:S(2)}) collective-permute-start(bf16[128,3072]{1,0:T(8,128)(2,1)S(1)} %pad_maximum_fusion.2.refs_1_), channel_id=1, source_target_pairs={{0,1},{1,0},{2,3},{3,2},{4,5},{5,4},{6,7},{7,6},{8,9},{9,8},{10,11... | collective-permute-start | bytes 2359304 | tf_op jit(solution)/shard_map/ppermute | solution.py:33
  70.7 36.0 %collective-permute-start.27 = (bf16[128,5632]{1,0:T(8,128)(2,1)S(1)}, bf16[128,5632]{1,0:T(8,128)(2,1)S(1)}, u32[]{:S(2)}, u32[]{:S(2)}) collective-permute-start(bf16[128,5632]{1,0:T(8,128)(2,1)S(1)} %constant_dynamic-update-slice_fusion.4.refs_0_.refs_16_), channel_id=1, source_target_pairs={{0,16},{16,0},{1,17},{17,1},{2,18},{18,2},{3,19},{19,3},{4,20},{20... | collective-permute-start | bytes 4325384 | tf_op jit(solution)/shard_map/ppermute | solution.py:29
  103.6 33.5 %collective-permute-start.23 = (bf16[128,5632]{1,0:T(8,128)(2,1)S(1)}, bf16[128,5632]{1,0:T(8,128)(2,1)}, u32[]{:S(2)}, u32[]{:S(2)}) collective-permute-start(bf16[128,5632]{1,0:T(8,128)(2,1)S(1)} %collective-permute-done.12.refs_4_.refs_20_), channel_id=1, source_target_pairs={{0,2},{2,0},{4,6},{6,4},{8,10},{10,8},{12,14},{14,12},{1,3},{3,1},... | collective-permute-start | bytes 4325384 | tf_op jit(solution)/shard_map/ppermute | solution.py:73
  104.2 20.0 %collective-permute-start.19 = (bf16[128,3072]{1,0:T(8,128)(2,1)S(1)}, bf16[128,3072]{1,0:T(8,128)(2,1)S(1)}, u32[]{:S(2)}, u32[]{:S(2)}) collective-permute-start(bf16[128,3072]{1,0:T(8,128)(2,1)S(1)} %pad_maximum_fusion.3.refs_2_), channel_id=1, source_target_pairs={{0,1},{1,0},{2,3},{3,2},{4,5},{5,4},{6,7},{7,6},{8,9},{9,8},{10,11... | collective-permute-start | bytes 2359304 | tf_op jit(solution)/shard_map/ppermute | solution.py:33
  104.2 34.0 %collective-permute-start.15 = (bf16[128,4096]{1,0:T(8,128)(2,1)S(1)}, bf16[128,4096]{1,0:T(8,128)(2,1)}, u32[]{:S(2)}, u32[]{:S(2)}) collective-permute-start(bf16[128,4096]{1,0:T(8,128)(2,1)S(1)} %slice.296), channel_id=1, source_target_pairs={{0,4},{2,6},{4,8},{6,10},{8,12},{10,14},{12,0},{14,2},{1,5},{3,7},... | collective-permute-start | bytes 3145736 | tf_op jit(solution)/shard_map/ppermute | solution.py:76
  106.6 33.7 %collective-permute-start.28 = (bf16[128,5632]{1,0:T(8,128)(2,1)S(1)}, bf16[128,5632]{1,0:T(8,128)(2,1)S(1)}, u32[]{:S(2)}, u32[]{:S(2)}) collective-permute-start(bf16[128,5632]{1,0:T(8,128)(2,1)S(1)} %collective-permute-done.8.refs_1_.refs_17_), channel_id=1, source_target_pairs={{0,16},{16,0},{1,17},{17,1},{2,18},{18,2},{3,19},{19,3},{4,20},{20... | collective-permute-start | bytes 4325384 | tf_op jit(solution)/shard_map/ppermute | solution.py:29
  106.8 33.7 %collective-permute-start.29 = (bf16[128,5632]{1,0:T(8,128)(2,1)S(1)}, bf16[128,5632]{1,0:T(8,128)(2,1)S(1)}, u32[]{:S(2)}, u32[]{:S(2)}) collective-permute-start(bf16[128,5632]{1,0:T(8,128)(2,1)S(1)} %collective-permute-done.7.refs_2_.refs_18_), channel_id=1, source_target_pairs={{0,16},{16,0},{1,17},{17,1},{2,18},{18,2},{3,19},{19,3},{4,20},{20... | collective-permute-start | bytes 4325384 | tf_op jit(solution)/shard_map/ppermute | solution.py:29
  124.2 18.8 %collective-permute-start.30 = (bf16[128,5632]{1,0:T(8,128)(2,1)S(1)}, bf16[128,5632]{1,0:T(8,128)(2,1)S(1)}, u32[]{:S(2)}, u32[]{:S(2)}) collective-permute-start(bf16[128,5632]{1,0:T(8,128)(2,1)S(1)} %collective-permute-done.13.refs_3_.refs_19_), channel_id=1, source_target_pairs={{0,16},{16,0},{1,17},{17,1},{2,18},{18,2},{3,19},{19,3},{4,20},{20... | collective-permute-start | bytes 4325384 | tf_op jit(solution)/shard_map/ppermute | solution.py:29
  139.7 25.5 %collective-permute-start.26 = (bf16[128,4096]{1,0:T(8,128)(2,1)}, bf16[128,4096]{1,0:T(8,128)(2,1)}, u32[]{:S(2)}, u32[]{:S(2)}) collective-permute-start(bf16[128,4096]{1,0:T(8,128)(2,1)} %collective-permute-done.15.refs_6_.refs_22_), channel_id=1, source_target_pairs={{0,2},{2,0},{4,6},{6,4},{8,10},{10,8},{12,14},{14,12},{1,3},{3,1},... | collective-permute-start | bytes 3145736 | tf_op jit(solution)/shard_map/ppermute | solution.py:73
  142.6 22.6 %collective-permute-start.24 = (bf16[128,3072]{1,0:T(8,128)(2,1)}, bf16[128,3072]{1,0:T(8,128)(2,1)}, u32[]{:S(2)}, u32[]{:S(2)}) collective-permute-start(bf16[128,3072]{1,0:T(8,128)(2,1)} %pad_maximum_fusion.4.refs_3_), channel_id=1, source_target_pairs={{0,16},{16,0},{1,17},{17,1},{2,18},{18,2},{3,19},{19,3},{4,20},{20... | collective-permute-start | bytes 2359304 | tf_op jit(solution)/shard_map/ppermute | solution.py:29
  142.9 24.2 %collective-permute-start.31 = (bf16[128,5632]{1,0:T(8,128)(2,1)S(1)}, bf16[128,5632]{1,0:T(8,128)(2,1)}, u32[]{:S(2)}, u32[]{:S(2)}) collective-permute-start(bf16[128,5632]{1,0:T(8,128)(2,1)S(1)} %collective-permute-done.12.refs_4_.refs_20_), channel_id=1, source_target_pairs={{0,16},{16,0},{1,17},{17,1},{2,18},{18,2},{3,19},{19,3},{4,20},{20... | collective-permute-start | bytes 4325384 | tf_op jit(solution)/shard_map/ppermute | solution.py:29
  144.0 23.7 %collective-permute-start.32 = (bf16[128,5632]{1,0:T(8,128)(2,1)}, bf16[128,5632]{1,0:T(8,128)(2,1)}, u32[]{:S(2)}, u32[]{:S(2)}) collective-permute-start(bf16[128,5632]{1,0:T(8,128)(2,1)} %collective-permute-done.23.refs_5_.refs_21_), channel_id=1, source_target_pairs={{0,16},{16,0},{1,17},{17,1},{2,18},{18,2},{3,19},{19,3},{4,20},{20... | collective-permute-start | bytes 4325384 | tf_op jit(solution)/shard_map/ppermute | solution.py:29
  144.3 23.2 %collective-permute-start.33 = (bf16[128,4096]{1,0:T(8,128)(2,1)}, bf16[128,4096]{1,0:T(8,128)(2,1)}, u32[]{:S(2)}, u32[]{:S(2)}) collective-permute-start(bf16[128,4096]{1,0:T(8,128)(2,1)} %collective-permute-done.15.refs_6_.refs_22_), channel_id=1, source_target_pairs={{0,16},{16,0},{1,17},{17,1},{2,18},{18,2},{3,19},{19,3},{4,20},{20... | collective-permute-start | bytes 3145736 | tf_op jit(solution)/shard_map/ppermute | solution.py:29
  165.2 33.8 %collective-permute-start.37 = (bf16[128,3072]{1,0:T(8,128)(2,1)}, bf16[128,3072]{1,0:T(8,128)(2,1)}, u32[]{:S(2)}, u32[]{:S(2)}) collective-permute-start(bf16[128,3072]{1,0:T(8,128)(2,1)} %pad_maximum_fusion.4.refs_3_), channel_id=1, source_target_pairs={{0,1},{1,0},{2,3},{3,2},{4,5},{5,4},{6,7},{7,6},{8,9},{9,8},{10,11... | collective-permute-start | bytes 2359304 | tf_op jit(solution)/shard_map/ppermute | solution.py:33
  167.2 43.9 %collective-permute-start.38 = (bf16[128,3072]{1,0:T(8,128)(2,1)}, bf16[128,3072]{1,0:T(8,128)(2,1)}, u32[]{:S(2)}, u32[]{:S(2)}) collective-permute-start(bf16[128,3072]{1,0:T(8,128)(2,1)} %copy-done.30), channel_id=1, source_target_pairs={{0,16},{16,0},{1,17},{17,1},{2,18},{18,2},{3,19},{19,3},{4,20},{20... | collective-permute-start | bytes 2359304 | tf_op jit(solution)/shard_map/ppermute | solution.py:29
  167.5 43.6 %collective-permute-start.39 = (bf16[128,3072]{1,0:T(8,128)(2,1)}, bf16[128,3072]{1,0:T(8,128)(2,1)}, u32[]{:S(2)}, u32[]{:S(2)}) collective-permute-start(bf16[128,3072]{1,0:T(8,128)(2,1)} %copy-done.31), channel_id=1, source_target_pairs={{0,16},{16,0},{1,17},{17,1},{2,18},{18,2},{3,19},{19,3},{4,20},{20... | collective-permute-start | bytes 2359304 | tf_op jit(solution)/shard_map/ppermute | solution.py:29
  167.7 43.4 %collective-permute-start.40 = (bf16[128,3072]{1,0:T(8,128)(2,1)}, bf16[128,3072]{1,0:T(8,128)(2,1)}, u32[]{:S(2)}, u32[]{:S(2)}) collective-permute-start(bf16[128,3072]{1,0:T(8,128)(2,1)} %copy-done.32), channel_id=1, source_target_pairs={{0,16},{16,0},{1,17},{17,1},{2,18},{18,2},{3,19},{19,3},{4,20},{20... | collective-permute-start | bytes 2359304 | tf_op jit(solution)/shard_map/ppermute | solution.py:29
  199.0 12.1 %collective-permute-start.41 = (bf16[128,3072]{1,0:T(8,128)(2,1)}, bf16[128,3072]{1,0:T(8,128)(2,1)S(1)}, u32[]{:S(2)}, u32[]{:S(2)}) collective-permute-start(bf16[128,3072]{1,0:T(8,128)(2,1)} %collective-permute-done.37.refs_7_), channel_id=1, source_target_pairs={{0,16},{16,0},{1,17},{17,1},{2,18},{18,2},{3,19},{19,3},{4,20},{20... | collective-permute-start | bytes 2359304 | tf_op jit(solution)/shard_map/ppermute | solution.py:29
  199.2 8.9 %collective-permute-start.35 = (bf16[128,1024]{1,0:T(8,128)(2,1)}, bf16[128,1024]{1,0:T(8,128)(2,1)S(1)}, u32[]{:S(2)}, u32[]{:S(2)}) collective-permute-start(bf16[128,1024]{1,0:T(8,128)(2,1)} %bitcast.111), channel_id=1, source_target_pairs={{0,1},{1,0},{2,3},{3,2},{4,5},{5,4},{6,7},{7,6},{8,9},{9,8},{10,11... | collective-permute-start | bytes 786440 | tf_op jit(solution)/shard_map/ppermute | solution.py:33
  208.0 35.1 %collective-permute-start.44 = (bf16[128,1024]{1,0:T(8,128)(2,1)}, bf16[128,1024]{1,0:T(8,128)(2,1)S(1)}, u32[]{:S(2)}, u32[]{:S(2)}) collective-permute-start(bf16[128,1024]{1,0:T(8,128)(2,1)} %bitcast.94), channel_id=1, source_target_pairs={{0,1},{1,0},{2,3},{3,2},{4,5},{5,4},{6,7},{7,6},{8,9},{9,8},{10,11... | collective-permute-start | bytes 786440 | tf_op jit(solution)/shard_map/ppermute | solution.py:33
  211.1 38.9 %collective-permute-start.36 = (bf16[256,1024]{1,0:T(8,128)(2,1)}, bf16[256,1024]{1,0:T(8,128)(2,1)S(1)}, u32[]{:S(2)}, u32[]{:S(2)}) collective-permute-start(bf16[256,1024]{1,0:T(8,128)(2,1)} %bitcast.107), channel_id=1, source_target_pairs={{0,16},{16,0},{1,17},{17,1},{2,18},{18,2},{3,19},{19,3},{4,20},{20... | collective-permute-start | bytes 1572872 | tf_op jit(solution)/shard_map/ppermute | solution.py:29
  243.1 9.1 %collective-permute-start.45 = (bf16[128,1024]{1,0:T(8,128)(2,1)}, bf16[128,1024]{1,0:T(8,128)(2,1)}, u32[]{:S(2)}, u32[]{:S(2)}) collective-permute-start(bf16[128,1024]{1,0:T(8,128)(2,1)} %get-tuple-element.132), channel_id=1, source_target_pairs={{0,1},{1,0},{2,3},{3,2},{4,5},{5,4},{6,7},{7,6},{8,9},{9,8},{10,11... | collective-permute-start | bytes 786440 | tf_op jit(solution)/shard_map/ppermute | solution.py:33
  245.0 7.2 %collective-permute-start.46 = (bf16[4,128,1024]{2,1,0:T(8,128)(2,1)S(1)}, bf16[4,128,1024]{2,1,0:T(8,128)(2,1)}, u32[]{:S(2)}, u32[]{:S(2)}) collective-permute-start(bf16[4,128,1024]{2,1,0:T(8,128)(2,1)S(1)} %pad_maximum_fusion.1.states_own), channel_id=1, source_target_pairs={{0,16},{16,0},{1,17},{17,1},{2,18},{18,2},{3,19},{19,3},{4,20},{20... | collective-permute-start | bytes 3145736 | tf_op jit(solution)/shard_map/ppermute | solution.py:29
  245.5 4.3 collective-permute-start.42
  245.6 6.6 %collective-permute-start.47 = (bf16[2,128,1024]{2,1,0:T(8,128)(2,1)S(1)}, bf16[2,128,1024]{2,1,0:T(8,128)(2,1)}, u32[]{:S(2)}, u32[]{:S(2)}) collective-permute-start(bf16[2,128,1024]{2,1,0:T(8,128)(2,1)S(1)} %copy-done.20), channel_id=1, source_target_pairs={{0,16},{16,0},{1,17},{17,1},{2,18},{18,2},{3,19},{19,3},{4,20},{20... | collective-permute-start | bytes 1572872 | tf_op jit(solution)/shard_map/ppermute | solution.py:29
  252.2 32.0 %collective-permute-start.48 = (bf16[2,128,1536]{2,1,0:T(8,128)(2,1)S(1)}, bf16[2,128,1536]{2,1,0:T(8,128)(2,1)S(1)}, u32[]{:S(2)}, u32[]{:S(2)}) collective-permute-start(bf16[2,128,1536]{2,1,0:T(8,128)(2,1)S(1)} %pad_maximum_fusion.5), channel_id=1, source_target_pairs={{0,1},{1,0},{2,3},{3,2},{4,5},{5,4},{6,7},{7,6},{8,9},{9,8},{10,11... | collective-permute-start | bytes 2359304 | tf_op jit(solution)/shard_map/ppermute | solution.py:33
  252.7 31.4 %collective-permute-start.49 = (bf16[2,128,1152]{2,1,0:T(8,128)(2,1)S(1)}, bf16[2,128,1152]{2,1,0:T(8,128)(2,1)S(1)}, u32[]{:S(2)}, u32[]{:S(2)}) collective-permute-start(bf16[2,128,1152]{2,1,0:T(8,128)(2,1)S(1)} %pad_maximum_fusion.6), channel_id=1, source_target_pairs={{0,1},{1,0},{2,3},{3,2},{4,5},{5,4},{6,7},{7,6},{8,9},{9,8},{10,11... | collective-permute-start | bytes 1769480 | tf_op jit(solution)/shard_map/ppermute | solution.py:33
  284.2 3.7 collective-permute-start.50
  284.3 3.6 collective-permute-start.51
  304.1 14.3 %collective-permute-start.52 = (bf16[256,768]{1,0:T(8,128)(2,1)}, bf16[256,768]{1,0:T(8,128)(2,1)S(1)}, u32[]{:S(2)}, u32[]{:S(2)}) collective-permute-start(bf16[256,768]{1,0:T(8,128)(2,1)} %get-tuple-element.152), channel_id=1, source_target_pairs={{0,4},{2,6},{4,8},{6,10},{8,12},{10,14},{12,0},{14,2},{1,5},{3,7},... | collective-permute-start | bytes 1179656 | tf_op jit(solution)/shard_map/ppermute | solution.py:76
  304.4 32.4 %collective-permute-start.58 = (bf16[128,5120]{1,0:T(8,128)(2,1)}, bf16[128,5120]{1,0:T(8,128)(2,1)}, u32[]{:S(2)}, u32[]{:S(2)}) collective-permute-start(bf16[128,5120]{1,0:T(8,128)(2,1)} %get-tuple-element.159), channel_id=1, source_target_pairs={{0,2},{2,0},{4,6},{6,4},{8,10},{10,8},{12,14},{14,12},{1,3},{3,1},... | collective-permute-start | bytes 3932168 | tf_op jit(solution)/shard_map/ppermute | solution.py:73
  309.2 42.5 %collective-permute-start.57 = (bf16[256,768]{1,0:T(8,128)(2,1)}, bf16[256,768]{1,0:T(8,128)(2,1)}, u32[]{:S(2)}, u32[]{:S(2)}) collective-permute-start(bf16[256,768]{1,0:T(8,128)(2,1)} %get-tuple-element.157), channel_id=1, source_target_pairs={{4,0},{6,2},{8,4},{10,6},{12,8},{14,10},{0,12},{2,14},{5,1},{7,3},... | collective-permute-start | bytes 1179656 | tf_op jit(solution)/shard_map/ppermute | solution.py:79
  328.3 3.4 collective-permute-start.55
  331.2 9.0 %collective-permute-start.53 = (f32[16,16,1024]{2,1,0:T(8,128)}, f32[16,16,1024]{2,1,0:T(8,128)S(1)}, u32[]{:S(2)}, u32[]{:S(2)}) collective-permute-start(f32[16,16,1024]{2,1,0:T(8,128)} %bitcast.83), channel_id=1, source_target_pairs={{0,16},{16,0},{1,17},{17,1},{2,18},{18,2},{3,19},{19,3},{4,20},{20... | collective-permute-start | bytes 3145736 | tf_op jit(solution)/shard_map/ppermute | solution.py:29
  331.7 4.3 collective-permute-start.56
  336.8 14.1 %collective-permute-start.59 = (bf16[256,768]{1,0:T(8,128)(2,1)}, bf16[256,768]{1,0:T(8,128)(2,1)S(1)}, u32[]{:S(2)}, u32[]{:S(2)}) collective-permute-start(bf16[256,768]{1,0:T(8,128)(2,1)} %add_convert_fusion.3), channel_id=1, source_target_pairs={{0,4},{2,6},{4,8},{6,10},{8,12},{10,14},{12,0},{14,2},{1,5},{3,7},... | collective-permute-start | bytes 1179656 | tf_op jit(solution)/shard_map/ppermute | solution.py:76
  339.1 30.2 %collective-permute-start.60 = (bf16[128,5120]{1,0:T(8,128)(2,1)S(1)}, bf16[128,5120]{1,0:T(8,128)(2,1)S(1)}, u32[]{:S(2)}, u32[]{:S(2)}) collective-permute-start(bf16[128,5120]{1,0:T(8,128)(2,1)S(1)} %copy-done.68), channel_id=1, source_target_pairs={{0,2},{2,0},{4,6},{6,4},{8,10},{10,8},{12,14},{14,12},{1,3},{3,1},... | collective-permute-start | bytes 3932168 | tf_op jit(solution)/shard_map/ppermute | solution.py:73
  339.7 37.8 %collective-permute-start.61 = (bf16[128,5120]{1,0:T(8,128)(2,1)S(1)}, bf16[128,5120]{1,0:T(8,128)(2,1)S(1)}, u32[]{:S(2)}, u32[]{:S(2)}) collective-permute-start(bf16[128,5120]{1,0:T(8,128)(2,1)S(1)} %add_convert_fusion.2), channel_id=1, source_target_pairs={{0,4},{2,6},{4,8},{6,10},{8,12},{10,14},{12,0},{14,2},{1,5},{3,7},... | collective-permute-start | bytes 3932168 | tf_op jit(solution)/shard_map/ppermute | solution.py:76
  341.1 37.5 %collective-permute-start.54 = (f32[32,16,1024]{2,1,0:T(8,128)S(1)}, f32[32,16,1024]{2,1,0:T(8,128)S(1)}, u32[]{:S(2)}, u32[]{:S(2)}) collective-permute-start(f32[32,16,1024]{2,1,0:T(8,128)S(1)} %pad_maximum_fusion), channel_id=1, source_target_pairs={{0,1},{17,16},{2,3},{19,18},{4,5},{21,20},{6,7},{23,22},{8,9},{25,... | collective-permute-start | bytes 6291464 | tf_op jit(solution)/shard_map/ppermute | solution.py:1048
  351.0 71.3 %collective-permute-start.67 = (bf16[128,4096]{1,0:T(8,128)(2,1)S(1)}, bf16[128,4096]{1,0:T(8,128)(2,1)S(1)}, u32[]{:S(2)}, u32[]{:S(2)}) collective-permute-start(bf16[128,4096]{1,0:T(8,128)(2,1)S(1)} %copy-done.28), channel_id=1, source_target_pairs={{0,0},{1,16},{16,1},{17,17},{2,2},{3,18},{18,3},{19,19},{4,4},{5,2... | collective-permute-start | bytes 3145736 | tf_op jit(solution)/shard_map/ppermute | solution.py:37
  378.6 9.2 %collective-permute-start.62 = (bf16[128,1024]{1,0:T(8,128)(2,1)S(1)}, bf16[128,1024]{1,0:T(8,128)(2,1)S(1)}, u32[]{:S(2)}, u32[]{:S(2)}) collective-permute-start(bf16[128,1024]{1,0:T(8,128)(2,1)S(1)} %pad_maximum_fusion.7), channel_id=1, source_target_pairs={{0,2},{2,0},{4,6},{6,4},{8,10},{10,8},{12,14},{14,12},{1,3},{3,1},... | collective-permute-start | bytes 786440 | tf_op jit(solution)/shard_map/ppermute | solution.py:73
  379.9 40.0 %collective-permute-start.65 = (bf16[128,5120]{1,0:T(8,128)(2,1)S(1)}, bf16[128,5120]{1,0:T(8,128)(2,1)S(1)}, u32[]{:S(2)}, u32[]{:S(2)}) collective-permute-start(bf16[128,5120]{1,0:T(8,128)(2,1)S(1)} %copy-done.67), channel_id=1, source_target_pairs={{0,2},{2,0},{4,6},{6,4},{8,10},{10,8},{12,14},{14,12},{1,3},{3,1},... | collective-permute-start | bytes 3932168 | tf_op jit(solution)/shard_map/ppermute | solution.py:73
  380.6 39.2 %collective-permute-start.66 = (bf16[128,5120]{1,0:T(8,128)(2,1)S(1)}, bf16[128,5120]{1,0:T(8,128)(2,1)S(1)}, u32[]{:S(2)}, u32[]{:S(2)}) collective-permute-start(bf16[128,5120]{1,0:T(8,128)(2,1)S(1)} %add_convert_fusion.1), channel_id=1, source_target_pairs={{0,4},{2,6},{4,8},{6,10},{8,12},{10,14},{12,0},{14,2},{1,5},{3,7},... | collective-permute-start | bytes 3932168 | tf_op jit(solution)/shard_map/ppermute | solution.py:76
  387.9 29.4 %collective-permute-start.63 = (bf16[128,640]{1,0:T(8,128)(2,1)S(1)}, bf16[128,640]{1,0:T(8,128)(2,1)}, u32[]{:S(2)}, u32[]{:S(2)}) collective-permute-start(bf16[128,640]{1,0:T(8,128)(2,1)S(1)} %pad_maximum_fusion.9), channel_id=1, source_target_pairs={{0,4},{2,6},{4,8},{6,10},{8,12},{10,14},{12,0},{14,2},{1,5},{3,7},... | collective-permute-start | bytes 491528 | tf_op jit(solution)/shard_map/ppermute | solution.py:76
  392.0 26.8 %collective-permute-start.64 = (bf16[128,640]{1,0:T(8,128)(2,1)S(1)}, bf16[128,640]{1,0:T(8,128)(2,1)S(1)}, u32[]{:S(2)}, u32[]{:S(2)}) collective-permute-start(bf16[128,640]{1,0:T(8,128)(2,1)S(1)} %pad_maximum_fusion.9), channel_id=1, source_target_pairs={{4,0},{6,2},{8,4},{10,6},{12,8},{14,10},{0,12},{2,14},{5,1},{7,3},... | collective-permute-start | bytes 491528 | tf_op jit(solution)/shard_map/ppermute | solution.py:79
  422.2 8.6 %collective-permute-start.68 = (bf16[128,640]{1,0:T(8,128)(2,1)}, bf16[128,640]{1,0:T(8,128)(2,1)}, u32[]{:S(2)}, u32[]{:S(2)}) collective-permute-start(bf16[128,640]{1,0:T(8,128)(2,1)} %collective-permute-done.63), channel_id=1, source_target_pairs={{0,4},{2,6},{4,8},{6,10},{8,12},{10,14},{12,0},{14,2},{1,5},{3,7},... | collective-permute-start | bytes 491528 | tf_op jit(solution)/shard_map/ppermute | solution.py:76
  424.8 12.9 %collective-permute-start.72 = (bf16[128,1024]{1,0:T(8,128)(2,1)}, bf16[128,1024]{1,0:T(8,128)(2,1)S(1)}, u32[]{:S(2)}, u32[]{:S(2)}) collective-permute-start(bf16[128,1024]{1,0:T(8,128)(2,1)} %slice.260), channel_id=1, source_target_pairs={{0,2},{2,0},{4,6},{6,4},{8,10},{10,8},{12,14},{14,12},{1,3},{3,1},... | collective-permute-start | bytes 786440 | tf_op jit(solution)/shard_map/ppermute | solution.py:73
  426.4 11.4 %collective-permute-start.73 = (bf16[128,1024]{1,0:T(8,128)(2,1)}, bf16[128,1024]{1,0:T(8,128)(2,1)S(1)}, u32[]{:S(2)}, u32[]{:S(2)}) collective-permute-start(bf16[128,1024]{1,0:T(8,128)(2,1)} %slice.318), channel_id=1, source_target_pairs={{0,4},{2,6},{4,8},{6,10},{8,12},{10,14},{12,0},{14,2},{1,5},{3,7},... | collective-permute-start | bytes 786440 | tf_op jit(solution)/shard_map/ppermute | solution.py:76
  427.1 28.0 %collective-permute-start.70 = (bf16[128,4096]{1,0:T(8,128)(2,1)}, bf16[128,4096]{1,0:T(8,128)(2,1)}, u32[]{:S(2)}, u32[]{:S(2)}) collective-permute-start(bf16[128,4096]{1,0:T(8,128)(2,1)} %slice.258), channel_id=1, source_target_pairs={{0,2},{1,18},{16,3},{17,19},{2,0},{3,16},{18,1},{19,17},{4,6},{5,2... | collective-permute-start | bytes 3145736 | tf_op jit(solution)/shard_map/ppermute | solution.py:1065
  427.6 30.9 %collective-permute-start.71 = (bf16[128,4096]{1,0:T(8,128)(2,1)}, bf16[128,4096]{1,0:T(8,128)(2,1)}, u32[]{:S(2)}, u32[]{:S(2)}) collective-permute-start(bf16[128,4096]{1,0:T(8,128)(2,1)} %slice.317), channel_id=1, source_target_pairs={{0,4},{1,20},{16,5},{17,21},{2,6},{3,22},{18,7},{19,23},{4,8},{5,2... | collective-permute-start | bytes 3145736 | tf_op jit(solution)/shard_map/ppermute | solution.py:1065
  (80 other events, 1221.9 us)

commit v10 on v9

--- a/solution.py
+++ b/solution.py
@@ -118,7 +118,10 @@
 
 def forward_kernel(count, column, places, normed, b_own, b_other, *refs):
     in_own, in_other, w_own, w_other = [refs[n * count : (n + 1) * count] for n in range(4)]
-    kept, given, before, gates, cells, wi, w, b, state, cell, sems = refs[4 * count :]
+    (
+        kept, given, before, gates_out, cells_out, gates, cells, wi, w, b, state, cell, sems,
+        gate_sems, cell_sems,
+    ) = refs[4 * count :]
     steps, rows, wide_full = gates.shape
     wide_half = wide_full // 2
     unit_half = wide_half // 4
@@ -171,9 +174,18 @@
             upper, lower = new_hidden[:eighth], new_hidden[eighth:]
             kept[t, :, units] = jnp.where(first_chip, upper, lower).astype(low)
             given[t, :, units] = jnp.where(first_chip, lower, upper).astype(low)
+        pltpu.make_async_copy(gates.at[t], gates_out.at[t], gate_sems.at[t]).start()
+        pltpu.make_async_copy(cells.at[t], cells_out.at[t], cell_sems.at[t]).start()
         return carried
 
     lax.fori_loop(0, steps, advance, 0)
+
+    def settle(t, carried):
+        pltpu.make_async_copy(gates.at[t], gates_out.at[t], gate_sems.at[t]).wait()
+        pltpu.make_async_copy(cells.at[t], cells_out.at[t], cell_sems.at[t]).wait()
+        return carried
+
+    lax.fori_loop(0, steps, settle, 0)
 
 
 def run_forward(places, normed, b_own, b_other, in_own, in_other, w_own, w_other, steps, column):
@@ -191,29 +203,44 @@
             jax.ShapeDtypeStruct((steps, rows, units), wide),
         ),
         in_specs=[in_smem] + [in_vmem] * 3 + [in_place] * (4 * count),
-        out_specs=[in_vmem] * 5,
+        out_specs=[in_vmem] * 3 + [in_place] * 2,
         scratch_shapes=[
+            pltpu.VMEM((steps, rows, 2 * wide_half), wide),
+            pltpu.VMEM((steps, rows, units), wide),
             pltpu.VMEM((units, 2 * wide_half), low),
             pltpu.VMEM((units, 2 * wide_half), low),
             pltpu.VMEM((1, 2 * wide_half), wide),
             pltpu.VMEM((rows, units), low),
             pltpu.VMEM((rows, units), wide),
             pltpu.SemaphoreType.DMA((4 * count,)),
+            pltpu.SemaphoreType.DMA((steps,)),
+            pltpu.SemaphoreType.DMA((steps,)),
         ],
         compiler_params=pltpu.CompilerParams(vmem_limit_bytes=56 << 20),
         name="recur_forward",
     )(places, normed, b_own, b_other, *in_own, *in_other, *w_own, *w_other)
 
 
-def backward_kernel(count, column, places, kept, taken, gates, cells, *refs):
+def backward_kernel(count, column, places, kept, taken, gates_in, cells_in, *refs):
     w_own, w_other = refs[:count], refs[count : 2 * count]
-    dz_own, dz_other, dz, stage, w, dh, dc, sems = refs[2 * count :]
+    dz_own, dz_other, gates, cells, dz, stage, w, dh, dc, sems, gate_sems, cell_sems = refs[
+        2 * count :
+    ]
     steps, rows, wide_full = gates.shape
     wide_half = wide_full // 2
     unit_half = wide_half // 4
     chunk = min(256, unit_half)
     s = places[0]
     first_chip = places[1] == 0
+
+    def gate_copy(t):
+        return pltpu.make_async_copy(gates_in.at[t], gates.at[t], gate_sems.at[t])
+
+    def cell_copy(t):
+        return pltpu.make_async_copy(cells_in.at[t], cells.at[t], cell_sems.at[t])
+
+    gate_copy(steps - 1).start()
+    cell_copy(steps - 1).start()
     jobs = []
     for n, (sources, at) in enumerate(((w_own, s), (w_other, 1 - s))):
         for k, block in enumerate(sources):
@@ -223,6 +250,9 @@
             )
             copy.start()
             jobs.append((copy, slot, at, places[2 + k] * block.shape[0]))
+    for t in range(steps - 2, -1, -1):
+        cell_copy(t).start()
+        gate_copy(t).start()
     dh[...] = jnp.zeros_like(dh)
     dc[...] = jnp.zeros_like(dc)
     height = w_own[0].shape[0]
@@ -240,9 +270,17 @@
 
         lax.fori_loop(0, 4, turn, 0)
 
+    cell_copy(steps - 1).wait()
+
     def retreat(k, carried):
         t = steps - 1 - k
         earlier = jnp.maximum(t - 1, 0)
+        gate_copy(t).wait()
+
+        @pl.when(t > 0)
+        def _():
+            cell_copy(earlier).wait()
+
         live = jnp.where(t > 0, 1.0, 0.0).astype(wide)
         for at in range(0, 2 * unit_half, chunk):
             half, inside = at // unit_half, at % unit_half
@@ -286,15 +324,19 @@
     return pl.pallas_call(
         functools.partial(backward_kernel, count, column),
         out_shape=(jax.ShapeDtypeStruct((steps, rows, wide_full // 2), low),) * 2,
-        in_specs=[in_smem] + [in_vmem] * 4 + [in_place] * (2 * count),
+        in_specs=[in_smem] + [in_vmem] * 2 + [in_place] * (2 + 2 * count),
         out_specs=[in_vmem] * 2,
         scratch_shapes=[
+            pltpu.VMEM((steps, rows, wide_full), wide),
+            pltpu.VMEM((steps, rows, units), wide),
             pltpu.VMEM((2, rows, wide_full // 2), low),
             pltpu.VMEM((2 * count, units // count, wide_full // 2), low),
             pltpu.VMEM((wide_full, units), low),
             pltpu.VMEM((rows, units), wide),
             pltpu.VMEM((rows, units), wide),
             pltpu.SemaphoreType.DMA((2 * count,)),
+            pltpu.SemaphoreType.DMA((steps,)),
+            pltpu.SemaphoreType.DMA((steps,)),
         ],
         compiler_params=pltpu.CompilerParams(vmem_limit_bytes=56 << 20),
         name="recur_backward",
@@ -505,8 +547,8 @@
         logits = logits + jnp.dot(pack[r, :, 5 * block :], v[r], preferred_element_type=wide)
     shifted = jnp.exp(logits - jnp.max(logits, axis=-1, keepdims=True))
     softmax = shifted / jnp.sum(shifted, axis=-1, keepdims=True)
-    onehot = (labels[...] == lax.broadcasted_iota(jnp.int32, softmax.shape, 1)).astype(wide)
-    grad_logits = ((softmax - onehot) * counted[...]).astype(low)
+    onehot = (labels[:, :1] == lax.broadcasted_iota(jnp.int32, softmax.shape, 1)).astype(wide)
+    grad_logits = ((softmax - onehot) * counted[:, :1]).astype(low)
     seen[1] = grad_logits
     sums[5:6, :] = jnp.sum(grad_logits.astype(wide), axis=0, keepdims=True)
     sums[6:8, :] = jnp.zeros((2, sums.shape[1]), wide)
@@ -875,8 +917,10 @@
     length_part = lax.dynamic_slice_in_dim(enc_lengths, start, quarter, axis=0)
     length_part = jnp.broadcast_to(length_part[:, None], (quarter, 128))
     label_part = lax.dynamic_slice_in_dim(labels, start, quarter, axis=0).T.reshape(rows, 1)
+    label_part = jnp.broadcast_to(label_part, (rows, 128))
     count_part = lax.dynamic_slice_in_dim(label_lengths, start, quarter, axis=0)
     counted = (jnp.arange(frames)[:, None] < count_part[None, :]).astype(wide).reshape(rows, 1)
+    counted = jnp.broadcast_to(counted, (rows, 128))
     bias_row = jnp.pad(vocab_bias, (0, vocab_pad - vocab_size), constant_values=-1e30)[None]
 
     vector_own = jnp.stack([mono_bias, mono_vec, span_bias, span_vec, out_bias])

time: 467 us -> 467 us (level)
    unnamed x154 -> x158, local copies, waits for them, and re-layouts: 14.8 us -> 16.1 us
  transfers between devices with their start and end apart: 74 -> 74, of which waited for: 27 -> 28; matrix products, arithmetic and copies ran while one was open for 11% -> 10% of each run, Pallas kernels for 22% -> 21%
where the time goes in v10:
time: 467 us; the launch traced here: 464 us
  waiting for transfers between devices  209 us (45%)
  Pallas kernels  114 us (24%)
  starting transfers between devices  67.4 us (14%)
  local copies, waits for them, and re-layouts  50.2 us (11%)
  other arithmetic  21.6 us (5%)
    ppermute x11, waiting for transfers between devices, across(): return lax.ppermute(array, 'dp', self.pair)  101 us
    ppermute x11, waiting for transfers between devices, onward(): return lax.ppermute(array, 'dp', self.ring)  48.2 us
    pallas_call x1, Pallas kernels, run_attend(): pl.pallas_call(functools.partial(attend_kernel, count), out_shape=(jax.Sh...  31.2 us
    ppermute x11, waiting for transfers between devices, across_chips(): return lax.ppermute(array, 'mp', core_swap)  31.2 us
    pallas_call x1, Pallas kernels, run_forward(): pl.pallas_call(functools.partial(forward_kernel, count, column), out_shap...  30 us
    pallas_call x1, Pallas kernels, run_backward(): pl.pallas_call(functools.partial(backward_kernel, count, column), out_sha...  28.9 us
    ppermute x2, waiting for transfers between devices, cornered(): return lambda array: lax.ppermute(array, ('section', 'dp', 'mp'), pairs)  19.9 us
    unnamed x158, local copies, waits for them, and re-layouts  16.1 us
  transfers between devices with their start and end apart: 74, of which 28 were waited for; matrix products, arithmetic and copies ran while one was open for 10% of the time, Pallas kernels for 21%

profile of v10, /device:TPU:0, one launch (start us, length us, event | category | flops | bytes accessed | tf_op | source)
XLA Modules:
  0.0 464.3 jit_solution(12251055421767246685)
XLA Ops:
  0.8 2.1 copy.65
  2.8 2.0 copy.66
  8.7 2.9 collective-permute-start.3
  11.6 1.6 collective-permute-start.2
  13.7 5.4 %collective-permute-start = (bf16[128,2048]{1,0:T(8,128)(2,1)}, bf16[128,2048]{1,0:T(8,128)(2,1)}, u32[]{:S(2)}, u32[]{:S(2)}) collective-permute-start(bf16[128,2048]{1,0:T(8,128)(2,1)} %bitcast.60), channel_id=1, source_target_pairs={{0,0},{1,16},{16,1},{17,17},{2,2},{3,18},{18,3},{19,19},{4,4},{5,2... | collective-permute-start | bytes 1572872 | tf_op jit(solution)/shard_map/ppermute | solution.py:37
  20.6 1.3 pad.25
  23.3 1.7 collective-permute-start.1
  26.7 1.4 constant_dynamic-update-slice_fusion.6
  28.8 1.6 collective-permute-start.7
  30.4 4.1 collective-permute-start.9
  34.5 2.0 collective-permute-start.5
  39.1 1.1 copy.58
  40.2 19.0 %collective-permute-done.8.refs_1_.refs_17_ = bf16[128,5632]{1,0:T(8,128)(2,1)S(1)} collective-permute-done((bf16[128,5632]{1,0:T(8,128)(2,1)S(1)}, bf16[128,5632]{1,0:T(8,128)(2,1)S(1)}, u32[]{:S(2)}, u32[]{:S(2)}) %collective-permute-start.8) | collective-permute-done | bytes 1441824 | tf_op jit(solution)/shard_map/ppermute | solution.py:73
  59.4 4.3 collective-permute-done.5
  63.7 1.7 broadcast_in_dim.23.noise
  67.4 1.5 collective-permute-start.13
  68.9 1.6 collective-permute-start.12
  70.5 1.7 collective-permute-start.14
  72.2 29.7 %collective-permute-done.13.refs_3_.refs_19_ = bf16[128,5632]{1,0:T(8,128)(2,1)S(1)} collective-permute-done((bf16[128,5632]{1,0:T(8,128)(2,1)S(1)}, bf16[128,5632]{1,0:T(8,128)(2,1)S(1)}, u32[]{:S(2)}, u32[]{:S(2)}) %collective-permute-start.13) | collective-permute-done | bytes 1441824 | tf_op jit(solution)/shard_map/ppermute | solution.py:73
  102.0 2.9 collective-permute-done.12.refs_4_.refs_20_
  105.7 2.3 collective-permute-done.20.refs_8_
  108.6 17.0 %collective-permute-done.19.refs_6_ = bf16[128,3072]{1,0:T(8,128)(2,1)S(1)} collective-permute-done((bf16[128,3072]{1,0:T(8,128)(2,1)S(1)}, bf16[128,3072]{1,0:T(8,128)(2,1)S(1)}, u32[]{:S(2)}, u32[]{:S(2)}) %collective-permute-start.19) | collective-permute-done | bytes 786464 | tf_op jit(solution)/shard_map/ppermute | solution.py:33
  125.6 12.9 %collective-permute-done.23.refs_5_.refs_21_ = bf16[128,5632]{1,0:T(8,128)(2,1)} collective-permute-done((bf16[128,5632]{1,0:T(8,128)(2,1)S(1)}, bf16[128,5632]{1,0:T(8,128)(2,1)}, u32[]{:S(2)}, u32[]{:S(2)}) %collective-permute-start.23) | collective-permute-done | bytes 1441824 | tf_op jit(solution)/shard_map/ppermute | solution.py:73
  142.5 1.3 collective-permute-done.25.b_other
  146.3 20.4 %collective-permute-done.26.refs_7_.refs_23_ = bf16[128,4096]{1,0:T(8,128)(2,1)} collective-permute-done((bf16[128,4096]{1,0:T(8,128)(2,1)}, bf16[128,4096]{1,0:T(8,128)(2,1)}, u32[]{:S(2)}, u32[]{:S(2)}) %collective-permute-start.26) | collective-permute-done | bytes 1048608 | tf_op jit(solution)/shard_map/ppermute | solution.py:73
  169.7 30.0 %recur_forward.1 = (bf16[16,8,1024]{2,1,0:T(8,128)(2,1)}, bf16[16,8,1024]{2,1,0:T(8,128)(2,1)}, bf16[16,16,1024]{2,1,0:T(8,128)(2,1)}, f32[16,16,4096]{2,1,0:T(8,128)}, f32[16,16,1024]{2,1,0:T(8,128)}) custom-call(s32[10]{0:T(128)} %stack.116.places, bf16[256,1024]{1,0:T(8,128)(2,1)} %bitcast.87, f32[1,2048]{1,0:T(1,128)} %copy-done.61, ...), custom_call_target="tpu_custom_call" | custom-call | tf_op jit(solution)/shard_map/recur_forward/pallas_call | solution.py:196
  199.8 1.9 collective-permute-start.35
  201.7 7.0 %collective-permute-done.35.taken = bf16[128,1024]{1,0:T(8,128)(2,1)S(1)} collective-permute-done((bf16[128,1024]{1,0:T(8,128)(2,1)}, bf16[128,1024]{1,0:T(8,128)(2,1)S(1)}, u32[]{:S(2)}, u32[]{:S(2)}) %collective-permute-start.35) | collective-permute-done | bytes 262176 | tf_op jit(solution)/shard_map/ppermute | solution.py:33
  208.7 1.6 collective-permute-start.44
  212.6 31.2 %attend.1 = (f32[128,1024]{1,0:T(8,128)}, bf16[128,1024]{1,0:T(8,128)(2,1)}, bf16[128,1536]{1,0:T(8,128)(2,1)}, bf16[128,1536]{1,0:T(8,128)(2,1)}, bf16[2,128,15...) custom-call(s32[10]{0:T(128)} %stack.116.places, ...), custom_call_target="tpu_custom_call" | custom-call | tf_op jit(solution)/shard_map/attend/pallas_call | solution.py:696
  249.1 1.3 collective-permute-done.42.pack_core
  250.5 2.3 collective-permute-done.45
  253.3 1.6 collective-permute-start.49
  254.9 28.9 %recur_backward.1 = (bf16[16,16,2048]{2,1,0:T(8,128)(2,1)}, bf16[16,16,2048]{2,1,0:T(8,128)(2,1)}) custom-call(s32[10]{0:T(128)} %stack.116.places, f32[16,8,1024]{2,1,0:T(8,128)} %bitcast.102, bf16[16,8,1024]{2,1,0:T(8,128)(2,1)} %bitcast.43.taken, f32[16,16,4096]{2,1,0:T(8,128)} %get-tuple-element.137.gates_in, ...), custom_call_target="tpu_custom_call" | custom-call | tf_op jit(solution)/shard_map/recur_backward/pallas_call | solution.py:324
  286.5 1.7 collective-permute-done.51.far_core
  289.2 15.2 %weight_gradients.1 = (bf16[128,5120]{1,0:T(8,128)(2,1)}, bf16[128,5120]{1,0:T(8,128)(2,1)}, bf16[128,5120]{1,0:T(8,128)(2,1)}, bf16[128,5120]{1,0:T(8,128)(2,1)...) custom-call(s32[13]{0:T(128)} %stack.123.order, ...), custom_call_target="tpu_custom_call" | custom-call | tf_op jit(solution)/shard_map/weight_gradients/pallas_call | solution.py:853
  305.5 2.3 slice.258
  307.9 1.7 slice.260
  309.5 3.7 collective-permute-start.57
  313.3 5.5 %collective-permute-done.52 = bf16[256,768]{1,0:T(8,128)(2,1)S(1)} collective-permute-done((bf16[256,768]{1,0:T(8,128)(2,1)}, bf16[256,768]{1,0:T(8,128)(2,1)S(1)}, u32[]{:S(2)}, u32[]{:S(2)}) %collective-permute-start.52) | collective-permute-done | bytes 393248 | tf_op jit(solution)/shard_map/ppermute | solution.py:76
  319.5 9.0 %input_back.1 = (f32[256,1024]{1,0:T(8,128)}, f32[1,1024]{1,0:T(1,128)}) custom-call(s32[10]{0:T(128)} %stack.116.places, bf16[256,1024]{1,0:T(8,128)(2,1)} %bitcast.91, f32[1,1024]{1,0:T(1,128)} %bitcast.114, bf16[256,2048]{1,0:T(8,128)(2,1)} %bitcast.85, bf16[256,2048]{1,0:T(8,128)(2,1)} %bitcast.99, bf16[128,5632]{1,0:T(8,128)(2,1)} %copy-done.3, ...), custom_call_target="tpu_custom_call" | custom-call | tf_op jit(solution)/shard_map/input_back/pallas_call | solution.py:375
  329.8 1.6 copy.74
  332.6 2.0 add_convert_fusion.3
  334.5 1.8 collective-permute-done.56
  337.3 2.1 add_convert_fusion.2
  341.5 2.8 collective-permute-start.54
  344.3 7.0 %collective-permute-done.59 = bf16[256,768]{1,0:T(8,128)(2,1)S(1)} collective-permute-done((bf16[256,768]{1,0:T(8,128)(2,1)}, bf16[256,768]{1,0:T(8,128)(2,1)S(1)}, u32[]{:S(2)}, u32[]{:S(2)}) %collective-permute-start.59) | collective-permute-done | bytes 393248 | tf_op jit(solution)/shard_map/ppermute | solution.py:76
  352.1 1.2 fusion.20
  353.4 16.2 %collective-permute-done.60 = bf16[128,5120]{1,0:T(8,128)(2,1)S(1)} collective-permute-done((bf16[128,5120]{1,0:T(8,128)(2,1)S(1)}, bf16[128,5120]{1,0:T(8,128)(2,1)S(1)}, u32[]{:S(2)}, u32[]{:S(2)}) %collective-permute-start.60) | collective-permute-done | bytes 1310752 | tf_op jit(solution)/shard_map/ppermute | solution.py:73
  369.6 8.2 %collective-permute-done.61 = bf16[128,5120]{1,0:T(8,128)(2,1)S(1)} collective-permute-done((bf16[128,5120]{1,0:T(8,128)(2,1)S(1)}, bf16[128,5120]{1,0:T(8,128)(2,1)S(1)}, u32[]{:S(2)}, u32[]{:S(2)}) %collective-permute-start.61) | collective-permute-done | bytes 1310752 | tf_op jit(solution)/shard_map/ppermute | solution.py:76
  378.9 1.3 collective-permute-start.62
  381.0 4.1 collective-permute-start.66
  385.1 1.7 select_bitcast_fusion
  386.8 1.4 collective-permute-done.62
  388.3 4.2 collective-permute-start.63
  393.3 24.4 %collective-permute-done.63 = bf16[128,640]{1,0:T(8,128)(2,1)} collective-permute-done((bf16[128,640]{1,0:T(8,128)(2,1)S(1)}, bf16[128,640]{1,0:T(8,128)(2,1)}, u32[]{:S(2)}, u32[]{:S(2)}) %collective-permute-start.63) | collective-permute-done | bytes 163872 | tf_op jit(solution)/shard_map/ppermute | solution.py:76
  422.6 1.2 collective-permute-start.68
  425.2 1.6 collective-permute-start.72
  427.9 3.0 collective-permute-start.71
  438.9 16.4 %collective-permute-done.70 = bf16[128,4096]{1,0:T(8,128)(2,1)} collective-permute-done((bf16[128,4096]{1,0:T(8,128)(2,1)}, bf16[128,4096]{1,0:T(8,128)(2,1)}, u32[]{:S(2)}, u32[]{:S(2)}) %collective-permute-start.70) | collective-permute-done | bytes 1048608 | tf_op jit(solution)/shard_map/ppermute | solution.py:1109
  455.4 3.5 collective-permute-done.71
  458.8 2.0 convert_add_fusion
  461.0 1.7 reshape.193
  462.7 1.7 reshape.194
  (374 shorter events, 63.1 us)
Async XLA Ops:
  8.7 16.3 %collective-permute-start.3 = (bf16[128,1536]{1,0:T(8,128)(2,1)}, bf16[128,1536]{1,0:T(8,128)(2,1)}, u32[]{:S(2)}, u32[]{:S(2)}) collective-permute-start(bf16[128,1536]{1,0:T(8,128)(2,1)} %get-tuple-element.215), channel_id=1, source_target_pairs={{0,2},{2,0},{4,6},{6,4},{8,10},{10,8},{12,14},{14,12},{1,3},{3,1},... | collective-permute-start | bytes 1179656 | tf_op jit(solution)/shard_map/ppermute | solution.py:73
  11.6 16.5 %collective-permute-start.2 = (bf16[128,1536]{1,0:T(8,128)(2,1)}, bf16[128,1536]{1,0:T(8,128)(2,1)S(1)}, u32[]{:S(2)}, u32[]{:S(2)}) collective-permute-start(bf16[128,1536]{1,0:T(8,128)(2,1)} %get-tuple-element.215), channel_id=1, source_target_pairs={{0,4},{2,6},{4,8},{6,10},{8,12},{10,14},{12,0},{14,2},{1,5},{3,7},... | collective-permute-start | bytes 1179656 | tf_op jit(solution)/shard_map/ppermute | solution.py:76
  13.2 21.3 %collective-permute-start.10 = (bf16[16,32,1024]{2,0,1:T(8,128)(2,1)S(1)}, bf16[16,32,1024]{2,0,1:T(8,128)(2,1)}, u32[]{:S(2)}, u32[]{:S(2)}) collective-permute-start(bf16[16,32,1024]{2,0,1:T(8,128)(2,1)S(1)} %bitcast.100), channel_id=1, source_target_pairs={{0,16},{16,0},{1,17},{17,1},{2,18},{18,2},{3,19},{19,3},{4,20},{20... | collective-permute-start | bytes 3145736 | tf_op jit(solution)/shard_map/ppermute | solution.py:29
  13.2 9.4 %collective-permute-start.11 = (f32[1024]{0:T(1024)S(1)}, f32[1024]{0:T(1024)S(1)}, u32[]{:S(2)}, u32[]{:S(2)}) collective-permute-start(f32[1024]{0:T(1024)S(1)} %bitcast.120), channel_id=1, source_target_pairs={{0,16},{16,0},{1,17},{17,1},{2,18},{18,2},{3,19},{19,3},{4,20},{20... | collective-permute-start | bytes 12296 | tf_op jit(solution)/shard_map/ppermute | solution.py:29
  13.7 12.9 %collective-permute-start = (bf16[128,2048]{1,0:T(8,128)(2,1)}, bf16[128,2048]{1,0:T(8,128)(2,1)}, u32[]{:S(2)}, u32[]{:S(2)}) collective-permute-start(bf16[128,2048]{1,0:T(8,128)(2,1)} %bitcast.60), channel_id=1, source_target_pairs={{0,0},{1,16},{16,1},{17,17},{2,2},{3,18},{18,3},{19,19},{4,4},{5,2... | collective-permute-start | bytes 1572872 | tf_op jit(solution)/shard_map/ppermute | solution.py:37
  23.3 4.8 %collective-permute-start.1 = (bf16[128,2048]{1,0:T(8,128)(2,1)}, bf16[128,2048]{1,0:T(8,128)(2,1)S(1)}, u32[]{:S(2)}, u32[]{:S(2)}) collective-permute-start(bf16[128,2048]{1,0:T(8,128)(2,1)} %bitcast.106), channel_id=1, source_target_pairs={{0,0},{1,16},{16,1},{17,17},{2,2},{3,18},{18,3},{19,19},{4,4},{5,2... | collective-permute-start | bytes 1572872 | tf_op jit(solution)/shard_map/ppermute | solution.py:37
  25.0 3.2 collective-permute-start.4
  28.2 31.0 %collective-permute-start.8 = (bf16[128,5632]{1,0:T(8,128)(2,1)S(1)}, bf16[128,5632]{1,0:T(8,128)(2,1)S(1)}, u32[]{:S(2)}, u32[]{:S(2)}) collective-permute-start(bf16[128,5632]{1,0:T(8,128)(2,1)S(1)} %constant_dynamic-update-slice_fusion.4.refs_0_.refs_16_), channel_id=1, source_target_pairs={{0,2},{2,0},{4,6},{6,4},{8,10},{10,8},{12,14},{14,12},{1,3},{3,1},... | collective-permute-start | bytes 4325384 | tf_op jit(solution)/shard_map/ppermute | solution.py:73
  28.8 34.9 %collective-permute-start.7 = (bf16[128,5632]{1,0:T(8,128)(2,1)S(1)}, bf16[128,5632]{1,0:T(8,128)(2,1)S(1)}, u32[]{:S(2)}, u32[]{:S(2)}) collective-permute-start(bf16[128,5632]{1,0:T(8,128)(2,1)S(1)} %constant_dynamic-update-slice_fusion.4.refs_0_.refs_16_), channel_id=1, source_target_pairs={{0,4},{2,6},{4,8},{6,10},{8,12},{10,14},{12,0},{14,2},{1,5},{3,7},... | collective-permute-start | bytes 4325384 | tf_op jit(solution)/shard_map/ppermute | solution.py:76
  30.4 33.3 %collective-permute-start.9 = (bf16[128,3072]{1,0:T(8,128)(2,1)S(1)}, bf16[128,3072]{1,0:T(8,128)(2,1)S(1)}, u32[]{:S(2)}, u32[]{:S(2)}) collective-permute-start(bf16[128,3072]{1,0:T(8,128)(2,1)S(1)} %constant_dynamic-update-slice_fusion.7.refs_0_), channel_id=1, source_target_pairs={{0,1},{1,0},{2,3},{3,2},{4,5},{5,4},{6,7},{7,6},{8,9},{9,8},{10,11... | collective-permute-start | bytes 2359304 | tf_op jit(solution)/shard_map/ppermute | solution.py:33
  34.5 29.1 %collective-permute-start.6 = (bf16[256,1024]{1,0:T(8,128)(2,1)S(1)}, bf16[256,1024]{1,0:T(8,128)(2,1)S(1)}, u32[]{:S(2)}, u32[]{:S(2)}) collective-permute-start(bf16[256,1024]{1,0:T(8,128)(2,1)S(1)} %pad.24.refs_16_), channel_id=1, source_target_pairs={{0,1},{1,0},{2,3},{3,2},{4,5},{5,4},{6,7},{7,6},{8,9},{9,8},{10,11... | collective-permute-start | bytes 1572872 | tf_op jit(solution)/shard_map/ppermute | solution.py:33
  34.5 29.1 %collective-permute-start.5 = (f32[5,256]{1,0:T(8,128)S(1)}, f32[5,256]{1,0:T(8,128)S(1)}, u32[]{:S(2)}, u32[]{:S(2)}) collective-permute-start(f32[5,256]{1,0:T(8,128)S(1)} %stack.129), channel_id=1, source_target_pairs={{0,1},{1,0},{2,3},{3,2},{4,5},{5,4},{6,7},{7,6},{8,9},{9,8},{10,11... | collective-permute-start | bytes 15368 | tf_op jit(solution)/shard_map/ppermute | solution.py:33
  67.4 34.5 %collective-permute-start.13 = (bf16[128,5632]{1,0:T(8,128)(2,1)S(1)}, bf16[128,5632]{1,0:T(8,128)(2,1)S(1)}, u32[]{:S(2)}, u32[]{:S(2)}) collective-permute-start(bf16[128,5632]{1,0:T(8,128)(2,1)S(1)} %collective-permute-done.7.refs_2_.refs_18_), channel_id=1, source_target_pairs={{0,2},{2,0},{4,6},{6,4},{8,10},{10,8},{12,14},{14,12},{1,3},{3,1},... | collective-permute-start | bytes 4325384 | tf_op jit(solution)/shard_map/ppermute | solution.py:73
  68.9 36.0 %collective-permute-start.12 = (bf16[128,5632]{1,0:T(8,128)(2,1)S(1)}, bf16[128,5632]{1,0:T(8,128)(2,1)S(1)}, u32[]{:S(2)}, u32[]{:S(2)}) collective-permute-start(bf16[128,5632]{1,0:T(8,128)(2,1)S(1)} %collective-permute-done.7.refs_2_.refs_18_), channel_id=1, source_target_pairs={{0,4},{2,6},{4,8},{6,10},{8,12},{10,14},{12,0},{14,2},{1,5},{3,7},... | collective-permute-start | bytes 4325384 | tf_op jit(solution)/shard_map/ppermute | solution.py:76
  70.5 34.5 %collective-permute-start.14 = (bf16[128,3072]{1,0:T(8,128)(2,1)S(1)}, bf16[128,3072]{1,0:T(8,128)(2,1)S(1)}, u32[]{:S(2)}, u32[]{:S(2)}) collective-permute-start(bf16[128,3072]{1,0:T(8,128)(2,1)S(1)} %pad_maximum_fusion.2.refs_1_), channel_id=1, source_target_pairs={{0,1},{1,0},{2,3},{3,2},{4,5},{5,4},{6,7},{7,6},{8,9},{9,8},{10,11... | collective-permute-start | bytes 2359304 | tf_op jit(solution)/shard_map/ppermute | solution.py:33
  72.2 36.0 %collective-permute-start.27 = (bf16[128,5632]{1,0:T(8,128)(2,1)S(1)}, bf16[128,5632]{1,0:T(8,128)(2,1)S(1)}, u32[]{:S(2)}, u32[]{:S(2)}) collective-permute-start(bf16[128,5632]{1,0:T(8,128)(2,1)S(1)} %constant_dynamic-update-slice_fusion.4.refs_0_.refs_16_), channel_id=1, source_target_pairs={{0,16},{16,0},{1,17},{17,1},{2,18},{18,2},{3,19},{19,3},{4,20},{20... | collective-permute-start | bytes 4325384 | tf_op jit(solution)/shard_map/ppermute | solution.py:29
  105.0 33.5 %collective-permute-start.23 = (bf16[128,5632]{1,0:T(8,128)(2,1)S(1)}, bf16[128,5632]{1,0:T(8,128)(2,1)}, u32[]{:S(2)}, u32[]{:S(2)}) collective-permute-start(bf16[128,5632]{1,0:T(8,128)(2,1)S(1)} %collective-permute-done.12.refs_4_.refs_20_), channel_id=1, source_target_pairs={{0,2},{2,0},{4,6},{6,4},{8,10},{10,8},{12,14},{14,12},{1,3},{3,1},... | collective-permute-start | bytes 4325384 | tf_op jit(solution)/shard_map/ppermute | solution.py:73
  105.6 20.0 %collective-permute-start.19 = (bf16[128,3072]{1,0:T(8,128)(2,1)S(1)}, bf16[128,3072]{1,0:T(8,128)(2,1)S(1)}, u32[]{:S(2)}, u32[]{:S(2)}) collective-permute-start(bf16[128,3072]{1,0:T(8,128)(2,1)S(1)} %pad_maximum_fusion.3.refs_2_), channel_id=1, source_target_pairs={{0,1},{1,0},{2,3},{3,2},{4,5},{5,4},{6,7},{7,6},{8,9},{9,8},{10,11... | collective-permute-start | bytes 2359304 | tf_op jit(solution)/shard_map/ppermute | solution.py:33
  105.6 34.0 %collective-permute-start.15 = (bf16[128,4096]{1,0:T(8,128)(2,1)S(1)}, bf16[128,4096]{1,0:T(8,128)(2,1)}, u32[]{:S(2)}, u32[]{:S(2)}) collective-permute-start(bf16[128,4096]{1,0:T(8,128)(2,1)S(1)} %slice.296), channel_id=1, source_target_pairs={{0,4},{2,6},{4,8},{6,10},{8,12},{10,14},{12,0},{14,2},{1,5},{3,7},... | collective-permute-start | bytes 3145736 | tf_op jit(solution)/shard_map/ppermute | solution.py:76
  108.1 33.8 %collective-permute-start.28 = (bf16[128,5632]{1,0:T(8,128)(2,1)S(1)}, bf16[128,5632]{1,0:T(8,128)(2,1)S(1)}, u32[]{:S(2)}, u32[]{:S(2)}) collective-permute-start(bf16[128,5632]{1,0:T(8,128)(2,1)S(1)} %collective-permute-done.8.refs_1_.refs_17_), channel_id=1, source_target_pairs={{0,16},{16,0},{1,17},{17,1},{2,18},{18,2},{3,19},{19,3},{4,20},{20... | collective-permute-start | bytes 4325384 | tf_op jit(solution)/shard_map/ppermute | solution.py:29
  108.2 33.7 %collective-permute-start.29 = (bf16[128,5632]{1,0:T(8,128)(2,1)S(1)}, bf16[128,5632]{1,0:T(8,128)(2,1)S(1)}, u32[]{:S(2)}, u32[]{:S(2)}) collective-permute-start(bf16[128,5632]{1,0:T(8,128)(2,1)S(1)} %collective-permute-done.7.refs_2_.refs_18_), channel_id=1, source_target_pairs={{0,16},{16,0},{1,17},{17,1},{2,18},{18,2},{3,19},{19,3},{4,20},{20... | collective-permute-start | bytes 4325384 | tf_op jit(solution)/shard_map/ppermute | solution.py:29
  125.6 18.8 %collective-permute-start.30 = (bf16[128,5632]{1,0:T(8,128)(2,1)S(1)}, bf16[128,5632]{1,0:T(8,128)(2,1)S(1)}, u32[]{:S(2)}, u32[]{:S(2)}) collective-permute-start(bf16[128,5632]{1,0:T(8,128)(2,1)S(1)} %collective-permute-done.13.refs_3_.refs_19_), channel_id=1, source_target_pairs={{0,16},{16,0},{1,17},{17,1},{2,18},{18,2},{3,19},{19,3},{4,20},{20... | collective-permute-start | bytes 4325384 | tf_op jit(solution)/shard_map/ppermute | solution.py:29
  141.2 25.5 %collective-permute-start.26 = (bf16[128,4096]{1,0:T(8,128)(2,1)}, bf16[128,4096]{1,0:T(8,128)(2,1)}, u32[]{:S(2)}, u32[]{:S(2)}) collective-permute-start(bf16[128,4096]{1,0:T(8,128)(2,1)} %collective-permute-done.15.refs_6_.refs_22_), channel_id=1, source_target_pairs={{0,2},{2,0},{4,6},{6,4},{8,10},{10,8},{12,14},{14,12},{1,3},{3,1},... | collective-permute-start | bytes 3145736 | tf_op jit(solution)/shard_map/ppermute | solution.py:73
  144.0 22.6 %collective-permute-start.24 = (bf16[128,3072]{1,0:T(8,128)(2,1)}, bf16[128,3072]{1,0:T(8,128)(2,1)}, u32[]{:S(2)}, u32[]{:S(2)}) collective-permute-start(bf16[128,3072]{1,0:T(8,128)(2,1)} %pad_maximum_fusion.4.refs_3_), channel_id=1, source_target_pairs={{0,16},{16,0},{1,17},{17,1},{2,18},{18,2},{3,19},{19,3},{4,20},{20... | collective-permute-start | bytes 2359304 | tf_op jit(solution)/shard_map/ppermute | solution.py:29
  144.4 24.3 %collective-permute-start.31 = (bf16[128,5632]{1,0:T(8,128)(2,1)S(1)}, bf16[128,5632]{1,0:T(8,128)(2,1)}, u32[]{:S(2)}, u32[]{:S(2)}) collective-permute-start(bf16[128,5632]{1,0:T(8,128)(2,1)S(1)} %collective-permute-done.12.refs_4_.refs_20_), channel_id=1, source_target_pairs={{0,16},{16,0},{1,17},{17,1},{2,18},{18,2},{3,19},{19,3},{4,20},{20... | collective-permute-start | bytes 4325384 | tf_op jit(solution)/shard_map/ppermute | solution.py:29
  145.5 23.7 %collective-permute-start.32 = (bf16[128,5632]{1,0:T(8,128)(2,1)}, bf16[128,5632]{1,0:T(8,128)(2,1)}, u32[]{:S(2)}, u32[]{:S(2)}) collective-permute-start(bf16[128,5632]{1,0:T(8,128)(2,1)} %collective-permute-done.23.refs_5_.refs_21_), channel_id=1, source_target_pairs={{0,16},{16,0},{1,17},{17,1},{2,18},{18,2},{3,19},{19,3},{4,20},{20... | collective-permute-start | bytes 4325384 | tf_op jit(solution)/shard_map/ppermute | solution.py:29
  145.8 23.2 %collective-permute-start.33 = (bf16[128,4096]{1,0:T(8,128)(2,1)}, bf16[128,4096]{1,0:T(8,128)(2,1)}, u32[]{:S(2)}, u32[]{:S(2)}) collective-permute-start(bf16[128,4096]{1,0:T(8,128)(2,1)} %collective-permute-done.15.refs_6_.refs_22_), channel_id=1, source_target_pairs={{0,16},{16,0},{1,17},{17,1},{2,18},{18,2},{3,19},{19,3},{4,20},{20... | collective-permute-start | bytes 3145736 | tf_op jit(solution)/shard_map/ppermute | solution.py:29
  166.7 33.0 %collective-permute-start.37 = (bf16[128,3072]{1,0:T(8,128)(2,1)}, bf16[128,3072]{1,0:T(8,128)(2,1)}, u32[]{:S(2)}, u32[]{:S(2)}) collective-permute-start(bf16[128,3072]{1,0:T(8,128)(2,1)} %pad_maximum_fusion.4.refs_3_), channel_id=1, source_target_pairs={{0,1},{1,0},{2,3},{3,2},{4,5},{5,4},{6,7},{7,6},{8,9},{9,8},{10,11... | collective-permute-start | bytes 2359304 | tf_op jit(solution)/shard_map/ppermute | solution.py:33
  168.7 41.6 %collective-permute-start.38 = (bf16[128,3072]{1,0:T(8,128)(2,1)}, bf16[128,3072]{1,0:T(8,128)(2,1)S(1)}, u32[]{:S(2)}, u32[]{:S(2)}) collective-permute-start(bf16[128,3072]{1,0:T(8,128)(2,1)} %copy-done.30), channel_id=1, source_target_pairs={{0,16},{16,0},{1,17},{17,1},{2,18},{18,2},{3,19},{19,3},{4,20},{20... | collective-permute-start | bytes 2359304 | tf_op jit(solution)/shard_map/ppermute | solution.py:29
  169.0 41.4 %collective-permute-start.39 = (bf16[128,3072]{1,0:T(8,128)(2,1)}, bf16[128,3072]{1,0:T(8,128)(2,1)S(1)}, u32[]{:S(2)}, u32[]{:S(2)}) collective-permute-start(bf16[128,3072]{1,0:T(8,128)(2,1)} %copy-done.31), channel_id=1, source_target_pairs={{0,16},{16,0},{1,17},{17,1},{2,18},{18,2},{3,19},{19,3},{4,20},{20... | collective-permute-start | bytes 2359304 | tf_op jit(solution)/shard_map/ppermute | solution.py:29
  169.2 41.2 %collective-permute-start.40 = (bf16[128,3072]{1,0:T(8,128)(2,1)}, bf16[128,3072]{1,0:T(8,128)(2,1)S(1)}, u32[]{:S(2)}, u32[]{:S(2)}) collective-permute-start(bf16[128,3072]{1,0:T(8,128)(2,1)} %copy-done.32), channel_id=1, source_target_pairs={{0,16},{16,0},{1,17},{17,1},{2,18},{18,2},{3,19},{19,3},{4,20},{20... | collective-permute-start | bytes 2359304 | tf_op jit(solution)/shard_map/ppermute | solution.py:29
  199.6 10.8 %collective-permute-start.41 = (bf16[128,3072]{1,0:T(8,128)(2,1)}, bf16[128,3072]{1,0:T(8,128)(2,1)S(1)}, u32[]{:S(2)}, u32[]{:S(2)}) collective-permute-start(bf16[128,3072]{1,0:T(8,128)(2,1)} %collective-permute-done.37.refs_7_), channel_id=1, source_target_pairs={{0,16},{16,0},{1,17},{17,1},{2,18},{18,2},{3,19},{19,3},{4,20},{20... | collective-permute-start | bytes 2359304 | tf_op jit(solution)/shard_map/ppermute | solution.py:29
  199.8 8.9 %collective-permute-start.35 = (bf16[128,1024]{1,0:T(8,128)(2,1)}, bf16[128,1024]{1,0:T(8,128)(2,1)S(1)}, u32[]{:S(2)}, u32[]{:S(2)}) collective-permute-start(bf16[128,1024]{1,0:T(8,128)(2,1)} %bitcast.111), channel_id=1, source_target_pairs={{0,1},{1,0},{2,3},{3,2},{4,5},{5,4},{6,7},{7,6},{8,9},{9,8},{10,11... | collective-permute-start | bytes 786440 | tf_op jit(solution)/shard_map/ppermute | solution.py:33
  208.7 35.2 %collective-permute-start.44 = (bf16[128,1024]{1,0:T(8,128)(2,1)}, bf16[128,1024]{1,0:T(8,128)(2,1)S(1)}, u32[]{:S(2)}, u32[]{:S(2)}) collective-permute-start(bf16[128,1024]{1,0:T(8,128)(2,1)} %bitcast.94), channel_id=1, source_target_pairs={{0,1},{1,0},{2,3},{3,2},{4,5},{5,4},{6,7},{7,6},{8,9},{9,8},{10,11... | collective-permute-start | bytes 786440 | tf_op jit(solution)/shard_map/ppermute | solution.py:33
  210.3 40.2 %collective-permute-start.36 = (bf16[256,1024]{1,0:T(8,128)(2,1)}, bf16[256,1024]{1,0:T(8,128)(2,1)S(1)}, u32[]{:S(2)}, u32[]{:S(2)}) collective-permute-start(bf16[256,1024]{1,0:T(8,128)(2,1)} %bitcast.107), channel_id=1, source_target_pairs={{0,16},{16,0},{1,17},{17,1},{2,18},{18,2},{3,19},{19,3},{4,20},{20... | collective-permute-start | bytes 1572872 | tf_op jit(solution)/shard_map/ppermute | solution.py:29
  243.8 8.9 %collective-permute-start.45 = (bf16[128,1024]{1,0:T(8,128)(2,1)}, bf16[128,1024]{1,0:T(8,128)(2,1)}, u32[]{:S(2)}, u32[]{:S(2)}) collective-permute-start(bf16[128,1024]{1,0:T(8,128)(2,1)} %get-tuple-element.132), channel_id=1, source_target_pairs={{0,1},{1,0},{2,3},{3,2},{4,5},{5,4},{6,7},{7,6},{8,9},{9,8},{10,11... | collective-permute-start | bytes 786440 | tf_op jit(solution)/shard_map/ppermute | solution.py:33
  245.5 7.3 %collective-permute-start.46 = (bf16[4,128,1024]{2,1,0:T(8,128)(2,1)S(1)}, bf16[4,128,1024]{2,1,0:T(8,128)(2,1)}, u32[]{:S(2)}, u32[]{:S(2)}) collective-permute-start(bf16[4,128,1024]{2,1,0:T(8,128)(2,1)S(1)} %pad_maximum_fusion.1.states_own), channel_id=1, source_target_pairs={{0,16},{16,0},{1,17},{17,1},{2,18},{18,2},{3,19},{19,3},{4,20},{20... | collective-permute-start | bytes 3145736 | tf_op jit(solution)/shard_map/ppermute | solution.py:29
  246.0 4.3 collective-permute-start.42
  246.1 6.7 %collective-permute-start.47 = (bf16[2,128,1024]{2,1,0:T(8,128)(2,1)S(1)}, bf16[2,128,1024]{2,1,0:T(8,128)(2,1)}, u32[]{:S(2)}, u32[]{:S(2)}) collective-permute-start(bf16[2,128,1024]{2,1,0:T(8,128)(2,1)S(1)} %copy-done.20), channel_id=1, source_target_pairs={{0,16},{16,0},{1,17},{17,1},{2,18},{18,2},{3,19},{19,3},{4,20},{20... | collective-permute-start | bytes 1572872 | tf_op jit(solution)/shard_map/ppermute | solution.py:29
  252.8 31.7 %collective-permute-start.48 = (bf16[2,128,1536]{2,1,0:T(8,128)(2,1)S(1)}, bf16[2,128,1536]{2,1,0:T(8,128)(2,1)S(1)}, u32[]{:S(2)}, u32[]{:S(2)}) collective-permute-start(bf16[2,128,1536]{2,1,0:T(8,128)(2,1)S(1)} %pad_maximum_fusion.5), channel_id=1, source_target_pairs={{0,1},{1,0},{2,3},{3,2},{4,5},{5,4},{6,7},{7,6},{8,9},{9,8},{10,11... | collective-permute-start | bytes 2359304 | tf_op jit(solution)/shard_map/ppermute | solution.py:33
  253.3 31.2 %collective-permute-start.49 = (bf16[2,128,1152]{2,1,0:T(8,128)(2,1)S(1)}, bf16[2,128,1152]{2,1,0:T(8,128)(2,1)S(1)}, u32[]{:S(2)}, u32[]{:S(2)}) collective-permute-start(bf16[2,128,1152]{2,1,0:T(8,128)(2,1)S(1)} %pad_maximum_fusion.6), channel_id=1, source_target_pairs={{0,1},{1,0},{2,3},{3,2},{4,5},{5,4},{6,7},{7,6},{8,9},{9,8},{10,11... | collective-permute-start | bytes 1769480 | tf_op jit(solution)/shard_map/ppermute | solution.py:33
  284.5 3.7 collective-permute-start.50
  284.6 3.6 collective-permute-start.51
  304.4 14.3 %collective-permute-start.52 = (bf16[256,768]{1,0:T(8,128)(2,1)}, bf16[256,768]{1,0:T(8,128)(2,1)S(1)}, u32[]{:S(2)}, u32[]{:S(2)}) collective-permute-start(bf16[256,768]{1,0:T(8,128)(2,1)} %get-tuple-element.152), channel_id=1, source_target_pairs={{0,4},{2,6},{4,8},{6,10},{8,12},{10,14},{12,0},{14,2},{1,5},{3,7},... | collective-permute-start | bytes 1179656 | tf_op jit(solution)/shard_map/ppermute | solution.py:76
  304.7 32.5 %collective-permute-start.58 = (bf16[128,5120]{1,0:T(8,128)(2,1)}, bf16[128,5120]{1,0:T(8,128)(2,1)}, u32[]{:S(2)}, u32[]{:S(2)}) collective-permute-start(bf16[128,5120]{1,0:T(8,128)(2,1)} %get-tuple-element.159), channel_id=1, source_target_pairs={{0,2},{2,0},{4,6},{6,4},{8,10},{10,8},{12,14},{14,12},{1,3},{3,1},... | collective-permute-start | bytes 3932168 | tf_op jit(solution)/shard_map/ppermute | solution.py:73
  309.5 42.5 %collective-permute-start.57 = (bf16[256,768]{1,0:T(8,128)(2,1)}, bf16[256,768]{1,0:T(8,128)(2,1)}, u32[]{:S(2)}, u32[]{:S(2)}) collective-permute-start(bf16[256,768]{1,0:T(8,128)(2,1)} %get-tuple-element.157), channel_id=1, source_target_pairs={{4,0},{6,2},{8,4},{10,6},{12,8},{14,10},{0,12},{2,14},{5,1},{7,3},... | collective-permute-start | bytes 1179656 | tf_op jit(solution)/shard_map/ppermute | solution.py:79
  328.5 3.4 collective-permute-start.55
  331.4 9.1 %collective-permute-start.53 = (f32[16,16,1024]{2,1,0:T(8,128)}, f32[16,16,1024]{2,1,0:T(8,128)S(1)}, u32[]{:S(2)}, u32[]{:S(2)}) collective-permute-start(f32[16,16,1024]{2,1,0:T(8,128)} %bitcast.83), channel_id=1, source_target_pairs={{0,16},{16,0},{1,17},{17,1},{2,18},{18,2},{3,19},{19,3},{4,20},{20... | collective-permute-start | bytes 3145736 | tf_op jit(solution)/shard_map/ppermute | solution.py:29
  331.9 4.4 collective-permute-start.56
  337.2 14.1 %collective-permute-start.59 = (bf16[256,768]{1,0:T(8,128)(2,1)}, bf16[256,768]{1,0:T(8,128)(2,1)S(1)}, u32[]{:S(2)}, u32[]{:S(2)}) collective-permute-start(bf16[256,768]{1,0:T(8,128)(2,1)} %add_convert_fusion.3), channel_id=1, source_target_pairs={{0,4},{2,6},{4,8},{6,10},{8,12},{10,14},{12,0},{14,2},{1,5},{3,7},... | collective-permute-start | bytes 1179656 | tf_op jit(solution)/shard_map/ppermute | solution.py:76
  339.4 30.2 %collective-permute-start.60 = (bf16[128,5120]{1,0:T(8,128)(2,1)S(1)}, bf16[128,5120]{1,0:T(8,128)(2,1)S(1)}, u32[]{:S(2)}, u32[]{:S(2)}) collective-permute-start(bf16[128,5120]{1,0:T(8,128)(2,1)S(1)} %copy-done.70), channel_id=1, source_target_pairs={{0,2},{2,0},{4,6},{6,4},{8,10},{10,8},{12,14},{14,12},{1,3},{3,1},... | collective-permute-start | bytes 3932168 | tf_op jit(solution)/shard_map/ppermute | solution.py:73
  340.0 37.8 %collective-permute-start.61 = (bf16[128,5120]{1,0:T(8,128)(2,1)S(1)}, bf16[128,5120]{1,0:T(8,128)(2,1)S(1)}, u32[]{:S(2)}, u32[]{:S(2)}) collective-permute-start(bf16[128,5120]{1,0:T(8,128)(2,1)S(1)} %add_convert_fusion.2), channel_id=1, source_target_pairs={{0,4},{2,6},{4,8},{6,10},{8,12},{10,14},{12,0},{14,2},{1,5},{3,7},... | collective-permute-start | bytes 3932168 | tf_op jit(solution)/shard_map/ppermute | solution.py:76
  341.5 37.5 %collective-permute-start.54 = (f32[32,16,1024]{2,1,0:T(8,128)S(1)}, f32[32,16,1024]{2,1,0:T(8,128)S(1)}, u32[]{:S(2)}, u32[]{:S(2)}) collective-permute-start(f32[32,16,1024]{2,1,0:T(8,128)S(1)} %pad_maximum_fusion), channel_id=1, source_target_pairs={{0,1},{17,16},{2,3},{19,18},{4,5},{21,20},{6,7},{23,22},{8,9},{25,... | collective-permute-start | bytes 6291464 | tf_op jit(solution)/shard_map/ppermute | solution.py:1092
  351.3 71.3 %collective-permute-start.67 = (bf16[128,4096]{1,0:T(8,128)(2,1)S(1)}, bf16[128,4096]{1,0:T(8,128)(2,1)S(1)}, u32[]{:S(2)}, u32[]{:S(2)}) collective-permute-start(bf16[128,4096]{1,0:T(8,128)(2,1)S(1)} %copy-done.28), channel_id=1, source_target_pairs={{0,0},{1,16},{16,1},{17,17},{2,2},{3,18},{18,3},{19,19},{4,4},{5,2... | collective-permute-start | bytes 3145736 | tf_op jit(solution)/shard_map/ppermute | solution.py:37
  378.9 9.2 %collective-permute-start.62 = (bf16[128,1024]{1,0:T(8,128)(2,1)S(1)}, bf16[128,1024]{1,0:T(8,128)(2,1)S(1)}, u32[]{:S(2)}, u32[]{:S(2)}) collective-permute-start(bf16[128,1024]{1,0:T(8,128)(2,1)S(1)} %pad_maximum_fusion.7), channel_id=1, source_target_pairs={{0,2},{2,0},{4,6},{6,4},{8,10},{10,8},{12,14},{14,12},{1,3},{3,1},... | collective-permute-start | bytes 786440 | tf_op jit(solution)/shard_map/ppermute | solution.py:73
  380.3 39.9 %collective-permute-start.65 = (bf16[128,5120]{1,0:T(8,128)(2,1)S(1)}, bf16[128,5120]{1,0:T(8,128)(2,1)S(1)}, u32[]{:S(2)}, u32[]{:S(2)}) collective-permute-start(bf16[128,5120]{1,0:T(8,128)(2,1)S(1)} %copy-done.69), channel_id=1, source_target_pairs={{0,2},{2,0},{4,6},{6,4},{8,10},{10,8},{12,14},{14,12},{1,3},{3,1},... | collective-permute-start | bytes 3932168 | tf_op jit(solution)/shard_map/ppermute | solution.py:73
  381.0 39.2 %collective-permute-start.66 = (bf16[128,5120]{1,0:T(8,128)(2,1)S(1)}, bf16[128,5120]{1,0:T(8,128)(2,1)S(1)}, u32[]{:S(2)}, u32[]{:S(2)}) collective-permute-start(bf16[128,5120]{1,0:T(8,128)(2,1)S(1)} %add_convert_fusion.1), channel_id=1, source_target_pairs={{0,4},{2,6},{4,8},{6,10},{8,12},{10,14},{12,0},{14,2},{1,5},{3,7},... | collective-permute-start | bytes 3932168 | tf_op jit(solution)/shard_map/ppermute | solution.py:76
  388.3 29.4 %collective-permute-start.63 = (bf16[128,640]{1,0:T(8,128)(2,1)S(1)}, bf16[128,640]{1,0:T(8,128)(2,1)}, u32[]{:S(2)}, u32[]{:S(2)}) collective-permute-start(bf16[128,640]{1,0:T(8,128)(2,1)S(1)} %pad_maximum_fusion.9), channel_id=1, source_target_pairs={{0,4},{2,6},{4,8},{6,10},{8,12},{10,14},{12,0},{14,2},{1,5},{3,7},... | collective-permute-start | bytes 491528 | tf_op jit(solution)/shard_map/ppermute | solution.py:76
  392.4 26.8 %collective-permute-start.64 = (bf16[128,640]{1,0:T(8,128)(2,1)S(1)}, bf16[128,640]{1,0:T(8,128)(2,1)S(1)}, u32[]{:S(2)}, u32[]{:S(2)}) collective-permute-start(bf16[128,640]{1,0:T(8,128)(2,1)S(1)} %pad_maximum_fusion.9), channel_id=1, source_target_pairs={{4,0},{6,2},{8,4},{10,6},{12,8},{14,10},{0,12},{2,14},{5,1},{7,3},... | collective-permute-start | bytes 491528 | tf_op jit(solution)/shard_map/ppermute | solution.py:79
  422.6 8.6 %collective-permute-start.68 = (bf16[128,640]{1,0:T(8,128)(2,1)}, bf16[128,640]{1,0:T(8,128)(2,1)}, u32[]{:S(2)}, u32[]{:S(2)}) collective-permute-start(bf16[128,640]{1,0:T(8,128)(2,1)} %collective-permute-done.63), channel_id=1, source_target_pairs={{0,4},{2,6},{4,8},{6,10},{8,12},{10,14},{12,0},{14,2},{1,5},{3,7},... | collective-permute-start | bytes 491528 | tf_op jit(solution)/shard_map/ppermute | solution.py:76
  425.2 12.9 %collective-permute-start.72 = (bf16[128,1024]{1,0:T(8,128)(2,1)}, bf16[128,1024]{1,0:T(8,128)(2,1)S(1)}, u32[]{:S(2)}, u32[]{:S(2)}) collective-permute-start(bf16[128,1024]{1,0:T(8,128)(2,1)} %slice.260), channel_id=1, source_target_pairs={{0,2},{2,0},{4,6},{6,4},{8,10},{10,8},{12,14},{14,12},{1,3},{3,1},... | collective-permute-start | bytes 786440 | tf_op jit(solution)/shard_map/ppermute | solution.py:73
  426.8 11.3 %collective-permute-start.73 = (bf16[128,1024]{1,0:T(8,128)(2,1)}, bf16[128,1024]{1,0:T(8,128)(2,1)S(1)}, u32[]{:S(2)}, u32[]{:S(2)}) collective-permute-start(bf16[128,1024]{1,0:T(8,128)(2,1)} %slice.318), channel_id=1, source_target_pairs={{0,4},{2,6},{4,8},{6,10},{8,12},{10,14},{12,0},{14,2},{1,5},{3,7},... | collective-permute-start | bytes 786440 | tf_op jit(solution)/shard_map/ppermute | solution.py:76
  427.4 27.9 %collective-permute-start.70 = (bf16[128,4096]{1,0:T(8,128)(2,1)}, bf16[128,4096]{1,0:T(8,128)(2,1)}, u32[]{:S(2)}, u32[]{:S(2)}) collective-permute-start(bf16[128,4096]{1,0:T(8,128)(2,1)} %slice.258), channel_id=1, source_target_pairs={{0,2},{1,18},{16,3},{17,19},{2,0},{3,16},{18,1},{19,17},{4,6},{5,2... | collective-permute-start | bytes 3145736 | tf_op jit(solution)/shard_map/ppermute | solution.py:1109
  427.9 30.9 %collective-permute-start.71 = (bf16[128,4096]{1,0:T(8,128)(2,1)}, bf16[128,4096]{1,0:T(8,128)(2,1)}, u32[]{:S(2)}, u32[]{:S(2)}) collective-permute-start(bf16[128,4096]{1,0:T(8,128)(2,1)} %slice.317), channel_id=1, source_target_pairs={{0,4},{1,20},{16,5},{17,21},{2,6},{3,22},{18,7},{19,23},{4,8},{5,2... | collective-permute-start | bytes 3145736 | tf_op jit(solution)/shard_map/ppermute | solution.py:1109
  (82 other events, 1233.9 us)

commit v11 on v10

--- a/solution.py
+++ b/solution.py
@@ -953,31 +953,38 @@
             if k < ring.outer - 1:
                 jobs.append((onward, held[:, :both] if k == ring.outer - 2 else held))
             if k == 0:
-                jobs += [(across_chips, vocab_own), (across_chips, vector_own)]
-            results = flow.step(*jobs, also=ready if k == 1 else ())
+                jobs.append((across_chips, vocab_own))
+            if k == 1:
+                jobs.append((across_chips, vector_own))
+            results = flow.step(*jobs)
             far.append(results[0])
             small_chip.append(results[1])
             if k == 0:
-                vocab_chip, vector_pair = results[3:]
-                vector_pair = jnp.concatenate([vector_own, vector_pair], axis=1)
+                vocab_chip = results[3]
+            if k == 1:
+                vector_pair = jnp.concatenate([vector_own, results[3]], axis=1)
             if k < ring.outer - 1:
                 small_own.append(jnp.concatenate([held[:, both:], far[k][:, both:]], axis=1))
                 held = results[2]
-        for a, b in zip(near, far):
-            near_core.append(across_cores(a))
+        for k, (a, b) in enumerate(zip(near, far)):
+            near_core.append(across_cores(a if k else tie(a, near[1], *ready)))
             far_core.append(across_cores(b))
-        small_core = [across_cores(a) for a in small_own]
         b_last, vocab_last, chip_last, vector_last = lax.optimization_barrier(
             (b_own, vocab_own, vocab_chip, vector_pair, held)
         )[:4]
         b_other = across_cores(b_last)
         vocab = [vocab_own, vocab_chip, across_cores(vocab_last), across_cores(chip_last)]
         vector_core = across_cores(vector_last)
+        for k in range(ring.outer):
+            places += [ring.back(k) * 2 + ring.x, ring.back(k) * 2 + 1 - ring.x]
+        places = jnp.stack([s, y] + places).astype(jnp.int32)
+        vectors = jnp.concatenate([vector_pair, vector_core], axis=1)
+        vectors = jnp.pad(vectors, ((0, 3), (0, 0)))
+        small_core = [across_cores(a) for a in small_own[:-1]]
+        small_core.append(across_cores(tie(small_own[-1], vectors, places)))
         in_own = [a for pair in zip(near, far) for a in pair]
         in_other = [a for pair in zip(near_core, far_core) for a in pair]
         rec_own, rec_other, rec_column = in_own, in_other, wide_half
-        for k in range(ring.outer):
-            places += [ring.back(k) * 2 + ring.x, ring.back(k) * 2 + 1 - ring.x]
     else:
         vocab_chip = across_chips(vocab_own)
         small, in_block, rec_block = [
@@ -994,9 +1001,9 @@
         vector_pair = across_chips(vector_own)
         vector_pair = jnp.concatenate([vector_own, vector_pair], axis=1)
         vector_core = across_cores(vector_pair)
-    vectors = jnp.concatenate([vector_pair, vector_core], axis=1)
-    vectors = jnp.pad(vectors, ((0, 3), (0, 0)))
-    places = jnp.stack([s, y] + places).astype(jnp.int32)
+        vectors = jnp.concatenate([vector_pair, vector_core], axis=1)
+        vectors = jnp.pad(vectors, ((0, 3), (0, 0)))
+        places = jnp.stack([s, y] + places).astype(jnp.int32)
     z, x = ring.z, ring.x
     if ring.short:
         steps_back = [ring.back(k) for k in range(1, 5)]

time: 467 us -> 460 us (0.985)
  waiting for transfers between devices: 209 us -> 196 us
    ppermute x11, waiting for transfers between devices: 31.2 us -> 21.2 us  [across_chips(): return lax.ppermute(array, 'mp', core_swap)]
    ppermute x11, waiting for transfers between devices: 101 us -> 92.6 us  [across(): return lax.ppermute(array, 'dp', self.pair)]
    ppermute x11, waiting for transfers between devices: 48.2 us -> 54.8 us  [onward(): return lax.ppermute(array, 'dp', self.ring)]
    unnamed x158 -> x138, local copies, waits for them, and re-layouts: 16.1 us -> 15.9 us
  transfers between devices with their start and end apart: 74 -> 74, of which waited for: 28 -> 29; matrix products, arithmetic and copies ran while one was open for 10% -> 13% of each run, Pallas kernels for 21% -> 22%
where the time goes in v11:
time: 460 us; the launch traced here: 459 us
  waiting for transfers between devices  196 us (43%)
  Pallas kernels  114 us (25%)
  starting transfers between devices  68 us (15%)
  local copies, waits for them, and re-layouts  54.5 us (12%)
  other arithmetic  24.5 us (5%)
    ppermute x11, waiting for transfers between devices, across(): return lax.ppermute(array, 'dp', self.pair)  92.6 us
    ppermute x11, waiting for transfers between devices, onward(): return lax.ppermute(array, 'dp', self.ring)  54.8 us
    pallas_call x1, Pallas kernels, run_attend(): pl.pallas_call(functools.partial(attend_kernel, count), out_shape=(jax.Sh...  31.2 us
    pallas_call x1, Pallas kernels, run_forward(): pl.pallas_call(functools.partial(forward_kernel, count, column), out_shap...  30 us
    pallas_call x1, Pallas kernels, run_backward(): pl.pallas_call(functools.partial(backward_kernel, count, column), out_sha...  28.9 us
    ppermute x11, waiting for transfers between devices, across_chips(): return lax.ppermute(array, 'mp', core_swap)  21.2 us
    ppermute x2, waiting for transfers between devices, cornered(): return lambda array: lax.ppermute(array, ('section', 'dp', 'mp'), pairs)  19.4 us
    unnamed x138, local copies, waits for them, and re-layouts  15.9 us
  transfers between devices with their start and end apart: 74, of which 29 were waited for; matrix products, arithmetic and copies ran while one was open for 13% of the time, Pallas kernels for 22%

profile of v11, /device:TPU:0, one launch (start us, length us, event | category | flops | bytes accessed | tf_op | source)
XLA Modules:
  0.0 458.8 jit_solution(7159320264152221750)
XLA Ops:
  0.7 1.3 copy.65
  7.1 2.9 collective-permute-start.3
  10.1 1.5 collective-permute-start
  11.6 1.5 collective-permute-start.1
  13.0 1.6 collective-permute-start.2
  14.6 1.2 collective-permute-start.4
  16.9 2.5 collective-permute-done.3
  22.4 2.8 collective-permute-done.2
  25.9 3.1 collective-permute-start.17
  29.7 2.7 collective-permute-start.7
  33.9 1.2 dynamic_slice.25
  35.2 1.3 pad.26
  38.0 20.8 %collective-permute-done.6.refs_1_.refs_17_ = bf16[128,5632]{1,0:T(8,128)(2,1)} collective-permute-done((bf16[128,5632]{1,0:T(8,128)(2,1)S(1)}, bf16[128,5632]{1,0:T(8,128)(2,1)}, u32[]{:S(2)}, u32[]{:S(2)}) %collective-permute-start.6) | collective-permute-done | bytes 1441824 | tf_op jit(solution)/shard_map/ppermute | solution.py:73
  61.6 1.6 collective-permute-start.11
  63.4 1.6 collective-permute-start.10
  65.3 3.0 collective-permute-start.12
  70.1 25.6 %collective-permute-done.11.refs_3_.refs_19_ = bf16[128,5632]{1,0:T(8,128)(2,1)} collective-permute-done((bf16[128,5632]{1,0:T(8,128)(2,1)}, bf16[128,5632]{1,0:T(8,128)(2,1)}, u32[]{:S(2)}, u32[]{:S(2)}) %collective-permute-start.11) | collective-permute-done | bytes 1441824 | tf_op jit(solution)/shard_map/ppermute | solution.py:73
  98.3 1.3 collective-permute-done.10.refs_4_.refs_20_
  99.8 1.3 collective-permute-start.23
  101.7 1.4 collective-permute-start.19
  105.6 1.3 broadcast_in_dim.23.noise
  109.6 10.7 %collective-permute-done.19.refs_6_ = bf16[128,3072]{1,0:T(8,128)(2,1)S(1)} collective-permute-done((bf16[128,3072]{1,0:T(8,128)(2,1)}, bf16[128,3072]{1,0:T(8,128)(2,1)S(1)}, u32[]{:S(2)}, u32[]{:S(2)}) %collective-permute-start.19) | collective-permute-done | bytes 786464 | tf_op jit(solution)/shard_map/ppermute | solution.py:33
  120.3 7.3 %collective-permute-done.13.refs_6_.refs_22_ = bf16[128,4096]{1,0:T(8,128)(2,1)} collective-permute-done((bf16[128,4096]{1,0:T(8,128)(2,1)S(1)}, bf16[128,4096]{1,0:T(8,128)(2,1)}, u32[]{:S(2)}, u32[]{:S(2)}) %collective-permute-start.13) | collective-permute-done | bytes 1048608 | tf_op jit(solution)/shard_map/ppermute | solution.py:76
  127.6 5.8 %collective-permute-done.23.refs_5_.refs_21_ = bf16[128,5632]{1,0:T(8,128)(2,1)S(1)} collective-permute-done((bf16[128,5632]{1,0:T(8,128)(2,1)S(1)}, bf16[128,5632]{1,0:T(8,128)(2,1)S(1)}, u32[]{:S(2)}, u32[]{:S(2)}) %collective-permute-start.23) | collective-permute-done | bytes 1441824 | tf_op jit(solution)/shard_map/ppermute | solution.py:73
  140.6 1.3 select_maximum_fusion.vectors
  142.9 18.6 %collective-permute-done.26.refs_7_.refs_23_ = bf16[128,4096]{1,0:T(8,128)(2,1)} collective-permute-done((bf16[128,4096]{1,0:T(8,128)(2,1)}, bf16[128,4096]{1,0:T(8,128)(2,1)}, u32[]{:S(2)}, u32[]{:S(2)}) %collective-permute-start.26) | collective-permute-done | bytes 1048608 | tf_op jit(solution)/shard_map/ppermute | solution.py:73
  163.2 1.3 collective-permute-done.34.refs_15_.refs_31_
  164.5 30.0 %recur_forward.1 = (bf16[16,8,1024]{2,1,0:T(8,128)(2,1)}, bf16[16,8,1024]{2,1,0:T(8,128)(2,1)}, bf16[16,16,1024]{2,1,0:T(8,128)(2,1)}, f32[16,16,4096]{2,1,0:T(8,128)}, f32[16,16,1024]{2,1,0:T(8,128)}) custom-call(s32[10]{0:T(128)} %stack.116.places, bf16[256,1024]{1,0:T(8,128)(2,1)} %bitcast.87, f32[1,2048]{1,0:T(1,128)} %copy-done.52, ...), custom_call_target="tpu_custom_call" | custom-call | tf_op jit(solution)/shard_map/recur_forward/pallas_call | solution.py:196
  195.6 8.0 %collective-permute-done.35.taken = bf16[128,1024]{1,0:T(8,128)(2,1)S(1)} collective-permute-done((bf16[128,1024]{1,0:T(8,128)(2,1)}, bf16[128,1024]{1,0:T(8,128)(2,1)S(1)}, u32[]{:S(2)}, u32[]{:S(2)}) %collective-permute-start.35) | collective-permute-done | bytes 262176 | tf_op jit(solution)/shard_map/ppermute | solution.py:33
  206.7 31.2 %attend.1 = (f32[128,1024]{1,0:T(8,128)}, bf16[128,1024]{1,0:T(8,128)(2,1)}, bf16[128,1536]{1,0:T(8,128)(2,1)}, bf16[128,1536]{1,0:T(8,128)(2,1)}, bf16[2,128,15...) custom-call(s32[10]{0:T(128)} %stack.116.places, ...), custom_call_target="tpu_custom_call" | custom-call | tf_op jit(solution)/shard_map/attend/pallas_call | solution.py:696
  237.9 1.4 collective-permute-start.45
  244.0 1.2 collective-permute-done.42.pack_core
  245.4 1.4 collective-permute-done.45
  246.8 1.4 collective-permute-start.48
  248.9 28.9 %recur_backward.1 = (bf16[16,16,2048]{2,1,0:T(8,128)(2,1)}, bf16[16,16,2048]{2,1,0:T(8,128)(2,1)}) custom-call(s32[10]{0:T(128)} %stack.116.places, f32[16,8,1024]{2,1,0:T(8,128)} %bitcast.102, bf16[16,8,1024]{2,1,0:T(8,128)(2,1)} %bitcast.43.taken, f32[16,16,4096]{2,1,0:T(8,128)} %get-tuple-element.141.gates_in, ...), custom_call_target="tpu_custom_call" | custom-call | tf_op jit(solution)/shard_map/recur_backward/pallas_call | solution.py:324
  280.5 1.7 collective-permute-done.51.far_core
  283.2 15.2 %weight_gradients.1 = (bf16[128,5120]{1,0:T(8,128)(2,1)}, bf16[128,5120]{1,0:T(8,128)(2,1)}, bf16[128,5120]{1,0:T(8,128)(2,1)}, bf16[128,5120]{1,0:T(8,128)(2,1)...) custom-call(s32[13]{0:T(128)} %stack.123.order, ...), custom_call_target="tpu_custom_call" | custom-call | tf_op jit(solution)/shard_map/weight_gradients/pallas_call | solution.py:853
  300.0 2.3 slice.258
  302.3 1.7 slice.260
  304.0 3.7 collective-permute-start.57
  307.7 5.0 %collective-permute-done.52 = bf16[256,768]{1,0:T(8,128)(2,1)S(1)} collective-permute-done((bf16[256,768]{1,0:T(8,128)(2,1)}, bf16[256,768]{1,0:T(8,128)(2,1)S(1)}, u32[]{:S(2)}, u32[]{:S(2)}) %collective-permute-start.52) | collective-permute-done | bytes 393248 | tf_op jit(solution)/shard_map/ppermute | solution.py:76
  313.5 9.0 %input_back.1 = (f32[256,1024]{1,0:T(8,128)}, f32[1,1024]{1,0:T(1,128)}) custom-call(s32[10]{0:T(128)} %stack.116.places, bf16[256,1024]{1,0:T(8,128)(2,1)} %bitcast.91, f32[1,1024]{1,0:T(1,128)} %bitcast.115, bf16[256,2048]{1,0:T(8,128)(2,1)} %bitcast.85, bf16[256,2048]{1,0:T(8,128)(2,1)} %bitcast.99, bf16[128,5632]{1,0:T(8,128)(2,1)} %copy-done.3, ...), custom_call_target="tpu_custom_call" | custom-call | tf_op jit(solution)/shard_map/input_back/pallas_call | solution.py:375
  323.9 1.6 copy.74
  327.0 2.0 add_convert_fusion.3
  329.0 1.4 collective-permute-done.56
  331.5 2.1 add_convert_fusion.2
  333.6 1.3 collective-permute-start.60
  336.2 3.4 collective-permute-start.54
  339.7 5.6 %collective-permute-done.59 = bf16[256,768]{1,0:T(8,128)(2,1)S(1)} collective-permute-done((bf16[256,768]{1,0:T(8,128)(2,1)}, bf16[256,768]{1,0:T(8,128)(2,1)S(1)}, u32[]{:S(2)}, u32[]{:S(2)}) %collective-permute-start.59) | collective-permute-done | bytes 393248 | tf_op jit(solution)/shard_map/ppermute | solution.py:76
  346.1 1.2 fusion.20
  347.4 16.1 %collective-permute-done.60 = bf16[128,5120]{1,0:T(8,128)(2,1)S(1)} collective-permute-done((bf16[128,5120]{1,0:T(8,128)(2,1)S(1)}, bf16[128,5120]{1,0:T(8,128)(2,1)S(1)}, u32[]{:S(2)}, u32[]{:S(2)}) %collective-permute-start.60) | collective-permute-done | bytes 1310752 | tf_op jit(solution)/shard_map/ppermute | solution.py:73
  363.6 8.2 %collective-permute-done.61 = bf16[128,5120]{1,0:T(8,128)(2,1)S(1)} collective-permute-done((bf16[128,5120]{1,0:T(8,128)(2,1)S(1)}, bf16[128,5120]{1,0:T(8,128)(2,1)S(1)}, u32[]{:S(2)}, u32[]{:S(2)}) %collective-permute-start.61) | collective-permute-done | bytes 1310752 | tf_op jit(solution)/shard_map/ppermute | solution.py:76
  372.4 1.9 collective-permute-done.54
  376.3 3.7 collective-permute-start.66
  380.1 1.7 select_bitcast_fusion
  381.8 1.7 collective-permute-done.62
  383.6 3.8 collective-permute-start.63
  388.4 23.8 %collective-permute-done.63 = bf16[128,640]{1,0:T(8,128)(2,1)} collective-permute-done((bf16[128,640]{1,0:T(8,128)(2,1)S(1)}, bf16[128,640]{1,0:T(8,128)(2,1)}, u32[]{:S(2)}, u32[]{:S(2)}) %collective-permute-start.63) | collective-permute-done | bytes 163872 | tf_op jit(solution)/shard_map/ppermute | solution.py:76
  422.4 3.0 collective-permute-start.71
  433.9 15.9 %collective-permute-done.70 = bf16[128,4096]{1,0:T(8,128)(2,1)} collective-permute-done((bf16[128,4096]{1,0:T(8,128)(2,1)}, bf16[128,4096]{1,0:T(8,128)(2,1)}, u32[]{:S(2)}, u32[]{:S(2)}) %collective-permute-start.70) | collective-permute-done | bytes 1048608 | tf_op jit(solution)/shard_map/ppermute | solution.py:1116
  449.8 3.5 collective-permute-done.71
  453.3 2.0 convert_add_fusion
  455.5 1.7 reshape.193
  457.1 1.7 reshape.194
  (354 shorter events, 80.6 us)
Async XLA Ops:
  7.1 12.3 %collective-permute-start.3 = (bf16[128,1536]{1,0:T(8,128)(2,1)}, bf16[128,1536]{1,0:T(8,128)(2,1)S(1)}, u32[]{:S(2)}, u32[]{:S(2)}) collective-permute-start(bf16[128,1536]{1,0:T(8,128)(2,1)} %get-tuple-element.219), channel_id=1, source_target_pairs={{0,2},{2,0},{4,6},{6,4},{8,10},{10,8},{12,14},{14,12},{1,3},{3,1},... | collective-permute-start | bytes 1179656 | tf_op jit(solution)/shard_map/ppermute | solution.py:73
  10.1 10.1 %collective-permute-start = (bf16[128,2048]{1,0:T(8,128)(2,1)S(1)}, bf16[128,2048]{1,0:T(8,128)(2,1)}, u32[]{:S(2)}, u32[]{:S(2)}) collective-permute-start(bf16[128,2048]{1,0:T(8,128)(2,1)S(1)} %bitcast.107), channel_id=1, source_target_pairs={{0,0},{1,16},{16,1},{17,17},{2,2},{3,18},{18,3},{19,19},{4,4},{5,2... | collective-permute-start | bytes 1572872 | tf_op jit(solution)/shard_map/ppermute | solution.py:37
  11.6 9.8 %collective-permute-start.1 = (bf16[128,2048]{1,0:T(8,128)(2,1)S(1)}, bf16[128,2048]{1,0:T(8,128)(2,1)}, u32[]{:S(2)}, u32[]{:S(2)}) collective-permute-start(bf16[128,2048]{1,0:T(8,128)(2,1)S(1)} %bitcast.106), channel_id=1, source_target_pairs={{0,0},{1,16},{16,1},{17,17},{2,2},{3,18},{18,3},{19,19},{4,4},{5,2... | collective-permute-start | bytes 1572872 | tf_op jit(solution)/shard_map/ppermute | solution.py:37
  13.0 12.2 %collective-permute-start.2 = (bf16[128,1536]{1,0:T(8,128)(2,1)}, bf16[128,1536]{1,0:T(8,128)(2,1)S(1)}, u32[]{:S(2)}, u32[]{:S(2)}) collective-permute-start(bf16[128,1536]{1,0:T(8,128)(2,1)} %get-tuple-element.219), channel_id=1, source_target_pairs={{0,4},{2,6},{4,8},{6,10},{8,12},{10,14},{12,0},{14,2},{1,5},{3,7},... | collective-permute-start | bytes 1179656 | tf_op jit(solution)/shard_map/ppermute | solution.py:76
  14.6 10.7 %collective-permute-start.4 = (bf16[1,2048]{1,0:T(2,128)(2,1)S(1)}, bf16[1,2048]{1,0:T(2,128)(2,1)}, u32[]{:S(2)}, u32[]{:S(2)}) collective-permute-start(bf16[1,2048]{1,0:T(2,128)(2,1)S(1)} %bitcast.119), channel_id=1, source_target_pairs={{0,0},{1,16},{16,1},{17,17},{2,2},{3,18},{18,3},{19,19},{4,4},{5,2... | collective-permute-start | bytes 12296 | tf_op jit(solution)/shard_map/ppermute | solution.py:37
  25.3 33.5 %collective-permute-start.6 = (bf16[128,5632]{1,0:T(8,128)(2,1)S(1)}, bf16[128,5632]{1,0:T(8,128)(2,1)}, u32[]{:S(2)}, u32[]{:S(2)}) collective-permute-start(bf16[128,5632]{1,0:T(8,128)(2,1)S(1)} %constant_dynamic-update-slice_fusion.4.refs_0_.refs_16_), channel_id=1, source_target_pairs={{0,2},{2,0},{4,6},{6,4},{8,10},{10,8},{12,14},{14,12},{1,3},{3,1},... | collective-permute-start | bytes 4325384 | tf_op jit(solution)/shard_map/ppermute | solution.py:73
  25.5 36.1 %collective-permute-start.5 = (bf16[128,5632]{1,0:T(8,128)(2,1)S(1)}, bf16[128,5632]{1,0:T(8,128)(2,1)}, u32[]{:S(2)}, u32[]{:S(2)}) collective-permute-start(bf16[128,5632]{1,0:T(8,128)(2,1)S(1)} %constant_dynamic-update-slice_fusion.4.refs_0_.refs_16_), channel_id=1, source_target_pairs={{0,4},{2,6},{4,8},{6,10},{8,12},{10,14},{12,0},{14,2},{1,5},{3,7},... | collective-permute-start | bytes 4325384 | tf_op jit(solution)/shard_map/ppermute | solution.py:76
  25.9 37.2 %collective-permute-start.17 = (bf16[16,32,1024]{2,0,1:T(8,128)(2,1)S(1)}, bf16[16,32,1024]{2,0,1:T(8,128)(2,1)}, u32[]{:S(2)}, u32[]{:S(2)}) collective-permute-start(bf16[16,32,1024]{2,0,1:T(8,128)(2,1)S(1)} %bitcast.100), channel_id=1, source_target_pairs={{0,16},{16,0},{1,17},{17,1},{2,18},{18,2},{3,19},{19,3},{4,20},{20... | collective-permute-start | bytes 3145736 | tf_op jit(solution)/shard_map/ppermute | solution.py:29
  29.0 8.2 %collective-permute-start.18 = (f32[1024]{0:T(1024)}, f32[1024]{0:T(1024)S(1)}, u32[]{:S(2)}, u32[]{:S(2)}) collective-permute-start(f32[1024]{0:T(1024)} %bitcast.30), channel_id=1, source_target_pairs={{0,16},{16,0},{1,17},{17,1},{2,18},{18,2},{3,19},{19,3},{4,20},{20... | collective-permute-start | bytes 12296 | tf_op jit(solution)/shard_map/ppermute | solution.py:29
  29.7 31.8 %collective-permute-start.7 = (bf16[128,3072]{1,0:T(8,128)(2,1)}, bf16[128,3072]{1,0:T(8,128)(2,1)}, u32[]{:S(2)}, u32[]{:S(2)}) collective-permute-start(bf16[128,3072]{1,0:T(8,128)(2,1)} %constant_dynamic-update-slice_fusion.7.refs_0_), channel_id=1, source_target_pairs={{0,1},{1,0},{2,3},{3,2},{4,5},{5,4},{6,7},{7,6},{8,9},{9,8},{10,11... | collective-permute-start | bytes 2359304 | tf_op jit(solution)/shard_map/ppermute | solution.py:33
  37.2 24.3 %collective-permute-start.8 = (bf16[256,1024]{1,0:T(8,128)(2,1)}, bf16[256,1024]{1,0:T(8,128)(2,1)S(1)}, u32[]{:S(2)}, u32[]{:S(2)}) collective-permute-start(bf16[256,1024]{1,0:T(8,128)(2,1)} %pad.24.refs_16_), channel_id=1, source_target_pairs={{0,1},{1,0},{2,3},{3,2},{4,5},{5,4},{6,7},{7,6},{8,9},{9,8},{10,11... | collective-permute-start | bytes 1572872 | tf_op jit(solution)/shard_map/ppermute | solution.py:33
  58.8 50.2 %collective-permute-start.20 = (bf16[128,3072]{1,0:T(8,128)(2,1)}, bf16[128,3072]{1,0:T(8,128)(2,1)S(1)}, u32[]{:S(2)}, u32[]{:S(2)}) collective-permute-start(bf16[128,3072]{1,0:T(8,128)(2,1)} %constant_dynamic-update-slice_fusion.7.refs_0_), channel_id=1, source_target_pairs={{0,16},{16,0},{1,17},{17,1},{2,18},{18,2},{3,19},{19,3},{4,20},{20... | collective-permute-start | bytes 2359304 | tf_op jit(solution)/shard_map/ppermute | solution.py:29
  61.6 34.1 %collective-permute-start.11 = (bf16[128,5632]{1,0:T(8,128)(2,1)}, bf16[128,5632]{1,0:T(8,128)(2,1)}, u32[]{:S(2)}, u32[]{:S(2)}) collective-permute-start(bf16[128,5632]{1,0:T(8,128)(2,1)} %collective-permute-done.5.refs_2_.refs_18_), channel_id=1, source_target_pairs={{0,2},{2,0},{4,6},{6,4},{8,10},{10,8},{12,14},{14,12},{1,3},{3,1},... | collective-permute-start | bytes 4325384 | tf_op jit(solution)/shard_map/ppermute | solution.py:73
  63.4 36.2 %collective-permute-start.10 = (bf16[128,5632]{1,0:T(8,128)(2,1)}, bf16[128,5632]{1,0:T(8,128)(2,1)S(1)}, u32[]{:S(2)}, u32[]{:S(2)}) collective-permute-start(bf16[128,5632]{1,0:T(8,128)(2,1)} %collective-permute-done.5.refs_2_.refs_18_), channel_id=1, source_target_pairs={{0,4},{2,6},{4,8},{6,10},{8,12},{10,14},{12,0},{14,2},{1,5},{3,7},... | collective-permute-start | bytes 4325384 | tf_op jit(solution)/shard_map/ppermute | solution.py:76
  65.3 34.4 %collective-permute-start.12 = (bf16[128,3072]{1,0:T(8,128)(2,1)S(1)}, bf16[128,3072]{1,0:T(8,128)(2,1)S(1)}, u32[]{:S(2)}, u32[]{:S(2)}) collective-permute-start(bf16[128,3072]{1,0:T(8,128)(2,1)S(1)} %pad_maximum_fusion.2.refs_1_), channel_id=1, source_target_pairs={{0,1},{1,0},{2,3},{3,2},{4,5},{5,4},{6,7},{7,6},{8,9},{9,8},{10,11... | collective-permute-start | bytes 2359304 | tf_op jit(solution)/shard_map/ppermute | solution.py:33
  69.0 40.2 %collective-permute-start.21 = (bf16[128,3072]{1,0:T(8,128)(2,1)S(1)}, bf16[128,3072]{1,0:T(8,128)(2,1)S(1)}, u32[]{:S(2)}, u32[]{:S(2)}) collective-permute-start(bf16[128,3072]{1,0:T(8,128)(2,1)S(1)} %pad_maximum_fusion.2.refs_1_), channel_id=1, source_target_pairs={{0,16},{16,0},{1,17},{17,1},{2,18},{18,2},{3,19},{19,3},{4,20},{20... | collective-permute-start | bytes 2359304 | tf_op jit(solution)/shard_map/ppermute | solution.py:29
  95.6 4.1 collective-permute-start.9
  99.8 33.7 %collective-permute-start.23 = (bf16[128,5632]{1,0:T(8,128)(2,1)S(1)}, bf16[128,5632]{1,0:T(8,128)(2,1)S(1)}, u32[]{:S(2)}, u32[]{:S(2)}) collective-permute-start(bf16[128,5632]{1,0:T(8,128)(2,1)S(1)} %collective-permute-done.10.refs_4_.refs_20_), channel_id=1, source_target_pairs={{0,2},{2,0},{4,6},{6,4},{8,10},{10,8},{12,14},{14,12},{1,3},{3,1},... | collective-permute-start | bytes 4325384 | tf_op jit(solution)/shard_map/ppermute | solution.py:73
  101.1 26.5 %collective-permute-start.13 = (bf16[128,4096]{1,0:T(8,128)(2,1)S(1)}, bf16[128,4096]{1,0:T(8,128)(2,1)}, u32[]{:S(2)}, u32[]{:S(2)}) collective-permute-start(bf16[128,4096]{1,0:T(8,128)(2,1)S(1)} %slice.296), channel_id=1, source_target_pairs={{0,4},{2,6},{4,8},{6,10},{8,12},{10,14},{12,0},{14,2},{1,5},{3,7},... | collective-permute-start | bytes 3145736 | tf_op jit(solution)/shard_map/ppermute | solution.py:76
  101.7 18.6 %collective-permute-start.19 = (bf16[128,3072]{1,0:T(8,128)(2,1)}, bf16[128,3072]{1,0:T(8,128)(2,1)S(1)}, u32[]{:S(2)}, u32[]{:S(2)}) collective-permute-start(bf16[128,3072]{1,0:T(8,128)(2,1)} %pad_maximum_fusion.3.refs_2_), channel_id=1, source_target_pairs={{0,1},{1,0},{2,3},{3,2},{4,5},{5,4},{6,7},{7,6},{8,9},{9,8},{10,11... | collective-permute-start | bytes 2359304 | tf_op jit(solution)/shard_map/ppermute | solution.py:33
  109.0 26.5 %collective-permute-start.27 = (bf16[128,5632]{1,0:T(8,128)(2,1)S(1)}, bf16[128,5632]{1,0:T(8,128)(2,1)S(1)}, u32[]{:S(2)}, u32[]{:S(2)}) collective-permute-start(bf16[128,5632]{1,0:T(8,128)(2,1)S(1)} %constant_dynamic-update-slice_fusion.4.refs_0_.refs_16_), channel_id=1, source_target_pairs={{0,16},{16,0},{1,17},{17,1},{2,18},{18,2},{3,19},{19,3},{4,20},{20... | collective-permute-start | bytes 4325384 | tf_op jit(solution)/shard_map/ppermute | solution.py:29
  109.1 29.3 %collective-permute-start.29 = (bf16[128,5632]{1,0:T(8,128)(2,1)}, bf16[128,5632]{1,0:T(8,128)(2,1)}, u32[]{:S(2)}, u32[]{:S(2)}) collective-permute-start(bf16[128,5632]{1,0:T(8,128)(2,1)} %collective-permute-done.5.refs_2_.refs_18_), channel_id=1, source_target_pairs={{0,16},{16,0},{1,17},{17,1},{2,18},{18,2},{3,19},{19,3},{4,20},{20... | collective-permute-start | bytes 4325384 | tf_op jit(solution)/shard_map/ppermute | solution.py:29
  120.3 18.2 %collective-permute-start.28 = (bf16[128,5632]{1,0:T(8,128)(2,1)}, bf16[128,5632]{1,0:T(8,128)(2,1)}, u32[]{:S(2)}, u32[]{:S(2)}) collective-permute-start(bf16[128,5632]{1,0:T(8,128)(2,1)} %collective-permute-done.6.refs_1_.refs_17_), channel_id=1, source_target_pairs={{0,16},{16,0},{1,17},{17,1},{2,18},{18,2},{3,19},{19,3},{4,20},{20... | collective-permute-start | bytes 4325384 | tf_op jit(solution)/shard_map/ppermute | solution.py:29
  127.6 14.6 %collective-permute-start.30 = (bf16[128,5632]{1,0:T(8,128)(2,1)}, bf16[128,5632]{1,0:T(8,128)(2,1)}, u32[]{:S(2)}, u32[]{:S(2)}) collective-permute-start(bf16[128,5632]{1,0:T(8,128)(2,1)} %collective-permute-done.11.refs_3_.refs_19_), channel_id=1, source_target_pairs={{0,16},{16,0},{1,17},{17,1},{2,18},{18,2},{3,19},{19,3},{4,20},{20... | collective-permute-start | bytes 4325384 | tf_op jit(solution)/shard_map/ppermute | solution.py:29
  133.5 6.2 %collective-permute-start.22 = (bf16[128,3072]{1,0:T(8,128)(2,1)}, bf16[128,3072]{1,0:T(8,128)(2,1)}, u32[]{:S(2)}, u32[]{:S(2)}) collective-permute-start(bf16[128,3072]{1,0:T(8,128)(2,1)} %pad_maximum_fusion.3.refs_2_), channel_id=1, source_target_pairs={{0,16},{16,0},{1,17},{17,1},{2,18},{18,2},{3,19},{19,3},{4,20},{20... | collective-permute-start | bytes 2359304 | tf_op jit(solution)/shard_map/ppermute | solution.py:29
  136.7 24.8 %collective-permute-start.26 = (bf16[128,4096]{1,0:T(8,128)(2,1)}, bf16[128,4096]{1,0:T(8,128)(2,1)}, u32[]{:S(2)}, u32[]{:S(2)}) collective-permute-start(bf16[128,4096]{1,0:T(8,128)(2,1)} %collective-permute-done.13.refs_6_.refs_22_), channel_id=1, source_target_pairs={{0,2},{2,0},{4,6},{6,4},{8,10},{10,8},{12,14},{14,12},{1,3},{3,1},... | collective-permute-start | bytes 3145736 | tf_op jit(solution)/shard_map/ppermute | solution.py:73
  141.9 19.6 %collective-permute-start.24 = (bf16[128,3072]{1,0:T(8,128)(2,1)}, bf16[128,3072]{1,0:T(8,128)(2,1)}, u32[]{:S(2)}, u32[]{:S(2)}) collective-permute-start(bf16[128,3072]{1,0:T(8,128)(2,1)} %pad_maximum_fusion.4.refs_3_), channel_id=1, source_target_pairs={{0,16},{16,0},{1,17},{17,1},{2,18},{18,2},{3,19},{19,3},{4,20},{20... | collective-permute-start | bytes 2359304 | tf_op jit(solution)/shard_map/ppermute | solution.py:29
  142.3 20.0 %collective-permute-start.31 = (bf16[128,5632]{1,0:T(8,128)(2,1)S(1)}, bf16[128,5632]{1,0:T(8,128)(2,1)S(1)}, u32[]{:S(2)}, u32[]{:S(2)}) collective-permute-start(bf16[128,5632]{1,0:T(8,128)(2,1)S(1)} %collective-permute-done.10.refs_4_.refs_20_), channel_id=1, source_target_pairs={{0,16},{16,0},{1,17},{17,1},{2,18},{18,2},{3,19},{19,3},{4,20},{20... | collective-permute-start | bytes 4325384 | tf_op jit(solution)/shard_map/ppermute | solution.py:29
  142.4 20.4 %collective-permute-start.32 = (bf16[128,5632]{1,0:T(8,128)(2,1)}, bf16[128,5632]{1,0:T(8,128)(2,1)}, u32[]{:S(2)}, u32[]{:S(2)}) collective-permute-start(bf16[128,5632]{1,0:T(8,128)(2,1)} %copy-done.4), channel_id=1, source_target_pairs={{0,16},{16,0},{1,17},{17,1},{2,18},{18,2},{3,19},{19,3},{4,20},{20... | collective-permute-start | bytes 4325384 | tf_op jit(solution)/shard_map/ppermute | solution.py:29
  142.8 19.9 %collective-permute-start.33 = (bf16[128,4096]{1,0:T(8,128)(2,1)}, bf16[128,4096]{1,0:T(8,128)(2,1)}, u32[]{:S(2)}, u32[]{:S(2)}) collective-permute-start(bf16[128,4096]{1,0:T(8,128)(2,1)} %collective-permute-done.13.refs_6_.refs_22_), channel_id=1, source_target_pairs={{0,16},{16,0},{1,17},{17,1},{2,18},{18,2},{3,19},{19,3},{4,20},{20... | collective-permute-start | bytes 3145736 | tf_op jit(solution)/shard_map/ppermute | solution.py:29
  161.5 33.0 %collective-permute-start.37 = (bf16[128,3072]{1,0:T(8,128)(2,1)}, bf16[128,3072]{1,0:T(8,128)(2,1)}, u32[]{:S(2)}, u32[]{:S(2)}) collective-permute-start(bf16[128,3072]{1,0:T(8,128)(2,1)} %pad_maximum_fusion.4.refs_3_), channel_id=1, source_target_pairs={{0,1},{1,0},{2,3},{3,2},{4,5},{5,4},{6,7},{7,6},{8,9},{9,8},{10,11... | collective-permute-start | bytes 2359304 | tf_op jit(solution)/shard_map/ppermute | solution.py:33
  162.2 42.1 %collective-permute-start.38 = (bf16[128,3072]{1,0:T(8,128)(2,1)}, bf16[128,3072]{1,0:T(8,128)(2,1)S(1)}, u32[]{:S(2)}, u32[]{:S(2)}) collective-permute-start(bf16[128,3072]{1,0:T(8,128)(2,1)} %collective-permute-done.7.refs_4_), channel_id=1, source_target_pairs={{0,16},{16,0},{1,17},{17,1},{2,18},{18,2},{3,19},{19,3},{4,20},{20... | collective-permute-start | bytes 2359304 | tf_op jit(solution)/shard_map/ppermute | solution.py:29
  162.7 41.7 %collective-permute-start.39 = (bf16[128,3072]{1,0:T(8,128)(2,1)}, bf16[128,3072]{1,0:T(8,128)(2,1)S(1)}, u32[]{:S(2)}, u32[]{:S(2)}) collective-permute-start(bf16[128,3072]{1,0:T(8,128)(2,1)} %copy-done.23), channel_id=1, source_target_pairs={{0,16},{16,0},{1,17},{17,1},{2,18},{18,2},{3,19},{19,3},{4,20},{20... | collective-permute-start | bytes 2359304 | tf_op jit(solution)/shard_map/ppermute | solution.py:29
  162.8 41.6 %collective-permute-start.40 = (bf16[128,3072]{1,0:T(8,128)(2,1)}, bf16[128,3072]{1,0:T(8,128)(2,1)S(1)}, u32[]{:S(2)}, u32[]{:S(2)}) collective-permute-start(bf16[128,3072]{1,0:T(8,128)(2,1)} %copy-done.25), channel_id=1, source_target_pairs={{0,16},{16,0},{1,17},{17,1},{2,18},{18,2},{3,19},{19,3},{4,20},{20... | collective-permute-start | bytes 2359304 | tf_op jit(solution)/shard_map/ppermute | solution.py:29
  194.6 9.9 %collective-permute-start.41 = (bf16[128,3072]{1,0:T(8,128)(2,1)}, bf16[128,3072]{1,0:T(8,128)(2,1)S(1)}, u32[]{:S(2)}, u32[]{:S(2)}) collective-permute-start(bf16[128,3072]{1,0:T(8,128)(2,1)} %collective-permute-done.37.refs_7_), channel_id=1, source_target_pairs={{0,16},{16,0},{1,17},{17,1},{2,18},{18,2},{3,19},{19,3},{4,20},{20... | collective-permute-start | bytes 2359304 | tf_op jit(solution)/shard_map/ppermute | solution.py:29
  194.7 8.9 %collective-permute-start.35 = (bf16[128,1024]{1,0:T(8,128)(2,1)}, bf16[128,1024]{1,0:T(8,128)(2,1)S(1)}, u32[]{:S(2)}, u32[]{:S(2)}) collective-permute-start(bf16[128,1024]{1,0:T(8,128)(2,1)} %bitcast.112), channel_id=1, source_target_pairs={{0,1},{1,0},{2,3},{3,2},{4,5},{5,4},{6,7},{7,6},{8,9},{9,8},{10,11... | collective-permute-start | bytes 786440 | tf_op jit(solution)/shard_map/ppermute | solution.py:33
  203.6 34.3 %collective-permute-start.44 = (bf16[128,1024]{1,0:T(8,128)(2,1)}, bf16[128,1024]{1,0:T(8,128)(2,1)S(1)}, u32[]{:S(2)}, u32[]{:S(2)}) collective-permute-start(bf16[128,1024]{1,0:T(8,128)(2,1)} %bitcast.94), channel_id=1, source_target_pairs={{0,1},{1,0},{2,3},{3,2},{4,5},{5,4},{6,7},{7,6},{8,9},{9,8},{10,11... | collective-permute-start | bytes 786440 | tf_op jit(solution)/shard_map/ppermute | solution.py:33
  204.3 41.1 %collective-permute-start.36 = (bf16[256,1024]{1,0:T(8,128)(2,1)}, bf16[256,1024]{1,0:T(8,128)(2,1)S(1)}, u32[]{:S(2)}, u32[]{:S(2)}) collective-permute-start(bf16[256,1024]{1,0:T(8,128)(2,1)} %bitcast.108), channel_id=1, source_target_pairs={{0,16},{16,0},{1,17},{17,1},{2,18},{18,2},{3,19},{19,3},{4,20},{20... | collective-permute-start | bytes 1572872 | tf_op jit(solution)/shard_map/ppermute | solution.py:29
  237.9 8.9 %collective-permute-start.45 = (bf16[128,1024]{1,0:T(8,128)(2,1)}, bf16[128,1024]{1,0:T(8,128)(2,1)}, u32[]{:S(2)}, u32[]{:S(2)}) collective-permute-start(bf16[128,1024]{1,0:T(8,128)(2,1)} %get-tuple-element.136), channel_id=1, source_target_pairs={{0,1},{1,0},{2,3},{3,2},{4,5},{5,4},{6,7},{7,6},{8,9},{9,8},{10,11... | collective-permute-start | bytes 786440 | tf_op jit(solution)/shard_map/ppermute | solution.py:33
  240.4 6.4 %collective-permute-start.46 = (bf16[4,128,1024]{2,1,0:T(8,128)(2,1)S(1)}, bf16[4,128,1024]{2,1,0:T(8,128)(2,1)}, u32[]{:S(2)}, u32[]{:S(2)}) collective-permute-start(bf16[4,128,1024]{2,1,0:T(8,128)(2,1)S(1)} %pad_maximum_fusion.1.states_own), channel_id=1, source_target_pairs={{0,16},{16,0},{1,17},{17,1},{2,18},{18,2},{3,19},{19,3},{4,20},{20... | collective-permute-start | bytes 3145736 | tf_op jit(solution)/shard_map/ppermute | solution.py:29
  241.0 4.3 collective-permute-start.42
  241.1 5.8 %collective-permute-start.47 = (bf16[2,128,1024]{2,1,0:T(8,128)(2,1)S(1)}, bf16[2,128,1024]{2,1,0:T(8,128)(2,1)}, u32[]{:S(2)}, u32[]{:S(2)}) collective-permute-start(bf16[2,128,1024]{2,1,0:T(8,128)(2,1)S(1)} %copy-done.13), channel_id=1, source_target_pairs={{0,16},{16,0},{1,17},{17,1},{2,18},{18,2},{3,19},{19,3},{4,20},{20... | collective-permute-start | bytes 1572872 | tf_op jit(solution)/shard_map/ppermute | solution.py:29
  246.8 31.7 %collective-permute-start.48 = (bf16[2,128,1536]{2,1,0:T(8,128)(2,1)S(1)}, bf16[2,128,1536]{2,1,0:T(8,128)(2,1)S(1)}, u32[]{:S(2)}, u32[]{:S(2)}) collective-permute-start(bf16[2,128,1536]{2,1,0:T(8,128)(2,1)S(1)} %pad_maximum_fusion.5), channel_id=1, source_target_pairs={{0,1},{1,0},{2,3},{3,2},{4,5},{5,4},{6,7},{7,6},{8,9},{9,8},{10,11... | collective-permute-start | bytes 2359304 | tf_op jit(solution)/shard_map/ppermute | solution.py:33
  248.2 30.3 %collective-permute-start.49 = (bf16[2,128,1152]{2,1,0:T(8,128)(2,1)S(1)}, bf16[2,128,1152]{2,1,0:T(8,128)(2,1)S(1)}, u32[]{:S(2)}, u32[]{:S(2)}) collective-permute-start(bf16[2,128,1152]{2,1,0:T(8,128)(2,1)S(1)} %pad_maximum_fusion.6), channel_id=1, source_target_pairs={{0,1},{1,0},{2,3},{3,2},{4,5},{5,4},{6,7},{7,6},{8,9},{9,8},{10,11... | collective-permute-start | bytes 1769480 | tf_op jit(solution)/shard_map/ppermute | solution.py:33
  298.5 14.3 %collective-permute-start.52 = (bf16[256,768]{1,0:T(8,128)(2,1)}, bf16[256,768]{1,0:T(8,128)(2,1)S(1)}, u32[]{:S(2)}, u32[]{:S(2)}) collective-permute-start(bf16[256,768]{1,0:T(8,128)(2,1)} %get-tuple-element.156), channel_id=1, source_target_pairs={{0,4},{2,6},{4,8},{6,10},{8,12},{10,14},{12,0},{14,2},{1,5},{3,7},... | collective-permute-start | bytes 1179656 | tf_op jit(solution)/shard_map/ppermute | solution.py:76
  298.7 32.4 %collective-permute-start.58 = (bf16[128,5120]{1,0:T(8,128)(2,1)}, bf16[128,5120]{1,0:T(8,128)(2,1)}, u32[]{:S(2)}, u32[]{:S(2)}) collective-permute-start(bf16[128,5120]{1,0:T(8,128)(2,1)} %get-tuple-element.163), channel_id=1, source_target_pairs={{0,2},{2,0},{4,6},{6,4},{8,10},{10,8},{12,14},{14,12},{1,3},{3,1},... | collective-permute-start | bytes 3932168 | tf_op jit(solution)/shard_map/ppermute | solution.py:73
  304.0 42.1 %collective-permute-start.57 = (bf16[256,768]{1,0:T(8,128)(2,1)}, bf16[256,768]{1,0:T(8,128)(2,1)}, u32[]{:S(2)}, u32[]{:S(2)}) collective-permute-start(bf16[256,768]{1,0:T(8,128)(2,1)} %get-tuple-element.161), channel_id=1, source_target_pairs={{4,0},{6,2},{8,4},{10,6},{12,8},{14,10},{0,12},{2,14},{5,1},{7,3},... | collective-permute-start | bytes 1179656 | tf_op jit(solution)/shard_map/ppermute | solution.py:79
  325.4 9.8 %collective-permute-start.53 = (f32[16,16,1024]{2,1,0:T(8,128)}, f32[16,16,1024]{2,1,0:T(8,128)S(1)}, u32[]{:S(2)}, u32[]{:S(2)}) collective-permute-start(f32[16,16,1024]{2,1,0:T(8,128)} %bitcast.83), channel_id=1, source_target_pairs={{0,16},{16,0},{1,17},{17,1},{2,18},{18,2},{3,19},{19,3},{4,20},{20... | collective-permute-start | bytes 3145736 | tf_op jit(solution)/shard_map/ppermute | solution.py:29
  326.0 4.4 collective-permute-start.56
  331.2 14.1 %collective-permute-start.59 = (bf16[256,768]{1,0:T(8,128)(2,1)}, bf16[256,768]{1,0:T(8,128)(2,1)S(1)}, u32[]{:S(2)}, u32[]{:S(2)}) collective-permute-start(bf16[256,768]{1,0:T(8,128)(2,1)} %add_convert_fusion.3), channel_id=1, source_target_pairs={{0,4},{2,6},{4,8},{6,10},{8,12},{10,14},{12,0},{14,2},{1,5},{3,7},... | collective-permute-start | bytes 1179656 | tf_op jit(solution)/shard_map/ppermute | solution.py:76
  333.6 29.9 %collective-permute-start.60 = (bf16[128,5120]{1,0:T(8,128)(2,1)S(1)}, bf16[128,5120]{1,0:T(8,128)(2,1)S(1)}, u32[]{:S(2)}, u32[]{:S(2)}) collective-permute-start(bf16[128,5120]{1,0:T(8,128)(2,1)S(1)} %copy-done.61), channel_id=1, source_target_pairs={{0,2},{2,0},{4,6},{6,4},{8,10},{10,8},{12,14},{14,12},{1,3},{3,1},... | collective-permute-start | bytes 3932168 | tf_op jit(solution)/shard_map/ppermute | solution.py:73
  334.9 36.9 %collective-permute-start.61 = (bf16[128,5120]{1,0:T(8,128)(2,1)S(1)}, bf16[128,5120]{1,0:T(8,128)(2,1)S(1)}, u32[]{:S(2)}, u32[]{:S(2)}) collective-permute-start(bf16[128,5120]{1,0:T(8,128)(2,1)S(1)} %add_convert_fusion.2), channel_id=1, source_target_pairs={{0,4},{2,6},{4,8},{6,10},{8,12},{10,14},{12,0},{14,2},{1,5},{3,7},... | collective-permute-start | bytes 3932168 | tf_op jit(solution)/shard_map/ppermute | solution.py:76
  336.2 38.1 %collective-permute-start.54 = (f32[32,16,1024]{2,1,0:T(8,128)S(1)}, f32[32,16,1024]{2,1,0:T(8,128)S(1)}, u32[]{:S(2)}, u32[]{:S(2)}) collective-permute-start(f32[32,16,1024]{2,1,0:T(8,128)S(1)} %pad_maximum_fusion), channel_id=1, source_target_pairs={{0,1},{17,16},{2,3},{19,18},{4,5},{21,20},{6,7},{23,22},{8,9},{25,... | collective-permute-start | bytes 6291464 | tf_op jit(solution)/shard_map/ppermute | solution.py:1099
  345.3 71.7 %collective-permute-start.67 = (bf16[128,4096]{1,0:T(8,128)(2,1)S(1)}, bf16[128,4096]{1,0:T(8,128)(2,1)S(1)}, u32[]{:S(2)}, u32[]{:S(2)}) collective-permute-start(bf16[128,4096]{1,0:T(8,128)(2,1)S(1)} %copy-done.21), channel_id=1, source_target_pairs={{0,0},{1,16},{16,1},{17,17},{2,2},{3,18},{18,3},{19,19},{4,4},{5,2... | collective-permute-start | bytes 3145736 | tf_op jit(solution)/shard_map/ppermute | solution.py:37
  374.3 9.2 %collective-permute-start.62 = (bf16[128,1024]{1,0:T(8,128)(2,1)S(1)}, bf16[128,1024]{1,0:T(8,128)(2,1)S(1)}, u32[]{:S(2)}, u32[]{:S(2)}) collective-permute-start(bf16[128,1024]{1,0:T(8,128)(2,1)S(1)} %pad_maximum_fusion.7), channel_id=1, source_target_pairs={{0,2},{2,0},{4,6},{6,4},{8,10},{10,8},{12,14},{14,12},{1,3},{3,1},... | collective-permute-start | bytes 786440 | tf_op jit(solution)/shard_map/ppermute | solution.py:73
  375.2 39.4 %collective-permute-start.65 = (bf16[128,5120]{1,0:T(8,128)(2,1)S(1)}, bf16[128,5120]{1,0:T(8,128)(2,1)S(1)}, u32[]{:S(2)}, u32[]{:S(2)}) collective-permute-start(bf16[128,5120]{1,0:T(8,128)(2,1)S(1)} %copy-done.60), channel_id=1, source_target_pairs={{0,2},{2,0},{4,6},{6,4},{8,10},{10,8},{12,14},{14,12},{1,3},{3,1},... | collective-permute-start | bytes 3932168 | tf_op jit(solution)/shard_map/ppermute | solution.py:73
  376.3 38.3 %collective-permute-start.66 = (bf16[128,5120]{1,0:T(8,128)(2,1)S(1)}, bf16[128,5120]{1,0:T(8,128)(2,1)S(1)}, u32[]{:S(2)}, u32[]{:S(2)}) collective-permute-start(bf16[128,5120]{1,0:T(8,128)(2,1)S(1)} %add_convert_fusion.1), channel_id=1, source_target_pairs={{0,4},{2,6},{4,8},{6,10},{8,12},{10,14},{12,0},{14,2},{1,5},{3,7},... | collective-permute-start | bytes 3932168 | tf_op jit(solution)/shard_map/ppermute | solution.py:76
  383.6 28.5 %collective-permute-start.63 = (bf16[128,640]{1,0:T(8,128)(2,1)S(1)}, bf16[128,640]{1,0:T(8,128)(2,1)}, u32[]{:S(2)}, u32[]{:S(2)}) collective-permute-start(bf16[128,640]{1,0:T(8,128)(2,1)S(1)} %pad_maximum_fusion.9), channel_id=1, source_target_pairs={{0,4},{2,6},{4,8},{6,10},{8,12},{10,14},{12,0},{14,2},{1,5},{3,7},... | collective-permute-start | bytes 491528 | tf_op jit(solution)/shard_map/ppermute | solution.py:76
  387.4 26.2 %collective-permute-start.64 = (bf16[128,640]{1,0:T(8,128)(2,1)S(1)}, bf16[128,640]{1,0:T(8,128)(2,1)S(1)}, u32[]{:S(2)}, u32[]{:S(2)}) collective-permute-start(bf16[128,640]{1,0:T(8,128)(2,1)S(1)} %pad_maximum_fusion.9), channel_id=1, source_target_pairs={{4,0},{6,2},{8,4},{10,6},{12,8},{14,10},{0,12},{2,14},{5,1},{7,3},... | collective-permute-start | bytes 491528 | tf_op jit(solution)/shard_map/ppermute | solution.py:79
  417.1 9.0 %collective-permute-start.68 = (bf16[128,640]{1,0:T(8,128)(2,1)}, bf16[128,640]{1,0:T(8,128)(2,1)}, u32[]{:S(2)}, u32[]{:S(2)}) collective-permute-start(bf16[128,640]{1,0:T(8,128)(2,1)} %collective-permute-done.63), channel_id=1, source_target_pairs={{0,4},{2,6},{4,8},{6,10},{8,12},{10,14},{12,0},{14,2},{1,5},{3,7},... | collective-permute-start | bytes 491528 | tf_op jit(solution)/shard_map/ppermute | solution.py:76
  419.6 13.3 %collective-permute-start.72 = (bf16[128,1024]{1,0:T(8,128)(2,1)}, bf16[128,1024]{1,0:T(8,128)(2,1)S(1)}, u32[]{:S(2)}, u32[]{:S(2)}) collective-permute-start(bf16[128,1024]{1,0:T(8,128)(2,1)} %slice.260), channel_id=1, source_target_pairs={{0,2},{2,0},{4,6},{6,4},{8,10},{10,8},{12,14},{14,12},{1,3},{3,1},... | collective-permute-start | bytes 786440 | tf_op jit(solution)/shard_map/ppermute | solution.py:73
  420.7 12.3 %collective-permute-start.73 = (bf16[128,1024]{1,0:T(8,128)(2,1)}, bf16[128,1024]{1,0:T(8,128)(2,1)S(1)}, u32[]{:S(2)}, u32[]{:S(2)}) collective-permute-start(bf16[128,1024]{1,0:T(8,128)(2,1)} %slice.318), channel_id=1, source_target_pairs={{0,4},{2,6},{4,8},{6,10},{8,12},{10,14},{12,0},{14,2},{1,5},{3,7},... | collective-permute-start | bytes 786440 | tf_op jit(solution)/shard_map/ppermute | solution.py:76
  421.4 28.4 %collective-permute-start.70 = (bf16[128,4096]{1,0:T(8,128)(2,1)}, bf16[128,4096]{1,0:T(8,128)(2,1)}, u32[]{:S(2)}, u32[]{:S(2)}) collective-permute-start(bf16[128,4096]{1,0:T(8,128)(2,1)} %slice.258), channel_id=1, source_target_pairs={{0,2},{1,18},{16,3},{17,19},{2,0},{3,16},{18,1},{19,17},{4,6},{5,2... | collective-permute-start | bytes 3145736 | tf_op jit(solution)/shard_map/ppermute | solution.py:1116
  422.4 30.9 %collective-permute-start.71 = (bf16[128,4096]{1,0:T(8,128)(2,1)}, bf16[128,4096]{1,0:T(8,128)(2,1)}, u32[]{:S(2)}, u32[]{:S(2)}) collective-permute-start(bf16[128,4096]{1,0:T(8,128)(2,1)} %slice.317), channel_id=1, source_target_pairs={{0,4},{1,20},{16,5},{17,21},{2,6},{3,22},{18,7},{19,23},{4,8},{5,2... | collective-permute-start | bytes 3145736 | tf_op jit(solution)/shard_map/ppermute | solution.py:1116
  (72 other events, 807.7 us)

commit v12 on v11

--- a/solution.py
+++ b/solution.py
@@ -927,6 +927,14 @@
     vocab_own = jnp.pad(vocab_weight, ((0, 0), (0, vocab_pad - vocab_size)))
     ready = (noise_part, length_part, label_part, counted, bias_row, normed_own, normed_other)
     places, in_own, rec_own, small_own, small_chip = [], [], [], [], []
+    z, x = ring.z, ring.x
+    if ring.short:
+        steps_back = [ring.back(k) for k in range(1, 5)]
+        order = [at * 2 + 1 - x for at in steps_back] + [at * 2 + x for at in steps_back]
+        order = [y] + order + steps_back
+    else:
+        order = [y] + [jnp.int32(k) for k in [*range(8), *range(4)]]
+    order = jnp.stack(order).astype(jnp.int32)
     small = jnp.concatenate(
         [
             tie(mono_mem, in_shard, rec_shard), span_mem, mono_dec, span_dec,
@@ -949,23 +957,23 @@
         near, far, near_core, far_core = [], [], [], []
         for k in range(ring.outer):
             near.append(held)
-            jobs = [(across, held), (across_chips, small_own[k])]
+            jobs = [(across, held)]
             if k < ring.outer - 1:
                 jobs.append((onward, held[:, :both] if k == ring.outer - 2 else held))
             if k == 0:
                 jobs.append((across_chips, vocab_own))
             if k == 1:
                 jobs.append((across_chips, vector_own))
-            results = flow.step(*jobs)
+            results = flow.step(*jobs, also=tuple(small_chip[-1:]))
             far.append(results[0])
-            small_chip.append(results[1])
+            small_chip.append(across_chips(small_own[k]))
             if k == 0:
-                vocab_chip = results[3]
+                vocab_chip = results[2]
             if k == 1:
-                vector_pair = jnp.concatenate([vector_own, results[3]], axis=1)
+                vector_pair = jnp.concatenate([vector_own, results[2]], axis=1)
             if k < ring.outer - 1:
                 small_own.append(jnp.concatenate([held[:, both:], far[k][:, both:]], axis=1))
-                held = results[2]
+                held = results[1]
         for k, (a, b) in enumerate(zip(near, far)):
             near_core.append(across_cores(a if k else tie(a, near[1], *ready)))
             far_core.append(across_cores(b))
@@ -981,7 +989,7 @@
         vectors = jnp.concatenate([vector_pair, vector_core], axis=1)
         vectors = jnp.pad(vectors, ((0, 3), (0, 0)))
         small_core = [across_cores(a) for a in small_own[:-1]]
-        small_core.append(across_cores(tie(small_own[-1], vectors, places)))
+        small_core.append(across_cores(tie(small_own[-1], vectors, places, order)))
         in_own = [a for pair in zip(near, far) for a in pair]
         in_other = [a for pair in zip(near_core, far_core) for a in pair]
         rec_own, rec_other, rec_column = in_own, in_other, wide_half
@@ -1004,14 +1012,6 @@
         vectors = jnp.concatenate([vector_pair, vector_core], axis=1)
         vectors = jnp.pad(vectors, ((0, 3), (0, 0)))
         places = jnp.stack([s, y] + places).astype(jnp.int32)
-    z, x = ring.z, ring.x
-    if ring.short:
-        steps_back = [ring.back(k) for k in range(1, 5)]
-        order = [at * 2 + 1 - x for at in steps_back] + [at * 2 + x for at in steps_back]
-        order = [y] + order + steps_back
-    else:
-        order = [y] + [jnp.int32(k) for k in [*range(8), *range(4)]]
-    order = jnp.stack(order).astype(jnp.int32)
     places = tie(places, order, vectors, *vocab, *ready, *small_chip[:-1], *small_core)
 
     kept, given, before, gates, cells = run_forward(

time: 460 us -> 465 us (1.011)
  waiting for transfers between devices: 196 us -> 201 us
    ppermute x11, waiting for transfers between devices: 21.2 us -> 45.8 us  [across_chips(): return lax.ppermute(array, 'mp', core_swap)]
    ppermute x11, waiting for transfers between devices: 92.6 us -> 68.2 us  [across(): return lax.ppermute(array, 'dp', self.pair)]
    unnamed x138 -> x150, local copies, waits for them, and re-layouts: 15.9 us -> 16.9 us
  transfers between devices with their start and end apart: 74 -> 74, of which waited for: 29 -> 28; matrix products, arithmetic and copies ran while one was open for 13% -> 13% of each run, Pallas kernels for 22% -> 21%
where the time goes in v12:
time: 465 us; the launch traced here: 463 us
  waiting for transfers between devices  201 us (43%)
  Pallas kernels  114 us (25%)
  starting transfers between devices  70.1 us (15%)
  local copies, waits for them, and re-layouts  51.7 us (11%)
  other arithmetic  24.1 us (5%)
    ppermute x11, waiting for transfers between devices, across(): return lax.ppermute(array, 'dp', self.pair)  68.2 us
    ppermute x11, waiting for transfers between devices, onward(): return lax.ppermute(array, 'dp', self.ring)  57.6 us
    ppermute x11, waiting for transfers between devices, across_chips(): return lax.ppermute(array, 'mp', core_swap)  45.8 us
    pallas_call x1, Pallas kernels, run_attend(): pl.pallas_call(functools.partial(attend_kernel, count), out_shape=(jax.Sh...  31.2 us
    pallas_call x1, Pallas kernels, run_forward(): pl.pallas_call(functools.partial(forward_kernel, count, column), out_shap...  30 us
    pallas_call x1, Pallas kernels, run_backward(): pl.pallas_call(functools.partial(backward_kernel, count, column), out_sha...  29 us
    ppermute x2, waiting for transfers between devices, cornered(): return lambda array: lax.ppermute(array, ('section', 'dp', 'mp'), pairs)  19.8 us
    unnamed x150, local copies, waits for them, and re-layouts  16.9 us
  transfers between devices with their start and end apart: 74, of which 28 were waited for; matrix products, arithmetic and copies ran while one was open for 13% of the time, Pallas kernels for 21%

profile of v12, /device:TPU:0, one launch (start us, length us, event | category | flops | bytes accessed | tf_op | source)
XLA Modules:
  0.0 463.5 jit_solution(8282322176787212020)
XLA Ops:
  2.0 1.9 copy.66
  4.0 1.5 collective-permute-start
  5.4 5.4 %collective-permute-start.1 = (bf16[128,2048]{1,0:T(8,128)(2,1)}, bf16[128,2048]{1,0:T(8,128)(2,1)}, u32[]{:S(2)}, u32[]{:S(2)}) collective-permute-start(bf16[128,2048]{1,0:T(8,128)(2,1)} %bitcast.63), channel_id=1, source_target_pairs={{0,0},{1,16},{16,1},{17,17},{2,2},{3,18},{18,3},{19,19},{4,4},{5,2... | collective-permute-start | bytes 1572872 | tf_op jit(solution)/shard_map/ppermute | solution.py:37
  14.8 3.0 collective-permute-start.2
  17.8 1.5 collective-permute-start.4
  20.2 1.3 constant_dynamic-update-slice_fusion.6
  22.8 5.2 %collective-permute-done.2 = bf16[128,1536]{1,0:T(8,128)(2,1)S(1)} collective-permute-done((bf16[128,1536]{1,0:T(8,128)(2,1)}, bf16[128,1536]{1,0:T(8,128)(2,1)S(1)}, u32[]{:S(2)}, u32[]{:S(2)}) %collective-permute-start.2) | collective-permute-done | bytes 393248 | tf_op jit(solution)/shard_map/ppermute | solution.py:76
  29.1 1.5 collective-permute-start.6
  30.6 1.8 constant_dynamic-update-slice_fusion.7.refs_0_
  32.4 2.7 collective-permute-start.8
  37.5 27.2 %collective-permute-done.7.refs_17_ = bf16[256,1024]{1,0:T(8,128)(2,1)S(1)} collective-permute-done((bf16[256,1024]{1,0:T(8,128)(2,1)S(1)}, bf16[256,1024]{1,0:T(8,128)(2,1)S(1)}, u32[]{:S(2)}, u32[]{:S(2)}) %collective-permute-start.7) | collective-permute-done | bytes 524320 | tf_op jit(solution)/shard_map/ppermute | solution.py:33
  65.3 1.3 broadcast_select_fusion
  66.8 1.6 collective-permute-start.10
  69.9 2.1 collective-permute-start.12
  73.6 25.5 %collective-permute-done.11.refs_3_.refs_19_ = bf16[128,5632]{1,0:T(8,128)(2,1)} collective-permute-done((bf16[128,5632]{1,0:T(8,128)(2,1)}, bf16[128,5632]{1,0:T(8,128)(2,1)}, u32[]{:S(2)}, u32[]{:S(2)}) %collective-permute-start.11) | collective-permute-done | bytes 1441824 | tf_op jit(solution)/shard_map/ppermute | solution.py:73
  99.1 1.7 collective-permute-start.9
  102.9 1.4 collective-permute-start.19
  104.5 1.6 collective-permute-start.23
  108.9 1.3 broadcast_in_dim.23.noise
  112.9 9.5 %collective-permute-done.19.refs_6_ = bf16[128,3072]{1,0:T(8,128)(2,1)} collective-permute-done((bf16[128,3072]{1,0:T(8,128)(2,1)}, bf16[128,3072]{1,0:T(8,128)(2,1)}, u32[]{:S(2)}, u32[]{:S(2)}) %collective-permute-start.19) | collective-permute-done | bytes 786464 | tf_op jit(solution)/shard_map/ppermute | solution.py:33
  122.4 9.3 %collective-permute-done.13.refs_6_.refs_22_ = bf16[128,4096]{1,0:T(8,128)(2,1)} collective-permute-done((bf16[128,4096]{1,0:T(8,128)(2,1)S(1)}, bf16[128,4096]{1,0:T(8,128)(2,1)}, u32[]{:S(2)}, u32[]{:S(2)}) %collective-permute-start.13) | collective-permute-done | bytes 1048608 | tf_op jit(solution)/shard_map/ppermute | solution.py:76
  131.8 4.7 %collective-permute-done.23.refs_5_.refs_21_ = bf16[128,5632]{1,0:T(8,128)(2,1)S(1)} collective-permute-done((bf16[128,5632]{1,0:T(8,128)(2,1)S(1)}, bf16[128,5632]{1,0:T(8,128)(2,1)S(1)}, u32[]{:S(2)}, u32[]{:S(2)}) %collective-permute-start.23) | collective-permute-done | bytes 1441824 | tf_op jit(solution)/shard_map/ppermute | solution.py:73
  137.7 1.7 collective-permute-start.26
  142.7 1.3 collective-permute-done.25.b_other
  145.0 17.5 %collective-permute-done.26.refs_7_.refs_23_ = bf16[128,4096]{1,0:T(8,128)(2,1)} collective-permute-done((bf16[128,4096]{1,0:T(8,128)(2,1)}, bf16[128,4096]{1,0:T(8,128)(2,1)}, u32[]{:S(2)}, u32[]{:S(2)}) %collective-permute-start.26) | collective-permute-done | bytes 1048608 | tf_op jit(solution)/shard_map/ppermute | solution.py:73
  162.6 1.6 collective-permute-start.37
  166.2 30.0 %recur_forward.1 = (bf16[16,8,1024]{2,1,0:T(8,128)(2,1)}, bf16[16,8,1024]{2,1,0:T(8,128)(2,1)}, bf16[16,16,1024]{2,1,0:T(8,128)(2,1)}, f32[16,16,4096]{2,1,0:T(8,128)}, f32[16,16,1024]{2,1,0:T(8,128)}) custom-call(s32[10]{0:T(128)} %stack.116.places, bf16[256,1024]{1,0:T(8,128)(2,1)} %bitcast.87, f32[1,2048]{1,0:T(1,128)} %copy-done.51, ...), custom_call_target="tpu_custom_call" | custom-call | tf_op jit(solution)/shard_map/recur_forward/pallas_call | solution.py:196
  197.5 7.7 %collective-permute-done.35.taken = bf16[128,1024]{1,0:T(8,128)(2,1)S(1)} collective-permute-done((bf16[128,1024]{1,0:T(8,128)(2,1)}, bf16[128,1024]{1,0:T(8,128)(2,1)S(1)}, u32[]{:S(2)}, u32[]{:S(2)}) %collective-permute-start.35) | collective-permute-done | bytes 262176 | tf_op jit(solution)/shard_map/ppermute | solution.py:33
  208.6 31.2 %attend.1 = (f32[128,1024]{1,0:T(8,128)}, bf16[128,1024]{1,0:T(8,128)(2,1)}, bf16[128,1536]{1,0:T(8,128)(2,1)}, bf16[128,1536]{1,0:T(8,128)(2,1)}, bf16[2,128,15...) custom-call(s32[10]{0:T(128)} %stack.116.places, ...), custom_call_target="tpu_custom_call" | custom-call | tf_op jit(solution)/shard_map/attend/pallas_call | solution.py:696
  244.4 2.4 collective-permute-done.42.pack_core
  246.8 1.3 pad_maximum_fusion.5
  250.8 29.0 %recur_backward.1 = (bf16[16,16,2048]{2,1,0:T(8,128)(2,1)}, bf16[16,16,2048]{2,1,0:T(8,128)(2,1)}) custom-call(s32[10]{0:T(128)} %stack.116.places, f32[16,8,1024]{2,1,0:T(8,128)} %bitcast.101, bf16[16,8,1024]{2,1,0:T(8,128)(2,1)} %bitcast.43.taken, f32[16,16,4096]{2,1,0:T(8,128)} %get-tuple-element.133.gates_in, ...), custom_call_target="tpu_custom_call" | custom-call | tf_op jit(solution)/shard_map/recur_backward/pallas_call | solution.py:324
  286.4 15.2 %weight_gradients.1 = (bf16[128,5120]{1,0:T(8,128)(2,1)}, bf16[128,5120]{1,0:T(8,128)(2,1)}, bf16[128,5120]{1,0:T(8,128)(2,1)}, bf16[128,5120]{1,0:T(8,128)(2,1)...) custom-call(s32[13]{0:T(128)} %stack.123.order, ...), custom_call_target="tpu_custom_call" | custom-call | tf_op jit(solution)/shard_map/weight_gradients/pallas_call | solution.py:853
  301.6 1.5 collective-permute-start.52
  303.8 2.3 slice.258
  306.1 1.7 slice.260
  307.8 3.6 collective-permute-start.57
  311.4 4.5 collective-permute-done.52
  316.7 9.1 %input_back.1 = (f32[256,1024]{1,0:T(8,128)}, f32[1,1024]{1,0:T(1,128)}) custom-call(s32[10]{0:T(128)} %stack.116.places, bf16[256,1024]{1,0:T(8,128)(2,1)} %bitcast.91, f32[1,1024]{1,0:T(1,128)} %bitcast.113, bf16[256,2048]{1,0:T(8,128)(2,1)} %bitcast.85, bf16[256,2048]{1,0:T(8,128)(2,1)} %bitcast.99, bf16[128,5632]{1,0:T(8,128)(2,1)} %copy-done.3, ...), custom_call_target="tpu_custom_call" | custom-call | tf_op jit(solution)/shard_map/input_back/pallas_call | solution.py:375
  327.1 1.6 copy.74
  329.2 1.5 collective-permute-start.56
  330.7 2.0 add_convert_fusion.3
  332.7 1.7 collective-permute-done.56
  335.6 2.1 add_convert_fusion.2
  338.3 1.7 collective-permute-start.61
  341.0 3.2 collective-permute-start.54
  344.2 5.1 %collective-permute-done.59 = bf16[256,768]{1,0:T(8,128)(2,1)S(1)} collective-permute-done((bf16[256,768]{1,0:T(8,128)(2,1)}, bf16[256,768]{1,0:T(8,128)(2,1)S(1)}, u32[]{:S(2)}, u32[]{:S(2)}) %collective-permute-start.59) | collective-permute-done | bytes 393248 | tf_op jit(solution)/shard_map/ppermute | solution.py:76
  351.4 15.9 %collective-permute-done.60 = bf16[128,5120]{1,0:T(8,128)(2,1)S(1)} collective-permute-done((bf16[128,5120]{1,0:T(8,128)(2,1)S(1)}, bf16[128,5120]{1,0:T(8,128)(2,1)S(1)}, u32[]{:S(2)}, u32[]{:S(2)}) %collective-permute-start.60) | collective-permute-done | bytes 1310752 | tf_op jit(solution)/shard_map/ppermute | solution.py:73
  367.4 8.1 %collective-permute-done.61 = bf16[128,5120]{1,0:T(8,128)(2,1)S(1)} collective-permute-done((bf16[128,5120]{1,0:T(8,128)(2,1)S(1)}, bf16[128,5120]{1,0:T(8,128)(2,1)S(1)}, u32[]{:S(2)}, u32[]{:S(2)}) %collective-permute-start.61) | collective-permute-done | bytes 1310752 | tf_op jit(solution)/shard_map/ppermute | solution.py:76
  376.0 2.8 collective-permute-done.54
  378.8 1.5 collective-permute-start.62
  380.9 2.7 collective-permute-start.66
  383.6 1.7 select_bitcast_fusion
  385.3 2.8 collective-permute-done.62
  388.2 2.7 collective-permute-start.63
  392.9 24.0 %collective-permute-done.63 = bf16[128,640]{1,0:T(8,128)(2,1)} collective-permute-done((bf16[128,640]{1,0:T(8,128)(2,1)S(1)}, bf16[128,640]{1,0:T(8,128)(2,1)}, u32[]{:S(2)}, u32[]{:S(2)}) %collective-permute-start.63) | collective-permute-done | bytes 163872 | tf_op jit(solution)/shard_map/ppermute | solution.py:76
  423.7 1.5 collective-permute-start.72
  426.4 2.6 collective-permute-start.71
  429.0 1.3 collective-permute-done.68
  438.2 16.4 %collective-permute-done.70 = bf16[128,4096]{1,0:T(8,128)(2,1)} collective-permute-done((bf16[128,4096]{1,0:T(8,128)(2,1)}, bf16[128,4096]{1,0:T(8,128)(2,1)}, u32[]{:S(2)}, u32[]{:S(2)}) %collective-permute-start.70) | collective-permute-done | bytes 1048608 | tf_op jit(solution)/shard_map/ppermute | solution.py:1116
  454.5 3.5 collective-permute-done.71
  458.0 2.0 convert_add_fusion
  460.1 1.7 reshape.193
  461.8 1.7 reshape.194
  (367 shorter events, 74.8 us)
Async XLA Ops:
  4.0 16.3 %collective-permute-start = (bf16[128,2048]{1,0:T(8,128)(2,1)S(1)}, bf16[128,2048]{1,0:T(8,128)(2,1)}, u32[]{:S(2)}, u32[]{:S(2)}) collective-permute-start(bf16[128,2048]{1,0:T(8,128)(2,1)S(1)} %bitcast.105), channel_id=1, source_target_pairs={{0,0},{1,16},{16,1},{17,17},{2,2},{3,18},{18,3},{19,19},{4,4},{5,2... | collective-permute-start | bytes 1572872 | tf_op jit(solution)/shard_map/ppermute | solution.py:37
  5.4 16.2 %collective-permute-start.1 = (bf16[128,2048]{1,0:T(8,128)(2,1)}, bf16[128,2048]{1,0:T(8,128)(2,1)}, u32[]{:S(2)}, u32[]{:S(2)}) collective-permute-start(bf16[128,2048]{1,0:T(8,128)(2,1)} %bitcast.63), channel_id=1, source_target_pairs={{0,0},{1,16},{16,1},{17,17},{2,2},{3,18},{18,3},{19,19},{4,4},{5,2... | collective-permute-start | bytes 1572872 | tf_op jit(solution)/shard_map/ppermute | solution.py:37
  14.8 13.2 %collective-permute-start.2 = (bf16[128,1536]{1,0:T(8,128)(2,1)}, bf16[128,1536]{1,0:T(8,128)(2,1)S(1)}, u32[]{:S(2)}, u32[]{:S(2)}) collective-permute-start(bf16[128,1536]{1,0:T(8,128)(2,1)} %get-tuple-element.211), channel_id=1, source_target_pairs={{0,4},{2,6},{4,8},{6,10},{8,12},{10,14},{12,0},{14,2},{1,5},{3,7},... | collective-permute-start | bytes 1179656 | tf_op jit(solution)/shard_map/ppermute | solution.py:76
  17.8 10.2 %collective-permute-start.4 = (bf16[128,1536]{1,0:T(8,128)(2,1)}, bf16[128,1536]{1,0:T(8,128)(2,1)}, u32[]{:S(2)}, u32[]{:S(2)}) collective-permute-start(bf16[128,1536]{1,0:T(8,128)(2,1)} %get-tuple-element.211), channel_id=1, source_target_pairs={{0,2},{2,0},{4,6},{6,4},{8,10},{10,8},{12,14},{14,12},{1,3},{3,1},... | collective-permute-start | bytes 1179656 | tf_op jit(solution)/shard_map/ppermute | solution.py:73
  19.3 8.7 %collective-permute-start.3 = (bf16[1,2048]{1,0:T(2,128)(2,1)S(1)}, bf16[1,2048]{1,0:T(2,128)(2,1)S(1)}, u32[]{:S(2)}, u32[]{:S(2)}) collective-permute-start(bf16[1,2048]{1,0:T(2,128)(2,1)S(1)} %bitcast.117), channel_id=1, source_target_pairs={{0,0},{1,16},{16,1},{17,17},{2,2},{3,18},{18,3},{19,19},{4,4},{5,2... | collective-permute-start | bytes 12296 | tf_op jit(solution)/shard_map/ppermute | solution.py:37
  28.0 36.7 %collective-permute-start.5 = (bf16[128,5632]{1,0:T(8,128)(2,1)S(1)}, bf16[128,5632]{1,0:T(8,128)(2,1)}, u32[]{:S(2)}, u32[]{:S(2)}) collective-permute-start(bf16[128,5632]{1,0:T(8,128)(2,1)S(1)} %constant_dynamic-update-slice_fusion.4.refs_0_.refs_16_), channel_id=1, source_target_pairs={{0,4},{2,6},{4,8},{6,10},{8,12},{10,14},{12,0},{14,2},{1,5},{3,7},... | collective-permute-start | bytes 4325384 | tf_op jit(solution)/shard_map/ppermute | solution.py:76
  29.1 35.6 %collective-permute-start.6 = (bf16[128,5632]{1,0:T(8,128)(2,1)S(1)}, bf16[128,5632]{1,0:T(8,128)(2,1)}, u32[]{:S(2)}, u32[]{:S(2)}) collective-permute-start(bf16[128,5632]{1,0:T(8,128)(2,1)S(1)} %constant_dynamic-update-slice_fusion.4.refs_0_.refs_16_), channel_id=1, source_target_pairs={{0,2},{2,0},{4,6},{6,4},{8,10},{10,8},{12,14},{14,12},{1,3},{3,1},... | collective-permute-start | bytes 4325384 | tf_op jit(solution)/shard_map/ppermute | solution.py:73
  30.6 34.7 %collective-permute-start.17 = (bf16[16,32,1024]{2,0,1:T(8,128)(2,1)}, bf16[16,32,1024]{2,0,1:T(8,128)(2,1)}, u32[]{:S(2)}, u32[]{:S(2)}) collective-permute-start(bf16[16,32,1024]{2,0,1:T(8,128)(2,1)} %bitcast.28), channel_id=1, source_target_pairs={{0,16},{16,0},{1,17},{17,1},{2,18},{18,2},{3,19},{19,3},{4,20},{20... | collective-permute-start | bytes 3145736 | tf_op jit(solution)/shard_map/ppermute | solution.py:29
  32.4 32.3 %collective-permute-start.8 = (bf16[128,3072]{1,0:T(8,128)(2,1)}, bf16[128,3072]{1,0:T(8,128)(2,1)}, u32[]{:S(2)}, u32[]{:S(2)}) collective-permute-start(bf16[128,3072]{1,0:T(8,128)(2,1)} %constant_dynamic-update-slice_fusion.7.refs_0_), channel_id=1, source_target_pairs={{0,1},{1,0},{2,3},{3,2},{4,5},{5,4},{6,7},{7,6},{8,9},{9,8},{10,11... | collective-permute-start | bytes 2359304 | tf_op jit(solution)/shard_map/ppermute | solution.py:33
  36.2 28.5 %collective-permute-start.7 = (bf16[256,1024]{1,0:T(8,128)(2,1)S(1)}, bf16[256,1024]{1,0:T(8,128)(2,1)S(1)}, u32[]{:S(2)}, u32[]{:S(2)}) collective-permute-start(bf16[256,1024]{1,0:T(8,128)(2,1)S(1)} %pad.24.refs_16_), channel_id=1, source_target_pairs={{0,1},{1,0},{2,3},{3,2},{4,5},{5,4},{6,7},{7,6},{8,9},{9,8},{10,11... | collective-permute-start | bytes 1572872 | tf_op jit(solution)/shard_map/ppermute | solution.py:33
  64.7 47.6 %collective-permute-start.20 = (bf16[128,3072]{1,0:T(8,128)(2,1)}, bf16[128,3072]{1,0:T(8,128)(2,1)S(1)}, u32[]{:S(2)}, u32[]{:S(2)}) collective-permute-start(bf16[128,3072]{1,0:T(8,128)(2,1)} %constant_dynamic-update-slice_fusion.7.refs_0_), channel_id=1, source_target_pairs={{0,16},{16,0},{1,17},{17,1},{2,18},{18,2},{3,19},{19,3},{4,20},{20... | collective-permute-start | bytes 2359304 | tf_op jit(solution)/shard_map/ppermute | solution.py:29
  64.7 34.4 %collective-permute-start.11 = (bf16[128,5632]{1,0:T(8,128)(2,1)}, bf16[128,5632]{1,0:T(8,128)(2,1)}, u32[]{:S(2)}, u32[]{:S(2)}) collective-permute-start(bf16[128,5632]{1,0:T(8,128)(2,1)} %collective-permute-done.5.refs_2_.refs_18_), channel_id=1, source_target_pairs={{0,2},{2,0},{4,6},{6,4},{8,10},{10,8},{12,14},{14,12},{1,3},{3,1},... | collective-permute-start | bytes 4325384 | tf_op jit(solution)/shard_map/ppermute | solution.py:73
  66.8 36.1 %collective-permute-start.10 = (bf16[128,5632]{1,0:T(8,128)(2,1)}, bf16[128,5632]{1,0:T(8,128)(2,1)S(1)}, u32[]{:S(2)}, u32[]{:S(2)}) collective-permute-start(bf16[128,5632]{1,0:T(8,128)(2,1)} %collective-permute-done.5.refs_2_.refs_18_), channel_id=1, source_target_pairs={{0,4},{2,6},{4,8},{6,10},{8,12},{10,14},{12,0},{14,2},{1,5},{3,7},... | collective-permute-start | bytes 4325384 | tf_op jit(solution)/shard_map/ppermute | solution.py:76
  69.9 34.6 %collective-permute-start.12 = (bf16[128,3072]{1,0:T(8,128)(2,1)S(1)}, bf16[128,3072]{1,0:T(8,128)(2,1)}, u32[]{:S(2)}, u32[]{:S(2)}) collective-permute-start(bf16[128,3072]{1,0:T(8,128)(2,1)S(1)} %pad_maximum_fusion.2.refs_1_), channel_id=1, source_target_pairs={{0,1},{1,0},{2,3},{3,2},{4,5},{5,4},{6,7},{7,6},{8,9},{9,8},{10,11... | collective-permute-start | bytes 2359304 | tf_op jit(solution)/shard_map/ppermute | solution.py:33
  72.3 40.1 %collective-permute-start.21 = (bf16[128,3072]{1,0:T(8,128)(2,1)S(1)}, bf16[128,3072]{1,0:T(8,128)(2,1)S(1)}, u32[]{:S(2)}, u32[]{:S(2)}) collective-permute-start(bf16[128,3072]{1,0:T(8,128)(2,1)S(1)} %pad_maximum_fusion.2.refs_1_), channel_id=1, source_target_pairs={{0,16},{16,0},{1,17},{17,1},{2,18},{18,2},{3,19},{19,3},{4,20},{20... | collective-permute-start | bytes 2359304 | tf_op jit(solution)/shard_map/ppermute | solution.py:29
  99.1 5.4 %collective-permute-start.9 = (f32[5,256]{1,0:T(8,128)S(1)}, f32[5,256]{1,0:T(8,128)S(1)}, u32[]{:S(2)}, u32[]{:S(2)}) collective-permute-start(f32[5,256]{1,0:T(8,128)S(1)} %stack.129), channel_id=1, source_target_pairs={{0,1},{1,0},{2,3},{3,2},{4,5},{5,4},{6,7},{7,6},{8,9},{9,8},{10,11... | collective-permute-start | bytes 15368 | tf_op jit(solution)/shard_map/ppermute | solution.py:33
  102.9 19.5 %collective-permute-start.19 = (bf16[128,3072]{1,0:T(8,128)(2,1)}, bf16[128,3072]{1,0:T(8,128)(2,1)}, u32[]{:S(2)}, u32[]{:S(2)}) collective-permute-start(bf16[128,3072]{1,0:T(8,128)(2,1)} %pad_maximum_fusion.3.refs_2_), channel_id=1, source_target_pairs={{0,1},{1,0},{2,3},{3,2},{4,5},{5,4},{6,7},{7,6},{8,9},{9,8},{10,11... | collective-permute-start | bytes 2359304 | tf_op jit(solution)/shard_map/ppermute | solution.py:33
  104.5 32.1 %collective-permute-start.23 = (bf16[128,5632]{1,0:T(8,128)(2,1)S(1)}, bf16[128,5632]{1,0:T(8,128)(2,1)S(1)}, u32[]{:S(2)}, u32[]{:S(2)}) collective-permute-start(bf16[128,5632]{1,0:T(8,128)(2,1)S(1)} %collective-permute-done.10.refs_4_.refs_20_), channel_id=1, source_target_pairs={{0,2},{2,0},{4,6},{6,4},{8,10},{10,8},{12,14},{14,12},{1,3},{3,1},... | collective-permute-start | bytes 4325384 | tf_op jit(solution)/shard_map/ppermute | solution.py:73
  106.3 25.5 %collective-permute-start.13 = (bf16[128,4096]{1,0:T(8,128)(2,1)S(1)}, bf16[128,4096]{1,0:T(8,128)(2,1)}, u32[]{:S(2)}, u32[]{:S(2)}) collective-permute-start(bf16[128,4096]{1,0:T(8,128)(2,1)S(1)} %slice.293), channel_id=1, source_target_pairs={{0,4},{2,6},{4,8},{6,10},{8,12},{10,14},{12,0},{14,2},{1,5},{3,7},... | collective-permute-start | bytes 3145736 | tf_op jit(solution)/shard_map/ppermute | solution.py:76
  112.3 24.2 %collective-permute-start.27 = (bf16[128,5632]{1,0:T(8,128)(2,1)S(1)}, bf16[128,5632]{1,0:T(8,128)(2,1)S(1)}, u32[]{:S(2)}, u32[]{:S(2)}) collective-permute-start(bf16[128,5632]{1,0:T(8,128)(2,1)S(1)} %constant_dynamic-update-slice_fusion.4.refs_0_.refs_16_), channel_id=1, source_target_pairs={{0,16},{16,0},{1,17},{17,1},{2,18},{18,2},{3,19},{19,3},{4,20},{20... | collective-permute-start | bytes 4325384 | tf_op jit(solution)/shard_map/ppermute | solution.py:29
  112.4 27.1 %collective-permute-start.29 = (bf16[128,5632]{1,0:T(8,128)(2,1)}, bf16[128,5632]{1,0:T(8,128)(2,1)}, u32[]{:S(2)}, u32[]{:S(2)}) collective-permute-start(bf16[128,5632]{1,0:T(8,128)(2,1)} %collective-permute-done.5.refs_2_.refs_18_), channel_id=1, source_target_pairs={{0,16},{16,0},{1,17},{17,1},{2,18},{18,2},{3,19},{19,3},{4,20},{20... | collective-permute-start | bytes 4325384 | tf_op jit(solution)/shard_map/ppermute | solution.py:29
  122.4 19.6 %collective-permute-start.28 = (bf16[128,5632]{1,0:T(8,128)(2,1)}, bf16[128,5632]{1,0:T(8,128)(2,1)}, u32[]{:S(2)}, u32[]{:S(2)}) collective-permute-start(bf16[128,5632]{1,0:T(8,128)(2,1)} %collective-permute-done.6.refs_1_.refs_17_), channel_id=1, source_target_pairs={{0,16},{16,0},{1,17},{17,1},{2,18},{18,2},{3,19},{19,3},{4,20},{20... | collective-permute-start | bytes 4325384 | tf_op jit(solution)/shard_map/ppermute | solution.py:29
  131.8 12.3 %collective-permute-start.30 = (bf16[128,5632]{1,0:T(8,128)(2,1)}, bf16[128,5632]{1,0:T(8,128)(2,1)}, u32[]{:S(2)}, u32[]{:S(2)}) collective-permute-start(bf16[128,5632]{1,0:T(8,128)(2,1)} %collective-permute-done.11.refs_3_.refs_19_), channel_id=1, source_target_pairs={{0,16},{16,0},{1,17},{17,1},{2,18},{18,2},{3,19},{19,3},{4,20},{20... | collective-permute-start | bytes 4325384 | tf_op jit(solution)/shard_map/ppermute | solution.py:29
  136.5 5.6 %collective-permute-start.22 = (bf16[128,3072]{1,0:T(8,128)(2,1)}, bf16[128,3072]{1,0:T(8,128)(2,1)}, u32[]{:S(2)}, u32[]{:S(2)}) collective-permute-start(bf16[128,3072]{1,0:T(8,128)(2,1)} %pad_maximum_fusion.3.refs_2_), channel_id=1, source_target_pairs={{0,16},{16,0},{1,17},{17,1},{2,18},{18,2},{3,19},{19,3},{4,20},{20... | collective-permute-start | bytes 2359304 | tf_op jit(solution)/shard_map/ppermute | solution.py:29
  137.7 24.8 %collective-permute-start.26 = (bf16[128,4096]{1,0:T(8,128)(2,1)}, bf16[128,4096]{1,0:T(8,128)(2,1)}, u32[]{:S(2)}, u32[]{:S(2)}) collective-permute-start(bf16[128,4096]{1,0:T(8,128)(2,1)} %collective-permute-done.13.refs_6_.refs_22_), channel_id=1, source_target_pairs={{0,2},{2,0},{4,6},{6,4},{8,10},{10,8},{12,14},{14,12},{1,3},{3,1},... | collective-permute-start | bytes 3145736 | tf_op jit(solution)/shard_map/ppermute | solution.py:73
  144.0 18.6 %collective-permute-start.24 = (bf16[128,3072]{1,0:T(8,128)(2,1)S(1)}, bf16[128,3072]{1,0:T(8,128)(2,1)S(1)}, u32[]{:S(2)}, u32[]{:S(2)}) collective-permute-start(bf16[128,3072]{1,0:T(8,128)(2,1)S(1)} %pad_maximum_fusion.4.refs_3_), channel_id=1, source_target_pairs={{0,16},{16,0},{1,17},{17,1},{2,18},{18,2},{3,19},{19,3},{4,20},{20... | collective-permute-start | bytes 2359304 | tf_op jit(solution)/shard_map/ppermute | solution.py:29
  144.1 20.1 %collective-permute-start.31 = (bf16[128,5632]{1,0:T(8,128)(2,1)S(1)}, bf16[128,5632]{1,0:T(8,128)(2,1)S(1)}, u32[]{:S(2)}, u32[]{:S(2)}) collective-permute-start(bf16[128,5632]{1,0:T(8,128)(2,1)S(1)} %collective-permute-done.10.refs_4_.refs_20_), channel_id=1, source_target_pairs={{0,16},{16,0},{1,17},{17,1},{2,18},{18,2},{3,19},{19,3},{4,20},{20... | collective-permute-start | bytes 4325384 | tf_op jit(solution)/shard_map/ppermute | solution.py:29
  144.5 20.2 %collective-permute-start.32 = (bf16[128,5632]{1,0:T(8,128)(2,1)S(1)}, bf16[128,5632]{1,0:T(8,128)(2,1)S(1)}, u32[]{:S(2)}, u32[]{:S(2)}) collective-permute-start(bf16[128,5632]{1,0:T(8,128)(2,1)S(1)} %copy-done.5), channel_id=1, source_target_pairs={{0,16},{16,0},{1,17},{17,1},{2,18},{18,2},{3,19},{19,3},{4,20},{20... | collective-permute-start | bytes 4325384 | tf_op jit(solution)/shard_map/ppermute | solution.py:29
  144.6 19.7 %collective-permute-start.33 = (bf16[128,4096]{1,0:T(8,128)(2,1)}, bf16[128,4096]{1,0:T(8,128)(2,1)S(1)}, u32[]{:S(2)}, u32[]{:S(2)}) collective-permute-start(bf16[128,4096]{1,0:T(8,128)(2,1)} %collective-permute-done.13.refs_6_.refs_22_), channel_id=1, source_target_pairs={{0,16},{16,0},{1,17},{17,1},{2,18},{18,2},{3,19},{19,3},{4,20},{20... | collective-permute-start | bytes 3145736 | tf_op jit(solution)/shard_map/ppermute | solution.py:29
  162.6 33.6 %collective-permute-start.37 = (bf16[128,3072]{1,0:T(8,128)(2,1)S(1)}, bf16[128,3072]{1,0:T(8,128)(2,1)}, u32[]{:S(2)}, u32[]{:S(2)}) collective-permute-start(bf16[128,3072]{1,0:T(8,128)(2,1)S(1)} %pad_maximum_fusion.4.refs_3_), channel_id=1, source_target_pairs={{0,1},{1,0},{2,3},{3,2},{4,5},{5,4},{6,7},{7,6},{8,9},{9,8},{10,11... | collective-permute-start | bytes 2359304 | tf_op jit(solution)/shard_map/ppermute | solution.py:33
  164.2 42.0 %collective-permute-start.38 = (bf16[128,3072]{1,0:T(8,128)(2,1)}, bf16[128,3072]{1,0:T(8,128)(2,1)S(1)}, u32[]{:S(2)}, u32[]{:S(2)}) collective-permute-start(bf16[128,3072]{1,0:T(8,128)(2,1)} %collective-permute-done.8.refs_4_), channel_id=1, source_target_pairs={{0,16},{16,0},{1,17},{17,1},{2,18},{18,2},{3,19},{19,3},{4,20},{20... | collective-permute-start | bytes 2359304 | tf_op jit(solution)/shard_map/ppermute | solution.py:29
  164.4 42.0 %collective-permute-start.39 = (bf16[128,3072]{1,0:T(8,128)(2,1)}, bf16[128,3072]{1,0:T(8,128)(2,1)S(1)}, u32[]{:S(2)}, u32[]{:S(2)}) collective-permute-start(bf16[128,3072]{1,0:T(8,128)(2,1)} %collective-permute-done.12.refs_5_), channel_id=1, source_target_pairs={{0,16},{16,0},{1,17},{17,1},{2,18},{18,2},{3,19},{19,3},{4,20},{20... | collective-permute-start | bytes 2359304 | tf_op jit(solution)/shard_map/ppermute | solution.py:29
  164.7 41.6 %collective-permute-start.40 = (bf16[128,3072]{1,0:T(8,128)(2,1)}, bf16[128,3072]{1,0:T(8,128)(2,1)S(1)}, u32[]{:S(2)}, u32[]{:S(2)}) collective-permute-start(bf16[128,3072]{1,0:T(8,128)(2,1)} %collective-permute-done.19.refs_6_), channel_id=1, source_target_pairs={{0,16},{16,0},{1,17},{17,1},{2,18},{18,2},{3,19},{19,3},{4,20},{20... | collective-permute-start | bytes 2359304 | tf_op jit(solution)/shard_map/ppermute | solution.py:29
  196.2 10.2 %collective-permute-start.41 = (bf16[128,3072]{1,0:T(8,128)(2,1)}, bf16[128,3072]{1,0:T(8,128)(2,1)S(1)}, u32[]{:S(2)}, u32[]{:S(2)}) collective-permute-start(bf16[128,3072]{1,0:T(8,128)(2,1)} %collective-permute-done.37.refs_7_), channel_id=1, source_target_pairs={{0,16},{16,0},{1,17},{17,1},{2,18},{18,2},{3,19},{19,3},{4,20},{20... | collective-permute-start | bytes 2359304 | tf_op jit(solution)/shard_map/ppermute | solution.py:29
  196.4 8.8 %collective-permute-start.35 = (bf16[128,1024]{1,0:T(8,128)(2,1)}, bf16[128,1024]{1,0:T(8,128)(2,1)S(1)}, u32[]{:S(2)}, u32[]{:S(2)}) collective-permute-start(bf16[128,1024]{1,0:T(8,128)(2,1)} %bitcast.110), channel_id=1, source_target_pairs={{0,1},{1,0},{2,3},{3,2},{4,5},{5,4},{6,7},{7,6},{8,9},{9,8},{10,11... | collective-permute-start | bytes 786440 | tf_op jit(solution)/shard_map/ppermute | solution.py:33
  205.2 34.6 %collective-permute-start.44 = (bf16[128,1024]{1,0:T(8,128)(2,1)}, bf16[128,1024]{1,0:T(8,128)(2,1)S(1)}, u32[]{:S(2)}, u32[]{:S(2)}) collective-permute-start(bf16[128,1024]{1,0:T(8,128)(2,1)} %bitcast.94), channel_id=1, source_target_pairs={{0,1},{1,0},{2,3},{3,2},{4,5},{5,4},{6,7},{7,6},{8,9},{9,8},{10,11... | collective-permute-start | bytes 786440 | tf_op jit(solution)/shard_map/ppermute | solution.py:33
  206.3 41.9 %collective-permute-start.36 = (bf16[256,1024]{1,0:T(8,128)(2,1)}, bf16[256,1024]{1,0:T(8,128)(2,1)}, u32[]{:S(2)}, u32[]{:S(2)}) collective-permute-start(bf16[256,1024]{1,0:T(8,128)(2,1)} %bitcast.106), channel_id=1, source_target_pairs={{0,16},{16,0},{1,17},{17,1},{2,18},{18,2},{3,19},{19,3},{4,20},{20... | collective-permute-start | bytes 1572872 | tf_op jit(solution)/shard_map/ppermute | solution.py:29
  239.8 8.9 %collective-permute-start.45 = (bf16[128,1024]{1,0:T(8,128)(2,1)}, bf16[128,1024]{1,0:T(8,128)(2,1)}, u32[]{:S(2)}, u32[]{:S(2)}) collective-permute-start(bf16[128,1024]{1,0:T(8,128)(2,1)} %get-tuple-element.128), channel_id=1, source_target_pairs={{0,1},{1,0},{2,3},{3,2},{4,5},{5,4},{6,7},{7,6},{8,9},{9,8},{10,11... | collective-permute-start | bytes 786440 | tf_op jit(solution)/shard_map/ppermute | solution.py:33
  241.9 6.8 %collective-permute-start.46 = (bf16[4,128,1024]{2,1,0:T(8,128)(2,1)S(1)}, bf16[4,128,1024]{2,1,0:T(8,128)(2,1)}, u32[]{:S(2)}, u32[]{:S(2)}) collective-permute-start(bf16[4,128,1024]{2,1,0:T(8,128)(2,1)S(1)} %pad_maximum_fusion.1.states_own), channel_id=1, source_target_pairs={{0,16},{16,0},{1,17},{17,1},{2,18},{18,2},{3,19},{19,3},{4,20},{20... | collective-permute-start | bytes 3145736 | tf_op jit(solution)/shard_map/ppermute | solution.py:29
  242.5 4.2 collective-permute-start.42
  242.6 6.1 %collective-permute-start.47 = (bf16[2,128,1024]{2,1,0:T(8,128)(2,1)S(1)}, bf16[2,128,1024]{2,1,0:T(8,128)(2,1)S(1)}, u32[]{:S(2)}, u32[]{:S(2)}) collective-permute-start(bf16[2,128,1024]{2,1,0:T(8,128)(2,1)S(1)} %copy-done.20), channel_id=1, source_target_pairs={{0,16},{16,0},{1,17},{17,1},{2,18},{18,2},{3,19},{19,3},{4,20},{20... | collective-permute-start | bytes 1572872 | tf_op jit(solution)/shard_map/ppermute | solution.py:29
  248.7 31.9 %collective-permute-start.48 = (bf16[2,128,1536]{2,1,0:T(8,128)(2,1)S(1)}, bf16[2,128,1536]{2,1,0:T(8,128)(2,1)S(1)}, u32[]{:S(2)}, u32[]{:S(2)}) collective-permute-start(bf16[2,128,1536]{2,1,0:T(8,128)(2,1)S(1)} %pad_maximum_fusion.5), channel_id=1, source_target_pairs={{0,1},{1,0},{2,3},{3,2},{4,5},{5,4},{6,7},{7,6},{8,9},{9,8},{10,11... | collective-permute-start | bytes 2359304 | tf_op jit(solution)/shard_map/ppermute | solution.py:33
  249.7 30.9 %collective-permute-start.49 = (bf16[2,128,1152]{2,1,0:T(8,128)(2,1)S(1)}, bf16[2,128,1152]{2,1,0:T(8,128)(2,1)}, u32[]{:S(2)}, u32[]{:S(2)}) collective-permute-start(bf16[2,128,1152]{2,1,0:T(8,128)(2,1)S(1)} %pad_maximum_fusion.6), channel_id=1, source_target_pairs={{0,1},{1,0},{2,3},{3,2},{4,5},{5,4},{6,7},{7,6},{8,9},{9,8},{10,11... | collective-permute-start | bytes 1769480 | tf_op jit(solution)/shard_map/ppermute | solution.py:33
  281.5 3.7 collective-permute-start.50
  301.6 14.3 %collective-permute-start.52 = (bf16[256,768]{1,0:T(8,128)(2,1)}, bf16[256,768]{1,0:T(8,128)(2,1)S(1)}, u32[]{:S(2)}, u32[]{:S(2)}) collective-permute-start(bf16[256,768]{1,0:T(8,128)(2,1)} %get-tuple-element.148), channel_id=1, source_target_pairs={{0,4},{2,6},{4,8},{6,10},{8,12},{10,14},{12,0},{14,2},{1,5},{3,7},... | collective-permute-start | bytes 1179656 | tf_op jit(solution)/shard_map/ppermute | solution.py:76
  303.1 32.1 %collective-permute-start.58 = (bf16[128,5120]{1,0:T(8,128)(2,1)}, bf16[128,5120]{1,0:T(8,128)(2,1)}, u32[]{:S(2)}, u32[]{:S(2)}) collective-permute-start(bf16[128,5120]{1,0:T(8,128)(2,1)} %get-tuple-element.155), channel_id=1, source_target_pairs={{0,2},{2,0},{4,6},{6,4},{8,10},{10,8},{12,14},{14,12},{1,3},{3,1},... | collective-permute-start | bytes 3932168 | tf_op jit(solution)/shard_map/ppermute | solution.py:73
  307.8 42.2 %collective-permute-start.57 = (bf16[256,768]{1,0:T(8,128)(2,1)}, bf16[256,768]{1,0:T(8,128)(2,1)}, u32[]{:S(2)}, u32[]{:S(2)}) collective-permute-start(bf16[256,768]{1,0:T(8,128)(2,1)} %get-tuple-element.153), channel_id=1, source_target_pairs={{4,0},{6,2},{8,4},{10,6},{12,8},{14,10},{0,12},{2,14},{5,1},{7,3},... | collective-permute-start | bytes 1179656 | tf_op jit(solution)/shard_map/ppermute | solution.py:79
  328.7 11.4 %collective-permute-start.53 = (f32[16,16,1024]{2,1,0:T(8,128)}, f32[16,16,1024]{2,1,0:T(8,128)S(1)}, u32[]{:S(2)}, u32[]{:S(2)}) collective-permute-start(f32[16,16,1024]{2,1,0:T(8,128)} %bitcast.83), channel_id=1, source_target_pairs={{0,16},{16,0},{1,17},{17,1},{2,18},{18,2},{3,19},{19,3},{4,20},{20... | collective-permute-start | bytes 3145736 | tf_op jit(solution)/shard_map/ppermute | solution.py:29
  329.2 5.2 %collective-permute-start.56 = (f32[8,768]{1,0:T(8,128)S(1)}, f32[8,768]{1,0:T(8,128)S(1)}, u32[]{:S(2)}, u32[]{:S(2)}) collective-permute-start(f32[8,768]{1,0:T(8,128)S(1)} %reshape.189), channel_id=1, source_target_pairs={{0,2},{2,0},{4,6},{6,4},{8,10},{10,8},{12,14},{14,12},{1,3},{3,1},... | collective-permute-start | bytes 73736 | tf_op jit(solution)/shard_map/ppermute | solution.py:73
  335.2 14.1 %collective-permute-start.59 = (bf16[256,768]{1,0:T(8,128)(2,1)}, bf16[256,768]{1,0:T(8,128)(2,1)S(1)}, u32[]{:S(2)}, u32[]{:S(2)}) collective-permute-start(bf16[256,768]{1,0:T(8,128)(2,1)} %add_convert_fusion.3), channel_id=1, source_target_pairs={{0,4},{2,6},{4,8},{6,10},{8,12},{10,14},{12,0},{14,2},{1,5},{3,7},... | collective-permute-start | bytes 1179656 | tf_op jit(solution)/shard_map/ppermute | solution.py:76
  337.7 29.6 %collective-permute-start.60 = (bf16[128,5120]{1,0:T(8,128)(2,1)S(1)}, bf16[128,5120]{1,0:T(8,128)(2,1)S(1)}, u32[]{:S(2)}, u32[]{:S(2)}) collective-permute-start(bf16[128,5120]{1,0:T(8,128)(2,1)S(1)} %copy-done.65), channel_id=1, source_target_pairs={{0,2},{2,0},{4,6},{6,4},{8,10},{10,8},{12,14},{14,12},{1,3},{3,1},... | collective-permute-start | bytes 3932168 | tf_op jit(solution)/shard_map/ppermute | solution.py:73
  338.3 37.1 %collective-permute-start.61 = (bf16[128,5120]{1,0:T(8,128)(2,1)S(1)}, bf16[128,5120]{1,0:T(8,128)(2,1)S(1)}, u32[]{:S(2)}, u32[]{:S(2)}) collective-permute-start(bf16[128,5120]{1,0:T(8,128)(2,1)S(1)} %add_convert_fusion.2), channel_id=1, source_target_pairs={{0,4},{2,6},{4,8},{6,10},{8,12},{10,14},{12,0},{14,2},{1,5},{3,7},... | collective-permute-start | bytes 3932168 | tf_op jit(solution)/shard_map/ppermute | solution.py:76
  341.0 37.9 %collective-permute-start.54 = (f32[32,16,1024]{2,1,0:T(8,128)S(1)}, f32[32,16,1024]{2,1,0:T(8,128)S(1)}, u32[]{:S(2)}, u32[]{:S(2)}) collective-permute-start(f32[32,16,1024]{2,1,0:T(8,128)S(1)} %pad_maximum_fusion), channel_id=1, source_target_pairs={{0,1},{17,16},{2,3},{19,18},{4,5},{21,20},{6,7},{23,22},{8,9},{25,... | collective-permute-start | bytes 6291464 | tf_op jit(solution)/shard_map/ppermute | solution.py:1099
  349.3 72.4 %collective-permute-start.67 = (bf16[128,4096]{1,0:T(8,128)(2,1)S(1)}, bf16[128,4096]{1,0:T(8,128)(2,1)S(1)}, u32[]{:S(2)}, u32[]{:S(2)}) collective-permute-start(bf16[128,4096]{1,0:T(8,128)(2,1)S(1)} %copy-done.27), channel_id=1, source_target_pairs={{0,0},{1,16},{16,1},{17,17},{2,2},{3,18},{18,3},{19,19},{4,4},{5,2... | collective-permute-start | bytes 3145736 | tf_op jit(solution)/shard_map/ppermute | solution.py:37
  378.8 9.2 %collective-permute-start.62 = (bf16[128,1024]{1,0:T(8,128)(2,1)S(1)}, bf16[128,1024]{1,0:T(8,128)(2,1)S(1)}, u32[]{:S(2)}, u32[]{:S(2)}) collective-permute-start(bf16[128,1024]{1,0:T(8,128)(2,1)S(1)} %pad_maximum_fusion.7), channel_id=1, source_target_pairs={{0,2},{2,0},{4,6},{6,4},{8,10},{10,8},{12,14},{14,12},{1,3},{3,1},... | collective-permute-start | bytes 786440 | tf_op jit(solution)/shard_map/ppermute | solution.py:73
  380.4 39.0 %collective-permute-start.65 = (bf16[128,5120]{1,0:T(8,128)(2,1)S(1)}, bf16[128,5120]{1,0:T(8,128)(2,1)S(1)}, u32[]{:S(2)}, u32[]{:S(2)}) collective-permute-start(bf16[128,5120]{1,0:T(8,128)(2,1)S(1)} %copy-done.64), channel_id=1, source_target_pairs={{0,2},{2,0},{4,6},{6,4},{8,10},{10,8},{12,14},{14,12},{1,3},{3,1},... | collective-permute-start | bytes 3932168 | tf_op jit(solution)/shard_map/ppermute | solution.py:73
  380.9 38.5 %collective-permute-start.66 = (bf16[128,5120]{1,0:T(8,128)(2,1)S(1)}, bf16[128,5120]{1,0:T(8,128)(2,1)S(1)}, u32[]{:S(2)}, u32[]{:S(2)}) collective-permute-start(bf16[128,5120]{1,0:T(8,128)(2,1)S(1)} %add_convert_fusion.1), channel_id=1, source_target_pairs={{0,4},{2,6},{4,8},{6,10},{8,12},{10,14},{12,0},{14,2},{1,5},{3,7},... | collective-permute-start | bytes 3932168 | tf_op jit(solution)/shard_map/ppermute | solution.py:76
  388.2 28.7 %collective-permute-start.63 = (bf16[128,640]{1,0:T(8,128)(2,1)S(1)}, bf16[128,640]{1,0:T(8,128)(2,1)}, u32[]{:S(2)}, u32[]{:S(2)}) collective-permute-start(bf16[128,640]{1,0:T(8,128)(2,1)S(1)} %pad_maximum_fusion.9), channel_id=1, source_target_pairs={{0,4},{2,6},{4,8},{6,10},{8,12},{10,14},{12,0},{14,2},{1,5},{3,7},... | collective-permute-start | bytes 491528 | tf_op jit(solution)/shard_map/ppermute | solution.py:76
  390.9 27.4 %collective-permute-start.64 = (bf16[128,640]{1,0:T(8,128)(2,1)S(1)}, bf16[128,640]{1,0:T(8,128)(2,1)S(1)}, u32[]{:S(2)}, u32[]{:S(2)}) collective-permute-start(bf16[128,640]{1,0:T(8,128)(2,1)S(1)} %pad_maximum_fusion.9), channel_id=1, source_target_pairs={{4,0},{6,2},{8,4},{10,6},{12,8},{14,10},{0,12},{2,14},{5,1},{7,3},... | collective-permute-start | bytes 491528 | tf_op jit(solution)/shard_map/ppermute | solution.py:79
  421.7 8.6 %collective-permute-start.68 = (bf16[128,640]{1,0:T(8,128)(2,1)}, bf16[128,640]{1,0:T(8,128)(2,1)}, u32[]{:S(2)}, u32[]{:S(2)}) collective-permute-start(bf16[128,640]{1,0:T(8,128)(2,1)} %collective-permute-done.63), channel_id=1, source_target_pairs={{0,4},{2,6},{4,8},{6,10},{8,12},{10,14},{12,0},{14,2},{1,5},{3,7},... | collective-permute-start | bytes 491528 | tf_op jit(solution)/shard_map/ppermute | solution.py:76
  423.7 13.5 %collective-permute-start.72 = (bf16[128,1024]{1,0:T(8,128)(2,1)}, bf16[128,1024]{1,0:T(8,128)(2,1)S(1)}, u32[]{:S(2)}, u32[]{:S(2)}) collective-permute-start(bf16[128,1024]{1,0:T(8,128)(2,1)} %slice.260), channel_id=1, source_target_pairs={{0,2},{2,0},{4,6},{6,4},{8,10},{10,8},{12,14},{14,12},{1,3},{3,1},... | collective-permute-start | bytes 786440 | tf_op jit(solution)/shard_map/ppermute | solution.py:73
  425.3 12.0 %collective-permute-start.73 = (bf16[128,1024]{1,0:T(8,128)(2,1)}, bf16[128,1024]{1,0:T(8,128)(2,1)S(1)}, u32[]{:S(2)}, u32[]{:S(2)}) collective-permute-start(bf16[128,1024]{1,0:T(8,128)(2,1)} %slice.318), channel_id=1, source_target_pairs={{0,4},{2,6},{4,8},{6,10},{8,12},{10,14},{12,0},{14,2},{1,5},{3,7},... | collective-permute-start | bytes 786440 | tf_op jit(solution)/shard_map/ppermute | solution.py:76
  425.9 28.6 %collective-permute-start.70 = (bf16[128,4096]{1,0:T(8,128)(2,1)}, bf16[128,4096]{1,0:T(8,128)(2,1)}, u32[]{:S(2)}, u32[]{:S(2)}) collective-permute-start(bf16[128,4096]{1,0:T(8,128)(2,1)} %slice.258), channel_id=1, source_target_pairs={{0,2},{1,18},{16,3},{17,19},{2,0},{3,16},{18,1},{19,17},{4,6},{5,2... | collective-permute-start | bytes 3145736 | tf_op jit(solution)/shard_map/ppermute | solution.py:1116
  426.4 31.6 %collective-permute-start.71 = (bf16[128,4096]{1,0:T(8,128)(2,1)}, bf16[128,4096]{1,0:T(8,128)(2,1)}, u32[]{:S(2)}, u32[]{:S(2)}) collective-permute-start(bf16[128,4096]{1,0:T(8,128)(2,1)} %slice.317), channel_id=1, source_target_pairs={{0,4},{1,20},{16,5},{17,21},{2,6},{3,22},{18,7},{19,23},{4,8},{5,2... | collective-permute-start | bytes 3145736 | tf_op jit(solution)/shard_map/ppermute | solution.py:1116
  (79 other events, 997.4 us)
